TPU v7x, 32 devices: a whole 2x2x4 slice. The times are simulated.
32 devices in a mesh: seq: 8 (over z, y), feat: 4 (over x, core).
Axes of the slice: x: 2, y: 2, z: 4, core: 2. Of those that a mesh axis runs over, the one named last changes fastest.
Arguments:
- activations_in: bfloat16 [6144, 512], P('seq', 'feat'), may hold values from -6 to 6
- cotangent: bfloat16 [6144, 512], P('seq', 'feat'), may hold values from -6 to 6
- seq_start: int32 [16], P('seq'), may hold values from 0 to 768, as said below
- seq_length: int32 [16], P('seq'), may hold values from 0 to 768, as said below
- input_matrix: float32 [2, 512, 768], P(None, 'feat'), may hold values from -0.25 to 0.25
- output_matrix: float32 [2, 1536, 512], P(None, None, 'feat'), may hold values from -1.25 to 1.25
- gate_matrix: float32 [2, 512, 512], P(None, None, 'feat'), may hold values from -0.25 to 0.25
- feature_vectors: float32 [2, 4, 512], P(None, None, 'feat'), may hold values from 0.1 to 1.9
- state_vectors: float32 [2, 3, 384], replicated, may hold values from -20 to 20, as said below
- velocity_input: float32 [2, 512, 768], P(None, 'feat'), may hold values from -6 to 6
- velocity_output: float32 [2, 1536, 512], P(None, None, 'feat'), may hold values from -6 to 6
- velocity_gate: float32 [2, 512, 512], P(None, None, 'feat'), may hold values from -6 to 6
- velocity_feature: float32 [2, 4, 512], P(None, None, 'feat'), may hold values from -6 to 6
- velocity_state: float32 [2, 3, 384], replicated, may hold values from -6 to 6
- average_input: float32 [2, 512, 768], P(None, 'feat'), may hold values from -0.25 to 0.25
- average_output: float32 [2, 1536, 512], P(None, None, 'feat'), may hold values from -1.25 to 1.25
- average_gate: float32 [2, 512, 512], P(None, None, 'feat'), may hold values from -0.25 to 0.25
- average_feature: float32 [2, 4, 512], P(None, None, 'feat'), may hold values from 0.1 to 1.9
- average_state: float32 [2, 3, 384], replicated, may hold values from -3 to 1
Outputs:
- activations_out: float32 [6144, 512], P('seq', 'feat')
- input_gradient: float32 [6144, 512], P('seq', 'feat')
- gradient_input: float32 [2, 512, 768], P(None, 'feat')
- gradient_output: float32 [2, 1536, 512], P(None, None, 'feat')
- gradient_gate: float32 [2, 512, 512], P(None, None, 'feat')
- gradient_feature: float32 [2, 4, 512], P(None, None, 'feat')
- gradient_state: float32 [2, 3, 384], replicated
- updated_input: float32 [2, 512, 768], P(None, 'feat')
- updated_output: float32 [2, 1536, 512], P(None, None, 'feat')
- updated_gate: float32 [2, 512, 512], P(None, None, 'feat')
- updated_feature: float32 [2, 4, 512], P(None, None, 'feat')
- state_change: float32 [2, 3, 384], replicated
- momentum_input: float32 [2, 512, 768], P(None, 'feat')
- momentum_output: float32 [2, 1536, 512], P(None, None, 'feat')
- momentum_gate: float32 [2, 512, 512], P(None, None, 'feat')
- momentum_feature: float32 [2, 4, 512], P(None, None, 'feat')
- momentum_state: float32 [2, 3, 384], replicated
- smoothed_input: float32 [2, 512, 768], P(None, 'feat')
- smoothed_output: float32 [2, 1536, 512], P(None, None, 'feat')
- smoothed_gate: float32 [2, 512, 512], P(None, None, 'feat')
- smoothed_feature: float32 [2, 4, 512], P(None, None, 'feat')
- smoothed_state: float32 [2, 3, 384], replicated
Inputs may be any that keep to these rules, and one draw needn't show every extreme that they name: `seq_length`: sequences of a device lie in its own buffer, ordered and without intersection; one device holds a single sequence of 768 tokens and an empty slot, every other device two sequences of 192 to 384 tokens. `seq_start`: positions within a device's buffer; a slot of length zero starts at 768. `state_vectors`: rows hold log(-Re Lambda), Im Lambda and the log timestep.
All inputs are finite; a program needn't handle non-finite values.
Results may differ from a plain program's by a relative error of at most 0.012.
The roundings to bfloat16 on the way count: a program that leaves them out, or rounds other values in their place, can miss the bound.
Values may be sent and summed in bfloat16 or wider, within the bound.
A program may use at most 448 MiB of HBM per device.

v0:
```python
import math

import jax
import jax.numpy as jnp
from jax import lax
from jax.sharding import PartitionSpec as P

epsilon = 1e-05
momentum = 0.9
smoothing = 0.5
slow_rate = 0.02
main_rate = 0.05
weight_decay = 0.1


def smooth(value):
    return jax.nn.gelu(value, approximate=False)


def combine(earlier, later):
    mult_real = later[0] * earlier[0] - later[1] * earlier[1]
    mult_imag = later[0] * earlier[1] + later[1] * earlier[0]
    add_real = later[0] * earlier[2] - later[1] * earlier[3] + later[2]
    add_imag = later[0] * earlier[3] + later[1] * earlier[2] + later[3]
    return (mult_real, mult_imag, add_real, add_imag)


def masks_of(starts, lengths, count):
    position = jnp.arange(count, dtype=jnp.int32)[:, None]
    begin = starts[None, :]
    finish = begin + lengths[None, :]
    inside = (position >= begin) & (position < finish)
    alive = jnp.any(inside, 1)
    opening = jnp.any(inside & (position == begin), 1)
    closing = jnp.any(inside & (position == finish - 1), 1)
    return (
        alive.astype(jnp.float32),
        (alive & ~opening).astype(jnp.float32),
        (alive & ~closing).astype(jnp.float32),
    )


def prefix(current, backward):
    length = current[2].shape[0]
    offset = 1
    while offset < length:

        def shifted(value):
            filler = jnp.zeros((offset,) + value.shape[1:], value.dtype)
            if backward:
                return jnp.concatenate([value[offset:], filler], 0)
            return jnp.concatenate([filler, value[: length - offset]], 0)

        earlier = tuple((shifted(value) for value in current))
        current = combine(earlier, current)
        offset = offset * 2
    return current


def scan_states(drive, state_row, alive, carry_prev, carry_next):
    width = state_row.shape[1]
    rate = -jnp.exp(state_row[0])
    frequency = state_row[1]
    timestep = jnp.exp(state_row[2])
    decay = jnp.exp(rate * timestep)
    angle = frequency * timestep
    pole_real = decay * jnp.cos(angle)
    pole_imag = decay * jnp.sin(angle)
    denom = rate * rate + frequency * frequency
    factor_real = ((pole_real - 1.0) * rate + pole_imag * frequency) / denom
    factor_imag = (pole_imag * rate - (pole_real - 1.0) * frequency) / denom
    drive_real = drive[:, :width]
    drive_imag = drive[:, width:]
    input_real = (drive_real * factor_real - drive_imag * factor_imag) * alive[:, None]
    input_imag = (drive_real * factor_imag + drive_imag * factor_real) * alive[:, None]
    ahead = prefix(
        (carry_prev[:, None] * pole_real, carry_prev[:, None] * pole_imag, input_real, input_imag),
        False,
    )
    behind = prefix(
        (carry_next[:, None] * pole_real, carry_next[:, None] * pole_imag, input_real, input_imag),
        True,
    )
    return jnp.concatenate([ahead[2], ahead[3], behind[2], behind[3]], 1)


def update(weight, gradient, velocity, average, rate, decay):
    adjusted = gradient + decay * weight
    velocity_new = momentum * velocity + adjusted
    change = -rate * (adjusted + momentum * velocity_new)
    weight_new = weight + change
    average_new = smoothing * average + (1.0 - smoothing) * weight_new
    return (weight_new, velocity_new, average_new, change)


def contract_rows(left, right):
    return lax.dot_general(
        left, right, (((0,), (0,)), ((), ())), preferred_element_type=jnp.float32
    )


def contract_cols(left, right):
    return lax.dot_general(
        left, right, (((1,), (1,)), ((), ())), preferred_element_type=jnp.float32
    )


def moments(stream):
    whole = lax.all_gather(stream, "feat", axis=1, tiled=True)
    center = jnp.mean(whole, 1, keepdims=True)
    spread = whole - center
    variance = jnp.mean(spread * spread, 1, keepdims=True)
    return (center, lax.rsqrt(variance + epsilon))


def back_moments(unit_grad, unit):
    spread_grad, crossed = (
        lax.all_gather(unit_grad, "feat", axis=1, tiled=True),
        lax.all_gather(unit_grad * unit, "feat", axis=1, tiled=True),
    )
    return (jnp.mean(spread_grad, 1, keepdims=True), jnp.mean(crossed, 1, keepdims=True))


def state_forward(normed_low, in_low, state_row, masks):
    partial_drive = jnp.dot(normed_low, in_low, preferred_element_type=jnp.float32)
    drive = lax.psum(partial_drive, "feat")
    states = scan_states(drive, state_row, masks[0], masks[1], masks[2])
    return (drive, states.astype(jnp.bfloat16))


def state_backward(drive, state_row, masks, mixed_low, out_low):

    def scanned(drive_in, rows_in):
        return scan_states(drive_in, rows_in, masks[0], masks[1], masks[2])

    partial_states = contract_cols(mixed_low, out_low)
    states_grad = lax.psum(partial_states, "feat")
    unused, pull = jax.vjp(scanned, drive, state_row)
    drive_grad, row_grad = pull(states_grad)
    return (drive_grad.astype(jnp.bfloat16), row_grad)


def body(
    activations_in,
    cotangent,
    seq_start,
    seq_length,
    input_matrix,
    output_matrix,
    gate_matrix,
    feature_vectors,
    state_vectors,
    velocity_input,
    velocity_output,
    velocity_gate,
    velocity_feature,
    velocity_state,
    average_input,
    average_output,
    average_gate,
    average_feature,
    average_state,
):
    count = activations_in.shape[0]
    layers = input_matrix.shape[0]
    masks = masks_of(seq_start, seq_length, count)
    stream = activations_in.astype(jnp.float32)
    saved = []
    for layer in range(layers):
        in_low = input_matrix[layer].astype(jnp.bfloat16)
        out_low = output_matrix[layer].astype(jnp.bfloat16)
        gate_low = gate_matrix[layer].astype(jnp.bfloat16)
        feature_row = feature_vectors[layer]
        center, scale = moments(stream)
        unit = (stream - center) * scale
        normed = unit * feature_row[0] + feature_row[1]
        normed_low = normed.astype(jnp.bfloat16)
        drive, states_low = state_forward(normed_low, in_low, state_vectors[layer], masks)
        mixed = (
            jnp.dot(states_low, out_low, preferred_element_type=jnp.float32)
            + feature_row[2] * normed
        )
        act = smooth(mixed)
        act_all = lax.all_gather(act.astype(jnp.bfloat16), "feat", axis=1, tiled=True)
        pre = jnp.dot(act_all, gate_low, preferred_element_type=jnp.float32) + feature_row[3]
        saved.append((scale, unit, normed, normed_low, drive, states_low, mixed, act, act_all, pre))
        stream = stream + act * jax.nn.sigmoid(pre)
    grad = cotangent.astype(jnp.float32) * masks[0][:, None]
    layer_grads = [None] * layers
    for layer in reversed(range(layers)):
        scale, unit, normed, normed_low, drive, states_low, mixed, act, act_all, pre = saved[layer]
        in_low = input_matrix[layer].astype(jnp.bfloat16)
        out_low = output_matrix[layer].astype(jnp.bfloat16)
        gate_low = gate_matrix[layer].astype(jnp.bfloat16)
        feature_row = feature_vectors[layer]
        gate = jax.nn.sigmoid(pre)
        pre_grad = (grad * act * gate * (1.0 - gate)).astype(jnp.bfloat16)
        gate_grad = contract_rows(act_all, pre_grad)
        gate_bias_grad = jnp.sum(pre_grad.astype(jnp.float32), 0)
        act_grad = grad * gate + lax.psum_scatter(
            contract_cols(pre_grad, gate_low), "feat", scatter_dimension=1, tiled=True
        )
        mixed_grad = jax.vjp(smooth, mixed)[1](act_grad)[0]
        skip_grad = jnp.sum(mixed_grad * normed, 0)
        mixed_low = mixed_grad.astype(jnp.bfloat16)
        out_grad = contract_rows(states_low, mixed_low)
        drive_low, row_grad = state_backward(drive, state_vectors[layer], masks, mixed_low, out_low)
        in_grad = contract_rows(normed_low, drive_low)
        normed_grad = mixed_grad * feature_row[2] + contract_cols(drive_low, in_low)
        gain_grad = jnp.sum(normed_grad * unit, 0)
        bias_grad = jnp.sum(normed_grad, 0)
        unit_grad = normed_grad * feature_row[0]
        first_mean, second_mean = back_moments(unit_grad, unit)
        grad = grad + scale * (unit_grad - first_mean - unit * second_mean)
        feature_grad = jnp.stack([gain_grad, bias_grad, skip_grad, gate_bias_grad])
        layer_grads[layer] = (in_grad, out_grad, gate_grad, feature_grad, row_grad)
    stacked_in = jnp.stack([entry[0] for entry in layer_grads])
    stacked_out = jnp.stack([entry[1] for entry in layer_grads])
    stacked_gate = jnp.stack([entry[2] for entry in layer_grads])
    stacked_feature = jnp.stack([entry[3] for entry in layer_grads])
    stacked_state = jnp.stack([entry[4] for entry in layer_grads])
    summed = lax.psum(
        (stacked_in, stacked_out, stacked_gate, stacked_feature, stacked_state), "seq"
    )
    factor = 1.0 / math.sqrt(count * lax.axis_size("seq"))
    grad_in = summed[0] * factor
    grad_out = summed[1] * factor
    grad_gate = summed[2] * factor
    grad_feature = summed[3] * factor
    grad_state = summed[4] * factor
    new_in = update(input_matrix, grad_in, velocity_input, average_input, slow_rate, 0.0)
    new_out = update(output_matrix, grad_out, velocity_output, average_output, slow_rate, 0.0)
    new_gate = update(gate_matrix, grad_gate, velocity_gate, average_gate, main_rate, weight_decay)
    new_feature = update(
        feature_vectors, grad_feature, velocity_feature, average_feature, main_rate, weight_decay
    )
    new_state = update(state_vectors, grad_state, velocity_state, average_state, slow_rate, 0.0)
    return (
        stream,
        grad,
        grad_in,
        grad_out,
        grad_gate,
        grad_feature,
        grad_state,
        new_in[0],
        new_out[0],
        new_gate[0],
        new_feature[0],
        new_state[3],
        new_in[1],
        new_out[1],
        new_gate[1],
        new_feature[1],
        new_state[1],
        new_in[2],
        new_out[2],
        new_gate[2],
        new_feature[2],
        new_state[2],
    )


def solution(mesh):
    return jax.shard_map(
        body,
        mesh=mesh,
        in_specs=(
            P("seq", "feat"),
            P("seq", "feat"),
            P("seq"),
            P("seq"),
            P(None, "feat", None),
            P(None, None, "feat"),
            P(None, None, "feat"),
            P(None, None, "feat"),
            P(),
            P(None, "feat", None),
            P(None, None, "feat"),
            P(None, None, "feat"),
            P(None, None, "feat"),
            P(),
            P(None, "feat", None),
            P(None, None, "feat"),
            P(None, None, "feat"),
            P(None, None, "feat"),
            P(),
        ),
        out_specs=(
            P("seq", "feat"),
            P("seq", "feat"),
            P(None, "feat", None),
            P(None, None, "feat"),
            P(None, None, "feat"),
            P(None, None, "feat"),
            P(),
            P(None, "feat", None),
            P(None, None, "feat"),
            P(None, None, "feat"),
            P(None, None, "feat"),
            P(),
            P(None, "feat", None),
            P(None, None, "feat"),
            P(None, None, "feat"),
            P(None, None, "feat"),
            P(),
            P(None, "feat", None),
            P(None, None, "feat"),
            P(None, None, "feat"),
            P(None, None, "feat"),
            P(),
        ),
        check_vma=False,
    )
```

profile of v0, /device:TPU:0, one launch (start us, length us, event | category | flops | bytes accessed | tf_op | source)
XLA Modules:
  0.0 1221.9 jit_solution(16966885579422786372)
XLA Ops:
  10.5 22.2 %all-gather.7.cloned.1.call-done = f32[768,512]{1,0:T(8,128)} async-done(((f32[768,128]{1,0:T(8,128)}), f32[768,512]{1,0:T(8,128)}) %all-gather.7.cloned.1.call-update) | async-done | bytes 1572880 | tf_op jit(solution)/shard_map/all_gather | solution.py:109
  43.4 52.2 %all-reduce.322.cloned.1.call-done = f32[768,768]{1,0:T(8,128)} async-done(((f32[768,768]{1,0:T(8,128)}), f32[768,768]{1,0:T(8,128)}) %all-reduce.322.cloned.1.call-update) | async-done | bytes 2359312 | tf_op jit(solution)/shard_map/psum | solution.py:126
  154.0 8.2 all_gather.25
  164.5 20.4 %all-gather.9.cloned.1.call-done = f32[768,512]{1,0:T(8,128)} async-done(((f32[768,128]{1,0:T(8,128)}), f32[768,512]{1,0:T(8,128)}) %all-gather.9.cloned.1.call-update) | async-done | bytes 1572880 | tf_op jit(solution)/shard_map/all_gather | solution.py:109
  192.1 55.7 %all-reduce.324.cloned.1.call-done = f32[768,768]{1,0:T(8,128)} async-done(((f32[768,768]{1,0:T(8,128)}), f32[768,768]{1,0:T(8,128)}) %all-reduce.324.cloned.1.call-update) | async-done | bytes 2359312 | tf_op jit(solution)/shard_map/psum | solution.py:126
  306.6 8.2 all_gather.27
  320.6 28.7 %reduce-scatter.3.cloned.1.call-done = f32[768,128]{1,0:T(8,128)} async-done(((f32[768,512]{1,0:T(8,128)}), f32[768,128]{1,0:T(8,128)}) %reduce-scatter.3.cloned.1.call-update) | async-done | bytes 393232 | tf_op jit(solution)/shard_map/reduce_scatter | solution.py:200
  352.7 3.9 fusion.341
  357.0 93.7 %all-reduce.326.cloned.1.call-done = f32[768,1536]{1,0:T(8,128)} async-done(((f32[768,1536]{1,0:T(8,128)}), f32[768,1536]{1,0:T(8,128)}) %all-reduce.326.cloned.1.call-update) | async-done | bytes 4718608 | tf_op jit(solution)/shard_map/psum | solution.py:137
  450.7 5.1 fusion.478
  461.6 5.8 fusion.447
  467.5 3.6 fusion.502
  494.3 4.0 fusion.445
  505.9 3.8 fusion.444
  517.5 4.0 fusion.432
  528.6 3.9 fusion.431
  540.6 3.4 fusion.443
  550.0 3.4 fusion.442
  561.7 3.8 fusion.430
  574.1 3.8 fusion.429
  585.8 4.0 fusion.441
  599.4 4.0 fusion.440
  611.3 3.9 fusion.439
  621.5 3.8 multiply_reduce_fusion.3
  628.9 3.4 fusion.428
  645.4 3.5 multiply_reduce_fusion.2
  659.3 19.4 %all-gather.13.cloned.1.call-done = f32[768,512]{1,0:T(8,128)} async-done(((f32[768,128]{1,0:T(8,128)}), f32[768,512]{1,0:T(8,128)}) %all-gather.13.cloned.1.call-update) | async-done | bytes 1572880 | tf_op jit(solution)/shard_map/all_gather | solution.py:119
  680.3 20.4 %all-gather.11.cloned.1.call-done = f32[768,512]{1,0:T(8,128)} async-done(((f32[768,128]{1,0:T(8,128)}), f32[768,512]{1,0:T(8,128)}) %all-gather.11.cloned.1.call-update) | async-done | bytes 1572880 | tf_op jit(solution)/shard_map/all_gather | solution.py:118
  707.4 28.3 %reduce-scatter.5.cloned.1.call-done = f32[768,128]{1,0:T(8,128)} async-done(((f32[768,512]{1,0:T(8,128)}), f32[768,128]{1,0:T(8,128)}) %reduce-scatter.5.cloned.1.call-update) | async-done | bytes 393232 | tf_op jit(solution)/shard_map/reduce_scatter | solution.py:200
  737.6 3.9 fusion.340
  741.7 94.0 %all-reduce.328.cloned.1.call-done = f32[768,1536]{1,0:T(8,128)} async-done(((f32[768,1536]{1,0:T(8,128)}), f32[768,1536]{1,0:T(8,128)}) %all-reduce.328.cloned.1.call-update) | async-done | bytes 4718608 | tf_op jit(solution)/shard_map/psum | solution.py:137
  835.6 4.8 fusion.477
  846.2 5.0 fusion.423
  851.2 3.6 fusion.486
  867.2 3.4 fusion.409
  885.2 3.4 fusion.420
  894.5 3.6 fusion.408
  904.4 4.1 fusion.407
  916.3 3.8 fusion.419
  927.9 3.8 fusion.418
  940.0 3.8 fusion.406
  952.4 3.9 fusion.405
  964.4 4.0 fusion.417
  978.0 4.0 fusion.416
  990.0 3.9 fusion.415
  1006.7 3.4 fusion.404
  1049.6 37.1 %all-reduce.314 = (f32[2,4,128]{2,1,0:T(4,128)S(1)}, f32[2,3,384]{2,1,0:T(4,128)S(1)}) all-reduce(f32[2,4,128]{2,1,0:T(4,128)S(1)} %pad_maximum_fusion.10, f32[2,3,384]{2,1,0:T(4,128)S(1)} %pad_maximum_fusion.9), channel_id=1, replica_groups=mesh['seq'=8,'feat'=4] {'seq'}, use_global_device_ids=true, to_apply=%region_28.0 | all-reduce | flops 3328 | bytes 26624 | tf_op jit(solution)/shard_map/psum | solution.py:222
  1095.2 110.1 %all-reduce.330.cloned.1.call-done = (f32[2,128,768]{2,1,0:T(8,128)}, f32[2,1536,128]{2,1,0:T(8,128)}, f32[2,512,128]{2,1,0:T(8,128)}) async-done(((f32[2,128,768]{2,1,0:T(8,128)}, f32[2,1536,128]{2,1,0:T(8,128)}, f32[2,512,128]{2,1,0:T(8,128)}), (f32[2,128,768]{2,1,0:T(8,128)}, f32[2,1536,128]{2,1,0:T(8,128)}, f32[2,512,128]{2,1,0:T(8,128)})) %all-reduce.330.cloned.1.call-update) | async-done | bytes 2883600 | tf_op jit(solution)/shard_map/psum | solution.py:222
  (1613 shorter events, 469.5 us)
Async XLA Ops:
  7.2 25.5 %all-gather.7.cloned.1.call-start = ((), (), s32[]{:S(2)}) async-start(), calls=%async_computation.2 | async-start | bytes 1966080 | tf_op jit(solution)/shard_map/all_gather | solution.py:109
  9.0 86.5 %all-reduce.322.cloned.1.call-start = ((), (), s32[]{:S(2)}) async-start(), calls=%async_computation.3 | async-start | bytes 4718592 | tf_op jit(solution)/shard_map/psum | solution.py:126
  39.8 145.2 %all-gather.9.cloned.1.call-start = ((), (), s32[]{:S(2)}) async-start(), calls=%async_computation.4 | async-start | bytes 1966080 | tf_op jit(solution)/shard_map/all_gather | solution.py:109
  43.4 54.2 %copy-start.553 = (f32[384]{0:T(512)}, f32[384]{0:T(512)S(1)}, u32[]{:S(2)}) copy-start(f32[384]{0:T(512)S(1)} %get-tuple-element.706) | copy-start | bytes 4612
  43.4 54.2 %copy-start.555 = (f32[384]{0:T(512)}, f32[384]{0:T(512)S(1)}, u32[]{:S(2)}) copy-start(f32[384]{0:T(512)S(1)} %get-tuple-element.707) | copy-start | bytes 4612
  100.3 27.4 %copy-start.16 = (f32[768,384]{1,0:T(8,128)}, f32[768,384]{1,0:T(8,128)S(1)}, u32[]{:S(2)}) copy-start(f32[768,384]{1,0:T(8,128)S(1)} %get-tuple-element.600) | copy-start | bytes 3538948
  100.3 27.4 %copy-start.20 = (f32[768,384]{1,0:T(8,128)}, f32[768,384]{1,0:T(8,128)S(1)}, u32[]{:S(2)}) copy-start(f32[768,384]{1,0:T(8,128)S(1)} %get-tuple-element.599) | copy-start | bytes 3538948
  106.2 21.8 %copy-start = (f32[768,384]{1,0:T(8,128)}, f32[768,384]{1,0:T(8,128)S(1)}, u32[]{:S(2)}) copy-start(f32[768,384]{1,0:T(8,128)S(1)} %get-tuple-element.376) | copy-start | bytes 3538948
  106.2 21.8 %copy-start.2 = (f32[768,384]{1,0:T(8,128)}, f32[768,384]{1,0:T(8,128)S(1)}, u32[]{:S(2)}) copy-start(f32[768,384]{1,0:T(8,128)S(1)} %get-tuple-element.377) | copy-start | bytes 3538948
  106.2 22.6 %copy-start.24 = (f32[768,384]{1,0:T(8,128)}, f32[768,384]{1,0:T(8,128)S(1)}, u32[]{:S(2)}) copy-start(f32[768,384]{1,0:T(8,128)S(1)} %get-tuple-element.375) | copy-start | bytes 3538948
  125.4 19.5 %copy-start.148 = (f32[768,384]{1,0:T(8,128)}, f32[768,384]{1,0:T(8,128)S(1)}, u32[]{:S(2)}) copy-start(f32[768,384]{1,0:T(8,128)S(1)} %get-tuple-element.382) | copy-start | bytes 3538948
  125.4 19.5 %copy-start.150 = (f32[768,384]{1,0:T(8,128)}, f32[768,384]{1,0:T(8,128)S(1)}, u32[]{:S(2)}) copy-start(f32[768,384]{1,0:T(8,128)S(1)} %get-tuple-element.383) | copy-start | bytes 3538948
  164.5 83.3 %all-reduce.324.cloned.1.call-start = ((), (), s32[]{:S(2)}) async-start(), calls=%async_computation.5 | async-start | bytes 4718592 | tf_op jit(solution)/shard_map/psum | solution.py:126
  192.0 157.3 %reduce-scatter.3.cloned.1.call-start = ((), (), s32[]{:S(2)}) async-start(), calls=%async_computation.6 | async-start | bytes 1966080 | tf_op jit(solution)/shard_map/reduce_scatter | solution.py:200
  192.1 57.7 %copy-start.557 = (f32[384]{0:T(512)}, f32[384]{0:T(512)S(1)}, u32[]{:S(2)}) copy-start(f32[384]{0:T(512)S(1)} %get-tuple-element.700) | copy-start | bytes 4612
  192.1 57.7 %copy-start.559 = (f32[384]{0:T(512)}, f32[384]{0:T(512)S(1)}, u32[]{:S(2)}) copy-start(f32[384]{0:T(512)S(1)} %get-tuple-element.701) | copy-start | bytes 4612
  253.7 27.1 %copy-start.18 = (f32[768,384]{1,0:T(8,128)}, f32[768,384]{1,0:T(8,128)S(1)}, u32[]{:S(2)}) copy-start(f32[768,384]{1,0:T(8,128)S(1)} %get-tuple-element.602) | copy-start | bytes 3538948
  253.7 27.1 %copy-start.22 = (f32[768,384]{1,0:T(8,128)}, f32[768,384]{1,0:T(8,128)S(1)}, u32[]{:S(2)}) copy-start(f32[768,384]{1,0:T(8,128)S(1)} %get-tuple-element.601) | copy-start | bytes 3538948
  259.6 21.5 %copy-start.4 = (f32[768,384]{1,0:T(8,128)}, f32[768,384]{1,0:T(8,128)S(1)}, u32[]{:S(2)}) copy-start(f32[768,384]{1,0:T(8,128)S(1)} %get-tuple-element.320) | copy-start | bytes 3538948
  259.6 21.5 %copy-start.6 = (f32[768,384]{1,0:T(8,128)}, f32[768,384]{1,0:T(8,128)S(1)}, u32[]{:S(2)}) copy-start(f32[768,384]{1,0:T(8,128)S(1)} %get-tuple-element.321) | copy-start | bytes 3538948
  259.6 22.4 %copy-start.30 = (f32[768,384]{1,0:T(8,128)}, f32[768,384]{1,0:T(8,128)S(1)}, u32[]{:S(2)}) copy-start(f32[768,384]{1,0:T(8,128)S(1)} %get-tuple-element.319) | copy-start | bytes 3538948
  278.5 19.5 %copy-start.156 = (f32[768,384]{1,0:T(8,128)}, f32[768,384]{1,0:T(8,128)S(1)}, u32[]{:S(2)}) copy-start(f32[768,384]{1,0:T(8,128)S(1)} %get-tuple-element.326) | copy-start | bytes 3538948
  278.5 19.5 %copy-start.158 = (f32[768,384]{1,0:T(8,128)}, f32[768,384]{1,0:T(8,128)S(1)}, u32[]{:S(2)}) copy-start(f32[768,384]{1,0:T(8,128)S(1)} %get-tuple-element.327) | copy-start | bytes 3538948
  320.5 130.2 %all-reduce.326.cloned.1.call-start = ((), (), s32[]{:S(2)}) async-start(), calls=%async_computation.7 | async-start | bytes 9437184 | tf_op jit(solution)/shard_map/psum | solution.py:137
  356.6 322.1 %all-gather.13.cloned.1.call-start = ((), (), s32[]{:S(2)}) async-start(), calls=%async_computation.9 | async-start | bytes 1966080 | tf_op jit(solution)/shard_map/all_gather | solution.py:119
  471.1 18.4 %copy-start.349 = (f32[768,384]{1,0:T(8,128)}, f32[768,384]{1,0:T(8,128)S(1)}, u32[]{:S(2)}) copy-start(f32[768,384]{1,0:T(8,128)S(1)} %get-tuple-element.654) | copy-start | bytes 3538948
  658.5 42.2 %all-gather.11.cloned.1.call-start = ((), (), s32[]{:S(2)}) async-start(), calls=%async_computation.8 | async-start | bytes 1966080 | tf_op jit(solution)/shard_map/all_gather | solution.py:118
  659.2 76.4 %reduce-scatter.5.cloned.1.call-start = ((), (), s32[]{:S(2)}) async-start(), calls=%async_computation.10 | async-start | bytes 1966080 | tf_op jit(solution)/shard_map/reduce_scatter | solution.py:200
  678.6 23.7 %copy-start.530 = (bf16[768,128]{1,0:T(8,128)(2,1)S(1)}, bf16[768,128]{1,0:T(8,128)(2,1)}, u32[]{:S(2)}) copy-start(bf16[768,128]{1,0:T(8,128)(2,1)} %param.20) | copy-start | bytes 589828
  680.3 22.1 %copy-start.497 = (f32[768,128]{1,0:T(8,128)S(1)}, f32[768,128]{1,0:T(8,128)}, u32[]{:S(2)}) copy-start(f32[768,128]{1,0:T(8,128)} %get-tuple-element.682) | copy-start | bytes 1179652
  680.3 22.1 %copy-start.522 = (f32[768,128]{1,0:T(8,128)S(1)}, f32[768,128]{1,0:T(8,128)}, u32[]{:S(2)}) copy-start(f32[768,128]{1,0:T(8,128)} %copy-done.521) | copy-start | bytes 1179652
  680.3 22.1 %copy-start.524 = (f32[768,128]{1,0:T(8,128)S(1)}, f32[768,128]{1,0:T(8,128)}, u32[]{:S(2)}) copy-start(f32[768,128]{1,0:T(8,128)} %copy-done.523) | copy-start | bytes 1179652
  680.3 22.1 %copy-start.525 = (f32[768,128]{1,0:T(8,128)S(1)}, f32[768,128]{1,0:T(8,128)}, u32[]{:S(2)}) copy-start(f32[768,128]{1,0:T(8,128)} %get-tuple-element.727) | copy-start | bytes 1179652
  704.2 31.4 %copy-start.498 = (f32[768,128]{1,0:T(8,128)}, f32[768,128]{1,0:T(8,128)S(1)}, u32[]{:S(2)}) copy-start(f32[768,128]{1,0:T(8,128)S(1)} %get-tuple-element.286) | copy-start | bytes 1179652
  707.3 128.3 %all-reduce.328.cloned.1.call-start = ((), (), s32[]{:S(2)}) async-start(), calls=%async_computation.11 | async-start | bytes 9437184 | tf_op jit(solution)/shard_map/psum | solution.py:137
  741.4 94.2 %copy-start.450 = (f32[256,384]{1,0:T(8,128)S(1)}, f32[256,384]{1,0:T(8,128)}, u32[]{:S(2)}) copy-start(f32[256,384]{1,0:T(8,128)} %copy-done.449) | copy-start | bytes 1179652
  741.4 94.2 %copy-start.452 = (f32[256,384]{1,0:T(8,128)S(1)}, f32[256,384]{1,0:T(8,128)}, u32[]{:S(2)}) copy-start(f32[256,384]{1,0:T(8,128)} %copy-done.451) | copy-start | bytes 1179652
  741.5 348.3 %all-gather.17.cloned.1.call-start = ((), (), s32[]{:S(2)}) async-start(), calls=%async_computation.13 | async-start | bytes 1966080 | tf_op jit(solution)/shard_map/all_gather | solution.py:119
  1035.6 55.9 %all-gather.15.cloned.1.call-start = ((), (), s32[]{:S(2)}) async-start(), calls=%async_computation.12 | async-start | bytes 1966080 | tf_op jit(solution)/shard_map/all_gather | solution.py:118
  1036.2 169.1 %all-reduce.330.cloned.1.call-start = ((), (), s32[]{:S(2)}) async-start(), calls=%async_computation.14 | async-start | bytes 5767168 | tf_op jit(solution)/shard_map/psum | solution.py:222
  1048.3 38.4 %copy-start.563 = (f32[2,3,384]{2,0,1:T(2,128)S(1)}, f32[2,3,384]{2,0,1:T(2,128)}, u32[]{:S(2)}) copy-start(f32[2,3,384]{2,0,1:T(2,128)} %param.37) | copy-start | bytes 27652
  1048.3 38.4 %copy-start.564 = (f32[2,3,384]{2,0,1:T(2,128)S(1)}, f32[2,3,384]{2,0,1:T(2,128)}, u32[]{:S(2)}) copy-start(f32[2,3,384]{2,0,1:T(2,128)} %param.32) | copy-start | bytes 27652
  1048.3 40.8 %copy-start.562 = (f32[2,4,128]{2,1,0:T(4,128)S(1)}, f32[2,4,128]{2,1,0:T(4,128)}, u32[]{:S(2)}) copy-start(f32[2,4,128]{2,1,0:T(4,128)} %param.26) | copy-start | bytes 12292
  1048.3 40.8 %copy-start.577 = (f32[2,4,128]{2,1,0:T(4,128)S(1)}, f32[2,4,128]{2,1,0:T(4,128)}, u32[]{:S(2)}) copy-start(f32[2,4,128]{2,1,0:T(4,128)} %param.36) | copy-start | bytes 12292
  1048.3 40.8 %copy-start.578 = (f32[2,4,128]{2,1,0:T(4,128)S(1)}, f32[2,4,128]{2,1,0:T(4,128)}, u32[]{:S(2)}) copy-start(f32[2,4,128]{2,1,0:T(4,128)} %param.31) | copy-start | bytes 12292
  1091.4 113.9 %copy-start.515 = (f32[2,512,128]{2,1,0:T(8,128)S(1)}, f32[2,512,128]{2,1,0:T(8,128)}, u32[]{:S(2)}) copy-start(f32[2,512,128]{2,1,0:T(8,128)} %param.25) | copy-start | bytes 1572868
  1091.4 113.9 %copy-start.547 = (f32[2,512,128]{2,1,0:T(8,128)S(1)}, f32[2,512,128]{2,1,0:T(8,128)}, u32[]{:S(2)}) copy-start(f32[2,512,128]{2,1,0:T(8,128)} %param.35) | copy-start | bytes 1572868
  1091.4 113.9 %copy-start.548 = (f32[2,512,128]{2,1,0:T(8,128)S(1)}, f32[2,512,128]{2,1,0:T(8,128)}, u32[]{:S(2)}) copy-start(f32[2,512,128]{2,1,0:T(8,128)} %param.30) | copy-start | bytes 1572868
  (557 other events, 1209.4 us)
Sparse Core Ops, SparseCore 0:
  10.2 22.5 all-gather.6
  39.9 55.6 all-reduce.321
  164.6 20.3 all-gather.8
  192.1 55.6 all-reduce.323
  320.7 28.6 reduce-scatter.2
  356.7 94.0 all-reduce.325
  658.6 19.9 all-gather.12
  680.8 19.8 all-gather.10
  707.4 28.1 reduce-scatter.4
  741.6 94.0 all-reduce.327
  1035.7 19.9 all-gather.16
  1057.7 19.8 all-gather.14
  1082.1 123.1 all-reduce.329
where the time goes:
time: 1230 us; the launch traced here: 1220 us
  waiting for transfers between devices  547 us (44%)
  other arithmetic  391 us (32%)
  local copies, waits for them, and re-layouts  167 us (14%)
  blocking collectives  53.4 us (4%)
  matrix products  42.7 us (3%)
  between operations  20.2 us (2%)
    psum x2, waiting for transfers between devices, state_backward(): states_grad = lax.psum(partial_states, 'feat')  188 us
    unnamed x1188, local copies, waits for them, and re-layouts  153 us
    neg x32, other arithmetic, combine(): mult_real = later[0] * earlier[0] - later[1] * earlier[1]  115 us
    psum x1, waiting for transfers between devices, body(): lax.psum((stacked_in, stacked_out, stacked_gate, stacked_feature, stacked...  110 us
    psum x2, waiting for transfers between devices, state_forward(): drive = lax.psum(partial_drive, 'feat')  108 us
    add_any x40, other arithmetic, combine(): add_real = later[0] * earlier[2] - later[1] * earlier[3] + later[2]  59.8 us
    neg x36, other arithmetic, combine(): add_real = later[0] * earlier[2] - later[1] * earlier[3] + later[2]  58.3 us
    reduce_scatter x2, waiting for transfers between devices, body(): lax.psum_scatter(contract_cols(pre_grad, gate_low), 'feat', scatter_dimen...  57 us
  transfers between devices with their start and end apart: 13, of which 11 were waited for; matrix products, arithmetic and copies ran while one was open for 2% of the time, Pallas kernels for 0%

commit v1 on v0

v1 whole, which is shorter than its diff:
```python
import math

import jax
import jax.numpy as jnp
from jax import lax
from jax.experimental import pallas as pl
from jax.experimental.pallas import tpu as pltpu
from jax.sharding import PartitionSpec as P

epsilon = 1e-05
momentum = 0.9
smoothing = 0.5
slow_rate = 0.02
main_rate = 0.05
weight_decay = 0.1


def smooth(value):
    return jax.nn.gelu(value, approximate=False)


def masks_of(starts, lengths, count):
    position = jnp.arange(count, dtype=jnp.int32)[:, None]
    begin = starts[None, :]
    finish = begin + lengths[None, :]
    inside = (position >= begin) & (position < finish)
    alive = jnp.any(inside, 1)
    opening = jnp.any(inside & (position == begin), 1)
    closing = jnp.any(inside & (position == finish - 1), 1)
    return (
        alive.astype(jnp.float32),
        (alive & ~opening).astype(jnp.float32),
        (alive & ~closing).astype(jnp.float32),
    )


def coefficients(state_row):
    rate = -jnp.exp(state_row[0])
    frequency = state_row[1]
    timestep = jnp.exp(state_row[2])
    decay = jnp.exp(rate * timestep)
    angle = frequency * timestep
    pole_real = decay * jnp.cos(angle)
    pole_imag = decay * jnp.sin(angle)
    denom = rate * rate + frequency * frequency
    factor_real = ((pole_real - 1.0) * rate + pole_imag * frequency) / denom
    factor_imag = (pole_imag * rate - (pole_real - 1.0) * frequency) / denom
    return (pole_real, pole_imag, factor_real, factor_imag)


def recurrence_kernel(ma_ref, mb_ref, w_ref, xa_ref, xb_ref, out_ref):
    count = xa_ref.shape[0]
    width = w_ref.shape[1]
    w_re = w_ref[0:1, :]
    w_im = w_ref[1:2, :]

    def advance(h_re, h_im, keep, x_ref, row):
        h_re = h_re * keep
        h_im = h_im * keep
        new_re = w_re * h_re - w_im * h_im + x_ref[pl.ds(row, 1), pl.ds(0, width)]
        new_im = w_re * h_im + w_im * h_re + x_ref[pl.ds(row, 1), pl.ds(width, width)]
        return new_re, new_im

    def step(i, carry):
        a_re, a_im, b_re, b_im = carry
        up = i
        down = count - 1 - i
        a_re, a_im = advance(a_re, a_im, ma_ref[up], xa_ref, up)
        b_re, b_im = advance(b_re, b_im, mb_ref[down], xb_ref, down)
        out_ref[pl.ds(up, 1), pl.ds(0, width)] = a_re
        out_ref[pl.ds(up, 1), pl.ds(width, width)] = a_im
        out_ref[pl.ds(down, 1), pl.ds(2 * width, width)] = b_re
        out_ref[pl.ds(down, 1), pl.ds(3 * width, width)] = b_im
        return (a_re, a_im, b_re, b_im)

    zeros = jnp.zeros((1, width), jnp.float32)
    lax.fori_loop(0, count, step, (zeros, zeros, zeros, zeros), unroll=8)


def recurrence(ma, mb, w, xa, xb):
    count, double = xa.shape
    return pl.pallas_call(
        recurrence_kernel,
        out_shape=jax.ShapeDtypeStruct((count, 2 * double), jnp.float32),
        in_specs=[
            pl.BlockSpec(memory_space=pltpu.SMEM),
            pl.BlockSpec(memory_space=pltpu.SMEM),
            pl.BlockSpec(memory_space=pltpu.VMEM),
            pl.BlockSpec(memory_space=pltpu.VMEM),
            pl.BlockSpec(memory_space=pltpu.VMEM),
        ],
        out_specs=pl.BlockSpec(memory_space=pltpu.VMEM),
        cost_estimate=pl.CostEstimate(
            flops=20 * count * double, transcendentals=0, bytes_accessed=16 * count * double
        ),
    )(ma, mb, w, xa, xb)


def update(weight, gradient, velocity, average, rate, decay):
    adjusted = gradient + decay * weight
    velocity_new = momentum * velocity + adjusted
    change = -rate * (adjusted + momentum * velocity_new)
    weight_new = weight + change
    average_new = smoothing * average + (1.0 - smoothing) * weight_new
    return (weight_new, velocity_new, average_new, change)


def contract_rows(left, right):
    return lax.dot_general(
        left, right, (((0,), (0,)), ((), ())), preferred_element_type=jnp.float32
    )


def contract_cols(left, right):
    return lax.dot_general(
        left, right, (((1,), (1,)), ((), ())), preferred_element_type=jnp.float32
    )


def gather_feat(value, axis):
    return lax.all_gather(value, "feat", axis=axis, tiled=True)


def body(
    activations_in,
    cotangent,
    seq_start,
    seq_length,
    input_matrix,
    output_matrix,
    gate_matrix,
    feature_vectors,
    state_vectors,
    velocity_input,
    velocity_output,
    velocity_gate,
    velocity_feature,
    velocity_state,
    average_input,
    average_output,
    average_gate,
    average_feature,
    average_state,
):
    count = activations_in.shape[0]
    shard = activations_in.shape[1]
    layers = input_matrix.shape[0]
    width = state_vectors.shape[2]
    me = lax.axis_index("feat")
    offset = me * shard

    def mine(value):
        return lax.dynamic_slice_in_dim(value, offset, shard, axis=value.ndim - 1)

    alive, carry_prev, carry_next = masks_of(seq_start, seq_length, count)
    zero = jnp.zeros((1,), jnp.float32)
    after_next = jnp.concatenate([zero, carry_next[:-1]])
    before_prev = jnp.concatenate([carry_prev[1:], zero])

    in_all = gather_feat(input_matrix.astype(jnp.bfloat16), 1)
    out_all = gather_feat(output_matrix.astype(jnp.bfloat16), 2)
    gate_all = gather_feat(gate_matrix.astype(jnp.bfloat16), 2)
    feature_all = gather_feat(feature_vectors, 2)
    stream = gather_feat(activations_in, 1).astype(jnp.float32)

    saved = []
    for layer in range(layers):
        in_low = in_all[layer]
        out_low = out_all[layer]
        gate_low = gate_all[layer]
        feature_row = feature_all[layer]
        pole_re, pole_im, factor_re, factor_im = coefficients(state_vectors[layer])
        center = jnp.mean(stream, 1, keepdims=True)
        spread = stream - center
        scale = lax.rsqrt(jnp.mean(spread * spread, 1, keepdims=True) + epsilon)
        unit = spread * scale
        normed = unit * feature_row[0] + feature_row[1]
        normed_low = normed.astype(jnp.bfloat16)
        drive = jnp.dot(normed_low, in_low, preferred_element_type=jnp.float32)
        drive_re = drive[:, :width]
        drive_im = drive[:, width:]
        source = jnp.concatenate(
            [
                (drive_re * factor_re - drive_im * factor_im) * alive[:, None],
                (drive_re * factor_im + drive_im * factor_re) * alive[:, None],
            ],
            1,
        )
        poles = jnp.stack([pole_re, pole_im])
        states = recurrence(carry_prev, carry_next, poles, source, source)
        states_low = states.astype(jnp.bfloat16)
        mixed = (
            jnp.dot(states_low, out_low, preferred_element_type=jnp.float32)
            + feature_row[2] * normed
        )
        act = smooth(mixed)
        act_low = act.astype(jnp.bfloat16)
        pre = jnp.dot(act_low, gate_low, preferred_element_type=jnp.float32) + feature_row[3]
        saved.append((scale, unit, normed_low, drive, states, states_low, mixed, act, act_low, pre))
        stream = stream + act * jax.nn.sigmoid(pre)

    grad = gather_feat(cotangent, 1).astype(jnp.float32) * alive[:, None]
    layer_grads = [None] * layers
    for layer in reversed(range(layers)):
        scale, unit, normed_low, drive, states, states_low, mixed, act, act_low, pre = saved[layer]
        in_low = in_all[layer]
        out_low = out_all[layer]
        gate_low = gate_all[layer]
        feature_row = feature_all[layer]
        state_row = state_vectors[layer]
        pole_re, pole_im, factor_re, factor_im = coefficients(state_row)
        gate = jax.nn.sigmoid(pre)
        pre_grad = (grad * act * gate * (1.0 - gate)).astype(jnp.bfloat16)
        gate_grad = contract_rows(act_low, mine(pre_grad))
        gate_bias_grad = jnp.sum(pre_grad.astype(jnp.float32), 0)
        act_grad = grad * gate + contract_cols(pre_grad, gate_low)
        mixed_grad = jax.vjp(smooth, mixed)[1](act_grad)[0]
        normed = unit * feature_row[0] + feature_row[1]
        skip_grad = jnp.sum(mixed_grad * normed, 0)
        mixed_low = mixed_grad.astype(jnp.bfloat16)
        out_grad = contract_rows(states_low, mine(mixed_low))
        states_grad = contract_cols(mixed_low, out_low)
        conj = jnp.stack([pole_re, -pole_im])
        lambdas = recurrence(
            after_next, before_prev, conj, states_grad[:, 2 * width :], states_grad[:, : 2 * width]
        )
        lb_re = lambdas[:, :width]
        lb_im = lambdas[:, width : 2 * width]
        la_re = lambdas[:, 2 * width : 3 * width]
        la_im = lambdas[:, 3 * width :]
        gu_re = la_re + lb_re
        gu_im = la_im + lb_im
        live = alive[:, None]
        dg_re = (factor_re * gu_re + factor_im * gu_im) * live
        dg_im = (factor_re * gu_im - factor_im * gu_re) * live
        drive_low = jnp.concatenate([dg_re, dg_im], 1).astype(jnp.bfloat16)
        d_re = drive[:, :width] * live
        d_im = drive[:, width:] * live
        gf_re = jnp.sum(d_re * gu_re + d_im * gu_im, 0)
        gf_im = jnp.sum(d_re * gu_im - d_im * gu_re, 0)
        zero_row = jnp.zeros((1, width), jnp.float32)
        a_re = jnp.concatenate([zero_row, states[:-1, :width]], 0) * carry_prev[:, None]
        a_im = jnp.concatenate([zero_row, states[:-1, width : 2 * width]], 0) * carry_prev[:, None]
        b_re = jnp.concatenate([states[1:, 2 * width : 3 * width], zero_row], 0) * carry_next[:, None]
        b_im = jnp.concatenate([states[1:, 3 * width :], zero_row], 0) * carry_next[:, None]
        gp_re = jnp.sum(a_re * la_re + a_im * la_im + b_re * lb_re + b_im * lb_im, 0)
        gp_im = jnp.sum(a_re * la_im - a_im * la_re + b_re * lb_im - b_im * lb_re, 0)
        row_grad = jax.vjp(coefficients, state_row)[1]((gp_re, gp_im, gf_re, gf_im))[0]
        in_grad = contract_rows(mine(normed_low), drive_low)
        normed_grad = mixed_grad * feature_row[2] + jnp.dot(
            drive_low, in_low.T, preferred_element_type=jnp.float32
        )
        gain_grad = jnp.sum(normed_grad * unit, 0)
        bias_grad = jnp.sum(normed_grad, 0)
        unit_grad = normed_grad * feature_row[0]
        first_mean = jnp.mean(unit_grad, 1, keepdims=True)
        second_mean = jnp.mean(unit_grad * unit, 1, keepdims=True)
        grad = grad + scale * (unit_grad - first_mean - unit * second_mean)
        feature_grad = mine(jnp.stack([gain_grad, bias_grad, skip_grad, gate_bias_grad]))
        layer_grads[layer] = (in_grad, out_grad, gate_grad, feature_grad, row_grad)
    stacked_in = jnp.stack([entry[0] for entry in layer_grads])
    stacked_out = jnp.stack([entry[1] for entry in layer_grads])
    stacked_gate = jnp.stack([entry[2] for entry in layer_grads])
    stacked_feature = jnp.stack([entry[3] for entry in layer_grads])
    stacked_state = jnp.stack([entry[4] for entry in layer_grads])
    summed = lax.psum(
        (stacked_in, stacked_out, stacked_gate, stacked_feature, stacked_state), "seq"
    )
    factor = 1.0 / math.sqrt(count * lax.axis_size("seq"))
    grad_in = summed[0] * factor
    grad_out = summed[1] * factor
    grad_gate = summed[2] * factor
    grad_feature = summed[3] * factor
    grad_state = summed[4] * factor
    new_in = update(input_matrix, grad_in, velocity_input, average_input, slow_rate, 0.0)
    new_out = update(output_matrix, grad_out, velocity_output, average_output, slow_rate, 0.0)
    new_gate = update(gate_matrix, grad_gate, velocity_gate, average_gate, main_rate, weight_decay)
    new_feature = update(
        feature_vectors, grad_feature, velocity_feature, average_feature, main_rate, weight_decay
    )
    new_state = update(state_vectors, grad_state, velocity_state, average_state, slow_rate, 0.0)
    return (
        mine(stream),
        mine(grad),
        grad_in,
        grad_out,
        grad_gate,
        grad_feature,
        grad_state,
        new_in[0],
        new_out[0],
        new_gate[0],
        new_feature[0],
        new_state[3],
        new_in[1],
        new_out[1],
        new_gate[1],
        new_feature[1],
        new_state[1],
        new_in[2],
        new_out[2],
        new_gate[2],
        new_feature[2],
        new_state[2],
    )


def solution(mesh):
    feat = P(None, None, "feat")
    rows = P(None, "feat", None)
    tokens = P("seq", "feat")
    return jax.shard_map(
        body,
        mesh=mesh,
        in_specs=(
            tokens,
            tokens,
            P("seq"),
            P("seq"),
            rows,
            feat,
            feat,
            feat,
            P(),
            rows,
            feat,
            feat,
            feat,
            P(),
            rows,
            feat,
            feat,
            feat,
            P(),
        ),
        out_specs=(
            tokens,
            tokens,
            rows,
            feat,
            feat,
            feat,
            P(),
            rows,
            feat,
            feat,
            feat,
            P(),
            rows,
            feat,
            feat,
            feat,
            P(),
            rows,
            feat,
            feat,
            feat,
            P(),
        ),
        check_vma=False,
    )
```

time: 1230 us -> 319 us (0.26)
  waiting for transfers between devices: 547 us -> 83.3 us
  other arithmetic: 391 us -> 44.1 us
  local copies, waits for them, and re-layouts: 167 us -> 28.9 us
  Pallas kernels: 0 us -> 39.9 us
    psum x4 -> x0, waiting for transfers between devices: 296 us -> none  [the longest x2 188 us: state_backward(): states_grad = lax.psum(partial_states, 'feat')]
    neg x68 -> x1, other arithmetic: 173 us -> 0.11 us  [body(): conj = jnp.stack([pole_re, -pole_im])]
    unnamed x1188 -> x130, local copies, waits for them, and re-layouts: 153 us -> 14 us
    add_any x90 -> x2, other arithmetic: 108 us -> 0.18 us  [coefficients(): angle = frequency * timestep]
    all_gather x6 -> x3, waiting for transfers between devices: 82.4 us -> 15.7 us  [gather_feat(): return lax.all_gather(value, 'feat', axis=axis, tiled=True)]
    reduce_scatter x2 -> x0, waiting for transfers between devices: 57 us -> none  [body(): lax.psum_scatter(contract_cols(pre_grad, gate_low), 'feat', scatter_dimen...]
    psum x1, waiting for transfers between devices: 110 us -> 67.5 us  [body(): lax.psum((stacked_in, stacked_out, stacked_gate, stacked_feature, stacked...]
    pallas_call x0 -> x4, Pallas kernels: none -> 39.9 us  [recurrence(): pl.pallas_call(recurrence_kernel, out_shape=jax.ShapeDtypeStruct((count,...]
  transfers between devices with their start and end apart: 13 -> 4, of which waited for: 11 -> 3; matrix products, arithmetic and copies ran while one was open for 2% -> 12% of each run, Pallas kernels for 0% -> 3%
where the time goes in v1:
time: 319 us
  waiting for transfers between devices  83.3 us (26%)
  blocking collectives  63.5 us (20%)
  matrix products  44.5 us (14%)
  other arithmetic  44.1 us (14%)
  Pallas kernels  39.9 us (13%)
  local copies, waits for them, and re-layouts  28.9 us (9%)
  between operations  14.4 us (5%)
    psum x1, waiting for transfers between devices, body(): lax.psum((stacked_in, stacked_out, stacked_gate, stacked_feature, stacked...  67.5 us
    pallas_call x4, Pallas kernels, recurrence(): pl.pallas_call(recurrence_kernel, out_shape=jax.ShapeDtypeStruct((count,...  39.9 us
    psum x1, blocking collectives, body(): lax.psum((stacked_in, stacked_out, stacked_gate, stacked_feature, stacked...  38.9 us
    all_gather x3, blocking collectives, gather_feat(): return lax.all_gather(value, 'feat', axis=axis, tiled=True)  24.6 us
    all_gather x3, waiting for transfers between devices, gather_feat(): return lax.all_gather(value, 'feat', axis=axis, tiled=True)  15.7 us
    unnamed x130, local copies, waits for them, and re-layouts  14 us
    dot_general x2, matrix products, body(): jnp.dot(states_low, out_low, preferred_element_type=jnp.float32)  13.3 us
    dot_general x4, matrix products, contract_cols(): lax.dot_general(left, right, (((1,), (1,)), ((), ())), preferred_element_...  10.2 us
  transfers between devices with their start and end apart: 4, of which 3 were waited for; matrix products, arithmetic and copies ran while one was open for 12% of the time, Pallas kernels for 3%

profile of v1, /device:TPU:0, one launch (start us, length us, event | category | flops | bytes accessed | tf_op | source)
XLA Modules:
  0.0 318.8 jit_solution(5194755036814497017)
XLA Ops:
  7.2 2.0 convert_element_type.70
  11.5 10.0 %all_gather.18 = bf16[768,512]{1,0:T(8,128)(2,1)S(1)} all-gather(bf16[768,128]{1,0:T(8,128)(2,1)S(1)} %copy-done.44), channel_id=1, replica_groups=mesh['seq'=8,'feat'=4] {'feat'}, dimensions={1}, use_global_device_ids=true | all-gather | bytes 983040 | tf_op jit(solution)/shard_map/all_gather | solution.py:121
  22.2 5.2 %all_gather.19 = f32[2,4,512]{2,1,0:T(4,128)S(1)} all-gather(f32[2,4,128]{2,1,0:T(4,128)S(1)} %copy-done.50), channel_id=1, replica_groups=mesh['seq'=8,'feat'=4] {'feat'}, dimensions={2}, use_global_device_ids=true | all-gather | bytes 20480 | tf_op jit(solution)/shard_map/all_gather | solution.py:121
  27.4 9.3 %all_gather.23 = bf16[768,512]{1,0:T(8,128)(2,1)} all-gather(bf16[768,128]{1,0:T(8,128)(2,1)S(1)} %copy-done.45), channel_id=1, replica_groups=mesh['seq'=8,'feat'=4] {'feat'}, dimensions={1}, use_global_device_ids=true | all-gather | bytes 983040 | tf_op jit(solution)/shard_map/all_gather | solution.py:121
  36.9 1.2 fusion.17
  39.5 2.2 fusion.23
  42.2 1.6 pad_maximum_fusion.xa_ref.xb_ref
  43.8 10.0 %shard_map.354 = f32[768,1536]{1,0:T(8,128)} custom-call(f32[768]{0:T(1024)} %copy-done.48, f32[768]{0:T(1024)} %copy-done.46, f32[2,384]{1,0:T(2,128)} %get-tuple-element.197.w_ref, f32[768,768]{1,0:T(8,128)} %pad_maximum_fusion.xa_ref.xb_ref, f32[768,768]{1,0:T(8,128)} %pad_maximum_fusion.xa_ref.xb_ref), custom_call_target="tpu_custom_call" | custom-call | flops 11796480 | bytes 9437184 | tf_op jit(solution)/shard_map/pallas_call | solution.py:82
  53.8 4.8 %fusion.104 = (f32[767,384]{1,0:T(8,128)}, f32[767,384]{1,0:T(8,128)}, f32[767,384]{1,0:T(8,128)}, f32[767,384]{1,0:T(8,128)}) fusion(f32[768,1536]{1,0:T(8,128)} %shard_map.354), kind=kLoop, calls=%fused_computation.327 | loop fusion | bytes 9424896 | tf_op jit(solution)/shard_map/slice | solution.py:245
  58.6 5.2 %all-gather.6.cloned.1.call-done = bf16[2,1536,512]{2,1,0:T(8,128)(2,1)} async-done(((bf16[2,1536,128]{2,1,0:T(8,128)(2,1)}), bf16[2,1536,512]{2,1,0:T(8,128)(2,1)}) %all-gather.6.cloned.1.call-update) | async-done | bytes 3145744 | tf_op jit(solution)/shard_map/all_gather | solution.py:121
  63.7 8.5 %multiply_multiply_fusion.11 = (f32[768,512]{1,0:T(8,128)}, f32[768,512]{1,0:T(8,128)}) fusion(f32[512]{0:T(512)S(1)} %bitcast.459, f32[512]{0:T(512)S(1)} %bitcast.462, f32[768]{0:T(1024)S(1)} %add_rsqrt_fusion.1, f32[768]{0:T(1024)S(1)} %broadcast_multiply_fusion.11, bf16[768,512]{1,0:T(8,128)(2,1)S(1)} %all_gather.18, f32[512]{0:T(512)S(1)} %bitcast.468, ...), kind=kOutput, calls=%fused_computation.72 | convolution fusion | flops 1237057536 | bytes 10235904 | tf_op jit(solution)/shard_map/dot_general | solution.py:193
  72.2 10.5 %all-gather.8.cloned.1.call-done = bf16[2,512,512]{2,1,0:T(8,128)(2,1)} async-done(((bf16[2,512,128]{2,1,0:T(8,128)(2,1)}), bf16[2,512,512]{2,1,0:T(8,128)(2,1)}) %all-gather.8.cloned.1.call-update) | async-done | bytes 1048592 | tf_op jit(solution)/shard_map/all_gather | solution.py:121
  82.8 4.0 %fusion.103 = (f32[768]{0:T(1024)S(1)}, f32[768,512]{1,0:T(8,128)S(1)}, f32[768,512]{1,0:T(8,128)}) fusion(f32[768,512]{1,0:T(8,128)} %get-tuple-element.203, bf16[768,512]{1,0:T(8,128)(2,1)S(1)} %all_gather.18, f32[512]{0:T(512)S(1)} %bitcast.473, bf16[2,512,512]{2,1,0:T(8,128)(2,1)} %all-gather.8.cloned.1.call-done), kind=kOutput, calls=%fused_computation.326 | convolution fusion | flops 406191360 | bytes 7607296 | tf_op jit(solution)/shard_map/dot_general | solution.py:198
  90.0 1.1 copy-done.1
  91.1 1.6 pad_maximum_fusion.1.xa_ref.xb_ref
  92.6 10.1 %shard_map.355 = f32[768,1536]{1,0:T(8,128)} custom-call(f32[768]{0:T(1024)} %copy-done.48, f32[768]{0:T(1024)} %copy-done.46, f32[2,384]{1,0:T(2,128)} %get-tuple-element.213.w_ref, f32[768,768]{1,0:T(8,128)} %pad_maximum_fusion.1.xa_ref.xb_ref, f32[768,768]{1,0:T(8,128)} %pad_maximum_fusion.1.xa_ref.xb_ref), custom_call_target="tpu_custom_call" | custom-call | flops 11796480 | bytes 9437184 | tf_op jit(solution)/shard_map/pallas_call | solution.py:82
  102.7 5.0 %fusion.105 = (f32[767,384]{1,0:T(8,128)}, f32[767,384]{1,0:T(8,128)}, f32[767,384]{1,0:T(8,128)}, f32[767,384]{1,0:T(8,128)}) fusion(f32[768,1536]{1,0:T(8,128)} %shard_map.355), kind=kLoop, calls=%fused_computation.328 | loop fusion | bytes 9424896 | tf_op jit(solution)/shard_map/slice | solution.py:245
  109.7 4.8 %multiply_multiply_fusion.10 = (f32[768,512]{1,0:T(8,128)S(1)}, f32[768,512]{1,0:T(8,128)S(1)}, f32[768,512]{1,0:T(8,128)S(1)}) fusion(f32[512]{0:T(512)S(1)} %bitcast.465, f32[512]{0:T(512)S(1)} %bitcast.455, f32[768]{0:T(1024)S(1)} %add_rsqrt_fusion, f32[768,512]{1,0:T(8,128)S(1)} %copy-done.3, f32[768]{0:T(1024)S(1)} %broadcast_multiply_fusion.10, ...), kind=kOutput, calls=%fused_computation.70 | convolution fusion | flops 1236664320 | bytes 12597248 | tf_op jit(solution)/shard_map/dot_general | solution.py:193
  114.5 1.0 convert_reduce_fusion.1
  116.1 2.5 fusion.110
  118.5 1.7 convolution_bitcast_fusion
  120.3 1.4 fusion.16
  121.7 2.5 fusion.107
  124.2 9.9 %shard_map.356 = f32[768,1536]{1,0:T(8,128)} custom-call(f32[768]{0:T(1024)} %get-tuple-element.215.ma_ref, f32[768]{0:T(1024)} %get-tuple-element.216.mb_ref, f32[2,384]{1,0:T(2,128)} %get-tuple-element.214.w_ref, f32[768,768]{1,0:T(8,128)} %get-tuple-element.165.xa_ref, f32[768,768]{1,0:T(8,128)} %get-tuple-element.164.xb_ref), custom_call_target="tpu_custom_call" | custom-call | flops 11796480 | bytes 9437184 | tf_op jit(solution)/shard_map/pallas_call | solution.py:82
  134.1 4.8 %add_reduce_fusion = (f32[384]{0:T(512)S(1)}, f32[384]{0:T(512)S(1)}, bf16[768,384]{1,0:T(8,128)(2,1)S(1)}, f32[768,384]{1,0:T(8,128)S(1)}, f32[768,384]{1,0:T(8,128)S(1)}) fusion(f32[767,384]{1,0:T(8,128)} %get-tuple-element.161, f32[767,384]{1,0:T(8,128)} %get-tuple-element.160, f32[767,384]{1,0:T(8,128)} %get-tuple-element.159, ...), kind=kLoop, calls=%fused_computation.82 | loop fusion | flops 7961856 | bytes 12395520 | tf_op jit(solution)/shard_map/reduce_sum | solution.py:246
  140.6 2.2 convolution_bitcast_fusion.2
  142.9 1.4 multiply_reduce_fusion.1
  145.0 1.1 convert_reduce_fusion.2
  146.1 1.1 convolution_bitcast_fusion.5
  147.3 1.3 copy-done.43
  148.6 5.0 %fusion.111 = (bf16[768,512]{1,0:T(8,128)(2,1)S(1)}, f32[768,512]{1,0:T(8,128)}) fusion(f32[768,512]{1,0:T(8,128)S(1)} %copy-done.60, bf16[768,512]{1,0:T(8,128)(2,1)S(1)} %get-tuple-element.133, bf16[2,512,512]{2,1,0:T(8,128)(2,1)S(1)} %copy-done.43, f32[768,512]{1,0:T(8,128)S(1)} %get-tuple-element.134, f32[768,512]{1,0:T(8,128)S(1)} %copy-done.27), kind=kOutput, calls=%fused_computation.334 | convolution fusion | flops 431751168 | bytes 8388608 | tf_op jit(solution)/shard_map/dot_general | solution.py:115
  153.5 1.7 convolution_bitcast_fusion.1
  155.6 1.4 fusion.15
  157.0 2.5 fusion.106
  159.5 9.9 %shard_map.357 = f32[768,1536]{1,0:T(8,128)} custom-call(f32[768]{0:T(1024)} %get-tuple-element.215.ma_ref, f32[768]{0:T(1024)} %get-tuple-element.216.mb_ref, f32[2,384]{1,0:T(2,128)} %get-tuple-element.196.w_ref, f32[768,768]{1,0:T(8,128)} %get-tuple-element.163.xa_ref, f32[768,768]{1,0:T(8,128)} %get-tuple-element.162.xb_ref), custom_call_target="tpu_custom_call" | custom-call | flops 11796480 | bytes 9437184 | tf_op jit(solution)/shard_map/pallas_call | solution.py:82
  169.4 4.3 %subtract_reduce_fusion.2 = (f32[384]{0:T(512)S(1)}, f32[384]{0:T(512)S(1)}, f32[384]{0:T(512)S(1)}, f32[384]{0:T(512)S(1)}, f32[768,384]{1,0:T(8,128)S(1)}, /*index=5*/f32[768,384]{1,0:T(8,128)S(1)}) fusion(f32[768,768]{1,0:T(8,128)S(1)} %fusion.23, f32[768]{0:T(1024)S(1)} %get-tuple-element.200, f32[768,384]{1,0:T(8,128)} %copy-done.5, ...), kind=kLoop, calls=%fused_computation.92 | loop fusion | flops 6486528 | bytes 14164992 | tf_op jit(solution)/shard_map/reduce_sum | solution.py:240
  175.7 1.2 pad_maximum_fusion.2
  176.9 1.3 convolution_bitcast_fusion.3
  179.2 1.2 copy-done.12
  180.9 3.9 %add_reduce_fusion.2 = (f32[384]{0:T(512)S(1)}, f32[384]{0:T(512)S(1)}) fusion(f32[767,384]{1,0:T(8,128)} %get-tuple-element.154, f32[767,384]{1,0:T(8,128)} %get-tuple-element.153, f32[767,384]{1,0:T(8,128)S(1)} %copy-done.13, f32[767,384]{1,0:T(8,128)S(1)} %copy-done.12, f32[768,1536]{1,0:T(8,128)} %shard_map.357, f32[768]{0:T(1024)S(1)} %copy-done.47, ...), kind=kLoop, calls=%fused_computation.90 | loop fusion | flops 5897472 | bytes 9440256 | tf_op jit(solution)/shard_map/reduce_sum | solution.py:246
  185.6 2.9 fusion.96
  189.1 38.9 %all-reduce.14 = (f32[2,4,128]{2,1,0:T(4,128)S(1)}, f32[2,3,384]{2,1,0:T(4,128)S(1)}) all-reduce(f32[2,4,128]{2,1,0:T(4,128)S(1)} %pad_maximum_fusion.14, f32[2,3,384]{2,1,0:T(4,128)S(1)} %pad_maximum_fusion.11), channel_id=1, replica_groups=mesh['seq'=8,'feat'=4] {'seq'}, use_global_device_ids=true, to_apply=%region_22.0 | all-reduce | flops 3328 | bytes 26624 | tf_op jit(solution)/shard_map/psum | solution.py:266
  230.5 2.2 dynamic-slice_add_fusion.1
  233.3 2.4 dynamic-slice_add_fusion
  235.7 67.5 %all-reduce.18.cloned.1.call-done = (f32[2,128,768]{2,1,0:T(8,128)}, f32[2,1536,128]{2,1,0:T(8,128)}, f32[2,512,128]{2,1,0:T(8,128)}) async-done(((f32[2,128,768]{2,1,0:T(8,128)}, f32[2,1536,128]{2,1,0:T(8,128)}, f32[2,512,128]{2,1,0:T(8,128)}), (f32[2,128,768]{2,1,0:T(8,128)}, f32[2,1536,128]{2,1,0:T(8,128)}, f32[2,512,128]{2,1,0:T(8,128)})) %all-reduce.18.cloned.1.call-update) | async-done | bytes 2883600 | tf_op jit(solution)/shard_map/psum | solution.py:266
  303.2 5.1 %add_multiply_fusion = (f32[2,1536,128]{2,1,0:T(8,128)}, f32[2,1536,128]{2,1,0:T(8,128)}, f32[2,1536,128]{2,1,0:T(8,128)}, f32[2,1536,128]{2,1,0:T(8,128)}) fusion(f32[2,1536,128]{2,1,0:T(8,128)S(1)} %copy-done.23, f32[2,1536,128]{2,1,0:T(8,128)S(1)} %copy-done.10, f32[2,1536,128]{2,1,0:T(8,128)} %param.29, f32[2,1536,128]{2,1,0:T(8,128)} %get-tuple-element.100), kind=kLoop, calls=%fused_computation.17 | loop fusion | flops 4325376 | bytes 12582912 | tf_op jit(solution)/shard_map/add | solution.py:104
  308.4 1.9 add_multiply_fusion.3
  310.8 1.5 add_multiply_fusion.4
  (183 shorter events, 21.2 us)
Async XLA Ops:
  7.2 2.2 copy-start.9
  7.2 32.3 %all-gather.4.cloned.1.call-start = ((), (), s32[]{:S(2)}) async-start(), calls=%async_computation | async-start | bytes 1966080 | tf_op jit(solution)/shard_map/all_gather | solution.py:121
  9.3 2.0 copy-start.41
  9.3 2.1 copy-start.44
  9.3 54.4 %all-gather.6.cloned.1.call-start = ((), (), s32[]{:S(2)}) async-start(), calls=%async_computation.1 | async-start | bytes 3932160 | tf_op jit(solution)/shard_map/all_gather | solution.py:121
  10.4 72.3 %all-gather.8.cloned.1.call-start = ((), (), s32[]{:S(2)}) async-start(), calls=%async_computation.2 | async-start | bytes 1310720 | tf_op jit(solution)/shard_map/all_gather | solution.py:121
  11.2 10.9 %copy-start.50 = (f32[2,4,128]{2,1,0:T(4,128)S(1)}, f32[2,4,128]{2,1,0:T(4,128)}, u32[]{:S(2)}) copy-start(f32[2,4,128]{2,1,0:T(4,128)} %param.26) | copy-start | bytes 12292
  11.2 16.2 %copy-start.45 = (bf16[768,128]{1,0:T(8,128)(2,1)S(1)}, bf16[768,128]{1,0:T(8,128)(2,1)}, u32[]{:S(2)}) copy-start(bf16[768,128]{1,0:T(8,128)(2,1)} %param.20) | copy-start | bytes 589828
  11.2 292.0 %all-reduce.18.cloned.1.call-start = ((), (), s32[]{:S(2)}) async-start(), calls=%async_computation.3 | async-start | bytes 5767168 | tf_op jit(solution)/shard_map/psum | solution.py:266
  11.5 25.2 %copy-start.55 = (s32[2]{0:T(128)S(1)}, s32[2]{0:T(128)}, u32[]{:S(2)}) copy-start(s32[2]{0:T(128)} %param.21) | copy-start | bytes 28
  11.5 25.2 %copy-start.56 = (s32[2]{0:T(128)S(1)}, s32[2]{0:T(128)}, u32[]{:S(2)}) copy-start(s32[2]{0:T(128)} %param.22) | copy-start | bytes 28
  36.8 5.0 %copy-start.46 = (f32[768]{0:T(1024)}, f32[768]{0:T(1024)S(1)}, u32[]{:S(2)}) copy-start(f32[768]{0:T(1024)S(1)} %get-tuple-element.201.mb_ref) | copy-start | bytes 9220
  36.8 5.0 %copy-start.48 = (f32[768]{0:T(1024)}, f32[768]{0:T(1024)S(1)}, u32[]{:S(2)}) copy-start(f32[768]{0:T(1024)S(1)} %get-tuple-element.202.ma_ref) | copy-start | bytes 9220
  102.7 5.0 %copy-start = (f32[768,1536]{1,0:T(8,128)S(1)}, f32[768,1536]{1,0:T(8,128)}, u32[]{:S(2)}) copy-start(f32[768,1536]{1,0:T(8,128)} %shard_map.355) | copy-start | bytes 14155780
  102.7 6.0 %copy-start.3 = (f32[768,512]{1,0:T(8,128)S(1)}, f32[768,512]{1,0:T(8,128)}, u32[]{:S(2)}) copy-start(f32[768,512]{1,0:T(8,128)} %copy-done.2) | copy-start | bytes 4718596
  102.7 6.9 %copy-start.57 = (bf16[2,1536,512]{2,1,0:T(8,128)(2,1)S(1)}, bf16[2,1536,512]{2,1,0:T(8,128)(2,1)}, u32[]{:S(2)}) copy-start(bf16[2,1536,512]{2,1,0:T(8,128)(2,1)} %all-gather.6.cloned.1.call-done) | copy-start | bytes 9437188
  109.7 4.9 %copy-start.7 = (bf16[768,512]{1,0:T(8,128)(2,1)S(1)}, bf16[768,512]{1,0:T(8,128)(2,1)}, u32[]{:S(2)}) copy-start(bf16[768,512]{1,0:T(8,128)(2,1)} %all_gather.23) | copy-start | bytes 2359300
  109.7 4.9 %copy-start.42 = (bf16[2,512,512]{2,1,0:T(8,128)(2,1)S(1)}, bf16[2,512,512]{2,1,0:T(8,128)(2,1)}, u32[]{:S(2)}) copy-start(bf16[2,512,512]{2,1,0:T(8,128)(2,1)} %all-gather.8.cloned.1.call-done) | copy-start | bytes 3145732
  115.6 3.0 copy-start.19
  124.2 10.0 %copy-start.47 = (f32[768]{0:T(1024)S(1)}, f32[768]{0:T(1024)}, u32[]{:S(2)}) copy-start(f32[768]{0:T(1024)} %copy-done.46) | copy-start | bytes 9220
  124.2 10.0 %copy-start.49 = (f32[768]{0:T(1024)S(1)}, f32[768]{0:T(1024)}, u32[]{:S(2)}) copy-start(f32[768]{0:T(1024)} %copy-done.48) | copy-start | bytes 9220
  140.3 2.6 copy-start.25
  140.3 2.6 copy-start.28
  140.6 2.2 copy-start.4
  142.9 2.1 copy-start.27
  145.0 2.3 copy-start.60
  145.0 8.5 %slice-start = ((s8[4718592]{0:T(1024)(128)(4,1)}), s8[4194304]{0:T(1024)(128)(4,1)S(1)}, s32[]{:S(2)}) async-start(s8[4718592]{0:T(1024)(128)(4,1)} %bitcast.451), calls=%async_computation.4 | async-start | bytes 8388608
  146.1 7.4 %copy-start.20 = (f32[768,512]{1,0:T(8,128)}, f32[768,512]{1,0:T(8,128)S(1)}, u32[]{:S(2)}) copy-start(f32[768,512]{1,0:T(8,128)S(1)} %get-tuple-element.134) | copy-start | bytes 4718596
  146.1 2.4 copy-start.43
  148.6 5.0 %slice-start.1 = ((s8[4718592]{0:T(1024)(128)(4,1)}), s8[524288]{0:T(1024)(128)(4,1)S(1)}, s32[]{:S(2)}) async-start(s8[4718592]{0:T(1024)(128)(4,1)} %bitcast.451), calls=%async_computation.5 | async-start | bytes 1048576
  153.5 2.1 copy-start.58
  174.7 2.2 copy-start.33
  174.7 2.2 copy-start.35
  180.8 3.9 %copy-start.26 = (bf16[2,512,768]{2,1,0:T(8,128)(2,1)S(1)}, bf16[2,512,768]{2,1,0:T(8,128)(2,1)}, u32[]{:S(2)}) copy-start(bf16[2,512,768]{2,1,0:T(8,128)(2,1)} %all-gather.4.cloned.1.call-done) | copy-start | bytes 4718596
  180.8 3.9 %copy-start.34 = (bf16[768,384]{1,0:T(8,128)(2,1)S(1)}, bf16[768,384]{1,0:T(8,128)(2,1)}, u32[]{:S(2)}) copy-start(bf16[768,384]{1,0:T(8,128)(2,1)} %copy-done.33) | copy-start | bytes 1769476
  180.8 3.9 %copy-start.36 = (bf16[768,384]{1,0:T(8,128)(2,1)S(1)}, bf16[768,384]{1,0:T(8,128)(2,1)}, u32[]{:S(2)}) copy-start(bf16[768,384]{1,0:T(8,128)(2,1)} %copy-done.35) | copy-start | bytes 1769476
  180.8 4.7 %copy-start.59 = (f32[768,512]{1,0:T(8,128)S(1)}, f32[768,512]{1,0:T(8,128)}, u32[]{:S(2)}) copy-start(f32[768,512]{1,0:T(8,128)} %get-tuple-element.212) | copy-start | bytes 4718596
  185.5 42.5 %copy-start.51 = (f32[2,3,384]{2,0,1:T(2,128)S(1)}, f32[2,3,384]{2,0,1:T(2,128)}, u32[]{:S(2)}) copy-start(f32[2,3,384]{2,0,1:T(2,128)} %param.37) | copy-start | bytes 27652
  185.6 42.5 %copy-start.52 = (f32[2,3,384]{2,0,1:T(2,128)S(1)}, f32[2,3,384]{2,0,1:T(2,128)}, u32[]{:S(2)}) copy-start(f32[2,3,384]{2,0,1:T(2,128)} %param.32) | copy-start | bytes 27652
  188.4 44.3 %copy-start.53 = (f32[2,4,128]{2,1,0:T(4,128)S(1)}, f32[2,4,128]{2,1,0:T(4,128)}, u32[]{:S(2)}) copy-start(f32[2,4,128]{2,1,0:T(4,128)} %param.36) | copy-start | bytes 12292
  188.4 44.3 %copy-start.54 = (f32[2,4,128]{2,1,0:T(4,128)S(1)}, f32[2,4,128]{2,1,0:T(4,128)}, u32[]{:S(2)}) copy-start(f32[2,4,128]{2,1,0:T(4,128)} %param.31) | copy-start | bytes 12292
  230.5 72.7 %copy-start.10 = (f32[2,1536,128]{2,1,0:T(8,128)S(1)}, f32[2,1536,128]{2,1,0:T(8,128)}, u32[]{:S(2)}) copy-start(f32[2,1536,128]{2,1,0:T(8,128)} %param.24) | copy-start | bytes 4718596
  230.5 72.7 %copy-start.23 = (f32[2,1536,128]{2,1,0:T(8,128)S(1)}, f32[2,1536,128]{2,1,0:T(8,128)}, u32[]{:S(2)}) copy-start(f32[2,1536,128]{2,1,0:T(8,128)} %param.34) | copy-start | bytes 4718596
  303.2 5.2 %copy-start.14 = (f32[2,128,768]{2,1,0:T(8,128)S(1)}, f32[2,128,768]{2,1,0:T(8,128)}, u32[]{:S(2)}) copy-start(f32[2,128,768]{2,1,0:T(8,128)} %param.23) | copy-start | bytes 2359300
  303.2 5.2 %copy-start.30 = (f32[2,128,768]{2,1,0:T(8,128)S(1)}, f32[2,128,768]{2,1,0:T(8,128)}, u32[]{:S(2)}) copy-start(f32[2,128,768]{2,1,0:T(8,128)} %param.33) | copy-start | bytes 2359300
  303.2 5.2 %copy-start.31 = (f32[2,128,768]{2,1,0:T(8,128)S(1)}, f32[2,128,768]{2,1,0:T(8,128)}, u32[]{:S(2)}) copy-start(f32[2,128,768]{2,1,0:T(8,128)} %param.28) | copy-start | bytes 2359300
  303.2 5.2 %copy-start.32 = (f32[2,128,768]{2,1,0:T(8,128)S(1)}, f32[2,128,768]{2,1,0:T(8,128)}, u32[]{:S(2)}) copy-start(f32[2,128,768]{2,1,0:T(8,128)} %get-tuple-element.99) | copy-start | bytes 2359300
  308.4 2.3 copy-start.39
  (19 other events, 27.7 us)
Sparse Core Ops, SparseCore 0:
  10.2 22.6 all-gather.3
  35.0 28.7 all-gather.5
  65.9 16.8 all-gather.7
  179.4 123.7 all-reduce.17

commit v2 on v1

--- a/solution.py
+++ b/solution.py
@@ -119,6 +119,20 @@
 
 def gather_feat(value, axis):
     return lax.all_gather(value, "feat", axis=axis, tiled=True)
+
+
+def reduce_seq(parts, earlier):
+    flat = jnp.concatenate([part.reshape(-1) for part in parts]).astype(jnp.bfloat16)
+    if earlier is not None:
+        earlier, flat = lax.optimization_barrier((earlier, flat))
+    total = lax.psum(flat, "seq")
+    pieces = [total]
+    total = total.astype(jnp.float32)
+    start = 0
+    for part in parts:
+        pieces.append(total[start : start + part.size].reshape(part.shape))
+        start += part.size
+    return pieces
 
 
 def body(
@@ -201,6 +215,7 @@
 
     grad = gather_feat(cotangent, 1).astype(jnp.float32) * alive[:, None]
     layer_grads = [None] * layers
+    previous = None
     for layer in reversed(range(layers)):
         scale, unit, normed_low, drive, states, states_low, mixed, act, act_low, pre = saved[layer]
         in_low = in_all[layer]
@@ -257,21 +272,14 @@
         second_mean = jnp.mean(unit_grad * unit, 1, keepdims=True)
         grad = grad + scale * (unit_grad - first_mean - unit * second_mean)
         feature_grad = mine(jnp.stack([gain_grad, bias_grad, skip_grad, gate_bias_grad]))
-        layer_grads[layer] = (in_grad, out_grad, gate_grad, feature_grad, row_grad)
-    stacked_in = jnp.stack([entry[0] for entry in layer_grads])
-    stacked_out = jnp.stack([entry[1] for entry in layer_grads])
-    stacked_gate = jnp.stack([entry[2] for entry in layer_grads])
-    stacked_feature = jnp.stack([entry[3] for entry in layer_grads])
-    stacked_state = jnp.stack([entry[4] for entry in layer_grads])
-    summed = lax.psum(
-        (stacked_in, stacked_out, stacked_gate, stacked_feature, stacked_state), "seq"
-    )
+        layer_grads[layer] = reduce_seq(
+            (in_grad, out_grad, gate_grad, feature_grad, row_grad), previous
+        )
+        previous = layer_grads[layer].pop(0)
     factor = 1.0 / math.sqrt(count * lax.axis_size("seq"))
-    grad_in = summed[0] * factor
-    grad_out = summed[1] * factor
-    grad_gate = summed[2] * factor
-    grad_feature = summed[3] * factor
-    grad_state = summed[4] * factor
+    grad_in, grad_out, grad_gate, grad_feature, grad_state = (
+        jnp.stack([entry[k] for entry in layer_grads]) * factor for k in range(5)
+    )
     new_in = update(input_matrix, grad_in, velocity_input, average_input, slow_rate, 0.0)
     new_out = update(output_matrix, grad_out, velocity_output, average_output, slow_rate, 0.0)
     new_gate = update(gate_matrix, grad_gate, velocity_gate, average_gate, main_rate, weight_decay)

time: 319 us -> 366 us (1.15)
  waiting for transfers between devices: 83.3 us -> 154 us
  blocking collectives: 63.5 us -> 24.6 us
  local copies, waits for them, and re-layouts: 28.9 us -> 38.4 us
  matrix products: 44.5 us -> 51.3 us
    psum x1 -> x2, waiting for transfers between devices: 67.5 us -> 139 us  [reduce_seq(): total = lax.psum(flat, 'seq')]
    psum x1 -> x0, blocking collectives: 38.9 us -> none  [body(): lax.psum((stacked_in, stacked_out, stacked_gate, stacked_feature, stacked...]
    dot_general x6, matrix products: 8.53 us -> 13.8 us  [contract_rows(): lax.dot_general(left, right, (((0,), (0,)), ((), ())), preferred_element_...]
    another operation x0 -> x10, local copies, waits for them, and re-layouts: none -> 3.95 us  [body(): jnp.stack([entry[k] for entry in layer_grads]) * factor]
    unnamed x130 -> x132, local copies, waits for them, and re-layouts: 14 us -> 14.2 us
  transfers between devices with their start and end apart: 4 -> 5, of which waited for: 3 -> 4; matrix products, arithmetic and copies ran while one was open for 12% -> 10% of each run, Pallas kernels for 3% -> 3%
where the time goes in v2:
time: 366 us; the launch traced here: 365 us
  waiting for transfers between devices  154 us (42%)
  matrix products  51.3 us (14%)
  other arithmetic  41.7 us (11%)
  Pallas kernels  40.1 us (11%)
  local copies, waits for them, and re-layouts  38.4 us (10%)
  blocking collectives  24.6 us (7%)
  between operations  14.6 us (4%)
    psum x2, waiting for transfers between devices, reduce_seq(): total = lax.psum(flat, 'seq')  139 us
    pallas_call x4, Pallas kernels, recurrence(): pl.pallas_call(recurrence_kernel, out_shape=jax.ShapeDtypeStruct((count,...  40.1 us
    all_gather x3, blocking collectives, gather_feat(): return lax.all_gather(value, 'feat', axis=axis, tiled=True)  24.6 us
    all_gather x3, waiting for transfers between devices, gather_feat(): return lax.all_gather(value, 'feat', axis=axis, tiled=True)  15.7 us
    unnamed x132, local copies, waits for them, and re-layouts  14.2 us
    dot_general x6, matrix products, contract_rows(): lax.dot_general(left, right, (((0,), (0,)), ((), ())), preferred_element_...  13.8 us
    dot_general x2, matrix products, body(): jnp.dot(states_low, out_low, preferred_element_type=jnp.float32)  13.3 us
    dot_general x4, matrix products, contract_cols(): lax.dot_general(left, right, (((1,), (1,)), ((), ())), preferred_element_...  10.2 us
  transfers between devices with their start and end apart: 5, of which 4 were waited for; matrix products, arithmetic and copies ran while one was open for 10% of the time, Pallas kernels for 3%

profile of v2, /device:TPU:0, one launch (start us, length us, event | category | flops | bytes accessed | tf_op | source)
XLA Modules:
  0.0 365.2 jit_solution(2626764585379373877)
XLA Ops:
  7.2 2.0 convert_element_type.78
  11.5 10.0 %all_gather.18 = bf16[768,512]{1,0:T(8,128)(2,1)S(1)} all-gather(bf16[768,128]{1,0:T(8,128)(2,1)S(1)} %copy-done.44), channel_id=1, replica_groups=mesh['seq'=8,'feat'=4] {'feat'}, dimensions={1}, use_global_device_ids=true | all-gather | bytes 983040 | tf_op jit(solution)/shard_map/all_gather | solution.py:121
  22.2 5.2 %all_gather.19 = f32[2,4,512]{2,1,0:T(4,128)S(1)} all-gather(f32[2,4,128]{2,1,0:T(4,128)S(1)} %copy-done.52), channel_id=1, replica_groups=mesh['seq'=8,'feat'=4] {'feat'}, dimensions={2}, use_global_device_ids=true | all-gather | bytes 20480 | tf_op jit(solution)/shard_map/all_gather | solution.py:121
  27.4 9.3 %all_gather.23 = bf16[768,512]{1,0:T(8,128)(2,1)} all-gather(bf16[768,128]{1,0:T(8,128)(2,1)S(1)} %copy-done.45), channel_id=1, replica_groups=mesh['seq'=8,'feat'=4] {'feat'}, dimensions={1}, use_global_device_ids=true | all-gather | bytes 983040 | tf_op jit(solution)/shard_map/all_gather | solution.py:121
  36.9 1.2 fusion.21
  39.5 2.2 fusion.31
  42.2 1.6 pad_maximum_fusion.xa_ref.xb_ref
  43.8 10.0 %shard_map.354 = f32[768,1536]{1,0:T(8,128)} custom-call(f32[768]{0:T(1024)} %copy-done.48, f32[768]{0:T(1024)} %copy-done.46, f32[2,384]{1,0:T(2,128)} %get-tuple-element.192.w_ref, f32[768,768]{1,0:T(8,128)} %pad_maximum_fusion.xa_ref.xb_ref, f32[768,768]{1,0:T(8,128)} %pad_maximum_fusion.xa_ref.xb_ref), custom_call_target="tpu_custom_call" | custom-call | flops 11796480 | bytes 9437184 | tf_op jit(solution)/shard_map/pallas_call | solution.py:82
  53.8 4.8 %fusion.113 = (f32[767,384]{1,0:T(8,128)}, f32[767,384]{1,0:T(8,128)}, f32[767,384]{1,0:T(8,128)}, f32[767,384]{1,0:T(8,128)}) fusion(f32[768,1536]{1,0:T(8,128)} %shard_map.354), kind=kLoop, calls=%fused_computation.339 | loop fusion | bytes 9424896 | tf_op jit(solution)/shard_map/slice | solution.py:260
  58.5 5.2 %all-gather.6.cloned.1.call-done = bf16[2,1536,512]{2,1,0:T(8,128)(2,1)} async-done(((bf16[2,1536,128]{2,1,0:T(8,128)(2,1)}), bf16[2,1536,512]{2,1,0:T(8,128)(2,1)}) %all-gather.6.cloned.1.call-update) | async-done | bytes 3145744 | tf_op jit(solution)/shard_map/all_gather | solution.py:121
  63.7 8.5 %multiply_multiply_fusion.11 = (f32[768,512]{1,0:T(8,128)}, f32[768,512]{1,0:T(8,128)}) fusion(f32[512]{0:T(512)S(1)} %bitcast.469, f32[512]{0:T(512)S(1)} %bitcast.472, f32[768]{0:T(1024)S(1)} %add_rsqrt_fusion.1, f32[768]{0:T(1024)S(1)} %broadcast_multiply_fusion.6, bf16[768,512]{1,0:T(8,128)(2,1)S(1)} %all_gather.18, f32[512]{0:T(512)S(1)} %bitcast.478, ...), kind=kOutput, calls=%fused_computation.76 | convolution fusion | flops 1237057536 | bytes 10235904 | tf_op jit(solution)/shard_map/dot_general | solution.py:207
  72.2 10.5 %all-gather.8.cloned.1.call-done = bf16[2,512,512]{2,1,0:T(8,128)(2,1)} async-done(((bf16[2,512,128]{2,1,0:T(8,128)(2,1)}), bf16[2,512,512]{2,1,0:T(8,128)(2,1)}) %all-gather.8.cloned.1.call-update) | async-done | bytes 1048592 | tf_op jit(solution)/shard_map/all_gather | solution.py:121
  82.8 4.1 %fusion.112 = (f32[768]{0:T(1024)S(1)}, f32[768,512]{1,0:T(8,128)S(1)}, f32[768,512]{1,0:T(8,128)}) fusion(f32[768,512]{1,0:T(8,128)} %get-tuple-element.198, bf16[768,512]{1,0:T(8,128)(2,1)S(1)} %all_gather.18, f32[512]{0:T(512)S(1)} %bitcast.487, bf16[2,512,512]{2,1,0:T(8,128)(2,1)} %all-gather.8.cloned.1.call-done), kind=kOutput, calls=%fused_computation.338 | convolution fusion | flops 406191360 | bytes 7607296 | tf_op jit(solution)/shard_map/dot_general | solution.py:212
  91.1 1.6 pad_maximum_fusion.1.xa_ref.xb_ref
  92.6 10.1 %shard_map.355 = f32[768,1536]{1,0:T(8,128)} custom-call(f32[768]{0:T(1024)} %copy-done.48, f32[768]{0:T(1024)} %copy-done.46, f32[2,384]{1,0:T(2,128)} %get-tuple-element.208.w_ref, f32[768,768]{1,0:T(8,128)} %pad_maximum_fusion.1.xa_ref.xb_ref, f32[768,768]{1,0:T(8,128)} %pad_maximum_fusion.1.xa_ref.xb_ref), custom_call_target="tpu_custom_call" | custom-call | flops 11796480 | bytes 9437184 | tf_op jit(solution)/shard_map/pallas_call | solution.py:82
  102.7 5.0 %fusion.114 = (f32[767,384]{1,0:T(8,128)}, f32[767,384]{1,0:T(8,128)}, f32[767,384]{1,0:T(8,128)}, f32[767,384]{1,0:T(8,128)}) fusion(f32[768,1536]{1,0:T(8,128)} %shard_map.355), kind=kLoop, calls=%fused_computation.340 | loop fusion | bytes 9424896 | tf_op jit(solution)/shard_map/slice | solution.py:260
  109.7 4.8 %multiply_multiply_fusion.10 = (f32[768,512]{1,0:T(8,128)S(1)}, f32[768,512]{1,0:T(8,128)S(1)}, f32[768,512]{1,0:T(8,128)S(1)}) fusion(f32[512]{0:T(512)S(1)} %bitcast.475, f32[512]{0:T(512)S(1)} %bitcast.465, f32[768]{0:T(1024)S(1)} %add_rsqrt_fusion, f32[768,512]{1,0:T(8,128)S(1)} %copy-done.4, f32[768]{0:T(1024)S(1)} %broadcast_multiply_fusion.5, ...), kind=kOutput, calls=%fused_computation.74 | convolution fusion | flops 1236664320 | bytes 12597248 | tf_op jit(solution)/shard_map/dot_general | solution.py:207
  115.6 2.4 fusion.119
  118.9 1.4 fusion.20
  120.3 2.5 fusion.116
  123.7 10.0 %shard_map.356 = f32[768,1536]{1,0:T(8,128)} custom-call(f32[768]{0:T(1024)} %get-tuple-element.210.ma_ref, f32[768]{0:T(1024)} %get-tuple-element.211.mb_ref, f32[2,384]{1,0:T(2,128)} %get-tuple-element.209.w_ref, f32[768,768]{1,0:T(8,128)} %get-tuple-element.164.xa_ref, f32[768,768]{1,0:T(8,128)} %get-tuple-element.163.xb_ref), custom_call_target="tpu_custom_call" | custom-call | flops 11796480 | bytes 9437184 | tf_op jit(solution)/shard_map/pallas_call | solution.py:82
  133.8 4.6 %add_reduce_fusion.2 = (f32[384]{0:T(512)S(1)}, f32[384]{0:T(512)S(1)}, bf16[768,384]{1,0:T(8,128)(2,1)S(1)}, f32[768,384]{1,0:T(8,128)S(1)}, f32[768,384]{1,0:T(8,128)S(1)}) fusion(f32[767,384]{1,0:T(8,128)} %get-tuple-element.160, f32[767,384]{1,0:T(8,128)} %get-tuple-element.159, f32[767,384]{1,0:T(8,128)} %get-tuple-element.158, ...), kind=kLoop, calls=%fused_computation.92 | loop fusion | flops 7961856 | bytes 12395520 | tf_op jit(solution)/shard_map/reduce_sum | solution.py:261
  138.7 2.3 convolution_convert_fusion.3
  141.6 1.4 multiply_reduce_fusion.3
  143.8 1.2 convert_reduce_fusion.1
  145.5 5.0 %fusion.120 = (bf16[768,512]{1,0:T(8,128)(2,1)S(1)}, f32[768,512]{1,0:T(8,128)}) fusion(f32[768,512]{1,0:T(8,128)S(1)} %copy-done.61, bf16[768,512]{1,0:T(8,128)(2,1)S(1)} %get-tuple-element.125, bf16[2,512,512]{2,1,0:T(8,128)(2,1)S(1)} %copy-done.43, f32[768,512]{1,0:T(8,128)S(1)} %get-tuple-element.126, f32[768,512]{1,0:T(8,128)S(1)} %copy-done.29), kind=kOutput, calls=%fused_computation.346 | convolution fusion | flops 431751168 | bytes 8388608 | tf_op jit(solution)/shard_map/dot_general | solution.py:115
  151.4 1.4 fusion.19
  152.8 2.6 fusion.115
  155.4 10.0 %shard_map.357 = f32[768,1536]{1,0:T(8,128)} custom-call(f32[768]{0:T(1024)} %get-tuple-element.210.ma_ref, f32[768]{0:T(1024)} %get-tuple-element.211.mb_ref, f32[2,384]{1,0:T(2,128)} %get-tuple-element.191.w_ref, f32[768,768]{1,0:T(8,128)} %get-tuple-element.162.xa_ref, f32[768,768]{1,0:T(8,128)} %get-tuple-element.161.xb_ref), custom_call_target="tpu_custom_call" | custom-call | flops 11796480 | bytes 9437184 | tf_op jit(solution)/shard_map/pallas_call | solution.py:82
  165.4 4.3 %subtract_reduce_fusion = (f32[384]{0:T(512)S(1)}, f32[384]{0:T(512)S(1)}, f32[384]{0:T(512)S(1)}, f32[384]{0:T(512)S(1)}, f32[768,384]{1,0:T(8,128)S(1)}, /*index=5*/f32[768,384]{1,0:T(8,128)S(1)}) fusion(f32[768,768]{1,0:T(8,128)S(1)} %fusion.31, f32[768]{0:T(1024)S(1)} %get-tuple-element.195, f32[768,384]{1,0:T(8,128)} %copy-done.6, ...), kind=kLoop, calls=%fused_computation.86 | loop fusion | flops 6486528 | bytes 14164992 | tf_op jit(solution)/shard_map/reduce_sum | solution.py:255
  170.9 2.1 convolution_convert_fusion.2
  172.9 1.1 reshape.1075
  174.1 3.3 fusion.1
  177.5 1.5 fusion.28
  179.1 2.8 add_reduce_fusion
  182.7 3.3 fusion.3
  186.0 1.4 fusion.30
  188.8 4.4 %fusion.106 = (f32[768]{0:T(1024)S(1)}, f32[768]{0:T(1024)S(1)}, f32[512]{0:T(512)S(1)}, f32[512]{0:T(512)S(1)}, f32[512]{0:T(512)S(1)}, /*index=5*/f32[768,512]{1,0:T(8,128)S(1)}, f32[768,512]{1,0:T(8,128)}) fusion(f32[768]{0:T(1024)S(1)} %add_rsqrt_fusion.1, f32[768]{0:T(1024)S(1)} %broadcast_multiply_fusion.6, bf16[768,512]{1,0:T(8,128)(2,1)S(1)} %all_gather.18, ...), kind=kOutput, calls=%fused_computation.335 | convolution fusion | flops 612627456 | bytes 7495680 | tf_op jit(solution)/shard_map/dot_general | solution.py:265
  193.3 1.7 dynamic-update-slice.3
  195.0 1.4 dynamic-update-slice.4
  196.4 2.2 dynamic-slice_add_fusion
  198.6 64.4 %all-reduce.17.cloned.1.call-done = bf16[362112]{0:T(1024)(128)(2,1)} async-done(((bf16[362112]{0:T(1024)(128)(2,1)}), bf16[362112]{0:T(1024)(128)(2,1)}) %all-reduce.17.cloned.1.call-update) | async-done | bytes 724240 | tf_op jit(solution)/shard_map/psum | solution.py:128
  264.4 1.2 convert_element_type.95
  266.5 74.1 %all-reduce.19.cloned.1.call-done = bf16[362112]{0:T(1024)(128)(2,1)} async-done(((bf16[362112]{0:T(1024)(128)(2,1)}), bf16[362112]{0:T(1024)(128)(2,1)}) %all-reduce.19.cloned.1.call-update) | async-done | bytes 724240 | tf_op jit(solution)/shard_map/psum | solution.py:128
  340.6 1.2 convert_element_type.94
  349.1 2.9 add_multiply_fusion.4
  352.1 4.7 %add_multiply_fusion = (f32[2,1536,128]{2,1,0:T(8,128)}, f32[2,1536,128]{2,1,0:T(8,128)}, f32[2,1536,128]{2,1,0:T(8,128)}, f32[2,1536,128]{2,1,0:T(8,128)}) fusion(f32[2,1536,128]{2,1,0:T(8,128)S(1)} %copy-done.25, f32[2,1536,128]{2,1,0:T(8,128)S(1)} %copy-done.11, f32[2,1536,128]{2,1,0:T(8,128)} %param.29, f32[1,1536,128]{2,1,0:T(8,128)S(1)} %slice_bitcast_fusion.6, ...), kind=kLoop, calls=%fused_computation.21 | loop fusion | flops 4718592 | bytes 12582912 | tf_op jit(solution)/shard_map/add | solution.py:104
  356.8 1.9 add_multiply_fusion.3
  (203 shorter events, 29.7 us)
Async XLA Ops:
  7.2 32.3 %all-gather.4.cloned.1.call-start = ((), (), s32[]{:S(2)}) async-start(), calls=%async_computation | async-start | bytes 1966080 | tf_op jit(solution)/shard_map/all_gather | solution.py:121
  9.3 54.4 %all-gather.6.cloned.1.call-start = ((), (), s32[]{:S(2)}) async-start(), calls=%async_computation.1 | async-start | bytes 3932160 | tf_op jit(solution)/shard_map/all_gather | solution.py:121
  10.4 72.3 %all-gather.8.cloned.1.call-start = ((), (), s32[]{:S(2)}) async-start(), calls=%async_computation.2 | async-start | bytes 1310720 | tf_op jit(solution)/shard_map/all_gather | solution.py:121
  11.2 10.9 %copy-start.52 = (f32[2,4,128]{2,1,0:T(4,128)S(1)}, f32[2,4,128]{2,1,0:T(4,128)}, u32[]{:S(2)}) copy-start(f32[2,4,128]{2,1,0:T(4,128)} %param.26) | copy-start | bytes 12292
  11.2 16.2 %copy-start.45 = (bf16[768,128]{1,0:T(8,128)(2,1)S(1)}, bf16[768,128]{1,0:T(8,128)(2,1)}, u32[]{:S(2)}) copy-start(bf16[768,128]{1,0:T(8,128)(2,1)} %param.20) | copy-start | bytes 589828
  11.2 251.8 %all-reduce.17.cloned.1.call-start = ((), (), s32[]{:S(2)}) async-start(), calls=%async_computation.3 | async-start | bytes 1449984 | tf_op jit(solution)/shard_map/psum | solution.py:128
  11.5 25.2 %copy-start.57 = (s32[2]{0:T(128)S(1)}, s32[2]{0:T(128)}, u32[]{:S(2)}) copy-start(s32[2]{0:T(128)} %param.21) | copy-start | bytes 28
  11.5 25.2 %copy-start.58 = (s32[2]{0:T(128)S(1)}, s32[2]{0:T(128)}, u32[]{:S(2)}) copy-start(s32[2]{0:T(128)} %param.22) | copy-start | bytes 28
  36.8 5.0 %copy-start.46 = (f32[768]{0:T(1024)}, f32[768]{0:T(1024)S(1)}, u32[]{:S(2)}) copy-start(f32[768]{0:T(1024)S(1)} %get-tuple-element.196.mb_ref) | copy-start | bytes 9220
  36.8 5.0 %copy-start.48 = (f32[768]{0:T(1024)}, f32[768]{0:T(1024)S(1)}, u32[]{:S(2)}) copy-start(f32[768]{0:T(1024)S(1)} %get-tuple-element.197.ma_ref) | copy-start | bytes 9220
  102.7 5.0 %copy-start.1 = (f32[768,1536]{1,0:T(8,128)S(1)}, f32[768,1536]{1,0:T(8,128)}, u32[]{:S(2)}) copy-start(f32[768,1536]{1,0:T(8,128)} %shard_map.355) | copy-start | bytes 14155780
  102.7 6.0 %copy-start.4 = (f32[768,512]{1,0:T(8,128)S(1)}, f32[768,512]{1,0:T(8,128)}, u32[]{:S(2)}) copy-start(f32[768,512]{1,0:T(8,128)} %copy-done.3) | copy-start | bytes 4718596
  102.7 6.9 %copy-start.59 = (bf16[2,1536,512]{2,1,0:T(8,128)(2,1)S(1)}, bf16[2,1536,512]{2,1,0:T(8,128)(2,1)}, u32[]{:S(2)}) copy-start(bf16[2,1536,512]{2,1,0:T(8,128)(2,1)} %all-gather.6.cloned.1.call-done) | copy-start | bytes 9437188
  109.7 4.9 %copy-start.8 = (bf16[768,512]{1,0:T(8,128)(2,1)S(1)}, bf16[768,512]{1,0:T(8,128)(2,1)}, u32[]{:S(2)}) copy-start(bf16[768,512]{1,0:T(8,128)(2,1)} %all_gather.23) | copy-start | bytes 2359300
  109.7 4.9 %copy-start.42 = (bf16[2,512,512]{2,1,0:T(8,128)(2,1)S(1)}, bf16[2,512,512]{2,1,0:T(8,128)(2,1)}, u32[]{:S(2)}) copy-start(bf16[2,512,512]{2,1,0:T(8,128)(2,1)} %all-gather.8.cloned.1.call-done) | copy-start | bytes 3145732
  114.5 8.3 %copy-start.19 = (f32[768,512]{1,0:T(8,128)}, f32[768,512]{1,0:T(8,128)S(1)}, u32[]{:S(2)}) copy-start(f32[768,512]{1,0:T(8,128)S(1)} %get-tuple-element.144) | copy-start | bytes 4718596
  115.6 2.4 copy-start.32
  123.7 10.0 %copy-start.47 = (f32[768]{0:T(1024)S(1)}, f32[768]{0:T(1024)}, u32[]{:S(2)}) copy-start(f32[768]{0:T(1024)} %copy-done.46) | copy-start | bytes 9220
  123.7 10.0 %copy-start.49 = (f32[768]{0:T(1024)S(1)}, f32[768]{0:T(1024)}, u32[]{:S(2)}) copy-start(f32[768]{0:T(1024)} %copy-done.48) | copy-start | bytes 9220
  138.3 2.7 copy-start.6
  138.3 2.7 copy-start.7
  138.3 2.7 copy-start.28
  138.3 2.8 copy-start.30
  138.7 3.0 copy-start.5
  145.0 5.5 %copy-start.21 = (f32[768,512]{1,0:T(8,128)}, f32[768,512]{1,0:T(8,128)S(1)}, u32[]{:S(2)}) copy-start(f32[768,512]{1,0:T(8,128)S(1)} %get-tuple-element.126) | copy-start | bytes 4718596
  145.0 5.5 %copy-start.33 = (bf16[768,512]{1,0:T(8,128)(2,1)}, bf16[768,512]{1,0:T(8,128)(2,1)S(1)}, u32[]{:S(2)}) copy-start(bf16[768,512]{1,0:T(8,128)(2,1)S(1)} %get-tuple-element.125) | copy-start | bytes 2359300
  145.5 5.9 %copy-start.60 = (bf16[2,1536,512]{2,1,0:T(8,128)(2,1)S(1)}, bf16[2,1536,512]{2,1,0:T(8,128)(2,1)}, u32[]{:S(2)}) copy-start(bf16[2,1536,512]{2,1,0:T(8,128)(2,1)} %all-gather.6.cloned.1.call-done) | copy-start | bytes 9437188
  170.1 4.0 %copy-start.40 = (bf16[768,384]{1,0:T(8,128)(2,1)}, bf16[768,384]{1,0:T(8,128)(2,1)S(1)}, u32[]{:S(2)}) copy-start(bf16[768,384]{1,0:T(8,128)(2,1)S(1)} %get-tuple-element.166) | copy-start | bytes 1769476
  170.9 8.1 %copy-start.15 = (f32[767,384]{1,0:T(8,128)S(1)}, f32[767,384]{1,0:T(8,128)}, u32[]{:S(2)}) copy-start(f32[767,384]{1,0:T(8,128)} %get-tuple-element.151) | copy-start | bytes 3534340
  174.1 3.4 copy-start.13
  174.1 4.9 %copy-start = (f32[768,1536]{1,0:T(8,128)S(1)}, f32[768,1536]{1,0:T(8,128)}, u32[]{:S(2)}) copy-start(f32[768,1536]{1,0:T(8,128)} %shard_map.357) | copy-start | bytes 14155780
  178.9 3.0 copy-start.34
  182.7 3.3 copy-start.20
  188.7 151.9 %all-reduce.19.cloned.1.call-start = ((), (), s32[]{:S(2)}) async-start(), calls=%async_computation.4 | async-start | bytes 1449984 | tf_op jit(solution)/shard_map/psum | solution.py:128
  263.0 3.3 copy-start.24
  341.8 2.4 copy-start.51
  341.9 2.4 copy-start.53
  342.6 5.9 %copy-start.55 = (f32[2,4,128]{2,1,0:T(4,128)S(1)}, f32[2,4,128]{2,1,0:T(4,128)}, u32[]{:S(2)}) copy-start(f32[2,4,128]{2,1,0:T(4,128)} %param.36) | copy-start | bytes 12292
  342.6 5.9 %copy-start.56 = (f32[2,4,128]{2,1,0:T(4,128)S(1)}, f32[2,4,128]{2,1,0:T(4,128)}, u32[]{:S(2)}) copy-start(f32[2,4,128]{2,1,0:T(4,128)} %param.31) | copy-start | bytes 12292
  342.6 6.5 %copy-start.23 = (f32[2,512,128]{2,1,0:T(8,128)S(1)}, f32[2,512,128]{2,1,0:T(8,128)}, u32[]{:S(2)}) copy-start(f32[2,512,128]{2,1,0:T(8,128)} %param.25) | copy-start | bytes 1572868
  342.6 6.5 %copy-start.36 = (f32[1,512,128]{2,1,0:T(8,128)S(1)}, f32[1,512,128]{2,1,0:T(8,128)}, u32[]{:S(2)}) copy-start(f32[1,512,128]{2,1,0:T(8,128)} %slice_bitcast_fusion.20) | copy-start | bytes 786436
  349.1 2.9 copy-start.11
  349.1 2.9 copy-start.17
  349.1 2.9 copy-start.25
  352.0 4.7 %copy-start.16 = (f32[2,128,768]{2,1,0:T(8,128)S(1)}, f32[2,128,768]{2,1,0:T(8,128)}, u32[]{:S(2)}) copy-start(f32[2,128,768]{2,1,0:T(8,128)} %param.23) | copy-start | bytes 2359300
  352.0 4.7 %copy-start.26 = (f32[1,128,768]{2,1,0:T(8,128)S(1)}, f32[1,128,768]{2,1,0:T(8,128)}, u32[]{:S(2)}) copy-start(f32[1,128,768]{2,1,0:T(8,128)} %stack_reshape.30) | copy-start | bytes 1179652
  352.0 4.7 %copy-start.37 = (f32[2,128,768]{2,1,0:T(8,128)S(1)}, f32[2,128,768]{2,1,0:T(8,128)}, u32[]{:S(2)}) copy-start(f32[2,128,768]{2,1,0:T(8,128)} %param.33) | copy-start | bytes 2359300
  352.1 4.7 %copy-start.38 = (f32[2,128,768]{2,1,0:T(8,128)S(1)}, f32[2,128,768]{2,1,0:T(8,128)}, u32[]{:S(2)}) copy-start(f32[2,128,768]{2,1,0:T(8,128)} %param.28) | copy-start | bytes 2359300
  (19 other events, 28.1 us)
Sparse Core Ops, SparseCore 0:
  10.2 22.6 all-gather.3
  35.0 28.7 all-gather.5
  65.9 16.8 all-gather.7
  188.8 74.1 all-reduce.16
  267.3 73.2 all-reduce.18

commit v3 on v1

--- a/solution.py
+++ b/solution.py
@@ -94,6 +94,145 @@
             flops=20 * count * double, transcendentals=0, bytes_accessed=16 * count * double
         ),
     )(ma, mb, w, xa, xb)
+
+
+MESH = pl.DeviceIdType.MESH
+
+
+def ring_place(position, n):
+    upper = position // (n // 2)
+    return (1 - upper) * (2 * position) + upper * (2 * (n - 1 - position) + 1)
+
+
+def ring_position(index, n):
+    odd = index % 2
+    return (1 - odd) * (index // 2) + odd * (n - 1 - index // 2)
+
+
+def ring_sum_kernel(n, x_ref, o_ref, slots, rs_send, rs_recv, credit, done, ag_send, ag_recv):
+    rows = x_ref.shape[0]
+    half = rows // 2
+    size = half // n
+    me = ring_position(lax.axis_index("seq"), n)
+    right = ring_place((me + 1) % n, n)
+    left = ring_place((me + n - 1) % n, n)
+    rings = ((0, me, right, left), (1, (n - me) % n, left, right))
+
+    barrier = pltpu.get_barrier_semaphore()
+    for neighbour in (left, right):
+        pl.semaphore_signal(barrier, 1, device_id={"seq": neighbour}, device_id_type=MESH)
+    pl.semaphore_wait(barrier, 2)
+    o_ref[...] = x_ref[...]
+
+    def block(ring, k):
+        return pl.ds(pl.multiple_of(ring * half + k * size, 8), size)
+
+    def scatter_copy(ring, place, target, s):
+        return pltpu.make_async_remote_copy(
+            src_ref=o_ref.at[block(ring, (place - s + n) % n)],
+            dst_ref=slots.at[ring, s % 2],
+            send_sem=rs_send.at[ring, s % 2],
+            recv_sem=rs_recv.at[ring, s % 2],
+            device_id={"seq": target},
+            device_id_type=MESH,
+        )
+
+    def scatter_step(s, carry):
+        copies = []
+        for ring, place, target, source in rings:
+
+            @pl.when(s >= 2)
+            def _():
+                pl.semaphore_wait(credit.at[ring], 1)
+
+            copy = scatter_copy(ring, place, target, s)
+            copy.start()
+            copies.append(copy)
+        for (ring, place, target, source), copy in zip(rings, copies):
+            copy.wait_recv()
+            into = block(ring, (place - s - 1 + 2 * n) % n)
+            o_ref[into] = o_ref[into] + slots[ring, s % 2]
+            copy.wait_send()
+
+            @pl.when(s <= n - 4)
+            def _():
+                pl.semaphore_signal(credit.at[ring], 1, device_id={"seq": source}, device_id_type=MESH)
+
+        return carry
+
+    lax.fori_loop(0, n - 1, scatter_step, 0)
+    for ring, place, target, source in rings:
+        pl.semaphore_signal(done.at[ring], 1, device_id={"seq": source}, device_id_type=MESH)
+    for ring, place, target, source in rings:
+        pl.semaphore_wait(done.at[ring], 1)
+
+    def gather_copy(ring, place, target, s):
+        where = block(ring, (place + 1 - s + n) % n)
+        return pltpu.make_async_remote_copy(
+            src_ref=o_ref.at[where],
+            dst_ref=o_ref.at[where],
+            send_sem=ag_send.at[ring, s],
+            recv_sem=ag_recv.at[ring, s],
+            device_id={"seq": target},
+            device_id_type=MESH,
+        )
+
+    def gather_step(s, carry):
+        for ring, place, target, source in rings:
+
+            @pl.when(s >= 1)
+            def _():
+                gather_copy(ring, place, target, s - 1).wait_recv()
+
+            gather_copy(ring, place, target, s).start()
+
+            @pl.when(s >= 1)
+            def _():
+                gather_copy(ring, place, target, s - 1).wait_send()
+
+        return carry
+
+    lax.fori_loop(0, n - 1, gather_step, 0)
+    for ring, place, target, source in rings:
+        last = gather_copy(ring, place, target, n - 2)
+        last.wait_recv()
+        last.wait_send()
+
+
+def ring_sum(x, n):
+    rows, lanes = x.shape
+    size = rows // (2 * n)
+    return pl.pallas_call(
+        lambda *refs: ring_sum_kernel(n, *refs),
+        out_shape=jax.ShapeDtypeStruct((rows, lanes), jnp.float32),
+        in_specs=[pl.BlockSpec(memory_space=pltpu.VMEM)],
+        out_specs=pl.BlockSpec(memory_space=pltpu.VMEM),
+        scratch_shapes=[
+            pltpu.VMEM((2, 2, size, lanes), jnp.float32),
+            pltpu.SemaphoreType.DMA((2, 2)),
+            pltpu.SemaphoreType.DMA((2, 2)),
+            pltpu.SemaphoreType.REGULAR((2,)),
+            pltpu.SemaphoreType.REGULAR((2,)),
+            pltpu.SemaphoreType.DMA((2, n - 1)),
+            pltpu.SemaphoreType.DMA((2, n - 1)),
+        ],
+        compiler_params=pltpu.CompilerParams(collective_id=0, has_side_effects=True),
+    )(x)
+
+
+def sum_over_seq(parts):
+    n = lax.axis_size("seq")
+    flat = jnp.concatenate([part.reshape(-1) for part in parts])
+    grain = 2 * n * 8 * 128
+    padded = -(-flat.size // grain) * grain
+    flat = jnp.pad(flat, (0, padded - flat.size)).reshape(padded // 128, 128)
+    total = ring_sum(flat, n).reshape(-1)
+    pieces = []
+    start = 0
+    for part in parts:
+        pieces.append(total[start : start + part.size].reshape(part.shape))
+        start += part.size
+    return pieces
 
 
 def update(weight, gradient, velocity, average, rate, decay):
@@ -263,9 +402,7 @@
     stacked_gate = jnp.stack([entry[2] for entry in layer_grads])
     stacked_feature = jnp.stack([entry[3] for entry in layer_grads])
     stacked_state = jnp.stack([entry[4] for entry in layer_grads])
-    summed = lax.psum(
-        (stacked_in, stacked_out, stacked_gate, stacked_feature, stacked_state), "seq"
-    )
+    summed = sum_over_seq((stacked_in, stacked_out, stacked_gate, stacked_feature, stacked_state))
     factor = 1.0 / math.sqrt(count * lax.axis_size("seq"))
     grad_in = summed[0] * factor
     grad_out = summed[1] * factor

time: 319 us -> 309 us (0.969)
  Pallas kernels: 39.9 us -> 126 us
  waiting for transfers between devices: 83.3 us -> 15.8 us
  blocking collectives: 63.5 us -> 24.6 us
  local copies, waits for them, and re-layouts: 28.9 us -> 34.9 us
    pallas_call x0 -> x1, Pallas kernels: none -> 85.5 us  [ring_sum(): pl.pallas_call(lambda *refs: ring_sum_kernel(n, *refs), out_shape=jax.Sha...]
    psum x1 -> x0, waiting for transfers between devices: 67.5 us -> none  [body(): lax.psum((stacked_in, stacked_out, stacked_gate, stacked_feature, stacked...]
    psum x1 -> x0, blocking collectives: 38.9 us -> none  [body(): lax.psum((stacked_in, stacked_out, stacked_gate, stacked_feature, stacked...]
    mul x0 -> x5, other arithmetic: none -> 7.46 us  [the longest x1 2.65 us: body(): grad_in = summed[0] * factor]
    unnamed x130 -> x142, local copies, waits for them, and re-layouts: 14 us -> 15.9 us
  transfers between devices with their start and end apart: 4 -> 3, of which waited for: 3 -> 2; matrix products, arithmetic and copies ran while one was open for 12% -> 7% of each run, Pallas kernels for 3% -> 3%
where the time goes in v3:
time: 309 us; the launch traced here: 308 us
  Pallas kernels  126 us (41%)
  other arithmetic  46.6 us (15%)
  matrix products  46 us (15%)
  local copies, waits for them, and re-layouts  34.9 us (11%)
  blocking collectives  24.6 us (8%)
  waiting for transfers between devices  15.8 us (5%)
  between operations  14.6 us (5%)
    pallas_call x1, Pallas kernels, ring_sum(): pl.pallas_call(lambda *refs: ring_sum_kernel(n, *refs), out_shape=jax.Sha...  85.5 us
    pallas_call x4, Pallas kernels, recurrence(): pl.pallas_call(recurrence_kernel, out_shape=jax.ShapeDtypeStruct((count,...  40 us
    all_gather x3, blocking collectives, gather_feat(): return lax.all_gather(value, 'feat', axis=axis, tiled=True)  24.6 us
    unnamed x142, local copies, waits for them, and re-layouts  15.9 us
    all_gather x3, waiting for transfers between devices, gather_feat(): return lax.all_gather(value, 'feat', axis=axis, tiled=True)  15.7 us
    dot_general x2, matrix products, body(): jnp.dot(states_low, out_low, preferred_element_type=jnp.float32)  13.3 us
    dot_general x4, matrix products, contract_cols(): lax.dot_general(left, right, (((1,), (1,)), ((), ())), preferred_element_...  10.2 us
    slice x2, local copies, waits for them, and re-layouts, body(): states[1:, 3 * width:]  9.82 us
  transfers between devices with their start and end apart: 3, of which 2 were waited for; matrix products, arithmetic and copies ran while one was open for 7% of the time, Pallas kernels for 3%

profile of v3, /device:TPU:0, one launch (start us, length us, event | category | flops | bytes accessed | tf_op | source)
XLA Modules:
  0.0 308.1 jit_solution(17771296343817341614)
XLA Ops:
  7.2 2.0 convert_element_type.72
  11.5 10.0 %all_gather.18 = bf16[768,512]{1,0:T(8,128)(2,1)S(1)} all-gather(bf16[768,128]{1,0:T(8,128)(2,1)S(1)} %copy-done.48), channel_id=1, replica_groups=mesh['seq'=8,'feat'=4] {'feat'}, dimensions={1}, use_global_device_ids=true | all-gather | bytes 983040 | tf_op jit(solution)/shard_map/all_gather | solution.py:260
  22.1 5.2 %all_gather.19 = f32[2,4,512]{2,1,0:T(4,128)S(1)} all-gather(f32[2,4,128]{2,1,0:T(4,128)S(1)} %copy-done.54), channel_id=1, replica_groups=mesh['seq'=8,'feat'=4] {'feat'}, dimensions={2}, use_global_device_ids=true | all-gather | bytes 20480 | tf_op jit(solution)/shard_map/all_gather | solution.py:260
  27.3 9.4 %all_gather.23 = bf16[768,512]{1,0:T(8,128)(2,1)} all-gather(bf16[768,128]{1,0:T(8,128)(2,1)S(1)} %copy-done.49), channel_id=1, replica_groups=mesh['seq'=8,'feat'=4] {'feat'}, dimensions={1}, use_global_device_ids=true | all-gather | bytes 983040 | tf_op jit(solution)/shard_map/all_gather | solution.py:260
  36.9 1.2 fusion.17
  39.5 2.2 fusion.23
  42.2 1.6 pad_maximum_fusion.xa_ref.xb_ref
  43.8 10.0 %shard_map.354 = f32[768,1536]{1,0:T(8,128)} custom-call(f32[768]{0:T(1024)} %copy-done.52, f32[768]{0:T(1024)} %copy-done.50, f32[2,384]{1,0:T(2,128)} %get-tuple-element.209.w_ref, f32[768,768]{1,0:T(8,128)} %pad_maximum_fusion.xa_ref.xb_ref, f32[768,768]{1,0:T(8,128)} %pad_maximum_fusion.xa_ref.xb_ref), custom_call_target="tpu_custom_call" | custom-call | flops 11796480 | bytes 9437184 | tf_op jit(solution)/shard_map/pallas_call | solution.py:82
  53.8 4.8 %fusion.104 = (f32[767,384]{1,0:T(8,128)}, f32[767,384]{1,0:T(8,128)}, f32[767,384]{1,0:T(8,128)}, f32[767,384]{1,0:T(8,128)}) fusion(f32[768,1536]{1,0:T(8,128)} %shard_map.354), kind=kLoop, calls=%fused_computation.333 | loop fusion | bytes 9424896 | tf_op jit(solution)/shard_map/slice | solution.py:384
  58.6 5.2 %all-gather.6.cloned.1.call-done = bf16[2,1536,512]{2,1,0:T(8,128)(2,1)} async-done(((bf16[2,1536,128]{2,1,0:T(8,128)(2,1)}), bf16[2,1536,512]{2,1,0:T(8,128)(2,1)}) %all-gather.6.cloned.1.call-update) | async-done | bytes 3145744 | tf_op jit(solution)/shard_map/all_gather | solution.py:260
  63.7 8.5 %multiply_multiply_fusion.11 = (f32[768,512]{1,0:T(8,128)}, f32[768,512]{1,0:T(8,128)}) fusion(f32[512]{0:T(512)S(1)} %bitcast.476, f32[512]{0:T(512)S(1)} %bitcast.479, f32[768]{0:T(1024)S(1)} %add_rsqrt_fusion.1, f32[768]{0:T(1024)S(1)} %broadcast_multiply_fusion.6, bf16[768,512]{1,0:T(8,128)(2,1)S(1)} %all_gather.18, f32[512]{0:T(512)S(1)} %bitcast.485, ...), kind=kOutput, calls=%fused_computation.74 | convolution fusion | flops 1237057536 | bytes 10235904 | tf_op jit(solution)/shard_map/dot_general | solution.py:332
  72.2 10.5 %all-gather.8.cloned.1.call-done = bf16[2,512,512]{2,1,0:T(8,128)(2,1)} async-done(((bf16[2,512,128]{2,1,0:T(8,128)(2,1)}), bf16[2,512,512]{2,1,0:T(8,128)(2,1)}) %all-gather.8.cloned.1.call-update) | async-done | bytes 1048592 | tf_op jit(solution)/shard_map/all_gather | solution.py:260
  82.8 4.1 %fusion.103 = (f32[768]{0:T(1024)S(1)}, f32[768,512]{1,0:T(8,128)S(1)}, f32[768,512]{1,0:T(8,128)}) fusion(f32[768,512]{1,0:T(8,128)} %get-tuple-element.215, bf16[768,512]{1,0:T(8,128)(2,1)S(1)} %all_gather.18, f32[512]{0:T(512)S(1)} %bitcast.490, bf16[2,512,512]{2,1,0:T(8,128)(2,1)} %all-gather.8.cloned.1.call-done), kind=kOutput, calls=%fused_computation.332 | convolution fusion | flops 406191360 | bytes 7607296 | tf_op jit(solution)/shard_map/dot_general | solution.py:337
  91.1 1.6 pad_maximum_fusion.1.xa_ref.xb_ref
  92.7 10.1 %shard_map.355 = f32[768,1536]{1,0:T(8,128)} custom-call(f32[768]{0:T(1024)} %copy-done.52, f32[768]{0:T(1024)} %copy-done.50, f32[2,384]{1,0:T(2,128)} %get-tuple-element.225.w_ref, f32[768,768]{1,0:T(8,128)} %pad_maximum_fusion.1.xa_ref.xb_ref, f32[768,768]{1,0:T(8,128)} %pad_maximum_fusion.1.xa_ref.xb_ref), custom_call_target="tpu_custom_call" | custom-call | flops 11796480 | bytes 9437184 | tf_op jit(solution)/shard_map/pallas_call | solution.py:82
  102.8 5.0 %fusion.105 = (f32[767,384]{1,0:T(8,128)}, f32[767,384]{1,0:T(8,128)}, f32[767,384]{1,0:T(8,128)}, f32[767,384]{1,0:T(8,128)}) fusion(f32[768,1536]{1,0:T(8,128)} %shard_map.355), kind=kLoop, calls=%fused_computation.334 | loop fusion | bytes 9424896 | tf_op jit(solution)/shard_map/slice | solution.py:384
  109.7 4.8 %multiply_multiply_fusion.10 = (f32[768,512]{1,0:T(8,128)S(1)}, f32[768,512]{1,0:T(8,128)S(1)}, f32[768,512]{1,0:T(8,128)S(1)}) fusion(f32[512]{0:T(512)S(1)} %bitcast.482, f32[512]{0:T(512)S(1)} %bitcast.469, f32[768]{0:T(1024)S(1)} %add_rsqrt_fusion, f32[768,512]{1,0:T(8,128)S(1)} %copy-done.4, f32[768]{0:T(1024)S(1)} %broadcast_multiply_fusion.5, ...), kind=kOutput, calls=%fused_computation.72 | convolution fusion | flops 1236664320 | bytes 12597248 | tf_op jit(solution)/shard_map/dot_general | solution.py:332
  116.2 2.4 fusion.110
  118.6 1.7 convolution_bitcast_fusion
  120.3 1.4 fusion.16
  121.7 2.5 fusion.107
  124.2 10.0 %shard_map.356 = f32[768,1536]{1,0:T(8,128)} custom-call(f32[768]{0:T(1024)} %get-tuple-element.227.ma_ref, f32[768]{0:T(1024)} %get-tuple-element.228.mb_ref, f32[2,384]{1,0:T(2,128)} %get-tuple-element.226.w_ref, f32[768,768]{1,0:T(8,128)} %get-tuple-element.178.xa_ref, f32[768,768]{1,0:T(8,128)} %get-tuple-element.177.xb_ref), custom_call_target="tpu_custom_call" | custom-call | flops 11796480 | bytes 9437184 | tf_op jit(solution)/shard_map/pallas_call | solution.py:82
  134.2 4.8 %add_reduce_fusion = (f32[384]{0:T(512)S(1)}, f32[384]{0:T(512)S(1)}, bf16[768,384]{1,0:T(8,128)(2,1)S(1)}, f32[768,384]{1,0:T(8,128)S(1)}, f32[768,384]{1,0:T(8,128)S(1)}) fusion(f32[767,384]{1,0:T(8,128)} %get-tuple-element.174, f32[767,384]{1,0:T(8,128)} %get-tuple-element.173, f32[767,384]{1,0:T(8,128)} %get-tuple-element.172, ...), kind=kLoop, calls=%fused_computation.84 | loop fusion | flops 7961856 | bytes 12395520 | tf_op jit(solution)/shard_map/reduce_sum | solution.py:385
  140.7 2.2 convolution_bitcast_fusion.2
  143.0 1.4 multiply_reduce_fusion.1
  145.1 1.1 convert_reduce_fusion.2
  146.3 1.1 convolution_bitcast_fusion.5
  147.4 1.3 copy-done.47
  148.7 4.9 %fusion.111 = (bf16[768,512]{1,0:T(8,128)(2,1)S(1)}, f32[768,512]{1,0:T(8,128)}) fusion(f32[768,512]{1,0:T(8,128)S(1)} %copy-done.64, bf16[768,512]{1,0:T(8,128)(2,1)S(1)} %get-tuple-element.146, bf16[2,512,512]{2,1,0:T(8,128)(2,1)S(1)} %copy-done.47, f32[768,512]{1,0:T(8,128)S(1)} %get-tuple-element.147, f32[768,512]{1,0:T(8,128)S(1)} %copy-done.34), kind=kOutput, calls=%fused_computation.340 | convolution fusion | flops 431751168 | bytes 8388608 | tf_op jit(solution)/shard_map/dot_general | solution.py:254
  153.6 1.7 convolution_bitcast_fusion.1
  155.7 1.4 fusion.15
  157.1 2.6 fusion.106
  159.6 9.9 %shard_map.357 = f32[768,1536]{1,0:T(8,128)} custom-call(f32[768]{0:T(1024)} %get-tuple-element.227.ma_ref, f32[768]{0:T(1024)} %get-tuple-element.228.mb_ref, f32[2,384]{1,0:T(2,128)} %get-tuple-element.208.w_ref, f32[768,768]{1,0:T(8,128)} %get-tuple-element.176.xa_ref, f32[768,768]{1,0:T(8,128)} %get-tuple-element.175.xb_ref), custom_call_target="tpu_custom_call" | custom-call | flops 11796480 | bytes 9437184 | tf_op jit(solution)/shard_map/pallas_call | solution.py:82
  169.6 5.4 %subtract_reduce_fusion.2 = (f32[384]{0:T(512)S(1)}, f32[384]{0:T(512)S(1)}, f32[384]{0:T(512)S(1)}, f32[384]{0:T(512)S(1)}, f32[768,384]{1,0:T(8,128)}, /*index=5*/f32[768,384]{1,0:T(8,128)}) fusion(f32[768,768]{1,0:T(8,128)S(1)} %fusion.23, f32[768]{0:T(1024)S(1)} %get-tuple-element.212, f32[768,384]{1,0:T(8,128)} %copy-done.6, f32[768,768]{1,0:T(8,128)} %copy-done.2, ...), kind=kLoop, calls=%fused_computation.94 | loop fusion | flops 6486528 | bytes 14164992 | tf_op jit(solution)/shard_map/reduce_sum | solution.py:379
  176.9 1.7 add_reduce_fusion.2
  179.7 1.6 convolution_bitcast_fusion.3
  183.0 4.1 %fusion.96 = (f32[512]{0:T(512)S(1)}, f32[512]{0:T(512)S(1)}, f32[512]{0:T(512)S(1)}, f32[768]{0:T(1024)S(1)}, f32[768]{0:T(1024)S(1)}, /*index=5*/f32[768,512]{1,0:T(8,128)}, f32[768,512]{1,0:T(8,128)}) fusion(f32[768]{0:T(1024)S(1)} %add_rsqrt_fusion.1, f32[768]{0:T(1024)S(1)} %broadcast_multiply_fusion.6, bf16[768,512]{1,0:T(8,128)(2,1)S(1)} %all_gather.18, ...), kind=kOutput, calls=%fused_computation.328 | convolution fusion | flops 612627456 | bytes 7497728 | tf_op jit(solution)/shard_map/dot_general | solution.py:389
  188.5 1.8 pad_bitcast_fusion.refs_0_
  190.3 85.5 %shard_map.358 = f32[5760,128]{1,0:T(8,128)} custom-call(f32[5760,128]{1,0:T(8,128)} %pad_bitcast_fusion.refs_0_), custom_call_target="tpu_custom_call" | custom-call | tf_op jit(solution)/shard_map/pallas_call | solution.py:205
  275.9 1.5 slice_multiply_fusion
  277.4 2.6 slice_multiply_fusion.1
  280.1 1.9 slice_multiply_fusion.2
  283.4 2.2 dynamic-slice_add_fusion.1
  285.5 2.2 mul.2220
  290.2 4.7 %add_multiply_fusion = (f32[2,1536,128]{2,1,0:T(8,128)}, f32[2,1536,128]{2,1,0:T(8,128)}, f32[2,1536,128]{2,1,0:T(8,128)}) fusion(f32[2,1536,128]{2,1,0:T(8,128)} %param.34, f32[2,1536,128]{2,1,0:T(8,128)S(1)} %copy-done.11, f32[2,1536,128]{2,1,0:T(8,128)S(1)} %bitcast.462, f32[2,1536,128]{2,1,0:T(8,128)} %param.29), kind=kLoop, calls=%fused_computation.18 | loop fusion | flops 3932160 | bytes 11010048 | tf_op jit(solution)/shard_map/add | solution.py:243
  294.9 1.6 add_multiply_fusion.3
  297.3 1.3 add_multiply_fusion.4
  299.2 2.4 dynamic-slice_add_fusion
  (203 shorter events, 26.1 us)
Async XLA Ops:
  7.2 2.2 copy-start.10
  7.2 32.3 %all-gather.4.cloned.1.call-start = ((), (), s32[]{:S(2)}) async-start(), calls=%async_computation | async-start | bytes 1966080 | tf_op jit(solution)/shard_map/all_gather | solution.py:260
  9.3 2.1 copy-start.48
  9.3 54.4 %all-gather.6.cloned.1.call-start = ((), (), s32[]{:S(2)}) async-start(), calls=%async_computation.1 | async-start | bytes 3932160 | tf_op jit(solution)/shard_map/all_gather | solution.py:260
  10.4 72.4 %all-gather.8.cloned.1.call-start = ((), (), s32[]{:S(2)}) async-start(), calls=%async_computation.2 | async-start | bytes 1310720 | tf_op jit(solution)/shard_map/all_gather | solution.py:260
  11.2 10.9 %copy-start.54 = (f32[2,4,128]{2,1,0:T(4,128)S(1)}, f32[2,4,128]{2,1,0:T(4,128)}, u32[]{:S(2)}) copy-start(f32[2,4,128]{2,1,0:T(4,128)} %param.26) | copy-start | bytes 12292
  11.2 16.1 %copy-start.49 = (bf16[768,128]{1,0:T(8,128)(2,1)S(1)}, bf16[768,128]{1,0:T(8,128)(2,1)}, u32[]{:S(2)}) copy-start(bf16[768,128]{1,0:T(8,128)(2,1)} %param.20) | copy-start | bytes 589828
  11.4 25.3 %copy-start.60 = (s32[2]{0:T(128)S(1)}, s32[2]{0:T(128)}, u32[]{:S(2)}) copy-start(s32[2]{0:T(128)} %param.21) | copy-start | bytes 28
  11.4 25.3 %copy-start.61 = (s32[2]{0:T(128)S(1)}, s32[2]{0:T(128)}, u32[]{:S(2)}) copy-start(s32[2]{0:T(128)} %param.22) | copy-start | bytes 28
  36.8 5.0 %copy-start.50 = (f32[768]{0:T(1024)}, f32[768]{0:T(1024)S(1)}, u32[]{:S(2)}) copy-start(f32[768]{0:T(1024)S(1)} %get-tuple-element.213.mb_ref) | copy-start | bytes 9220
  36.8 5.0 %copy-start.52 = (f32[768]{0:T(1024)}, f32[768]{0:T(1024)S(1)}, u32[]{:S(2)}) copy-start(f32[768]{0:T(1024)S(1)} %get-tuple-element.214.ma_ref) | copy-start | bytes 9220
  102.8 5.0 %copy-start.1 = (f32[768,1536]{1,0:T(8,128)S(1)}, f32[768,1536]{1,0:T(8,128)}, u32[]{:S(2)}) copy-start(f32[768,1536]{1,0:T(8,128)} %shard_map.355) | copy-start | bytes 14155780
  102.8 6.0 %copy-start.4 = (f32[768,512]{1,0:T(8,128)S(1)}, f32[768,512]{1,0:T(8,128)}, u32[]{:S(2)}) copy-start(f32[768,512]{1,0:T(8,128)} %copy-done.3) | copy-start | bytes 4718596
  102.8 6.9 %copy-start.62 = (bf16[2,1536,512]{2,1,0:T(8,128)(2,1)S(1)}, bf16[2,1536,512]{2,1,0:T(8,128)(2,1)}, u32[]{:S(2)}) copy-start(bf16[2,1536,512]{2,1,0:T(8,128)(2,1)} %all-gather.6.cloned.1.call-done) | copy-start | bytes 9437188
  109.7 4.9 %copy-start.8 = (bf16[768,512]{1,0:T(8,128)(2,1)S(1)}, bf16[768,512]{1,0:T(8,128)(2,1)}, u32[]{:S(2)}) copy-start(bf16[768,512]{1,0:T(8,128)(2,1)} %all_gather.23) | copy-start | bytes 2359300
  109.7 4.9 %copy-start.46 = (bf16[2,512,512]{2,1,0:T(8,128)(2,1)S(1)}, bf16[2,512,512]{2,1,0:T(8,128)(2,1)}, u32[]{:S(2)}) copy-start(bf16[2,512,512]{2,1,0:T(8,128)(2,1)} %all-gather.8.cloned.1.call-done) | copy-start | bytes 3145732
  115.7 2.9 copy-start.26
  124.2 10.0 %copy-start.51 = (f32[768]{0:T(1024)S(1)}, f32[768]{0:T(1024)}, u32[]{:S(2)}) copy-start(f32[768]{0:T(1024)} %copy-done.50) | copy-start | bytes 9220
  124.2 10.0 %copy-start.53 = (f32[768]{0:T(1024)S(1)}, f32[768]{0:T(1024)}, u32[]{:S(2)}) copy-start(f32[768]{0:T(1024)} %copy-done.52) | copy-start | bytes 9220
  140.4 2.6 copy-start.32
  140.4 2.6 copy-start.35
  140.7 2.2 copy-start.5
  143.0 2.1 copy-start.34
  145.1 2.3 copy-start.64
  145.1 8.5 %slice-start = ((s8[4718592]{0:T(1024)(128)(4,1)}), s8[4194304]{0:T(1024)(128)(4,1)S(1)}, s32[]{:S(2)}) async-start(s8[4718592]{0:T(1024)(128)(4,1)} %bitcast.459), calls=%async_computation.3 | async-start | bytes 8388608
  146.2 7.4 %copy-start.27 = (f32[768,512]{1,0:T(8,128)}, f32[768,512]{1,0:T(8,128)S(1)}, u32[]{:S(2)}) copy-start(f32[768,512]{1,0:T(8,128)S(1)} %get-tuple-element.147) | copy-start | bytes 4718596
  146.2 2.4 copy-start.47
  148.7 5.0 %slice-start.1 = ((s8[4718592]{0:T(1024)(128)(4,1)}), s8[524288]{0:T(1024)(128)(4,1)S(1)}, s32[]{:S(2)}) async-start(s8[4718592]{0:T(1024)(128)(4,1)} %bitcast.459), calls=%async_computation.4 | async-start | bytes 1048576
  153.6 2.1 copy-start.63
  169.5 6.0 %copy-start = (f32[768,1536]{1,0:T(8,128)S(1)}, f32[768,1536]{1,0:T(8,128)}, u32[]{:S(2)}) copy-start(f32[768,1536]{1,0:T(8,128)} %shard_map.357) | copy-start | bytes 14155780
  169.5 6.3 %copy-start.16 = (f32[767,384]{1,0:T(8,128)S(1)}, f32[767,384]{1,0:T(8,128)}, u32[]{:S(2)}) copy-start(f32[767,384]{1,0:T(8,128)} %get-tuple-element.164) | copy-start | bytes 3534340
  169.5 6.7 %copy-start.17 = (f32[767,384]{1,0:T(8,128)S(1)}, f32[767,384]{1,0:T(8,128)}, u32[]{:S(2)}) copy-start(f32[767,384]{1,0:T(8,128)} %get-tuple-element.165) | copy-start | bytes 3534340
  169.6 7.0 %copy-start.18 = (f32[767,384]{1,0:T(8,128)S(1)}, f32[767,384]{1,0:T(8,128)}, u32[]{:S(2)}) copy-start(f32[767,384]{1,0:T(8,128)} %get-tuple-element.166) | copy-start | bytes 3534340
  169.6 7.3 %copy-start.19 = (f32[767,384]{1,0:T(8,128)S(1)}, f32[767,384]{1,0:T(8,128)}, u32[]{:S(2)}) copy-start(f32[767,384]{1,0:T(8,128)} %get-tuple-element.167) | copy-start | bytes 3534340
  176.9 2.3 copy-start.14
  176.9 2.3 copy-start.15
  183.0 4.3 %copy-start.36 = (f32[1,512,128]{2,1,0:T(8,128)S(1)}, f32[1,512,128]{2,1,0:T(8,128)}, u32[]{:S(2)}) copy-start(f32[1,512,128]{2,1,0:T(8,128)} %convolution_bitcast_fusion.5) | copy-start | bytes 786436
  183.0 4.3 %copy-start.23 = (f32[1,1536,128]{2,1,0:T(8,128)S(1)}, f32[1,1536,128]{2,1,0:T(8,128)}, u32[]{:S(2)}) copy-start(f32[1,1536,128]{2,1,0:T(8,128)} %convolution_bitcast_fusion.1) | copy-start | bytes 2359300
  277.4 12.7 %copy-start.13 = (f32[3072,128]{1,0:T(8,128)}, f32[3072,128]{1,0:T(8,128)S(1)}, u32[]{:S(2)}) copy-start(f32[3072,128]{1,0:T(8,128)S(1)} %slice_multiply_fusion) | copy-start | bytes 4718596
  283.3 15.2 %copy-start.55 = (f32[8,128]{1,0:T(8,128)}, f32[8,128]{1,0:T(8,128)S(1)}, u32[]{:S(2)}) copy-start(f32[8,128]{1,0:T(8,128)S(1)} %slice_multiply_fusion.4) | copy-start | bytes 12292
  283.3 5.0 %copy-start.56 = (f32[2,3,384]{2,0,1:T(2,128)S(1)}, f32[2,3,384]{2,0,1:T(2,128)}, u32[]{:S(2)}) copy-start(f32[2,3,384]{2,0,1:T(2,128)} %param.37) | copy-start | bytes 27652
  283.3 5.0 %copy-start.57 = (f32[2,3,384]{2,0,1:T(2,128)S(1)}, f32[2,3,384]{2,0,1:T(2,128)}, u32[]{:S(2)}) copy-start(f32[2,3,384]{2,0,1:T(2,128)} %param.32) | copy-start | bytes 27652
  283.3 6.8 %copy-start.11 = (f32[2,1536,128]{2,1,0:T(8,128)S(1)}, f32[2,1536,128]{2,1,0:T(8,128)}, u32[]{:S(2)}) copy-start(f32[2,1536,128]{2,1,0:T(8,128)} %param.24) | copy-start | bytes 4718596
  290.2 4.7 %copy-start.20 = (f32[2,128,768]{2,1,0:T(8,128)S(1)}, f32[2,128,768]{2,1,0:T(8,128)}, u32[]{:S(2)}) copy-start(f32[2,128,768]{2,1,0:T(8,128)} %param.23) | copy-start | bytes 2359300
  290.2 4.7 %copy-start.21 = (f32[2,128,768]{2,1,0:T(8,128)S(1)}, f32[2,128,768]{2,1,0:T(8,128)}, u32[]{:S(2)}) copy-start(f32[2,128,768]{2,1,0:T(8,128)} %mul.2220) | copy-start | bytes 2359300
  290.2 4.7 %copy-start.37 = (f32[2,128,768]{2,1,0:T(8,128)S(1)}, f32[2,128,768]{2,1,0:T(8,128)}, u32[]{:S(2)}) copy-start(f32[2,128,768]{2,1,0:T(8,128)} %param.33) | copy-start | bytes 2359300
  290.2 4.7 %copy-start.38 = (f32[2,128,768]{2,1,0:T(8,128)S(1)}, f32[2,128,768]{2,1,0:T(8,128)}, u32[]{:S(2)}) copy-start(f32[2,128,768]{2,1,0:T(8,128)} %param.28) | copy-start | bytes 2359300
  294.9 2.3 copy-start.43
  (22 other events, 31.4 us)
Sparse Core Ops, SparseCore 0:
  10.2 22.6 all-gather.3
  35.0 28.6 all-gather.5
  65.9 16.8 all-gather.7

commit v4 on v3

--- a/solution.py
+++ b/solution.py
@@ -109,7 +109,7 @@
     return (1 - odd) * (index // 2) + odd * (n - 1 - index // 2)
 
 
-def ring_sum_kernel(n, x_ref, o_ref, slots, rs_send, rs_recv, credit, done, ag_send, ag_recv):
+def ring_sum_kernel(n, x_ref, r_ref, o_ref, slots, rs_send, rs_recv, credit, done, ag_send, ag_recv):
     rows = x_ref.shape[0]
     half = rows // 2
     size = half // n
@@ -164,13 +164,16 @@
     for ring, place, target, source in rings:
         pl.semaphore_signal(done.at[ring], 1, device_id={"seq": source}, device_id_type=MESH)
     for ring, place, target, source in rings:
+        final = block(ring, (place + 1) % n)
+        r_ref[final] = o_ref[final].astype(r_ref.dtype)
+    for ring, place, target, source in rings:
         pl.semaphore_wait(done.at[ring], 1)
 
     def gather_copy(ring, place, target, s):
         where = block(ring, (place + 1 - s + n) % n)
         return pltpu.make_async_remote_copy(
-            src_ref=o_ref.at[where],
-            dst_ref=o_ref.at[where],
+            src_ref=r_ref.at[where],
+            dst_ref=r_ref.at[where],
             send_sem=ag_send.at[ring, s],
             recv_sem=ag_recv.at[ring, s],
             device_id={"seq": target},
@@ -204,10 +207,11 @@
     size = rows // (2 * n)
     return pl.pallas_call(
         lambda *refs: ring_sum_kernel(n, *refs),
-        out_shape=jax.ShapeDtypeStruct((rows, lanes), jnp.float32),
+        out_shape=jax.ShapeDtypeStruct((rows, lanes), jnp.bfloat16),
         in_specs=[pl.BlockSpec(memory_space=pltpu.VMEM)],
         out_specs=pl.BlockSpec(memory_space=pltpu.VMEM),
         scratch_shapes=[
+            pltpu.VMEM((rows, lanes), jnp.float32),
             pltpu.VMEM((2, 2, size, lanes), jnp.float32),
             pltpu.SemaphoreType.DMA((2, 2)),
             pltpu.SemaphoreType.DMA((2, 2)),
@@ -223,10 +227,10 @@
 def sum_over_seq(parts):
     n = lax.axis_size("seq")
     flat = jnp.concatenate([part.reshape(-1) for part in parts])
-    grain = 2 * n * 8 * 128
+    grain = 2 * n * 16 * 128
     padded = -(-flat.size // grain) * grain
     flat = jnp.pad(flat, (0, padded - flat.size)).reshape(padded // 128, 128)
-    total = ring_sum(flat, n).reshape(-1)
+    total = ring_sum(flat, n).astype(jnp.float32).reshape(-1)
     pieces = []
     start = 0
     for part in parts:

time: 309 us -> 292 us (0.945)
  Pallas kernels: 126 us -> 113 us
  other arithmetic: 46.6 us -> 42.7 us
    pallas_call x1, Pallas kernels: 85.5 us -> 72.7 us  [ring_sum(): pl.pallas_call(lambda *refs: ring_sum_kernel(n, *refs), out_shape=jax.Sha...]
  transfers between devices with their start and end apart: 3 -> 3, of which waited for: 2 -> 2; matrix products, arithmetic and copies ran while one was open for 7% -> 8% of each run, Pallas kernels for 3% -> 3%
where the time goes in v4:
time: 292 us; the launch traced here: 291 us
  Pallas kernels  113 us (39%)
  matrix products  46 us (16%)
  other arithmetic  42.7 us (15%)
  local copies, waits for them, and re-layouts  34.9 us (12%)
  blocking collectives  24.6 us (8%)
  waiting for transfers between devices  15.8 us (5%)
  between operations  14.6 us (5%)
    pallas_call x1, Pallas kernels, ring_sum(): pl.pallas_call(lambda *refs: ring_sum_kernel(n, *refs), out_shape=jax.Sha...  72.7 us
    pallas_call x4, Pallas kernels, recurrence(): pl.pallas_call(recurrence_kernel, out_shape=jax.ShapeDtypeStruct((count,...  40 us
    all_gather x3, blocking collectives, gather_feat(): return lax.all_gather(value, 'feat', axis=axis, tiled=True)  24.6 us
    unnamed x142, local copies, waits for them, and re-layouts  15.9 us
    all_gather x3, waiting for transfers between devices, gather_feat(): return lax.all_gather(value, 'feat', axis=axis, tiled=True)  15.7 us
    dot_general x2, matrix products, body(): jnp.dot(states_low, out_low, preferred_element_type=jnp.float32)  13.3 us
    dot_general x4, matrix products, contract_cols(): lax.dot_general(left, right, (((1,), (1,)), ((), ())), preferred_element_...  10.2 us
    slice x2, local copies, waits for them, and re-layouts, body(): states[1:, 3 * width:]  9.82 us
  transfers between devices with their start and end apart: 3, of which 2 were waited for; matrix products, arithmetic and copies ran while one was open for 8% of the time, Pallas kernels for 3%

profile of v4, /device:TPU:0, one launch (start us, length us, event | category | flops | bytes accessed | tf_op | source)
XLA Modules:
  0.0 291.4 jit_solution(6373282573095858636)
XLA Ops:
  7.2 2.0 convert_element_type.75
  11.5 10.0 %all_gather.18 = bf16[768,512]{1,0:T(8,128)(2,1)S(1)} all-gather(bf16[768,128]{1,0:T(8,128)(2,1)S(1)} %copy-done.48), channel_id=1, replica_groups=mesh['seq'=8,'feat'=4] {'feat'}, dimensions={1}, use_global_device_ids=true | all-gather | bytes 983040 | tf_op jit(solution)/shard_map/all_gather | solution.py:264
  22.1 5.2 %all_gather.19 = f32[2,4,512]{2,1,0:T(4,128)S(1)} all-gather(f32[2,4,128]{2,1,0:T(4,128)S(1)} %copy-done.54), channel_id=1, replica_groups=mesh['seq'=8,'feat'=4] {'feat'}, dimensions={2}, use_global_device_ids=true | all-gather | bytes 20480 | tf_op jit(solution)/shard_map/all_gather | solution.py:264
  27.3 9.4 %all_gather.23 = bf16[768,512]{1,0:T(8,128)(2,1)} all-gather(bf16[768,128]{1,0:T(8,128)(2,1)S(1)} %copy-done.49), channel_id=1, replica_groups=mesh['seq'=8,'feat'=4] {'feat'}, dimensions={1}, use_global_device_ids=true | all-gather | bytes 983040 | tf_op jit(solution)/shard_map/all_gather | solution.py:264
  36.9 1.2 fusion.17
  39.5 2.2 fusion.23
  42.2 1.6 pad_maximum_fusion.xa_ref.xb_ref
  43.8 10.0 %shard_map.354 = f32[768,1536]{1,0:T(8,128)} custom-call(f32[768]{0:T(1024)} %copy-done.52, f32[768]{0:T(1024)} %copy-done.50, f32[2,384]{1,0:T(2,128)} %get-tuple-element.209.w_ref, f32[768,768]{1,0:T(8,128)} %pad_maximum_fusion.xa_ref.xb_ref, f32[768,768]{1,0:T(8,128)} %pad_maximum_fusion.xa_ref.xb_ref), custom_call_target="tpu_custom_call" | custom-call | flops 11796480 | bytes 9437184 | tf_op jit(solution)/shard_map/pallas_call | solution.py:82
  53.8 4.8 %fusion.104 = (f32[767,384]{1,0:T(8,128)}, f32[767,384]{1,0:T(8,128)}, f32[767,384]{1,0:T(8,128)}, f32[767,384]{1,0:T(8,128)}) fusion(f32[768,1536]{1,0:T(8,128)} %shard_map.354), kind=kLoop, calls=%fused_computation.333 | loop fusion | bytes 9424896 | tf_op jit(solution)/shard_map/slice | solution.py:388
  58.6 5.2 %all-gather.6.cloned.1.call-done = bf16[2,1536,512]{2,1,0:T(8,128)(2,1)} async-done(((bf16[2,1536,128]{2,1,0:T(8,128)(2,1)}), bf16[2,1536,512]{2,1,0:T(8,128)(2,1)}) %all-gather.6.cloned.1.call-update) | async-done | bytes 3145744 | tf_op jit(solution)/shard_map/all_gather | solution.py:264
  63.7 8.5 %multiply_multiply_fusion.11 = (f32[768,512]{1,0:T(8,128)}, f32[768,512]{1,0:T(8,128)}) fusion(f32[512]{0:T(512)S(1)} %bitcast.476, f32[512]{0:T(512)S(1)} %bitcast.479, f32[768]{0:T(1024)S(1)} %add_rsqrt_fusion.1, f32[768]{0:T(1024)S(1)} %broadcast_multiply_fusion.6, bf16[768,512]{1,0:T(8,128)(2,1)S(1)} %all_gather.18, f32[512]{0:T(512)S(1)} %bitcast.485, ...), kind=kOutput, calls=%fused_computation.74 | convolution fusion | flops 1237057536 | bytes 10235904 | tf_op jit(solution)/shard_map/dot_general | solution.py:336
  72.2 10.5 %all-gather.8.cloned.1.call-done = bf16[2,512,512]{2,1,0:T(8,128)(2,1)} async-done(((bf16[2,512,128]{2,1,0:T(8,128)(2,1)}), bf16[2,512,512]{2,1,0:T(8,128)(2,1)}) %all-gather.8.cloned.1.call-update) | async-done | bytes 1048592 | tf_op jit(solution)/shard_map/all_gather | solution.py:264
  82.8 4.1 %fusion.103 = (f32[768]{0:T(1024)S(1)}, f32[768,512]{1,0:T(8,128)S(1)}, f32[768,512]{1,0:T(8,128)}) fusion(f32[768,512]{1,0:T(8,128)} %get-tuple-element.215, bf16[768,512]{1,0:T(8,128)(2,1)S(1)} %all_gather.18, f32[512]{0:T(512)S(1)} %bitcast.490, bf16[2,512,512]{2,1,0:T(8,128)(2,1)} %all-gather.8.cloned.1.call-done), kind=kOutput, calls=%fused_computation.332 | convolution fusion | flops 406191360 | bytes 7607296 | tf_op jit(solution)/shard_map/dot_general | solution.py:341
  90.1 1.0 copy-done.2
  91.1 1.6 pad_maximum_fusion.1.xa_ref.xb_ref
  92.7 10.1 %shard_map.355 = f32[768,1536]{1,0:T(8,128)} custom-call(f32[768]{0:T(1024)} %copy-done.52, f32[768]{0:T(1024)} %copy-done.50, f32[2,384]{1,0:T(2,128)} %get-tuple-element.225.w_ref, f32[768,768]{1,0:T(8,128)} %pad_maximum_fusion.1.xa_ref.xb_ref, f32[768,768]{1,0:T(8,128)} %pad_maximum_fusion.1.xa_ref.xb_ref), custom_call_target="tpu_custom_call" | custom-call | flops 11796480 | bytes 9437184 | tf_op jit(solution)/shard_map/pallas_call | solution.py:82
  102.8 5.0 %fusion.105 = (f32[767,384]{1,0:T(8,128)}, f32[767,384]{1,0:T(8,128)}, f32[767,384]{1,0:T(8,128)}, f32[767,384]{1,0:T(8,128)}) fusion(f32[768,1536]{1,0:T(8,128)} %shard_map.355), kind=kLoop, calls=%fused_computation.334 | loop fusion | bytes 9424896 | tf_op jit(solution)/shard_map/slice | solution.py:388
  109.7 4.8 %multiply_multiply_fusion.10 = (f32[768,512]{1,0:T(8,128)S(1)}, f32[768,512]{1,0:T(8,128)S(1)}, f32[768,512]{1,0:T(8,128)S(1)}) fusion(f32[512]{0:T(512)S(1)} %bitcast.482, f32[512]{0:T(512)S(1)} %bitcast.469, f32[768]{0:T(1024)S(1)} %add_rsqrt_fusion, f32[768,512]{1,0:T(8,128)S(1)} %copy-done.4, f32[768]{0:T(1024)S(1)} %broadcast_multiply_fusion.5, ...), kind=kOutput, calls=%fused_computation.72 | convolution fusion | flops 1236664320 | bytes 12597248 | tf_op jit(solution)/shard_map/dot_general | solution.py:336
  114.6 1.0 convert_reduce_fusion.1
  116.2 2.4 fusion.110
  118.6 1.7 convolution_bitcast_fusion
  120.3 1.4 fusion.16
  121.7 2.5 fusion.107
  124.2 10.0 %shard_map.356 = f32[768,1536]{1,0:T(8,128)} custom-call(f32[768]{0:T(1024)} %get-tuple-element.227.ma_ref, f32[768]{0:T(1024)} %get-tuple-element.228.mb_ref, f32[2,384]{1,0:T(2,128)} %get-tuple-element.226.w_ref, f32[768,768]{1,0:T(8,128)} %get-tuple-element.178.xa_ref, f32[768,768]{1,0:T(8,128)} %get-tuple-element.177.xb_ref), custom_call_target="tpu_custom_call" | custom-call | flops 11796480 | bytes 9437184 | tf_op jit(solution)/shard_map/pallas_call | solution.py:82
  134.2 4.8 %add_reduce_fusion = (f32[384]{0:T(512)S(1)}, f32[384]{0:T(512)S(1)}, bf16[768,384]{1,0:T(8,128)(2,1)S(1)}, f32[768,384]{1,0:T(8,128)S(1)}, f32[768,384]{1,0:T(8,128)S(1)}) fusion(f32[767,384]{1,0:T(8,128)} %get-tuple-element.174, f32[767,384]{1,0:T(8,128)} %get-tuple-element.173, f32[767,384]{1,0:T(8,128)} %get-tuple-element.172, ...), kind=kLoop, calls=%fused_computation.84 | loop fusion | flops 7961856 | bytes 12395520 | tf_op jit(solution)/shard_map/reduce_sum | solution.py:389
  140.7 2.2 convolution_bitcast_fusion.2
  143.0 1.4 multiply_reduce_fusion.1
  145.1 1.1 convert_reduce_fusion.2
  146.3 1.1 convolution_bitcast_fusion.5
  147.4 1.3 copy-done.47
  148.7 4.9 %fusion.111 = (bf16[768,512]{1,0:T(8,128)(2,1)S(1)}, f32[768,512]{1,0:T(8,128)}) fusion(f32[768,512]{1,0:T(8,128)S(1)} %copy-done.64, bf16[768,512]{1,0:T(8,128)(2,1)S(1)} %get-tuple-element.146, bf16[2,512,512]{2,1,0:T(8,128)(2,1)S(1)} %copy-done.47, f32[768,512]{1,0:T(8,128)S(1)} %get-tuple-element.147, f32[768,512]{1,0:T(8,128)S(1)} %copy-done.34), kind=kOutput, calls=%fused_computation.340 | convolution fusion | flops 431751168 | bytes 8388608 | tf_op jit(solution)/shard_map/dot_general | solution.py:258
  153.6 1.7 convolution_bitcast_fusion.1
  155.7 1.4 fusion.15
  157.1 2.6 fusion.106
  159.6 9.9 %shard_map.357 = f32[768,1536]{1,0:T(8,128)} custom-call(f32[768]{0:T(1024)} %get-tuple-element.227.ma_ref, f32[768]{0:T(1024)} %get-tuple-element.228.mb_ref, f32[2,384]{1,0:T(2,128)} %get-tuple-element.208.w_ref, f32[768,768]{1,0:T(8,128)} %get-tuple-element.176.xa_ref, f32[768,768]{1,0:T(8,128)} %get-tuple-element.175.xb_ref), custom_call_target="tpu_custom_call" | custom-call | flops 11796480 | bytes 9437184 | tf_op jit(solution)/shard_map/pallas_call | solution.py:82
  169.6 5.4 %subtract_reduce_fusion.2 = (f32[384]{0:T(512)S(1)}, f32[384]{0:T(512)S(1)}, f32[384]{0:T(512)S(1)}, f32[384]{0:T(512)S(1)}, f32[768,384]{1,0:T(8,128)}, /*index=5*/f32[768,384]{1,0:T(8,128)}) fusion(f32[768,768]{1,0:T(8,128)S(1)} %fusion.23, f32[768]{0:T(1024)S(1)} %get-tuple-element.212, f32[768,384]{1,0:T(8,128)} %copy-done.6, f32[768,768]{1,0:T(8,128)} %copy-done.2, ...), kind=kLoop, calls=%fused_computation.94 | loop fusion | flops 6486528 | bytes 14164992 | tf_op jit(solution)/shard_map/reduce_sum | solution.py:383
  176.9 1.7 add_reduce_fusion.2
  179.7 1.6 convolution_bitcast_fusion.3
  183.0 4.1 %fusion.96 = (f32[512]{0:T(512)S(1)}, f32[512]{0:T(512)S(1)}, f32[512]{0:T(512)S(1)}, f32[768]{0:T(1024)S(1)}, f32[768]{0:T(1024)S(1)}, /*index=5*/f32[768,512]{1,0:T(8,128)}, f32[768,512]{1,0:T(8,128)}) fusion(f32[768]{0:T(1024)S(1)} %add_rsqrt_fusion.1, f32[768]{0:T(1024)S(1)} %broadcast_multiply_fusion.6, bf16[768,512]{1,0:T(8,128)(2,1)S(1)} %all_gather.18, ...), kind=kOutput, calls=%fused_computation.328 | convolution fusion | flops 612627456 | bytes 7497728 | tf_op jit(solution)/shard_map/dot_general | solution.py:393
  188.5 1.8 pad_bitcast_fusion.refs_0_
  190.3 72.7 %shard_map.358 = bf16[5888,128]{1,0:T(8,128)(2,1)} custom-call(f32[5888,128]{1,0:T(8,128)} %pad_bitcast_fusion.refs_0_), custom_call_target="tpu_custom_call" | custom-call | tf_op jit(solution)/shard_map/pallas_call | solution.py:208
  263.0 1.6 convert_element_type.91
  266.7 2.2 dynamic-slice_add_fusion.1
  268.9 2.2 mul.2220
  273.5 4.7 %add_multiply_fusion = (f32[2,1536,128]{2,1,0:T(8,128)}, f32[2,1536,128]{2,1,0:T(8,128)}, f32[2,1536,128]{2,1,0:T(8,128)}) fusion(f32[2,1536,128]{2,1,0:T(8,128)} %param.34, f32[2,1536,128]{2,1,0:T(8,128)S(1)} %copy-done.11, f32[2,1536,128]{2,1,0:T(8,128)S(1)} %bitcast.462, f32[2,1536,128]{2,1,0:T(8,128)} %param.29), kind=kLoop, calls=%fused_computation.19 | loop fusion | flops 3932160 | bytes 11010048 | tf_op jit(solution)/shard_map/add | solution.py:247
  278.3 1.6 add_multiply_fusion.3
  280.6 1.3 add_multiply_fusion.4
  282.5 2.4 dynamic-slice_add_fusion
  (204 shorter events, 24.7 us)
Async XLA Ops:
  7.2 2.2 copy-start.10
  7.2 32.3 %all-gather.4.cloned.1.call-start = ((), (), s32[]{:S(2)}) async-start(), calls=%async_computation | async-start | bytes 1966080 | tf_op jit(solution)/shard_map/all_gather | solution.py:264
  9.3 2.1 copy-start.48
  9.3 54.4 %all-gather.6.cloned.1.call-start = ((), (), s32[]{:S(2)}) async-start(), calls=%async_computation.1 | async-start | bytes 3932160 | tf_op jit(solution)/shard_map/all_gather | solution.py:264
  10.4 72.4 %all-gather.8.cloned.1.call-start = ((), (), s32[]{:S(2)}) async-start(), calls=%async_computation.2 | async-start | bytes 1310720 | tf_op jit(solution)/shard_map/all_gather | solution.py:264
  11.2 10.9 %copy-start.54 = (f32[2,4,128]{2,1,0:T(4,128)S(1)}, f32[2,4,128]{2,1,0:T(4,128)}, u32[]{:S(2)}) copy-start(f32[2,4,128]{2,1,0:T(4,128)} %param.26) | copy-start | bytes 12292
  11.2 16.1 %copy-start.49 = (bf16[768,128]{1,0:T(8,128)(2,1)S(1)}, bf16[768,128]{1,0:T(8,128)(2,1)}, u32[]{:S(2)}) copy-start(bf16[768,128]{1,0:T(8,128)(2,1)} %param.20) | copy-start | bytes 589828
  11.4 25.3 %copy-start.60 = (s32[2]{0:T(128)S(1)}, s32[2]{0:T(128)}, u32[]{:S(2)}) copy-start(s32[2]{0:T(128)} %param.21) | copy-start | bytes 28
  11.4 25.3 %copy-start.61 = (s32[2]{0:T(128)S(1)}, s32[2]{0:T(128)}, u32[]{:S(2)}) copy-start(s32[2]{0:T(128)} %param.22) | copy-start | bytes 28
  36.8 5.0 %copy-start.50 = (f32[768]{0:T(1024)}, f32[768]{0:T(1024)S(1)}, u32[]{:S(2)}) copy-start(f32[768]{0:T(1024)S(1)} %get-tuple-element.213.mb_ref) | copy-start | bytes 9220
  36.8 5.0 %copy-start.52 = (f32[768]{0:T(1024)}, f32[768]{0:T(1024)S(1)}, u32[]{:S(2)}) copy-start(f32[768]{0:T(1024)S(1)} %get-tuple-element.214.ma_ref) | copy-start | bytes 9220
  102.8 5.0 %copy-start.1 = (f32[768,1536]{1,0:T(8,128)S(1)}, f32[768,1536]{1,0:T(8,128)}, u32[]{:S(2)}) copy-start(f32[768,1536]{1,0:T(8,128)} %shard_map.355) | copy-start | bytes 14155780
  102.8 6.0 %copy-start.4 = (f32[768,512]{1,0:T(8,128)S(1)}, f32[768,512]{1,0:T(8,128)}, u32[]{:S(2)}) copy-start(f32[768,512]{1,0:T(8,128)} %copy-done.3) | copy-start | bytes 4718596
  102.8 6.9 %copy-start.62 = (bf16[2,1536,512]{2,1,0:T(8,128)(2,1)S(1)}, bf16[2,1536,512]{2,1,0:T(8,128)(2,1)}, u32[]{:S(2)}) copy-start(bf16[2,1536,512]{2,1,0:T(8,128)(2,1)} %all-gather.6.cloned.1.call-done) | copy-start | bytes 9437188
  109.7 4.9 %copy-start.8 = (bf16[768,512]{1,0:T(8,128)(2,1)S(1)}, bf16[768,512]{1,0:T(8,128)(2,1)}, u32[]{:S(2)}) copy-start(bf16[768,512]{1,0:T(8,128)(2,1)} %all_gather.23) | copy-start | bytes 2359300
  109.7 4.9 %copy-start.46 = (bf16[2,512,512]{2,1,0:T(8,128)(2,1)S(1)}, bf16[2,512,512]{2,1,0:T(8,128)(2,1)}, u32[]{:S(2)}) copy-start(bf16[2,512,512]{2,1,0:T(8,128)(2,1)} %all-gather.8.cloned.1.call-done) | copy-start | bytes 3145732
  115.7 2.9 %copy-start.26 = (f32[768,512]{1,0:T(8,128)}, f32[768,512]{1,0:T(8,128)S(1)}, u32[]{:S(2)}) copy-start(f32[768,512]{1,0:T(8,128)S(1)} %get-tuple-element.219) | copy-start | bytes 4718596
  124.2 10.0 %copy-start.51 = (f32[768]{0:T(1024)S(1)}, f32[768]{0:T(1024)}, u32[]{:S(2)}) copy-start(f32[768]{0:T(1024)} %copy-done.50) | copy-start | bytes 9220
  124.2 10.0 %copy-start.53 = (f32[768]{0:T(1024)S(1)}, f32[768]{0:T(1024)}, u32[]{:S(2)}) copy-start(f32[768]{0:T(1024)} %copy-done.52) | copy-start | bytes 9220
  140.4 2.6 copy-start.32
  140.4 2.6 copy-start.35
  140.7 2.2 copy-start.5
  143.0 2.1 copy-start.34
  145.1 2.3 copy-start.64
  145.1 8.5 %slice-start = ((s8[4718592]{0:T(1024)(128)(4,1)}), s8[4194304]{0:T(1024)(128)(4,1)S(1)}, s32[]{:S(2)}) async-start(s8[4718592]{0:T(1024)(128)(4,1)} %bitcast.459), calls=%async_computation.3 | async-start | bytes 8388608
  146.2 7.4 %copy-start.27 = (f32[768,512]{1,0:T(8,128)}, f32[768,512]{1,0:T(8,128)S(1)}, u32[]{:S(2)}) copy-start(f32[768,512]{1,0:T(8,128)S(1)} %get-tuple-element.147) | copy-start | bytes 4718596
  146.2 2.4 copy-start.47
  148.7 5.0 %slice-start.1 = ((s8[4718592]{0:T(1024)(128)(4,1)}), s8[524288]{0:T(1024)(128)(4,1)S(1)}, s32[]{:S(2)}) async-start(s8[4718592]{0:T(1024)(128)(4,1)} %bitcast.459), calls=%async_computation.4 | async-start | bytes 1048576
  153.6 2.1 copy-start.63
  169.5 6.0 %copy-start = (f32[768,1536]{1,0:T(8,128)S(1)}, f32[768,1536]{1,0:T(8,128)}, u32[]{:S(2)}) copy-start(f32[768,1536]{1,0:T(8,128)} %shard_map.357) | copy-start | bytes 14155780
  169.5 6.3 %copy-start.16 = (f32[767,384]{1,0:T(8,128)S(1)}, f32[767,384]{1,0:T(8,128)}, u32[]{:S(2)}) copy-start(f32[767,384]{1,0:T(8,128)} %get-tuple-element.164) | copy-start | bytes 3534340
  169.5 6.7 %copy-start.17 = (f32[767,384]{1,0:T(8,128)S(1)}, f32[767,384]{1,0:T(8,128)}, u32[]{:S(2)}) copy-start(f32[767,384]{1,0:T(8,128)} %get-tuple-element.165) | copy-start | bytes 3534340
  169.6 7.0 %copy-start.18 = (f32[767,384]{1,0:T(8,128)S(1)}, f32[767,384]{1,0:T(8,128)}, u32[]{:S(2)}) copy-start(f32[767,384]{1,0:T(8,128)} %get-tuple-element.166) | copy-start | bytes 3534340
  169.6 7.3 %copy-start.19 = (f32[767,384]{1,0:T(8,128)S(1)}, f32[767,384]{1,0:T(8,128)}, u32[]{:S(2)}) copy-start(f32[767,384]{1,0:T(8,128)} %get-tuple-element.167) | copy-start | bytes 3534340
  176.9 2.3 copy-start.14
  176.9 2.3 copy-start.15
  183.0 4.3 %copy-start.36 = (f32[1,512,128]{2,1,0:T(8,128)S(1)}, f32[1,512,128]{2,1,0:T(8,128)}, u32[]{:S(2)}) copy-start(f32[1,512,128]{2,1,0:T(8,128)} %convolution_bitcast_fusion.5) | copy-start | bytes 786436
  183.0 4.3 %copy-start.23 = (f32[1,1536,128]{2,1,0:T(8,128)S(1)}, f32[1,1536,128]{2,1,0:T(8,128)}, u32[]{:S(2)}) copy-start(f32[1,1536,128]{2,1,0:T(8,128)} %convolution_bitcast_fusion.1) | copy-start | bytes 2359300
  264.8 8.7 %copy-start.13 = (f32[3072,128]{1,0:T(8,128)}, f32[3072,128]{1,0:T(8,128)S(1)}, u32[]{:S(2)}) copy-start(f32[3072,128]{1,0:T(8,128)S(1)} %slice_multiply_fusion) | copy-start | bytes 4718596
  266.6 15.2 %copy-start.55 = (f32[8,128]{1,0:T(8,128)}, f32[8,128]{1,0:T(8,128)S(1)}, u32[]{:S(2)}) copy-start(f32[8,128]{1,0:T(8,128)S(1)} %slice_multiply_fusion.4) | copy-start | bytes 12292
  266.7 5.0 %copy-start.56 = (f32[2,3,384]{2,0,1:T(2,128)S(1)}, f32[2,3,384]{2,0,1:T(2,128)}, u32[]{:S(2)}) copy-start(f32[2,3,384]{2,0,1:T(2,128)} %param.37) | copy-start | bytes 27652
  266.7 5.0 %copy-start.57 = (f32[2,3,384]{2,0,1:T(2,128)S(1)}, f32[2,3,384]{2,0,1:T(2,128)}, u32[]{:S(2)}) copy-start(f32[2,3,384]{2,0,1:T(2,128)} %param.32) | copy-start | bytes 27652
  266.7 6.8 %copy-start.11 = (f32[2,1536,128]{2,1,0:T(8,128)S(1)}, f32[2,1536,128]{2,1,0:T(8,128)}, u32[]{:S(2)}) copy-start(f32[2,1536,128]{2,1,0:T(8,128)} %param.24) | copy-start | bytes 4718596
  273.5 4.7 %copy-start.20 = (f32[2,128,768]{2,1,0:T(8,128)S(1)}, f32[2,128,768]{2,1,0:T(8,128)}, u32[]{:S(2)}) copy-start(f32[2,128,768]{2,1,0:T(8,128)} %param.23) | copy-start | bytes 2359300
  273.5 4.7 %copy-start.21 = (f32[2,128,768]{2,1,0:T(8,128)S(1)}, f32[2,128,768]{2,1,0:T(8,128)}, u32[]{:S(2)}) copy-start(f32[2,128,768]{2,1,0:T(8,128)} %mul.2220) | copy-start | bytes 2359300
  273.5 4.7 %copy-start.37 = (f32[2,128,768]{2,1,0:T(8,128)S(1)}, f32[2,128,768]{2,1,0:T(8,128)}, u32[]{:S(2)}) copy-start(f32[2,128,768]{2,1,0:T(8,128)} %param.33) | copy-start | bytes 2359300
  273.5 4.7 %copy-start.38 = (f32[2,128,768]{2,1,0:T(8,128)S(1)}, f32[2,128,768]{2,1,0:T(8,128)}, u32[]{:S(2)}) copy-start(f32[2,128,768]{2,1,0:T(8,128)} %param.28) | copy-start | bytes 2359300
  278.3 2.3 copy-start.43
  (22 other events, 31.4 us)
Sparse Core Ops, SparseCore 0:
  10.2 22.6 all-gather.3
  35.0 28.6 all-gather.5
  65.9 16.8 all-gather.7

commit v5 on v4

--- a/solution.py
+++ b/solution.py
@@ -109,7 +109,7 @@
     return (1 - odd) * (index // 2) + odd * (n - 1 - index // 2)
 
 
-def ring_sum_kernel(n, x_ref, r_ref, o_ref, slots, rs_send, rs_recv, credit, done, ag_send, ag_recv):
+def ring_sum_kernel(n, x_ref, r_ref, o_ref, low, slots, rs_send, rs_recv, credit, done, ag_send, ag_recv):
     rows = x_ref.shape[0]
     half = rows // 2
     size = half // n
@@ -123,13 +123,14 @@
         pl.semaphore_signal(barrier, 1, device_id={"seq": neighbour}, device_id_type=MESH)
     pl.semaphore_wait(barrier, 2)
     o_ref[...] = x_ref[...]
+    low[...] = x_ref[...].astype(low.dtype)
 
     def block(ring, k):
         return pl.ds(pl.multiple_of(ring * half + k * size, 8), size)
 
     def scatter_copy(ring, place, target, s):
         return pltpu.make_async_remote_copy(
-            src_ref=o_ref.at[block(ring, (place - s + n) % n)],
+            src_ref=low.at[block(ring, (place - s + n) % n)],
             dst_ref=slots.at[ring, s % 2],
             send_sem=rs_send.at[ring, s % 2],
             recv_sem=rs_recv.at[ring, s % 2],
@@ -151,7 +152,9 @@
         for (ring, place, target, source), copy in zip(rings, copies):
             copy.wait_recv()
             into = block(ring, (place - s - 1 + 2 * n) % n)
-            o_ref[into] = o_ref[into] + slots[ring, s % 2]
+            total = o_ref[into] + slots[ring, s % 2].astype(jnp.float32)
+            o_ref[into] = total
+            low[into] = total.astype(low.dtype)
             copy.wait_send()
 
             @pl.when(s <= n - 4)
@@ -212,7 +215,8 @@
         out_specs=pl.BlockSpec(memory_space=pltpu.VMEM),
         scratch_shapes=[
             pltpu.VMEM((rows, lanes), jnp.float32),
-            pltpu.VMEM((2, 2, size, lanes), jnp.float32),
+            pltpu.VMEM((rows, lanes), jnp.bfloat16),
+            pltpu.VMEM((2, 2, size, lanes), jnp.bfloat16),
             pltpu.SemaphoreType.DMA((2, 2)),
             pltpu.SemaphoreType.DMA((2, 2)),
             pltpu.SemaphoreType.REGULAR((2,)),

time: 292 us -> 281 us (0.962)
  Pallas kernels: 113 us -> 101 us
    pallas_call x1, Pallas kernels: 72.7 us -> 61.2 us  [ring_sum(): pl.pallas_call(lambda *refs: ring_sum_kernel(n, *refs), out_shape=jax.Sha...]
  transfers between devices with their start and end apart: 3 -> 3, of which waited for: 2 -> 2; matrix products, arithmetic and copies ran while one was open for 8% -> 8% of each run, Pallas kernels for 3% -> 4%
where the time goes in v5:
time: 281 us; the launch traced here: 280 us
  Pallas kernels  101 us (36%)
  matrix products  46 us (16%)
  other arithmetic  42.7 us (15%)
  local copies, waits for them, and re-layouts  34.9 us (12%)
  blocking collectives  24.6 us (9%)
  waiting for transfers between devices  15.8 us (6%)
  between operations  14.6 us (5%)
    pallas_call x1, Pallas kernels, ring_sum(): pl.pallas_call(lambda *refs: ring_sum_kernel(n, *refs), out_shape=jax.Sha...  61.2 us
    pallas_call x4, Pallas kernels, recurrence(): pl.pallas_call(recurrence_kernel, out_shape=jax.ShapeDtypeStruct((count,...  40 us
    all_gather x3, blocking collectives, gather_feat(): return lax.all_gather(value, 'feat', axis=axis, tiled=True)  24.6 us
    unnamed x142, local copies, waits for them, and re-layouts  15.9 us
    all_gather x3, waiting for transfers between devices, gather_feat(): return lax.all_gather(value, 'feat', axis=axis, tiled=True)  15.7 us
    dot_general x2, matrix products, body(): jnp.dot(states_low, out_low, preferred_element_type=jnp.float32)  13.3 us
    dot_general x4, matrix products, contract_cols(): lax.dot_general(left, right, (((1,), (1,)), ((), ())), preferred_element_...  10.2 us
    slice x2, local copies, waits for them, and re-layouts, body(): states[1:, 3 * width:]  9.82 us
  transfers between devices with their start and end apart: 3, of which 2 were waited for; matrix products, arithmetic and copies ran while one was open for 8% of the time, Pallas kernels for 4%

profile of v5, /device:TPU:0, one launch (start us, length us, event | category | flops | bytes accessed | tf_op | source)
XLA Modules:
  0.0 279.9 jit_solution(16471630827012277115)
XLA Ops:
  7.2 2.0 convert_element_type.75
  11.5 10.0 %all_gather.18 = bf16[768,512]{1,0:T(8,128)(2,1)S(1)} all-gather(bf16[768,128]{1,0:T(8,128)(2,1)S(1)} %copy-done.48), channel_id=1, replica_groups=mesh['seq'=8,'feat'=4] {'feat'}, dimensions={1}, use_global_device_ids=true | all-gather | bytes 983040 | tf_op jit(solution)/shard_map/all_gather | solution.py:268
  22.1 5.2 %all_gather.19 = f32[2,4,512]{2,1,0:T(4,128)S(1)} all-gather(f32[2,4,128]{2,1,0:T(4,128)S(1)} %copy-done.54), channel_id=1, replica_groups=mesh['seq'=8,'feat'=4] {'feat'}, dimensions={2}, use_global_device_ids=true | all-gather | bytes 20480 | tf_op jit(solution)/shard_map/all_gather | solution.py:268
  27.3 9.4 %all_gather.23 = bf16[768,512]{1,0:T(8,128)(2,1)} all-gather(bf16[768,128]{1,0:T(8,128)(2,1)S(1)} %copy-done.49), channel_id=1, replica_groups=mesh['seq'=8,'feat'=4] {'feat'}, dimensions={1}, use_global_device_ids=true | all-gather | bytes 983040 | tf_op jit(solution)/shard_map/all_gather | solution.py:268
  36.9 1.2 fusion.17
  39.5 2.2 fusion.23
  42.2 1.6 pad_maximum_fusion.xa_ref.xb_ref
  43.8 10.0 %shard_map.354 = f32[768,1536]{1,0:T(8,128)} custom-call(f32[768]{0:T(1024)} %copy-done.52, f32[768]{0:T(1024)} %copy-done.50, f32[2,384]{1,0:T(2,128)} %get-tuple-element.209.w_ref, f32[768,768]{1,0:T(8,128)} %pad_maximum_fusion.xa_ref.xb_ref, f32[768,768]{1,0:T(8,128)} %pad_maximum_fusion.xa_ref.xb_ref), custom_call_target="tpu_custom_call" | custom-call | flops 11796480 | bytes 9437184 | tf_op jit(solution)/shard_map/pallas_call | solution.py:82
  53.8 4.8 %fusion.104 = (f32[767,384]{1,0:T(8,128)}, f32[767,384]{1,0:T(8,128)}, f32[767,384]{1,0:T(8,128)}, f32[767,384]{1,0:T(8,128)}) fusion(f32[768,1536]{1,0:T(8,128)} %shard_map.354), kind=kLoop, calls=%fused_computation.333 | loop fusion | bytes 9424896 | tf_op jit(solution)/shard_map/slice | solution.py:392
  58.6 5.2 %all-gather.6.cloned.1.call-done = bf16[2,1536,512]{2,1,0:T(8,128)(2,1)} async-done(((bf16[2,1536,128]{2,1,0:T(8,128)(2,1)}), bf16[2,1536,512]{2,1,0:T(8,128)(2,1)}) %all-gather.6.cloned.1.call-update) | async-done | bytes 3145744 | tf_op jit(solution)/shard_map/all_gather | solution.py:268
  63.7 8.5 %multiply_multiply_fusion.11 = (f32[768,512]{1,0:T(8,128)}, f32[768,512]{1,0:T(8,128)}) fusion(f32[512]{0:T(512)S(1)} %bitcast.476, f32[512]{0:T(512)S(1)} %bitcast.479, f32[768]{0:T(1024)S(1)} %add_rsqrt_fusion.1, f32[768]{0:T(1024)S(1)} %broadcast_multiply_fusion.6, bf16[768,512]{1,0:T(8,128)(2,1)S(1)} %all_gather.18, f32[512]{0:T(512)S(1)} %bitcast.485, ...), kind=kOutput, calls=%fused_computation.74 | convolution fusion | flops 1237057536 | bytes 10235904 | tf_op jit(solution)/shard_map/dot_general | solution.py:340
  72.2 10.5 %all-gather.8.cloned.1.call-done = bf16[2,512,512]{2,1,0:T(8,128)(2,1)} async-done(((bf16[2,512,128]{2,1,0:T(8,128)(2,1)}), bf16[2,512,512]{2,1,0:T(8,128)(2,1)}) %all-gather.8.cloned.1.call-update) | async-done | bytes 1048592 | tf_op jit(solution)/shard_map/all_gather | solution.py:268
  82.8 4.1 %fusion.103 = (f32[768]{0:T(1024)S(1)}, f32[768,512]{1,0:T(8,128)S(1)}, f32[768,512]{1,0:T(8,128)}) fusion(f32[768,512]{1,0:T(8,128)} %get-tuple-element.215, bf16[768,512]{1,0:T(8,128)(2,1)S(1)} %all_gather.18, f32[512]{0:T(512)S(1)} %bitcast.490, bf16[2,512,512]{2,1,0:T(8,128)(2,1)} %all-gather.8.cloned.1.call-done), kind=kOutput, calls=%fused_computation.332 | convolution fusion | flops 406191360 | bytes 7607296 | tf_op jit(solution)/shard_map/dot_general | solution.py:345
  90.1 1.0 copy-done.2
  91.1 1.6 pad_maximum_fusion.1.xa_ref.xb_ref
  92.7 10.1 %shard_map.355 = f32[768,1536]{1,0:T(8,128)} custom-call(f32[768]{0:T(1024)} %copy-done.52, f32[768]{0:T(1024)} %copy-done.50, f32[2,384]{1,0:T(2,128)} %get-tuple-element.225.w_ref, f32[768,768]{1,0:T(8,128)} %pad_maximum_fusion.1.xa_ref.xb_ref, f32[768,768]{1,0:T(8,128)} %pad_maximum_fusion.1.xa_ref.xb_ref), custom_call_target="tpu_custom_call" | custom-call | flops 11796480 | bytes 9437184 | tf_op jit(solution)/shard_map/pallas_call | solution.py:82
  102.8 5.0 %fusion.105 = (f32[767,384]{1,0:T(8,128)}, f32[767,384]{1,0:T(8,128)}, f32[767,384]{1,0:T(8,128)}, f32[767,384]{1,0:T(8,128)}) fusion(f32[768,1536]{1,0:T(8,128)} %shard_map.355), kind=kLoop, calls=%fused_computation.334 | loop fusion | bytes 9424896 | tf_op jit(solution)/shard_map/slice | solution.py:392
  109.7 4.8 %multiply_multiply_fusion.10 = (f32[768,512]{1,0:T(8,128)S(1)}, f32[768,512]{1,0:T(8,128)S(1)}, f32[768,512]{1,0:T(8,128)S(1)}) fusion(f32[512]{0:T(512)S(1)} %bitcast.482, f32[512]{0:T(512)S(1)} %bitcast.469, f32[768]{0:T(1024)S(1)} %add_rsqrt_fusion, f32[768,512]{1,0:T(8,128)S(1)} %copy-done.4, f32[768]{0:T(1024)S(1)} %broadcast_multiply_fusion.5, ...), kind=kOutput, calls=%fused_computation.72 | convolution fusion | flops 1236664320 | bytes 12597248 | tf_op jit(solution)/shard_map/dot_general | solution.py:340
  114.6 1.0 convert_reduce_fusion.1
  116.2 2.4 fusion.110
  118.6 1.7 convolution_bitcast_fusion
  120.3 1.4 fusion.16
  121.7 2.5 fusion.107
  124.2 10.0 %shard_map.356 = f32[768,1536]{1,0:T(8,128)} custom-call(f32[768]{0:T(1024)} %get-tuple-element.227.ma_ref, f32[768]{0:T(1024)} %get-tuple-element.228.mb_ref, f32[2,384]{1,0:T(2,128)} %get-tuple-element.226.w_ref, f32[768,768]{1,0:T(8,128)} %get-tuple-element.178.xa_ref, f32[768,768]{1,0:T(8,128)} %get-tuple-element.177.xb_ref), custom_call_target="tpu_custom_call" | custom-call | flops 11796480 | bytes 9437184 | tf_op jit(solution)/shard_map/pallas_call | solution.py:82
  134.2 4.8 %add_reduce_fusion = (f32[384]{0:T(512)S(1)}, f32[384]{0:T(512)S(1)}, bf16[768,384]{1,0:T(8,128)(2,1)S(1)}, f32[768,384]{1,0:T(8,128)S(1)}, f32[768,384]{1,0:T(8,128)S(1)}) fusion(f32[767,384]{1,0:T(8,128)} %get-tuple-element.174, f32[767,384]{1,0:T(8,128)} %get-tuple-element.173, f32[767,384]{1,0:T(8,128)} %get-tuple-element.172, ...), kind=kLoop, calls=%fused_computation.84 | loop fusion | flops 7961856 | bytes 12395520 | tf_op jit(solution)/shard_map/reduce_sum | solution.py:393
  140.7 2.2 convolution_bitcast_fusion.2
  143.0 1.4 multiply_reduce_fusion.1
  145.1 1.1 convert_reduce_fusion.2
  146.3 1.1 convolution_bitcast_fusion.5
  147.4 1.3 copy-done.47
  148.7 4.9 %fusion.111 = (bf16[768,512]{1,0:T(8,128)(2,1)S(1)}, f32[768,512]{1,0:T(8,128)}) fusion(f32[768,512]{1,0:T(8,128)S(1)} %copy-done.64, bf16[768,512]{1,0:T(8,128)(2,1)S(1)} %get-tuple-element.146, bf16[2,512,512]{2,1,0:T(8,128)(2,1)S(1)} %copy-done.47, f32[768,512]{1,0:T(8,128)S(1)} %get-tuple-element.147, f32[768,512]{1,0:T(8,128)S(1)} %copy-done.34), kind=kOutput, calls=%fused_computation.340 | convolution fusion | flops 431751168 | bytes 8388608 | tf_op jit(solution)/shard_map/dot_general | solution.py:262
  153.6 1.7 convolution_bitcast_fusion.1
  155.7 1.4 fusion.15
  157.1 2.6 fusion.106
  159.6 9.9 %shard_map.357 = f32[768,1536]{1,0:T(8,128)} custom-call(f32[768]{0:T(1024)} %get-tuple-element.227.ma_ref, f32[768]{0:T(1024)} %get-tuple-element.228.mb_ref, f32[2,384]{1,0:T(2,128)} %get-tuple-element.208.w_ref, f32[768,768]{1,0:T(8,128)} %get-tuple-element.176.xa_ref, f32[768,768]{1,0:T(8,128)} %get-tuple-element.175.xb_ref), custom_call_target="tpu_custom_call" | custom-call | flops 11796480 | bytes 9437184 | tf_op jit(solution)/shard_map/pallas_call | solution.py:82
  169.6 5.4 %subtract_reduce_fusion.2 = (f32[384]{0:T(512)S(1)}, f32[384]{0:T(512)S(1)}, f32[384]{0:T(512)S(1)}, f32[384]{0:T(512)S(1)}, f32[768,384]{1,0:T(8,128)}, /*index=5*/f32[768,384]{1,0:T(8,128)}) fusion(f32[768,768]{1,0:T(8,128)S(1)} %fusion.23, f32[768]{0:T(1024)S(1)} %get-tuple-element.212, f32[768,384]{1,0:T(8,128)} %copy-done.6, f32[768,768]{1,0:T(8,128)} %copy-done.2, ...), kind=kLoop, calls=%fused_computation.94 | loop fusion | flops 6486528 | bytes 14164992 | tf_op jit(solution)/shard_map/reduce_sum | solution.py:387
  176.9 1.7 add_reduce_fusion.2
  179.7 1.6 convolution_bitcast_fusion.3
  183.0 4.1 %fusion.96 = (f32[512]{0:T(512)S(1)}, f32[512]{0:T(512)S(1)}, f32[512]{0:T(512)S(1)}, f32[768]{0:T(1024)S(1)}, f32[768]{0:T(1024)S(1)}, /*index=5*/f32[768,512]{1,0:T(8,128)}, f32[768,512]{1,0:T(8,128)}) fusion(f32[768]{0:T(1024)S(1)} %add_rsqrt_fusion.1, f32[768]{0:T(1024)S(1)} %broadcast_multiply_fusion.6, bf16[768,512]{1,0:T(8,128)(2,1)S(1)} %all_gather.18, ...), kind=kOutput, calls=%fused_computation.328 | convolution fusion | flops 612627456 | bytes 7497728 | tf_op jit(solution)/shard_map/dot_general | solution.py:397
  188.5 1.8 pad_bitcast_fusion.refs_0_
  190.3 61.2 %shard_map.358 = bf16[5888,128]{1,0:T(8,128)(2,1)} custom-call(f32[5888,128]{1,0:T(8,128)} %pad_bitcast_fusion.refs_0_), custom_call_target="tpu_custom_call" | custom-call | tf_op jit(solution)/shard_map/pallas_call | solution.py:211
  251.5 1.6 convert_element_type.91
  255.2 2.2 dynamic-slice_add_fusion.1
  257.3 2.2 mul.2220
  262.0 4.7 %add_multiply_fusion = (f32[2,1536,128]{2,1,0:T(8,128)}, f32[2,1536,128]{2,1,0:T(8,128)}, f32[2,1536,128]{2,1,0:T(8,128)}) fusion(f32[2,1536,128]{2,1,0:T(8,128)} %param.34, f32[2,1536,128]{2,1,0:T(8,128)S(1)} %copy-done.11, f32[2,1536,128]{2,1,0:T(8,128)S(1)} %bitcast.462, f32[2,1536,128]{2,1,0:T(8,128)} %param.29), kind=kLoop, calls=%fused_computation.19 | loop fusion | flops 3932160 | bytes 11010048 | tf_op jit(solution)/shard_map/add | solution.py:251
  266.8 1.6 add_multiply_fusion.3
  269.1 1.3 add_multiply_fusion.4
  271.0 2.4 dynamic-slice_add_fusion
  (204 shorter events, 24.7 us)
Async XLA Ops:
  7.2 2.2 copy-start.10
  7.2 32.3 %all-gather.4.cloned.1.call-start = ((), (), s32[]{:S(2)}) async-start(), calls=%async_computation | async-start | bytes 1966080 | tf_op jit(solution)/shard_map/all_gather | solution.py:268
  9.3 2.1 copy-start.48
  9.3 54.4 %all-gather.6.cloned.1.call-start = ((), (), s32[]{:S(2)}) async-start(), calls=%async_computation.1 | async-start | bytes 3932160 | tf_op jit(solution)/shard_map/all_gather | solution.py:268
  10.4 72.4 %all-gather.8.cloned.1.call-start = ((), (), s32[]{:S(2)}) async-start(), calls=%async_computation.2 | async-start | bytes 1310720 | tf_op jit(solution)/shard_map/all_gather | solution.py:268
  11.2 10.9 %copy-start.54 = (f32[2,4,128]{2,1,0:T(4,128)S(1)}, f32[2,4,128]{2,1,0:T(4,128)}, u32[]{:S(2)}) copy-start(f32[2,4,128]{2,1,0:T(4,128)} %param.26) | copy-start | bytes 12292
  11.2 16.1 %copy-start.49 = (bf16[768,128]{1,0:T(8,128)(2,1)S(1)}, bf16[768,128]{1,0:T(8,128)(2,1)}, u32[]{:S(2)}) copy-start(bf16[768,128]{1,0:T(8,128)(2,1)} %param.20) | copy-start | bytes 589828
  11.4 25.3 %copy-start.60 = (s32[2]{0:T(128)S(1)}, s32[2]{0:T(128)}, u32[]{:S(2)}) copy-start(s32[2]{0:T(128)} %param.21) | copy-start | bytes 28
  11.4 25.3 %copy-start.61 = (s32[2]{0:T(128)S(1)}, s32[2]{0:T(128)}, u32[]{:S(2)}) copy-start(s32[2]{0:T(128)} %param.22) | copy-start | bytes 28
  36.8 5.0 %copy-start.50 = (f32[768]{0:T(1024)}, f32[768]{0:T(1024)S(1)}, u32[]{:S(2)}) copy-start(f32[768]{0:T(1024)S(1)} %get-tuple-element.213.mb_ref) | copy-start | bytes 9220
  36.8 5.0 %copy-start.52 = (f32[768]{0:T(1024)}, f32[768]{0:T(1024)S(1)}, u32[]{:S(2)}) copy-start(f32[768]{0:T(1024)S(1)} %get-tuple-element.214.ma_ref) | copy-start | bytes 9220
  102.8 5.0 %copy-start.1 = (f32[768,1536]{1,0:T(8,128)S(1)}, f32[768,1536]{1,0:T(8,128)}, u32[]{:S(2)}) copy-start(f32[768,1536]{1,0:T(8,128)} %shard_map.355) | copy-start | bytes 14155780
  102.8 6.0 %copy-start.4 = (f32[768,512]{1,0:T(8,128)S(1)}, f32[768,512]{1,0:T(8,128)}, u32[]{:S(2)}) copy-start(f32[768,512]{1,0:T(8,128)} %copy-done.3) | copy-start | bytes 4718596
  102.8 6.9 %copy-start.62 = (bf16[2,1536,512]{2,1,0:T(8,128)(2,1)S(1)}, bf16[2,1536,512]{2,1,0:T(8,128)(2,1)}, u32[]{:S(2)}) copy-start(bf16[2,1536,512]{2,1,0:T(8,128)(2,1)} %all-gather.6.cloned.1.call-done) | copy-start | bytes 9437188
  109.7 4.9 %copy-start.8 = (bf16[768,512]{1,0:T(8,128)(2,1)S(1)}, bf16[768,512]{1,0:T(8,128)(2,1)}, u32[]{:S(2)}) copy-start(bf16[768,512]{1,0:T(8,128)(2,1)} %all_gather.23) | copy-start | bytes 2359300
  109.7 4.9 %copy-start.46 = (bf16[2,512,512]{2,1,0:T(8,128)(2,1)S(1)}, bf16[2,512,512]{2,1,0:T(8,128)(2,1)}, u32[]{:S(2)}) copy-start(bf16[2,512,512]{2,1,0:T(8,128)(2,1)} %all-gather.8.cloned.1.call-done) | copy-start | bytes 3145732
  115.7 2.9 %copy-start.26 = (f32[768,512]{1,0:T(8,128)}, f32[768,512]{1,0:T(8,128)S(1)}, u32[]{:S(2)}) copy-start(f32[768,512]{1,0:T(8,128)S(1)} %get-tuple-element.219) | copy-start | bytes 4718596
  124.2 10.0 %copy-start.51 = (f32[768]{0:T(1024)S(1)}, f32[768]{0:T(1024)}, u32[]{:S(2)}) copy-start(f32[768]{0:T(1024)} %copy-done.50) | copy-start | bytes 9220
  124.2 10.0 %copy-start.53 = (f32[768]{0:T(1024)S(1)}, f32[768]{0:T(1024)}, u32[]{:S(2)}) copy-start(f32[768]{0:T(1024)} %copy-done.52) | copy-start | bytes 9220
  140.4 2.6 copy-start.32
  140.4 2.6 copy-start.35
  140.7 2.2 copy-start.5
  143.0 2.1 copy-start.34
  145.1 2.3 copy-start.64
  145.1 8.5 %slice-start = ((s8[4718592]{0:T(1024)(128)(4,1)}), s8[4194304]{0:T(1024)(128)(4,1)S(1)}, s32[]{:S(2)}) async-start(s8[4718592]{0:T(1024)(128)(4,1)} %bitcast.459), calls=%async_computation.3 | async-start | bytes 8388608
  146.2 7.4 %copy-start.27 = (f32[768,512]{1,0:T(8,128)}, f32[768,512]{1,0:T(8,128)S(1)}, u32[]{:S(2)}) copy-start(f32[768,512]{1,0:T(8,128)S(1)} %get-tuple-element.147) | copy-start | bytes 4718596
  146.2 2.4 copy-start.47
  148.7 5.0 %slice-start.1 = ((s8[4718592]{0:T(1024)(128)(4,1)}), s8[524288]{0:T(1024)(128)(4,1)S(1)}, s32[]{:S(2)}) async-start(s8[4718592]{0:T(1024)(128)(4,1)} %bitcast.459), calls=%async_computation.4 | async-start | bytes 1048576
  153.6 2.1 copy-start.63
  169.5 6.0 %copy-start = (f32[768,1536]{1,0:T(8,128)S(1)}, f32[768,1536]{1,0:T(8,128)}, u32[]{:S(2)}) copy-start(f32[768,1536]{1,0:T(8,128)} %shard_map.357) | copy-start | bytes 14155780
  169.5 6.3 %copy-start.16 = (f32[767,384]{1,0:T(8,128)S(1)}, f32[767,384]{1,0:T(8,128)}, u32[]{:S(2)}) copy-start(f32[767,384]{1,0:T(8,128)} %get-tuple-element.164) | copy-start | bytes 3534340
  169.5 6.7 %copy-start.17 = (f32[767,384]{1,0:T(8,128)S(1)}, f32[767,384]{1,0:T(8,128)}, u32[]{:S(2)}) copy-start(f32[767,384]{1,0:T(8,128)} %get-tuple-element.165) | copy-start | bytes 3534340
  169.6 7.0 %copy-start.18 = (f32[767,384]{1,0:T(8,128)S(1)}, f32[767,384]{1,0:T(8,128)}, u32[]{:S(2)}) copy-start(f32[767,384]{1,0:T(8,128)} %get-tuple-element.166) | copy-start | bytes 3534340
  169.6 7.3 %copy-start.19 = (f32[767,384]{1,0:T(8,128)S(1)}, f32[767,384]{1,0:T(8,128)}, u32[]{:S(2)}) copy-start(f32[767,384]{1,0:T(8,128)} %get-tuple-element.167) | copy-start | bytes 3534340
  176.9 2.3 copy-start.14
  176.9 2.3 copy-start.15
  183.0 4.3 %copy-start.36 = (f32[1,512,128]{2,1,0:T(8,128)S(1)}, f32[1,512,128]{2,1,0:T(8,128)}, u32[]{:S(2)}) copy-start(f32[1,512,128]{2,1,0:T(8,128)} %convolution_bitcast_fusion.5) | copy-start | bytes 786436
  183.0 4.3 %copy-start.23 = (f32[1,1536,128]{2,1,0:T(8,128)S(1)}, f32[1,1536,128]{2,1,0:T(8,128)}, u32[]{:S(2)}) copy-start(f32[1,1536,128]{2,1,0:T(8,128)} %convolution_bitcast_fusion.1) | copy-start | bytes 2359300
  253.2 8.7 %copy-start.13 = (f32[3072,128]{1,0:T(8,128)}, f32[3072,128]{1,0:T(8,128)S(1)}, u32[]{:S(2)}) copy-start(f32[3072,128]{1,0:T(8,128)S(1)} %slice_multiply_fusion) | copy-start | bytes 4718596
  255.1 15.2 %copy-start.55 = (f32[8,128]{1,0:T(8,128)}, f32[8,128]{1,0:T(8,128)S(1)}, u32[]{:S(2)}) copy-start(f32[8,128]{1,0:T(8,128)S(1)} %slice_multiply_fusion.4) | copy-start | bytes 12292
  255.1 5.0 %copy-start.56 = (f32[2,3,384]{2,0,1:T(2,128)S(1)}, f32[2,3,384]{2,0,1:T(2,128)}, u32[]{:S(2)}) copy-start(f32[2,3,384]{2,0,1:T(2,128)} %param.37) | copy-start | bytes 27652
  255.1 5.0 %copy-start.57 = (f32[2,3,384]{2,0,1:T(2,128)S(1)}, f32[2,3,384]{2,0,1:T(2,128)}, u32[]{:S(2)}) copy-start(f32[2,3,384]{2,0,1:T(2,128)} %param.32) | copy-start | bytes 27652
  255.2 6.8 %copy-start.11 = (f32[2,1536,128]{2,1,0:T(8,128)S(1)}, f32[2,1536,128]{2,1,0:T(8,128)}, u32[]{:S(2)}) copy-start(f32[2,1536,128]{2,1,0:T(8,128)} %param.24) | copy-start | bytes 4718596
  262.0 4.7 %copy-start.20 = (f32[2,128,768]{2,1,0:T(8,128)S(1)}, f32[2,128,768]{2,1,0:T(8,128)}, u32[]{:S(2)}) copy-start(f32[2,128,768]{2,1,0:T(8,128)} %param.23) | copy-start | bytes 2359300
  262.0 4.7 %copy-start.21 = (f32[2,128,768]{2,1,0:T(8,128)S(1)}, f32[2,128,768]{2,1,0:T(8,128)}, u32[]{:S(2)}) copy-start(f32[2,128,768]{2,1,0:T(8,128)} %mul.2220) | copy-start | bytes 2359300
  262.0 4.7 %copy-start.37 = (f32[2,128,768]{2,1,0:T(8,128)S(1)}, f32[2,128,768]{2,1,0:T(8,128)}, u32[]{:S(2)}) copy-start(f32[2,128,768]{2,1,0:T(8,128)} %param.33) | copy-start | bytes 2359300
  262.0 4.7 %copy-start.38 = (f32[2,128,768]{2,1,0:T(8,128)S(1)}, f32[2,128,768]{2,1,0:T(8,128)}, u32[]{:S(2)}) copy-start(f32[2,128,768]{2,1,0:T(8,128)} %param.28) | copy-start | bytes 2359300
  266.7 2.3 copy-start.43
  (22 other events, 31.4 us)
Sparse Core Ops, SparseCore 0:
  10.2 22.6 all-gather.3
  35.0 28.6 all-gather.5
  65.9 16.8 all-gather.7

commit v6 on v5

--- a/solution.py
+++ b/solution.py
@@ -241,6 +241,103 @@
         pieces.append(total[start : start + part.size].reshape(part.shape))
         start += part.size
     return pieces
+
+
+def adjoint_kernel(ma_ref, mb_ref, coef_ref, masks_ref, g_ref, states_ref, drive_ref, dg_ref, sums_ref, lam):
+    count = g_ref.shape[0]
+    width = coef_ref.shape[1]
+    pad = 8
+    w_re = coef_ref[0:1, :]
+    w_im = -coef_ref[1:2, :]
+    f_re = coef_ref[2:3, :]
+    f_im = coef_ref[3:4, :]
+    zero_rows = jnp.zeros((pad, 4 * width), jnp.float32)
+    lam[0:pad, :] = zero_rows
+    lam[pad + count : 2 * pad + count, :] = zero_rows
+
+    def advance(h_re, h_im, keep, column, row):
+        h_re = h_re * keep
+        h_im = h_im * keep
+        new_re = w_re * h_re - w_im * h_im + g_ref[pl.ds(row, 1), pl.ds(column, width)]
+        new_im = w_re * h_im + w_im * h_re + g_ref[pl.ds(row, 1), pl.ds(column + width, width)]
+        return new_re, new_im
+
+    def step(i, carry):
+        b_re, b_im, a_re, a_im = carry
+        up = i
+        down = count - 1 - i
+        b_re, b_im = advance(b_re, b_im, ma_ref[up], 2 * width, up)
+        a_re, a_im = advance(a_re, a_im, mb_ref[down], 0, down)
+        lam[pl.ds(pad + up, 1), pl.ds(0, width)] = b_re
+        lam[pl.ds(pad + up, 1), pl.ds(width, width)] = b_im
+        lam[pl.ds(pad + down, 1), pl.ds(2 * width, width)] = a_re
+        lam[pl.ds(pad + down, 1), pl.ds(3 * width, width)] = a_im
+        return (b_re, b_im, a_re, a_im)
+
+    zeros = jnp.zeros((1, width), jnp.float32)
+    lax.fori_loop(0, count, step, (zeros, zeros, zeros, zeros), unroll=8)
+
+    rows = 16
+
+    def part(ref, start, column):
+        return ref[pl.ds(start, rows), pl.ds(column, width)]
+
+    def epilogue(k, sums):
+        gp_re, gp_im, gf_re, gf_im = sums
+        r0 = pl.multiple_of(k * rows, rows)
+        live = masks_ref[pl.ds(r0, rows), 0:1]
+        keep_prev = masks_ref[pl.ds(r0, rows), 1:2]
+        keep_next = masks_ref[pl.ds(r0, rows), 2:3]
+        lb_re = part(lam, pad + r0, 0)
+        lb_im = part(lam, pad + r0, width)
+        la_re = part(lam, pad + r0, 2 * width)
+        la_im = part(lam, pad + r0, 3 * width)
+        gu_re = la_re + lb_re
+        gu_im = la_im + lb_im
+        dg_ref[pl.ds(r0, rows), pl.ds(0, width)] = ((f_re * gu_re + f_im * gu_im) * live).astype(dg_ref.dtype)
+        dg_ref[pl.ds(r0, rows), pl.ds(width, width)] = ((f_re * gu_im - f_im * gu_re) * live).astype(dg_ref.dtype)
+        d_re = part(drive_ref, r0, 0) * live
+        d_im = part(drive_ref, r0, width) * live
+        gf_re = gf_re + d_re * gu_re + d_im * gu_im
+        gf_im = gf_im + d_re * gu_im - d_im * gu_re
+        a_re = part(states_ref, r0, 0) * keep_next
+        a_im = part(states_ref, r0, width) * keep_next
+        b_re = part(states_ref, r0, 2 * width) * keep_prev
+        b_im = part(states_ref, r0, 3 * width) * keep_prev
+        ahead_rows = lam[pl.ds(pad + r0, rows + 8), pl.ds(2 * width, 2 * width)][1 : rows + 1]
+        behind_rows = lam[pl.ds(r0, rows + 8), pl.ds(0, 2 * width)][pad - 1 : pad - 1 + rows]
+        na_re = ahead_rows[:, :width]
+        na_im = ahead_rows[:, width:]
+        pb_re = behind_rows[:, :width]
+        pb_im = behind_rows[:, width:]
+        gp_re = gp_re + a_re * na_re + a_im * na_im + b_re * pb_re + b_im * pb_im
+        gp_im = gp_im + a_re * na_im - a_im * na_re + b_re * pb_im - b_im * pb_re
+        return (gp_re, gp_im, gf_re, gf_im)
+
+    block = jnp.zeros((rows, width), jnp.float32)
+    sums = lax.fori_loop(0, count // rows, epilogue, (block, block, block, block))
+    for k, value in enumerate(sums):
+        sums_ref[k : k + 1, :] = jnp.sum(value, 0, keepdims=True)
+
+
+def adjoint(ma, mb, coef, masks, states_grad, states, drive):
+    count, quad = states_grad.shape
+    width = quad // 4
+    vmem = pl.BlockSpec(memory_space=pltpu.VMEM)
+    smem = pl.BlockSpec(memory_space=pltpu.SMEM)
+    return pl.pallas_call(
+        adjoint_kernel,
+        out_shape=(
+            jax.ShapeDtypeStruct((count, 2 * width), jnp.bfloat16),
+            jax.ShapeDtypeStruct((4, width), jnp.float32),
+        ),
+        in_specs=[smem, smem, vmem, vmem, vmem, vmem, vmem],
+        out_specs=(vmem, vmem),
+        scratch_shapes=[pltpu.VMEM((count + 16, 4 * width), jnp.float32)],
+        cost_estimate=pl.CostEstimate(
+            flops=60 * count * width, transcendentals=0, bytes_accessed=48 * count * width
+        ),
+    )(ma, mb, coef, masks, states_grad, states, drive)
 
 
 def update(weight, gradient, velocity, average, rate, decay):
@@ -303,6 +400,7 @@
     zero = jnp.zeros((1,), jnp.float32)
     after_next = jnp.concatenate([zero, carry_next[:-1]])
     before_prev = jnp.concatenate([carry_prev[1:], zero])
+    mask_columns = jnp.stack([alive, carry_prev, carry_next, jnp.zeros_like(alive)], 1)
 
     in_all = gather_feat(input_matrix.astype(jnp.bfloat16), 1)
     out_all = gather_feat(output_matrix.astype(jnp.bfloat16), 2)
@@ -367,31 +465,9 @@
         mixed_low = mixed_grad.astype(jnp.bfloat16)
         out_grad = contract_rows(states_low, mine(mixed_low))
         states_grad = contract_cols(mixed_low, out_low)
-        conj = jnp.stack([pole_re, -pole_im])
-        lambdas = recurrence(
-            after_next, before_prev, conj, states_grad[:, 2 * width :], states_grad[:, : 2 * width]
-        )
-        lb_re = lambdas[:, :width]
-        lb_im = lambdas[:, width : 2 * width]
-        la_re = lambdas[:, 2 * width : 3 * width]
-        la_im = lambdas[:, 3 * width :]
-        gu_re = la_re + lb_re
-        gu_im = la_im + lb_im
-        live = alive[:, None]
-        dg_re = (factor_re * gu_re + factor_im * gu_im) * live
-        dg_im = (factor_re * gu_im - factor_im * gu_re) * live
-        drive_low = jnp.concatenate([dg_re, dg_im], 1).astype(jnp.bfloat16)
-        d_re = drive[:, :width] * live
-        d_im = drive[:, width:] * live
-        gf_re = jnp.sum(d_re * gu_re + d_im * gu_im, 0)
-        gf_im = jnp.sum(d_re * gu_im - d_im * gu_re, 0)
-        zero_row = jnp.zeros((1, width), jnp.float32)
-        a_re = jnp.concatenate([zero_row, states[:-1, :width]], 0) * carry_prev[:, None]
-        a_im = jnp.concatenate([zero_row, states[:-1, width : 2 * width]], 0) * carry_prev[:, None]
-        b_re = jnp.concatenate([states[1:, 2 * width : 3 * width], zero_row], 0) * carry_next[:, None]
-        b_im = jnp.concatenate([states[1:, 3 * width :], zero_row], 0) * carry_next[:, None]
-        gp_re = jnp.sum(a_re * la_re + a_im * la_im + b_re * lb_re + b_im * lb_im, 0)
-        gp_im = jnp.sum(a_re * la_im - a_im * la_re + b_re * lb_im - b_im * lb_re, 0)
+        coef = jnp.stack([pole_re, pole_im, factor_re, factor_im])
+        drive_low, sums = adjoint(after_next, before_prev, coef, mask_columns, states_grad, states, drive)
+        gp_re, gp_im, gf_re, gf_im = sums[0], sums[1], sums[2], sums[3]
         row_grad = jax.vjp(coefficients, state_row)[1]((gp_re, gp_im, gf_re, gf_im))[0]
         in_grad = contract_rows(mine(normed_low), drive_low)
         normed_grad = mixed_grad * feature_row[2] + jnp.dot(

time: 281 us -> 283 us (level)
  local copies, waits for them, and re-layouts: 34.9 us -> 17.3 us
  Pallas kernels: 101 us -> 115 us
  matrix products: 46 us -> 55 us
  other arithmetic: 42.7 us -> 35.2 us
  blocking collectives: 24.6 us -> 28.8 us
    pallas_call x0 -> x2, Pallas kernels: none -> 34.1 us  [adjoint(): pl.pallas_call(adjoint_kernel, out_shape=(jax.ShapeDtypeStruct((count, 2...]
    pallas_call x4 -> x2, Pallas kernels: 40 us -> 20 us  [recurrence(): pl.pallas_call(recurrence_kernel, out_shape=jax.ShapeDtypeStruct((count,...]
    slice x4 -> x0, local copies, waits for them, and re-layouts: 14.9 us -> none  [the longest x2 9.82 us: body(): states[1:, 3 * width:]]
    reduce_sum x3 -> x0, other arithmetic: 11.9 us -> none  [the longest x2 6.5 us: body(): jnp.sum(a_re * la_re + a_im * la_im + b_re * lb_re + b_im * lb_im, 0)]
    unnamed x142 -> x210, local copies, waits for them, and re-layouts: 15.9 us -> 10.9 us
    dot_general x4, matrix products: 10.2 us -> 14.5 us  [contract_cols(): lax.dot_general(left, right, (((1,), (1,)), ((), ())), preferred_element_...]
    all_gather x3, blocking collectives: 24.6 us -> 28.8 us  [gather_feat(): return lax.all_gather(value, 'feat', axis=axis, tiled=True)]
where the time goes in v6:
time: 283 us; the launch traced here: 282 us
  Pallas kernels  115 us (41%)
  matrix products  55 us (19%)
  other arithmetic  35.2 us (12%)
  blocking collectives  28.8 us (10%)
  local copies, waits for them, and re-layouts  17.3 us (6%)
  waiting for transfers between devices  15.5 us (5%)
  between operations  15 us (5%)
    pallas_call x1, Pallas kernels, ring_sum(): pl.pallas_call(lambda *refs: ring_sum_kernel(n, *refs), out_shape=jax.Sha...  61 us
    pallas_call x2, Pallas kernels, adjoint(): pl.pallas_call(adjoint_kernel, out_shape=(jax.ShapeDtypeStruct((count, 2...  34.1 us
    all_gather x3, blocking collectives, gather_feat(): return lax.all_gather(value, 'feat', axis=axis, tiled=True)  28.8 us
    pallas_call x2, Pallas kernels, recurrence(): pl.pallas_call(recurrence_kernel, out_shape=jax.ShapeDtypeStruct((count,...  20 us
    dot_general x2, matrix products, body(): jnp.dot(states_low, out_low, preferred_element_type=jnp.float32)  15.8 us
    all_gather x3, waiting for transfers between devices, gather_feat(): return lax.all_gather(value, 'feat', axis=axis, tiled=True)  15.5 us
    dot_general x4, matrix products, contract_cols(): lax.dot_general(left, right, (((1,), (1,)), ((), ())), preferred_element_...  14.5 us
    unnamed x210, local copies, waits for them, and re-layouts  10.9 us
  transfers between devices with their start and end apart: 3, of which 2 were waited for; matrix products, arithmetic and copies ran while one was open for 8% of the time, Pallas kernels for 4%

profile of v6, /device:TPU:0, one launch (start us, length us, event | category | flops | bytes accessed | tf_op | source)
XLA Modules:
  0.0 282.1 jit_solution(15691669507878980876)
XLA Ops:
  7.2 2.0 convert_element_type.90
  9.4 1.0 convert_element_type.93
  14.9 6.1 %all_gather.19 = f32[2,4,512]{2,1,0:T(4,128)S(1)} all-gather(f32[2,4,128]{2,1,0:T(4,128)S(1)} %copy-done.62), channel_id=1, replica_groups=mesh['seq'=8,'feat'=4] {'feat'}, dimensions={2}, use_global_device_ids=true | all-gather | bytes 20480 | tf_op jit(solution)/shard_map/all_gather | solution.py:365
  21.2 0.9 copy.86.masks_ref
  22.2 13.6 %all_gather.18 = bf16[768,512]{1,0:T(8,128)(2,1)S(1)} all-gather(bf16[768,128]{1,0:T(8,128)(2,1)S(1)} %copy-done.32), channel_id=1, replica_groups=mesh['seq'=8,'feat'=4] {'feat'}, dimensions={1}, use_global_device_ids=true | all-gather | bytes 983040 | tf_op jit(solution)/shard_map/all_gather | solution.py:365
  36.4 9.2 %all_gather.23 = bf16[768,512]{1,0:T(8,128)(2,1)} all-gather(bf16[768,128]{1,0:T(8,128)(2,1)S(1)} %copy-done.33), channel_id=1, replica_groups=mesh['seq'=8,'feat'=4] {'feat'}, dimensions={1}, use_global_device_ids=true | all-gather | bytes 983040 | tf_op jit(solution)/shard_map/all_gather | solution.py:365
  46.8 1.2 fusion.17
  48.1 2.2 fusion.23.drive_ref
  50.7 1.0 copy-done
  51.7 1.6 pad_maximum_fusion.xa_ref.xb_ref
  53.3 9.9 %shard_map.354.states_ref = f32[768,1536]{1,0:T(8,128)} custom-call(f32[768]{0:T(1024)} %copy-done.35, f32[768]{0:T(1024)} %copy-done.34, f32[2,384]{1,0:T(2,128)} %pad_maximum_fusion.11.w_ref, f32[768,768]{1,0:T(8,128)} %pad_maximum_fusion.xa_ref.xb_ref, f32[768,768]{1,0:T(8,128)} %pad_maximum_fusion.xa_ref.xb_ref), custom_call_target="tpu_custom_call" | custom-call | flops 11796480 | bytes 9437184 | tf_op jit(solution)/shard_map/pallas_call | solution.py:82
  63.2 4.7 %all-gather.6.cloned.1.call-done = bf16[2,1536,512]{2,1,0:T(8,128)(2,1)} async-done(((bf16[2,1536,128]{2,1,0:T(8,128)(2,1)}), bf16[2,1536,512]{2,1,0:T(8,128)(2,1)}) %all-gather.6.cloned.1.call-update) | async-done | bytes 3145744 | tf_op jit(solution)/shard_map/all_gather | solution.py:365
  67.9 8.2 %multiply_multiply_fusion.11 = (f32[768,512]{1,0:T(8,128)S(1)}, f32[768,512]{1,0:T(8,128)}) fusion(f32[512]{0:T(512)S(1)} %bitcast.453, f32[512]{0:T(512)S(1)} %bitcast.456, f32[768]{0:T(1024)S(1)} %add_rsqrt_fusion.1, f32[768]{0:T(1024)S(1)} %broadcast_multiply_fusion.6, bf16[768,512]{1,0:T(8,128)(2,1)S(1)} %all_gather.18, f32[512]{0:T(512)S(1)} %bitcast.462, ...), kind=kOutput, calls=%fused_computation.74 | convolution fusion | flops 1237057536 | bytes 10235904 | tf_op jit(solution)/shard_map/dot_general | solution.py:438
  76.1 10.8 %all-gather.8.cloned.1.call-done = bf16[2,512,512]{2,1,0:T(8,128)(2,1)} async-done(((bf16[2,512,128]{2,1,0:T(8,128)(2,1)}), bf16[2,512,512]{2,1,0:T(8,128)(2,1)}) %all-gather.8.cloned.1.call-update) | async-done | bytes 1048592 | tf_op jit(solution)/shard_map/all_gather | solution.py:365
  86.9 3.0 %fusion.105 = (f32[768]{0:T(1024)S(1)}, f32[768,512]{1,0:T(8,128)S(1)}, f32[768,512]{1,0:T(8,128)}) fusion(f32[768,512]{1,0:T(8,128)S(1)} %get-tuple-element.219, bf16[768,512]{1,0:T(8,128)(2,1)S(1)} %all_gather.18, f32[512]{0:T(512)S(1)} %bitcast.467, bf16[2,512,512]{2,1,0:T(8,128)(2,1)} %all-gather.8.cloned.1.call-done), kind=kOutput, calls=%fused_computation.299 | convolution fusion | flops 406191360 | bytes 7607296 | tf_op jit(solution)/shard_map/dot_general | solution.py:443
  93.1 1.0 copy-done.1
  94.2 1.6 pad_maximum_fusion.1.xa_ref.xb_ref
  95.8 10.0 %shard_map.355.states_ref = f32[768,1536]{1,0:T(8,128)} custom-call(f32[768]{0:T(1024)} %copy-done.35, f32[768]{0:T(1024)} %copy-done.34, f32[2,384]{1,0:T(2,128)} %pad_maximum_fusion.12.w_ref, f32[768,768]{1,0:T(8,128)} %pad_maximum_fusion.1.xa_ref.xb_ref, f32[768,768]{1,0:T(8,128)} %pad_maximum_fusion.1.xa_ref.xb_ref), custom_call_target="tpu_custom_call" | custom-call | flops 11796480 | bytes 9437184 | tf_op jit(solution)/shard_map/pallas_call | solution.py:82
  105.9 7.6 %multiply_multiply_fusion.10 = (f32[768,512]{1,0:T(8,128)S(1)}, f32[768,512]{1,0:T(8,128)S(1)}, f32[768,512]{1,0:T(8,128)S(1)}) fusion(f32[512]{0:T(512)S(1)} %bitcast.459, f32[512]{0:T(512)S(1)} %bitcast.446, f32[768]{0:T(1024)S(1)} %add_rsqrt_fusion, f32[768,512]{1,0:T(8,128)S(1)} %copy-done.3, f32[768]{0:T(1024)S(1)} %broadcast_multiply_fusion.5, ...), kind=kOutput, calls=%fused_computation.72 | convolution fusion | flops 1236664320 | bytes 12595200 | tf_op jit(solution)/shard_map/dot_general | solution.py:438
  113.5 1.6 convert_reduce_fusion.1
  115.2 1.1 convolution_bitcast_fusion.4
  116.3 2.4 fusion.108
  118.7 1.7 convolution_bitcast_fusion
  120.7 3.6 %fusion.16.g_ref = f32[768,1536]{1,0:T(8,128)} fusion(bf16[768,512]{1,0:T(8,128)(2,1)S(1)} %get-tuple-element.224, bf16[2,1536,512]{2,1,0:T(8,128)(2,1)S(1)} %copy-done.94), kind=kOutput, calls=%fused_computation.76 | convolution fusion | flops 1207959552 | bytes 7077888 | tf_op jit(solution)/shard_map/dot_general | solution.py:359
  124.4 17.1 %shard_map.356 = (bf16[768,768]{1,0:T(8,128)(2,1)}, f32[4,384]{1,0:T(4,128)}) custom-call(f32[768]{0:T(1024)} %pad_maximum_fusion.8.ma_ref, f32[768]{0:T(1024)} %pad_maximum_fusion.9.mb_ref, f32[4,384]{1,0:T(4,128)} %pad_maximum_fusion.6.coef_ref, f32[768,4]{1,0:T(8,128)} %copy.86.masks_ref, f32[768,1536]{1,0:T(8,128)} %fusion.16.g_ref, ...), custom_call_target="tpu_custom_call" | custom-call | flops 17694720 | bytes 14155776 | tf_op jit(solution)/shard_map/pallas_call | solution.py:328
  141.6 1.8 convolution_bitcast_fusion.2
  144.9 3.9 %multiply_reduce_fusion.1 = (f32[512]{0:T(512)}, f32[768]{0:T(1024)S(1)}, f32[512]{0:T(512)}, f32[768]{0:T(1024)S(1)}, f32[512]{0:T(512)}, /*index=5*/f32[768,512]{1,0:T(8,128)S(1)}) fusion(f32[768]{0:T(1024)S(1)} %copy-done.53, f32[768,512]{1,0:T(8,128)S(1)} %copy-done.3, f32[768]{0:T(1024)S(1)} %copy-done.37, f32[512]{0:T(512)S(1)} %bitcast.447, ...), kind=kOutput, calls=%fused_computation.25 | convolution fusion | flops 609874944 | bytes 6711296 | tf_op jit(solution)/shard_map/dot_general | solution.py:473
  148.8 1.8 convert_reduce_fusion.2
  150.6 1.1 convolution_bitcast_fusion.5
  152.5 5.0 %fusion.109 = (bf16[768,512]{1,0:T(8,128)(2,1)S(1)}, f32[768,512]{1,0:T(8,128)}) fusion(f32[768,512]{1,0:T(8,128)S(1)} %copy-done.96, bf16[768,512]{1,0:T(8,128)(2,1)S(1)} %get-tuple-element.158, bf16[2,512,512]{2,1,0:T(8,128)(2,1)S(1)} %copy-done.31, f32[768,512]{1,0:T(8,128)S(1)} %get-tuple-element.159, f32[768,512]{1,0:T(8,128)S(1)} %copy-done.24), kind=kOutput, calls=%fused_computation.303 | convolution fusion | flops 431751168 | bytes 8388608 | tf_op jit(solution)/shard_map/dot_general | solution.py:359
  157.5 1.7 convolution_bitcast_fusion.1
  159.8 3.6 %fusion.15.g_ref = f32[768,1536]{1,0:T(8,128)} fusion(bf16[768,512]{1,0:T(8,128)(2,1)S(1)} %get-tuple-element.227, bf16[2,1536,512]{2,1,0:T(8,128)(2,1)S(1)} %copy-done.95), kind=kOutput, calls=%fused_computation.75 | convolution fusion | flops 1207959552 | bytes 7077888 | tf_op jit(solution)/shard_map/dot_general | solution.py:359
  163.4 17.1 %shard_map.357 = (bf16[768,768]{1,0:T(8,128)(2,1)}, f32[4,384]{1,0:T(4,128)}) custom-call(f32[768]{0:T(1024)} %pad_maximum_fusion.8.ma_ref, f32[768]{0:T(1024)} %pad_maximum_fusion.9.mb_ref, f32[4,384]{1,0:T(4,128)} %pad_maximum_fusion.7.coef_ref, f32[768,4]{1,0:T(8,128)} %copy.86.masks_ref, f32[768,1536]{1,0:T(8,128)} %fusion.15.g_ref, ...), custom_call_target="tpu_custom_call" | custom-call | flops 17694720 | bytes 14155776 | tf_op jit(solution)/shard_map/pallas_call | solution.py:328
  180.5 1.7 convolution_bitcast_fusion.3
  182.2 0.9 pad_maximum_fusion.3
  183.2 1.2 reshape.706
  184.9 1.1 pad_maximum_fusion.4
  186.4 1.3 copy-done.23
  188.1 3.8 %fusion.88 = (f32[512]{0:T(512)S(1)}, f32[512]{0:T(512)S(1)}, f32[512]{0:T(512)S(1)}, f32[768]{0:T(1024)S(1)}, f32[768]{0:T(1024)S(1)}, /*index=5*/f32[768,512]{1,0:T(8,128)}, f32[768,512]{1,0:T(8,128)}) fusion(f32[768]{0:T(1024)S(1)} %copy-done.49, f32[768]{0:T(1024)S(1)} %copy-done.51, bf16[768,512]{1,0:T(8,128)(2,1)S(1)} %all_gather.18, ...), kind=kOutput, calls=%fused_computation.293 | convolution fusion | flops 610268160 | bytes 7497728 | tf_op jit(solution)/shard_map/dot_general | solution.py:473
  192.2 1.8 pad_bitcast_fusion.refs_0_
  194.0 61.0 %shard_map.358 = bf16[5888,128]{1,0:T(8,128)(2,1)} custom-call(f32[5888,128]{1,0:T(8,128)} %pad_bitcast_fusion.refs_0_), custom_call_target="tpu_custom_call" | custom-call | tf_op jit(solution)/shard_map/pallas_call | solution.py:211
  255.0 1.6 convert_element_type.112
  257.5 0.9 slice_multiply_fusion.1
  261.1 2.2 mul.1534
  263.9 3.0 %add_multiply_fusion.4 = (f32[2,512,128]{2,1,0:T(8,128)}, f32[2,512,128]{2,1,0:T(8,128)}, f32[2,512,128]{2,1,0:T(8,128)}) fusion(f32[2,512,128]{2,1,0:T(8,128)} %param.35, f32[2,512,128]{2,1,0:T(8,128)} %param.25, f32[2,512,128]{2,1,0:T(8,128)} %bitcast.441, f32[2,512,128]{2,1,0:T(8,128)} %param.30), kind=kLoop, calls=%fused_computation.107 | loop fusion | flops 1310720 | bytes 3670016 | tf_op jit(solution)/shard_map/add | solution.py:348
  266.9 1.6 add_multiply_fusion.3
  270.1 2.7 add_multiply_fusion
  272.8 2.7 dynamic-slice_add_fusion
  (271 shorter events, 20.2 us)
Async XLA Ops:
  7.2 40.9 %all-gather.4.cloned.1.call-start = ((), (), s32[]{:S(2)}) async-start(), calls=%async_computation | async-start | bytes 1966080 | tf_op jit(solution)/shard_map/all_gather | solution.py:365
  9.4 58.5 %all-gather.6.cloned.1.call-start = ((), (), s32[]{:S(2)}) async-start(), calls=%async_computation.1 | async-start | bytes 3932160 | tf_op jit(solution)/shard_map/all_gather | solution.py:365
  10.4 4.5 %copy-start.62 = (f32[2,4,128]{2,1,0:T(4,128)S(1)}, f32[2,4,128]{2,1,0:T(4,128)}, u32[]{:S(2)}) copy-start(f32[2,4,128]{2,1,0:T(4,128)} %param.26) | copy-start | bytes 12292
  10.4 11.8 %copy-start.32 = (bf16[768,128]{1,0:T(8,128)(2,1)S(1)}, bf16[768,128]{1,0:T(8,128)(2,1)}, u32[]{:S(2)}) copy-start(bf16[768,128]{1,0:T(8,128)(2,1)} %param.19) | copy-start | bytes 589828
  10.4 76.5 %all-gather.8.cloned.1.call-start = ((), (), s32[]{:S(2)}) async-start(), calls=%async_computation.2 | async-start | bytes 1310720 | tf_op jit(solution)/shard_map/all_gather | solution.py:365
  11.4 24.9 %copy-start.34 = (f32[768]{0:T(1024)}, f32[768]{0:T(1024)S(1)}, u32[]{:S(2)}) copy-start(f32[768]{0:T(1024)S(1)} %get-tuple-element.217.mb_ref) | copy-start | bytes 9220
  11.4 24.9 %copy-start.35 = (f32[768]{0:T(1024)}, f32[768]{0:T(1024)S(1)}, u32[]{:S(2)}) copy-start(f32[768]{0:T(1024)S(1)} %get-tuple-element.218.ma_ref) | copy-start | bytes 9220
  12.2 33.4 %copy-start.38 = (f32[1,384]{1,0:T(1,128)}, f32[1,384]{1,0:T(1,128)S(1)}, u32[]{:S(2)}) copy-start(f32[1,384]{1,0:T(1,128)S(1)} %get-tuple-element.173) | copy-start | bytes 4612
  12.2 33.4 %copy-start.40 = (f32[1,384]{1,0:T(1,128)}, f32[1,384]{1,0:T(1,128)S(1)}, u32[]{:S(2)}) copy-start(f32[1,384]{1,0:T(1,128)S(1)} %get-tuple-element.174) | copy-start | bytes 4612
  12.2 24.1 %copy-start.33 = (bf16[768,128]{1,0:T(8,128)(2,1)S(1)}, bf16[768,128]{1,0:T(8,128)(2,1)}, u32[]{:S(2)}) copy-start(bf16[768,128]{1,0:T(8,128)(2,1)} %param.20) | copy-start | bytes 589828
  14.9 31.3 %copy-start.42 = (f32[1,384]{1,0:T(1,128)}, f32[1,384]{1,0:T(1,128)S(1)}, u32[]{:S(2)}) copy-start(f32[1,384]{1,0:T(1,128)S(1)} %get-tuple-element.210) | copy-start | bytes 4612
  14.9 31.3 %copy-start.45 = (f32[1,384]{1,0:T(1,128)}, f32[1,384]{1,0:T(1,128)S(1)}, u32[]{:S(2)}) copy-start(f32[1,384]{1,0:T(1,128)S(1)} %get-tuple-element.211) | copy-start | bytes 4612
  21.0 46.9 %copy-start.67 = (f32[1,1,512]{2,1,0:T(1,128)}, f32[1,1,512]{2,1,0:T(1,128)S(1)}, u32[]{:S(2)}) copy-start(f32[1,1,512]{2,1,0:T(1,128)S(1)} %get-tuple-element.203) | copy-start | bytes 6148
  21.0 46.9 %copy-start.69 = (f32[1,1,512]{2,1,0:T(1,128)}, f32[1,1,512]{2,1,0:T(1,128)S(1)}, u32[]{:S(2)}) copy-start(f32[1,1,512]{2,1,0:T(1,128)S(1)} %get-tuple-element.204) | copy-start | bytes 6148
  21.0 46.9 %copy-start.84 = (f32[1,1,512]{2,1,0:T(1,128)}, f32[1,1,512]{2,1,0:T(1,128)S(1)}, u32[]{:S(2)}) copy-start(f32[1,1,512]{2,1,0:T(1,128)S(1)} %get-tuple-element.202) | copy-start | bytes 6148
  21.0 84.8 %copy-start.60 = (f32[1,1,512]{2,1,0:T(1,128)}, f32[1,1,512]{2,1,0:T(1,128)S(1)}, u32[]{:S(2)}) copy-start(f32[1,1,512]{2,1,0:T(1,128)S(1)} %get-tuple-element.200) | copy-start | bytes 6148
  21.0 84.8 %copy-start.71 = (f32[1,1,512]{2,1,0:T(1,128)}, f32[1,1,512]{2,1,0:T(1,128)S(1)}, u32[]{:S(2)}) copy-start(f32[1,1,512]{2,1,0:T(1,128)S(1)} %get-tuple-element.199) | copy-start | bytes 6148
  21.1 84.8 %copy-start.86 = (f32[1,1,512]{2,1,0:T(1,128)}, f32[1,1,512]{2,1,0:T(1,128)S(1)}, u32[]{:S(2)}) copy-start(f32[1,1,512]{2,1,0:T(1,128)S(1)} %get-tuple-element.197) | copy-start | bytes 6148
  35.9 32.0 %copy-start.50 = (f32[768]{0:T(1024)}, f32[768]{0:T(1024)S(1)}, u32[]{:S(2)}) copy-start(f32[768]{0:T(1024)S(1)} %broadcast_multiply_fusion.6) | copy-start | bytes 9220
  36.4 31.5 %copy-start.48 = (f32[768]{0:T(1024)}, f32[768]{0:T(1024)S(1)}, u32[]{:S(2)}) copy-start(f32[768]{0:T(1024)S(1)} %add_rsqrt_fusion.1) | copy-start | bytes 9220
  76.1 13.8 %copy-start.7 = (f32[768,512]{1,0:T(8,128)}, f32[768,512]{1,0:T(8,128)S(1)}, u32[]{:S(2)}) copy-start(f32[768,512]{1,0:T(8,128)S(1)} %get-tuple-element.219) | copy-start | bytes 4718596
  89.9 15.9 %copy-start.36 = (f32[768]{0:T(1024)}, f32[768]{0:T(1024)S(1)}, u32[]{:S(2)}) copy-start(f32[768]{0:T(1024)S(1)} %broadcast_multiply_fusion.5) | copy-start | bytes 9220
  90.3 15.5 %copy-start.52 = (f32[768]{0:T(1024)}, f32[768]{0:T(1024)S(1)}, u32[]{:S(2)}) copy-start(f32[768]{0:T(1024)S(1)} %add_rsqrt_fusion) | copy-start | bytes 9220
  95.8 10.1 %copy-start.3 = (f32[768,512]{1,0:T(8,128)S(1)}, f32[768,512]{1,0:T(8,128)}, u32[]{:S(2)}) copy-start(f32[768,512]{1,0:T(8,128)} %copy-done.2) | copy-start | bytes 4718596
  105.9 7.6 %copy-start.4 = (bf16[768,512]{1,0:T(8,128)(2,1)S(1)}, bf16[768,512]{1,0:T(8,128)(2,1)}, u32[]{:S(2)}) copy-start(bf16[768,512]{1,0:T(8,128)(2,1)} %all_gather.23) | copy-start | bytes 2359300
  105.9 7.6 %copy-start.30 = (bf16[2,512,512]{2,1,0:T(8,128)(2,1)S(1)}, bf16[2,512,512]{2,1,0:T(8,128)(2,1)}, u32[]{:S(2)}) copy-start(bf16[2,512,512]{2,1,0:T(8,128)(2,1)} %all-gather.8.cloned.1.call-done) | copy-start | bytes 3145732
  115.2 3.5 %copy-start.16 = (f32[768,512]{1,0:T(8,128)}, f32[768,512]{1,0:T(8,128)S(1)}, u32[]{:S(2)}) copy-start(f32[768,512]{1,0:T(8,128)S(1)} %get-tuple-element.223) | copy-start | bytes 4718596
  115.2 3.5 %slice-start.2 = ((s8[4718592]{0:T(1024)(128)(4,1)}), s8[4194304]{0:T(1024)(128)(4,1)S(1)}, s32[]{:S(2)}) async-start(s8[4718592]{0:T(1024)(128)(4,1)} %bitcast.436), calls=%async_computation.5 | async-start | bytes 8388608
  141.5 3.4 %copy-start.22 = (bf16[2,512,768]{2,1,0:T(8,128)(2,1)S(1)}, bf16[2,512,768]{2,1,0:T(8,128)(2,1)}, u32[]{:S(2)}) copy-start(bf16[2,512,768]{2,1,0:T(8,128)(2,1)} %all-gather.4.cloned.1.call-done) | copy-start | bytes 4718596
  141.5 3.4 %copy-start.37 = (f32[768]{0:T(1024)S(1)}, f32[768]{0:T(1024)}, u32[]{:S(2)}) copy-start(f32[768]{0:T(1024)} %copy-done.36) | copy-start | bytes 9220
  141.5 3.4 %copy-start.53 = (f32[768]{0:T(1024)S(1)}, f32[768]{0:T(1024)}, u32[]{:S(2)}) copy-start(f32[768]{0:T(1024)} %copy-done.52) | copy-start | bytes 9220
  141.5 3.3 %copy-start.61 = (f32[1,1,512]{2,1,0:T(1,128)S(1)}, f32[1,1,512]{2,1,0:T(1,128)}, u32[]{:S(2)}) copy-start(f32[1,1,512]{2,1,0:T(1,128)} %copy-done.60) | copy-start | bytes 6148
  141.6 3.3 %copy-start.72 = (f32[1,1,512]{2,1,0:T(1,128)S(1)}, f32[1,1,512]{2,1,0:T(1,128)}, u32[]{:S(2)}) copy-start(f32[1,1,512]{2,1,0:T(1,128)} %copy-done.71) | copy-start | bytes 6148
  144.9 3.9 %copy-start.8 = (f32[768,512]{1,0:T(8,128)S(1)}, f32[768,512]{1,0:T(8,128)}, u32[]{:S(2)}) copy-start(f32[768,512]{1,0:T(8,128)} %copy-done.7) | copy-start | bytes 4718596
  144.9 3.9 %copy-start.24 = (f32[768,512]{1,0:T(8,128)S(1)}, f32[768,512]{1,0:T(8,128)}, u32[]{:S(2)}) copy-start(f32[768,512]{1,0:T(8,128)} %get-tuple-element.221) | copy-start | bytes 4718596
  148.8 8.6 %slice-start = ((s8[4718592]{0:T(1024)(128)(4,1)}), s8[4194304]{0:T(1024)(128)(4,1)S(1)}, s32[]{:S(2)}) async-start(s8[4718592]{0:T(1024)(128)(4,1)} %bitcast.434), calls=%async_computation.3 | async-start | bytes 8388608
  150.6 6.8 %copy-start.17 = (f32[768,512]{1,0:T(8,128)}, f32[768,512]{1,0:T(8,128)S(1)}, u32[]{:S(2)}) copy-start(f32[768,512]{1,0:T(8,128)S(1)} %get-tuple-element.159) | copy-start | bytes 4718596
  152.5 5.0 %slice-start.1 = ((s8[4718592]{0:T(1024)(128)(4,1)}), s8[524288]{0:T(1024)(128)(4,1)S(1)}, s32[]{:S(2)}) async-start(s8[4718592]{0:T(1024)(128)(4,1)} %bitcast.434), calls=%async_computation.4 | async-start | bytes 1048576
  188.0 3.9 %copy-start.73 = (f32[512]{0:T(512)S(1)}, f32[512]{0:T(512)}, u32[]{:S(2)}) copy-start(f32[512]{0:T(512)} %get-tuple-element.157) | copy-start | bytes 6148
  188.0 3.9 %copy-start.89 = (f32[512]{0:T(512)S(1)}, f32[512]{0:T(512)}, u32[]{:S(2)}) copy-start(f32[512]{0:T(512)} %get-tuple-element.160) | copy-start | bytes 6148
  188.0 3.9 %copy-start.90 = (f32[512]{0:T(512)S(1)}, f32[512]{0:T(512)}, u32[]{:S(2)}) copy-start(f32[512]{0:T(512)} %get-tuple-element.118) | copy-start | bytes 6148
  188.0 3.9 %copy-start.91 = (f32[512]{0:T(512)S(1)}, f32[512]{0:T(512)}, u32[]{:S(2)}) copy-start(f32[512]{0:T(512)} %get-tuple-element.120) | copy-start | bytes 6148
  188.0 3.9 %copy-start.92 = (f32[512]{0:T(512)S(1)}, f32[512]{0:T(512)}, u32[]{:S(2)}) copy-start(f32[512]{0:T(512)} %get-tuple-element.124) | copy-start | bytes 6148
  256.6 6.7 %copy-start.64 = (f32[8,128]{1,0:T(8,128)}, f32[8,128]{1,0:T(8,128)S(1)}, u32[]{:S(2)}) copy-start(f32[8,128]{1,0:T(8,128)S(1)} %slice_multiply_fusion.4) | copy-start | bytes 12292
  258.6 10.0 %copy-start.9 = (f32[3072,128]{1,0:T(8,128)}, f32[3072,128]{1,0:T(8,128)S(1)}, u32[]{:S(2)}) copy-start(f32[3072,128]{1,0:T(8,128)S(1)} %slice_multiply_fusion) | copy-start | bytes 4718596
  258.6 4.7 %copy-start.63 = (f32[2,4,128]{2,1,0:T(4,128)S(1)}, f32[2,4,128]{2,1,0:T(4,128)}, u32[]{:S(2)}) copy-start(f32[2,4,128]{2,1,0:T(4,128)} %param.26) | copy-start | bytes 12292
  258.6 4.7 %copy-start.82 = (f32[2,4,128]{2,1,0:T(4,128)S(1)}, f32[2,4,128]{2,1,0:T(4,128)}, u32[]{:S(2)}) copy-start(f32[2,4,128]{2,1,0:T(4,128)} %param.36) | copy-start | bytes 12292
  258.6 4.7 %copy-start.83 = (f32[2,4,128]{2,1,0:T(4,128)S(1)}, f32[2,4,128]{2,1,0:T(4,128)}, u32[]{:S(2)}) copy-start(f32[2,4,128]{2,1,0:T(4,128)} %param.31) | copy-start | bytes 12292
  (56 other events, 105.1 us)
Sparse Core Ops, SparseCore 0:
  10.2 26.5 all-gather.3
  38.9 28.9 all-gather.5
  70.0 16.8 all-gather.7

commit v7 on v6

--- a/solution.py
+++ b/solution.py
@@ -365,6 +365,24 @@
     return lax.all_gather(value, "feat", axis=axis, tiled=True)
 
 
+def gather_layer_weights(in_shard, out_shard, gate_shard, after=None):
+    pieces = (in_shard.T, out_shard, gate_shard)
+    packed = jnp.concatenate([piece.astype(jnp.bfloat16) for piece in pieces], 0)
+    if after is not None:
+        packed, after = lax.optimization_barrier((packed, after))
+    stacked = lax.all_gather(packed, "feat", axis=0, tiled=False)
+    result = []
+    start = 0
+    for piece in pieces:
+        result.append(stacked[:, start : start + piece.shape[0]])
+        start += piece.shape[0]
+    return result
+
+
+def lanes_of(value, parts):
+    return value.reshape(value.shape[0], parts, value.shape[1] // parts)
+
+
 def body(
     activations_in,
     cotangent,
@@ -402,17 +420,14 @@
     before_prev = jnp.concatenate([carry_prev[1:], zero])
     mask_columns = jnp.stack([alive, carry_prev, carry_next, jnp.zeros_like(alive)], 1)
 
-    in_all = gather_feat(input_matrix.astype(jnp.bfloat16), 1)
-    out_all = gather_feat(output_matrix.astype(jnp.bfloat16), 2)
-    gate_all = gather_feat(gate_matrix.astype(jnp.bfloat16), 2)
+    weights = [gather_layer_weights(input_matrix[0], output_matrix[0], gate_matrix[0])]
+    parts = lax.axis_size("feat")
     feature_all = gather_feat(feature_vectors, 2)
     stream = gather_feat(activations_in, 1).astype(jnp.float32)
 
     saved = []
     for layer in range(layers):
-        in_low = in_all[layer]
-        out_low = out_all[layer]
-        gate_low = gate_all[layer]
+        in_t, out_w, gate_w = weights[layer]
         feature_row = feature_all[layer]
         pole_re, pole_im, factor_re, factor_im = coefficients(state_vectors[layer])
         center = jnp.mean(stream, 1, keepdims=True)
@@ -421,7 +436,9 @@
         unit = spread * scale
         normed = unit * feature_row[0] + feature_row[1]
         normed_low = normed.astype(jnp.bfloat16)
-        drive = jnp.dot(normed_low, in_low, preferred_element_type=jnp.float32)
+        drive = jnp.einsum(
+            "tfk,fck->tc", lanes_of(normed_low, parts), in_t, preferred_element_type=jnp.float32
+        )
         drive_re = drive[:, :width]
         drive_im = drive[:, width:]
         source = jnp.concatenate(
@@ -433,24 +450,36 @@
         )
         poles = jnp.stack([pole_re, pole_im])
         states = recurrence(carry_prev, carry_next, poles, source, source)
+        if layer + 1 < layers:
+            weights.append(
+                gather_layer_weights(
+                    input_matrix[layer + 1], output_matrix[layer + 1], gate_matrix[layer + 1], states
+                )
+            )
         states_low = states.astype(jnp.bfloat16)
         mixed = (
-            jnp.dot(states_low, out_low, preferred_element_type=jnp.float32)
+            jnp.einsum("tk,fkc->tfc", states_low, out_w, preferred_element_type=jnp.float32).reshape(
+                count, -1
+            )
             + feature_row[2] * normed
         )
         act = smooth(mixed)
         act_low = act.astype(jnp.bfloat16)
-        pre = jnp.dot(act_low, gate_low, preferred_element_type=jnp.float32) + feature_row[3]
+        pre = (
+            jnp.einsum("tk,fkc->tfc", act_low, gate_w, preferred_element_type=jnp.float32).reshape(
+                count, -1
+            )
+            + feature_row[3]
+        )
         saved.append((scale, unit, normed_low, drive, states, states_low, mixed, act, act_low, pre))
         stream = stream + act * jax.nn.sigmoid(pre)
 
+    first_stream, cotangent = lax.optimization_barrier((saved[0][7], cotangent))
     grad = gather_feat(cotangent, 1).astype(jnp.float32) * alive[:, None]
     layer_grads = [None] * layers
     for layer in reversed(range(layers)):
         scale, unit, normed_low, drive, states, states_low, mixed, act, act_low, pre = saved[layer]
-        in_low = in_all[layer]
-        out_low = out_all[layer]
-        gate_low = gate_all[layer]
+        in_t, out_w, gate_w = weights[layer]
         feature_row = feature_all[layer]
         state_row = state_vectors[layer]
         pole_re, pole_im, factor_re, factor_im = coefficients(state_row)
@@ -458,21 +487,25 @@
         pre_grad = (grad * act * gate * (1.0 - gate)).astype(jnp.bfloat16)
         gate_grad = contract_rows(act_low, mine(pre_grad))
         gate_bias_grad = jnp.sum(pre_grad.astype(jnp.float32), 0)
-        act_grad = grad * gate + contract_cols(pre_grad, gate_low)
+        act_grad = grad * gate + jnp.einsum(
+            "tfc,fkc->tk", lanes_of(pre_grad, parts), gate_w, preferred_element_type=jnp.float32
+        )
         mixed_grad = jax.vjp(smooth, mixed)[1](act_grad)[0]
         normed = unit * feature_row[0] + feature_row[1]
         skip_grad = jnp.sum(mixed_grad * normed, 0)
         mixed_low = mixed_grad.astype(jnp.bfloat16)
         out_grad = contract_rows(states_low, mine(mixed_low))
-        states_grad = contract_cols(mixed_low, out_low)
+        states_grad = jnp.einsum(
+            "tfc,fkc->tk", lanes_of(mixed_low, parts), out_w, preferred_element_type=jnp.float32
+        )
         coef = jnp.stack([pole_re, pole_im, factor_re, factor_im])
         drive_low, sums = adjoint(after_next, before_prev, coef, mask_columns, states_grad, states, drive)
         gp_re, gp_im, gf_re, gf_im = sums[0], sums[1], sums[2], sums[3]
         row_grad = jax.vjp(coefficients, state_row)[1]((gp_re, gp_im, gf_re, gf_im))[0]
         in_grad = contract_rows(mine(normed_low), drive_low)
-        normed_grad = mixed_grad * feature_row[2] + jnp.dot(
-            drive_low, in_low.T, preferred_element_type=jnp.float32
-        )
+        normed_grad = mixed_grad * feature_row[2] + jnp.einsum(
+            "tc,fck->tfk", drive_low, in_t, preferred_element_type=jnp.float32
+        ).reshape(count, -1)
         gain_grad = jnp.sum(normed_grad * unit, 0)
         bias_grad = jnp.sum(normed_grad, 0)
         unit_grad = normed_grad * feature_row[0]

time: 283 us -> 304 us (1.074)
  local copies, waits for them, and re-layouts: 17.3 us -> 41.1 us
  waiting for transfers between devices: 15.5 us -> 8.17 us
    unnamed x0 -> x6, matrix products: none -> 29.9 us
    dot_general x12 -> x6, matrix products: 45.7 us -> 18.9 us  [the longest x2 7.3 us: body(): jnp.einsum('tfc,fkc->tk', lanes_of(mixed_low, parts), out_w, preferred_el...]
    slice x0 -> x12, local copies, waits for them, and re-layouts: none -> 21.3 us  [gather_layer_weights(): result.append(stacked[:, start:start + piece.shape[0]])]
    all_gather x3 -> x2, waiting for transfers between devices: 15.5 us -> 8.13 us  [gather_layer_weights(): stacked = lax.all_gather(packed, 'feat', axis=0, tiled=False)]
    convert_element_type x3 -> x0, other arithmetic: 3.75 us -> none  [the longest x1 2.03 us: body(): in_all = gather_feat(input_matrix.astype(jnp.bfloat16), 1)]
    unnamed x210 -> x224, local copies, waits for them, and re-layouts: 10.9 us -> 14.1 us
  transfers between devices with their start and end apart: 3 -> 2, of which waited for: 2 -> 1; matrix products, arithmetic and copies ran while one was open for 8% -> 11% of each run, Pallas kernels for 4% -> 0%
where the time goes in v7:
time: 304 us; the launch traced here: 303 us
  Pallas kernels  116 us (38%)
  matrix products  57.9 us (19%)
  local copies, waits for them, and re-layouts  41.1 us (14%)
  other arithmetic  35.3 us (12%)
  blocking collectives  28.6 us (9%)
  between operations  15.2 us (5%)
  waiting for transfers between devices  8.17 us (3%)
    pallas_call x1, Pallas kernels, ring_sum(): pl.pallas_call(lambda *refs: ring_sum_kernel(n, *refs), out_shape=jax.Sha...  62.3 us
    pallas_call x2, Pallas kernels, adjoint(): pl.pallas_call(adjoint_kernel, out_shape=(jax.ShapeDtypeStruct((count, 2...  34.1 us
    unnamed x6, matrix products  29.9 us
    all_gather x3, blocking collectives, gather_feat(): return lax.all_gather(value, 'feat', axis=axis, tiled=True)  28.6 us
    slice x12, local copies, waits for them, and re-layouts, gather_layer_weights(): result.append(stacked[:, start:start + piece.shape[0]])  21.3 us
    pallas_call x2, Pallas kernels, recurrence(): pl.pallas_call(recurrence_kernel, out_shape=jax.ShapeDtypeStruct((count,...  20 us
    unnamed x224, local copies, waits for them, and re-layouts  14.1 us
    dot_general x6, matrix products, contract_rows(): lax.dot_general(left, right, (((0,), (0,)), ((), ())), preferred_element_...  9.08 us
  transfers between devices with their start and end apart: 2, of which 1 were waited for; matrix products, arithmetic and copies ran while one was open for 11% of the time, Pallas kernels for 0%

profile of v7, /device:TPU:0, one launch (start us, length us, event | category | flops | bytes accessed | tf_op | source)
XLA Modules:
  0.0 302.8 jit_solution(290178970942735655)
XLA Ops:
  8.4 1.6 convert.16
  11.5 6.1 %all_gather.22 = f32[2,4,512]{2,1,0:T(4,128)S(1)} all-gather(f32[2,4,128]{2,1,0:T(4,128)S(1)} %copy-done.67), channel_id=1, replica_groups=mesh['seq'=8,'feat'=4] {'feat'}, dimensions={2}, use_global_device_ids=true | all-gather | bytes 20480 | tf_op jit(solution)/shard_map/all_gather | solution.py:365
  19.7 13.3 %all_gather.21 = bf16[768,512]{0,1:T(8,128)(2,1)S(1)} all-gather(bf16[768,128]{0,1:T(8,128)(2,1)S(1)} %copy.139), channel_id=1, replica_groups=mesh['seq'=8,'feat'=4] {'feat'}, dimensions={1}, use_global_device_ids=true | all-gather | bytes 983040 | tf_op jit(solution)/shard_map/all_gather | solution.py:365
  36.8 8.1 %all-gather.5.cloned.1.call-done = bf16[11264,128]{1,0:T(8,128)(2,1)} async-done(((bf16[2816,128]{1,0:T(8,128)(2,1)}), bf16[11264,128]{1,0:T(8,128)(2,1)}) %all-gather.5.cloned.1.call-update) | async-done | bytes 2883600 | tf_op jit(solution)/shard_map/all_gather | solution.py:373
  44.9 2.2 convolution_bitcast_fusion.5.drive_ref
  48.5 1.6 pad_maximum_fusion.xa_ref.xb_ref
  50.1 9.9 %shard_map.354.states_ref = f32[768,1536]{1,0:T(8,128)} custom-call(f32[768]{0:T(1024)} %get-tuple-element.228.ma_ref, f32[768]{0:T(1024)} %get-tuple-element.227.mb_ref, f32[2,384]{1,0:T(2,128)} %pad_maximum_fusion.13.w_ref, f32[768,768]{1,0:T(8,128)} %pad_maximum_fusion.xa_ref.xb_ref, f32[768,768]{1,0:T(8,128)} %pad_maximum_fusion.xa_ref.xb_ref), custom_call_target="tpu_custom_call" | custom-call | flops 11796480 | bytes 9437184 | tf_op jit(solution)/shard_map/pallas_call | solution.py:82
  64.5 1.5 slice.255
  66.0 1.9 slice.257
  69.1 1.6 copy.144
  70.7 2.0 copy.146
  72.8 8.7 %multiply_multiply_fusion.11 = (f32[768,512]{0,1:T(8,128)S(1)}, f32[768,512]{0,1:T(8,128)}) fusion(f32[512]{0:T(512)S(1)} %bitcast.547, f32[512]{0:T(512)S(1)} %bitcast.550, f32[768]{0:T(1024)S(1)} %add_rsqrt_fusion.1, f32[768]{0:T(1024)S(1)} %broadcast_multiply_fusion.6, bf16[768,512]{0,1:T(8,128)(2,1)S(1)} %all_gather.21, f32[512]{0:T(512)S(1)} %bitcast.556, ...), kind=kOutput, calls=%fused_computation.86 | convolution fusion | flops 1237057536 | bytes 10235904
  82.9 3.0 fusion.115
  87.8 9.2 %all_gather.27 = bf16[768,512]{0,1:T(8,128)(2,1)} all-gather(bf16[768,128]{0,1:T(8,128)(2,1)S(1)} %copy.153), channel_id=1, replica_groups=mesh['seq'=8,'feat'=4] {'feat'}, dimensions={1}, use_global_device_ids=true | all-gather | bytes 983040 | tf_op jit(solution)/shard_map/all_gather | solution.py:365
  97.0 1.5 slice.267
  98.5 1.9 slice.269
  100.4 2.1 slice.264
  102.4 1.6 copy.150
  104.0 2.2 convolution_bitcast_fusion.4.drive_ref
  106.3 2.4 copy.152
  109.1 1.6 pad_maximum_fusion.1.xa_ref.xb_ref
  110.7 10.1 %shard_map.355.states_ref = f32[768,1536]{1,0:T(8,128)} custom-call(f32[768]{0:T(1024)} %get-tuple-element.228.ma_ref, f32[768]{0:T(1024)} %get-tuple-element.227.mb_ref, f32[2,384]{1,0:T(2,128)} %pad_maximum_fusion.14.w_ref, f32[768,768]{1,0:T(8,128)} %pad_maximum_fusion.1.xa_ref.xb_ref, f32[768,768]{1,0:T(8,128)} %pad_maximum_fusion.1.xa_ref.xb_ref), custom_call_target="tpu_custom_call" | custom-call | flops 11796480 | bytes 9437184 | tf_op jit(solution)/shard_map/pallas_call | solution.py:82
  120.8 7.9 %multiply_multiply_fusion.10 = (f32[768,512]{0,1:T(8,128)S(1)}, f32[768,512]{0,1:T(8,128)S(1)}, f32[768,512]{0,1:T(8,128)S(1)}) fusion(f32[512]{0:T(512)S(1)} %bitcast.553, f32[512]{0:T(512)S(1)} %bitcast.540, f32[768]{0:T(1024)S(1)} %add_rsqrt_fusion, f32[768,512]{0,1:T(8,128)S(1)} %copy-done.3, f32[768]{0:T(1024)S(1)} %broadcast_multiply_fusion.5, ...), kind=kOutput, calls=%fused_computation.84 | convolution fusion | flops 1236664320 | bytes 12595200
  128.7 1.6 convert_reduce_fusion.1
  131.4 2.3 fusion.118
  133.7 1.7 convolution_bitcast_fusion.2
  135.4 3.7 %convolution_bitcast_fusion.1.g_ref = f32[768,1536]{1,0:T(8,128)} fusion(bf16[768,4,128]{0,2,1:T(8,128)(2,1)S(1)} %bitcast.530, bf16[4,2816,128]{2,1,0:T(8,128)(2,1)S(1)} %bitcast.516), kind=kOutput, calls=%fused_computation.1 | convolution fusion | flops 1207959552 | bytes 7077888 | tf_op jit(solution)/shard_map/tfc,fkc->tk/dot_general | solution.py:498
  139.0 2.3 copy.158
  141.3 17.1 %shard_map.356 = (bf16[768,768]{1,0:T(8,128)(2,1)}, f32[4,384]{1,0:T(4,128)}) custom-call(f32[768]{0:T(1024)} %pad_maximum_fusion.10.ma_ref, f32[768]{0:T(1024)} %pad_maximum_fusion.11.mb_ref, f32[4,384]{1,0:T(4,128)} %pad_maximum_fusion.8.coef_ref, f32[768,4]{1,0:T(8,128)} %copy.156.masks_ref, f32[768,1536]{1,0:T(8,128)} %convolution_bitcast_fusion.1.g_ref, ...), custom_call_target="tpu_custom_call" | custom-call | flops 17694720 | bytes 14155776 | tf_op jit(solution)/shard_map/pallas_call | solution.py:328
  158.4 1.8 convolution_bitcast_fusion.6
  160.3 3.7 %multiply_reduce_fusion.1 = (f32[512]{0:T(512)}, f32[768]{0:T(1024)S(1)}, f32[512]{0:T(512)}, f32[768]{0:T(1024)S(1)}, f32[512]{0:T(512)}, /*index=5*/f32[768,512]{0,1:T(8,128)S(1)}) fusion(f32[768]{0:T(1024)S(1)} %copy-done.56, f32[768,512]{0,1:T(8,128)S(1)} %copy-done.3, f32[768]{0:T(1024)S(1)} %copy-done.37, f32[512]{0:T(512)S(1)} %bitcast.541, ...), kind=kOutput, calls=%fused_computation.43 | convolution fusion | flops 609874944 | bytes 6709248
  164.0 1.6 convert_reduce_fusion.2
  167.7 5.0 %fusion.119 = (bf16[768,512]{0,1:T(8,128)(2,1)S(1)}, f32[768,512]{0,1:T(8,128)}) fusion(f32[768,512]{0,1:T(8,128)S(1)} %copy-done.101, bf16[768,4,128]{0,2,1:T(8,128)(2,1)S(1)} %bitcast.532, bf16[4,2816,128]{2,1,0:T(8,128)(2,1)S(1)} %bitcast.521, f32[768,512]{0,1:T(8,128)S(1)} %get-tuple-element.163, f32[768,512]{0,1:T(8,128)S(1)} %copy-done.24), kind=kOutput, calls=%fused_computation.321 | convolution fusion | flops 431751168 | bytes 8388608 | tf_op jit(solution)/shard_map/tfc,fkc->tk/dot_general | solution.py:490
  172.7 1.7 convolution_bitcast_fusion.3
  174.5 3.6 %convolution_bitcast_fusion.g_ref = f32[768,1536]{1,0:T(8,128)} fusion(bf16[768,4,128]{0,2,1:T(8,128)(2,1)S(1)} %bitcast.538, bf16[4,2816,128]{2,1,0:T(8,128)(2,1)S(1)} %bitcast.522), kind=kOutput, calls=%fused_computation | convolution fusion | flops 1207959552 | bytes 7077888 | tf_op jit(solution)/shard_map/tfc,fkc->tk/dot_general | solution.py:498
  179.5 17.1 %shard_map.357 = (bf16[768,768]{1,0:T(8,128)(2,1)}, f32[4,384]{1,0:T(4,128)}) custom-call(f32[768]{0:T(1024)} %pad_maximum_fusion.10.ma_ref, f32[768]{0:T(1024)} %pad_maximum_fusion.11.mb_ref, f32[4,384]{1,0:T(4,128)} %pad_maximum_fusion.9.coef_ref, f32[768,4]{1,0:T(8,128)} %copy.156.masks_ref, f32[768,1536]{1,0:T(8,128)} %convolution_bitcast_fusion.g_ref, ...), custom_call_target="tpu_custom_call" | custom-call | flops 17694720 | bytes 14155776 | tf_op jit(solution)/shard_map/pallas_call | solution.py:328
  196.5 1.7 convolution_bitcast_fusion.7
  199.4 2.1 constant_dynamic-update-slice_fusion.4
  202.0 5.0 %fusion.98 = (f32[512]{0:T(512)S(1)}, f32[512]{0:T(512)S(1)}, f32[512]{0:T(512)S(1)}, f32[768]{0:T(1024)S(1)}, f32[768]{0:T(1024)S(1)}, /*index=5*/f32[768,512]{0,1:T(8,128)}, f32[768,512]{0,1:T(8,128)}) fusion(f32[768]{0:T(1024)S(1)} %copy-done.51, f32[768]{0:T(1024)S(1)} %copy-done.54, bf16[768,512]{0,1:T(8,128)(2,1)S(1)} %all_gather.21, ...), kind=kOutput, calls=%fused_computation.311 | convolution fusion | flops 610268160 | bytes 7495680
  207.1 1.7 copy-done.10
  210.7 1.8 pad_bitcast_fusion.refs_0_
  212.5 62.3 %shard_map.358 = bf16[5888,128]{1,0:T(8,128)(2,1)} custom-call(f32[5888,128]{1,0:T(8,128)} %pad_bitcast_fusion.refs_0_), custom_call_target="tpu_custom_call" | custom-call | tf_op jit(solution)/shard_map/pallas_call | solution.py:211
  274.8 1.6 convert_element_type.138
  279.0 2.4 dynamic-slice_add_fusion
  281.4 2.0 copy.168
  287.8 3.4 %add_multiply_fusion.3 = (f32[2,128,768]{2,1,0:T(8,128)}, f32[2,128,768]{2,1,0:T(8,128)}, f32[2,128,768]{2,1,0:T(8,128)}) fusion(f32[2,128,768]{2,1,0:T(8,128)} %param.33, f32[2,128,768]{2,1,0:T(8,128)S(1)} %copy-done.14, f32[2,128,768]{2,1,0:T(8,128)} %mul.1534, f32[2,128,768]{2,1,0:T(8,128)} %param.28), kind=kLoop, calls=%fused_computation.104 | loop fusion | flops 1966080 | bytes 5505024 | tf_op jit(solution)/shard_map/add | solution.py:348
  291.3 2.7 add_multiply_fusion
  294.0 1.3 add_multiply_fusion.4
  (299 shorter events, 34.6 us)
Async XLA Ops:
  7.2 37.8 %all-gather.5.cloned.1.call-start = ((), (), s32[]{:S(2)}) async-start(), calls=%async_computation | async-start | bytes 3604480 | tf_op jit(solution)/shard_map/all_gather | solution.py:373
  10.3 7.3 %copy-start.31 = (f32[2,3,384]{2,0,1:T(2,128)S(1)}, f32[2,3,384]{2,0,1:T(2,128)}, u32[]{:S(2)}) copy-start(f32[2,3,384]{2,0,1:T(2,128)} %param.27) | copy-start | bytes 27652
  10.3 9.3 %copy-start.95 = (s32[2]{0:T(128)S(1)}, s32[2]{0:T(128)}, u32[]{:S(2)}) copy-start(s32[2]{0:T(128)} %param.21) | copy-start | bytes 28
  10.3 9.3 %copy-start.100 = (s32[2]{0:T(128)S(1)}, s32[2]{0:T(128)}, u32[]{:S(2)}) copy-start(s32[2]{0:T(128)} %param.22) | copy-start | bytes 28
  11.3 85.7 %all-gather.7.cloned.1.call-start = ((), (), s32[]{:S(2)}) async-start(), calls=%async_computation.1 | async-start | bytes 3604480 | tf_op jit(solution)/shard_map/all_gather | solution.py:373
  18.3 17.6 %copy-start.57 = (f32[1,384]{1,0:T(1,128)}, f32[1,384]{1,0:T(1,128)S(1)}, u32[]{:S(2)}) copy-start(f32[1,384]{1,0:T(1,128)S(1)} %get-tuple-element.176) | copy-start | bytes 4612
  18.3 44.9 %copy-start.38 = (f32[1,384]{1,0:T(1,128)}, f32[1,384]{1,0:T(1,128)S(1)}, u32[]{:S(2)}) copy-start(f32[1,384]{1,0:T(1,128)S(1)} %get-tuple-element.177) | copy-start | bytes 4612
  18.3 44.9 %copy-start.40 = (f32[1,384]{1,0:T(1,128)}, f32[1,384]{1,0:T(1,128)S(1)}, u32[]{:S(2)}) copy-start(f32[1,384]{1,0:T(1,128)S(1)} %get-tuple-element.178) | copy-start | bytes 4612
  18.9 17.0 %copy-start.43 = (f32[1,384]{1,0:T(1,128)}, f32[1,384]{1,0:T(1,128)S(1)}, u32[]{:S(2)}) copy-start(f32[1,384]{1,0:T(1,128)S(1)} %get-tuple-element.220) | copy-start | bytes 4612
  18.9 17.0 %copy-start.46 = (f32[1,384]{1,0:T(1,128)}, f32[1,384]{1,0:T(1,128)S(1)}, u32[]{:S(2)}) copy-start(f32[1,384]{1,0:T(1,128)S(1)} %get-tuple-element.221) | copy-start | bytes 4612
  33.2 39.6 %copy-start.53 = (f32[768]{0:T(1024)}, f32[768]{0:T(1024)S(1)}, u32[]{:S(2)}) copy-start(f32[768]{0:T(1024)S(1)} %broadcast_multiply_fusion.6) | copy-start | bytes 9220
  33.4 39.3 %copy-start.50 = (f32[768]{0:T(1024)}, f32[768]{0:T(1024)S(1)}, u32[]{:S(2)}) copy-start(f32[768]{0:T(1024)S(1)} %add_rsqrt_fusion.1) | copy-start | bytes 9220
  34.7 38.1 %copy-start.72 = (f32[1,1,512]{2,1,0:T(1,128)}, f32[1,1,512]{2,1,0:T(1,128)S(1)}, u32[]{:S(2)}) copy-start(f32[1,1,512]{2,1,0:T(1,128)S(1)} %get-tuple-element.213) | copy-start | bytes 6148
  34.7 38.1 %copy-start.74 = (f32[1,1,512]{2,1,0:T(1,128)}, f32[1,1,512]{2,1,0:T(1,128)S(1)}, u32[]{:S(2)}) copy-start(f32[1,1,512]{2,1,0:T(1,128)S(1)} %get-tuple-element.214) | copy-start | bytes 6148
  34.7 38.1 %copy-start.90 = (f32[1,1,512]{2,1,0:T(1,128)}, f32[1,1,512]{2,1,0:T(1,128)S(1)}, u32[]{:S(2)}) copy-start(f32[1,1,512]{2,1,0:T(1,128)S(1)} %get-tuple-element.212) | copy-start | bytes 6148
  50.1 10.0 %copy-start.35 = (f32[768]{0:T(1024)S(1)}, f32[768]{0:T(1024)}, u32[]{:S(2)}) copy-start(f32[768]{0:T(1024)} %get-tuple-element.228.ma_ref) | copy-start | bytes 9220
  50.1 10.1 %copy-start.34 = (f32[768]{0:T(1024)S(1)}, f32[768]{0:T(1024)}, u32[]{:S(2)}) copy-start(f32[768]{0:T(1024)} %get-tuple-element.227.mb_ref) | copy-start | bytes 9220
  72.8 8.8 %copy-start.33 = (bf16[768,128]{1,0:T(8,128)(2,1)S(1)}, bf16[768,128]{1,0:T(8,128)(2,1)}, u32[]{:S(2)}) copy-start(bf16[768,128]{1,0:T(8,128)(2,1)} %param.20) | copy-start | bytes 589828
  81.5 4.4 %copy-start.6 = (f32[768,512]{0,1:T(8,128)}, f32[768,512]{0,1:T(8,128)S(1)}, u32[]{:S(2)}) copy-start(f32[768,512]{0,1:T(8,128)S(1)} %get-tuple-element.229) | copy-start | bytes 4718596
  86.0 34.8 %copy-start.36 = (f32[768]{0:T(1024)}, f32[768]{0:T(1024)S(1)}, u32[]{:S(2)}) copy-start(f32[768]{0:T(1024)S(1)} %broadcast_multiply_fusion.5) | copy-start | bytes 9220
  86.2 34.5 %copy-start.55 = (f32[768]{0:T(1024)}, f32[768]{0:T(1024)S(1)}, u32[]{:S(2)}) copy-start(f32[768]{0:T(1024)S(1)} %add_rsqrt_fusion) | copy-start | bytes 9220
  104.0 4.6 %copy-start.78 = (f32[384]{0:T(512)S(1)}, f32[384]{0:T(512)}, u32[]{:S(2)}) copy-start(f32[384]{0:T(512)} %get-tuple-element.222) | copy-start | bytes 4612
  104.0 4.6 %copy-start.79 = (f32[384]{0:T(512)S(1)}, f32[384]{0:T(512)}, u32[]{:S(2)}) copy-start(f32[384]{0:T(512)} %get-tuple-element.223) | copy-start | bytes 4612
  110.7 10.1 %copy-start.3 = (f32[768,512]{0,1:T(8,128)S(1)}, f32[768,512]{0,1:T(8,128)}, u32[]{:S(2)}) copy-start(f32[768,512]{0,1:T(8,128)} %copy-done.2) | copy-start | bytes 4718596
  110.7 10.1 %copy-start.92 = (f32[1,1,512]{2,1,0:T(1,128)S(1)}, f32[1,1,512]{2,1,0:T(1,128)}, u32[]{:S(2)}) copy-start(f32[1,1,512]{2,1,0:T(1,128)} %get-tuple-element.207) | copy-start | bytes 6148
  120.8 7.9 %copy-start.4 = (bf16[768,512]{0,1:T(8,128)(2,1)S(1)}, bf16[768,512]{0,1:T(8,128)(2,1)}, u32[]{:S(2)}) copy-start(bf16[768,512]{0,1:T(8,128)(2,1)} %all_gather.27) | copy-start | bytes 2359300
  120.8 7.9 %copy-start.30 = (bf16[4,512,128]{1,2,0:T(8,128)(2,1)S(1)}, bf16[4,512,128]{1,2,0:T(8,128)(2,1)}, u32[]{:S(2)}) copy-start(bf16[4,512,128]{1,2,0:T(8,128)(2,1)} %copy.152) | copy-start | bytes 1572868
  120.8 7.9 %copy-start.94 = (f32[1,1,512]{2,1,0:T(1,128)S(1)}, f32[1,1,512]{2,1,0:T(1,128)}, u32[]{:S(2)}) copy-start(f32[1,1,512]{2,1,0:T(1,128)} %get-tuple-element.208) | copy-start | bytes 6148
  160.3 3.7 %copy-start.7 = (f32[768,512]{0,1:T(8,128)S(1)}, f32[768,512]{0,1:T(8,128)}, u32[]{:S(2)}) copy-start(f32[768,512]{0,1:T(8,128)} %copy-done.6) | copy-start | bytes 4718596
  160.3 3.7 %copy-start.24 = (f32[768,512]{0,1:T(8,128)S(1)}, f32[768,512]{0,1:T(8,128)}, u32[]{:S(2)}) copy-start(f32[768,512]{0,1:T(8,128)} %get-tuple-element.231) | copy-start | bytes 4718596
  164.0 8.7 %slice-start = ((s8[4718592]{0:T(1024)(128)(4,1)}), s8[524288]{0:T(1024)(128)(4,1)S(1)}, s32[]{:S(2)}) async-start(s8[4718592]{0:T(1024)(128)(4,1)} %bitcast.504), calls=%async_computation.2 | async-start | bytes 1048576
  165.6 7.1 %copy-start.19 = (f32[768,512]{0,1:T(8,128)}, f32[768,512]{0,1:T(8,128)S(1)}, u32[]{:S(2)}) copy-start(f32[768,512]{0,1:T(8,128)S(1)} %get-tuple-element.163) | copy-start | bytes 4718596
  167.7 5.0 %slice-start.1 = ((s8[4718592]{0:T(1024)(128)(4,1)}), s8[4194304]{0:T(1024)(128)(4,1)S(1)}, s32[]{:S(2)}) async-start(s8[4718592]{0:T(1024)(128)(4,1)} %bitcast.504), calls=%async_computation.3 | async-start | bytes 8388608
  174.4 3.7 %copy-start.39 = (f32[1,384]{1,0:T(1,128)S(1)}, f32[1,384]{1,0:T(1,128)}, u32[]{:S(2)}) copy-start(f32[1,384]{1,0:T(1,128)} %copy-done.38) | copy-start | bytes 4612
  174.4 3.7 %copy-start.41 = (f32[1,384]{1,0:T(1,128)S(1)}, f32[1,384]{1,0:T(1,128)}, u32[]{:S(2)}) copy-start(f32[1,384]{1,0:T(1,128)} %copy-done.40) | copy-start | bytes 4612
  174.4 3.7 %copy-start.44 = (f32[1,384]{1,0:T(1,128)S(1)}, f32[1,384]{1,0:T(1,128)}, u32[]{:S(2)}) copy-start(f32[1,384]{1,0:T(1,128)} %copy-done.43) | copy-start | bytes 4612
  174.4 3.7 %copy-start.47 = (f32[1,384]{1,0:T(1,128)S(1)}, f32[1,384]{1,0:T(1,128)}, u32[]{:S(2)}) copy-start(f32[1,384]{1,0:T(1,128)} %copy-done.46) | copy-start | bytes 4612
  174.4 3.7 %copy-start.58 = (f32[1,384]{1,0:T(1,128)S(1)}, f32[1,384]{1,0:T(1,128)}, u32[]{:S(2)}) copy-start(f32[1,384]{1,0:T(1,128)} %copy-done.57) | copy-start | bytes 4612
  174.4 3.7 %copy-start.60 = (f32[1,384]{1,0:T(1,128)S(1)}, f32[1,384]{1,0:T(1,128)}, u32[]{:S(2)}) copy-start(f32[1,384]{1,0:T(1,128)} %get-tuple-element.218) | copy-start | bytes 4612
  174.5 3.7 %copy-start.63 = (f32[4,384]{1,0:T(4,128)S(1)}, f32[4,384]{1,0:T(4,128)}, u32[]{:S(2)}) copy-start(f32[4,384]{1,0:T(4,128)} %get-tuple-element.33) | copy-start | bytes 18436
  174.5 3.7 %copy-start.81 = (f32[1,384]{1,0:T(1,128)S(1)}, f32[1,384]{1,0:T(1,128)}, u32[]{:S(2)}) copy-start(f32[1,384]{1,0:T(1,128)} %get-tuple-element.175) | copy-start | bytes 4612
  174.5 3.7 %copy-start.82 = (f32[1,384]{1,0:T(1,128)S(1)}, f32[1,384]{1,0:T(1,128)}, u32[]{:S(2)}) copy-start(f32[1,384]{1,0:T(1,128)} %get-tuple-element.180) | copy-start | bytes 4612
  174.5 4.4 %copy-start.84 = (f32[1,384]{1,0:T(1,128)S(1)}, f32[1,384]{1,0:T(1,128)}, u32[]{:S(2)}) copy-start(f32[1,384]{1,0:T(1,128)} %get-tuple-element.217) | copy-start | bytes 4612
  202.0 5.0 %copy-start.15 = (f32[1,1536,128]{2,1,0:T(8,128)S(1)}, f32[1,1536,128]{2,1,0:T(8,128)}, u32[]{:S(2)}) copy-start(f32[1,1536,128]{2,1,0:T(8,128)} %convolution_bitcast_fusion.2) | copy-start | bytes 2359300
  202.0 5.0 %copy-start.16 = (f32[1,1536,128]{2,1,0:T(8,128)S(1)}, f32[1,1536,128]{2,1,0:T(8,128)}, u32[]{:S(2)}) copy-start(f32[1,1536,128]{2,1,0:T(8,128)} %convolution_bitcast_fusion.3) | copy-start | bytes 2359300
  277.5 13.7 %copy-start.8 = (f32[3072,128]{1,0:T(8,128)}, f32[3072,128]{1,0:T(8,128)S(1)}, u32[]{:S(2)}) copy-start(f32[3072,128]{1,0:T(8,128)S(1)} %slice_multiply_fusion) | copy-start | bytes 4718596
  278.4 16.9 %copy-start.69 = (f32[8,128]{1,0:T(8,128)}, f32[8,128]{1,0:T(8,128)S(1)}, u32[]{:S(2)}) copy-start(f32[8,128]{1,0:T(8,128)S(1)} %slice_multiply_fusion.4) | copy-start | bytes 12292
  281.4 6.4 %copy-start.14 = (f32[2,128,768]{2,1,0:T(8,128)S(1)}, f32[2,128,768]{2,1,0:T(8,128)}, u32[]{:S(2)}) copy-start(f32[2,128,768]{2,1,0:T(8,128)} %param.23) | copy-start | bytes 2359300
  (60 other events, 135.6 us)
Sparse Core Ops, SparseCore 0:
  11.4 33.5 all-gather.4
  60.2 27.4 all-gather.6

commit v8 on v6

--- a/solution.py
+++ b/solution.py
@@ -365,6 +365,31 @@
     return lax.all_gather(value, "feat", axis=axis, tiled=True)
 
 
+def gather_layer_weights(in_shard, out_shard, gate_shard, after=None):
+    pieces = (in_shard.T, out_shard, gate_shard)
+    packed = jnp.concatenate([piece.astype(jnp.bfloat16) for piece in pieces], 0)
+    if after is not None:
+        packed, after = lax.optimization_barrier((packed, after))
+    stacked = lax.all_gather(packed, "feat", axis=0, tiled=False)
+    result = []
+    start = 0
+    for piece in pieces:
+        result.append(stacked[:, start : start + piece.shape[0]])
+        start += piece.shape[0]
+    in_t, out_w, gate_w = result
+    in_full = jnp.transpose(in_t, (0, 2, 1)).reshape(-1, in_t.shape[1])
+    return [in_full, lanes_joined(out_w), lanes_joined(gate_w), stacked]
+
+
+def lanes_joined(stacked):
+    moved = jnp.moveaxis(stacked, 0, 1)
+    return moved.reshape(moved.shape[0], -1)
+
+
+def lanes_of(value, parts):
+    return value.reshape(value.shape[0], parts, value.shape[1] // parts)
+
+
 def body(
     activations_in,
     cotangent,
@@ -402,17 +427,17 @@
     before_prev = jnp.concatenate([carry_prev[1:], zero])
     mask_columns = jnp.stack([alive, carry_prev, carry_next, jnp.zeros_like(alive)], 1)
 
-    in_all = gather_feat(input_matrix.astype(jnp.bfloat16), 1)
-    out_all = gather_feat(output_matrix.astype(jnp.bfloat16), 2)
-    gate_all = gather_feat(gate_matrix.astype(jnp.bfloat16), 2)
+    weights = [gather_layer_weights(input_matrix[0], output_matrix[0], gate_matrix[0])]
+    for k in range(1, layers):
+        weights.append(
+            gather_layer_weights(input_matrix[k], output_matrix[k], gate_matrix[k], weights[-1][3])
+        )
     feature_all = gather_feat(feature_vectors, 2)
     stream = gather_feat(activations_in, 1).astype(jnp.float32)
 
     saved = []
     for layer in range(layers):
-        in_low = in_all[layer]
-        out_low = out_all[layer]
-        gate_low = gate_all[layer]
+        in_low, out_low, gate_low, _ = weights[layer]
         feature_row = feature_all[layer]
         pole_re, pole_im, factor_re, factor_im = coefficients(state_vectors[layer])
         center = jnp.mean(stream, 1, keepdims=True)
@@ -444,13 +469,12 @@
         saved.append((scale, unit, normed_low, drive, states, states_low, mixed, act, act_low, pre))
         stream = stream + act * jax.nn.sigmoid(pre)
 
+    stream, cotangent = lax.optimization_barrier((stream, cotangent))
     grad = gather_feat(cotangent, 1).astype(jnp.float32) * alive[:, None]
     layer_grads = [None] * layers
     for layer in reversed(range(layers)):
         scale, unit, normed_low, drive, states, states_low, mixed, act, act_low, pre = saved[layer]
-        in_low = in_all[layer]
-        out_low = out_all[layer]
-        gate_low = gate_all[layer]
+        in_low, out_low, gate_low, _ = weights[layer]
         feature_row = feature_all[layer]
         state_row = state_vectors[layer]
         pole_re, pole_im, factor_re, factor_im = coefficients(state_row)

time: 283 us -> 288 us (1.018)
  local copies, waits for them, and re-layouts: 17.3 us -> 32.6 us
  waiting for transfers between devices: 15.5 us -> 6.36 us
    transpose x0 -> x12, local copies, waits for them, and re-layouts: none -> 16.9 us  [the longest x8 11.9 us: lanes_joined(): moved = jnp.moveaxis(stacked, 0, 1)]
    all_gather x3 -> x2, waiting for transfers between devices: 15.5 us -> 6.33 us  [gather_layer_weights(): stacked = lax.all_gather(packed, 'feat', axis=0, tiled=False)]
    convert_element_type x3 -> x0, other arithmetic: 3.75 us -> none  [the longest x1 2.03 us: body(): in_all = gather_feat(input_matrix.astype(jnp.bfloat16), 1)]
    unnamed x210 -> x209, local copies, waits for them, and re-layouts: 10.9 us -> 8.78 us
  transfers between devices with their start and end apart: 3 -> 2, of which waited for: 2 -> 1; matrix products, arithmetic and copies ran while one was open for 8% -> 10% of each run, Pallas kernels for 4% -> 3%
where the time goes in v8:
time: 288 us; the launch traced here: 287 us
  Pallas kernels  117 us (41%)
  matrix products  54.2 us (19%)
  other arithmetic  33.4 us (12%)
  local copies, waits for them, and re-layouts  32.6 us (11%)
  blocking collectives  28.5 us (10%)
  between operations  15.4 us (5%)
  waiting for transfers between devices  6.36 us (2%)
    pallas_call x1, Pallas kernels, ring_sum(): pl.pallas_call(lambda *refs: ring_sum_kernel(n, *refs), out_shape=jax.Sha...  62.4 us
    pallas_call x2, Pallas kernels, adjoint(): pl.pallas_call(adjoint_kernel, out_shape=(jax.ShapeDtypeStruct((count, 2...  34.3 us
    all_gather x3, blocking collectives, gather_feat(): return lax.all_gather(value, 'feat', axis=axis, tiled=True)  28.5 us
    pallas_call x2, Pallas kernels, recurrence(): pl.pallas_call(recurrence_kernel, out_shape=jax.ShapeDtypeStruct((count,...  20.1 us
    dot_general x2, matrix products, body(): jnp.dot(states_low, out_low, preferred_element_type=jnp.float32)  15.2 us
    dot_general x4, matrix products, contract_cols(): lax.dot_general(left, right, (((1,), (1,)), ((), ())), preferred_element_...  14.5 us
    transpose x8, local copies, waits for them, and re-layouts, lanes_joined(): moved = jnp.moveaxis(stacked, 0, 1)  11.9 us
    dot_general x6, matrix products, contract_rows(): lax.dot_general(left, right, (((0,), (0,)), ((), ())), preferred_element_...  10.2 us
  transfers between devices with their start and end apart: 2, of which 1 were waited for; matrix products, arithmetic and copies ran while one was open for 10% of the time, Pallas kernels for 3%

profile of v8, /device:TPU:0, one launch (start us, length us, event | category | flops | bytes accessed | tf_op | source)
XLA Modules:
  0.0 287.4 jit_solution(5378334313362972510)
XLA Ops:
  8.4 1.6 convert.16
  12.7 6.1 %all_gather.22 = f32[2,4,512]{2,1,0:T(4,128)S(1)} all-gather(f32[2,4,128]{2,1,0:T(4,128)S(1)} %copy-done.64), channel_id=1, replica_groups=mesh['seq'=8,'feat'=4] {'feat'}, dimensions={2}, use_global_device_ids=true | all-gather | bytes 20480 | tf_op jit(solution)/shard_map/all_gather | solution.py:365
  23.3 13.6 %all_gather.21 = bf16[768,512]{1,0:T(8,128)(2,1)S(1)} all-gather(bf16[768,128]{1,0:T(8,128)(2,1)S(1)} %copy-done.37), channel_id=1, replica_groups=mesh['seq'=8,'feat'=4] {'feat'}, dimensions={1}, use_global_device_ids=true | all-gather | bytes 983040 | tf_op jit(solution)/shard_map/all_gather | solution.py:365
  39.1 6.3 %all-gather.5.cloned.1.call-done = bf16[11264,128]{1,0:T(8,128)(2,1)} async-done(((bf16[2816,128]{1,0:T(8,128)(2,1)}), bf16[11264,128]{1,0:T(8,128)(2,1)}) %all-gather.5.cloned.1.call-update) | async-done | bytes 2883600 | tf_op jit(solution)/shard_map/all_gather | solution.py:373
  45.4 1.5 slice_bitcast_fusion.1
  46.9 1.8 copy.119
  48.7 1.2 slice_bitcast_fusion.3
  50.2 1.4 slice_bitcast_fusion.5
  54.7 1.7 pad_maximum_fusion.xa_ref.xb_ref
  56.4 10.1 %shard_map.354.states_ref = f32[768,1536]{1,0:T(8,128)} custom-call(f32[768]{0:T(1024)} %copy-done.40, f32[768]{0:T(1024)} %copy-done.39, f32[2,384]{1,0:T(2,128)} %pad_maximum_fusion.13.w_ref, f32[768,768]{1,0:T(8,128)} %pad_maximum_fusion.xa_ref.xb_ref, f32[768,768]{1,0:T(8,128)} %pad_maximum_fusion.xa_ref.xb_ref), custom_call_target="tpu_custom_call" | custom-call | flops 11796480 | bytes 9437184 | tf_op jit(solution)/shard_map/pallas_call | solution.py:82
  66.5 7.9 %multiply_multiply_fusion.11 = (f32[768,512]{1,0:T(8,128)S(1)}, f32[768,512]{1,0:T(8,128)}) fusion(f32[512]{0:T(512)S(1)} %bitcast.480, f32[512]{0:T(512)S(1)} %bitcast.483, f32[768]{0:T(1024)S(1)} %add_rsqrt_fusion.1, f32[768]{0:T(1024)S(1)} %broadcast_multiply_fusion.6, bf16[768,512]{1,0:T(8,128)(2,1)S(1)} %all_gather.21, f32[512]{0:T(512)S(1)} %bitcast.489, ...), kind=kOutput, calls=%fused_computation.75 | convolution fusion | flops 1237057536 | bytes 10235904 | tf_op jit(solution)/shard_map/dot_general | solution.py:463
  74.4 2.1 fusion.101
  78.0 1.8 slice_bitcast_fusion
  79.8 2.1 slice_bitcast_fusion.2
  81.8 1.9 slice_bitcast_fusion.4
  83.7 1.6 copy.124
  85.3 1.5 copy.121
  90.0 1.6 pad_maximum_fusion.1.xa_ref.xb_ref
  91.6 10.0 %shard_map.355.states_ref = f32[768,1536]{1,0:T(8,128)} custom-call(f32[768]{0:T(1024)} %copy-done.40, f32[768]{0:T(1024)} %copy-done.39, f32[2,384]{1,0:T(2,128)} %pad_maximum_fusion.14.w_ref, f32[768,768]{1,0:T(8,128)} %pad_maximum_fusion.1.xa_ref.xb_ref, f32[768,768]{1,0:T(8,128)} %pad_maximum_fusion.1.xa_ref.xb_ref), custom_call_target="tpu_custom_call" | custom-call | flops 11796480 | bytes 9437184 | tf_op jit(solution)/shard_map/pallas_call | solution.py:82
  101.7 7.3 %multiply_multiply_fusion.10 = (f32[768,512]{1,0:T(8,128)S(1)}, f32[768,512]{1,0:T(8,128)S(1)}, f32[768,512]{1,0:T(8,128)S(1)}) fusion(f32[512]{0:T(512)S(1)} %bitcast.486, f32[512]{0:T(512)S(1)} %bitcast.472, f32[768]{0:T(1024)S(1)} %add_rsqrt_fusion, f32[768,512]{1,0:T(8,128)S(1)} %copy-done.3, f32[768]{0:T(1024)S(1)} %broadcast_multiply_fusion.5, ...), kind=kOutput, calls=%fused_computation.73 | convolution fusion | flops 1236664320 | bytes 12595200 | tf_op jit(solution)/shard_map/dot_general | solution.py:463
  109.1 2.0 multiply_add_fusion.8
  111.1 8.9 %all_gather.27 = bf16[768,512]{1,0:T(8,128)(2,1)S(1)} all-gather(bf16[768,128]{1,0:T(8,128)(2,1)S(1)} %copy-done.38), channel_id=1, replica_groups=mesh['seq'=8,'feat'=4] {'feat'}, dimensions={1}, use_global_device_ids=true | all-gather | bytes 983040 | tf_op jit(solution)/shard_map/all_gather | solution.py:365
  120.0 1.1 convert_reduce_fusion.1
  121.1 2.3 fusion.104
  123.4 3.6 %fusion.108.g_ref = f32[768,1536]{1,0:T(8,128)} fusion(bf16[768,512]{1,0:T(8,128)(2,1)S(1)} %get-tuple-element.259, bf16[1536,512]{0,1:T(8,128)(2,1)S(1)} %bitcast.449), kind=kOutput, calls=%fused_computation.310 | convolution fusion | flops 1207959552 | bytes 7077888 | tf_op jit(solution)/shard_map/dot_general | solution.py:359
  127.0 1.8 convolution_bitcast_fusion
  128.8 17.2 %shard_map.356 = (bf16[768,768]{1,0:T(8,128)(2,1)}, f32[4,384]{1,0:T(4,128)}) custom-call(f32[768]{0:T(1024)} %pad_maximum_fusion.10.ma_ref, f32[768]{0:T(1024)} %pad_maximum_fusion.11.mb_ref, f32[4,384]{1,0:T(4,128)} %pad_maximum_fusion.8.coef_ref, f32[768,4]{1,0:T(8,128)} %copy.126.masks_ref, f32[768,1536]{1,0:T(8,128)} %fusion.108.g_ref, ...), custom_call_target="tpu_custom_call" | custom-call | flops 17694720 | bytes 14155776 | tf_op jit(solution)/shard_map/pallas_call | solution.py:328
  146.0 1.8 convolution_bitcast_fusion.2
  147.9 3.9 %multiply_reduce_fusion.1 = (f32[512]{0:T(512)}, f32[768]{0:T(1024)S(1)}, f32[512]{0:T(512)}, f32[768]{0:T(1024)S(1)}, f32[512]{0:T(512)}, /*index=5*/f32[768,512]{1,0:T(8,128)S(1)}) fusion(f32[768]{0:T(1024)S(1)} %copy-done.56, f32[768,512]{1,0:T(8,128)S(1)} %copy-done.3, f32[768]{0:T(1024)S(1)} %copy-done.42, f32[512]{0:T(512)S(1)} %bitcast.473, ...), kind=kOutput, calls=%fused_computation.25 | convolution fusion | flops 609874944 | bytes 6709248 | tf_op jit(solution)/shard_map/dot_general | solution.py:497
  151.8 1.7 convert_reduce_fusion.2
  153.5 5.1 %fusion.105 = (bf16[768,512]{1,0:T(8,128)(2,1)S(1)}, f32[768,512]{1,0:T(8,128)}) fusion(f32[768,512]{1,0:T(8,128)S(1)} %copy-done.95, bf16[768,512]{1,0:T(8,128)(2,1)S(1)} %get-tuple-element.186, bf16[512,512]{0,1:T(8,128)(2,1)S(1)} %bitcast.469, f32[768,512]{1,0:T(8,128)S(1)} %get-tuple-element.187, f32[768,512]{1,0:T(8,128)S(1)} %copy-done.29), kind=kOutput, calls=%fused_computation.307 | convolution fusion | flops 431751168 | bytes 8388608 | tf_op jit(solution)/shard_map/dot_general | solution.py:359
  158.6 3.6 %fusion.109.g_ref = f32[768,1536]{1,0:T(8,128)} fusion(bf16[768,512]{1,0:T(8,128)(2,1)S(1)} %get-tuple-element.262, bf16[1536,512]{0,1:T(8,128)(2,1)S(1)} %bitcast.447), kind=kOutput, calls=%fused_computation.311 | convolution fusion | flops 1207959552 | bytes 7077888 | tf_op jit(solution)/shard_map/dot_general | solution.py:359
  162.2 1.7 convolution_bitcast_fusion.1
  164.0 2.0 convolution_bitcast_fusion.4
  166.0 1.1 convolution_bitcast_fusion.5
  167.9 17.1 %shard_map.357 = (bf16[768,768]{1,0:T(8,128)(2,1)}, f32[4,384]{1,0:T(4,128)}) custom-call(f32[768]{0:T(1024)} %pad_maximum_fusion.10.ma_ref, f32[768]{0:T(1024)} %pad_maximum_fusion.11.mb_ref, f32[4,384]{1,0:T(4,128)} %pad_maximum_fusion.9.coef_ref, f32[768,4]{1,0:T(8,128)} %copy.126.masks_ref, f32[768,1536]{1,0:T(8,128)} %fusion.109.g_ref, ...), custom_call_target="tpu_custom_call" | custom-call | flops 17694720 | bytes 14155776 | tf_op jit(solution)/shard_map/pallas_call | solution.py:328
  185.1 1.8 convolution_bitcast_fusion.3
  187.0 4.8 %fusion.84 = (f32[512]{0:T(512)S(1)}, f32[512]{0:T(512)S(1)}, f32[512]{0:T(512)S(1)}, f32[768]{0:T(1024)}, f32[768]{0:T(1024)}, /*index=5*/f32[768,512]{1,0:T(8,128)}, f32[768,512]{1,0:T(8,128)}) fusion(f32[768]{0:T(1024)S(1)} %copy-done.52, f32[768]{0:T(1024)S(1)} %copy-done.54, bf16[768,512]{1,0:T(8,128)(2,1)S(1)} %all_gather.21, ...), kind=kOutput, calls=%fused_computation.297 | convolution fusion | flops 610268160 | bytes 7495680 | tf_op jit(solution)/shard_map/dot_general | solution.py:497
  192.8 1.2 constant_dynamic-update-slice_fusion.4
  194.3 1.5 pad_maximum_fusion.2
  197.7 1.8 pad_bitcast_fusion.refs_0_
  199.5 62.4 %shard_map.358 = bf16[5888,128]{1,0:T(8,128)(2,1)} custom-call(f32[5888,128]{1,0:T(8,128)} %pad_bitcast_fusion.refs_0_), custom_call_target="tpu_custom_call" | custom-call | tf_op jit(solution)/shard_map/pallas_call | solution.py:211
  261.8 1.6 convert_element_type.138
  264.6 1.9 constant_dynamic-slice_fusion
  270.0 3.4 %add_multiply_fusion.3 = (f32[2,128,768]{2,1,0:T(8,128)}, f32[2,128,768]{2,1,0:T(8,128)}, f32[2,128,768]{2,1,0:T(8,128)}) fusion(f32[2,128,768]{2,1,0:T(8,128)} %param.33, f32[2,128,768]{2,1,0:T(8,128)S(1)} %copy-done.17, f32[2,128,768]{2,1,0:T(8,128)} %mul.1534, f32[2,128,768]{2,1,0:T(8,128)} %param.28), kind=kLoop, calls=%fused_computation.95 | loop fusion | flops 1966080 | bytes 5505024 | tf_op jit(solution)/shard_map/add | solution.py:348
  273.5 2.7 add_multiply_fusion
  276.2 1.3 add_multiply_fusion.4
  278.2 2.4 dynamic-slice_add_fusion
  (284 shorter events, 27.7 us)
Async XLA Ops:
  7.2 38.2 %all-gather.5.cloned.1.call-start = ((), (), s32[]{:S(2)}) async-start(), calls=%async_computation | async-start | bytes 3604480 | tf_op jit(solution)/shard_map/all_gather | solution.py:373
  10.3 8.5 %copy-start.36 = (f32[2,3,384]{2,0,1:T(2,128)S(1)}, f32[2,3,384]{2,0,1:T(2,128)}, u32[]{:S(2)}) copy-start(f32[2,3,384]{2,0,1:T(2,128)} %param.27) | copy-start | bytes 27652
  10.3 12.9 %copy-start.37 = (bf16[768,128]{1,0:T(8,128)(2,1)S(1)}, bf16[768,128]{1,0:T(8,128)(2,1)}, u32[]{:S(2)}) copy-start(bf16[768,128]{1,0:T(8,128)(2,1)} %param.19) | copy-start | bytes 589828
  11.3 66.7 %all-gather.7.cloned.1.call-start = ((), (), s32[]{:S(2)}) async-start(), calls=%async_computation.1 | async-start | bytes 3604480 | tf_op jit(solution)/shard_map/all_gather | solution.py:373
  11.5 26.0 %copy-start.39 = (f32[768]{0:T(1024)}, f32[768]{0:T(1024)S(1)}, u32[]{:S(2)}) copy-start(f32[768]{0:T(1024)S(1)} %get-tuple-element.251.mb_ref) | copy-start | bytes 9220
  11.5 25.9 %copy-start.40 = (f32[768]{0:T(1024)}, f32[768]{0:T(1024)S(1)}, u32[]{:S(2)}) copy-start(f32[768]{0:T(1024)S(1)} %get-tuple-element.252.ma_ref) | copy-start | bytes 9220
  19.4 18.6 %copy-start.43 = (f32[1,384]{1,0:T(1,128)}, f32[1,384]{1,0:T(1,128)S(1)}, u32[]{:S(2)}) copy-start(f32[1,384]{1,0:T(1,128)S(1)} %get-tuple-element.201) | copy-start | bytes 4612
  19.4 18.6 %copy-start.45 = (f32[1,384]{1,0:T(1,128)}, f32[1,384]{1,0:T(1,128)S(1)}, u32[]{:S(2)}) copy-start(f32[1,384]{1,0:T(1,128)S(1)} %get-tuple-element.202) | copy-start | bytes 4612
  19.4 18.6 %copy-start.57 = (f32[1,384]{1,0:T(1,128)}, f32[1,384]{1,0:T(1,128)S(1)}, u32[]{:S(2)}) copy-start(f32[1,384]{1,0:T(1,128)S(1)} %get-tuple-element.200) | copy-start | bytes 4612
  20.7 17.4 %copy-start.47 = (f32[1,384]{1,0:T(1,128)}, f32[1,384]{1,0:T(1,128)S(1)}, u32[]{:S(2)}) copy-start(f32[1,384]{1,0:T(1,128)S(1)} %get-tuple-element.244) | copy-start | bytes 4612
  20.7 17.4 %copy-start.49 = (f32[1,384]{1,0:T(1,128)}, f32[1,384]{1,0:T(1,128)S(1)}, u32[]{:S(2)}) copy-start(f32[1,384]{1,0:T(1,128)S(1)} %get-tuple-element.245) | copy-start | bytes 4612
  37.0 29.4 %copy-start.53 = (f32[768]{0:T(1024)}, f32[768]{0:T(1024)S(1)}, u32[]{:S(2)}) copy-start(f32[768]{0:T(1024)S(1)} %broadcast_multiply_fusion.6) | copy-start | bytes 9220
  37.5 29.0 %copy-start.51 = (f32[768]{0:T(1024)}, f32[768]{0:T(1024)S(1)}, u32[]{:S(2)}) copy-start(f32[768]{0:T(1024)S(1)} %add_rsqrt_fusion.1) | copy-start | bytes 9220
  37.6 28.9 %copy-start.70 = (f32[1,1,512]{2,1,0:T(1,128)}, f32[1,1,512]{2,1,0:T(1,128)S(1)}, u32[]{:S(2)}) copy-start(f32[1,1,512]{2,1,0:T(1,128)S(1)} %get-tuple-element.237) | copy-start | bytes 6148
  37.6 28.9 %copy-start.72 = (f32[1,1,512]{2,1,0:T(1,128)}, f32[1,1,512]{2,1,0:T(1,128)S(1)}, u32[]{:S(2)}) copy-start(f32[1,1,512]{2,1,0:T(1,128)S(1)} %get-tuple-element.238) | copy-start | bytes 6148
  37.6 28.9 %copy-start.85 = (f32[1,1,512]{2,1,0:T(1,128)}, f32[1,1,512]{2,1,0:T(1,128)S(1)}, u32[]{:S(2)}) copy-start(f32[1,1,512]{2,1,0:T(1,128)S(1)} %get-tuple-element.236) | copy-start | bytes 6148
  37.6 64.1 %copy-start.62 = (f32[1,1,512]{2,1,0:T(1,128)}, f32[1,1,512]{2,1,0:T(1,128)S(1)}, u32[]{:S(2)}) copy-start(f32[1,1,512]{2,1,0:T(1,128)S(1)} %get-tuple-element.234) | copy-start | bytes 6148
  37.6 64.0 %copy-start.74 = (f32[1,1,512]{2,1,0:T(1,128)}, f32[1,1,512]{2,1,0:T(1,128)S(1)}, u32[]{:S(2)}) copy-start(f32[1,1,512]{2,1,0:T(1,128)S(1)} %get-tuple-element.233) | copy-start | bytes 6148
  37.7 64.0 %copy-start.87 = (f32[1,1,512]{2,1,0:T(1,128)}, f32[1,1,512]{2,1,0:T(1,128)S(1)}, u32[]{:S(2)}) copy-start(f32[1,1,512]{2,1,0:T(1,128)S(1)} %get-tuple-element.232) | copy-start | bytes 6148
  38.1 14.5 %copy-start.14 = (bf16[768,512]{1,0:T(8,128)(2,1)}, bf16[768,512]{1,0:T(8,128)(2,1)S(1)}, u32[]{:S(2)}) copy-start(bf16[768,512]{1,0:T(8,128)(2,1)S(1)} %fusion.15) | copy-start | bytes 2359300
  56.4 10.1 %copy-start.4 = (bf16[1536,4,128]{0,2,1:T(8,128)(2,1)S(1)}, bf16[1536,4,128]{0,2,1:T(8,128)(2,1)}, u32[]{:S(2)}) copy-start(bf16[1536,4,128]{0,2,1:T(8,128)(2,1)} %copy.119) | copy-start | bytes 4718596
  66.5 7.9 %copy-start.34 = (bf16[512,4,128]{0,2,1:T(8,128)(2,1)S(1)}, bf16[512,4,128]{0,2,1:T(8,128)(2,1)}, u32[]{:S(2)}) copy-start(bf16[512,4,128]{0,2,1:T(8,128)(2,1)} %copy.120) | copy-start | bytes 1572868
  76.5 25.2 %copy-start.41 = (f32[768]{0:T(1024)}, f32[768]{0:T(1024)S(1)}, u32[]{:S(2)}) copy-start(f32[768]{0:T(1024)S(1)} %broadcast_multiply_fusion.5) | copy-start | bytes 9220
  76.9 24.9 %copy-start.55 = (f32[768]{0:T(1024)}, f32[768]{0:T(1024)S(1)}, u32[]{:S(2)}) copy-start(f32[768]{0:T(1024)S(1)} %add_rsqrt_fusion) | copy-start | bytes 9220
  77.9 9.9 %copy-start.15 = (bf16[768,512]{1,0:T(8,128)(2,1)}, bf16[768,512]{1,0:T(8,128)(2,1)S(1)}, u32[]{:S(2)}) copy-start(bf16[768,512]{1,0:T(8,128)(2,1)S(1)} %fusion.16) | copy-start | bytes 2359300
  91.6 10.1 %copy-start.3 = (f32[768,512]{1,0:T(8,128)S(1)}, f32[768,512]{1,0:T(8,128)}, u32[]{:S(2)}) copy-start(f32[768,512]{1,0:T(8,128)} %copy-done.2) | copy-start | bytes 4718596
  101.7 7.3 %copy-start.25 = (bf16[512,4,128]{0,2,1:T(8,128)(2,1)S(1)}, bf16[512,4,128]{0,2,1:T(8,128)(2,1)}, u32[]{:S(2)}) copy-start(bf16[512,4,128]{0,2,1:T(8,128)(2,1)} %copy.125) | copy-start | bytes 1572868
  109.0 10.9 %copy-start.6 = (f32[768,512]{1,0:T(8,128)}, f32[768,512]{1,0:T(8,128)S(1)}, u32[]{:S(2)}) copy-start(f32[768,512]{1,0:T(8,128)S(1)} %get-tuple-element.205) | copy-start | bytes 4718596
  120.0 7.0 %slice-start.2 = ((s8[4718592]{0:T(1024)(128)(4,1)}), s8[524288]{0:T(1024)(128)(4,1)S(1)}, s32[]{:S(2)}) async-start(s8[4718592]{0:T(1024)(128)(4,1)} %bitcast.444), calls=%async_computation.4 | async-start | bytes 1048576
  121.1 5.9 %slice-start.3 = ((s8[4718592]{0:T(1024)(128)(4,1)}), s8[4194304]{0:T(1024)(128)(4,1)S(1)}, s32[]{:S(2)}) async-start(s8[4718592]{0:T(1024)(128)(4,1)} %bitcast.444), calls=%async_computation.5 | async-start | bytes 8388608
  147.8 3.9 %copy-start.11 = (f32[768,512]{1,0:T(8,128)S(1)}, f32[768,512]{1,0:T(8,128)}, u32[]{:S(2)}) copy-start(f32[768,512]{1,0:T(8,128)} %copy-done.10) | copy-start | bytes 4718596
  147.8 3.9 %copy-start.29 = (f32[768,512]{1,0:T(8,128)S(1)}, f32[768,512]{1,0:T(8,128)}, u32[]{:S(2)}) copy-start(f32[768,512]{1,0:T(8,128)} %get-tuple-element.255) | copy-start | bytes 4718596
  151.7 10.4 %slice-start = ((s8[4718592]{0:T(1024)(128)(4,1)}), s8[524288]{0:T(1024)(128)(4,1)S(1)}, s32[]{:S(2)}) async-start(s8[4718592]{0:T(1024)(128)(4,1)} %bitcast.442), calls=%async_computation.2 | async-start | bytes 1048576
  153.5 5.1 %copy-start.22 = (f32[768,512]{1,0:T(8,128)}, f32[768,512]{1,0:T(8,128)S(1)}, u32[]{:S(2)}) copy-start(f32[768,512]{1,0:T(8,128)S(1)} %get-tuple-element.187) | copy-start | bytes 4718596
  153.5 5.1 %copy-start.5 = (bf16[1536,4,128]{0,2,1:T(8,128)(2,1)S(1)}, bf16[1536,4,128]{0,2,1:T(8,128)(2,1)}, u32[]{:S(2)}) copy-start(bf16[1536,4,128]{0,2,1:T(8,128)(2,1)} %copy.119) | copy-start | bytes 4718596
  153.5 8.6 %slice-start.1 = ((s8[4718592]{0:T(1024)(128)(4,1)}), s8[4194304]{0:T(1024)(128)(4,1)S(1)}, s32[]{:S(2)}) async-start(s8[4718592]{0:T(1024)(128)(4,1)} %bitcast.442), calls=%async_computation.3 | async-start | bytes 8388608
  164.0 3.4 %copy-start.79 = (f32[1,384]{1,0:T(1,128)S(1)}, f32[1,384]{1,0:T(1,128)}, u32[]{:S(2)}) copy-start(f32[1,384]{1,0:T(1,128)} %get-tuple-element.241) | copy-start | bytes 4612
  167.9 19.0 %copy-start.94 = (f32[768,512]{1,0:T(8,128)S(1)}, f32[768,512]{1,0:T(8,128)}, u32[]{:S(2)}) copy-start(f32[768,512]{1,0:T(8,128)} %get-tuple-element.263) | copy-start | bytes 4718596
  263.7 9.8 %copy-start.12 = (f32[3072,128]{1,0:T(8,128)}, f32[3072,128]{1,0:T(8,128)S(1)}, u32[]{:S(2)}) copy-start(f32[3072,128]{1,0:T(8,128)S(1)} %slice_multiply_fusion) | copy-start | bytes 4718596
  263.7 4.5 %copy-start.67 = (f32[2,3,384]{2,0,1:T(2,128)S(1)}, f32[2,3,384]{2,0,1:T(2,128)}, u32[]{:S(2)}) copy-start(f32[2,3,384]{2,0,1:T(2,128)} %param.37) | copy-start | bytes 27652
  263.7 4.5 %copy-start.68 = (f32[2,3,384]{2,0,1:T(2,128)S(1)}, f32[2,3,384]{2,0,1:T(2,128)}, u32[]{:S(2)}) copy-start(f32[2,3,384]{2,0,1:T(2,128)} %param.32) | copy-start | bytes 27652
  263.7 6.3 %copy-start.83 = (f32[768]{0:T(1024)S(1)}, f32[768]{0:T(1024)}, u32[]{:S(2)}) copy-start(f32[768]{0:T(1024)} %get-tuple-element.212) | copy-start | bytes 9220
  263.7 6.3 %copy-start.84 = (f32[768]{0:T(1024)S(1)}, f32[768]{0:T(1024)}, u32[]{:S(2)}) copy-start(f32[768]{0:T(1024)} %get-tuple-element.213) | copy-start | bytes 9220
  263.7 6.3 %copy-start.17 = (f32[2,128,768]{2,1,0:T(8,128)S(1)}, f32[2,128,768]{2,1,0:T(8,128)}, u32[]{:S(2)}) copy-start(f32[2,128,768]{2,1,0:T(8,128)} %param.23) | copy-start | bytes 2359300
  264.6 13.0 %copy-start.66 = (f32[8,128]{1,0:T(8,128)}, f32[8,128]{1,0:T(8,128)S(1)}, u32[]{:S(2)}) copy-start(f32[8,128]{1,0:T(8,128)S(1)} %slice_multiply_fusion.4) | copy-start | bytes 12292
  270.0 3.4 %copy-start.9 = (f32[2,1536,128]{2,1,0:T(8,128)S(1)}, f32[2,1536,128]{2,1,0:T(8,128)}, u32[]{:S(2)}) copy-start(f32[2,1536,128]{2,1,0:T(8,128)} %param.24) | copy-start | bytes 4718596
  270.0 3.4 %copy-start.27 = (f32[2,1536,128]{2,1,0:T(8,128)S(1)}, f32[2,1536,128]{2,1,0:T(8,128)}, u32[]{:S(2)}) copy-start(f32[2,1536,128]{2,1,0:T(8,128)} %param.34) | copy-start | bytes 4718596
  270.0 3.4 %copy-start.28 = (f32[2,1536,128]{2,1,0:T(8,128)S(1)}, f32[2,1536,128]{2,1,0:T(8,128)}, u32[]{:S(2)}) copy-start(f32[2,1536,128]{2,1,0:T(8,128)} %param.29) | copy-start | bytes 4718596
  (54 other events, 107.4 us)
Sparse Core Ops, SparseCore 0:
  11.4 33.9 all-gather.4
  46.9 27.0 all-gather.6

commit v9 on v8

--- a/solution.py
+++ b/solution.py
@@ -365,25 +365,50 @@
     return lax.all_gather(value, "feat", axis=axis, tiled=True)
 
 
-def gather_layer_weights(in_shard, out_shard, gate_shard, after=None):
-    pieces = (in_shard.T, out_shard, gate_shard)
-    packed = jnp.concatenate([piece.astype(jnp.bfloat16) for piece in pieces], 0)
+def split_exact(value):
+    high = lax.reduce_precision(value, exponent_bits=8, mantissa_bits=7)
+    rest = value - high
+    middle = lax.reduce_precision(rest, exponent_bits=8, mantissa_bits=7)
+    low = rest - middle
+    return jnp.concatenate([high, middle, low], 0).astype(jnp.bfloat16)
+
+
+def join_exact(pieces):
+    third = pieces.shape[-2] // 3
+    pieces = pieces.astype(jnp.float32)
+    return pieces[..., :third, :] + (pieces[..., third : 2 * third, :] + pieces[..., 2 * third :, :])
+
+
+def gather_packed(pieces, after=None):
+    packed = jnp.concatenate(pieces, 0)
     if after is not None:
         packed, after = lax.optimization_barrier((packed, after))
-    stacked = lax.all_gather(packed, "feat", axis=0, tiled=False)
+    parts = lax.axis_size("feat")
+    cores = 2
+    across = [[c + cores * k for k in range(parts // cores)] for c in range(cores)]
+    within = [[cores * k + c for c in range(cores)] for k in range(parts // cores)]
+    stage = lax.all_gather(packed, "feat", axis=0, tiled=False, axis_index_groups=across)
+    stage = lax.all_gather(stage, "feat", axis=0, tiled=False, axis_index_groups=within)
+    stacked = jnp.swapaxes(stage, 0, 1).reshape((parts,) + packed.shape)
     result = []
     start = 0
     for piece in pieces:
         result.append(stacked[:, start : start + piece.shape[0]])
         start += piece.shape[0]
-    in_t, out_w, gate_w = result
-    in_full = jnp.transpose(in_t, (0, 2, 1)).reshape(-1, in_t.shape[1])
-    return [in_full, lanes_joined(out_w), lanes_joined(gate_w), stacked]
+    return result
 
 
 def lanes_joined(stacked):
     moved = jnp.moveaxis(stacked, 0, 1)
     return moved.reshape(moved.shape[0], -1)
+
+
+def layer_weights(in_shard, out_shard, gate_shard, extra, after=None):
+    pieces = [in_shard.T.astype(jnp.bfloat16), out_shard.astype(jnp.bfloat16), gate_shard.astype(jnp.bfloat16)]
+    gathered = gather_packed(pieces + list(extra), after)
+    in_t, out_w, gate_w = gathered[:3]
+    in_full = jnp.transpose(in_t, (0, 2, 1)).reshape(-1, in_t.shape[1])
+    return [in_full, lanes_joined(out_w), lanes_joined(gate_w), gathered[3:]]
 
 
 def lanes_of(value, parts):
@@ -427,13 +452,23 @@
     before_prev = jnp.concatenate([carry_prev[1:], zero])
     mask_columns = jnp.stack([alive, carry_prev, carry_next, jnp.zeros_like(alive)], 1)
 
-    weights = [gather_layer_weights(input_matrix[0], output_matrix[0], gate_matrix[0])]
+    feature_pieces = split_exact(feature_vectors.reshape(-1, shard))
+    weights = [
+        layer_weights(
+            input_matrix[0],
+            output_matrix[0],
+            gate_matrix[0],
+            (feature_pieces, activations_in) + (() if layers > 1 else (cotangent,)),
+        )
+    ]
     for k in range(1, layers):
+        extra = (cotangent,) if k == layers - 1 else ()
         weights.append(
-            gather_layer_weights(input_matrix[k], output_matrix[k], gate_matrix[k], weights[-1][3])
+            layer_weights(input_matrix[k], output_matrix[k], gate_matrix[k], extra, weights[-1][3][0])
         )
-    feature_all = gather_feat(feature_vectors, 2)
-    stream = gather_feat(activations_in, 1).astype(jnp.float32)
+    feature_all = lanes_joined(join_exact(weights[0][3][0])).reshape(feature_vectors.shape[:-1] + (-1,))
+    stream = lanes_joined(weights[0][3][1]).astype(jnp.float32)
+    cotangent_all = lanes_joined(weights[-1][3][-1]) if layers > 1 else lanes_joined(weights[0][3][2])
 
     saved = []
     for layer in range(layers):
@@ -469,8 +504,7 @@
         saved.append((scale, unit, normed_low, drive, states, states_low, mixed, act, act_low, pre))
         stream = stream + act * jax.nn.sigmoid(pre)
 
-    stream, cotangent = lax.optimization_barrier((stream, cotangent))
-    grad = gather_feat(cotangent, 1).astype(jnp.float32) * alive[:, None]
+    grad = cotangent_all.astype(jnp.float32) * alive[:, None]
     layer_grads = [None] * layers
     for layer in reversed(range(layers)):
         scale, unit, normed_low, drive, states, states_low, mixed, act, act_low, pre = saved[layer]

time: 288 us -> 338 us (1.17)
  waiting for transfers between devices: 6.36 us -> 76.5 us
  blocking collectives: 28.5 us -> 0 us
  local copies, waits for them, and re-layouts: 32.6 us -> 39.4 us
    all_gather x2 -> x4, waiting for transfers between devices: 6.33 us -> 76.5 us  [the longest x2 63.4 us: gather_packed(): lax.all_gather(packed, 'feat', axis=0, tiled=False, axis_index_groups=acr...]
    all_gather x3 -> x0, blocking collectives: 28.5 us -> none  [gather_feat(): return lax.all_gather(value, 'feat', axis=axis, tiled=True)]
    transpose x8 -> x4, local copies, waits for them, and re-layouts: 11.9 us -> 1.84 us  [lanes_joined(): moved = jnp.moveaxis(stacked, 0, 1)]
    unnamed x209 -> x228, local copies, waits for them, and re-layouts: 8.78 us -> 15.8 us
    transpose x4 -> x3, local copies, waits for them, and re-layouts: 5 us -> 10.1 us  [the longest x2 9.77 us: gather_packed(): stacked = jnp.swapaxes(stage, 0, 1).reshape((parts,) + packed.shape)]
    convert_element_type x3 -> x5, local copies, waits for them, and re-layouts: 0.1 us -> 4.11 us  [the longest x2 4.06 us: body(): stream = lanes_joined(weights[0][3][1]).astype(jnp.float32)]
    dot_general x4, matrix products: 14.5 us -> 18.2 us  [contract_cols(): lax.dot_general(left, right, (((1,), (1,)), ((), ())), preferred_element_...]
  transfers between devices with their start and end apart: 2 -> 4, of which waited for: 1 -> 4; matrix products, arithmetic and copies ran while one was open for 10% -> 5% of each run, Pallas kernels for 3% -> 0%
where the time goes in v9:
time: 338 us; the launch traced here: 337 us
  Pallas kernels  116 us (34%)
  waiting for transfers between devices  76.5 us (23%)
  matrix products  53.6 us (16%)
  local copies, waits for them, and re-layouts  39.4 us (12%)
  other arithmetic  36.5 us (11%)
  between operations  15 us (4%)
    all_gather x2, waiting for transfers between devices, gather_packed(): lax.all_gather(packed, 'feat', axis=0, tiled=False, axis_index_groups=acr...  63.4 us
    pallas_call x1, Pallas kernels, ring_sum(): pl.pallas_call(lambda *refs: ring_sum_kernel(n, *refs), out_shape=jax.Sha...  61.8 us
    pallas_call x2, Pallas kernels, adjoint(): pl.pallas_call(adjoint_kernel, out_shape=(jax.ShapeDtypeStruct((count, 2...  34.1 us
    pallas_call x2, Pallas kernels, recurrence(): pl.pallas_call(recurrence_kernel, out_shape=jax.ShapeDtypeStruct((count,...  20.1 us
    dot_general x4, matrix products, contract_cols(): lax.dot_general(left, right, (((1,), (1,)), ((), ())), preferred_element_...  18.2 us
    unnamed x228, local copies, waits for them, and re-layouts  15.8 us
    dot_general x2, matrix products, body(): jnp.dot(states_low, out_low, preferred_element_type=jnp.float32)  13.4 us
    all_gather x2, waiting for transfers between devices, gather_packed(): lax.all_gather(stage, 'feat', axis=0, tiled=False, axis_index_groups=within)  13 us
  transfers between devices with their start and end apart: 4, of which 4 were waited for; matrix products, arithmetic and copies ran while one was open for 5% of the time, Pallas kernels for 0%

profile of v9, /device:TPU:0, one launch (start us, length us, event | category | flops | bytes accessed | tf_op | source)
XLA Modules:
  0.0 337.3 jit_solution(15883252670882451280)
XLA Ops:
  7.3 1.2 convert.30
  12.9 31.1 %all-gather.13.cloned.1.call-done = bf16[7168,128]{1,0:T(8,128)(2,1)} async-done(((bf16[3584,128]{1,0:T(8,128)(2,1)}), bf16[7168,128]{1,0:T(8,128)(2,1)}) %all-gather.13.cloned.1.call-update) | async-done | bytes 1835024 | tf_op jit(solution)/shard_map/all_gather | solution.py:390
  44.0 32.4 %all-gather.9.cloned.1.call-done = bf16[7216,128]{1,0:T(8,128)(2,1)} async-done(((bf16[3608,128]{1,0:T(8,128)(2,1)}), bf16[7216,128]{1,0:T(8,128)(2,1)}) %all-gather.9.cloned.1.call-update) | async-done | bytes 1847312 | tf_op jit(solution)/shard_map/all_gather | solution.py:390
  81.7 9.2 %all-gather.15.cloned.1.call-done = bf16[4,3584,128]{2,1,0:T(8,128)(2,1)} async-done(((bf16[2,3584,128]{2,1,0:T(8,128)(2,1)}), bf16[4,3584,128]{2,1,0:T(8,128)(2,1)}) %all-gather.15.cloned.1.call-update) | async-done | bytes 3670032 | tf_op jit(solution)/shard_map/all_gather | solution.py:391
  90.9 7.5 %copy.111 = bf16[2,2,3584,128]{3,1,0,2:T(2,128)(2,1)S(1)} copy(bf16[2,2,3584,128]{3,2,0,1:T(8,128)(2,1)} %bitcast.525) | data formatting | bytes 7340032 | tf_op jit(solution)/shard_map/transpose | solution.py:392
  99.4 1.4 slice.298
  100.9 1.7 slice_convert_fusion
  102.6 3.8 %all-gather.11.cloned.1.call-done = bf16[4,3608,128]{2,1,0:T(8,128)(2,1)} async-done(((bf16[2,3608,128]{2,1,0:T(8,128)(2,1)}), bf16[4,3608,128]{2,1,0:T(8,128)(2,1)}) %all-gather.11.cloned.1.call-update) | async-done | bytes 3694608 | tf_op jit(solution)/shard_map/all_gather | solution.py:391
  106.5 2.3 copy.103
  109.1 1.9 slice_bitcast_fusion.1
  113.6 2.4 copy.104
  116.0 1.6 copy.110
  117.6 2.3 convolution_bitcast_fusion.2.drive_ref
  121.3 1.6 pad_maximum_fusion.xa_ref.xb_ref
  122.9 10.0 %shard_map.354.states_ref = f32[768,1536]{1,0:T(8,128)} custom-call(f32[768]{0:T(1024)} %copy-done.48, f32[768]{0:T(1024)} %copy-done.47, f32[2,384]{1,0:T(2,128)} %pad_maximum_fusion.12.w_ref, f32[768,768]{1,0:T(8,128)} %pad_maximum_fusion.xa_ref.xb_ref, f32[768,768]{1,0:T(8,128)} %pad_maximum_fusion.xa_ref.xb_ref), custom_call_target="tpu_custom_call" | custom-call | flops 11796480 | bytes 9437184 | tf_op jit(solution)/shard_map/pallas_call | solution.py:82
  133.0 1.5 multiply_add_fusion.12
  134.4 2.0 copy-done
  136.4 5.8 %multiply_multiply_fusion.11 = (f32[768,512]{1,0:T(8,128)S(1)}, f32[768,512]{1,0:T(8,128)}) fusion(f32[768,512]{1,0:T(8,128)S(1)} %get-tuple-element.182, f32[512]{0:T(512)S(1)} %bitcast.554, bf16[1536,512]{0,1:T(8,128)(2,1)S(1)} %bitcast.515, f32[768,1536]{1,0:T(8,128)S(1)} %copy-done), kind=kOutput, calls=%fused_computation.83 | convolution fusion | flops 1235091456 | bytes 11012096 | tf_op jit(solution)/shard_map/dot_general | solution.py:498
  142.2 2.0 fusion.130
  147.2 1.0 copy-done.2
  148.2 1.6 pad_maximum_fusion.1.xa_ref.xb_ref
  149.8 10.1 %shard_map.355.states_ref = f32[768,1536]{1,0:T(8,128)} custom-call(f32[768]{0:T(1024)} %copy-done.48, f32[768]{0:T(1024)} %copy-done.47, f32[2,384]{1,0:T(2,128)} %pad_maximum_fusion.13.w_ref, f32[768,768]{1,0:T(8,128)} %pad_maximum_fusion.1.xa_ref.xb_ref, f32[768,768]{1,0:T(8,128)} %pad_maximum_fusion.1.xa_ref.xb_ref), custom_call_target="tpu_custom_call" | custom-call | flops 11796480 | bytes 9437184 | tf_op jit(solution)/shard_map/pallas_call | solution.py:82
  159.9 7.6 %multiply_multiply_fusion.10 = (f32[768,512]{1,0:T(8,128)S(1)}, f32[768,512]{1,0:T(8,128)S(1)}) fusion(f32[512]{0:T(512)S(1)} %bitcast.559, f32[512]{0:T(512)S(1)} %bitcast.548, f32[768]{0:T(1024)S(1)} %add_rsqrt_fusion, f32[768,512]{1,0:T(8,128)S(1)} %copy-done.4, f32[768]{0:T(1024)S(1)} %broadcast_multiply_fusion.5, f32[512]{0:T(512)S(1)} %bitcast.564, ...), kind=kOutput, calls=%fused_computation.81 | convolution fusion | flops 1236664320 | bytes 11022336 | tf_op jit(solution)/shard_map/dot_general | solution.py:498
  167.5 1.6 convert_reduce_fusion.1
  169.1 1.1 convolution_bitcast_fusion.5
  171.1 5.2 %fusion.133 = (bf16[768,512]{1,0:T(8,128)(2,1)S(1)}, f32[768,512]{1,0:T(8,128)}) fusion(f32[768,512]{1,0:T(8,128)S(1)} %get-tuple-element.225, bf16[768,512]{1,0:T(8,128)(2,1)S(1)} %get-tuple-element.162, bf16[64,8,4,128]{3,2,1,0:T(4,128)(2,1)S(1)} %bitcast.539, f32[768,512]{1,0:T(8,128)S(1)} %get-tuple-element.226, f32[768]{0:T(1024)S(1)} %get-tuple-element.218, ...), kind=kOutput, calls=%fused_computation.344 | convolution fusion | flops 432144384 | bytes 8391680 | tf_op jit(solution)/shard_map/dot_general | solution.py:359
  176.4 1.7 convolution_bitcast_fusion
  178.1 3.6 %fusion.8.g_ref = f32[768,1536]{1,0:T(8,128)} fusion(bf16[768,512]{1,0:T(8,128)(2,1)S(1)} %get-tuple-element.227, bf16[192,8,4,128]{3,2,1,0:T(4,128)(2,1)S(1)} %bitcast.535), kind=kOutput, calls=%fused_computation.19 | convolution fusion | flops 1207959552 | bytes 7077888 | tf_op jit(solution)/shard_map/dot_general | solution.py:359
  181.8 17.1 %shard_map.356 = (bf16[768,768]{1,0:T(8,128)(2,1)}, f32[4,384]{1,0:T(4,128)}) custom-call(f32[768]{0:T(1024)} %get-tuple-element.233.ma_ref, f32[768]{0:T(1024)} %get-tuple-element.234.mb_ref, f32[4,384]{1,0:T(4,128)} %pad_maximum_fusion.7.coef_ref, f32[768,4]{1,0:T(8,128)} %copy.114.masks_ref, f32[768,1536]{1,0:T(8,128)} %fusion.8.g_ref, ...), custom_call_target="tpu_custom_call" | custom-call | flops 17694720 | bytes 14155776 | tf_op jit(solution)/shard_map/pallas_call | solution.py:328
  198.9 1.8 convolution_bitcast_fusion.3
  200.8 3.8 %multiply_reduce_fusion.1 = (f32[512]{0:T(512)}, f32[768]{0:T(1024)S(1)}, f32[512]{0:T(512)}, f32[768]{0:T(1024)S(1)}, f32[512]{0:T(512)}, /*index=5*/f32[768,512]{1,0:T(8,128)S(1)}) fusion(f32[768]{0:T(1024)S(1)} %copy-done.63, f32[768,512]{1,0:T(8,128)S(1)} %copy-done.4, f32[768]{0:T(1024)S(1)} %copy-done.50, f32[512]{0:T(512)S(1)} %bitcast.549, ...), kind=kOutput, calls=%fused_computation.33 | convolution fusion | flops 609874944 | bytes 6709248 | tf_op jit(solution)/shard_map/dot_general | solution.py:531
  204.6 1.7 convert_reduce_fusion.2
  206.4 1.1 convolution_bitcast_fusion.6
  208.4 5.7 %multiply_reduce_fusion.2 = (f32[512]{0:T(512)}, bf16[768,512]{1,0:T(8,128)(2,1)S(1)}, f32[768,512]{1,0:T(8,128)}) fusion(f32[768,512]{1,0:T(8,128)S(1)} %copy-done.29, f32[768,512]{1,0:T(8,128)S(1)} %copy-done.103, bf16[768,512]{1,0:T(8,128)(2,1)S(1)} %get-tuple-element.159, bf16[512,512]{0,1:T(8,128)(2,1)S(1)} %bitcast.537, ...), kind=kOutput, calls=%fused_computation.35 | convolution fusion | flops 432537088 | bytes 9963520 | tf_op jit(solution)/shard_map/dot_general | solution.py:359
  214.2 1.7 convolution_bitcast_fusion.1
  215.9 3.6 %fusion.134.g_ref = f32[768,1536]{1,0:T(8,128)} fusion(bf16[768,512]{1,0:T(8,128)(2,1)S(1)} %get-tuple-element.193, bf16[1536,512]{0,1:T(8,128)(2,1)S(1)} %bitcast.516), kind=kOutput, calls=%fused_computation.345 | convolution fusion | flops 1207959552 | bytes 7077888 | tf_op jit(solution)/shard_map/dot_general | solution.py:359
  222.2 17.1 %shard_map.357 = (bf16[768,768]{1,0:T(8,128)(2,1)}, f32[4,384]{1,0:T(4,128)}) custom-call(f32[768]{0:T(1024)} %get-tuple-element.233.ma_ref, f32[768]{0:T(1024)} %get-tuple-element.234.mb_ref, f32[4,384]{1,0:T(4,128)} %pad_maximum_fusion.8.coef_ref, f32[768,4]{1,0:T(8,128)} %copy.114.masks_ref, f32[768,1536]{1,0:T(8,128)} %fusion.134.g_ref, ...), custom_call_target="tpu_custom_call" | custom-call | flops 17694720 | bytes 14155776 | tf_op jit(solution)/shard_map/pallas_call | solution.py:328
  239.2 1.8 convolution_bitcast_fusion.4
  242.5 1.4 pad_maximum_fusion.2
  244.6 2.3 fusion.115
  247.3 1.8 pad_bitcast_fusion.refs_0_
  249.1 61.8 %shard_map.358 = bf16[5888,128]{1,0:T(8,128)(2,1)} custom-call(f32[5888,128]{1,0:T(8,128)} %pad_bitcast_fusion.refs_0_), custom_call_target="tpu_custom_call" | custom-call | tf_op jit(solution)/shard_map/pallas_call | solution.py:211
  310.9 1.6 convert_element_type.170
  317.0 2.2 mul.1557
  319.3 2.4 dynamic-slice_add_fusion
  322.3 2.5 add_multiply_fusion.4
  324.9 1.6 add_multiply_fusion.3
  328.1 2.7 add_multiply_fusion
  (312 shorter events, 31.3 us)
Async XLA Ops:
  7.2 36.7 %all-gather.13.cloned.1.call-start = ((), (), s32[]{:S(2)}) async-start(), calls=%async_computation.2 | async-start | bytes 2752512 | tf_op jit(solution)/shard_map/all_gather | solution.py:390
  10.9 65.5 %all-gather.9.cloned.1.call-start = ((), (), s32[]{:S(2)}) async-start(), calls=%async_computation | async-start | bytes 2770944 | tf_op jit(solution)/shard_map/all_gather | solution.py:390
  12.8 78.1 %all-gather.15.cloned.1.call-start = ((), (), s32[]{:S(2)}) async-start(), calls=%async_computation.3 | async-start | bytes 5505024 | tf_op jit(solution)/shard_map/all_gather | solution.py:391
  44.0 32.5 %copy-start.96 = (s32[2]{0:T(128)S(1)}, s32[2]{0:T(128)}, u32[]{:S(2)}) copy-start(s32[2]{0:T(128)} %param.21) | copy-start | bytes 28
  44.0 32.5 %copy-start.102 = (s32[2]{0:T(128)S(1)}, s32[2]{0:T(128)}, u32[]{:S(2)}) copy-start(s32[2]{0:T(128)} %param.22) | copy-start | bytes 28
  44.0 33.8 %copy-start.44 = (f32[2,3,384]{2,0,1:T(2,128)S(1)}, f32[2,3,384]{2,0,1:T(2,128)}, u32[]{:S(2)}) copy-start(f32[2,3,384]{2,0,1:T(2,128)} %param.27) | copy-start | bytes 27652
  44.0 62.5 %all-gather.11.cloned.1.call-start = ((), (), s32[]{:S(2)}) async-start(), calls=%async_computation.1 | async-start | bytes 5541888 | tf_op jit(solution)/shard_map/all_gather | solution.py:391
  76.6 21.8 %copy-start.47 = (f32[768]{0:T(1024)}, f32[768]{0:T(1024)S(1)}, u32[]{:S(2)}) copy-start(f32[768]{0:T(1024)S(1)} %get-tuple-element.219.mb_ref) | copy-start | bytes 9220
  76.6 21.8 %copy-start.48 = (f32[768]{0:T(1024)}, f32[768]{0:T(1024)S(1)}, u32[]{:S(2)}) copy-start(f32[768]{0:T(1024)S(1)} %get-tuple-element.220.ma_ref) | copy-start | bytes 9220
  78.5 19.9 %copy-start.53 = (f32[1,384]{1,0:T(1,128)}, f32[1,384]{1,0:T(1,128)S(1)}, u32[]{:S(2)}) copy-start(f32[1,384]{1,0:T(1,128)S(1)} %get-tuple-element.174) | copy-start | bytes 4612
  78.5 20.0 %copy-start.55 = (f32[1,384]{1,0:T(1,128)}, f32[1,384]{1,0:T(1,128)S(1)}, u32[]{:S(2)}) copy-start(f32[1,384]{1,0:T(1,128)S(1)} %get-tuple-element.175) | copy-start | bytes 4612
  78.5 20.0 %copy-start.66 = (f32[1,384]{1,0:T(1,128)}, f32[1,384]{1,0:T(1,128)S(1)}, u32[]{:S(2)}) copy-start(f32[1,384]{1,0:T(1,128)S(1)} %get-tuple-element.173) | copy-start | bytes 4612
  79.8 18.7 %copy-start.57 = (f32[1,384]{1,0:T(1,128)}, f32[1,384]{1,0:T(1,128)S(1)}, u32[]{:S(2)}) copy-start(f32[1,384]{1,0:T(1,128)S(1)} %get-tuple-element.212) | copy-start | bytes 4612
  79.8 18.7 %copy-start.59 = (f32[1,384]{1,0:T(1,128)}, f32[1,384]{1,0:T(1,128)S(1)}, u32[]{:S(2)}) copy-start(f32[1,384]{1,0:T(1,128)S(1)} %get-tuple-element.213) | copy-start | bytes 4612
  111.7 21.2 %copy-start.64 = (f32[768]{0:T(1024)}, f32[768]{0:T(1024)S(1)}, u32[]{:S(2)}) copy-start(f32[768]{0:T(1024)S(1)} %add_rsqrt_fusion.1) | copy-start | bytes 9220
  111.8 21.1 %copy-start.72 = (f32[1,4,128]{2,0,1:T(1,128)}, f32[1,4,128]{2,0,1:T(1,128)S(1)}, u32[]{:S(2)}) copy-start(f32[1,4,128]{2,0,1:T(1,128)S(1)} %get-tuple-element.206) | copy-start | bytes 6148
  111.8 22.6 %copy-start.79 = (f32[1,4,128]{2,0,1:T(1,128)}, f32[1,4,128]{2,0,1:T(1,128)S(1)}, u32[]{:S(2)}) copy-start(f32[1,4,128]{2,0,1:T(1,128)S(1)} %get-tuple-element.204) | copy-start | bytes 6148
  111.8 48.0 %copy-start.74 = (f32[1,4,128]{2,0,1:T(1,128)}, f32[1,4,128]{2,0,1:T(1,128)S(1)}, u32[]{:S(2)}) copy-start(f32[1,4,128]{2,0,1:T(1,128)S(1)} %get-tuple-element.202) | copy-start | bytes 6148
  111.8 48.0 %copy-start.81 = (f32[1,4,128]{2,0,1:T(1,128)}, f32[1,4,128]{2,0,1:T(1,128)S(1)}, u32[]{:S(2)}) copy-start(f32[1,4,128]{2,0,1:T(1,128)S(1)} %get-tuple-element.201) | copy-start | bytes 6148
  111.8 48.0 %copy-start.94 = (f32[1,4,128]{2,0,1:T(1,128)}, f32[1,4,128]{2,0,1:T(1,128)S(1)}, u32[]{:S(2)}) copy-start(f32[1,4,128]{2,0,1:T(1,128)S(1)} %get-tuple-element.199) | copy-start | bytes 6148
  113.6 20.9 %copy-start.7 = (bf16[1536,4,128]{0,2,1:T(8,128)(2,1)}, bf16[1536,4,128]{0,2,1:T(8,128)(2,1)S(1)}, u32[]{:S(2)}) copy-start(bf16[1536,4,128]{0,2,1:T(8,128)(2,1)S(1)} %copy.107) | copy-start | bytes 4718596
  122.9 10.1 %copy-start.9 = (f32[768,512]{1,0:T(8,128)S(1)}, f32[768,512]{1,0:T(8,128)}, u32[]{:S(2)}) copy-start(f32[768,512]{1,0:T(8,128)} %copy.110) | copy-start | bytes 4718596
  133.0 3.5 %copy-start = (f32[768,1536]{1,0:T(8,128)S(1)}, f32[768,1536]{1,0:T(8,128)}, u32[]{:S(2)}) copy-start(f32[768,1536]{1,0:T(8,128)} %shard_map.354.states_ref) | copy-start | bytes 14155780
  134.4 7.8 %copy-start.28 = (f32[768,512]{1,0:T(8,128)}, f32[768,512]{1,0:T(8,128)S(1)}, u32[]{:S(2)}) copy-start(f32[768,512]{1,0:T(8,128)S(1)} %get-tuple-element.182) | copy-start | bytes 4718596
  136.4 5.8 %copy-start.41 = (bf16[512,4,128]{0,2,1:T(8,128)(2,1)S(1)}, bf16[512,4,128]{0,2,1:T(8,128)(2,1)}, u32[]{:S(2)}) copy-start(bf16[512,4,128]{0,2,1:T(8,128)(2,1)} %copy.109) | copy-start | bytes 1572868
  144.3 15.6 %copy-start.49 = (f32[768]{0:T(1024)}, f32[768]{0:T(1024)S(1)}, u32[]{:S(2)}) copy-start(f32[768]{0:T(1024)S(1)} %broadcast_multiply_fusion.5) | copy-start | bytes 9220
  144.6 15.2 %copy-start.62 = (f32[768]{0:T(1024)}, f32[768]{0:T(1024)S(1)}, u32[]{:S(2)}) copy-start(f32[768]{0:T(1024)S(1)} %add_rsqrt_fusion) | copy-start | bytes 9220
  149.8 10.1 %copy-start.4 = (f32[768,512]{1,0:T(8,128)S(1)}, f32[768,512]{1,0:T(8,128)}, u32[]{:S(2)}) copy-start(f32[768,512]{1,0:T(8,128)} %copy-done.3) | copy-start | bytes 4718596
  159.9 7.6 %copy-start.15 = (f32[4,768,128]{2,0,1:T(4,128)S(1)}, f32[4,768,128]{2,0,1:T(4,128)}, u32[]{:S(2)}) copy-start(f32[4,768,128]{2,0,1:T(4,128)} %get-tuple-element.186) | copy-start | bytes 4718596
  159.9 7.6 %copy-start.43 = (bf16[4,512,128]{2,0,1:T(4,128)(2,1)S(1)}, bf16[4,512,128]{2,0,1:T(4,128)(2,1)}, u32[]{:S(2)}) copy-start(bf16[4,512,128]{2,0,1:T(4,128)(2,1)} %slice.300) | copy-start | bytes 1572868
  170.2 6.2 %slice-start.2 = ((s8[4718592]{0:T(1024)(128)(4,1)}), s8[4194304]{0:T(1024)(128)(4,1)S(1)}, s32[]{:S(2)}) async-start(s8[4718592]{0:T(1024)(128)(4,1)} %bitcast.503), calls=%async_computation.6 | async-start | bytes 8388608
  171.1 5.3 %slice-start.3 = ((s8[4718592]{0:T(1024)(128)(4,1)}), s8[524288]{0:T(1024)(128)(4,1)S(1)}, s32[]{:S(2)}) async-start(s8[4718592]{0:T(1024)(128)(4,1)} %bitcast.503), calls=%async_computation.7 | async-start | bytes 1048576
  200.7 3.8 %copy-start.13 = (f32[768,512]{1,0:T(8,128)S(1)}, f32[768,512]{1,0:T(8,128)}, u32[]{:S(2)}) copy-start(f32[768,512]{1,0:T(8,128)} %copy-done.12) | copy-start | bytes 4718596
  200.7 3.8 %copy-start.34 = (f32[768,512]{1,0:T(8,128)S(1)}, f32[768,512]{1,0:T(8,128)}, u32[]{:S(2)}) copy-start(f32[768,512]{1,0:T(8,128)} %get-tuple-element.223) | copy-start | bytes 4718596
  204.6 9.5 %slice-start = ((s8[4718592]{0:T(1024)(128)(4,1)}), s8[524288]{0:T(1024)(128)(4,1)S(1)}, s32[]{:S(2)}) async-start(s8[4718592]{0:T(1024)(128)(4,1)} %bitcast.501), calls=%async_computation.4 | async-start | bytes 1048576
  206.4 7.8 %copy-start.25 = (f32[768,512]{1,0:T(8,128)}, f32[768,512]{1,0:T(8,128)S(1)}, u32[]{:S(2)}) copy-start(f32[768,512]{1,0:T(8,128)S(1)} %get-tuple-element.160) | copy-start | bytes 4718596
  208.4 5.7 %slice-start.1 = ((s8[4718592]{0:T(1024)(128)(4,1)}), s8[4194304]{0:T(1024)(128)(4,1)S(1)}, s32[]{:S(2)}) async-start(s8[4718592]{0:T(1024)(128)(4,1)} %bitcast.501), calls=%async_computation.5 | async-start | bytes 8388608
  215.9 3.7 %copy-start.20 = (bf16[4,128,768]{1,2,0:T(8,128)(2,1)S(1)}, bf16[4,128,768]{1,2,0:T(8,128)(2,1)}, u32[]{:S(2)}) copy-start(bf16[4,128,768]{1,2,0:T(8,128)(2,1)} %get-tuple-element.184) | copy-start | bytes 2359300
  312.5 9.1 %copy-start.76 = (f32[8,128]{1,0:T(8,128)}, f32[8,128]{1,0:T(8,128)S(1)}, u32[]{:S(2)}) copy-start(f32[8,128]{1,0:T(8,128)S(1)} %slice_multiply_fusion.4) | copy-start | bytes 12292
  314.4 12.1 %copy-start.14 = (f32[3072,128]{1,0:T(8,128)}, f32[3072,128]{1,0:T(8,128)S(1)}, u32[]{:S(2)}) copy-start(f32[3072,128]{1,0:T(8,128)S(1)} %slice_multiply_fusion) | copy-start | bytes 4718596
  314.5 4.8 %copy-start.65 = (f32[768]{0:T(1024)S(1)}, f32[768]{0:T(1024)}, u32[]{:S(2)}) copy-start(f32[768]{0:T(1024)} %copy-done.64) | copy-start | bytes 9220
  317.0 4.6 %copy-start.52 = (f32[2,4,128]{2,1,0:T(4,128)S(1)}, f32[2,4,128]{2,1,0:T(4,128)}, u32[]{:S(2)}) copy-start(f32[2,4,128]{2,1,0:T(4,128)} %param.26) | copy-start | bytes 12292
  317.0 4.6 %copy-start.92 = (f32[2,4,128]{2,1,0:T(4,128)S(1)}, f32[2,4,128]{2,1,0:T(4,128)}, u32[]{:S(2)}) copy-start(f32[2,4,128]{2,1,0:T(4,128)} %param.36) | copy-start | bytes 12292
  317.0 4.6 %copy-start.93 = (f32[2,4,128]{2,1,0:T(4,128)S(1)}, f32[2,4,128]{2,1,0:T(4,128)}, u32[]{:S(2)}) copy-start(f32[2,4,128]{2,1,0:T(4,128)} %param.31) | copy-start | bytes 12292
  319.3 3.0 copy-start.26
  319.3 3.0 copy-start.27
  319.3 3.0 copy-start.40
  324.9 3.2 copy-start.33
  (64 other events, 98.5 us)
Sparse Core Ops, SparseCore 0:
  11.1 32.8 all-gather.12
  46.1 30.2 all-gather.8
  78.0 12.8 all-gather.14
  92.3 14.0 all-gather.10

commit v10 on v6

--- a/solution.py
+++ b/solution.py
@@ -48,52 +48,93 @@
     return (pole_real, pole_imag, factor_real, factor_imag)
 
 
-def recurrence_kernel(ma_ref, mb_ref, w_ref, xa_ref, xb_ref, out_ref):
-    count = xa_ref.shape[0]
-    width = w_ref.shape[1]
-    w_re = w_ref[0:1, :]
-    w_im = w_ref[1:2, :]
-
-    def advance(h_re, h_im, keep, x_ref, row):
-        h_re = h_re * keep
-        h_im = h_im * keep
-        new_re = w_re * h_re - w_im * h_im + x_ref[pl.ds(row, 1), pl.ds(0, width)]
-        new_im = w_re * h_im + w_im * h_re + x_ref[pl.ds(row, 1), pl.ds(width, width)]
-        return new_re, new_im
+def tile_scan(x_re, x_im, keep, powers, down):
+    reps = x_re.shape[1] // keep.shape[1]
+    rows = lax.broadcasted_iota(jnp.int32, keep.shape, 0)
+    b_re, b_im = x_re, x_im
+    for level, k in enumerate((1, 2, 4)):
+        shift = 8 - k if down else k
+        valid = rows <= 7 - k if down else rows >= k
+        gate = jnp.tile(jnp.where(valid, keep, 0.0), (1, reps))
+        p_re = pltpu.roll(b_re, shift, 0)
+        p_im = pltpu.roll(b_im, shift, 0)
+        w_re = powers[0][(0, 1, 3)[level] : (0, 1, 3)[level] + 1]
+        w_im = powers[1][(0, 1, 3)[level] : (0, 1, 3)[level] + 1]
+        b_re = b_re + gate * (w_re * p_re - w_im * p_im)
+        b_im = b_im + gate * (w_re * p_im + w_im * p_re)
+        keep = keep * jnp.where(valid, pltpu.roll(keep, shift, 0), 1.0)
+    return b_re, b_im, jnp.tile(keep, (1, reps))
+
+
+def blocked_scan(count, width, pow_ref, up_keep, down_keep, load_up, load_down, store_up, store_down):
+    tiles = count // 8
+    up_powers = (pow_ref[0], pow_ref[1])
+    down_powers = (pow_ref[2], pow_ref[3])
+
+    def carry_in(b_re, b_im, reach, powers, h_re, h_im):
+        q_re = powers[0] * h_re - powers[1] * h_im
+        q_im = powers[0] * h_im + powers[1] * h_re
+        return b_re + reach * q_re, b_im + reach * q_im
 
     def step(i, carry):
-        a_re, a_im, b_re, b_im = carry
-        up = i
-        down = count - 1 - i
-        a_re, a_im = advance(a_re, a_im, ma_ref[up], xa_ref, up)
-        b_re, b_im = advance(b_re, b_im, mb_ref[down], xb_ref, down)
-        out_ref[pl.ds(up, 1), pl.ds(0, width)] = a_re
-        out_ref[pl.ds(up, 1), pl.ds(width, width)] = a_im
-        out_ref[pl.ds(down, 1), pl.ds(2 * width, width)] = b_re
-        out_ref[pl.ds(down, 1), pl.ds(3 * width, width)] = b_im
-        return (a_re, a_im, b_re, b_im)
+        u_re, u_im, d_re, d_im = carry
+        tu = pl.multiple_of(i * 8, 8)
+        td = pl.multiple_of((tiles - 1 - i) * 8, 8)
+        xu_re, xu_im = load_up(tu)
+        xd_re, xd_im = load_down(td)
+        bu_re, bu_im, ru = tile_scan(xu_re, xu_im, up_keep[pl.ds(tu, 8), :], up_powers, False)
+        bd_re, bd_im, rd = tile_scan(xd_re, xd_im, down_keep[pl.ds(td, 8), :], up_powers, True)
+        hu_re, hu_im = carry_in(bu_re, bu_im, ru, up_powers, u_re, u_im)
+        hd_re, hd_im = carry_in(bd_re, bd_im, rd, down_powers, d_re, d_im)
+        store_up(tu, hu_re, hu_im)
+        store_down(td, hd_re, hd_im)
+        return (hu_re[7:8], hu_im[7:8], hd_re[0:1], hd_im[0:1])
 
     zeros = jnp.zeros((1, width), jnp.float32)
-    lax.fori_loop(0, count, step, (zeros, zeros, zeros, zeros), unroll=8)
-
-
-def recurrence(ma, mb, w, xa, xb):
-    count, double = xa.shape
+    lax.fori_loop(0, tiles, step, (zeros, zeros, zeros, zeros), unroll=2)
+
+
+def pole_powers(p_re, p_im):
+    rows_re = [p_re]
+    rows_im = [p_im]
+    for _ in range(7):
+        a, b = rows_re[-1], rows_im[-1]
+        rows_re.append(a * p_re - b * p_im)
+        rows_im.append(a * p_im + b * p_re)
+    up_re = jnp.stack(rows_re)
+    up_im = jnp.stack(rows_im)
+    return jnp.stack([up_re, up_im, up_re[::-1], up_im[::-1]])
+
+
+def recurrence_kernel(up_ref, down_ref, pow_ref, x_ref, out_ref):
+    count = x_ref.shape[0]
+    width = pow_ref.shape[2]
+
+    def load(t):
+        return x_ref[pl.ds(t, 8), pl.ds(0, width)], x_ref[pl.ds(t, 8), pl.ds(width, width)]
+
+    def store(column):
+        def put(t, h_re, h_im):
+            out_ref[pl.ds(t, 8), pl.ds(column, width)] = h_re
+            out_ref[pl.ds(t, 8), pl.ds(column + width, width)] = h_im
+
+        return put
+
+    blocked_scan(count, width, pow_ref, up_ref, down_ref, load, load, store(0), store(2 * width))
+
+
+def recurrence(up, down, powers, x):
+    count, double = x.shape
+    vmem = pl.BlockSpec(memory_space=pltpu.VMEM)
     return pl.pallas_call(
         recurrence_kernel,
         out_shape=jax.ShapeDtypeStruct((count, 2 * double), jnp.float32),
-        in_specs=[
-            pl.BlockSpec(memory_space=pltpu.SMEM),
-            pl.BlockSpec(memory_space=pltpu.SMEM),
-            pl.BlockSpec(memory_space=pltpu.VMEM),
-            pl.BlockSpec(memory_space=pltpu.VMEM),
-            pl.BlockSpec(memory_space=pltpu.VMEM),
-        ],
-        out_specs=pl.BlockSpec(memory_space=pltpu.VMEM),
+        in_specs=[vmem, vmem, vmem, vmem],
+        out_specs=vmem,
         cost_estimate=pl.CostEstimate(
             flops=20 * count * double, transcendentals=0, bytes_accessed=16 * count * double
         ),
-    )(ma, mb, w, xa, xb)
+    )(up, down, powers, x)
 
 
 MESH = pl.DeviceIdType.MESH
@@ -243,39 +284,30 @@
     return pieces
 
 
-def adjoint_kernel(ma_ref, mb_ref, coef_ref, masks_ref, g_ref, states_ref, drive_ref, dg_ref, sums_ref, lam):
+def adjoint_kernel(ma_ref, mb_ref, pow_ref, coef_ref, masks_ref, g_ref, states_ref, drive_ref, dg_ref, sums_ref, lam):
     count = g_ref.shape[0]
     width = coef_ref.shape[1]
     pad = 8
-    w_re = coef_ref[0:1, :]
-    w_im = -coef_ref[1:2, :]
     f_re = coef_ref[2:3, :]
     f_im = coef_ref[3:4, :]
     zero_rows = jnp.zeros((pad, 4 * width), jnp.float32)
     lam[0:pad, :] = zero_rows
     lam[pad + count : 2 * pad + count, :] = zero_rows
 
-    def advance(h_re, h_im, keep, column, row):
-        h_re = h_re * keep
-        h_im = h_im * keep
-        new_re = w_re * h_re - w_im * h_im + g_ref[pl.ds(row, 1), pl.ds(column, width)]
-        new_im = w_re * h_im + w_im * h_re + g_ref[pl.ds(row, 1), pl.ds(column + width, width)]
-        return new_re, new_im
-
-    def step(i, carry):
-        b_re, b_im, a_re, a_im = carry
-        up = i
-        down = count - 1 - i
-        b_re, b_im = advance(b_re, b_im, ma_ref[up], 2 * width, up)
-        a_re, a_im = advance(a_re, a_im, mb_ref[down], 0, down)
-        lam[pl.ds(pad + up, 1), pl.ds(0, width)] = b_re
-        lam[pl.ds(pad + up, 1), pl.ds(width, width)] = b_im
-        lam[pl.ds(pad + down, 1), pl.ds(2 * width, width)] = a_re
-        lam[pl.ds(pad + down, 1), pl.ds(3 * width, width)] = a_im
-        return (b_re, b_im, a_re, a_im)
-
-    zeros = jnp.zeros((1, width), jnp.float32)
-    lax.fori_loop(0, count, step, (zeros, zeros, zeros, zeros), unroll=8)
+    def load(column):
+        def get(t):
+            return g_ref[pl.ds(t, 8), pl.ds(column, width)], g_ref[pl.ds(t, 8), pl.ds(column + width, width)]
+
+        return get
+
+    def store(column):
+        def put(t, h_re, h_im):
+            lam[pl.ds(pad + t, 8), pl.ds(column, width)] = h_re
+            lam[pl.ds(pad + t, 8), pl.ds(column + width, width)] = h_im
+
+        return put
+
+    blocked_scan(count, width, pow_ref, ma_ref, mb_ref, load(2 * width), load(0), store(0), store(2 * width))
 
     rows = 16
 
@@ -320,24 +352,23 @@
         sums_ref[k : k + 1, :] = jnp.sum(value, 0, keepdims=True)
 
 
-def adjoint(ma, mb, coef, masks, states_grad, states, drive):
+def adjoint(ma, mb, powers, coef, masks, states_grad, states, drive):
     count, quad = states_grad.shape
     width = quad // 4
     vmem = pl.BlockSpec(memory_space=pltpu.VMEM)
-    smem = pl.BlockSpec(memory_space=pltpu.SMEM)
     return pl.pallas_call(
         adjoint_kernel,
         out_shape=(
             jax.ShapeDtypeStruct((count, 2 * width), jnp.bfloat16),
             jax.ShapeDtypeStruct((4, width), jnp.float32),
         ),
-        in_specs=[smem, smem, vmem, vmem, vmem, vmem, vmem],
+        in_specs=[vmem] * 8,
         out_specs=(vmem, vmem),
         scratch_shapes=[pltpu.VMEM((count + 16, 4 * width), jnp.float32)],
         cost_estimate=pl.CostEstimate(
             flops=60 * count * width, transcendentals=0, bytes_accessed=48 * count * width
         ),
-    )(ma, mb, coef, masks, states_grad, states, drive)
+    )(ma, mb, powers, coef, masks, states_grad, states, drive)
 
 
 def update(weight, gradient, velocity, average, rate, decay):
@@ -402,6 +433,12 @@
     before_prev = jnp.concatenate([carry_prev[1:], zero])
     mask_columns = jnp.stack([alive, carry_prev, carry_next, jnp.zeros_like(alive)], 1)
 
+    def lanes(mask):
+        return jnp.broadcast_to(mask[:, None], (count, 128))
+
+    keep_prev, keep_next = lanes(carry_prev), lanes(carry_next)
+    keep_after_next, keep_before_prev = lanes(after_next), lanes(before_prev)
+
     in_all = gather_feat(input_matrix.astype(jnp.bfloat16), 1)
     out_all = gather_feat(output_matrix.astype(jnp.bfloat16), 2)
     gate_all = gather_feat(gate_matrix.astype(jnp.bfloat16), 2)
@@ -431,8 +468,7 @@
             ],
             1,
         )
-        poles = jnp.stack([pole_re, pole_im])
-        states = recurrence(carry_prev, carry_next, poles, source, source)
+        states = recurrence(keep_prev, keep_next, pole_powers(pole_re, pole_im), source)
         states_low = states.astype(jnp.bfloat16)
         mixed = (
             jnp.dot(states_low, out_low, preferred_element_type=jnp.float32)
@@ -466,7 +502,16 @@
         out_grad = contract_rows(states_low, mine(mixed_low))
         states_grad = contract_cols(mixed_low, out_low)
         coef = jnp.stack([pole_re, pole_im, factor_re, factor_im])
-        drive_low, sums = adjoint(after_next, before_prev, coef, mask_columns, states_grad, states, drive)
+        drive_low, sums = adjoint(
+            keep_after_next,
+            keep_before_prev,
+            pole_powers(pole_re, -pole_im),
+            coef,
+            mask_columns,
+            states_grad,
+            states,
+            drive,
+        )
         gp_re, gp_im, gf_re, gf_im = sums[0], sums[1], sums[2], sums[3]
         row_grad = jax.vjp(coefficients, state_row)[1]((gp_re, gp_im, gf_re, gf_im))[0]
         in_grad = contract_rows(mine(normed_low), drive_low)

time: 283 us -> 279 us (0.986)
  Pallas kernels: 115 us -> 110 us
  local copies, waits for them, and re-layouts: 17.3 us -> 21.3 us
  waiting for transfers between devices: 15.5 us -> 12.3 us
    broadcast_in_dim x0 -> x4, local copies, waits for them, and re-layouts: none -> 3.65 us  [lanes(): return jnp.broadcast_to(mask[:, None], (count, 128))]
    all_gather x3, waiting for transfers between devices: 15.5 us -> 12.3 us  [gather_feat(): return lax.all_gather(value, 'feat', axis=axis, tiled=True)]
    pallas_call x2, Pallas kernels: 34.1 us -> 31.2 us  [adjoint(): pl.pallas_call(adjoint_kernel, out_shape=(jax.ShapeDtypeStruct((count, 2...]
    rev x0 -> x8, local copies, waits for them, and re-layouts: none -> 2.9 us  [pole_powers(): return jnp.stack([up_re, up_im, up_re[::-1], up_im[::-1]])]
    unnamed x210 -> x236, local copies, waits for them, and re-layouts: 10.9 us -> 11.4 us
  transfers between devices with their start and end apart: 3 -> 3, of which waited for: 2 -> 2; matrix products, arithmetic and copies ran while one was open for 8% -> 9% of each run, Pallas kernels for 4% -> 3%
where the time goes in v10:
time: 279 us
  Pallas kernels  110 us (39%)
  matrix products  55.9 us (20%)
  other arithmetic  34.8 us (12%)
  blocking collectives  28.7 us (10%)
  local copies, waits for them, and re-layouts  21.3 us (8%)
  between operations  15.3 us (5%)
  waiting for transfers between devices  12.3 us (4%)
    pallas_call x1, Pallas kernels, ring_sum(): pl.pallas_call(lambda *refs: ring_sum_kernel(n, *refs), out_shape=jax.Sha...  61.2 us
    pallas_call x2, Pallas kernels, adjoint(): pl.pallas_call(adjoint_kernel, out_shape=(jax.ShapeDtypeStruct((count, 2...  31.2 us
    all_gather x3, blocking collectives, gather_feat(): return lax.all_gather(value, 'feat', axis=axis, tiled=True)  28.7 us
    pallas_call x2, Pallas kernels, recurrence(): pl.pallas_call(recurrence_kernel, out_shape=jax.ShapeDtypeStruct((count,...  17.7 us
    dot_general x4, matrix products, contract_cols(): lax.dot_general(left, right, (((1,), (1,)), ((), ())), preferred_element_...  17.2 us
    dot_general x2, matrix products, body(): jnp.dot(states_low, out_low, preferred_element_type=jnp.float32)  15.9 us
    all_gather x3, waiting for transfers between devices, gather_feat(): return lax.all_gather(value, 'feat', axis=axis, tiled=True)  12.3 us
    unnamed x236, local copies, waits for them, and re-layouts  11.4 us
  transfers between devices with their start and end apart: 3, of which 2 were waited for; matrix products, arithmetic and copies ran while one was open for 9% of the time, Pallas kernels for 3%

profile of v10, /device:TPU:0, one launch (start us, length us, event | category | flops | bytes accessed | tf_op | source)
XLA Modules:
  0.0 278.6 jit_solution(16957171076097621089)
XLA Ops:
  7.2 2.0 convert_element_type.108
  9.4 1.0 convert_element_type.111
  12.3 6.1 %all_gather.19 = f32[2,4,512]{2,1,0:T(4,128)S(1)} all-gather(f32[2,4,128]{2,1,0:T(4,128)S(1)} %copy-done.67), channel_id=1, replica_groups=mesh['seq'=8,'feat'=4] {'feat'}, dimensions={2}, use_global_device_ids=true | all-gather | bytes 20480 | tf_op jit(solution)/shard_map/all_gather | solution.py:396
  20.2 1.2 rev.30
  22.0 0.9 copy.86.masks_ref
  23.0 13.2 %all_gather.18 = bf16[768,512]{1,0:T(8,128)(2,1)S(1)} all-gather(bf16[768,128]{1,0:T(8,128)(2,1)S(1)} %copy-done.33), channel_id=1, replica_groups=mesh['seq'=8,'feat'=4] {'feat'}, dimensions={1}, use_global_device_ids=true | all-gather | bytes 983040 | tf_op jit(solution)/shard_map/all_gather | solution.py:396
  36.8 9.4 %all_gather.23 = bf16[768,512]{1,0:T(8,128)(2,1)} all-gather(bf16[768,128]{1,0:T(8,128)(2,1)S(1)} %copy-done.34), channel_id=1, replica_groups=mesh['seq'=8,'feat'=4] {'feat'}, dimensions={1}, use_global_device_ids=true | all-gather | bytes 983040 | tf_op jit(solution)/shard_map/all_gather | solution.py:396
  46.8 1.2 fusion.17
  50.1 2.2 fusion.23.drive_ref
  52.6 1.0 copy-done
  53.6 1.6 pad_maximum_fusion.x_ref
  55.2 0.9 broadcast_in_dim.8.up_ref
  56.1 0.9 broadcast_in_dim.9.down_ref
  57.0 8.9 %shard_map.354.states_ref = f32[768,1536]{1,0:T(8,128)} custom-call(f32[768,128]{1,0:T(8,128)} %broadcast_in_dim.8.up_ref, f32[768,128]{1,0:T(8,128)} %broadcast_in_dim.9.down_ref, f32[4,8,384]{2,1,0:T(8,128)} %pad_maximum_fusion.5.pow_ref, f32[768,768]{1,0:T(8,128)} %pad_maximum_fusion.x_ref), custom_call_target="tpu_custom_call" | custom-call | flops 11796480 | bytes 9437184 | tf_op jit(solution)/shard_map/pallas_call | solution.py:129
  65.9 1.5 all-gather.6.cloned.1.call-done
  67.5 8.2 %multiply_multiply_fusion.11 = (f32[768,512]{1,0:T(8,128)S(1)}, f32[768,512]{1,0:T(8,128)}) fusion(f32[512]{0:T(512)S(1)} %bitcast.485, f32[512]{0:T(512)S(1)} %bitcast.488, f32[768]{0:T(1024)S(1)} %add_rsqrt_fusion.1, f32[768]{0:T(1024)S(1)} %broadcast_multiply_fusion.6, bf16[768,512]{1,0:T(8,128)(2,1)S(1)} %copy-done.5, f32[512]{0:T(512)S(1)} %bitcast.494, ...), kind=kOutput, calls=%fused_computation.74 | convolution fusion | flops 1237057536 | bytes 10235904 | tf_op jit(solution)/shard_map/dot_general | solution.py:474
  75.7 10.7 %all-gather.8.cloned.1.call-done = bf16[2,512,512]{2,1,0:T(8,128)(2,1)} async-done(((bf16[2,512,128]{2,1,0:T(8,128)(2,1)}), bf16[2,512,512]{2,1,0:T(8,128)(2,1)}) %all-gather.8.cloned.1.call-update) | async-done | bytes 1048592 | tf_op jit(solution)/shard_map/all_gather | solution.py:396
  86.5 3.0 %fusion.105 = (f32[768]{0:T(1024)S(1)}, f32[768,512]{1,0:T(8,128)S(1)}, f32[768,512]{1,0:T(8,128)}) fusion(f32[768,512]{1,0:T(8,128)S(1)} %get-tuple-element.295, bf16[768,512]{1,0:T(8,128)(2,1)S(1)} %copy-done.5, f32[512]{0:T(512)S(1)} %bitcast.499, bf16[2,512,512]{2,1,0:T(8,128)(2,1)} %all-gather.8.cloned.1.call-done), kind=kOutput, calls=%fused_computation.355 | convolution fusion | flops 406191360 | bytes 7607296 | tf_op jit(solution)/shard_map/dot_general | solution.py:479
  92.7 1.1 copy-done.1
  93.8 1.6 pad_maximum_fusion.1.x_ref
  95.4 8.8 %shard_map.355.states_ref = f32[768,1536]{1,0:T(8,128)} custom-call(f32[768,128]{1,0:T(8,128)} %broadcast_in_dim.8.up_ref, f32[768,128]{1,0:T(8,128)} %broadcast_in_dim.9.down_ref, f32[4,8,384]{2,1,0:T(8,128)} %pad_maximum_fusion.6.pow_ref, f32[768,768]{1,0:T(8,128)} %pad_maximum_fusion.1.x_ref), custom_call_target="tpu_custom_call" | custom-call | flops 11796480 | bytes 9437184 | tf_op jit(solution)/shard_map/pallas_call | solution.py:129
  104.3 7.6 %multiply_multiply_fusion.10 = (f32[768,512]{1,0:T(8,128)S(1)}, f32[768,512]{1,0:T(8,128)S(1)}, f32[768,512]{1,0:T(8,128)S(1)}) fusion(f32[512]{0:T(512)S(1)} %bitcast.491, f32[512]{0:T(512)S(1)} %bitcast.478, f32[768]{0:T(1024)S(1)} %add_rsqrt_fusion, f32[768,512]{1,0:T(8,128)S(1)} %copy-done.3, f32[768]{0:T(1024)S(1)} %broadcast_multiply_fusion.5, ...), kind=kOutput, calls=%fused_computation.72 | convolution fusion | flops 1236664320 | bytes 12595200 | tf_op jit(solution)/shard_map/dot_general | solution.py:474
  112.0 1.6 convert_reduce_fusion.1
  113.6 1.1 convolution_bitcast_fusion.4
  115.6 2.3 fusion.108
  118.0 1.7 convolution_bitcast_fusion
  120.0 3.6 %fusion.16.g_ref = f32[768,1536]{1,0:T(8,128)} fusion(bf16[768,512]{1,0:T(8,128)(2,1)S(1)} %get-tuple-element.300, bf16[2,1536,512]{2,1,0:T(8,128)(2,1)S(1)} %copy-done.107), kind=kOutput, calls=%fused_computation.76 | convolution fusion | flops 1207959552 | bytes 7077888 | tf_op jit(solution)/shard_map/dot_general | solution.py:390
  123.7 0.9 broadcast_in_dim.10.ma_ref
  124.6 0.9 broadcast_in_dim.11.mb_ref
  125.5 15.6 %shard_map.356 = (bf16[768,768]{1,0:T(8,128)(2,1)}, f32[4,384]{1,0:T(4,128)}) custom-call(f32[768,128]{1,0:T(8,128)} %broadcast_in_dim.10.ma_ref, f32[768,128]{1,0:T(8,128)} %broadcast_in_dim.11.mb_ref, f32[4,8,384]{2,1,0:T(8,128)} %pad_maximum_fusion.7.pow_ref, f32[4,384]{1,0:T(4,128)} %pad_maximum_fusion.10.coef_ref, f32[768,4]{1,0:T(8,128)} %copy.86.masks_ref, ...), custom_call_target="tpu_custom_call" | custom-call | flops 17694720 | bytes 14155776 | tf_op jit(solution)/shard_map/pallas_call | solution.py:359
  141.1 1.8 convolution_bitcast_fusion.2
  143.1 3.9 %multiply_reduce_fusion.1 = (f32[512]{0:T(512)}, f32[768]{0:T(1024)S(1)}, f32[512]{0:T(512)}, f32[768]{0:T(1024)S(1)}, f32[512]{0:T(512)}, /*index=5*/f32[768,512]{1,0:T(8,128)S(1)}) fusion(f32[768]{0:T(1024)S(1)} %copy-done.58, f32[768,512]{1,0:T(8,128)S(1)} %copy-done.3, f32[768]{0:T(1024)S(1)} %copy-done.50, f32[512]{0:T(512)S(1)} %bitcast.479, ...), kind=kOutput, calls=%fused_computation.25 | convolution fusion | flops 609874944 | bytes 6711296 | tf_op jit(solution)/shard_map/dot_general | solution.py:518
  147.0 2.7 convert_reduce_fusion.2
  149.8 1.1 convolution_bitcast_fusion.5
  152.5 1.2 rev.31
  153.7 7.6 %fusion.109 = (bf16[768,512]{1,0:T(8,128)(2,1)S(1)}, f32[768,512]{1,0:T(8,128)}) fusion(f32[768,512]{1,0:T(8,128)} %get-tuple-element.296, bf16[768,512]{1,0:T(8,128)(2,1)} %copy-done.25, bf16[2,512,512]{2,1,0:T(8,128)(2,1)} %all-gather.8.cloned.1.call-done, f32[768,512]{1,0:T(8,128)S(1)} %copy-done.17, f32[768,512]{1,0:T(8,128)} %get-tuple-element.297), kind=kOutput, calls=%fused_computation.359 | convolution fusion | flops 431751168 | bytes 8388608 | tf_op jit(solution)/shard_map/dot_general | solution.py:390
  163.5 3.6 %fusion.15.g_ref = f32[768,1536]{1,0:T(8,128)} fusion(bf16[768,512]{1,0:T(8,128)(2,1)S(1)} %get-tuple-element.303, bf16[2,1536,512]{2,1,0:T(8,128)(2,1)S(1)} %copy-done.108), kind=kOutput, calls=%fused_computation.75 | convolution fusion | flops 1207959552 | bytes 7077888 | tf_op jit(solution)/shard_map/dot_general | solution.py:390
  167.1 15.5 %shard_map.357 = (bf16[768,768]{1,0:T(8,128)(2,1)}, f32[4,384]{1,0:T(4,128)}) custom-call(f32[768,128]{1,0:T(8,128)} %broadcast_in_dim.10.ma_ref, f32[768,128]{1,0:T(8,128)} %broadcast_in_dim.11.mb_ref, f32[4,8,384]{2,1,0:T(8,128)} %pad_maximum_fusion.8.pow_ref, f32[4,384]{1,0:T(4,128)} %pad_maximum_fusion.11.coef_ref, f32[768,4]{1,0:T(8,128)} %copy.86.masks_ref, ...), custom_call_target="tpu_custom_call" | custom-call | flops 17694720 | bytes 14155776 | tf_op jit(solution)/shard_map/pallas_call | solution.py:359
  182.7 1.7 convolution_bitcast_fusion.3
  188.4 2.9 %fusion.88 = (f32[512]{0:T(512)S(1)}, f32[512]{0:T(512)S(1)}, f32[512]{0:T(512)S(1)}, f32[768]{0:T(1024)S(1)}, f32[768]{0:T(1024)S(1)}, /*index=5*/f32[768,512]{1,0:T(8,128)}, f32[768,512]{1,0:T(8,128)}) fusion(f32[768]{0:T(1024)S(1)} %copy-done.54, f32[768]{0:T(1024)S(1)} %copy-done.56, bf16[768,512]{1,0:T(8,128)(2,1)S(1)} %copy-done.5, ...), kind=kOutput, calls=%fused_computation.349 | convolution fusion | flops 610268160 | bytes 7497728 | tf_op jit(solution)/shard_map/dot_general | solution.py:518
  191.6 1.8 pad_bitcast_fusion.refs_0_
  193.4 61.2 %shard_map.358 = bf16[5888,128]{1,0:T(8,128)(2,1)} custom-call(f32[5888,128]{1,0:T(8,128)} %pad_bitcast_fusion.refs_0_), custom_call_target="tpu_custom_call" | custom-call | tf_op jit(solution)/shard_map/pallas_call | solution.py:252
  254.7 1.6 convert_element_type.130
  260.8 3.0 %add_multiply_fusion.4 = (f32[2,512,128]{2,1,0:T(8,128)}, f32[2,512,128]{2,1,0:T(8,128)}, f32[2,512,128]{2,1,0:T(8,128)}) fusion(f32[2,512,128]{2,1,0:T(8,128)} %param.35, f32[2,512,128]{2,1,0:T(8,128)} %param.25, f32[2,512,128]{2,1,0:T(8,128)} %bitcast.457, f32[2,512,128]{2,1,0:T(8,128)} %param.30), kind=kLoop, calls=%fused_computation.107 | loop fusion | flops 1310720 | bytes 3670016 | tf_op jit(solution)/shard_map/add | solution.py:379
  263.8 1.7 add_multiply_fusion.3
  265.6 0.9 copy-done.19
  267.0 2.7 add_multiply_fusion
  269.7 2.4 dynamic-slice_add_fusion
  (324 shorter events, 24.7 us)
Async XLA Ops:
  7.2 42.9 %all-gather.4.cloned.1.call-start = ((), (), s32[]{:S(2)}) async-start(), calls=%async_computation | async-start | bytes 1966080 | tf_op jit(solution)/shard_map/all_gather | solution.py:396
  9.4 2.9 %copy-start.67 = (f32[2,4,128]{2,1,0:T(4,128)S(1)}, f32[2,4,128]{2,1,0:T(4,128)}, u32[]{:S(2)}) copy-start(f32[2,4,128]{2,1,0:T(4,128)} %param.26) | copy-start | bytes 12292
  9.4 58.1 %all-gather.6.cloned.1.call-start = ((), (), s32[]{:S(2)}) async-start(), calls=%async_computation.1 | async-start | bytes 3932160 | tf_op jit(solution)/shard_map/all_gather | solution.py:396
  10.4 12.5 %copy-start.33 = (bf16[768,128]{1,0:T(8,128)(2,1)S(1)}, bf16[768,128]{1,0:T(8,128)(2,1)}, u32[]{:S(2)}) copy-start(bf16[768,128]{1,0:T(8,128)(2,1)} %param.19) | copy-start | bytes 589828
  10.4 76.0 %all-gather.8.cloned.1.call-start = ((), (), s32[]{:S(2)}) async-start(), calls=%async_computation.2 | async-start | bytes 1310720 | tf_op jit(solution)/shard_map/all_gather | solution.py:396
  12.2 9.5 %copy-start.59 = (f32[1,384]{1,0:T(1,128)}, f32[1,384]{1,0:T(1,128)S(1)}, u32[]{:S(2)}) copy-start(f32[1,384]{1,0:T(1,128)S(1)} %get-tuple-element.183) | copy-start | bytes 4612
  12.2 34.0 %copy-start.35 = (f32[1,384]{1,0:T(1,128)}, f32[1,384]{1,0:T(1,128)S(1)}, u32[]{:S(2)}) copy-start(f32[1,384]{1,0:T(1,128)S(1)} %get-tuple-element.184) | copy-start | bytes 4612
  12.2 34.0 %copy-start.43 = (f32[1,384]{1,0:T(1,128)}, f32[1,384]{1,0:T(1,128)S(1)}, u32[]{:S(2)}) copy-start(f32[1,384]{1,0:T(1,128)S(1)} %get-tuple-element.185) | copy-start | bytes 4612
  18.4 49.1 %copy-start.75 = (f32[1,1,512]{2,1,0:T(1,128)}, f32[1,1,512]{2,1,0:T(1,128)S(1)}, u32[]{:S(2)}) copy-start(f32[1,1,512]{2,1,0:T(1,128)S(1)} %get-tuple-element.247) | copy-start | bytes 6148
  18.4 49.1 %copy-start.77 = (f32[1,1,512]{2,1,0:T(1,128)}, f32[1,1,512]{2,1,0:T(1,128)S(1)}, u32[]{:S(2)}) copy-start(f32[1,1,512]{2,1,0:T(1,128)S(1)} %get-tuple-element.248) | copy-start | bytes 6148
  18.4 49.0 %copy-start.97 = (f32[1,1,512]{2,1,0:T(1,128)}, f32[1,1,512]{2,1,0:T(1,128)S(1)}, u32[]{:S(2)}) copy-start(f32[1,1,512]{2,1,0:T(1,128)S(1)} %get-tuple-element.246) | copy-start | bytes 6148
  18.4 85.8 %copy-start.65 = (f32[1,1,512]{2,1,0:T(1,128)}, f32[1,1,512]{2,1,0:T(1,128)S(1)}, u32[]{:S(2)}) copy-start(f32[1,1,512]{2,1,0:T(1,128)S(1)} %get-tuple-element.244) | copy-start | bytes 6148
  18.4 85.8 %copy-start.79 = (f32[1,1,512]{2,1,0:T(1,128)}, f32[1,1,512]{2,1,0:T(1,128)S(1)}, u32[]{:S(2)}) copy-start(f32[1,1,512]{2,1,0:T(1,128)S(1)} %get-tuple-element.243) | copy-start | bytes 6148
  18.4 85.8 %copy-start.99 = (f32[1,1,512]{2,1,0:T(1,128)}, f32[1,1,512]{2,1,0:T(1,128)S(1)}, u32[]{:S(2)}) copy-start(f32[1,1,512]{2,1,0:T(1,128)S(1)} %get-tuple-element.241) | copy-start | bytes 6148
  19.2 2.8 %copy-start.37 = (f32[1,384]{1,0:T(1,128)}, f32[1,384]{1,0:T(1,128)S(1)}, u32[]{:S(2)}) copy-start(f32[1,384]{1,0:T(1,128)S(1)} %get-tuple-element.255) | copy-start | bytes 4612
  21.6 15.2 %copy-start.34 = (bf16[768,128]{1,0:T(8,128)(2,1)S(1)}, bf16[768,128]{1,0:T(8,128)(2,1)}, u32[]{:S(2)}) copy-start(bf16[768,128]{1,0:T(8,128)(2,1)} %param.20) | copy-start | bytes 589828
  36.2 11.9 %copy-start.4 = (bf16[768,512]{1,0:T(8,128)(2,1)}, bf16[768,512]{1,0:T(8,128)(2,1)S(1)}, u32[]{:S(2)}) copy-start(bf16[768,512]{1,0:T(8,128)(2,1)S(1)} %all_gather.18) | copy-start | bytes 2359300
  36.4 31.1 %copy-start.55 = (f32[768]{0:T(1024)}, f32[768]{0:T(1024)S(1)}, u32[]{:S(2)}) copy-start(f32[768]{0:T(1024)S(1)} %broadcast_multiply_fusion.6) | copy-start | bytes 9220
  36.8 30.7 %copy-start.53 = (f32[768]{0:T(1024)}, f32[768]{0:T(1024)S(1)}, u32[]{:S(2)}) copy-start(f32[768]{0:T(1024)S(1)} %add_rsqrt_fusion.1) | copy-start | bytes 9220
  57.0 10.5 %copy-start.5 = (bf16[768,512]{1,0:T(8,128)(2,1)S(1)}, bf16[768,512]{1,0:T(8,128)(2,1)}, u32[]{:S(2)}) copy-start(bf16[768,512]{1,0:T(8,128)(2,1)} %copy-done.4) | copy-start | bytes 2359300
  75.7 13.8 %copy-start.10 = (f32[768,512]{1,0:T(8,128)}, f32[768,512]{1,0:T(8,128)S(1)}, u32[]{:S(2)}) copy-start(f32[768,512]{1,0:T(8,128)S(1)} %get-tuple-element.295) | copy-start | bytes 4718596
  89.5 14.7 %copy-start.49 = (f32[768]{0:T(1024)}, f32[768]{0:T(1024)S(1)}, u32[]{:S(2)}) copy-start(f32[768]{0:T(1024)S(1)} %broadcast_multiply_fusion.5) | copy-start | bytes 9220
  89.9 14.4 %copy-start.57 = (f32[768]{0:T(1024)}, f32[768]{0:T(1024)S(1)}, u32[]{:S(2)}) copy-start(f32[768]{0:T(1024)S(1)} %add_rsqrt_fusion) | copy-start | bytes 9220
  95.4 8.9 %copy-start.3 = (f32[768,512]{1,0:T(8,128)S(1)}, f32[768,512]{1,0:T(8,128)}, u32[]{:S(2)}) copy-start(f32[768,512]{1,0:T(8,128)} %copy-done.2) | copy-start | bytes 4718596
  104.3 7.7 %copy-start.6 = (bf16[768,512]{1,0:T(8,128)(2,1)S(1)}, bf16[768,512]{1,0:T(8,128)(2,1)}, u32[]{:S(2)}) copy-start(bf16[768,512]{1,0:T(8,128)(2,1)} %all_gather.23) | copy-start | bytes 2359300
  104.3 7.7 %copy-start.32 = (bf16[2,512,512]{2,1,0:T(8,128)(2,1)S(1)}, bf16[2,512,512]{2,1,0:T(8,128)(2,1)}, u32[]{:S(2)}) copy-start(bf16[2,512,512]{2,1,0:T(8,128)(2,1)} %all-gather.8.cloned.1.call-done) | copy-start | bytes 3145732
  114.7 3.2 %slice-start.2 = ((s8[4718592]{0:T(1024)(128)(4,1)}), s8[4194304]{0:T(1024)(128)(4,1)S(1)}, s32[]{:S(2)}) async-start(s8[4718592]{0:T(1024)(128)(4,1)} %bitcast.452), calls=%async_computation.5 | async-start | bytes 8388608
  143.0 3.9 %copy-start.7 = (bf16[768,512]{1,0:T(8,128)(2,1)S(1)}, bf16[768,512]{1,0:T(8,128)(2,1)}, u32[]{:S(2)}) copy-start(bf16[768,512]{1,0:T(8,128)(2,1)} %all_gather.23) | copy-start | bytes 2359300
  143.1 3.9 %copy-start.11 = (f32[768,512]{1,0:T(8,128)S(1)}, f32[768,512]{1,0:T(8,128)}, u32[]{:S(2)}) copy-start(f32[768,512]{1,0:T(8,128)} %copy-done.10) | copy-start | bytes 4718596
  143.1 3.9 %copy-start.24 = (f32[768,512]{1,0:T(8,128)S(1)}, f32[768,512]{1,0:T(8,128)}, u32[]{:S(2)}) copy-start(f32[768,512]{1,0:T(8,128)} %get-tuple-element.297) | copy-start | bytes 4718596
  147.0 14.3 %slice-start = ((s8[4718592]{0:T(1024)(128)(4,1)}), s8[524288]{0:T(1024)(128)(4,1)S(1)}, s32[]{:S(2)}) async-start(s8[4718592]{0:T(1024)(128)(4,1)} %bitcast.450), calls=%async_computation.3 | async-start | bytes 1048576
  149.7 2.7 copy-start.85
  149.8 2.7 copy-start.86
  149.8 3.9 %copy-start.17 = (f32[768,512]{1,0:T(8,128)S(1)}, f32[768,512]{1,0:T(8,128)}, u32[]{:S(2)}) copy-start(f32[768,512]{1,0:T(8,128)} %get-tuple-element.159) | copy-start | bytes 4718596
  152.5 8.9 %copy-start.41 = (f32[8,384]{1,0:T(8,128)}, f32[8,384]{1,0:T(8,128)S(1)}, u32[]{:S(2)}) copy-start(f32[8,384]{1,0:T(8,128)S(1)} %stack.268) | copy-start | bytes 36868
  153.7 7.6 %slice-start.1 = ((s8[4718592]{0:T(1024)(128)(4,1)}), s8[4194304]{0:T(1024)(128)(4,1)S(1)}, s32[]{:S(2)}) async-start(s8[4718592]{0:T(1024)(128)(4,1)} %bitcast.450), calls=%async_computation.4 | async-start | bytes 8388608
  188.4 2.9 %copy-start.81 = (f32[512]{0:T(512)S(1)}, f32[512]{0:T(512)}, u32[]{:S(2)}) copy-start(f32[512]{0:T(512)} %get-tuple-element.157) | copy-start | bytes 6148
  256.3 3.8 %copy-start.69 = (f32[8,128]{1,0:T(8,128)}, f32[8,128]{1,0:T(8,128)S(1)}, u32[]{:S(2)}) copy-start(f32[8,128]{1,0:T(8,128)S(1)} %slice_multiply_fusion.4) | copy-start | bytes 12292
  257.4 8.1 %copy-start.12 = (f32[3072,128]{1,0:T(8,128)}, f32[3072,128]{1,0:T(8,128)S(1)}, u32[]{:S(2)}) copy-start(f32[3072,128]{1,0:T(8,128)S(1)} %slice_multiply_fusion) | copy-start | bytes 4718596
  257.4 2.7 copy-start.68
  257.4 2.7 copy-start.95
  257.4 2.7 copy-start.96
  260.0 3.7 %copy-start.15 = (f32[2,128,768]{2,1,0:T(8,128)}, f32[2,128,768]{2,1,0:T(8,128)S(1)}, u32[]{:S(2)}) copy-start(f32[2,128,768]{2,1,0:T(8,128)S(1)} %mul.6070) | copy-start | bytes 2359300
  260.8 3.0 %copy-start.14 = (f32[2,128,768]{2,1,0:T(8,128)S(1)}, f32[2,128,768]{2,1,0:T(8,128)}, u32[]{:S(2)}) copy-start(f32[2,128,768]{2,1,0:T(8,128)} %param.23) | copy-start | bytes 2359300
  260.8 3.0 %copy-start.29 = (f32[2,128,768]{2,1,0:T(8,128)S(1)}, f32[2,128,768]{2,1,0:T(8,128)}, u32[]{:S(2)}) copy-start(f32[2,128,768]{2,1,0:T(8,128)} %param.33) | copy-start | bytes 2359300
  260.8 3.0 %copy-start.30 = (f32[2,128,768]{2,1,0:T(8,128)S(1)}, f32[2,128,768]{2,1,0:T(8,128)}, u32[]{:S(2)}) copy-start(f32[2,128,768]{2,1,0:T(8,128)} %param.28) | copy-start | bytes 2359300
  263.8 2.7 copy-start.19
  263.8 3.2 %copy-start.20 = (f32[2,1536,128]{2,1,0:T(8,128)S(1)}, f32[2,1536,128]{2,1,0:T(8,128)}, u32[]{:S(2)}) copy-start(f32[2,1536,128]{2,1,0:T(8,128)} %param.29) | copy-start | bytes 4718596
  (69 other events, 99.2 us)
Sparse Core Ops, SparseCore 0:
  10.2 26.4 all-gather.3
  38.8 28.5 all-gather.5
  69.6 16.8 all-gather.7

commit v11 on v10

--- a/solution.py
+++ b/solution.py
@@ -138,6 +138,73 @@
 
 
 MESH = pl.DeviceIdType.MESH
+
+
+def recurrence_gather_kernel(parts, up_ref, down_ref, pow_ref, x_ref, c_ref, out_ref, c_all, local, sends, recvs):
+    count = x_ref.shape[0]
+    width = pow_ref.shape[2]
+    lanes = c_ref.shape[1]
+    me = lax.axis_index("feat")
+    mine = pl.ds(pl.multiple_of(me * lanes, lanes), lanes)
+
+    barrier = pltpu.get_barrier_semaphore()
+    for j in range(1, parts):
+        pl.semaphore_signal(barrier, 1, device_id={"feat": (me + j) % parts}, device_id_type=MESH)
+    pl.semaphore_wait(barrier, parts - 1)
+
+    own = pltpu.make_async_copy(c_ref, c_all.at[:, mine], local)
+    own.start()
+    copies = []
+    for j in range(1, parts):
+        copy = pltpu.make_async_remote_copy(
+            src_ref=c_ref,
+            dst_ref=c_all.at[:, mine],
+            send_sem=sends.at[j - 1],
+            recv_sem=recvs.at[j - 1],
+            device_id={"feat": (me + j) % parts},
+            device_id_type=MESH,
+        )
+        copy.start()
+        copies.append(copy)
+
+    def load(t):
+        return x_ref[pl.ds(t, 8), pl.ds(0, width)], x_ref[pl.ds(t, 8), pl.ds(width, width)]
+
+    def store(column):
+        def put(t, h_re, h_im):
+            out_ref[pl.ds(t, 8), pl.ds(column, width)] = h_re
+            out_ref[pl.ds(t, 8), pl.ds(column + width, width)] = h_im
+
+        return put
+
+    blocked_scan(count, width, pow_ref, up_ref, down_ref, load, load, store(0), store(2 * width))
+    own.wait()
+    for copy in copies:
+        copy.wait_send()
+        copy.wait_recv()
+
+
+def recurrence_gather(up, down, powers, x, c, parts):
+    count, double = x.shape
+    vmem = pl.BlockSpec(memory_space=pltpu.VMEM)
+    return pl.pallas_call(
+        lambda *refs: recurrence_gather_kernel(parts, *refs),
+        out_shape=(
+            jax.ShapeDtypeStruct((count, 2 * double), jnp.float32),
+            jax.ShapeDtypeStruct((c.shape[0], c.shape[1] * parts), c.dtype),
+        ),
+        in_specs=[vmem] * 5,
+        out_specs=(vmem, vmem),
+        scratch_shapes=[
+            pltpu.SemaphoreType.DMA(()),
+            pltpu.SemaphoreType.DMA((parts - 1,)),
+            pltpu.SemaphoreType.DMA((parts - 1,)),
+        ],
+        compiler_params=pltpu.CompilerParams(collective_id=1, has_side_effects=True),
+        cost_estimate=pl.CostEstimate(
+            flops=20 * count * double, transcendentals=0, bytes_accessed=16 * count * double
+        ),
+    )(up, down, powers, x, c)
 
 
 def ring_place(position, n):
@@ -468,7 +535,13 @@
             ],
             1,
         )
-        states = recurrence(keep_prev, keep_next, pole_powers(pole_re, pole_im), source)
+        powers = pole_powers(pole_re, pole_im)
+        if layer == layers - 1:
+            states, cotangent_all = recurrence_gather(
+                keep_prev, keep_next, powers, source, cotangent, lax.axis_size("feat")
+            )
+        else:
+            states = recurrence(keep_prev, keep_next, powers, source)
         states_low = states.astype(jnp.bfloat16)
         mixed = (
             jnp.dot(states_low, out_low, preferred_element_type=jnp.float32)
@@ -480,7 +553,7 @@
         saved.append((scale, unit, normed_low, drive, states, states_low, mixed, act, act_low, pre))
         stream = stream + act * jax.nn.sigmoid(pre)
 
-    grad = gather_feat(cotangent, 1).astype(jnp.float32) * alive[:, None]
+    grad = cotangent_all.astype(jnp.float32) * alive[:, None]
     layer_grads = [None] * layers
     for layer in reversed(range(layers)):
         scale, unit, normed_low, drive, states, states_low, mixed, act, act_low, pre = saved[layer]

time: 279 us -> 289 us (1.036)
  waiting for transfers between devices: 12.3 us -> 22.6 us
  blocking collectives: 28.7 us -> 19.4 us
  Pallas kernels: 110 us -> 116 us
    pallas_call x0 -> x1, Pallas kernels: none -> 13.8 us  [recurrence_gather(): pl.pallas_call(lambda *refs: recurrence_gather_kernel(parts, *refs), out_...]
    all_gather x3, waiting for transfers between devices: 12.3 us -> 22.5 us  [gather_feat(): return lax.all_gather(value, 'feat', axis=axis, tiled=True)]
    all_gather x3 -> x2, blocking collectives: 28.7 us -> 19.4 us  [gather_feat(): return lax.all_gather(value, 'feat', axis=axis, tiled=True)]
    pallas_call x2 -> x1, Pallas kernels: 17.7 us -> 8.81 us  [recurrence(): pl.pallas_call(recurrence_kernel, out_shape=jax.ShapeDtypeStruct((count,...]
    unnamed x236 -> x208, local copies, waits for them, and re-layouts: 11.4 us -> 9.41 us
where the time goes in v11:
time: 289 us; the launch traced here: 288 us
  Pallas kernels  116 us (40%)
  matrix products  57 us (20%)
  other arithmetic  36.2 us (13%)
  waiting for transfers between devices  22.6 us (8%)
  local copies, waits for them, and re-layouts  21.4 us (7%)
  blocking collectives  19.4 us (7%)
  between operations  15.2 us (5%)
    pallas_call x1, Pallas kernels, ring_sum(): pl.pallas_call(lambda *refs: ring_sum_kernel(n, *refs), out_shape=jax.Sha...  62.4 us
    pallas_call x2, Pallas kernels, adjoint(): pl.pallas_call(adjoint_kernel, out_shape=(jax.ShapeDtypeStruct((count, 2...  31.2 us
    all_gather x3, waiting for transfers between devices, gather_feat(): return lax.all_gather(value, 'feat', axis=axis, tiled=True)  22.5 us
    all_gather x2, blocking collectives, gather_feat(): return lax.all_gather(value, 'feat', axis=axis, tiled=True)  19.4 us
    dot_general x4, matrix products, contract_cols(): lax.dot_general(left, right, (((1,), (1,)), ((), ())), preferred_element_...  17.2 us
    dot_general x2, matrix products, body(): jnp.dot(states_low, out_low, preferred_element_type=jnp.float32)  16.1 us
    pallas_call x1, Pallas kernels, recurrence_gather(): pl.pallas_call(lambda *refs: recurrence_gather_kernel(parts, *refs), out_...  13.8 us
    unnamed x208, local copies, waits for them, and re-layouts  9.41 us
  transfers between devices with their start and end apart: 3, of which 2 were waited for; matrix products, arithmetic and copies ran while one was open for 9% of the time, Pallas kernels for 3%

profile of v11, /device:TPU:0, one launch (start us, length us, event | category | flops | bytes accessed | tf_op | source)
XLA Modules:
  0.0 288.1 jit_solution(12002001298066020582)
XLA Ops:
  7.2 2.0 convert_element_type.108
  9.4 1.0 convert_element_type.111
  12.2 6.1 %all_gather.16 = f32[2,4,512]{2,1,0:T(4,128)S(1)} all-gather(f32[2,4,128]{2,1,0:T(4,128)S(1)} %copy-done.57), channel_id=1, replica_groups=mesh['seq'=8,'feat'=4] {'feat'}, dimensions={2}, use_global_device_ids=true | all-gather | bytes 20480 | tf_op jit(solution)/shard_map/all_gather | solution.py:463
  20.1 1.2 rev.30
  21.9 0.9 copy.86.masks_ref
  22.9 13.3 %all_gather.15 = bf16[768,512]{1,0:T(8,128)(2,1)S(1)} all-gather(bf16[768,128]{1,0:T(8,128)(2,1)S(1)} %copy-done.28), channel_id=1, replica_groups=mesh['seq'=8,'feat'=4] {'feat'}, dimensions={1}, use_global_device_ids=true | all-gather | bytes 983040 | tf_op jit(solution)/shard_map/all_gather | solution.py:463
  40.0 1.9 fusion.23.drive_ref
  42.3 1.0 copy-done
  43.3 1.6 pad_maximum_fusion.x_ref
  44.9 0.9 broadcast_in_dim.8.up_ref.refs_0_
  45.8 0.9 broadcast_in_dim.9.down_ref.refs_1_
  46.7 8.8 %shard_map.354.states_ref = f32[768,1536]{1,0:T(8,128)} custom-call(f32[768,128]{1,0:T(8,128)} %broadcast_in_dim.8.up_ref.refs_0_, f32[768,128]{1,0:T(8,128)} %broadcast_in_dim.9.down_ref.refs_1_, f32[4,8,384]{2,1,0:T(8,128)} %pad_maximum_fusion.5.pow_ref, f32[768,768]{1,0:T(8,128)} %pad_maximum_fusion.x_ref), custom_call_target="tpu_custom_call" | custom-call | flops 11796480 | bytes 9437184 | tf_op jit(solution)/shard_map/pallas_call | solution.py:129
  55.5 12.0 %all-gather.6.cloned.1.call-done = bf16[2,1536,512]{2,1,0:T(8,128)(2,1)} async-done(((bf16[2,1536,128]{2,1,0:T(8,128)(2,1)}), bf16[2,1536,512]{2,1,0:T(8,128)(2,1)}) %all-gather.6.cloned.1.call-update) | async-done | bytes 3145744 | tf_op jit(solution)/shard_map/all_gather | solution.py:463
  67.6 8.5 %multiply_multiply_fusion.11 = (f32[768,512]{1,0:T(8,128)}, f32[768,512]{1,0:T(8,128)}) fusion(f32[512]{0:T(512)S(1)} %bitcast.485, f32[512]{0:T(512)S(1)} %bitcast.488, f32[768]{0:T(1024)S(1)} %add_rsqrt_fusion.1, f32[768]{0:T(1024)S(1)} %broadcast_multiply_fusion.6, bf16[768,512]{1,0:T(8,128)(2,1)S(1)} %all_gather.15, f32[512]{0:T(512)S(1)} %bitcast.494, ...), kind=kOutput, calls=%fused_computation.74 | convolution fusion | flops 1237057536 | bytes 10235904 | tf_op jit(solution)/shard_map/dot_general | solution.py:547
  76.0 10.5 %all-gather.8.cloned.1.call-done = bf16[2,512,512]{2,1,0:T(8,128)(2,1)} async-done(((bf16[2,512,128]{2,1,0:T(8,128)(2,1)}), bf16[2,512,512]{2,1,0:T(8,128)(2,1)}) %all-gather.8.cloned.1.call-update) | async-done | bytes 1048592 | tf_op jit(solution)/shard_map/all_gather | solution.py:463
  86.5 4.0 %fusion.105 = (f32[768]{0:T(1024)S(1)}, f32[768,512]{1,0:T(8,128)S(1)}, f32[768,512]{1,0:T(8,128)}) fusion(f32[768,512]{1,0:T(8,128)} %get-tuple-element.299, bf16[768,512]{1,0:T(8,128)(2,1)S(1)} %all_gather.15, f32[512]{0:T(512)S(1)} %bitcast.499, bf16[2,512,512]{2,1,0:T(8,128)(2,1)} %all-gather.8.cloned.1.call-done), kind=kOutput, calls=%fused_computation.355 | convolution fusion | flops 406191360 | bytes 7607296 | tf_op jit(solution)/shard_map/dot_general | solution.py:552
  91.3 1.1 copy-done.17
  93.6 1.0 copy-done.1
  94.6 1.6 pad_maximum_fusion.1.refs_3_
  96.2 13.8 %shard_map.355 = (f32[768,1536]{1,0:T(8,128)}, bf16[768,512]{1,0:T(8,128)(2,1)}) custom-call(f32[768,128]{1,0:T(8,128)} %broadcast_in_dim.8.up_ref.refs_0_, f32[768,128]{1,0:T(8,128)} %broadcast_in_dim.9.down_ref.refs_1_, f32[4,8,384]{2,1,0:T(8,128)} %pad_maximum_fusion.6.refs_2_, f32[768,768]{1,0:T(8,128)} %pad_maximum_fusion.1.refs_3_, ...), custom_call_target="tpu_custom_call" | custom-call | flops 11796480 | bytes 9437184 | tf_op jit(solution)/shard_map/pallas_call | solution.py:190
  110.1 7.6 %multiply_multiply_fusion.10 = (f32[768,512]{1,0:T(8,128)S(1)}, f32[768,512]{1,0:T(8,128)S(1)}, f32[768,512]{1,0:T(8,128)S(1)}) fusion(f32[512]{0:T(512)S(1)} %bitcast.491, f32[512]{0:T(512)S(1)} %bitcast.478, f32[768]{0:T(1024)S(1)} %add_rsqrt_fusion, f32[768,512]{1,0:T(8,128)S(1)} %get-tuple-element.206, f32[768]{0:T(1024)S(1)} %broadcast_multiply_fusion.5, ...), kind=kOutput, calls=%fused_computation.72 | convolution fusion | flops 1236664320 | bytes 12595200 | tf_op jit(solution)/shard_map/dot_general | solution.py:547
  117.7 1.6 convert_reduce_fusion.1
  120.6 2.3 fusion.108
  123.0 1.7 convolution_bitcast_fusion
  125.0 3.6 %fusion.16.g_ref = f32[768,1536]{1,0:T(8,128)} fusion(bf16[768,512]{1,0:T(8,128)(2,1)S(1)} %get-tuple-element.304, bf16[2,1536,512]{2,1,0:T(8,128)(2,1)S(1)} %copy-done.93), kind=kOutput, calls=%fused_computation.76 | convolution fusion | flops 1207959552 | bytes 7077888 | tf_op jit(solution)/shard_map/dot_general | solution.py:457
  129.6 0.9 broadcast_in_dim.11.mb_ref
  130.5 15.7 %shard_map.356 = (bf16[768,768]{1,0:T(8,128)(2,1)}, f32[4,384]{1,0:T(4,128)}) custom-call(f32[768,128]{1,0:T(8,128)} %broadcast_in_dim.10.ma_ref, f32[768,128]{1,0:T(8,128)} %broadcast_in_dim.11.mb_ref, f32[4,8,384]{2,1,0:T(8,128)} %pad_maximum_fusion.7.pow_ref, f32[4,384]{1,0:T(4,128)} %pad_maximum_fusion.10.coef_ref, f32[768,4]{1,0:T(8,128)} %copy.86.masks_ref, ...), custom_call_target="tpu_custom_call" | custom-call | flops 17694720 | bytes 14155776 | tf_op jit(solution)/shard_map/pallas_call | solution.py:426
  146.2 1.8 convolution_bitcast_fusion.2
  148.1 3.9 %multiply_reduce_fusion.1 = (f32[512]{0:T(512)}, f32[768]{0:T(1024)S(1)}, f32[512]{0:T(512)}, f32[768]{0:T(1024)S(1)}, f32[512]{0:T(512)}, /*index=5*/f32[768,512]{1,0:T(8,128)S(1)}) fusion(f32[768]{0:T(1024)S(1)} %add_rsqrt_fusion, f32[768,512]{1,0:T(8,128)S(1)} %get-tuple-element.206, f32[768]{0:T(1024)S(1)} %broadcast_multiply_fusion.5, ...), kind=kOutput, calls=%fused_computation.25 | convolution fusion | flops 609874944 | bytes 6711296 | tf_op jit(solution)/shard_map/dot_general | solution.py:591
  152.0 3.5 %convert_reduce_fusion.2 = (f32[512]{0:T(512)}, bf16[768,512]{1,0:T(8,128)(2,1)S(1)}, f32[768,512]{1,0:T(8,128)}) fusion(f32[768,512]{1,0:T(8,128)S(1)} %copy-done.20, f32[768,512]{1,0:T(8,128)S(1)} %copy-done.4, f32[768]{0:T(1024)S(1)} %broadcast_multiply_fusion.3, f32[768,512]{1,0:T(8,128)S(1)} %get-tuple-element.206, f32[768]{0:T(1024)} %copy-done.41, ...), kind=kLoop, calls=%fused_computation.26 | loop fusion | flops 6684160 | bytes 9456640 | tf_op jit(solution)/shard_map/reduce_sum | solution.py:569
  155.6 1.2 convolution_bitcast_fusion.5
  158.2 1.4 stack.268
  159.6 2.0 rev.31
  161.6 7.6 %fusion.109 = (bf16[768,512]{1,0:T(8,128)(2,1)S(1)}, f32[768,512]{1,0:T(8,128)}) fusion(f32[768,512]{1,0:T(8,128)} %get-tuple-element.300, bf16[768,512]{1,0:T(8,128)(2,1)} %copy-done.21, bf16[2,512,512]{2,1,0:T(8,128)(2,1)} %all-gather.8.cloned.1.call-done, f32[768,512]{1,0:T(8,128)S(1)} %copy-done.13, f32[768,512]{1,0:T(8,128)} %get-tuple-element.301), kind=kOutput, calls=%fused_computation.359 | convolution fusion | flops 431751168 | bytes 8388608 | tf_op jit(solution)/shard_map/dot_general | solution.py:457
  169.3 1.7 convolution_bitcast_fusion.1
  172.2 3.6 %fusion.15.g_ref = f32[768,1536]{1,0:T(8,128)} fusion(bf16[768,512]{1,0:T(8,128)(2,1)S(1)} %get-tuple-element.307, bf16[2,1536,512]{2,1,0:T(8,128)(2,1)S(1)} %copy-done.94), kind=kOutput, calls=%fused_computation.75 | convolution fusion | flops 1207959552 | bytes 7077888 | tf_op jit(solution)/shard_map/dot_general | solution.py:457
  175.8 15.5 %shard_map.357 = (bf16[768,768]{1,0:T(8,128)(2,1)}, f32[4,384]{1,0:T(4,128)}) custom-call(f32[768,128]{1,0:T(8,128)} %broadcast_in_dim.10.ma_ref, f32[768,128]{1,0:T(8,128)} %broadcast_in_dim.11.mb_ref, f32[4,8,384]{2,1,0:T(8,128)} %pad_maximum_fusion.8.pow_ref, f32[4,384]{1,0:T(4,128)} %pad_maximum_fusion.11.coef_ref, f32[768,4]{1,0:T(8,128)} %copy.86.masks_ref, ...), custom_call_target="tpu_custom_call" | custom-call | flops 17694720 | bytes 14155776 | tf_op jit(solution)/shard_map/pallas_call | solution.py:426
  191.4 1.7 convolution_bitcast_fusion.3
  194.6 1.4 pad_maximum_fusion.2
  196.7 2.9 %fusion.88 = (f32[512]{0:T(512)S(1)}, f32[512]{0:T(512)S(1)}, f32[512]{0:T(512)S(1)}, f32[768]{0:T(1024)S(1)}, f32[768]{0:T(1024)S(1)}, /*index=5*/f32[768,512]{1,0:T(8,128)}, f32[768,512]{1,0:T(8,128)}) fusion(f32[768]{0:T(1024)S(1)} %copy-done.45, f32[768]{0:T(1024)S(1)} %copy-done.47, bf16[768,512]{1,0:T(8,128)(2,1)S(1)} %all_gather.15, ...), kind=kOutput, calls=%fused_computation.349 | convolution fusion | flops 610268160 | bytes 7497728 | tf_op jit(solution)/shard_map/dot_general | solution.py:591
  199.9 1.8 pad_bitcast_fusion.refs_0_
  201.7 62.4 %shard_map.358 = bf16[5888,128]{1,0:T(8,128)(2,1)} custom-call(f32[5888,128]{1,0:T(8,128)} %pad_bitcast_fusion.refs_0_), custom_call_target="tpu_custom_call" | custom-call | tf_op jit(solution)/shard_map/pallas_call | solution.py:319
  264.1 1.6 convert_element_type.130
  270.3 3.0 %add_multiply_fusion.4 = (f32[2,512,128]{2,1,0:T(8,128)}, f32[2,512,128]{2,1,0:T(8,128)}, f32[2,512,128]{2,1,0:T(8,128)}) fusion(f32[2,512,128]{2,1,0:T(8,128)} %param.35, f32[2,512,128]{2,1,0:T(8,128)} %param.25, f32[2,512,128]{2,1,0:T(8,128)} %bitcast.457, f32[2,512,128]{2,1,0:T(8,128)} %param.30), kind=kLoop, calls=%fused_computation.107 | loop fusion | flops 1310720 | bytes 3670016 | tf_op jit(solution)/shard_map/add | solution.py:446
  273.3 1.7 add_multiply_fusion.3
  275.1 0.9 copy-done.15
  276.5 2.7 add_multiply_fusion
  279.2 2.4 dynamic-slice_add_fusion
  (295 shorter events, 22.5 us)
Async XLA Ops:
  7.2 32.8 %all-gather.4.cloned.1.call-start = ((), (), s32[]{:S(2)}) async-start(), calls=%async_computation | async-start | bytes 1966080 | tf_op jit(solution)/shard_map/all_gather | solution.py:463
  9.4 2.9 copy-start.57
  9.4 58.2 %all-gather.6.cloned.1.call-start = ((), (), s32[]{:S(2)}) async-start(), calls=%async_computation.1 | async-start | bytes 3932160 | tf_op jit(solution)/shard_map/all_gather | solution.py:463
  10.4 12.5 %copy-start.28 = (bf16[768,128]{1,0:T(8,128)(2,1)S(1)}, bf16[768,128]{1,0:T(8,128)(2,1)}, u32[]{:S(2)}) copy-start(bf16[768,128]{1,0:T(8,128)(2,1)} %param.19) | copy-start | bytes 589828
  10.4 76.1 %all-gather.8.cloned.1.call-start = ((), (), s32[]{:S(2)}) async-start(), calls=%async_computation.2 | async-start | bytes 1310720 | tf_op jit(solution)/shard_map/all_gather | solution.py:463
  12.1 9.5 %copy-start.49 = (f32[1,384]{1,0:T(1,128)}, f32[1,384]{1,0:T(1,128)S(1)}, u32[]{:S(2)}) copy-start(f32[1,384]{1,0:T(1,128)S(1)} %get-tuple-element.187) | copy-start | bytes 4612
  12.1 24.7 %copy-start.29 = (f32[1,384]{1,0:T(1,128)}, f32[1,384]{1,0:T(1,128)S(1)}, u32[]{:S(2)}) copy-start(f32[1,384]{1,0:T(1,128)S(1)} %get-tuple-element.188) | copy-start | bytes 4612
  12.1 24.7 %copy-start.36 = (f32[1,384]{1,0:T(1,128)}, f32[1,384]{1,0:T(1,128)S(1)}, u32[]{:S(2)}) copy-start(f32[1,384]{1,0:T(1,128)S(1)} %get-tuple-element.189) | copy-start | bytes 4612
  18.3 49.2 %copy-start.65 = (f32[1,1,512]{2,1,0:T(1,128)}, f32[1,1,512]{2,1,0:T(1,128)S(1)}, u32[]{:S(2)}) copy-start(f32[1,1,512]{2,1,0:T(1,128)S(1)} %get-tuple-element.251) | copy-start | bytes 6148
  18.4 49.2 %copy-start.67 = (f32[1,1,512]{2,1,0:T(1,128)}, f32[1,1,512]{2,1,0:T(1,128)S(1)}, u32[]{:S(2)}) copy-start(f32[1,1,512]{2,1,0:T(1,128)S(1)} %get-tuple-element.252) | copy-start | bytes 6148
  18.4 49.2 %copy-start.83 = (f32[1,1,512]{2,1,0:T(1,128)}, f32[1,1,512]{2,1,0:T(1,128)S(1)}, u32[]{:S(2)}) copy-start(f32[1,1,512]{2,1,0:T(1,128)S(1)} %get-tuple-element.250) | copy-start | bytes 6148
  18.4 91.7 %copy-start.55 = (f32[1,1,512]{2,1,0:T(1,128)}, f32[1,1,512]{2,1,0:T(1,128)S(1)}, u32[]{:S(2)}) copy-start(f32[1,1,512]{2,1,0:T(1,128)S(1)} %get-tuple-element.248) | copy-start | bytes 6148
  18.4 91.7 %copy-start.69 = (f32[1,1,512]{2,1,0:T(1,128)}, f32[1,1,512]{2,1,0:T(1,128)S(1)}, u32[]{:S(2)}) copy-start(f32[1,1,512]{2,1,0:T(1,128)S(1)} %get-tuple-element.247) | copy-start | bytes 6148
  18.4 91.7 %copy-start.85 = (f32[1,1,512]{2,1,0:T(1,128)}, f32[1,1,512]{2,1,0:T(1,128)S(1)}, u32[]{:S(2)}) copy-start(f32[1,1,512]{2,1,0:T(1,128)S(1)} %get-tuple-element.245) | copy-start | bytes 6148
  19.1 2.5 copy-start.38
  19.1 17.6 %copy-start.31 = (f32[1,384]{1,0:T(1,128)}, f32[1,384]{1,0:T(1,128)S(1)}, u32[]{:S(2)}) copy-start(f32[1,384]{1,0:T(1,128)S(1)} %get-tuple-element.259) | copy-start | bytes 4612
  20.1 16.6 %copy-start.33 = (f32[8,384]{1,0:T(8,128)}, f32[8,384]{1,0:T(8,128)S(1)}, u32[]{:S(2)}) copy-start(f32[8,384]{1,0:T(8,128)S(1)} %stack.266) | copy-start | bytes 36868
  36.3 31.2 %copy-start.46 = (f32[768]{0:T(1024)}, f32[768]{0:T(1024)S(1)}, u32[]{:S(2)}) copy-start(f32[768]{0:T(1024)S(1)} %broadcast_multiply_fusion.6) | copy-start | bytes 9220
  36.8 30.8 %copy-start.44 = (f32[768]{0:T(1024)}, f32[768]{0:T(1024)S(1)}, u32[]{:S(2)}) copy-start(f32[768]{0:T(1024)S(1)} %add_rsqrt_fusion.1) | copy-start | bytes 9220
  37.9 4.1 %copy-start.6 = (bf16[768,512]{1,0:T(8,128)(2,1)}, bf16[768,512]{1,0:T(8,128)(2,1)S(1)}, u32[]{:S(2)}) copy-start(bf16[768,512]{1,0:T(8,128)(2,1)S(1)} %fusion.17) | copy-start | bytes 2359300
  90.6 57.4 %copy-start.41 = (f32[768]{0:T(1024)}, f32[768]{0:T(1024)S(1)}, u32[]{:S(2)}) copy-start(f32[768]{0:T(1024)S(1)} %broadcast_multiply_fusion.5) | copy-start | bytes 9220
  91.0 57.1 %copy-start.48 = (f32[768]{0:T(1024)}, f32[768]{0:T(1024)S(1)}, u32[]{:S(2)}) copy-start(f32[768]{0:T(1024)S(1)} %add_rsqrt_fusion) | copy-start | bytes 9220
  110.1 7.6 %copy-start.11 = (bf16[768,512]{1,0:T(8,128)(2,1)S(1)}, bf16[768,512]{1,0:T(8,128)(2,1)}, u32[]{:S(2)}) copy-start(bf16[768,512]{1,0:T(8,128)(2,1)} %get-tuple-element.29) | copy-start | bytes 2359300
  110.1 7.6 %copy-start.27 = (bf16[2,512,512]{2,1,0:T(8,128)(2,1)S(1)}, bf16[2,512,512]{2,1,0:T(8,128)(2,1)}, u32[]{:S(2)}) copy-start(bf16[2,512,512]{2,1,0:T(8,128)(2,1)} %all-gather.8.cloned.1.call-done) | copy-start | bytes 3145732
  119.7 3.3 %slice-start.2 = ((s8[4718592]{0:T(1024)(128)(4,1)}), s8[4194304]{0:T(1024)(128)(4,1)S(1)}, s32[]{:S(2)}) async-start(s8[4718592]{0:T(1024)(128)(4,1)} %bitcast.452), calls=%async_computation.5 | async-start | bytes 8388608
  148.1 3.9 %copy-start.4 = (f32[768,512]{1,0:T(8,128)S(1)}, f32[768,512]{1,0:T(8,128)}, u32[]{:S(2)}) copy-start(f32[768,512]{1,0:T(8,128)} %get-tuple-element.299) | copy-start | bytes 4718596
  148.1 3.9 %copy-start.12 = (bf16[768,512]{1,0:T(8,128)(2,1)S(1)}, bf16[768,512]{1,0:T(8,128)(2,1)}, u32[]{:S(2)}) copy-start(bf16[768,512]{1,0:T(8,128)(2,1)} %get-tuple-element.29) | copy-start | bytes 2359300
  148.1 3.9 %copy-start.20 = (f32[768,512]{1,0:T(8,128)S(1)}, f32[768,512]{1,0:T(8,128)}, u32[]{:S(2)}) copy-start(f32[768,512]{1,0:T(8,128)} %get-tuple-element.301) | copy-start | bytes 4718596
  152.0 17.2 %slice-start = ((s8[4718592]{0:T(1024)(128)(4,1)}), s8[524288]{0:T(1024)(128)(4,1)S(1)}, s32[]{:S(2)}) async-start(s8[4718592]{0:T(1024)(128)(4,1)} %bitcast.450), calls=%async_computation.3 | async-start | bytes 1048576
  155.6 5.9 %copy-start.13 = (f32[768,512]{1,0:T(8,128)S(1)}, f32[768,512]{1,0:T(8,128)}, u32[]{:S(2)}) copy-start(f32[768,512]{1,0:T(8,128)} %get-tuple-element.163) | copy-start | bytes 4718596
  161.6 7.6 %slice-start.1 = ((s8[4718592]{0:T(1024)(128)(4,1)}), s8[4194304]{0:T(1024)(128)(4,1)S(1)}, s32[]{:S(2)}) async-start(s8[4718592]{0:T(1024)(128)(4,1)} %bitcast.450), calls=%async_computation.4 | async-start | bytes 8388608
  169.2 2.4 copy-start.34
  169.2 2.4 copy-start.35
  169.2 2.4 copy-start.42
  169.3 2.4 copy-start.43
  169.3 3.0 %copy-start.94 = (bf16[2,1536,512]{2,1,0:T(8,128)(2,1)S(1)}, bf16[2,1536,512]{2,1,0:T(8,128)(2,1)}, u32[]{:S(2)}) copy-start(bf16[2,1536,512]{2,1,0:T(8,128)(2,1)} %all-gather.6.cloned.1.call-done) | copy-start | bytes 9437188
  196.7 2.9 %copy-start.71 = (f32[512]{0:T(512)S(1)}, f32[512]{0:T(512)}, u32[]{:S(2)}) copy-start(f32[512]{0:T(512)} %get-tuple-element.161) | copy-start | bytes 6148
  265.7 3.8 %copy-start.59 = (f32[8,128]{1,0:T(8,128)}, f32[8,128]{1,0:T(8,128)S(1)}, u32[]{:S(2)}) copy-start(f32[8,128]{1,0:T(8,128)S(1)} %slice_multiply_fusion.4) | copy-start | bytes 12292
  266.8 8.1 %copy-start.5 = (f32[3072,128]{1,0:T(8,128)}, f32[3072,128]{1,0:T(8,128)S(1)}, u32[]{:S(2)}) copy-start(f32[3072,128]{1,0:T(8,128)S(1)} %slice_multiply_fusion) | copy-start | bytes 4718596
  266.8 2.7 copy-start.58
  266.9 2.7 copy-start.81
  266.9 2.7 copy-start.82
  269.5 3.7 %copy-start.9 = (f32[2,128,768]{2,1,0:T(8,128)}, f32[2,128,768]{2,1,0:T(8,128)S(1)}, u32[]{:S(2)}) copy-start(f32[2,128,768]{2,1,0:T(8,128)S(1)} %mul.6070) | copy-start | bytes 2359300
  270.3 3.0 %copy-start.8 = (f32[2,128,768]{2,1,0:T(8,128)S(1)}, f32[2,128,768]{2,1,0:T(8,128)}, u32[]{:S(2)}) copy-start(f32[2,128,768]{2,1,0:T(8,128)} %param.23) | copy-start | bytes 2359300
  270.3 3.0 %copy-start.24 = (f32[2,128,768]{2,1,0:T(8,128)S(1)}, f32[2,128,768]{2,1,0:T(8,128)}, u32[]{:S(2)}) copy-start(f32[2,128,768]{2,1,0:T(8,128)} %param.33) | copy-start | bytes 2359300
  270.3 3.0 %copy-start.25 = (f32[2,128,768]{2,1,0:T(8,128)S(1)}, f32[2,128,768]{2,1,0:T(8,128)}, u32[]{:S(2)}) copy-start(f32[2,128,768]{2,1,0:T(8,128)} %param.28) | copy-start | bytes 2359300
  273.3 2.7 copy-start.15
  273.3 3.2 %copy-start.16 = (f32[2,1536,128]{2,1,0:T(8,128)S(1)}, f32[2,1536,128]{2,1,0:T(8,128)}, u32[]{:S(2)}) copy-start(f32[2,1536,128]{2,1,0:T(8,128)} %param.29) | copy-start | bytes 4718596
  (55 other events, 82.0 us)
Sparse Core Ops, SparseCore 0:
  10.2 26.5 all-gather.3
  38.9 28.6 all-gather.5
  69.7 16.8 all-gather.7

commit v12 on v10

--- a/solution.py
+++ b/solution.py
@@ -138,6 +138,100 @@
 
 
 MESH = pl.DeviceIdType.MESH
+
+
+def forward_gather_kernel(x_ref, o_ref, local, sends, recvs):
+    me = lax.axis_index("feat")
+    partner = me + 1 - 2 * (me % 2)
+    across = (me + 2) % 4
+    diagonal = partner + 2 - 4 * (partner // 2)
+
+    barrier = pltpu.get_barrier_semaphore()
+    for peer in (partner, across):
+        pl.semaphore_signal(barrier, 1, device_id={"feat": peer}, device_id_type=MESH)
+    pl.semaphore_wait(barrier, 2)
+
+    own = pltpu.make_async_copy(x_ref, o_ref.at[me], local)
+    own.start()
+
+    def remote(src, slot, peer, k):
+        return pltpu.make_async_remote_copy(
+            src_ref=src,
+            dst_ref=o_ref.at[slot],
+            send_sem=sends.at[k],
+            recv_sem=recvs.at[k],
+            device_id={"feat": peer},
+            device_id_type=MESH,
+        )
+
+    to_across = remote(x_ref, me, across, 0)
+    to_partner = remote(x_ref, me, partner, 1)
+    to_across.start()
+    to_partner.start()
+    remote(x_ref, across, across, 0).wait_recv()
+    onward = remote(o_ref.at[across], across, partner, 2)
+    onward.start()
+    remote(x_ref, partner, partner, 1).wait_recv()
+    remote(x_ref, diagonal, partner, 2).wait_recv()
+    own.wait()
+    to_across.wait_send()
+    to_partner.wait_send()
+    onward.wait_send()
+
+
+def forward_gather(x):
+    rows, lanes = x.shape
+    anywhere = pl.BlockSpec(memory_space=pl.ANY)
+    return pl.pallas_call(
+        forward_gather_kernel,
+        out_shape=jax.ShapeDtypeStruct((4, rows, lanes), x.dtype),
+        in_specs=[anywhere],
+        out_specs=anywhere,
+        scratch_shapes=[
+            pltpu.SemaphoreType.DMA(()),
+            pltpu.SemaphoreType.DMA((3,)),
+            pltpu.SemaphoreType.DMA((3,)),
+        ],
+        compiler_params=pltpu.CompilerParams(collective_id=1, has_side_effects=True),
+    )(x)
+
+
+def split_exact(value):
+    high = lax.reduce_precision(value, exponent_bits=8, mantissa_bits=7)
+    rest = value - high
+    middle = lax.reduce_precision(rest, exponent_bits=8, mantissa_bits=7)
+    low = rest - middle
+    return jnp.concatenate([high, middle, low], 0).astype(jnp.bfloat16)
+
+
+def join_exact(pieces):
+    third = pieces.shape[-2] // 3
+    pieces = pieces.astype(jnp.float32)
+    return pieces[..., :third, :] + (pieces[..., third : 2 * third, :] + pieces[..., 2 * third :, :])
+
+
+def lanes_joined(stacked):
+    moved = jnp.moveaxis(stacked, 0, 1)
+    return moved.reshape(moved.shape[0], -1)
+
+
+def unpack(stacked, pieces):
+    result = []
+    start = 0
+    for piece in pieces:
+        result.append(stacked[:, start : start + piece.shape[0]])
+        start += piece.shape[0]
+    return result
+
+
+def layer_pieces(in_shard, out_shard, gate_shard):
+    return [in_shard.T.astype(jnp.bfloat16), out_shard.astype(jnp.bfloat16), gate_shard.astype(jnp.bfloat16)]
+
+
+def layer_full(gathered):
+    in_t, out_w, gate_w = gathered[:3]
+    in_full = jnp.transpose(in_t, (0, 2, 1)).reshape(-1, in_t.shape[1])
+    return [in_full, lanes_joined(out_w), lanes_joined(gate_w)]
 
 
 def ring_place(position, n):
@@ -439,11 +533,33 @@
     keep_prev, keep_next = lanes(carry_prev), lanes(carry_next)
     keep_after_next, keep_before_prev = lanes(after_next), lanes(before_prev)
 
-    in_all = gather_feat(input_matrix.astype(jnp.bfloat16), 1)
-    out_all = gather_feat(output_matrix.astype(jnp.bfloat16), 2)
-    gate_all = gather_feat(gate_matrix.astype(jnp.bfloat16), 2)
-    feature_all = gather_feat(feature_vectors, 2)
-    stream = gather_feat(activations_in, 1).astype(jnp.float32)
+    parts = lax.axis_size("feat")
+    first = layer_pieces(input_matrix[0], output_matrix[0], gate_matrix[0])
+    feature_pieces = split_exact(feature_vectors.reshape(-1, shard))
+    first_pieces = first + [feature_pieces, activations_in] + ([] if layers > 1 else [cotangent])
+    if parts == 4:
+        stacked = forward_gather(jnp.concatenate(first_pieces, 0))
+    else:
+        stacked = lax.all_gather(jnp.concatenate(first_pieces, 0), "feat", axis=0, tiled=False)
+    gathered = unpack(stacked, first_pieces)
+    weights = [layer_full(gathered)]
+    feature_all = lanes_joined(join_exact(gathered[3])).reshape(feature_vectors.shape[:-1] + (-1,))
+    stream = lanes_joined(gathered[4]).astype(jnp.float32)
+    cotangent_all = lanes_joined(gathered[5]) if layers == 1 else None
+    previous = stacked
+    for k in range(1, layers):
+        later = layer_pieces(input_matrix[k], output_matrix[k], gate_matrix[k])
+        later = later + ([cotangent] if k == layers - 1 else [])
+        packed = jnp.concatenate(later, 0)
+        packed, previous = lax.optimization_barrier((packed, previous))
+        previous = lax.all_gather(packed, "feat", axis=0, tiled=False)
+        gathered = unpack(previous, later)
+        weights.append(layer_full(gathered))
+        if k == layers - 1:
+            cotangent_all = lanes_joined(gathered[3])
+    in_all = [entry[0] for entry in weights]
+    out_all = [entry[1] for entry in weights]
+    gate_all = [entry[2] for entry in weights]
 
     saved = []
     for layer in range(layers):
@@ -480,7 +596,7 @@
         saved.append((scale, unit, normed_low, drive, states, states_low, mixed, act, act_low, pre))
         stream = stream + act * jax.nn.sigmoid(pre)
 
-    grad = gather_feat(cotangent, 1).astype(jnp.float32) * alive[:, None]
+    grad = cotangent_all.astype(jnp.float32) * alive[:, None]
     layer_grads = [None] * layers
     for layer in reversed(range(layers)):
         scale, unit, normed_low, drive, states, states_low, mixed, act, act_low, pre = saved[layer]

time: 279 us -> 294 us (1.054)
  Pallas kernels: 110 us -> 143 us
  blocking collectives: 28.7 us -> 0 us
  local copies, waits for them, and re-layouts: 21.3 us -> 44.4 us
  waiting for transfers between devices: 12.3 us -> 0.04 us
  matrix products: 55.9 us -> 51.4 us
  other arithmetic: 34.8 us -> 39 us
    pallas_call x0 -> x1, Pallas kernels: none -> 32.1 us  [forward_gather(): pl.pallas_call(forward_gather_kernel, out_shape=jax.ShapeDtypeStruct((4,...]
    all_gather x3 -> x0, blocking collectives: 28.7 us -> none  [gather_feat(): return lax.all_gather(value, 'feat', axis=axis, tiled=True)]
    all_gather x3 -> x1, waiting for transfers between devices: 12.3 us -> 0.02 us  [body(): previous = lax.all_gather(packed, 'feat', axis=0, tiled=False)]
    unnamed x236 -> x153, local copies, waits for them, and re-layouts: 11.4 us -> 20.3 us
    transpose x0 -> x5, local copies, waits for them, and re-layouts: none -> 7.17 us  [the longest x4 4.31 us: lanes_joined(): moved = jnp.moveaxis(stacked, 0, 1)]
    convert_element_type x0 -> x5, local copies, waits for them, and re-layouts: none -> 4.22 us  [the longest x2 3.49 us: body(): stream = lanes_joined(gathered[4]).astype(jnp.float32)]
    unnamed x2 -> x6, other arithmetic: 0.01 us -> 3.06 us
    convert_element_type x3 -> x1, other arithmetic: 3.75 us -> 0.76 us  [join_exact(): pieces = pieces.astype(jnp.float32)]
  transfers between devices with their start and end apart: 3 -> 1, of which waited for: 2 -> 0; matrix products, arithmetic and copies ran while one was open for 9% -> 13% of each run, Pallas kernels for 3% -> 3%
where the time goes in v12:
time: 294 us; the launch traced here: 293 us
  Pallas kernels  143 us (49%)
  matrix products  51.4 us (17%)
  local copies, waits for them, and re-layouts  44.4 us (15%)
  other arithmetic  39 us (13%)
  between operations  15.1 us (5%)
    pallas_call x1, Pallas kernels, ring_sum(): pl.pallas_call(lambda *refs: ring_sum_kernel(n, *refs), out_shape=jax.Sha...  62.5 us
    pallas_call x1, Pallas kernels, forward_gather(): pl.pallas_call(forward_gather_kernel, out_shape=jax.ShapeDtypeStruct((4,...  32.1 us
    pallas_call x2, Pallas kernels, adjoint(): pl.pallas_call(adjoint_kernel, out_shape=(jax.ShapeDtypeStruct((count, 2...  31.1 us
    unnamed x153, local copies, waits for them, and re-layouts  20.3 us
    dot_general x4, matrix products, contract_cols(): lax.dot_general(left, right, (((1,), (1,)), ((), ())), preferred_element_...  18.2 us
    pallas_call x2, Pallas kernels, recurrence(): pl.pallas_call(recurrence_kernel, out_shape=jax.ShapeDtypeStruct((count,...  17.7 us
    dot_general x2, matrix products, body(): jnp.dot(states_low, out_low, preferred_element_type=jnp.float32)  12.9 us
    dot_general x6, matrix products, contract_rows(): lax.dot_general(left, right, (((0,), (0,)), ((), ())), preferred_element_...  7.51 us
  transfers between devices with their start and end apart: 1, of which 0 were waited for; matrix products, arithmetic and copies ran while one was open for 13% of the time, Pallas kernels for 3%

profile of v12, /device:TPU:0, one launch (start us, length us, event | category | flops | bytes accessed | tf_op | source)
XLA Modules:
  0.0 293.3 jit_solution(10065762570070603151)
XLA Ops:
  7.3 1.5 copy.106
  11.5 32.1 %shard_map.354 = bf16[4,3608,128]{2,1,0:T(8,128)(2,1)} custom-call(bf16[3608,128]{1,0:T(8,128)(2,1)} %copy-done.35), custom_call_target="tpu_custom_call" | custom-call | tf_op jit(solution)/shard_map/pallas_call | solution.py:185
  45.0 1.3 convert_reduce_fusion
  46.3 1.1 slice_bitcast_fusion.2
  47.4 1.5 slice_bitcast_fusion
  48.9 2.9 slice_bitcast_fusion.1
  54.1 1.5 fusion.2
  57.3 2.9 copy.124
  60.2 1.9 copy.107
  62.1 1.6 copy.113
  65.2 2.3 convolution_bitcast_fusion.2.drive_ref
  68.8 1.6 pad_maximum_fusion.x_ref
  72.3 8.8 %shard_map.355.states_ref = f32[768,1536]{1,0:T(8,128)} custom-call(f32[768,128]{1,0:T(8,128)} %broadcast_in_dim.8.up_ref, f32[768,128]{1,0:T(8,128)} %broadcast_in_dim.9.down_ref, f32[4,8,384]{2,1,0:T(8,128)} %pad_maximum_fusion.6.pow_ref, f32[768,768]{1,0:T(8,128)} %pad_maximum_fusion.x_ref), custom_call_target="tpu_custom_call" | custom-call | flops 11796480 | bytes 9437184 | tf_op jit(solution)/shard_map/pallas_call | solution.py:129
  83.0 1.5 multiply_add_fusion.12
  84.5 2.0 copy-done
  86.5 5.8 %multiply_multiply_fusion.11 = (f32[768,512]{1,0:T(8,128)S(1)}, f32[768,512]{1,0:T(8,128)}) fusion(f32[768,512]{1,0:T(8,128)S(1)} %get-tuple-element.226, f32[512]{0:T(512)S(1)} %bitcast.546, bf16[1536,512]{0,1:T(8,128)(2,1)S(1)} %bitcast.495, f32[768,1536]{1,0:T(8,128)S(1)} %copy-done), kind=kOutput, calls=%fused_computation.80 | convolution fusion | flops 1235091456 | bytes 11012096 | tf_op jit(solution)/shard_map/dot_general | solution.py:590
  92.3 2.0 fusion.113
  95.9 1.3 slice.295
  97.2 1.5 slice.293
  98.7 3.0 %convert_bitcast_fusion.1 = (f32[4,96,8,128]{3,2,1,0:T(8,128)}, bf16[4,768,128]{2,1,0:T(8,128)(2,1)}) fusion(bf16[4,3584,128]{2,1,0:T(8,128)(2,1)} %bitcast.505), kind=kLoop, calls=%fused_computation.22 | loop fusion | flops 393216 | bytes 3932160
  102.8 1.4 copy.138
  104.2 1.6 copy.139
  108.1 1.6 pad_maximum_fusion.1.x_ref
  109.6 8.8 %shard_map.356.states_ref = f32[768,1536]{1,0:T(8,128)} custom-call(f32[768,128]{1,0:T(8,128)} %broadcast_in_dim.8.up_ref, f32[768,128]{1,0:T(8,128)} %broadcast_in_dim.9.down_ref, f32[4,8,384]{2,1,0:T(8,128)} %pad_maximum_fusion.7.pow_ref, f32[768,768]{1,0:T(8,128)} %pad_maximum_fusion.1.x_ref), custom_call_target="tpu_custom_call" | custom-call | flops 11796480 | bytes 9437184 | tf_op jit(solution)/shard_map/pallas_call | solution.py:129
  118.5 7.1 %multiply_multiply_fusion.10 = (f32[768,512]{1,0:T(8,128)S(1)}, f32[768,512]{1,0:T(8,128)S(1)}) fusion(f32[512]{0:T(512)S(1)} %bitcast.551, f32[512]{0:T(512)S(1)} %bitcast.540, f32[768]{0:T(1024)S(1)} %add_rsqrt_fusion, f32[768,512]{1,0:T(8,128)S(1)} %copy-done.3, f32[768]{0:T(1024)S(1)} %broadcast_multiply_fusion.5, f32[512]{0:T(512)S(1)} %bitcast.556, ...), kind=kOutput, calls=%fused_computation.78 | convolution fusion | flops 1236664320 | bytes 11022336 | tf_op jit(solution)/shard_map/dot_general | solution.py:590
  125.6 1.6 convert_reduce_fusion.1
  128.5 5.3 %fusion.116 = (bf16[768,512]{1,0:T(8,128)(2,1)S(1)}, f32[768,512]{1,0:T(8,128)}) fusion(f32[768,512]{1,0:T(8,128)S(1)} %get-tuple-element.301, bf16[768,512]{1,0:T(8,128)(2,1)S(1)} %get-tuple-element.162, bf16[512,512]{0,1:T(8,128)(2,1)S(1)} %bitcast.515, f32[768,512]{1,0:T(8,128)S(1)} %get-tuple-element.302, f32[768]{0:T(1024)S(1)} %get-tuple-element.294, ...), kind=kOutput, calls=%fused_computation.385 | convolution fusion | flops 432144384 | bytes 8391680 | tf_op jit(solution)/shard_map/dot_general | solution.py:484
  133.8 1.7 convolution_bitcast_fusion
  135.5 3.6 %fusion.118.g_ref = f32[768,1536]{1,0:T(8,128)} fusion(bf16[768,512]{1,0:T(8,128)(2,1)S(1)} %get-tuple-element.303, bf16[1536,512]{0,1:T(8,128)(2,1)S(1)} %bitcast.498), kind=kOutput, calls=%fused_computation.387 | convolution fusion | flops 1207959552 | bytes 7077888 | tf_op jit(solution)/shard_map/dot_general | solution.py:484
  141.0 15.6 %shard_map.357 = (bf16[768,768]{1,0:T(8,128)(2,1)}, f32[4,384]{1,0:T(4,128)}) custom-call(f32[768,128]{1,0:T(8,128)} %broadcast_in_dim.10.ma_ref, f32[768,128]{1,0:T(8,128)} %broadcast_in_dim.11.mb_ref, f32[4,8,384]{2,1,0:T(8,128)} %pad_maximum_fusion.8.pow_ref, f32[4,384]{1,0:T(4,128)} %pad_maximum_fusion.11.coef_ref, f32[768,4]{1,0:T(8,128)} %copy.120.masks_ref, ...), custom_call_target="tpu_custom_call" | custom-call | flops 17694720 | bytes 14155776 | tf_op jit(solution)/shard_map/pallas_call | solution.py:453
  156.6 1.8 convolution_bitcast_fusion.3
  158.5 3.9 %multiply_reduce_fusion.1 = (f32[512]{0:T(512)}, f32[768]{0:T(1024)S(1)}, f32[512]{0:T(512)}, f32[768]{0:T(1024)S(1)}, f32[512]{0:T(512)}, /*index=5*/f32[768,512]{1,0:T(8,128)S(1)}) fusion(f32[768]{0:T(1024)S(1)} %add_rsqrt_fusion, f32[768,512]{1,0:T(8,128)S(1)} %copy-done.3, f32[768]{0:T(1024)S(1)} %broadcast_multiply_fusion.5, f32[512]{0:T(512)S(1)} %bitcast.541, ...), kind=kOutput, calls=%fused_computation.29 | convolution fusion | flops 609874944 | bytes 6709248 | tf_op jit(solution)/shard_map/dot_general | solution.py:634
  162.4 1.2 convert_reduce_fusion.2
  163.6 1.1 convolution_bitcast_fusion.6
  165.6 5.7 %multiply_reduce_fusion.2 = (f32[512]{0:T(512)}, bf16[768,512]{1,0:T(8,128)(2,1)S(1)}, f32[768,512]{1,0:T(8,128)}) fusion(f32[768,512]{1,0:T(8,128)S(1)} %copy-done.30, f32[768,512]{1,0:T(8,128)S(1)} %copy-done.64, bf16[768,512]{1,0:T(8,128)(2,1)S(1)} %get-tuple-element.159, bf16[512,512]{0,1:T(8,128)(2,1)S(1)} %bitcast.513, ...), kind=kOutput, calls=%fused_computation.31 | convolution fusion | flops 432537088 | bytes 9963520 | tf_op jit(solution)/shard_map/dot_general | solution.py:484
  172.8 3.6 %fusion.119.g_ref = f32[768,1536]{1,0:T(8,128)} fusion(bf16[768,512]{1,0:T(8,128)(2,1)S(1)} %get-tuple-element.237, bf16[1536,512]{0,1:T(8,128)(2,1)S(1)} %bitcast.496), kind=kOutput, calls=%fused_computation.388 | convolution fusion | flops 1207959552 | bytes 7077888 | tf_op jit(solution)/shard_map/dot_general | solution.py:484
  178.4 15.5 %shard_map.358 = (bf16[768,768]{1,0:T(8,128)(2,1)}, f32[4,384]{1,0:T(4,128)}) custom-call(f32[768,128]{1,0:T(8,128)} %broadcast_in_dim.10.ma_ref, f32[768,128]{1,0:T(8,128)} %broadcast_in_dim.11.mb_ref, f32[4,8,384]{2,1,0:T(8,128)} %pad_maximum_fusion.9.pow_ref, f32[4,384]{1,0:T(4,128)} %pad_maximum_fusion.12.coef_ref, f32[768,4]{1,0:T(8,128)} %copy.120.masks_ref, ...), custom_call_target="tpu_custom_call" | custom-call | flops 17694720 | bytes 14155776 | tf_op jit(solution)/shard_map/pallas_call | solution.py:453
  194.0 1.6 convolution_bitcast_fusion.4
  196.6 1.1 pad_maximum_fusion.5
  199.7 2.3 fusion.98
  202.3 1.8 pad_bitcast_fusion.refs_0_
  204.1 62.5 %shard_map.359 = bf16[5888,128]{1,0:T(8,128)(2,1)} custom-call(f32[5888,128]{1,0:T(8,128)} %pad_bitcast_fusion.refs_0_), custom_call_target="tpu_custom_call" | custom-call | tf_op jit(solution)/shard_map/pallas_call | solution.py:346
  266.6 1.6 convert_element_type.188
  272.7 2.2 mul.6093
  274.9 2.4 dynamic-slice_add_fusion
  278.0 2.5 add_multiply_fusion.4
  280.5 1.6 add_multiply_fusion.3
  283.7 2.7 add_multiply_fusion
  (252 shorter events, 36.5 us)
Async XLA Ops:
  7.2 2.3 copy-start.26
  7.2 2.3 copy-start.10
  7.2 88.6 %all-gather.3.cloned.1.call-start = ((), (), s32[]{:S(2)}) async-start(), calls=%async_computation | async-start | bytes 4587520 | tf_op jit(solution)/shard_map/all_gather | solution.py:555
  11.5 32.1 %copy-start.36 = (bf16[768,128]{1,0:T(8,128)(2,1)S(1)}, bf16[768,128]{1,0:T(8,128)(2,1)}, u32[]{:S(2)}) copy-start(bf16[768,128]{1,0:T(8,128)(2,1)} %slice_bitcast_fusion.5) | copy-start | bytes 589828
  11.5 32.1 %copy-start.44 = (bf16[768,128]{1,0:T(8,128)(2,1)S(1)}, bf16[768,128]{1,0:T(8,128)(2,1)}, u32[]{:S(2)}) copy-start(bf16[768,128]{1,0:T(8,128)(2,1)} %param.20) | copy-start | bytes 589828
  57.3 27.2 %copy-start.6 = (bf16[1536,4,128]{0,2,1:T(8,128)(2,1)}, bf16[1536,4,128]{0,2,1:T(8,128)(2,1)S(1)}, u32[]{:S(2)}) copy-start(bf16[1536,4,128]{0,2,1:T(8,128)(2,1)S(1)} %copy.110) | copy-start | bytes 4718596
  65.2 53.3 %copy-start.55 = (f32[1,4,128]{2,0,1:T(1,128)}, f32[1,4,128]{2,0,1:T(1,128)S(1)}, u32[]{:S(2)}) copy-start(f32[1,4,128]{2,0,1:T(1,128)S(1)} %get-tuple-element.243) | copy-start | bytes 6148
  72.3 10.8 %copy-start.9 = (f32[768,512]{1,0:T(8,128)S(1)}, f32[768,512]{1,0:T(8,128)}, u32[]{:S(2)}) copy-start(f32[768,512]{1,0:T(8,128)} %copy.113) | copy-start | bytes 4718596
  83.0 3.5 %copy-start = (f32[768,1536]{1,0:T(8,128)S(1)}, f32[768,1536]{1,0:T(8,128)}, u32[]{:S(2)}) copy-start(f32[768,1536]{1,0:T(8,128)} %shard_map.355.states_ref) | copy-start | bytes 14155780
  84.5 7.8 %copy-start.29 = (f32[768,512]{1,0:T(8,128)}, f32[768,512]{1,0:T(8,128)S(1)}, u32[]{:S(2)}) copy-start(f32[768,512]{1,0:T(8,128)S(1)} %get-tuple-element.226) | copy-start | bytes 4718596
  86.5 5.8 %copy-start.40 = (bf16[512,4,128]{0,2,1:T(8,128)(2,1)S(1)}, bf16[512,4,128]{0,2,1:T(8,128)(2,1)}, u32[]{:S(2)}) copy-start(bf16[512,4,128]{0,2,1:T(8,128)(2,1)} %copy.112) | copy-start | bytes 1572868
  92.3 2.0 copy-start.12
  95.8 10.0 %copy-start.18 = (bf16[768,512]{1,0:T(8,128)(2,1)}, bf16[768,512]{1,0:T(8,128)(2,1)S(1)}, u32[]{:S(2)}) copy-start(bf16[768,512]{1,0:T(8,128)(2,1)S(1)} %fusion.18) | copy-start | bytes 2359300
  109.6 8.9 %copy-start.3 = (f32[768,512]{1,0:T(8,128)S(1)}, f32[768,512]{1,0:T(8,128)}, u32[]{:S(2)}) copy-start(f32[768,512]{1,0:T(8,128)} %copy-done.2) | copy-start | bytes 4718596
  109.6 8.9 %copy-start.8 = (bf16[4,1536,128]{1,2,0:T(8,128)(2,1)S(1)}, bf16[4,1536,128]{1,2,0:T(8,128)(2,1)}, u32[]{:S(2)}) copy-start(bf16[4,1536,128]{1,2,0:T(8,128)(2,1)} %copy.139) | copy-start | bytes 4718596
  118.5 7.1 %copy-start.15 = (f32[4,96,8,128]{3,2,1,0:T(8,128)S(1)}, f32[4,96,8,128]{3,2,1,0:T(8,128)}, u32[]{:S(2)}) copy-start(f32[4,96,8,128]{3,2,1,0:T(8,128)} %get-tuple-element.230) | copy-start | bytes 4718596
  118.5 7.1 %copy-start.42 = (bf16[4,512,128]{1,2,0:T(8,128)(2,1)S(1)}, bf16[4,512,128]{1,2,0:T(8,128)(2,1)}, u32[]{:S(2)}) copy-start(bf16[4,512,128]{1,2,0:T(8,128)(2,1)} %copy.140) | copy-start | bytes 1572868
  127.6 6.2 %slice-start.2 = ((s8[4718592]{0:T(1024)(128)(4,1)}), s8[4194304]{0:T(1024)(128)(4,1)S(1)}, s32[]{:S(2)}) async-start(s8[4718592]{0:T(1024)(128)(4,1)} %bitcast.493), calls=%async_computation.3 | async-start | bytes 8388608
  128.5 5.3 %slice-start.3 = ((s8[4718592]{0:T(1024)(128)(4,1)}), s8[524288]{0:T(1024)(128)(4,1)S(1)}, s32[]{:S(2)}) async-start(s8[4718592]{0:T(1024)(128)(4,1)} %bitcast.493), calls=%async_computation.4 | async-start | bytes 1048576
  158.4 3.9 %copy-start.13 = (f32[768,512]{1,0:T(8,128)S(1)}, f32[768,512]{1,0:T(8,128)}, u32[]{:S(2)}) copy-start(f32[768,512]{1,0:T(8,128)} %copy-done.12) | copy-start | bytes 4718596
  158.4 3.9 %copy-start.16 = (f32[4,96,8,128]{3,2,1,0:T(8,128)S(1)}, f32[4,96,8,128]{3,2,1,0:T(8,128)}, u32[]{:S(2)}) copy-start(f32[4,96,8,128]{3,2,1,0:T(8,128)} %get-tuple-element.230) | copy-start | bytes 4718596
  158.4 3.9 %copy-start.34 = (f32[768,512]{1,0:T(8,128)S(1)}, f32[768,512]{1,0:T(8,128)}, u32[]{:S(2)}) copy-start(f32[768,512]{1,0:T(8,128)} %get-tuple-element.299) | copy-start | bytes 4718596
  162.3 2.4 copy-start.41
  162.3 2.4 copy-start.64
  162.4 9.0 %slice-start = ((s8[4718592]{0:T(1024)(128)(4,1)}), s8[524288]{0:T(1024)(128)(4,1)S(1)}, s32[]{:S(2)}) async-start(s8[4718592]{0:T(1024)(128)(4,1)} %bitcast.491), calls=%async_computation.1 | async-start | bytes 1048576
  163.6 7.8 %copy-start.25 = (f32[768,512]{1,0:T(8,128)}, f32[768,512]{1,0:T(8,128)S(1)}, u32[]{:S(2)}) copy-start(f32[768,512]{1,0:T(8,128)S(1)} %get-tuple-element.160) | copy-start | bytes 4718596
  163.6 2.1 copy-start.30
  165.6 5.7 %slice-start.1 = ((s8[4718592]{0:T(1024)(128)(4,1)}), s8[4194304]{0:T(1024)(128)(4,1)S(1)}, s32[]{:S(2)}) async-start(s8[4718592]{0:T(1024)(128)(4,1)} %bitcast.491), calls=%async_computation.2 | async-start | bytes 8388608
  172.8 3.6 %copy-start.47 = (f32[4,384]{1,0:T(4,128)S(1)}, f32[4,384]{1,0:T(4,128)}, u32[]{:S(2)}) copy-start(f32[4,384]{1,0:T(4,128)} %get-tuple-element.31) | copy-start | bytes 18436
  195.7 2.0 copy-start.24
  199.6 2.3 copy-start.58
  199.6 2.3 copy-start.59
  199.6 2.3 copy-start.60
  199.6 2.3 copy-start.61
  199.6 2.4 copy-start.62
  268.2 9.1 %copy-start.49 = (f32[8,128]{1,0:T(8,128)}, f32[8,128]{1,0:T(8,128)S(1)}, u32[]{:S(2)}) copy-start(f32[8,128]{1,0:T(8,128)S(1)} %slice_multiply_fusion.4) | copy-start | bytes 12292
  270.1 12.0 %copy-start.14 = (f32[3072,128]{1,0:T(8,128)}, f32[3072,128]{1,0:T(8,128)S(1)}, u32[]{:S(2)}) copy-start(f32[3072,128]{1,0:T(8,128)S(1)} %slice_multiply_fusion) | copy-start | bytes 4718596
  272.7 4.6 %copy-start.53 = (f32[2,4,128]{2,1,0:T(4,128)S(1)}, f32[2,4,128]{2,1,0:T(4,128)}, u32[]{:S(2)}) copy-start(f32[2,4,128]{2,1,0:T(4,128)} %param.36) | copy-start | bytes 12292
  272.7 4.6 %copy-start.54 = (f32[2,4,128]{2,1,0:T(4,128)S(1)}, f32[2,4,128]{2,1,0:T(4,128)}, u32[]{:S(2)}) copy-start(f32[2,4,128]{2,1,0:T(4,128)} %param.31) | copy-start | bytes 12292
  274.9 3.0 %copy-start.27 = (f32[2,512,128]{2,1,0:T(8,128)S(1)}, f32[2,512,128]{2,1,0:T(8,128)}, u32[]{:S(2)}) copy-start(f32[2,512,128]{2,1,0:T(8,128)} %param.25) | copy-start | bytes 1572868
  274.9 3.0 %copy-start.28 = (f32[1024,128]{1,0:T(8,128)S(1)}, f32[1024,128]{1,0:T(8,128)}, u32[]{:S(2)}) copy-start(f32[1024,128]{1,0:T(8,128)} %slice_multiply_fusion.2) | copy-start | bytes 1572868
  274.9 3.0 %copy-start.39 = (f32[2,512,128]{2,1,0:T(8,128)S(1)}, f32[2,512,128]{2,1,0:T(8,128)}, u32[]{:S(2)}) copy-start(f32[2,512,128]{2,1,0:T(8,128)} %param.35) | copy-start | bytes 1572868
  277.9 2.6 copy-start.20
  277.9 2.6 copy-start.23
  277.9 2.5 copy-start.37
  278.0 2.5 copy-start.38
  280.5 2.7 copy-start.32
  280.5 3.2 %copy-start.33 = (f32[2,1536,128]{2,1,0:T(8,128)S(1)}, f32[2,1536,128]{2,1,0:T(8,128)}, u32[]{:S(2)}) copy-start(f32[2,1536,128]{2,1,0:T(8,128)} %param.29) | copy-start | bytes 4718596
  (22 other events, 28.2 us)
Sparse Core Ops, SparseCore 0:
  44.7 31.8 all-gather.2

commit v13 on v10

--- a/solution.py
+++ b/solution.py
@@ -66,8 +66,22 @@
     return b_re, b_im, jnp.tile(keep, (1, reps))
 
 
-def blocked_scan(count, width, pow_ref, up_keep, down_keep, load_up, load_down, store_up, store_down):
+def blocked_scan(count, width, pow_ref, starts_ref, lengths_ref, load_up, load_down, store_up, store_down):
     tiles = count // 8
+    slots = starts_ref.shape[0]
+
+    def keeps(t0, downward):
+        rows = lax.broadcasted_iota(jnp.int32, (8, 128), 0) + t0
+        inside = jnp.zeros((8, 128), jnp.bool_)
+        for slot in range(slots):
+            begin = starts_ref[slot]
+            finish = begin + lengths_ref[slot]
+            if downward:
+                inside = inside | ((rows >= begin) & (rows < finish - 1))
+            else:
+                inside = inside | ((rows > begin) & (rows < finish))
+        return inside.astype(jnp.float32)
+
     up_powers = (pow_ref[0], pow_ref[1])
     down_powers = (pow_ref[2], pow_ref[3])
 
@@ -82,8 +96,8 @@
         td = pl.multiple_of((tiles - 1 - i) * 8, 8)
         xu_re, xu_im = load_up(tu)
         xd_re, xd_im = load_down(td)
-        bu_re, bu_im, ru = tile_scan(xu_re, xu_im, up_keep[pl.ds(tu, 8), :], up_powers, False)
-        bd_re, bd_im, rd = tile_scan(xd_re, xd_im, down_keep[pl.ds(td, 8), :], up_powers, True)
+        bu_re, bu_im, ru = tile_scan(xu_re, xu_im, keeps(tu, False), up_powers, False)
+        bd_re, bd_im, rd = tile_scan(xd_re, xd_im, keeps(td, True), up_powers, True)
         hu_re, hu_im = carry_in(bu_re, bu_im, ru, up_powers, u_re, u_im)
         hd_re, hd_im = carry_in(bd_re, bd_im, rd, down_powers, d_re, d_im)
         store_up(tu, hu_re, hu_im)
@@ -106,7 +120,7 @@
     return jnp.stack([up_re, up_im, up_re[::-1], up_im[::-1]])
 
 
-def recurrence_kernel(up_ref, down_ref, pow_ref, x_ref, out_ref):
+def recurrence_kernel(starts_ref, lengths_ref, pow_ref, x_ref, out_ref):
     count = x_ref.shape[0]
     width = pow_ref.shape[2]
 
@@ -120,21 +134,22 @@
 
         return put
 
-    blocked_scan(count, width, pow_ref, up_ref, down_ref, load, load, store(0), store(2 * width))
-
-
-def recurrence(up, down, powers, x):
+    blocked_scan(count, width, pow_ref, starts_ref, lengths_ref, load, load, store(0), store(2 * width))
+
+
+def recurrence(starts, lengths, powers, x):
     count, double = x.shape
     vmem = pl.BlockSpec(memory_space=pltpu.VMEM)
+    smem = pl.BlockSpec(memory_space=pltpu.SMEM)
     return pl.pallas_call(
         recurrence_kernel,
         out_shape=jax.ShapeDtypeStruct((count, 2 * double), jnp.float32),
-        in_specs=[vmem, vmem, vmem, vmem],
+        in_specs=[smem, smem, vmem, vmem],
         out_specs=vmem,
         cost_estimate=pl.CostEstimate(
             flops=20 * count * double, transcendentals=0, bytes_accessed=16 * count * double
         ),
-    )(up, down, powers, x)
+    )(starts, lengths, powers, x)
 
 
 MESH = pl.DeviceIdType.MESH
@@ -284,7 +299,7 @@
     return pieces
 
 
-def adjoint_kernel(ma_ref, mb_ref, pow_ref, coef_ref, masks_ref, g_ref, states_ref, drive_ref, dg_ref, sums_ref, lam):
+def adjoint_kernel(starts_ref, lengths_ref, pow_ref, coef_ref, masks_ref, g_ref, states_ref, drive_ref, dg_ref, sums_ref, lam):
     count = g_ref.shape[0]
     width = coef_ref.shape[1]
     pad = 8
@@ -307,7 +322,7 @@
 
         return put
 
-    blocked_scan(count, width, pow_ref, ma_ref, mb_ref, load(2 * width), load(0), store(0), store(2 * width))
+    blocked_scan(count, width, pow_ref, starts_ref, lengths_ref, load(2 * width), load(0), store(0), store(2 * width))
 
     rows = 16
 
@@ -352,23 +367,24 @@
         sums_ref[k : k + 1, :] = jnp.sum(value, 0, keepdims=True)
 
 
-def adjoint(ma, mb, powers, coef, masks, states_grad, states, drive):
+def adjoint(starts, lengths, powers, coef, masks, states_grad, states, drive):
     count, quad = states_grad.shape
     width = quad // 4
     vmem = pl.BlockSpec(memory_space=pltpu.VMEM)
+    smem = pl.BlockSpec(memory_space=pltpu.SMEM)
     return pl.pallas_call(
         adjoint_kernel,
         out_shape=(
             jax.ShapeDtypeStruct((count, 2 * width), jnp.bfloat16),
             jax.ShapeDtypeStruct((4, width), jnp.float32),
         ),
-        in_specs=[vmem] * 8,
+        in_specs=[smem, smem] + [vmem] * 6,
         out_specs=(vmem, vmem),
         scratch_shapes=[pltpu.VMEM((count + 16, 4 * width), jnp.float32)],
         cost_estimate=pl.CostEstimate(
             flops=60 * count * width, transcendentals=0, bytes_accessed=48 * count * width
         ),
-    )(ma, mb, powers, coef, masks, states_grad, states, drive)
+    )(starts, lengths, powers, coef, masks, states_grad, states, drive)
 
 
 def update(weight, gradient, velocity, average, rate, decay):
@@ -433,11 +449,6 @@
     before_prev = jnp.concatenate([carry_prev[1:], zero])
     mask_columns = jnp.stack([alive, carry_prev, carry_next, jnp.zeros_like(alive)], 1)
 
-    def lanes(mask):
-        return jnp.broadcast_to(mask[:, None], (count, 128))
-
-    keep_prev, keep_next = lanes(carry_prev), lanes(carry_next)
-    keep_after_next, keep_before_prev = lanes(after_next), lanes(before_prev)
 
     in_all = gather_feat(input_matrix.astype(jnp.bfloat16), 1)
     out_all = gather_feat(output_matrix.astype(jnp.bfloat16), 2)
@@ -468,7 +479,7 @@
             ],
             1,
         )
-        states = recurrence(keep_prev, keep_next, pole_powers(pole_re, pole_im), source)
+        states = recurrence(seq_start, seq_length, pole_powers(pole_re, pole_im), source)
         states_low = states.astype(jnp.bfloat16)
         mixed = (
             jnp.dot(states_low, out_low, preferred_element_type=jnp.float32)
@@ -503,8 +514,8 @@
         states_grad = contract_cols(mixed_low, out_low)
         coef = jnp.stack([pole_re, pole_im, factor_re, factor_im])
         drive_low, sums = adjoint(
-            keep_after_next,
-            keep_before_prev,
+            seq_start,
+            seq_length,
             pole_powers(pole_re, -pole_im),
             coef,
             mask_columns,

time: 279 us -> 277 us (level)
  local copies, waits for them, and re-layouts: 21.3 us -> 17.6 us
    broadcast_in_dim x4 -> x0, local copies, waits for them, and re-layouts: 3.65 us -> none  [lanes(): return jnp.broadcast_to(mask[:, None], (count, 128))]
where the time goes in v13:
time: 277 us; the launch traced here: 276 us
  Pallas kernels  110 us (40%)
  matrix products  55.8 us (20%)
  other arithmetic  34.7 us (13%)
  blocking collectives  28.8 us (10%)
  local copies, waits for them, and re-layouts  17.6 us (6%)
  between operations  15.3 us (6%)
  waiting for transfers between devices  14.5 us (5%)
    pallas_call x1, Pallas kernels, ring_sum(): pl.pallas_call(lambda *refs: ring_sum_kernel(n, *refs), out_shape=jax.Sha...  61.3 us
    pallas_call x2, Pallas kernels, adjoint(): pl.pallas_call(adjoint_kernel, out_shape=(jax.ShapeDtypeStruct((count, 2...  30.9 us
    all_gather x3, blocking collectives, gather_feat(): return lax.all_gather(value, 'feat', axis=axis, tiled=True)  28.8 us
    pallas_call x2, Pallas kernels, recurrence(): pl.pallas_call(recurrence_kernel, out_shape=jax.ShapeDtypeStruct((count,...  17.4 us
    dot_general x4, matrix products, contract_cols(): lax.dot_general(left, right, (((1,), (1,)), ((), ())), preferred_element_...  17.2 us
    dot_general x2, matrix products, body(): jnp.dot(states_low, out_low, preferred_element_type=jnp.float32)  15.9 us
    all_gather x3, waiting for transfers between devices, gather_feat(): return lax.all_gather(value, 'feat', axis=axis, tiled=True)  14.5 us
    unnamed x236, local copies, waits for them, and re-layouts  11.4 us
  transfers between devices with their start and end apart: 3, of which 2 were waited for; matrix products, arithmetic and copies ran while one was open for 9% of the time, Pallas kernels for 3%

profile of v13, /device:TPU:0, one launch (start us, length us, event | category | flops | bytes accessed | tf_op | source)
XLA Modules:
  0.0 276.5 jit_solution(17907902799515568058)
XLA Ops:
  7.2 2.0 convert_element_type.100
  9.4 1.0 convert_element_type.103
  12.1 6.1 %all_gather.19 = f32[2,4,512]{2,1,0:T(4,128)S(1)} all-gather(f32[2,4,128]{2,1,0:T(4,128)S(1)} %copy-done.68), channel_id=1, replica_groups=mesh['seq'=8,'feat'=4] {'feat'}, dimensions={2}, use_global_device_ids=true | all-gather | bytes 20480 | tf_op jit(solution)/shard_map/all_gather | solution.py:412
  20.1 1.2 rev.30
  21.9 0.9 copy.86.masks_ref
  22.8 13.3 %all_gather.18 = bf16[768,512]{1,0:T(8,128)(2,1)S(1)} all-gather(bf16[768,128]{1,0:T(8,128)(2,1)S(1)} %copy-done.33), channel_id=1, replica_groups=mesh['seq'=8,'feat'=4] {'feat'}, dimensions={1}, use_global_device_ids=true | all-gather | bytes 983040 | tf_op jit(solution)/shard_map/all_gather | solution.py:412
  36.8 9.4 %all_gather.23 = bf16[768,512]{1,0:T(8,128)(2,1)} all-gather(bf16[768,128]{1,0:T(8,128)(2,1)S(1)} %copy-done.34), channel_id=1, replica_groups=mesh['seq'=8,'feat'=4] {'feat'}, dimensions={1}, use_global_device_ids=true | all-gather | bytes 983040 | tf_op jit(solution)/shard_map/all_gather | solution.py:412
  46.8 1.2 fusion.17
  50.0 2.2 fusion.23.drive_ref
  52.5 1.0 copy-done
  53.5 1.6 pad_maximum_fusion.x_ref
  55.1 8.7 %shard_map.354.states_ref = f32[768,1536]{1,0:T(8,128)} custom-call(s32[2]{0:T(128)} %starts_ref.7, s32[2]{0:T(128)} %lengths_ref.7, f32[4,8,384]{2,1,0:T(8,128)} %pad_maximum_fusion.5.pow_ref, f32[768,768]{1,0:T(8,128)} %pad_maximum_fusion.x_ref), custom_call_target="tpu_custom_call" | custom-call | flops 11796480 | bytes 9437184 | tf_op jit(solution)/shard_map/pallas_call | solution.py:144
  63.8 3.8 %all-gather.6.cloned.1.call-done = bf16[2,1536,512]{2,1,0:T(8,128)(2,1)} async-done(((bf16[2,1536,128]{2,1,0:T(8,128)(2,1)}), bf16[2,1536,512]{2,1,0:T(8,128)(2,1)}) %all-gather.6.cloned.1.call-update) | async-done | bytes 3145744 | tf_op jit(solution)/shard_map/all_gather | solution.py:412
  67.6 8.2 %multiply_multiply_fusion.11 = (f32[768,512]{1,0:T(8,128)S(1)}, f32[768,512]{1,0:T(8,128)}) fusion(f32[512]{0:T(512)S(1)} %bitcast.483, f32[512]{0:T(512)S(1)} %bitcast.486, f32[768]{0:T(1024)S(1)} %add_rsqrt_fusion.1, f32[768]{0:T(1024)S(1)} %broadcast_multiply_fusion.6, bf16[768,512]{1,0:T(8,128)(2,1)S(1)} %copy-done.5, f32[512]{0:T(512)S(1)} %bitcast.492, ...), kind=kOutput, calls=%fused_computation.74 | convolution fusion | flops 1237057536 | bytes 10235904 | tf_op jit(solution)/shard_map/dot_general | solution.py:485
  75.8 10.7 %all-gather.8.cloned.1.call-done = bf16[2,512,512]{2,1,0:T(8,128)(2,1)} async-done(((bf16[2,512,128]{2,1,0:T(8,128)(2,1)}), bf16[2,512,512]{2,1,0:T(8,128)(2,1)}) %all-gather.8.cloned.1.call-update) | async-done | bytes 1048592 | tf_op jit(solution)/shard_map/all_gather | solution.py:412
  86.6 3.0 %fusion.105 = (f32[768]{0:T(1024)S(1)}, f32[768,512]{1,0:T(8,128)S(1)}, f32[768,512]{1,0:T(8,128)}) fusion(f32[768,512]{1,0:T(8,128)S(1)} %get-tuple-element.295, bf16[768,512]{1,0:T(8,128)(2,1)S(1)} %copy-done.5, f32[512]{0:T(512)S(1)} %bitcast.497, bf16[2,512,512]{2,1,0:T(8,128)(2,1)} %all-gather.8.cloned.1.call-done), kind=kOutput, calls=%fused_computation.353 | convolution fusion | flops 406191360 | bytes 7607296 | tf_op jit(solution)/shard_map/dot_general | solution.py:490
  90.8 0.8 copy-done.21
  92.8 1.1 copy-done.1
  93.9 1.6 pad_maximum_fusion.1.x_ref
  95.5 8.7 %shard_map.355.states_ref = f32[768,1536]{1,0:T(8,128)} custom-call(s32[2]{0:T(128)} %starts_ref.7, s32[2]{0:T(128)} %lengths_ref.7, f32[4,8,384]{2,1,0:T(8,128)} %pad_maximum_fusion.6.pow_ref, f32[768,768]{1,0:T(8,128)} %pad_maximum_fusion.1.x_ref), custom_call_target="tpu_custom_call" | custom-call | flops 11796480 | bytes 9437184 | tf_op jit(solution)/shard_map/pallas_call | solution.py:144
  104.3 7.6 %multiply_multiply_fusion.10 = (f32[768,512]{1,0:T(8,128)S(1)}, f32[768,512]{1,0:T(8,128)S(1)}, f32[768,512]{1,0:T(8,128)S(1)}) fusion(f32[512]{0:T(512)S(1)} %bitcast.489, f32[512]{0:T(512)S(1)} %bitcast.476, f32[768]{0:T(1024)S(1)} %add_rsqrt_fusion, f32[768,512]{1,0:T(8,128)S(1)} %copy-done.3, f32[768]{0:T(1024)S(1)} %broadcast_multiply_fusion.5, ...), kind=kOutput, calls=%fused_computation.72 | convolution fusion | flops 1236664320 | bytes 12595200 | tf_op jit(solution)/shard_map/dot_general | solution.py:485
  112.0 1.6 convert_reduce_fusion.1
  113.6 1.1 convolution_bitcast_fusion.4
  114.7 0.9 dynamic-slice_add_fusion.1
  115.6 2.3 fusion.107
  118.0 1.7 convolution_bitcast_fusion
  120.0 3.6 %fusion.16.g_ref = f32[768,1536]{1,0:T(8,128)} fusion(bf16[768,512]{1,0:T(8,128)(2,1)S(1)} %get-tuple-element.300, bf16[2,1536,512]{2,1,0:T(8,128)(2,1)S(1)} %copy-done.107), kind=kOutput, calls=%fused_computation.76 | convolution fusion | flops 1207959552 | bytes 7077888 | tf_op jit(solution)/shard_map/dot_general | solution.py:406
  123.7 15.5 %shard_map.356 = (bf16[768,768]{1,0:T(8,128)(2,1)}, f32[4,384]{1,0:T(4,128)}) custom-call(s32[2]{0:T(128)} %starts_ref.7, s32[2]{0:T(128)} %lengths_ref.7, f32[4,8,384]{2,1,0:T(8,128)} %pad_maximum_fusion.7.pow_ref, f32[4,384]{1,0:T(4,128)} %pad_maximum_fusion.10.coef_ref, f32[768,4]{1,0:T(8,128)} %copy.86.masks_ref, f32[768,1536]{1,0:T(8,128)} %fusion.16.g_ref, ...), custom_call_target="tpu_custom_call" | custom-call | flops 17694720 | bytes 14155776 | tf_op jit(solution)/shard_map/pallas_call | solution.py:375
  139.2 1.8 convolution_bitcast_fusion.2
  141.1 3.9 %multiply_reduce_fusion.1 = (f32[512]{0:T(512)}, f32[768]{0:T(1024)S(1)}, f32[512]{0:T(512)}, f32[768]{0:T(1024)S(1)}, f32[512]{0:T(512)}, /*index=5*/f32[768,512]{1,0:T(8,128)S(1)}) fusion(f32[768]{0:T(1024)S(1)} %copy-done.58, f32[768,512]{1,0:T(8,128)S(1)} %copy-done.3, f32[768]{0:T(1024)S(1)} %copy-done.50, f32[512]{0:T(512)S(1)} %bitcast.477, ...), kind=kOutput, calls=%fused_computation.25 | convolution fusion | flops 609874944 | bytes 6711296 | tf_op jit(solution)/shard_map/dot_general | solution.py:529
  145.0 2.7 convert_reduce_fusion.2
  147.8 1.1 convolution_bitcast_fusion.5
  150.5 1.2 rev.31
  151.7 7.6 %fusion.108 = (bf16[768,512]{1,0:T(8,128)(2,1)S(1)}, f32[768,512]{1,0:T(8,128)}) fusion(f32[768,512]{1,0:T(8,128)} %get-tuple-element.296, bf16[768,512]{1,0:T(8,128)(2,1)} %copy-done.25, bf16[2,512,512]{2,1,0:T(8,128)(2,1)} %all-gather.8.cloned.1.call-done, f32[768,512]{1,0:T(8,128)S(1)} %copy-done.17, f32[768,512]{1,0:T(8,128)} %get-tuple-element.297), kind=kOutput, calls=%fused_computation.356 | convolution fusion | flops 431751168 | bytes 8388608 | tf_op jit(solution)/shard_map/dot_general | solution.py:406
  161.5 3.6 %fusion.15.g_ref = f32[768,1536]{1,0:T(8,128)} fusion(bf16[768,512]{1,0:T(8,128)(2,1)S(1)} %get-tuple-element.303, bf16[2,1536,512]{2,1,0:T(8,128)(2,1)S(1)} %copy-done.108), kind=kOutput, calls=%fused_computation.75 | convolution fusion | flops 1207959552 | bytes 7077888 | tf_op jit(solution)/shard_map/dot_general | solution.py:406
  165.1 15.4 %shard_map.357 = (bf16[768,768]{1,0:T(8,128)(2,1)}, f32[4,384]{1,0:T(4,128)}) custom-call(s32[2]{0:T(128)} %starts_ref.7, s32[2]{0:T(128)} %lengths_ref.7, f32[4,8,384]{2,1,0:T(8,128)} %pad_maximum_fusion.8.pow_ref, f32[4,384]{1,0:T(4,128)} %pad_maximum_fusion.11.coef_ref, f32[768,4]{1,0:T(8,128)} %copy.86.masks_ref, f32[768,1536]{1,0:T(8,128)} %fusion.15.g_ref, ...), custom_call_target="tpu_custom_call" | custom-call | flops 17694720 | bytes 14155776 | tf_op jit(solution)/shard_map/pallas_call | solution.py:375
  180.5 1.7 convolution_bitcast_fusion.3
  183.4 0.9 copy-done.28
  186.3 2.9 %fusion.88 = (f32[512]{0:T(512)S(1)}, f32[512]{0:T(512)S(1)}, f32[512]{0:T(512)S(1)}, f32[768]{0:T(1024)S(1)}, f32[768]{0:T(1024)S(1)}, /*index=5*/f32[768,512]{1,0:T(8,128)}, f32[768,512]{1,0:T(8,128)}) fusion(f32[768]{0:T(1024)S(1)} %copy-done.54, f32[768]{0:T(1024)S(1)} %copy-done.56, bf16[768,512]{1,0:T(8,128)(2,1)S(1)} %copy-done.5, ...), kind=kOutput, calls=%fused_computation.347 | convolution fusion | flops 610268160 | bytes 7497728 | tf_op jit(solution)/shard_map/dot_general | solution.py:529
  189.4 1.8 pad_bitcast_fusion.refs_0_
  191.2 61.3 %shard_map.358 = bf16[5888,128]{1,0:T(8,128)(2,1)} custom-call(f32[5888,128]{1,0:T(8,128)} %pad_bitcast_fusion.refs_0_), custom_call_target="tpu_custom_call" | custom-call | tf_op jit(solution)/shard_map/pallas_call | solution.py:267
  252.6 1.6 convert_element_type.122
  254.2 0.8 slice_multiply_fusion.2
  258.7 3.0 %add_multiply_fusion.4 = (f32[2,512,128]{2,1,0:T(8,128)}, f32[2,512,128]{2,1,0:T(8,128)}, f32[2,512,128]{2,1,0:T(8,128)}) fusion(f32[2,512,128]{2,1,0:T(8,128)} %param.35, f32[2,512,128]{2,1,0:T(8,128)} %param.25, f32[2,512,128]{2,1,0:T(8,128)} %bitcast.456, f32[2,512,128]{2,1,0:T(8,128)} %param.30), kind=kLoop, calls=%fused_computation.107 | loop fusion | flops 1310720 | bytes 3670016 | tf_op jit(solution)/shard_map/add | solution.py:395
  261.7 1.7 add_multiply_fusion.3
  263.5 0.9 copy-done.19
  264.9 2.7 add_multiply_fusion
  267.6 2.4 dynamic-slice_add_fusion
  (318 shorter events, 21.1 us)
Async XLA Ops:
  7.2 42.8 %all-gather.4.cloned.1.call-start = ((), (), s32[]{:S(2)}) async-start(), calls=%async_computation | async-start | bytes 1966080 | tf_op jit(solution)/shard_map/all_gather | solution.py:412
  9.4 2.8 %copy-start.68 = (f32[2,4,128]{2,1,0:T(4,128)S(1)}, f32[2,4,128]{2,1,0:T(4,128)}, u32[]{:S(2)}) copy-start(f32[2,4,128]{2,1,0:T(4,128)} %param.26) | copy-start | bytes 12292
  9.4 58.2 %all-gather.6.cloned.1.call-start = ((), (), s32[]{:S(2)}) async-start(), calls=%async_computation.1 | async-start | bytes 3932160 | tf_op jit(solution)/shard_map/all_gather | solution.py:412
  10.4 12.4 %copy-start.33 = (bf16[768,128]{1,0:T(8,128)(2,1)S(1)}, bf16[768,128]{1,0:T(8,128)(2,1)}, u32[]{:S(2)}) copy-start(bf16[768,128]{1,0:T(8,128)(2,1)} %param.19) | copy-start | bytes 589828
  10.4 76.1 %all-gather.8.cloned.1.call-start = ((), (), s32[]{:S(2)}) async-start(), calls=%async_computation.2 | async-start | bytes 1310720 | tf_op jit(solution)/shard_map/all_gather | solution.py:412
  11.9 9.7 %copy-start.59 = (f32[1,384]{1,0:T(1,128)}, f32[1,384]{1,0:T(1,128)S(1)}, u32[]{:S(2)}) copy-start(f32[1,384]{1,0:T(1,128)S(1)} %get-tuple-element.183) | copy-start | bytes 4612
  11.9 34.3 %copy-start.35 = (f32[1,384]{1,0:T(1,128)}, f32[1,384]{1,0:T(1,128)S(1)}, u32[]{:S(2)}) copy-start(f32[1,384]{1,0:T(1,128)S(1)} %get-tuple-element.184) | copy-start | bytes 4612
  11.9 34.3 %copy-start.43 = (f32[1,384]{1,0:T(1,128)}, f32[1,384]{1,0:T(1,128)S(1)}, u32[]{:S(2)}) copy-start(f32[1,384]{1,0:T(1,128)S(1)} %get-tuple-element.185) | copy-start | bytes 4612
  18.3 49.3 %copy-start.77 = (f32[1,1,512]{2,1,0:T(1,128)}, f32[1,1,512]{2,1,0:T(1,128)S(1)}, u32[]{:S(2)}) copy-start(f32[1,1,512]{2,1,0:T(1,128)S(1)} %get-tuple-element.247) | copy-start | bytes 6148
  18.3 49.3 %copy-start.79 = (f32[1,1,512]{2,1,0:T(1,128)}, f32[1,1,512]{2,1,0:T(1,128)S(1)}, u32[]{:S(2)}) copy-start(f32[1,1,512]{2,1,0:T(1,128)S(1)} %get-tuple-element.248) | copy-start | bytes 6148
  18.3 49.3 %copy-start.99 = (f32[1,1,512]{2,1,0:T(1,128)}, f32[1,1,512]{2,1,0:T(1,128)S(1)}, u32[]{:S(2)}) copy-start(f32[1,1,512]{2,1,0:T(1,128)S(1)} %get-tuple-element.246) | copy-start | bytes 6148
  18.3 86.0 %copy-start.65 = (f32[1,1,512]{2,1,0:T(1,128)}, f32[1,1,512]{2,1,0:T(1,128)S(1)}, u32[]{:S(2)}) copy-start(f32[1,1,512]{2,1,0:T(1,128)S(1)} %get-tuple-element.244) | copy-start | bytes 6148
  18.3 85.9 %copy-start.81 = (f32[1,1,512]{2,1,0:T(1,128)}, f32[1,1,512]{2,1,0:T(1,128)S(1)}, u32[]{:S(2)}) copy-start(f32[1,1,512]{2,1,0:T(1,128)S(1)} %get-tuple-element.243) | copy-start | bytes 6148
  18.3 85.9 %copy-start.101 = (f32[1,1,512]{2,1,0:T(1,128)}, f32[1,1,512]{2,1,0:T(1,128)S(1)}, u32[]{:S(2)}) copy-start(f32[1,1,512]{2,1,0:T(1,128)S(1)} %get-tuple-element.241) | copy-start | bytes 6148
  19.0 2.8 %copy-start.37 = (f32[1,384]{1,0:T(1,128)}, f32[1,384]{1,0:T(1,128)S(1)}, u32[]{:S(2)}) copy-start(f32[1,384]{1,0:T(1,128)S(1)} %get-tuple-element.255) | copy-start | bytes 4612
  21.4 15.3 %copy-start.34 = (bf16[768,128]{1,0:T(8,128)(2,1)S(1)}, bf16[768,128]{1,0:T(8,128)(2,1)}, u32[]{:S(2)}) copy-start(bf16[768,128]{1,0:T(8,128)(2,1)} %param.20) | copy-start | bytes 589828
  36.2 11.8 %copy-start.4 = (bf16[768,512]{1,0:T(8,128)(2,1)}, bf16[768,512]{1,0:T(8,128)(2,1)S(1)}, u32[]{:S(2)}) copy-start(bf16[768,512]{1,0:T(8,128)(2,1)S(1)} %all_gather.18) | copy-start | bytes 2359300
  36.4 31.2 %copy-start.55 = (f32[768]{0:T(1024)}, f32[768]{0:T(1024)S(1)}, u32[]{:S(2)}) copy-start(f32[768]{0:T(1024)S(1)} %broadcast_multiply_fusion.6) | copy-start | bytes 9220
  36.8 30.8 %copy-start.53 = (f32[768]{0:T(1024)}, f32[768]{0:T(1024)S(1)}, u32[]{:S(2)}) copy-start(f32[768]{0:T(1024)S(1)} %add_rsqrt_fusion.1) | copy-start | bytes 9220
  55.1 12.5 %copy-start.5 = (bf16[768,512]{1,0:T(8,128)(2,1)S(1)}, bf16[768,512]{1,0:T(8,128)(2,1)}, u32[]{:S(2)}) copy-start(bf16[768,512]{1,0:T(8,128)(2,1)} %copy-done.4) | copy-start | bytes 2359300
  75.8 13.8 %copy-start.10 = (f32[768,512]{1,0:T(8,128)}, f32[768,512]{1,0:T(8,128)S(1)}, u32[]{:S(2)}) copy-start(f32[768,512]{1,0:T(8,128)S(1)} %get-tuple-element.295) | copy-start | bytes 4718596
  89.6 14.7 %copy-start.49 = (f32[768]{0:T(1024)}, f32[768]{0:T(1024)S(1)}, u32[]{:S(2)}) copy-start(f32[768]{0:T(1024)S(1)} %broadcast_multiply_fusion.5) | copy-start | bytes 9220
  90.0 14.3 %copy-start.57 = (f32[768]{0:T(1024)}, f32[768]{0:T(1024)S(1)}, u32[]{:S(2)}) copy-start(f32[768]{0:T(1024)S(1)} %add_rsqrt_fusion) | copy-start | bytes 9220
  95.5 8.8 %copy-start.3 = (f32[768,512]{1,0:T(8,128)S(1)}, f32[768,512]{1,0:T(8,128)}, u32[]{:S(2)}) copy-start(f32[768,512]{1,0:T(8,128)} %copy-done.2) | copy-start | bytes 4718596
  104.3 7.7 %copy-start.6 = (bf16[768,512]{1,0:T(8,128)(2,1)S(1)}, bf16[768,512]{1,0:T(8,128)(2,1)}, u32[]{:S(2)}) copy-start(bf16[768,512]{1,0:T(8,128)(2,1)} %all_gather.23) | copy-start | bytes 2359300
  104.3 7.7 %copy-start.32 = (bf16[2,512,512]{2,1,0:T(8,128)(2,1)S(1)}, bf16[2,512,512]{2,1,0:T(8,128)(2,1)}, u32[]{:S(2)}) copy-start(bf16[2,512,512]{2,1,0:T(8,128)(2,1)} %all-gather.8.cloned.1.call-done) | copy-start | bytes 3145732
  114.7 3.2 %slice-start.2 = ((s8[4718592]{0:T(1024)(128)(4,1)}), s8[4194304]{0:T(1024)(128)(4,1)S(1)}, s32[]{:S(2)}) async-start(s8[4718592]{0:T(1024)(128)(4,1)} %bitcast.451), calls=%async_computation.5 | async-start | bytes 8388608
  141.1 3.9 %copy-start.7 = (bf16[768,512]{1,0:T(8,128)(2,1)S(1)}, bf16[768,512]{1,0:T(8,128)(2,1)}, u32[]{:S(2)}) copy-start(bf16[768,512]{1,0:T(8,128)(2,1)} %all_gather.23) | copy-start | bytes 2359300
  141.1 3.9 %copy-start.11 = (f32[768,512]{1,0:T(8,128)S(1)}, f32[768,512]{1,0:T(8,128)}, u32[]{:S(2)}) copy-start(f32[768,512]{1,0:T(8,128)} %copy-done.10) | copy-start | bytes 4718596
  141.1 3.9 %copy-start.24 = (f32[768,512]{1,0:T(8,128)S(1)}, f32[768,512]{1,0:T(8,128)}, u32[]{:S(2)}) copy-start(f32[768,512]{1,0:T(8,128)} %get-tuple-element.297) | copy-start | bytes 4718596
  145.0 14.3 %slice-start = ((s8[4718592]{0:T(1024)(128)(4,1)}), s8[524288]{0:T(1024)(128)(4,1)S(1)}, s32[]{:S(2)}) async-start(s8[4718592]{0:T(1024)(128)(4,1)} %bitcast.449), calls=%async_computation.3 | async-start | bytes 1048576
  147.8 2.6 copy-start.87
  147.8 2.6 copy-start.88
  147.8 3.9 %copy-start.17 = (f32[768,512]{1,0:T(8,128)S(1)}, f32[768,512]{1,0:T(8,128)}, u32[]{:S(2)}) copy-start(f32[768,512]{1,0:T(8,128)} %get-tuple-element.159) | copy-start | bytes 4718596
  150.5 8.9 %copy-start.41 = (f32[8,384]{1,0:T(8,128)}, f32[8,384]{1,0:T(8,128)S(1)}, u32[]{:S(2)}) copy-start(f32[8,384]{1,0:T(8,128)S(1)} %stack.268) | copy-start | bytes 36868
  151.7 7.6 %slice-start.1 = ((s8[4718592]{0:T(1024)(128)(4,1)}), s8[4194304]{0:T(1024)(128)(4,1)S(1)}, s32[]{:S(2)}) async-start(s8[4718592]{0:T(1024)(128)(4,1)} %bitcast.449), calls=%async_computation.4 | async-start | bytes 8388608
  186.3 2.9 %copy-start.83 = (f32[512]{0:T(512)S(1)}, f32[512]{0:T(512)}, u32[]{:S(2)}) copy-start(f32[512]{0:T(512)} %get-tuple-element.157) | copy-start | bytes 6148
  254.2 3.8 %copy-start.70 = (f32[8,128]{1,0:T(8,128)}, f32[8,128]{1,0:T(8,128)S(1)}, u32[]{:S(2)}) copy-start(f32[8,128]{1,0:T(8,128)S(1)} %slice_multiply_fusion.4) | copy-start | bytes 12292
  255.3 8.1 %copy-start.12 = (f32[3072,128]{1,0:T(8,128)}, f32[3072,128]{1,0:T(8,128)S(1)}, u32[]{:S(2)}) copy-start(f32[3072,128]{1,0:T(8,128)S(1)} %slice_multiply_fusion) | copy-start | bytes 4718596
  255.3 2.7 copy-start.69
  255.3 2.7 copy-start.97
  255.3 2.7 copy-start.98
  257.9 3.7 %copy-start.15 = (f32[2,128,768]{2,1,0:T(8,128)}, f32[2,128,768]{2,1,0:T(8,128)S(1)}, u32[]{:S(2)}) copy-start(f32[2,128,768]{2,1,0:T(8,128)S(1)} %mul.6070) | copy-start | bytes 2359300
  258.7 3.0 %copy-start.14 = (f32[2,128,768]{2,1,0:T(8,128)S(1)}, f32[2,128,768]{2,1,0:T(8,128)}, u32[]{:S(2)}) copy-start(f32[2,128,768]{2,1,0:T(8,128)} %param.23) | copy-start | bytes 2359300
  258.7 3.0 %copy-start.29 = (f32[2,128,768]{2,1,0:T(8,128)S(1)}, f32[2,128,768]{2,1,0:T(8,128)}, u32[]{:S(2)}) copy-start(f32[2,128,768]{2,1,0:T(8,128)} %param.33) | copy-start | bytes 2359300
  258.7 3.0 %copy-start.30 = (f32[2,128,768]{2,1,0:T(8,128)S(1)}, f32[2,128,768]{2,1,0:T(8,128)}, u32[]{:S(2)}) copy-start(f32[2,128,768]{2,1,0:T(8,128)} %param.28) | copy-start | bytes 2359300
  261.7 2.7 copy-start.19
  261.7 3.2 %copy-start.20 = (f32[2,1536,128]{2,1,0:T(8,128)S(1)}, f32[2,1536,128]{2,1,0:T(8,128)}, u32[]{:S(2)}) copy-start(f32[2,1536,128]{2,1,0:T(8,128)} %param.29) | copy-start | bytes 4718596
  (69 other events, 100.3 us)
Sparse Core Ops, SparseCore 0:
  10.2 26.5 all-gather.3
  38.9 28.6 all-gather.5
  69.7 16.8 all-gather.7

commit v14 on v13

--- a/solution.py
+++ b/solution.py
@@ -290,11 +290,11 @@
     grain = 2 * n * 16 * 128
     padded = -(-flat.size // grain) * grain
     flat = jnp.pad(flat, (0, padded - flat.size)).reshape(padded // 128, 128)
-    total = ring_sum(flat, n).astype(jnp.float32).reshape(-1)
+    total = ring_sum(flat, n).reshape(-1)
     pieces = []
     start = 0
     for part in parts:
-        pieces.append(total[start : start + part.size].reshape(part.shape))
+        pieces.append(total[start : start + part.size].reshape(part.shape).astype(jnp.float32))
         start += part.size
     return pieces
 

time: 277 us -> 279 us (level)
    unnamed x236 -> x238, local copies, waits for them, and re-layouts: 11.4 us -> 11.5 us
  transfers between devices with their start and end apart: 3 -> 3, of which waited for: 2 -> 2; matrix products, arithmetic and copies ran while one was open for 9% -> 8% of each run, Pallas kernels for 3% -> 3%
where the time goes in v14:
time: 279 us; the launch traced here: 278 us
  Pallas kernels  109 us (39%)
  matrix products  55.9 us (20%)
  other arithmetic  36.5 us (13%)
  blocking collectives  28.8 us (10%)
  local copies, waits for them, and re-layouts  17.7 us (6%)
  between operations  15.3 us (5%)
  waiting for transfers between devices  14.5 us (5%)
    pallas_call x1, Pallas kernels, ring_sum(): pl.pallas_call(lambda *refs: ring_sum_kernel(n, *refs), out_shape=jax.Sha...  61.2 us
    pallas_call x2, Pallas kernels, adjoint(): pl.pallas_call(adjoint_kernel, out_shape=(jax.ShapeDtypeStruct((count, 2...  30.9 us
    all_gather x3, blocking collectives, gather_feat(): return lax.all_gather(value, 'feat', axis=axis, tiled=True)  28.8 us
    pallas_call x2, Pallas kernels, recurrence(): pl.pallas_call(recurrence_kernel, out_shape=jax.ShapeDtypeStruct((count,...  17.4 us
    dot_general x4, matrix products, contract_cols(): lax.dot_general(left, right, (((1,), (1,)), ((), ())), preferred_element_...  17.2 us
    dot_general x2, matrix products, body(): jnp.dot(states_low, out_low, preferred_element_type=jnp.float32)  15.9 us
    all_gather x3, waiting for transfers between devices, gather_feat(): return lax.all_gather(value, 'feat', axis=axis, tiled=True)  14.5 us
    unnamed x238, local copies, waits for them, and re-layouts  11.5 us
  transfers between devices with their start and end apart: 3, of which 2 were waited for; matrix products, arithmetic and copies ran while one was open for 8% of the time, Pallas kernels for 3%

profile of v14, /device:TPU:0, one launch (start us, length us, event | category | flops | bytes accessed | tf_op | source)
XLA Modules:
  0.0 278.3 jit_solution(16608000892196876901)
XLA Ops:
  7.2 2.0 convert_element_type.117
  9.4 1.0 convert_element_type.120
  12.1 6.1 %all_gather.19 = f32[2,4,512]{2,1,0:T(4,128)S(1)} all-gather(f32[2,4,128]{2,1,0:T(4,128)S(1)} %copy-done.69), channel_id=1, replica_groups=mesh['seq'=8,'feat'=4] {'feat'}, dimensions={2}, use_global_device_ids=true | all-gather | bytes 20480 | tf_op jit(solution)/shard_map/all_gather | solution.py:412
  20.1 1.2 rev.30
  21.9 0.9 copy.86.masks_ref
  22.8 13.3 %all_gather.18 = bf16[768,512]{1,0:T(8,128)(2,1)S(1)} all-gather(bf16[768,128]{1,0:T(8,128)(2,1)S(1)} %copy-done.34), channel_id=1, replica_groups=mesh['seq'=8,'feat'=4] {'feat'}, dimensions={1}, use_global_device_ids=true | all-gather | bytes 983040 | tf_op jit(solution)/shard_map/all_gather | solution.py:412
  36.8 9.4 %all_gather.23 = bf16[768,512]{1,0:T(8,128)(2,1)} all-gather(bf16[768,128]{1,0:T(8,128)(2,1)S(1)} %copy-done.35), channel_id=1, replica_groups=mesh['seq'=8,'feat'=4] {'feat'}, dimensions={1}, use_global_device_ids=true | all-gather | bytes 983040 | tf_op jit(solution)/shard_map/all_gather | solution.py:412
  46.8 1.2 fusion.17
  50.0 2.2 fusion.23.drive_ref
  52.5 1.0 copy-done
  53.5 1.6 pad_maximum_fusion.x_ref
  55.1 8.7 %shard_map.354.states_ref = f32[768,1536]{1,0:T(8,128)} custom-call(s32[2]{0:T(128)} %starts_ref.7, s32[2]{0:T(128)} %lengths_ref.7, f32[4,8,384]{2,1,0:T(8,128)} %pad_maximum_fusion.5.pow_ref, f32[768,768]{1,0:T(8,128)} %pad_maximum_fusion.x_ref), custom_call_target="tpu_custom_call" | custom-call | flops 11796480 | bytes 9437184 | tf_op jit(solution)/shard_map/pallas_call | solution.py:144
  63.8 3.8 %all-gather.6.cloned.1.call-done = bf16[2,1536,512]{2,1,0:T(8,128)(2,1)} async-done(((bf16[2,1536,128]{2,1,0:T(8,128)(2,1)}), bf16[2,1536,512]{2,1,0:T(8,128)(2,1)}) %all-gather.6.cloned.1.call-update) | async-done | bytes 3145744 | tf_op jit(solution)/shard_map/all_gather | solution.py:412
  67.6 8.2 %multiply_multiply_fusion.11 = (f32[768,512]{1,0:T(8,128)S(1)}, f32[768,512]{1,0:T(8,128)}) fusion(f32[512]{0:T(512)S(1)} %bitcast.483, f32[512]{0:T(512)S(1)} %bitcast.486, f32[768]{0:T(1024)S(1)} %add_rsqrt_fusion.1, f32[768]{0:T(1024)S(1)} %broadcast_multiply_fusion.6, bf16[768,512]{1,0:T(8,128)(2,1)S(1)} %copy-done.5, f32[512]{0:T(512)S(1)} %bitcast.492, ...), kind=kOutput, calls=%fused_computation.74 | convolution fusion | flops 1237057536 | bytes 10235904 | tf_op jit(solution)/shard_map/dot_general | solution.py:485
  75.8 10.7 %all-gather.8.cloned.1.call-done = bf16[2,512,512]{2,1,0:T(8,128)(2,1)} async-done(((bf16[2,512,128]{2,1,0:T(8,128)(2,1)}), bf16[2,512,512]{2,1,0:T(8,128)(2,1)}) %all-gather.8.cloned.1.call-update) | async-done | bytes 1048592 | tf_op jit(solution)/shard_map/all_gather | solution.py:412
  86.6 3.0 %fusion.105 = (f32[768]{0:T(1024)S(1)}, f32[768,512]{1,0:T(8,128)S(1)}, f32[768,512]{1,0:T(8,128)}) fusion(f32[768,512]{1,0:T(8,128)S(1)} %get-tuple-element.295, bf16[768,512]{1,0:T(8,128)(2,1)S(1)} %copy-done.5, f32[512]{0:T(512)S(1)} %bitcast.497, bf16[2,512,512]{2,1,0:T(8,128)(2,1)} %all-gather.8.cloned.1.call-done), kind=kOutput, calls=%fused_computation.353 | convolution fusion | flops 406191360 | bytes 7607296 | tf_op jit(solution)/shard_map/dot_general | solution.py:490
  90.8 0.8 copy-done.22
  92.8 1.1 copy-done.1
  93.9 1.6 pad_maximum_fusion.1.x_ref
  95.5 8.7 %shard_map.355.states_ref = f32[768,1536]{1,0:T(8,128)} custom-call(s32[2]{0:T(128)} %starts_ref.7, s32[2]{0:T(128)} %lengths_ref.7, f32[4,8,384]{2,1,0:T(8,128)} %pad_maximum_fusion.6.pow_ref, f32[768,768]{1,0:T(8,128)} %pad_maximum_fusion.1.x_ref), custom_call_target="tpu_custom_call" | custom-call | flops 11796480 | bytes 9437184 | tf_op jit(solution)/shard_map/pallas_call | solution.py:144
  104.3 7.6 %multiply_multiply_fusion.10 = (f32[768,512]{1,0:T(8,128)S(1)}, f32[768,512]{1,0:T(8,128)S(1)}, f32[768,512]{1,0:T(8,128)S(1)}) fusion(f32[512]{0:T(512)S(1)} %bitcast.489, f32[512]{0:T(512)S(1)} %bitcast.476, f32[768]{0:T(1024)S(1)} %add_rsqrt_fusion, f32[768,512]{1,0:T(8,128)S(1)} %copy-done.3, f32[768]{0:T(1024)S(1)} %broadcast_multiply_fusion.5, ...), kind=kOutput, calls=%fused_computation.72 | convolution fusion | flops 1236664320 | bytes 12595200 | tf_op jit(solution)/shard_map/dot_general | solution.py:485
  112.0 1.6 convert_reduce_fusion.1
  113.6 1.1 convolution_bitcast_fusion.4
  114.8 0.9 dynamic-slice_add_fusion.1
  115.7 2.3 fusion.107
  118.0 1.7 convolution_bitcast_fusion
  120.0 3.6 %fusion.16.g_ref = f32[768,1536]{1,0:T(8,128)} fusion(bf16[768,512]{1,0:T(8,128)(2,1)S(1)} %get-tuple-element.300, bf16[2,1536,512]{2,1,0:T(8,128)(2,1)S(1)} %copy-done.108), kind=kOutput, calls=%fused_computation.76 | convolution fusion | flops 1207959552 | bytes 7077888 | tf_op jit(solution)/shard_map/dot_general | solution.py:406
  123.7 15.5 %shard_map.356 = (bf16[768,768]{1,0:T(8,128)(2,1)}, f32[4,384]{1,0:T(4,128)}) custom-call(s32[2]{0:T(128)} %starts_ref.7, s32[2]{0:T(128)} %lengths_ref.7, f32[4,8,384]{2,1,0:T(8,128)} %pad_maximum_fusion.7.pow_ref, f32[4,384]{1,0:T(4,128)} %pad_maximum_fusion.10.coef_ref, f32[768,4]{1,0:T(8,128)} %copy.86.masks_ref, f32[768,1536]{1,0:T(8,128)} %fusion.16.g_ref, ...), custom_call_target="tpu_custom_call" | custom-call | flops 17694720 | bytes 14155776 | tf_op jit(solution)/shard_map/pallas_call | solution.py:375
  139.2 1.8 convolution_bitcast_fusion.2
  141.1 3.9 %multiply_reduce_fusion.1 = (f32[512]{0:T(512)}, f32[768]{0:T(1024)S(1)}, f32[512]{0:T(512)}, f32[768]{0:T(1024)S(1)}, f32[512]{0:T(512)}, /*index=5*/f32[768,512]{1,0:T(8,128)S(1)}) fusion(f32[768]{0:T(1024)S(1)} %copy-done.59, f32[768,512]{1,0:T(8,128)S(1)} %copy-done.3, f32[768]{0:T(1024)S(1)} %copy-done.51, f32[512]{0:T(512)S(1)} %bitcast.477, ...), kind=kOutput, calls=%fused_computation.25 | convolution fusion | flops 609874944 | bytes 6711296 | tf_op jit(solution)/shard_map/dot_general | solution.py:529
  145.0 2.7 convert_reduce_fusion.2
  147.8 1.1 convolution_bitcast_fusion.5
  150.5 1.2 rev.31
  151.7 7.6 %fusion.108 = (bf16[768,512]{1,0:T(8,128)(2,1)S(1)}, f32[768,512]{1,0:T(8,128)}) fusion(f32[768,512]{1,0:T(8,128)} %get-tuple-element.296, bf16[768,512]{1,0:T(8,128)(2,1)} %copy-done.26, bf16[2,512,512]{2,1,0:T(8,128)(2,1)} %all-gather.8.cloned.1.call-done, f32[768,512]{1,0:T(8,128)S(1)} %copy-done.18, f32[768,512]{1,0:T(8,128)} %get-tuple-element.297), kind=kOutput, calls=%fused_computation.356 | convolution fusion | flops 431751168 | bytes 8388608 | tf_op jit(solution)/shard_map/dot_general | solution.py:406
  161.5 3.6 %fusion.15.g_ref = f32[768,1536]{1,0:T(8,128)} fusion(bf16[768,512]{1,0:T(8,128)(2,1)S(1)} %get-tuple-element.303, bf16[2,1536,512]{2,1,0:T(8,128)(2,1)S(1)} %copy-done.109), kind=kOutput, calls=%fused_computation.75 | convolution fusion | flops 1207959552 | bytes 7077888 | tf_op jit(solution)/shard_map/dot_general | solution.py:406
  165.2 15.4 %shard_map.357 = (bf16[768,768]{1,0:T(8,128)(2,1)}, f32[4,384]{1,0:T(4,128)}) custom-call(s32[2]{0:T(128)} %starts_ref.7, s32[2]{0:T(128)} %lengths_ref.7, f32[4,8,384]{2,1,0:T(8,128)} %pad_maximum_fusion.8.pow_ref, f32[4,384]{1,0:T(4,128)} %pad_maximum_fusion.11.coef_ref, f32[768,4]{1,0:T(8,128)} %copy.86.masks_ref, f32[768,1536]{1,0:T(8,128)} %fusion.15.g_ref, ...), custom_call_target="tpu_custom_call" | custom-call | flops 17694720 | bytes 14155776 | tf_op jit(solution)/shard_map/pallas_call | solution.py:375
  180.6 1.7 convolution_bitcast_fusion.3
  183.5 0.9 copy-done.29
  186.3 2.9 %fusion.88 = (f32[512]{0:T(512)S(1)}, f32[512]{0:T(512)S(1)}, f32[512]{0:T(512)S(1)}, f32[768]{0:T(1024)S(1)}, f32[768]{0:T(1024)S(1)}, /*index=5*/f32[768,512]{1,0:T(8,128)}, f32[768,512]{1,0:T(8,128)}) fusion(f32[768]{0:T(1024)S(1)} %copy-done.55, f32[768]{0:T(1024)S(1)} %copy-done.57, bf16[768,512]{1,0:T(8,128)(2,1)S(1)} %copy-done.5, ...), kind=kOutput, calls=%fused_computation.347 | convolution fusion | flops 610268160 | bytes 7497728 | tf_op jit(solution)/shard_map/dot_general | solution.py:529
  189.5 1.8 pad_bitcast_fusion.refs_0_
  191.3 61.2 %shard_map.358 = bf16[5888,128]{1,0:T(8,128)(2,1)} custom-call(f32[5888,128]{1,0:T(8,128)} %pad_bitcast_fusion.refs_0_), custom_call_target="tpu_custom_call" | custom-call | tf_op jit(solution)/shard_map/pallas_call | solution.py:267
  253.9 1.8 convert_multiply_fusion.3
  255.7 1.1 convert_multiply_fusion.2
  260.5 3.0 %add_multiply_fusion.4 = (f32[2,512,128]{2,1,0:T(8,128)}, f32[2,512,128]{2,1,0:T(8,128)}, f32[2,512,128]{2,1,0:T(8,128)}) fusion(f32[2,512,128]{2,1,0:T(8,128)} %param.35, f32[2,512,128]{2,1,0:T(8,128)} %param.25, f32[2,512,128]{2,1,0:T(8,128)} %bitcast.456, f32[2,512,128]{2,1,0:T(8,128)} %param.30), kind=kLoop, calls=%fused_computation.106 | loop fusion | flops 1310720 | bytes 3670016 | tf_op jit(solution)/shard_map/add | solution.py:395
  263.5 1.7 add_multiply_fusion.3
  265.3 0.9 copy-done.20
  266.7 2.7 add_multiply_fusion
  269.4 2.4 dynamic-slice_add_fusion
  (319 shorter events, 22.5 us)
Async XLA Ops:
  7.2 42.8 %all-gather.4.cloned.1.call-start = ((), (), s32[]{:S(2)}) async-start(), calls=%async_computation | async-start | bytes 1966080 | tf_op jit(solution)/shard_map/all_gather | solution.py:412
  9.4 2.8 copy-start.69
  9.4 58.2 %all-gather.6.cloned.1.call-start = ((), (), s32[]{:S(2)}) async-start(), calls=%async_computation.1 | async-start | bytes 3932160 | tf_op jit(solution)/shard_map/all_gather | solution.py:412
  10.4 12.4 %copy-start.34 = (bf16[768,128]{1,0:T(8,128)(2,1)S(1)}, bf16[768,128]{1,0:T(8,128)(2,1)}, u32[]{:S(2)}) copy-start(bf16[768,128]{1,0:T(8,128)(2,1)} %param.19) | copy-start | bytes 589828
  10.4 76.1 %all-gather.8.cloned.1.call-start = ((), (), s32[]{:S(2)}) async-start(), calls=%async_computation.2 | async-start | bytes 1310720 | tf_op jit(solution)/shard_map/all_gather | solution.py:412
  11.9 9.7 %copy-start.60 = (f32[1,384]{1,0:T(1,128)}, f32[1,384]{1,0:T(1,128)S(1)}, u32[]{:S(2)}) copy-start(f32[1,384]{1,0:T(1,128)S(1)} %get-tuple-element.183) | copy-start | bytes 4612
  11.9 34.3 %copy-start.36 = (f32[1,384]{1,0:T(1,128)}, f32[1,384]{1,0:T(1,128)S(1)}, u32[]{:S(2)}) copy-start(f32[1,384]{1,0:T(1,128)S(1)} %get-tuple-element.184) | copy-start | bytes 4612
  11.9 34.3 %copy-start.44 = (f32[1,384]{1,0:T(1,128)}, f32[1,384]{1,0:T(1,128)S(1)}, u32[]{:S(2)}) copy-start(f32[1,384]{1,0:T(1,128)S(1)} %get-tuple-element.185) | copy-start | bytes 4612
  18.3 49.3 %copy-start.78 = (f32[1,1,512]{2,1,0:T(1,128)}, f32[1,1,512]{2,1,0:T(1,128)S(1)}, u32[]{:S(2)}) copy-start(f32[1,1,512]{2,1,0:T(1,128)S(1)} %get-tuple-element.247) | copy-start | bytes 6148
  18.3 49.3 %copy-start.80 = (f32[1,1,512]{2,1,0:T(1,128)}, f32[1,1,512]{2,1,0:T(1,128)S(1)}, u32[]{:S(2)}) copy-start(f32[1,1,512]{2,1,0:T(1,128)S(1)} %get-tuple-element.248) | copy-start | bytes 6148
  18.3 49.3 %copy-start.100 = (f32[1,1,512]{2,1,0:T(1,128)}, f32[1,1,512]{2,1,0:T(1,128)S(1)}, u32[]{:S(2)}) copy-start(f32[1,1,512]{2,1,0:T(1,128)S(1)} %get-tuple-element.246) | copy-start | bytes 6148
  18.3 86.0 %copy-start.66 = (f32[1,1,512]{2,1,0:T(1,128)}, f32[1,1,512]{2,1,0:T(1,128)S(1)}, u32[]{:S(2)}) copy-start(f32[1,1,512]{2,1,0:T(1,128)S(1)} %get-tuple-element.244) | copy-start | bytes 6148
  18.3 86.0 %copy-start.82 = (f32[1,1,512]{2,1,0:T(1,128)}, f32[1,1,512]{2,1,0:T(1,128)S(1)}, u32[]{:S(2)}) copy-start(f32[1,1,512]{2,1,0:T(1,128)S(1)} %get-tuple-element.243) | copy-start | bytes 6148
  18.3 85.9 %copy-start.102 = (f32[1,1,512]{2,1,0:T(1,128)}, f32[1,1,512]{2,1,0:T(1,128)S(1)}, u32[]{:S(2)}) copy-start(f32[1,1,512]{2,1,0:T(1,128)S(1)} %get-tuple-element.241) | copy-start | bytes 6148
  19.0 2.8 %copy-start.38 = (f32[1,384]{1,0:T(1,128)}, f32[1,384]{1,0:T(1,128)S(1)}, u32[]{:S(2)}) copy-start(f32[1,384]{1,0:T(1,128)S(1)} %get-tuple-element.255) | copy-start | bytes 4612
  21.4 15.3 %copy-start.35 = (bf16[768,128]{1,0:T(8,128)(2,1)S(1)}, bf16[768,128]{1,0:T(8,128)(2,1)}, u32[]{:S(2)}) copy-start(bf16[768,128]{1,0:T(8,128)(2,1)} %param.20) | copy-start | bytes 589828
  36.2 11.8 %copy-start.4 = (bf16[768,512]{1,0:T(8,128)(2,1)}, bf16[768,512]{1,0:T(8,128)(2,1)S(1)}, u32[]{:S(2)}) copy-start(bf16[768,512]{1,0:T(8,128)(2,1)S(1)} %all_gather.18) | copy-start | bytes 2359300
  36.4 31.2 %copy-start.56 = (f32[768]{0:T(1024)}, f32[768]{0:T(1024)S(1)}, u32[]{:S(2)}) copy-start(f32[768]{0:T(1024)S(1)} %broadcast_multiply_fusion.6) | copy-start | bytes 9220
  36.8 30.8 %copy-start.54 = (f32[768]{0:T(1024)}, f32[768]{0:T(1024)S(1)}, u32[]{:S(2)}) copy-start(f32[768]{0:T(1024)S(1)} %add_rsqrt_fusion.1) | copy-start | bytes 9220
  55.1 12.5 %copy-start.5 = (bf16[768,512]{1,0:T(8,128)(2,1)S(1)}, bf16[768,512]{1,0:T(8,128)(2,1)}, u32[]{:S(2)}) copy-start(bf16[768,512]{1,0:T(8,128)(2,1)} %copy-done.4) | copy-start | bytes 2359300
  75.8 13.8 %copy-start.10 = (f32[768,512]{1,0:T(8,128)}, f32[768,512]{1,0:T(8,128)S(1)}, u32[]{:S(2)}) copy-start(f32[768,512]{1,0:T(8,128)S(1)} %get-tuple-element.295) | copy-start | bytes 4718596
  89.6 14.7 %copy-start.50 = (f32[768]{0:T(1024)}, f32[768]{0:T(1024)S(1)}, u32[]{:S(2)}) copy-start(f32[768]{0:T(1024)S(1)} %broadcast_multiply_fusion.5) | copy-start | bytes 9220
  90.0 14.3 %copy-start.58 = (f32[768]{0:T(1024)}, f32[768]{0:T(1024)S(1)}, u32[]{:S(2)}) copy-start(f32[768]{0:T(1024)S(1)} %add_rsqrt_fusion) | copy-start | bytes 9220
  95.5 8.8 %copy-start.3 = (f32[768,512]{1,0:T(8,128)S(1)}, f32[768,512]{1,0:T(8,128)}, u32[]{:S(2)}) copy-start(f32[768,512]{1,0:T(8,128)} %copy-done.2) | copy-start | bytes 4718596
  104.3 7.7 %copy-start.6 = (bf16[768,512]{1,0:T(8,128)(2,1)S(1)}, bf16[768,512]{1,0:T(8,128)(2,1)}, u32[]{:S(2)}) copy-start(bf16[768,512]{1,0:T(8,128)(2,1)} %all_gather.23) | copy-start | bytes 2359300
  104.3 7.7 %copy-start.33 = (bf16[2,512,512]{2,1,0:T(8,128)(2,1)S(1)}, bf16[2,512,512]{2,1,0:T(8,128)(2,1)}, u32[]{:S(2)}) copy-start(bf16[2,512,512]{2,1,0:T(8,128)(2,1)} %all-gather.8.cloned.1.call-done) | copy-start | bytes 3145732
  114.8 3.3 %slice-start.2 = ((s8[4718592]{0:T(1024)(128)(4,1)}), s8[4194304]{0:T(1024)(128)(4,1)S(1)}, s32[]{:S(2)}) async-start(s8[4718592]{0:T(1024)(128)(4,1)} %bitcast.451), calls=%async_computation.5 | async-start | bytes 8388608
  141.1 3.9 %copy-start.7 = (bf16[768,512]{1,0:T(8,128)(2,1)S(1)}, bf16[768,512]{1,0:T(8,128)(2,1)}, u32[]{:S(2)}) copy-start(bf16[768,512]{1,0:T(8,128)(2,1)} %all_gather.23) | copy-start | bytes 2359300
  141.1 3.9 %copy-start.11 = (f32[768,512]{1,0:T(8,128)S(1)}, f32[768,512]{1,0:T(8,128)}, u32[]{:S(2)}) copy-start(f32[768,512]{1,0:T(8,128)} %copy-done.10) | copy-start | bytes 4718596
  141.1 3.9 %copy-start.25 = (f32[768,512]{1,0:T(8,128)S(1)}, f32[768,512]{1,0:T(8,128)}, u32[]{:S(2)}) copy-start(f32[768,512]{1,0:T(8,128)} %get-tuple-element.297) | copy-start | bytes 4718596
  145.0 14.3 %slice-start = ((s8[4718592]{0:T(1024)(128)(4,1)}), s8[524288]{0:T(1024)(128)(4,1)S(1)}, s32[]{:S(2)}) async-start(s8[4718592]{0:T(1024)(128)(4,1)} %bitcast.449), calls=%async_computation.3 | async-start | bytes 1048576
  147.8 2.6 copy-start.88
  147.8 3.9 %copy-start.18 = (f32[768,512]{1,0:T(8,128)S(1)}, f32[768,512]{1,0:T(8,128)}, u32[]{:S(2)}) copy-start(f32[768,512]{1,0:T(8,128)} %get-tuple-element.159) | copy-start | bytes 4718596
  150.5 8.9 %copy-start.42 = (f32[8,384]{1,0:T(8,128)}, f32[8,384]{1,0:T(8,128)S(1)}, u32[]{:S(2)}) copy-start(f32[8,384]{1,0:T(8,128)S(1)} %stack.268) | copy-start | bytes 36868
  151.7 7.6 %slice-start.1 = ((s8[4718592]{0:T(1024)(128)(4,1)}), s8[4194304]{0:T(1024)(128)(4,1)S(1)}, s32[]{:S(2)}) async-start(s8[4718592]{0:T(1024)(128)(4,1)} %bitcast.449), calls=%async_computation.4 | async-start | bytes 8388608
  186.3 2.9 %copy-start.84 = (f32[512]{0:T(512)S(1)}, f32[512]{0:T(512)}, u32[]{:S(2)}) copy-start(f32[512]{0:T(512)} %get-tuple-element.157) | copy-start | bytes 6148
  252.5 4.3 %copy-start.13 = (bf16[5888,128]{1,0:T(8,128)(2,1)S(1)}, bf16[5888,128]{1,0:T(8,128)(2,1)}, u32[]{:S(2)}) copy-start(bf16[5888,128]{1,0:T(8,128)(2,1)} %shard_map.358) | copy-start | bytes 4521988
  253.2 6.5 %copy-start.71 = (f32[8,128]{1,0:T(8,128)}, f32[8,128]{1,0:T(8,128)S(1)}, u32[]{:S(2)}) copy-start(f32[8,128]{1,0:T(8,128)S(1)} %convert_multiply_fusion.5) | copy-start | bytes 12292
  256.8 2.9 %copy-start.70 = (f32[2,4,128]{2,1,0:T(4,128)S(1)}, f32[2,4,128]{2,1,0:T(4,128)}, u32[]{:S(2)}) copy-start(f32[2,4,128]{2,1,0:T(4,128)} %param.26) | copy-start | bytes 12292
  256.8 2.9 %copy-start.98 = (f32[2,4,128]{2,1,0:T(4,128)S(1)}, f32[2,4,128]{2,1,0:T(4,128)}, u32[]{:S(2)}) copy-start(f32[2,4,128]{2,1,0:T(4,128)} %param.36) | copy-start | bytes 12292
  256.9 2.9 %copy-start.99 = (f32[2,4,128]{2,1,0:T(4,128)S(1)}, f32[2,4,128]{2,1,0:T(4,128)}, u32[]{:S(2)}) copy-start(f32[2,4,128]{2,1,0:T(4,128)} %param.31) | copy-start | bytes 12292
  257.0 8.2 %copy-start.12 = (f32[3072,128]{1,0:T(8,128)}, f32[3072,128]{1,0:T(8,128)S(1)}, u32[]{:S(2)}) copy-start(f32[3072,128]{1,0:T(8,128)S(1)} %convert_multiply_fusion) | copy-start | bytes 4718596
  259.7 3.7 %copy-start.16 = (f32[2,128,768]{2,1,0:T(8,128)}, f32[2,128,768]{2,1,0:T(8,128)S(1)}, u32[]{:S(2)}) copy-start(f32[2,128,768]{2,1,0:T(8,128)S(1)} %mul.6070) | copy-start | bytes 2359300
  260.5 3.0 %copy-start.15 = (f32[2,128,768]{2,1,0:T(8,128)S(1)}, f32[2,128,768]{2,1,0:T(8,128)}, u32[]{:S(2)}) copy-start(f32[2,128,768]{2,1,0:T(8,128)} %param.23) | copy-start | bytes 2359300
  260.5 3.0 %copy-start.30 = (f32[2,128,768]{2,1,0:T(8,128)S(1)}, f32[2,128,768]{2,1,0:T(8,128)}, u32[]{:S(2)}) copy-start(f32[2,128,768]{2,1,0:T(8,128)} %param.33) | copy-start | bytes 2359300
  260.5 3.0 %copy-start.31 = (f32[2,128,768]{2,1,0:T(8,128)S(1)}, f32[2,128,768]{2,1,0:T(8,128)}, u32[]{:S(2)}) copy-start(f32[2,128,768]{2,1,0:T(8,128)} %param.28) | copy-start | bytes 2359300
  263.5 2.7 copy-start.20
  263.5 3.2 %copy-start.21 = (f32[2,1536,128]{2,1,0:T(8,128)S(1)}, f32[2,1536,128]{2,1,0:T(8,128)}, u32[]{:S(2)}) copy-start(f32[2,1536,128]{2,1,0:T(8,128)} %param.29) | copy-start | bytes 4718596
  (70 other events, 105.1 us)
Sparse Core Ops, SparseCore 0:
  10.2 26.5 all-gather.3
  38.9 28.6 all-gather.5
  69.7 16.8 all-gather.7

commit v15 on v13

--- a/solution.py
+++ b/solution.py
@@ -451,7 +451,7 @@
 
 
     in_all = gather_feat(input_matrix.astype(jnp.bfloat16), 1)
-    out_all = gather_feat(output_matrix.astype(jnp.bfloat16), 2)
+    out_all = [gather_feat(output_matrix[k].astype(jnp.bfloat16), 1) for k in range(layers)]
     gate_all = gather_feat(gate_matrix.astype(jnp.bfloat16), 2)
     feature_all = gather_feat(feature_vectors, 2)
     stream = gather_feat(activations_in, 1).astype(jnp.float32)

time: 277 us -> 271 us (0.978)
  waiting for transfers between devices: 14.5 us -> 9.26 us
    all_gather x3 -> x4, waiting for transfers between devices: 14.5 us -> 8.69 us  [gather_feat(): return lax.all_gather(value, 'feat', axis=axis, tiled=True)]
  transfers between devices with their start and end apart: 3 -> 4, of which waited for: 2 -> 2; matrix products, arithmetic and copies ran while one was open for 9% -> 11% of each run, Pallas kernels for 3% -> 7%
where the time goes in v15:
time: 271 us; the launch traced here: 270 us
  Pallas kernels  110 us (41%)
  matrix products  55.5 us (20%)
  other arithmetic  33.8 us (12%)
  blocking collectives  27.9 us (10%)
  local copies, waits for them, and re-layouts  18.3 us (7%)
  between operations  15.3 us (6%)
  waiting for transfers between devices  9.26 us (3%)
    pallas_call x1, Pallas kernels, ring_sum(): pl.pallas_call(lambda *refs: ring_sum_kernel(n, *refs), out_shape=jax.Sha...  61.3 us
    pallas_call x2, Pallas kernels, adjoint(): pl.pallas_call(adjoint_kernel, out_shape=(jax.ShapeDtypeStruct((count, 2...  30.8 us
    all_gather x3, blocking collectives, gather_feat(): return lax.all_gather(value, 'feat', axis=axis, tiled=True)  27.9 us
    pallas_call x2, Pallas kernels, recurrence(): pl.pallas_call(recurrence_kernel, out_shape=jax.ShapeDtypeStruct((count,...  17.8 us
    dot_general x4, matrix products, contract_cols(): lax.dot_general(left, right, (((1,), (1,)), ((), ())), preferred_element_...  17.2 us
    dot_general x2, matrix products, body(): jnp.dot(states_low, out_low, preferred_element_type=jnp.float32)  15.6 us
    unnamed x236, local copies, waits for them, and re-layouts  11.1 us
    all_gather x4, waiting for transfers between devices, gather_feat(): return lax.all_gather(value, 'feat', axis=axis, tiled=True)  8.69 us
  transfers between devices with their start and end apart: 4, of which 2 were waited for; matrix products, arithmetic and copies ran while one was open for 11% of the time, Pallas kernels for 7%

profile of v15, /device:TPU:0, one launch (start us, length us, event | category | flops | bytes accessed | tf_op | source)
XLA Modules:
  0.0 270.2 jit_solution(3755988773833925627)
XLA Ops:
  7.2 2.0 convert_element_type.105
  9.5 0.9 fusion.116
  12.8 6.1 %all_gather.22 = f32[2,4,512]{2,1,0:T(4,128)S(1)} all-gather(f32[2,4,128]{2,1,0:T(4,128)S(1)} %copy-done.68), channel_id=1, replica_groups=mesh['seq'=8,'feat'=4] {'feat'}, dimensions={2}, use_global_device_ids=true | all-gather | bytes 20480 | tf_op jit(solution)/shard_map/all_gather | solution.py:412
  20.8 1.2 rev.30
  22.6 0.9 copy.86.masks_ref
  23.5 12.7 %all_gather.21 = bf16[768,512]{1,0:T(8,128)(2,1)S(1)} all-gather(bf16[768,128]{1,0:T(8,128)(2,1)S(1)} %copy-done.33), channel_id=1, replica_groups=mesh['seq'=8,'feat'=4] {'feat'}, dimensions={1}, use_global_device_ids=true | all-gather | bytes 983040 | tf_op jit(solution)/shard_map/all_gather | solution.py:412
  36.8 9.2 %all_gather.27 = bf16[768,512]{1,0:T(8,128)(2,1)} all-gather(bf16[768,128]{1,0:T(8,128)(2,1)S(1)} %copy-done.34), channel_id=1, replica_groups=mesh['seq'=8,'feat'=4] {'feat'}, dimensions={1}, use_global_device_ids=true | all-gather | bytes 983040 | tf_op jit(solution)/shard_map/all_gather | solution.py:412
  46.6 1.2 fusion.27
  49.8 2.1 fusion.33.drive_ref
  52.3 1.0 copy-done
  53.3 1.6 pad_maximum_fusion.x_ref
  54.9 8.9 %shard_map.354.states_ref = f32[768,1536]{1,0:T(8,128)} custom-call(s32[2]{0:T(128)} %starts_ref.7, s32[2]{0:T(128)} %lengths_ref.7, f32[4,8,384]{2,1,0:T(8,128)} %pad_maximum_fusion.5.pow_ref, f32[768,768]{1,0:T(8,128)} %pad_maximum_fusion.x_ref), custom_call_target="tpu_custom_call" | custom-call | flops 11796480 | bytes 9437184 | tf_op jit(solution)/shard_map/pallas_call | solution.py:144
  63.8 8.3 %multiply_multiply_fusion.11 = (f32[768,512]{1,0:T(8,128)S(1)}, f32[768,512]{1,0:T(8,128)}) fusion(f32[512]{0:T(512)S(1)} %bitcast.489, f32[512]{0:T(512)S(1)} %bitcast.492, f32[768]{0:T(1024)S(1)} %add_rsqrt_fusion.1, f32[768]{0:T(1024)S(1)} %broadcast_multiply_fusion.6, bf16[768,512]{1,0:T(8,128)(2,1)S(1)} %copy-done.5, f32[512]{0:T(512)S(1)} %bitcast.498, ...), kind=kOutput, calls=%fused_computation.80 | convolution fusion | flops 1237057536 | bytes 10235904 | tf_op jit(solution)/shard_map/dot_general | solution.py:485
  72.1 4.7 %all-gather.9.cloned.1.call-done = bf16[2,512,512]{2,1,0:T(8,128)(2,1)} async-done(((bf16[2,512,128]{2,1,0:T(8,128)(2,1)}), bf16[2,512,512]{2,1,0:T(8,128)(2,1)}) %all-gather.9.cloned.1.call-update) | async-done | bytes 1048592 | tf_op jit(solution)/shard_map/all_gather | solution.py:412
  76.8 3.0 %fusion.115 = (f32[768]{0:T(1024)S(1)}, f32[768,512]{1,0:T(8,128)S(1)}, f32[768,512]{1,0:T(8,128)}) fusion(f32[768,512]{1,0:T(8,128)S(1)} %get-tuple-element.297, bf16[768,512]{1,0:T(8,128)(2,1)S(1)} %copy-done.5, f32[512]{0:T(512)S(1)} %bitcast.503, bf16[2,512,512]{2,1,0:T(8,128)(2,1)} %all-gather.9.cloned.1.call-done), kind=kOutput, calls=%fused_computation.357 | convolution fusion | flops 406191360 | bytes 7607296 | tf_op jit(solution)/shard_map/dot_general | solution.py:490
  81.0 0.8 copy-done.21
  83.0 1.1 copy-done.1
  84.1 1.6 pad_maximum_fusion.1.x_ref
  85.7 8.9 %shard_map.355.states_ref = f32[768,1536]{1,0:T(8,128)} custom-call(s32[2]{0:T(128)} %starts_ref.7, s32[2]{0:T(128)} %lengths_ref.7, f32[4,8,384]{2,1,0:T(8,128)} %pad_maximum_fusion.6.pow_ref, f32[768,768]{1,0:T(8,128)} %pad_maximum_fusion.1.x_ref), custom_call_target="tpu_custom_call" | custom-call | flops 11796480 | bytes 9437184 | tf_op jit(solution)/shard_map/pallas_call | solution.py:144
  94.7 4.0 %all-gather.13.cloned.1.call-done = bf16[1,1536,512]{2,1,0:T(8,128)(2,1)} async-done(((bf16[1,1536,128]{2,1,0:T(8,128)(2,1)}), bf16[1,1536,512]{2,1,0:T(8,128)(2,1)}) %all-gather.13.cloned.1.call-update) | async-done | bytes 1572880 | tf_op jit(solution)/shard_map/all_gather | solution.py:412
  98.7 7.3 %multiply_multiply_fusion.10 = (f32[768,512]{1,0:T(8,128)S(1)}, f32[768,512]{1,0:T(8,128)S(1)}, f32[768,512]{1,0:T(8,128)S(1)}) fusion(f32[512]{0:T(512)S(1)} %bitcast.495, f32[512]{0:T(512)S(1)} %bitcast.482, f32[768]{0:T(1024)S(1)} %add_rsqrt_fusion, f32[768,512]{1,0:T(8,128)S(1)} %copy-done.3, f32[768]{0:T(1024)S(1)} %broadcast_multiply_fusion.5, ...), kind=kOutput, calls=%fused_computation.78 | convolution fusion | flops 1236664320 | bytes 12595200 | tf_op jit(solution)/shard_map/dot_general | solution.py:485
  106.0 1.6 convert_reduce_fusion.1
  107.6 1.1 convolution_bitcast_fusion.4
  108.8 0.9 dynamic-slice_add_fusion.1
  109.7 2.3 fusion.118
  112.0 1.7 convolution_bitcast_fusion
  113.8 3.6 %fusion.5.g_ref = f32[768,1536]{1,0:T(8,128)} fusion(bf16[768,512]{1,0:T(8,128)(2,1)S(1)} %get-tuple-element.302, bf16[1,1536,512]{2,1,0:T(8,128)(2,1)S(1)} %copy-done.108), kind=kOutput, calls=%fused_computation.17 | convolution fusion | flops 1207959552 | bytes 7077888 | tf_op jit(solution)/shard_map/dot_general | solution.py:406
  117.4 15.4 %shard_map.356 = (bf16[768,768]{1,0:T(8,128)(2,1)}, f32[4,384]{1,0:T(4,128)}) custom-call(s32[2]{0:T(128)} %starts_ref.7, s32[2]{0:T(128)} %lengths_ref.7, f32[4,8,384]{2,1,0:T(8,128)} %pad_maximum_fusion.7.pow_ref, f32[4,384]{1,0:T(4,128)} %pad_maximum_fusion.10.coef_ref, f32[768,4]{1,0:T(8,128)} %copy.86.masks_ref, f32[768,1536]{1,0:T(8,128)} %fusion.5.g_ref, ...), custom_call_target="tpu_custom_call" | custom-call | flops 17694720 | bytes 14155776 | tf_op jit(solution)/shard_map/pallas_call | solution.py:375
  132.9 1.8 convolution_bitcast_fusion.2
  134.8 3.9 %multiply_reduce_fusion.1 = (f32[512]{0:T(512)}, f32[768]{0:T(1024)S(1)}, f32[512]{0:T(512)}, f32[768]{0:T(1024)S(1)}, f32[512]{0:T(512)}, /*index=5*/f32[768,512]{1,0:T(8,128)S(1)}) fusion(f32[768]{0:T(1024)S(1)} %copy-done.58, f32[768,512]{1,0:T(8,128)S(1)} %copy-done.3, f32[768]{0:T(1024)S(1)} %copy-done.50, f32[512]{0:T(512)S(1)} %bitcast.483, ...), kind=kOutput, calls=%fused_computation.31 | convolution fusion | flops 609874944 | bytes 6711296 | tf_op jit(solution)/shard_map/dot_general | solution.py:529
  138.7 2.6 convert_reduce_fusion.2
  141.5 1.2 convolution_bitcast_fusion.5
  144.2 1.2 rev.31
  145.4 7.6 %fusion.119 = (bf16[768,512]{1,0:T(8,128)(2,1)S(1)}, f32[768,512]{1,0:T(8,128)}) fusion(f32[768,512]{1,0:T(8,128)} %get-tuple-element.298, bf16[768,512]{1,0:T(8,128)(2,1)} %copy-done.25, bf16[2,512,512]{2,1,0:T(8,128)(2,1)} %all-gather.9.cloned.1.call-done, f32[768,512]{1,0:T(8,128)S(1)} %copy-done.17, f32[768,512]{1,0:T(8,128)} %get-tuple-element.299), kind=kOutput, calls=%fused_computation.361 | convolution fusion | flops 431751168 | bytes 8388608 | tf_op jit(solution)/shard_map/dot_general | solution.py:406
  155.2 3.6 %fusion.9.g_ref = f32[768,1536]{1,0:T(8,128)} fusion(bf16[768,512]{1,0:T(8,128)(2,1)S(1)} %get-tuple-element.305, bf16[1,1536,512]{2,1,0:T(8,128)(2,1)S(1)} %copy-done.107), kind=kOutput, calls=%fused_computation.21 | convolution fusion | flops 1207959552 | bytes 7077888 | tf_op jit(solution)/shard_map/dot_general | solution.py:406
  158.8 15.4 %shard_map.357 = (bf16[768,768]{1,0:T(8,128)(2,1)}, f32[4,384]{1,0:T(4,128)}) custom-call(s32[2]{0:T(128)} %starts_ref.7, s32[2]{0:T(128)} %lengths_ref.7, f32[4,8,384]{2,1,0:T(8,128)} %pad_maximum_fusion.8.pow_ref, f32[4,384]{1,0:T(4,128)} %pad_maximum_fusion.11.coef_ref, f32[768,4]{1,0:T(8,128)} %copy.86.masks_ref, f32[768,1536]{1,0:T(8,128)} %fusion.9.g_ref, ...), custom_call_target="tpu_custom_call" | custom-call | flops 17694720 | bytes 14155776 | tf_op jit(solution)/shard_map/pallas_call | solution.py:375
  174.2 1.7 convolution_bitcast_fusion.3
  177.1 0.9 copy-done.28
  180.0 2.9 %fusion.98 = (f32[512]{0:T(512)S(1)}, f32[512]{0:T(512)S(1)}, f32[512]{0:T(512)S(1)}, f32[768]{0:T(1024)S(1)}, f32[768]{0:T(1024)S(1)}, /*index=5*/f32[768,512]{1,0:T(8,128)}, f32[768,512]{1,0:T(8,128)}) fusion(f32[768]{0:T(1024)S(1)} %copy-done.54, f32[768]{0:T(1024)S(1)} %copy-done.56, bf16[768,512]{1,0:T(8,128)(2,1)S(1)} %copy-done.5, ...), kind=kOutput, calls=%fused_computation.351 | convolution fusion | flops 610268160 | bytes 7497728 | tf_op jit(solution)/shard_map/dot_general | solution.py:529
  183.1 1.8 pad_bitcast_fusion.refs_0_
  184.9 61.3 %shard_map.358 = bf16[5888,128]{1,0:T(8,128)(2,1)} custom-call(f32[5888,128]{1,0:T(8,128)} %pad_bitcast_fusion.refs_0_), custom_call_target="tpu_custom_call" | custom-call | tf_op jit(solution)/shard_map/pallas_call | solution.py:267
  246.3 1.6 convert_element_type.128
  247.9 0.8 slice_multiply_fusion.2
  252.4 3.0 %add_multiply_fusion.4 = (f32[2,512,128]{2,1,0:T(8,128)}, f32[2,512,128]{2,1,0:T(8,128)}, f32[2,512,128]{2,1,0:T(8,128)}) fusion(f32[2,512,128]{2,1,0:T(8,128)} %param.35, f32[2,512,128]{2,1,0:T(8,128)} %param.25, f32[2,512,128]{2,1,0:T(8,128)} %bitcast.462, f32[2,512,128]{2,1,0:T(8,128)} %param.30), kind=kLoop, calls=%fused_computation.111 | loop fusion | flops 1310720 | bytes 3670016 | tf_op jit(solution)/shard_map/add | solution.py:395
  255.4 1.7 add_multiply_fusion.3
  257.2 0.9 copy-done.19
  258.6 2.7 add_multiply_fusion
  261.3 2.4 dynamic-slice_add_fusion
  (322 shorter events, 21.5 us)
Async XLA Ops:
  7.2 42.6 %all-gather.7.cloned.1.call-start = ((), (), s32[]{:S(2)}) async-start(), calls=%async_computation | async-start | bytes 1966080 | tf_op jit(solution)/shard_map/all_gather | solution.py:412
  9.3 54.5 %all-gather.11.cloned.1.call-start = ((), (), s32[]{:S(2)}) async-start(), calls=%async_computation.2 | async-start | bytes 1966080 | tf_op jit(solution)/shard_map/all_gather | solution.py:412
  9.5 3.1 %copy-start.67 = (s32[2]{0:T(128)S(1)}, s32[2]{0:T(128)}, u32[]{:S(2)}) copy-start(s32[2]{0:T(128)} %starts_ref.7) | copy-start | bytes 28
  9.5 3.1 %copy-start.74 = (s32[2]{0:T(128)S(1)}, s32[2]{0:T(128)}, u32[]{:S(2)}) copy-start(s32[2]{0:T(128)} %lengths_ref.7) | copy-start | bytes 28
  9.5 3.3 %copy-start.68 = (f32[2,4,128]{2,1,0:T(4,128)S(1)}, f32[2,4,128]{2,1,0:T(4,128)}, u32[]{:S(2)}) copy-start(f32[2,4,128]{2,1,0:T(4,128)} %param.26) | copy-start | bytes 12292
  10.5 13.0 %copy-start.33 = (bf16[768,128]{1,0:T(8,128)(2,1)S(1)}, bf16[768,128]{1,0:T(8,128)(2,1)}, u32[]{:S(2)}) copy-start(bf16[768,128]{1,0:T(8,128)(2,1)} %param.19) | copy-start | bytes 589828
  10.5 66.3 %all-gather.9.cloned.1.call-start = ((), (), s32[]{:S(2)}) async-start(), calls=%async_computation.1 | async-start | bytes 1310720 | tf_op jit(solution)/shard_map/all_gather | solution.py:412
  11.4 87.3 %all-gather.13.cloned.1.call-start = ((), (), s32[]{:S(2)}) async-start(), calls=%async_computation.3 | async-start | bytes 1966080 | tf_op jit(solution)/shard_map/all_gather | solution.py:412
  12.6 9.7 %copy-start.59 = (f32[1,384]{1,0:T(1,128)}, f32[1,384]{1,0:T(1,128)S(1)}, u32[]{:S(2)}) copy-start(f32[1,384]{1,0:T(1,128)S(1)} %get-tuple-element.183) | copy-start | bytes 4612
  12.6 33.4 %copy-start.35 = (f32[1,384]{1,0:T(1,128)}, f32[1,384]{1,0:T(1,128)S(1)}, u32[]{:S(2)}) copy-start(f32[1,384]{1,0:T(1,128)S(1)} %get-tuple-element.184) | copy-start | bytes 4612
  12.6 33.4 %copy-start.43 = (f32[1,384]{1,0:T(1,128)}, f32[1,384]{1,0:T(1,128)S(1)}, u32[]{:S(2)}) copy-start(f32[1,384]{1,0:T(1,128)S(1)} %get-tuple-element.185) | copy-start | bytes 4612
  19.0 44.8 %copy-start.77 = (f32[1,1,512]{2,1,0:T(1,128)}, f32[1,1,512]{2,1,0:T(1,128)S(1)}, u32[]{:S(2)}) copy-start(f32[1,1,512]{2,1,0:T(1,128)S(1)} %get-tuple-element.249) | copy-start | bytes 6148
  19.0 44.8 %copy-start.79 = (f32[1,1,512]{2,1,0:T(1,128)}, f32[1,1,512]{2,1,0:T(1,128)S(1)}, u32[]{:S(2)}) copy-start(f32[1,1,512]{2,1,0:T(1,128)S(1)} %get-tuple-element.250) | copy-start | bytes 6148
  19.0 44.8 %copy-start.99 = (f32[1,1,512]{2,1,0:T(1,128)}, f32[1,1,512]{2,1,0:T(1,128)S(1)}, u32[]{:S(2)}) copy-start(f32[1,1,512]{2,1,0:T(1,128)S(1)} %get-tuple-element.248) | copy-start | bytes 6148
  19.0 79.7 %copy-start.65 = (f32[1,1,512]{2,1,0:T(1,128)}, f32[1,1,512]{2,1,0:T(1,128)S(1)}, u32[]{:S(2)}) copy-start(f32[1,1,512]{2,1,0:T(1,128)S(1)} %get-tuple-element.246) | copy-start | bytes 6148
  19.0 79.7 %copy-start.81 = (f32[1,1,512]{2,1,0:T(1,128)}, f32[1,1,512]{2,1,0:T(1,128)S(1)}, u32[]{:S(2)}) copy-start(f32[1,1,512]{2,1,0:T(1,128)S(1)} %get-tuple-element.245) | copy-start | bytes 6148
  19.0 79.7 %copy-start.101 = (f32[1,1,512]{2,1,0:T(1,128)}, f32[1,1,512]{2,1,0:T(1,128)S(1)}, u32[]{:S(2)}) copy-start(f32[1,1,512]{2,1,0:T(1,128)S(1)} %get-tuple-element.243) | copy-start | bytes 6148
  19.7 2.8 %copy-start.37 = (f32[1,384]{1,0:T(1,128)}, f32[1,384]{1,0:T(1,128)S(1)}, u32[]{:S(2)}) copy-start(f32[1,384]{1,0:T(1,128)S(1)} %get-tuple-element.257) | copy-start | bytes 4612
  22.1 14.7 %copy-start.34 = (bf16[768,128]{1,0:T(8,128)(2,1)S(1)}, bf16[768,128]{1,0:T(8,128)(2,1)}, u32[]{:S(2)}) copy-start(bf16[768,128]{1,0:T(8,128)(2,1)} %param.20) | copy-start | bytes 589828
  36.2 11.7 %copy-start.4 = (bf16[768,512]{1,0:T(8,128)(2,1)}, bf16[768,512]{1,0:T(8,128)(2,1)S(1)}, u32[]{:S(2)}) copy-start(bf16[768,512]{1,0:T(8,128)(2,1)S(1)} %all_gather.21) | copy-start | bytes 2359300
  36.4 27.5 %copy-start.55 = (f32[768]{0:T(1024)}, f32[768]{0:T(1024)S(1)}, u32[]{:S(2)}) copy-start(f32[768]{0:T(1024)S(1)} %broadcast_multiply_fusion.6) | copy-start | bytes 9220
  36.8 27.0 %copy-start.53 = (f32[768]{0:T(1024)}, f32[768]{0:T(1024)S(1)}, u32[]{:S(2)}) copy-start(f32[768]{0:T(1024)S(1)} %add_rsqrt_fusion.1) | copy-start | bytes 9220
  54.9 8.9 %copy-start.5 = (bf16[768,512]{1,0:T(8,128)(2,1)S(1)}, bf16[768,512]{1,0:T(8,128)(2,1)}, u32[]{:S(2)}) copy-start(bf16[768,512]{1,0:T(8,128)(2,1)} %copy-done.4) | copy-start | bytes 2359300
  72.1 7.7 %copy-start.10 = (f32[768,512]{1,0:T(8,128)}, f32[768,512]{1,0:T(8,128)S(1)}, u32[]{:S(2)}) copy-start(f32[768,512]{1,0:T(8,128)S(1)} %get-tuple-element.297) | copy-start | bytes 4718596
  79.8 18.8 %copy-start.49 = (f32[768]{0:T(1024)}, f32[768]{0:T(1024)S(1)}, u32[]{:S(2)}) copy-start(f32[768]{0:T(1024)S(1)} %broadcast_multiply_fusion.5) | copy-start | bytes 9220
  80.2 18.5 %copy-start.57 = (f32[768]{0:T(1024)}, f32[768]{0:T(1024)S(1)}, u32[]{:S(2)}) copy-start(f32[768]{0:T(1024)S(1)} %add_rsqrt_fusion) | copy-start | bytes 9220
  85.7 12.9 %copy-start.3 = (f32[768,512]{1,0:T(8,128)S(1)}, f32[768,512]{1,0:T(8,128)}, u32[]{:S(2)}) copy-start(f32[768,512]{1,0:T(8,128)} %copy-done.2) | copy-start | bytes 4718596
  98.7 7.3 %copy-start.6 = (bf16[768,512]{1,0:T(8,128)(2,1)S(1)}, bf16[768,512]{1,0:T(8,128)(2,1)}, u32[]{:S(2)}) copy-start(bf16[768,512]{1,0:T(8,128)(2,1)} %all_gather.27) | copy-start | bytes 2359300
  98.7 7.3 %copy-start.32 = (bf16[2,512,512]{2,1,0:T(8,128)(2,1)S(1)}, bf16[2,512,512]{2,1,0:T(8,128)(2,1)}, u32[]{:S(2)}) copy-start(bf16[2,512,512]{2,1,0:T(8,128)(2,1)} %all-gather.9.cloned.1.call-done) | copy-start | bytes 3145732
  108.8 3.3 %slice-start.2 = ((s8[4718592]{0:T(1024)(128)(4,1)}), s8[4194304]{0:T(1024)(128)(4,1)S(1)}, s32[]{:S(2)}) async-start(s8[4718592]{0:T(1024)(128)(4,1)} %bitcast.457), calls=%async_computation.6 | async-start | bytes 8388608
  134.8 3.9 %copy-start.7 = (bf16[768,512]{1,0:T(8,128)(2,1)S(1)}, bf16[768,512]{1,0:T(8,128)(2,1)}, u32[]{:S(2)}) copy-start(bf16[768,512]{1,0:T(8,128)(2,1)} %all_gather.27) | copy-start | bytes 2359300
  134.8 3.9 %copy-start.11 = (f32[768,512]{1,0:T(8,128)S(1)}, f32[768,512]{1,0:T(8,128)}, u32[]{:S(2)}) copy-start(f32[768,512]{1,0:T(8,128)} %copy-done.10) | copy-start | bytes 4718596
  134.8 3.9 %copy-start.24 = (f32[768,512]{1,0:T(8,128)S(1)}, f32[768,512]{1,0:T(8,128)}, u32[]{:S(2)}) copy-start(f32[768,512]{1,0:T(8,128)} %get-tuple-element.299) | copy-start | bytes 4718596
  138.7 14.3 %slice-start = ((s8[4718592]{0:T(1024)(128)(4,1)}), s8[524288]{0:T(1024)(128)(4,1)S(1)}, s32[]{:S(2)}) async-start(s8[4718592]{0:T(1024)(128)(4,1)} %bitcast.455), calls=%async_computation.4 | async-start | bytes 1048576
  141.5 3.9 %copy-start.17 = (f32[768,512]{1,0:T(8,128)S(1)}, f32[768,512]{1,0:T(8,128)}, u32[]{:S(2)}) copy-start(f32[768,512]{1,0:T(8,128)} %get-tuple-element.159) | copy-start | bytes 4718596
  144.1 8.9 %copy-start.41 = (f32[8,384]{1,0:T(8,128)}, f32[8,384]{1,0:T(8,128)S(1)}, u32[]{:S(2)}) copy-start(f32[8,384]{1,0:T(8,128)S(1)} %stack.268) | copy-start | bytes 36868
  145.4 7.6 %slice-start.1 = ((s8[4718592]{0:T(1024)(128)(4,1)}), s8[4194304]{0:T(1024)(128)(4,1)S(1)}, s32[]{:S(2)}) async-start(s8[4718592]{0:T(1024)(128)(4,1)} %bitcast.455), calls=%async_computation.5 | async-start | bytes 8388608
  180.0 2.9 %copy-start.83 = (f32[512]{0:T(512)S(1)}, f32[512]{0:T(512)}, u32[]{:S(2)}) copy-start(f32[512]{0:T(512)} %get-tuple-element.157) | copy-start | bytes 6148
  247.9 3.8 %copy-start.70 = (f32[8,128]{1,0:T(8,128)}, f32[8,128]{1,0:T(8,128)S(1)}, u32[]{:S(2)}) copy-start(f32[8,128]{1,0:T(8,128)S(1)} %slice_multiply_fusion.4) | copy-start | bytes 12292
  249.0 8.1 %copy-start.12 = (f32[3072,128]{1,0:T(8,128)}, f32[3072,128]{1,0:T(8,128)S(1)}, u32[]{:S(2)}) copy-start(f32[3072,128]{1,0:T(8,128)S(1)} %slice_multiply_fusion) | copy-start | bytes 4718596
  249.0 2.7 copy-start.69
  249.0 2.7 copy-start.97
  251.7 3.7 %copy-start.15 = (f32[2,128,768]{2,1,0:T(8,128)}, f32[2,128,768]{2,1,0:T(8,128)S(1)}, u32[]{:S(2)}) copy-start(f32[2,128,768]{2,1,0:T(8,128)S(1)} %mul.6070) | copy-start | bytes 2359300
  252.4 3.0 %copy-start.14 = (f32[2,128,768]{2,1,0:T(8,128)S(1)}, f32[2,128,768]{2,1,0:T(8,128)}, u32[]{:S(2)}) copy-start(f32[2,128,768]{2,1,0:T(8,128)} %param.23) | copy-start | bytes 2359300
  252.4 3.0 %copy-start.29 = (f32[2,128,768]{2,1,0:T(8,128)S(1)}, f32[2,128,768]{2,1,0:T(8,128)}, u32[]{:S(2)}) copy-start(f32[2,128,768]{2,1,0:T(8,128)} %param.33) | copy-start | bytes 2359300
  252.4 3.0 %copy-start.30 = (f32[2,128,768]{2,1,0:T(8,128)S(1)}, f32[2,128,768]{2,1,0:T(8,128)}, u32[]{:S(2)}) copy-start(f32[2,128,768]{2,1,0:T(8,128)} %param.28) | copy-start | bytes 2359300
  255.4 2.7 %copy-start.19 = (f32[2,1536,128]{2,1,0:T(8,128)S(1)}, f32[2,1536,128]{2,1,0:T(8,128)}, u32[]{:S(2)}) copy-start(f32[2,1536,128]{2,1,0:T(8,128)} %param.34) | copy-start | bytes 4718596
  255.4 3.2 %copy-start.20 = (f32[2,1536,128]{2,1,0:T(8,128)S(1)}, f32[2,1536,128]{2,1,0:T(8,128)}, u32[]{:S(2)}) copy-start(f32[2,1536,128]{2,1,0:T(8,128)} %param.29) | copy-start | bytes 4718596
  (70 other events, 103.2 us)
Sparse Core Ops, SparseCore 0:
  10.2 26.0 all-gather.6
  38.4 19.3 all-gather.10
  59.9 16.8 all-gather.8
  78.8 19.8 all-gather.12

commit v16 on v15

--- a/solution.py
+++ b/solution.py
@@ -451,8 +451,13 @@
 
 
     in_all = gather_feat(input_matrix.astype(jnp.bfloat16), 1)
-    out_all = [gather_feat(output_matrix[k].astype(jnp.bfloat16), 1) for k in range(layers)]
-    gate_all = gather_feat(gate_matrix.astype(jnp.bfloat16), 2)
+    rows_out = output_matrix.shape[1]
+    paired = [
+        gather_feat(jnp.concatenate([output_matrix[k], gate_matrix[k]], 0).astype(jnp.bfloat16), 1)
+        for k in range(layers)
+    ]
+    out_all = [pair[:rows_out] for pair in paired]
+    gate_all = [pair[rows_out:] for pair in paired]
     feature_all = gather_feat(feature_vectors, 2)
     stream = gather_feat(activations_in, 1).astype(jnp.float32)
 

time: 271 us -> 264 us (0.974)
  waiting for transfers between devices: 9.26 us -> 0.05 us
    all_gather x4 -> x3, waiting for transfers between devices: 8.69 us -> 0.01 us  [gather_feat(): return lax.all_gather(value, 'feat', axis=axis, tiled=True)]
    unnamed x236 -> x234, local copies, waits for them, and re-layouts: 11.1 us -> 11.1 us
  transfers between devices with their start and end apart: 4 -> 3, of which waited for: 2 -> 0; matrix products, arithmetic and copies ran while one was open for 11% -> 12% of each run, Pallas kernels for 7% -> 7%
where the time goes in v16:
time: 264 us; the launch traced here: 263 us
  Pallas kernels  111 us (42%)
  matrix products  56.3 us (21%)
  other arithmetic  34.8 us (13%)
  blocking collectives  28.6 us (11%)
  local copies, waits for them, and re-layouts  17.4 us (7%)
  between operations  15.3 us (6%)
    pallas_call x1, Pallas kernels, ring_sum(): pl.pallas_call(lambda *refs: ring_sum_kernel(n, *refs), out_shape=jax.Sha...  62.4 us
    pallas_call x2, Pallas kernels, adjoint(): pl.pallas_call(adjoint_kernel, out_shape=(jax.ShapeDtypeStruct((count, 2...  30.8 us
    all_gather x3, blocking collectives, gather_feat(): return lax.all_gather(value, 'feat', axis=axis, tiled=True)  28.6 us
    pallas_call x2, Pallas kernels, recurrence(): pl.pallas_call(recurrence_kernel, out_shape=jax.ShapeDtypeStruct((count,...  17.4 us
    dot_general x4, matrix products, contract_cols(): lax.dot_general(left, right, (((1,), (1,)), ((), ())), preferred_element_...  17.2 us
    dot_general x2, matrix products, body(): jnp.dot(states_low, out_low, preferred_element_type=jnp.float32)  15.9 us
    unnamed x234, local copies, waits for them, and re-layouts  11.1 us
    dot_general x6, matrix products, contract_rows(): lax.dot_general(left, right, (((0,), (0,)), ((), ())), preferred_element_...  8.4 us
  transfers between devices with their start and end apart: 3, of which 0 were waited for; matrix products, arithmetic and copies ran while one was open for 12% of the time, Pallas kernels for 7%

profile of v16, /device:TPU:0, one launch (start us, length us, event | category | flops | bytes accessed | tf_op | source)
XLA Modules:
  0.0 263.2 jit_solution(2873839659068586216)
XLA Ops:
  7.3 2.1 convert_element_type.96
  9.7 0.8 pad_maximum_fusion.4
  10.6 0.8 pad_maximum_fusion.5
  12.4 6.1 %all_gather.19 = f32[2,4,512]{2,1,0:T(4,128)S(1)} all-gather(f32[2,4,128]{2,1,0:T(4,128)S(1)} %copy-done.68), channel_id=1, replica_groups=mesh['seq'=8,'feat'=4] {'feat'}, dimensions={2}, use_global_device_ids=true | all-gather | bytes 20480 | tf_op jit(solution)/shard_map/all_gather | solution.py:412
  20.3 1.2 rev.30
  22.1 0.9 copy.86.masks_ref
  23.1 13.1 %all_gather.18 = bf16[768,512]{1,0:T(8,128)(2,1)S(1)} all-gather(bf16[768,128]{1,0:T(8,128)(2,1)S(1)} %copy-done.32), channel_id=1, replica_groups=mesh['seq'=8,'feat'=4] {'feat'}, dimensions={1}, use_global_device_ids=true | all-gather | bytes 983040 | tf_op jit(solution)/shard_map/all_gather | solution.py:412
  36.8 9.4 %all_gather.23 = bf16[768,512]{1,0:T(8,128)(2,1)} all-gather(bf16[768,128]{1,0:T(8,128)(2,1)S(1)} %copy-done.33), channel_id=1, replica_groups=mesh['seq'=8,'feat'=4] {'feat'}, dimensions={1}, use_global_device_ids=true | all-gather | bytes 983040 | tf_op jit(solution)/shard_map/all_gather | solution.py:412
  46.8 1.2 fusion.21
  50.0 2.1 fusion.27.drive_ref
  52.5 1.0 copy-done
  53.5 1.6 pad_maximum_fusion.x_ref
  55.1 8.7 %shard_map.354.states_ref = f32[768,1536]{1,0:T(8,128)} custom-call(s32[2]{0:T(128)} %starts_ref.7, s32[2]{0:T(128)} %lengths_ref.7, f32[4,8,384]{2,1,0:T(8,128)} %pad_maximum_fusion.7.pow_ref, f32[768,768]{1,0:T(8,128)} %pad_maximum_fusion.x_ref), custom_call_target="tpu_custom_call" | custom-call | flops 11796480 | bytes 9437184 | tf_op jit(solution)/shard_map/pallas_call | solution.py:144
  63.9 8.2 %multiply_multiply_fusion.11 = (f32[768,512]{1,0:T(8,128)S(1)}, f32[768,512]{1,0:T(8,128)}) fusion(f32[512]{0:T(512)S(1)} %bitcast.463, f32[512]{0:T(512)S(1)} %bitcast.466, f32[768]{0:T(1024)S(1)} %add_rsqrt_fusion.1, f32[768]{0:T(1024)S(1)} %broadcast_multiply_fusion.6, bf16[768,512]{1,0:T(8,128)(2,1)S(1)} %copy-done.5, f32[512]{0:T(512)S(1)} %bitcast.472, ...), kind=kOutput, calls=%fused_computation.72 | convolution fusion | flops 1237057536 | bytes 10235904 | tf_op jit(solution)/shard_map/dot_general | solution.py:490
  72.1 3.5 %fusion.113 = (f32[768]{0:T(1024)S(1)}, f32[768,512]{1,0:T(8,128)S(1)}, f32[768,512]{1,0:T(8,128)}) fusion(f32[768,512]{1,0:T(8,128)S(1)} %get-tuple-element.299, bf16[768,512]{1,0:T(8,128)(2,1)S(1)} %copy-done.5, f32[512]{0:T(512)S(1)} %bitcast.477, bf16[2048,512]{1,0:T(8,128)(2,1)} %all-gather.6.cloned.1.call-done), kind=kOutput, calls=%fused_computation.363 | convolution fusion | flops 406191360 | bytes 7607296 | tf_op jit(solution)/shard_map/dot_general | solution.py:495
  76.7 0.8 copy-done.21
  78.8 1.1 copy-done.1
  79.8 1.6 pad_maximum_fusion.1.x_ref
  81.4 8.7 %shard_map.355.states_ref = f32[768,1536]{1,0:T(8,128)} custom-call(s32[2]{0:T(128)} %starts_ref.7, s32[2]{0:T(128)} %lengths_ref.7, f32[4,8,384]{2,1,0:T(8,128)} %pad_maximum_fusion.8.pow_ref, f32[768,768]{1,0:T(8,128)} %pad_maximum_fusion.1.x_ref), custom_call_target="tpu_custom_call" | custom-call | flops 11796480 | bytes 9437184 | tf_op jit(solution)/shard_map/pallas_call | solution.py:144
  90.3 7.7 %multiply_multiply_fusion.10 = (f32[768,512]{1,0:T(8,128)S(1)}, f32[768,512]{1,0:T(8,128)S(1)}, f32[768,512]{1,0:T(8,128)S(1)}) fusion(f32[512]{0:T(512)S(1)} %bitcast.469, f32[512]{0:T(512)S(1)} %bitcast.456, f32[768]{0:T(1024)S(1)} %add_rsqrt_fusion, f32[768,512]{1,0:T(8,128)S(1)} %copy-done.3, f32[768]{0:T(1024)S(1)} %broadcast_multiply_fusion.5, ...), kind=kOutput, calls=%fused_computation.70 | convolution fusion | flops 1236664320 | bytes 12595200 | tf_op jit(solution)/shard_map/dot_general | solution.py:490
  97.9 1.6 convert_reduce_fusion.1
  99.6 1.1 convolution_bitcast_fusion.4
  100.7 0.9 dynamic-slice_add_fusion.1
  101.6 2.3 fusion.115
  103.9 1.7 convolution_bitcast_fusion
  105.7 3.6 %fusion.15.g_ref = f32[768,1536]{1,0:T(8,128)} fusion(bf16[768,512]{1,0:T(8,128)(2,1)S(1)} %get-tuple-element.304, bf16[2048,512]{1,0:T(8,128)(2,1)S(1)} %copy-done.34), kind=kOutput, calls=%fused_computation.73 | convolution fusion | flops 1207959552 | bytes 7077888 | tf_op jit(solution)/shard_map/dot_general | solution.py:406
  109.3 15.4 %shard_map.356 = (bf16[768,768]{1,0:T(8,128)(2,1)}, f32[4,384]{1,0:T(4,128)}) custom-call(s32[2]{0:T(128)} %starts_ref.7, s32[2]{0:T(128)} %lengths_ref.7, f32[4,8,384]{2,1,0:T(8,128)} %pad_maximum_fusion.9.pow_ref, f32[4,384]{1,0:T(4,128)} %pad_maximum_fusion.12.coef_ref, f32[768,4]{1,0:T(8,128)} %copy.86.masks_ref, f32[768,1536]{1,0:T(8,128)} %fusion.15.g_ref, ...), custom_call_target="tpu_custom_call" | custom-call | flops 17694720 | bytes 14155776 | tf_op jit(solution)/shard_map/pallas_call | solution.py:375
  124.8 1.8 convolution_bitcast_fusion.2
  126.7 3.9 %multiply_reduce_fusion.1 = (f32[512]{0:T(512)}, f32[768]{0:T(1024)S(1)}, f32[512]{0:T(512)}, f32[768]{0:T(1024)S(1)}, f32[512]{0:T(512)}, /*index=5*/f32[768,512]{1,0:T(8,128)S(1)}) fusion(f32[768]{0:T(1024)S(1)} %copy-done.58, f32[768,512]{1,0:T(8,128)S(1)} %copy-done.3, f32[768]{0:T(1024)S(1)} %copy-done.50, f32[512]{0:T(512)S(1)} %bitcast.457, ...), kind=kOutput, calls=%fused_computation.23 | convolution fusion | flops 609874944 | bytes 6711296 | tf_op jit(solution)/shard_map/dot_general | solution.py:534
  130.6 2.7 %convert_reduce_fusion.2 = (f32[512]{0:T(512)}, bf16[768,512]{1,0:T(8,128)(2,1)S(1)}, f32[768,512]{1,0:T(8,128)}) fusion(f32[768,512]{1,0:T(8,128)S(1)} %copy-done.24, f32[768,512]{1,0:T(8,128)S(1)} %copy-done.11, f32[768]{0:T(1024)S(1)} %broadcast_multiply_fusion.3, f32[768,512]{1,0:T(8,128)S(1)} %copy-done.3, f32[768]{0:T(1024)S(1)} %copy-done.50, ...), kind=kLoop, calls=%fused_computation.24 | loop fusion | flops 6684160 | bytes 9456640 | tf_op jit(solution)/shard_map/reduce_sum | solution.py:512
  133.4 1.1 convolution_bitcast_fusion.5
  136.1 1.2 rev.31
  137.3 7.6 %fusion.116 = (bf16[768,512]{1,0:T(8,128)(2,1)S(1)}, f32[768,512]{1,0:T(8,128)}) fusion(f32[768,512]{1,0:T(8,128)} %get-tuple-element.300, bf16[768,512]{1,0:T(8,128)(2,1)} %copy-done.25, bf16[2048,512]{1,0:T(8,128)(2,1)} %all-gather.6.cloned.1.call-done, f32[768,512]{1,0:T(8,128)S(1)} %copy-done.17, f32[768,512]{1,0:T(8,128)} %get-tuple-element.301), kind=kOutput, calls=%fused_computation.366 | convolution fusion | flops 431751168 | bytes 8388608 | tf_op jit(solution)/shard_map/dot_general | solution.py:406
  145.0 0.8 convolution_bitcast_fusion.1
  147.1 3.6 %fusion.18.g_ref = f32[768,1536]{1,0:T(8,128)} fusion(bf16[768,512]{1,0:T(8,128)(2,1)S(1)} %get-tuple-element.307, bf16[2048,512]{1,0:T(8,128)(2,1)S(1)} %copy-done.107), kind=kOutput, calls=%fused_computation.76 | convolution fusion | flops 1207959552 | bytes 7077888 | tf_op jit(solution)/shard_map/dot_general | solution.py:406
  150.7 15.4 %shard_map.357 = (bf16[768,768]{1,0:T(8,128)(2,1)}, f32[4,384]{1,0:T(4,128)}) custom-call(s32[2]{0:T(128)} %starts_ref.7, s32[2]{0:T(128)} %lengths_ref.7, f32[4,8,384]{2,1,0:T(8,128)} %pad_maximum_fusion.10.pow_ref, f32[4,384]{1,0:T(4,128)} %pad_maximum_fusion.13.coef_ref, f32[768,4]{1,0:T(8,128)} %copy.86.masks_ref, f32[768,1536]{1,0:T(8,128)} %fusion.18.g_ref, ...), custom_call_target="tpu_custom_call" | custom-call | flops 17694720 | bytes 14155776 | tf_op jit(solution)/shard_map/pallas_call | solution.py:375
  166.1 1.7 convolution_bitcast_fusion.3
  169.0 0.9 copy-done.28
  171.9 2.9 %fusion.96 = (f32[512]{0:T(512)S(1)}, f32[512]{0:T(512)S(1)}, f32[512]{0:T(512)S(1)}, f32[768]{0:T(1024)S(1)}, f32[768]{0:T(1024)S(1)}, /*index=5*/f32[768,512]{1,0:T(8,128)}, f32[768,512]{1,0:T(8,128)}) fusion(f32[768]{0:T(1024)S(1)} %copy-done.54, f32[768]{0:T(1024)S(1)} %copy-done.56, bf16[768,512]{1,0:T(8,128)(2,1)S(1)} %copy-done.5, ...), kind=kOutput, calls=%fused_computation.357 | convolution fusion | flops 610268160 | bytes 7497728 | tf_op jit(solution)/shard_map/dot_general | solution.py:534
  175.1 1.8 pad_bitcast_fusion.refs_0_
  176.8 62.4 %shard_map.358 = bf16[5888,128]{1,0:T(8,128)(2,1)} custom-call(f32[5888,128]{1,0:T(8,128)} %pad_bitcast_fusion.refs_0_), custom_call_target="tpu_custom_call" | custom-call | tf_op jit(solution)/shard_map/pallas_call | solution.py:267
  239.3 1.6 convert_element_type.116
  240.9 0.8 slice_multiply_fusion.2
  245.4 3.0 %add_multiply_fusion.4 = (f32[2,512,128]{2,1,0:T(8,128)}, f32[2,512,128]{2,1,0:T(8,128)}, f32[2,512,128]{2,1,0:T(8,128)}) fusion(f32[2,512,128]{2,1,0:T(8,128)} %param.35, f32[2,512,128]{2,1,0:T(8,128)} %param.25, f32[2,512,128]{2,1,0:T(8,128)} %bitcast.436, f32[2,512,128]{2,1,0:T(8,128)} %param.30), kind=kLoop, calls=%fused_computation.109 | loop fusion | flops 1310720 | bytes 3670016 | tf_op jit(solution)/shard_map/add | solution.py:395
  248.4 1.7 add_multiply_fusion.3
  250.2 0.9 copy-done.19
  251.6 2.7 %add_multiply_fusion = (f32[2,1536,128]{2,1,0:T(8,128)}, f32[2,1536,128]{2,1,0:T(8,128)}, f32[2,1536,128]{2,1,0:T(8,128)}) fusion(f32[2,1536,128]{2,1,0:T(8,128)S(1)} %copy-done.19, f32[2,1536,128]{2,1,0:T(8,128)S(1)} %copy-done.9, f32[2,1536,128]{2,1,0:T(8,128)S(1)} %bitcast.434, f32[2,1536,128]{2,1,0:T(8,128)S(1)} %copy-done.20), kind=kLoop, calls=%fused_computation.17 | loop fusion | flops 3932160 | bytes 11010048 | tf_op jit(solution)/shard_map/add | solution.py:395
  254.3 2.4 dynamic-slice_add_fusion
  (320 shorter events, 19.5 us)
Async XLA Ops:
  7.2 42.8 %all-gather.4.cloned.1.call-start = ((), (), s32[]{:S(2)}) async-start(), calls=%async_computation | async-start | bytes 1966080 | tf_op jit(solution)/shard_map/all_gather | solution.py:412
  9.3 54.5 %all-gather.6.cloned.1.call-start = ((), (), s32[]{:S(2)}) async-start(), calls=%async_computation.1 | async-start | bytes 2621440 | tf_op jit(solution)/shard_map/all_gather | solution.py:412
  9.7 2.7 %copy-start.68 = (f32[2,4,128]{2,1,0:T(4,128)S(1)}, f32[2,4,128]{2,1,0:T(4,128)}, u32[]{:S(2)}) copy-start(f32[2,4,128]{2,1,0:T(4,128)} %param.26) | copy-start | bytes 12292
  10.5 12.5 %copy-start.32 = (bf16[768,128]{1,0:T(8,128)(2,1)S(1)}, bf16[768,128]{1,0:T(8,128)(2,1)}, u32[]{:S(2)}) copy-start(bf16[768,128]{1,0:T(8,128)(2,1)} %param.19) | copy-start | bytes 589828
  10.6 79.6 %all-gather.8.cloned.1.call-start = ((), (), s32[]{:S(2)}) async-start(), calls=%async_computation.2 | async-start | bytes 2621440 | tf_op jit(solution)/shard_map/all_gather | solution.py:412
  12.2 9.7 %copy-start.59 = (f32[1,384]{1,0:T(1,128)}, f32[1,384]{1,0:T(1,128)S(1)}, u32[]{:S(2)}) copy-start(f32[1,384]{1,0:T(1,128)S(1)} %get-tuple-element.183) | copy-start | bytes 4612
  12.2 34.0 %copy-start.35 = (f32[1,384]{1,0:T(1,128)}, f32[1,384]{1,0:T(1,128)S(1)}, u32[]{:S(2)}) copy-start(f32[1,384]{1,0:T(1,128)S(1)} %get-tuple-element.184) | copy-start | bytes 4612
  12.2 34.0 %copy-start.43 = (f32[1,384]{1,0:T(1,128)}, f32[1,384]{1,0:T(1,128)S(1)}, u32[]{:S(2)}) copy-start(f32[1,384]{1,0:T(1,128)S(1)} %get-tuple-element.185) | copy-start | bytes 4612
  18.5 45.3 %copy-start.77 = (f32[1,1,512]{2,1,0:T(1,128)}, f32[1,1,512]{2,1,0:T(1,128)S(1)}, u32[]{:S(2)}) copy-start(f32[1,1,512]{2,1,0:T(1,128)S(1)} %get-tuple-element.251) | copy-start | bytes 6148
  18.5 45.3 %copy-start.79 = (f32[1,1,512]{2,1,0:T(1,128)}, f32[1,1,512]{2,1,0:T(1,128)S(1)}, u32[]{:S(2)}) copy-start(f32[1,1,512]{2,1,0:T(1,128)S(1)} %get-tuple-element.252) | copy-start | bytes 6148
  18.6 45.3 %copy-start.99 = (f32[1,1,512]{2,1,0:T(1,128)}, f32[1,1,512]{2,1,0:T(1,128)S(1)}, u32[]{:S(2)}) copy-start(f32[1,1,512]{2,1,0:T(1,128)S(1)} %get-tuple-element.250) | copy-start | bytes 6148
  18.6 71.6 %copy-start.65 = (f32[1,1,512]{2,1,0:T(1,128)}, f32[1,1,512]{2,1,0:T(1,128)S(1)}, u32[]{:S(2)}) copy-start(f32[1,1,512]{2,1,0:T(1,128)S(1)} %get-tuple-element.248) | copy-start | bytes 6148
  18.6 71.6 %copy-start.81 = (f32[1,1,512]{2,1,0:T(1,128)}, f32[1,1,512]{2,1,0:T(1,128)S(1)}, u32[]{:S(2)}) copy-start(f32[1,1,512]{2,1,0:T(1,128)S(1)} %get-tuple-element.247) | copy-start | bytes 6148
  18.6 71.6 %copy-start.101 = (f32[1,1,512]{2,1,0:T(1,128)}, f32[1,1,512]{2,1,0:T(1,128)S(1)}, u32[]{:S(2)}) copy-start(f32[1,1,512]{2,1,0:T(1,128)S(1)} %get-tuple-element.245) | copy-start | bytes 6148
  19.3 2.8 %copy-start.37 = (f32[1,384]{1,0:T(1,128)}, f32[1,384]{1,0:T(1,128)S(1)}, u32[]{:S(2)}) copy-start(f32[1,384]{1,0:T(1,128)S(1)} %get-tuple-element.259) | copy-start | bytes 4612
  21.7 15.1 %copy-start.33 = (bf16[768,128]{1,0:T(8,128)(2,1)S(1)}, bf16[768,128]{1,0:T(8,128)(2,1)}, u32[]{:S(2)}) copy-start(bf16[768,128]{1,0:T(8,128)(2,1)} %param.20) | copy-start | bytes 589828
  36.2 11.8 %copy-start.4 = (bf16[768,512]{1,0:T(8,128)(2,1)}, bf16[768,512]{1,0:T(8,128)(2,1)S(1)}, u32[]{:S(2)}) copy-start(bf16[768,512]{1,0:T(8,128)(2,1)S(1)} %all_gather.18) | copy-start | bytes 2359300
  36.4 27.5 %copy-start.55 = (f32[768]{0:T(1024)}, f32[768]{0:T(1024)S(1)}, u32[]{:S(2)}) copy-start(f32[768]{0:T(1024)S(1)} %broadcast_multiply_fusion.6) | copy-start | bytes 9220
  36.8 27.0 %copy-start.53 = (f32[768]{0:T(1024)}, f32[768]{0:T(1024)S(1)}, u32[]{:S(2)}) copy-start(f32[768]{0:T(1024)S(1)} %add_rsqrt_fusion.1) | copy-start | bytes 9220
  55.1 8.7 %copy-start.5 = (bf16[768,512]{1,0:T(8,128)(2,1)S(1)}, bf16[768,512]{1,0:T(8,128)(2,1)}, u32[]{:S(2)}) copy-start(bf16[768,512]{1,0:T(8,128)(2,1)} %copy-done.4) | copy-start | bytes 2359300
  72.1 3.5 %copy-start.10 = (f32[768,512]{1,0:T(8,128)}, f32[768,512]{1,0:T(8,128)S(1)}, u32[]{:S(2)}) copy-start(f32[768,512]{1,0:T(8,128)S(1)} %get-tuple-element.299) | copy-start | bytes 4718596
  75.6 14.7 %copy-start.49 = (f32[768]{0:T(1024)}, f32[768]{0:T(1024)S(1)}, u32[]{:S(2)}) copy-start(f32[768]{0:T(1024)S(1)} %broadcast_multiply_fusion.5) | copy-start | bytes 9220
  75.9 14.3 %copy-start.57 = (f32[768]{0:T(1024)}, f32[768]{0:T(1024)S(1)}, u32[]{:S(2)}) copy-start(f32[768]{0:T(1024)S(1)} %add_rsqrt_fusion) | copy-start | bytes 9220
  81.4 8.8 %copy-start.3 = (f32[768,512]{1,0:T(8,128)S(1)}, f32[768,512]{1,0:T(8,128)}, u32[]{:S(2)}) copy-start(f32[768,512]{1,0:T(8,128)} %copy-done.2) | copy-start | bytes 4718596
  90.2 7.7 %copy-start.6 = (bf16[768,512]{1,0:T(8,128)(2,1)S(1)}, bf16[768,512]{1,0:T(8,128)(2,1)}, u32[]{:S(2)}) copy-start(bf16[768,512]{1,0:T(8,128)(2,1)} %all_gather.23) | copy-start | bytes 2359300
  90.2 7.7 %copy-start.34 = (bf16[2048,512]{1,0:T(8,128)(2,1)S(1)}, bf16[2048,512]{1,0:T(8,128)(2,1)}, u32[]{:S(2)}) copy-start(bf16[2048,512]{1,0:T(8,128)(2,1)} %all-gather.8.cloned.1.call-done) | copy-start | bytes 6291460
  100.7 3.3 %slice-start.2 = ((s8[4718592]{0:T(1024)(128)(4,1)}), s8[4194304]{0:T(1024)(128)(4,1)S(1)}, s32[]{:S(2)}) async-start(s8[4718592]{0:T(1024)(128)(4,1)} %bitcast.431), calls=%async_computation.5 | async-start | bytes 8388608
  126.7 3.9 %copy-start.7 = (bf16[768,512]{1,0:T(8,128)(2,1)S(1)}, bf16[768,512]{1,0:T(8,128)(2,1)}, u32[]{:S(2)}) copy-start(bf16[768,512]{1,0:T(8,128)(2,1)} %all_gather.23) | copy-start | bytes 2359300
  126.7 3.9 %copy-start.11 = (f32[768,512]{1,0:T(8,128)S(1)}, f32[768,512]{1,0:T(8,128)}, u32[]{:S(2)}) copy-start(f32[768,512]{1,0:T(8,128)} %copy-done.10) | copy-start | bytes 4718596
  126.7 3.9 %copy-start.24 = (f32[768,512]{1,0:T(8,128)S(1)}, f32[768,512]{1,0:T(8,128)}, u32[]{:S(2)}) copy-start(f32[768,512]{1,0:T(8,128)} %get-tuple-element.301) | copy-start | bytes 4718596
  130.6 14.3 %slice-start = ((s8[4718592]{0:T(1024)(128)(4,1)}), s8[524288]{0:T(1024)(128)(4,1)S(1)}, s32[]{:S(2)}) async-start(s8[4718592]{0:T(1024)(128)(4,1)} %bitcast.429), calls=%async_computation.3 | async-start | bytes 1048576
  133.4 2.6 %copy-start.87 = (f32[1,384]{1,0:T(1,128)S(1)}, f32[1,384]{1,0:T(1,128)}, u32[]{:S(2)}) copy-start(f32[1,384]{1,0:T(1,128)} %get-tuple-element.174) | copy-start | bytes 4612
  133.4 2.6 %copy-start.88 = (f32[1,384]{1,0:T(1,128)S(1)}, f32[1,384]{1,0:T(1,128)}, u32[]{:S(2)}) copy-start(f32[1,384]{1,0:T(1,128)} %get-tuple-element.176) | copy-start | bytes 4612
  133.4 3.9 %copy-start.17 = (f32[768,512]{1,0:T(8,128)S(1)}, f32[768,512]{1,0:T(8,128)}, u32[]{:S(2)}) copy-start(f32[768,512]{1,0:T(8,128)} %get-tuple-element.159) | copy-start | bytes 4718596
  136.0 8.9 %copy-start.41 = (f32[8,384]{1,0:T(8,128)}, f32[8,384]{1,0:T(8,128)S(1)}, u32[]{:S(2)}) copy-start(f32[8,384]{1,0:T(8,128)S(1)} %stack.268) | copy-start | bytes 36868
  137.3 7.6 %slice-start.1 = ((s8[4718592]{0:T(1024)(128)(4,1)}), s8[4194304]{0:T(1024)(128)(4,1)S(1)}, s32[]{:S(2)}) async-start(s8[4718592]{0:T(1024)(128)(4,1)} %bitcast.429), calls=%async_computation.4 | async-start | bytes 8388608
  171.9 2.9 %copy-start.83 = (f32[512]{0:T(512)S(1)}, f32[512]{0:T(512)}, u32[]{:S(2)}) copy-start(f32[512]{0:T(512)} %get-tuple-element.157) | copy-start | bytes 6148
  240.9 3.8 %copy-start.70 = (f32[8,128]{1,0:T(8,128)}, f32[8,128]{1,0:T(8,128)S(1)}, u32[]{:S(2)}) copy-start(f32[8,128]{1,0:T(8,128)S(1)} %slice_multiply_fusion.4) | copy-start | bytes 12292
  242.0 8.1 %copy-start.12 = (f32[3072,128]{1,0:T(8,128)}, f32[3072,128]{1,0:T(8,128)S(1)}, u32[]{:S(2)}) copy-start(f32[3072,128]{1,0:T(8,128)S(1)} %slice_multiply_fusion) | copy-start | bytes 4718596
  242.0 2.7 %copy-start.69 = (f32[2,4,128]{2,1,0:T(4,128)S(1)}, f32[2,4,128]{2,1,0:T(4,128)}, u32[]{:S(2)}) copy-start(f32[2,4,128]{2,1,0:T(4,128)} %param.26) | copy-start | bytes 12292
  242.0 2.7 %copy-start.97 = (f32[2,4,128]{2,1,0:T(4,128)S(1)}, f32[2,4,128]{2,1,0:T(4,128)}, u32[]{:S(2)}) copy-start(f32[2,4,128]{2,1,0:T(4,128)} %param.36) | copy-start | bytes 12292
  242.0 2.7 %copy-start.98 = (f32[2,4,128]{2,1,0:T(4,128)S(1)}, f32[2,4,128]{2,1,0:T(4,128)}, u32[]{:S(2)}) copy-start(f32[2,4,128]{2,1,0:T(4,128)} %param.31) | copy-start | bytes 12292
  244.6 3.7 %copy-start.15 = (f32[2,128,768]{2,1,0:T(8,128)}, f32[2,128,768]{2,1,0:T(8,128)S(1)}, u32[]{:S(2)}) copy-start(f32[2,128,768]{2,1,0:T(8,128)S(1)} %mul.6070) | copy-start | bytes 2359300
  245.4 3.0 %copy-start.14 = (f32[2,128,768]{2,1,0:T(8,128)S(1)}, f32[2,128,768]{2,1,0:T(8,128)}, u32[]{:S(2)}) copy-start(f32[2,128,768]{2,1,0:T(8,128)} %param.23) | copy-start | bytes 2359300
  245.4 3.0 %copy-start.29 = (f32[2,128,768]{2,1,0:T(8,128)S(1)}, f32[2,128,768]{2,1,0:T(8,128)}, u32[]{:S(2)}) copy-start(f32[2,128,768]{2,1,0:T(8,128)} %param.33) | copy-start | bytes 2359300
  245.4 3.0 %copy-start.30 = (f32[2,128,768]{2,1,0:T(8,128)S(1)}, f32[2,128,768]{2,1,0:T(8,128)}, u32[]{:S(2)}) copy-start(f32[2,128,768]{2,1,0:T(8,128)} %param.28) | copy-start | bytes 2359300
  248.4 2.7 %copy-start.19 = (f32[2,1536,128]{2,1,0:T(8,128)S(1)}, f32[2,1536,128]{2,1,0:T(8,128)}, u32[]{:S(2)}) copy-start(f32[2,1536,128]{2,1,0:T(8,128)} %param.34) | copy-start | bytes 4718596
  248.4 3.2 %copy-start.20 = (f32[2,1536,128]{2,1,0:T(8,128)S(1)}, f32[2,1536,128]{2,1,0:T(8,128)}, u32[]{:S(2)}) copy-start(f32[2,1536,128]{2,1,0:T(8,128)} %param.29) | copy-start | bytes 4718596
  (68 other events, 98.9 us)
Sparse Core Ops, SparseCore 0:
  10.2 26.4 all-gather.3
  38.8 22.4 all-gather.5
  63.4 22.8 all-gather.7

commit v17 on v16

--- a/solution.py
+++ b/solution.py
@@ -452,12 +452,21 @@
 
     in_all = gather_feat(input_matrix.astype(jnp.bfloat16), 1)
     rows_out = output_matrix.shape[1]
+    rows_gate = gate_matrix.shape[1]
     paired = [
-        gather_feat(jnp.concatenate([output_matrix[k], gate_matrix[k]], 0).astype(jnp.bfloat16), 1)
+        gather_feat(
+            jnp.concatenate(
+                [output_matrix[k].astype(jnp.bfloat16), gate_matrix[k].astype(jnp.bfloat16)]
+                + ([cotangent] if k == layers - 1 else []),
+                0,
+            ),
+            1,
+        )
         for k in range(layers)
     ]
     out_all = [pair[:rows_out] for pair in paired]
-    gate_all = [pair[rows_out:] for pair in paired]
+    gate_all = [pair[rows_out : rows_out + rows_gate] for pair in paired]
+    cotangent_all = paired[-1][rows_out + rows_gate :]
     feature_all = gather_feat(feature_vectors, 2)
     stream = gather_feat(activations_in, 1).astype(jnp.float32)
 
@@ -496,7 +505,7 @@
         saved.append((scale, unit, normed_low, drive, states, states_low, mixed, act, act_low, pre))
         stream = stream + act * jax.nn.sigmoid(pre)
 
-    grad = gather_feat(cotangent, 1).astype(jnp.float32) * alive[:, None]
+    grad = cotangent_all.astype(jnp.float32) * alive[:, None]
     layer_grads = [None] * layers
     for layer in reversed(range(layers)):
         scale, unit, normed_low, drive, states, states_low, mixed, act, act_low, pre = saved[layer]

time: 264 us -> 264 us (level)
  waiting for transfers between devices: 0.05 us -> 9.87 us
  blocking collectives: 28.6 us -> 19.2 us
    all_gather x3, waiting for transfers between devices: 0.01 us -> 9.82 us  [gather_feat(): return lax.all_gather(value, 'feat', axis=axis, tiled=True)]
    all_gather x3 -> x2, blocking collectives: 28.6 us -> 19.2 us  [gather_feat(): return lax.all_gather(value, 'feat', axis=axis, tiled=True)]
    unnamed x234 -> x232, local copies, waits for them, and re-layouts: 11.1 us -> 11.1 us
  transfers between devices with their start and end apart: 3 -> 3, of which waited for: 0 -> 2; matrix products, arithmetic and copies ran while one was open for 12% -> 12% of each run, Pallas kernels for 7% -> 7%
where the time goes in v17:
time: 264 us
  Pallas kernels  110 us (42%)
  matrix products  56.3 us (21%)
  other arithmetic  35.9 us (14%)
  blocking collectives  19.2 us (7%)
  local copies, waits for them, and re-layouts  17.4 us (7%)
  between operations  15.3 us (6%)
  waiting for transfers between devices  9.87 us (4%)
    pallas_call x1, Pallas kernels, ring_sum(): pl.pallas_call(lambda *refs: ring_sum_kernel(n, *refs), out_shape=jax.Sha...  61.3 us
    pallas_call x2, Pallas kernels, adjoint(): pl.pallas_call(adjoint_kernel, out_shape=(jax.ShapeDtypeStruct((count, 2...  30.8 us
    all_gather x2, blocking collectives, gather_feat(): return lax.all_gather(value, 'feat', axis=axis, tiled=True)  19.2 us
    pallas_call x2, Pallas kernels, recurrence(): pl.pallas_call(recurrence_kernel, out_shape=jax.ShapeDtypeStruct((count,...  17.5 us
    dot_general x4, matrix products, contract_cols(): lax.dot_general(left, right, (((1,), (1,)), ((), ())), preferred_element_...  17.2 us
    dot_general x2, matrix products, body(): jnp.dot(states_low, out_low, preferred_element_type=jnp.float32)  15.9 us
    unnamed x232, local copies, waits for them, and re-layouts  11.1 us
    all_gather x3, waiting for transfers between devices, gather_feat(): return lax.all_gather(value, 'feat', axis=axis, tiled=True)  9.82 us
  transfers between devices with their start and end apart: 3, of which 2 were waited for; matrix products, arithmetic and copies ran while one was open for 12% of the time, Pallas kernels for 7%

profile of v17, /device:TPU:0, one launch (start us, length us, event | category | flops | bytes accessed | tf_op | source)
XLA Modules:
  0.0 263.7 jit_solution(11861292316075654955)
XLA Ops:
  7.3 2.1 convert_element_type.110
  9.7 0.8 pad_maximum_fusion.5
  10.6 0.9 pad_maximum_fusion.4
  12.4 6.1 %all_gather.16 = f32[2,4,512]{2,1,0:T(4,128)S(1)} all-gather(f32[2,4,128]{2,1,0:T(4,128)S(1)} %copy-done.67), channel_id=1, replica_groups=mesh['seq'=8,'feat'=4] {'feat'}, dimensions={2}, use_global_device_ids=true | all-gather | bytes 20480 | tf_op jit(solution)/shard_map/all_gather | solution.py:412
  20.4 1.2 rev.30
  22.1 0.9 copy.86.masks_ref
  23.1 13.1 %all_gather.15 = bf16[768,512]{1,0:T(8,128)(2,1)S(1)} all-gather(bf16[768,128]{1,0:T(8,128)(2,1)S(1)} %copy-done.32), channel_id=1, replica_groups=mesh['seq'=8,'feat'=4] {'feat'}, dimensions={1}, use_global_device_ids=true | all-gather | bytes 983040 | tf_op jit(solution)/shard_map/all_gather | solution.py:412
  37.4 1.2 fusion.21
  40.6 2.1 fusion.27.drive_ref
  43.1 1.0 copy-done
  44.2 1.6 pad_maximum_fusion.x_ref
  45.8 8.8 %shard_map.354.states_ref = f32[768,1536]{1,0:T(8,128)} custom-call(s32[2]{0:T(128)} %starts_ref.7, s32[2]{0:T(128)} %lengths_ref.7, f32[4,8,384]{2,1,0:T(8,128)} %pad_maximum_fusion.7.pow_ref, f32[768,768]{1,0:T(8,128)} %pad_maximum_fusion.x_ref), custom_call_target="tpu_custom_call" | custom-call | flops 11796480 | bytes 9437184 | tf_op jit(solution)/shard_map/pallas_call | solution.py:144
  54.6 6.7 %all-gather.6.cloned.1.call-done = bf16[2048,512]{1,0:T(8,128)(2,1)} async-done(((bf16[2048,128]{1,0:T(8,128)(2,1)}), bf16[2048,512]{1,0:T(8,128)(2,1)}) %all-gather.6.cloned.1.call-update) | async-done | bytes 2097168 | tf_op jit(solution)/shard_map/all_gather | solution.py:412
  61.3 8.2 %multiply_multiply_fusion.11 = (f32[768,512]{1,0:T(8,128)S(1)}, f32[768,512]{1,0:T(8,128)}) fusion(f32[512]{0:T(512)S(1)} %bitcast.463, f32[512]{0:T(512)S(1)} %bitcast.466, f32[768]{0:T(1024)S(1)} %add_rsqrt_fusion.1, f32[768]{0:T(1024)S(1)} %broadcast_multiply_fusion.6, bf16[768,512]{1,0:T(8,128)(2,1)S(1)} %copy-done.5, f32[512]{0:T(512)S(1)} %bitcast.472, ...), kind=kOutput, calls=%fused_computation.72 | convolution fusion | flops 1237057536 | bytes 10235904 | tf_op jit(solution)/shard_map/dot_general | solution.py:499
  69.5 3.5 %fusion.113 = (f32[768]{0:T(1024)S(1)}, f32[768,512]{1,0:T(8,128)S(1)}, f32[768,512]{1,0:T(8,128)}) fusion(f32[768,512]{1,0:T(8,128)S(1)} %get-tuple-element.299, bf16[768,512]{1,0:T(8,128)(2,1)S(1)} %copy-done.5, f32[512]{0:T(512)S(1)} %bitcast.477, bf16[2048,512]{1,0:T(8,128)(2,1)} %all-gather.6.cloned.1.call-done), kind=kOutput, calls=%fused_computation.363 | convolution fusion | flops 406191360 | bytes 7607296 | tf_op jit(solution)/shard_map/dot_general | solution.py:504
  74.1 0.9 copy-done.19
  76.2 1.1 copy-done.1
  77.3 1.6 pad_maximum_fusion.1.x_ref
  78.9 8.7 %shard_map.355.states_ref = f32[768,1536]{1,0:T(8,128)} custom-call(s32[2]{0:T(128)} %starts_ref.7, s32[2]{0:T(128)} %lengths_ref.7, f32[4,8,384]{2,1,0:T(8,128)} %pad_maximum_fusion.8.pow_ref, f32[768,768]{1,0:T(8,128)} %pad_maximum_fusion.1.x_ref), custom_call_target="tpu_custom_call" | custom-call | flops 11796480 | bytes 9437184 | tf_op jit(solution)/shard_map/pallas_call | solution.py:144
  87.7 3.2 %all-gather.8.cloned.1.call-done = bf16[2816,512]{1,0:T(8,128)(2,1)} async-done(((bf16[2816,128]{1,0:T(8,128)(2,1)}), bf16[2816,512]{1,0:T(8,128)(2,1)}) %all-gather.8.cloned.1.call-update) | async-done | bytes 2883600 | tf_op jit(solution)/shard_map/all_gather | solution.py:412
  90.9 7.6 %multiply_multiply_fusion.10 = (f32[768,512]{1,0:T(8,128)S(1)}, f32[768,512]{1,0:T(8,128)S(1)}, f32[768,512]{1,0:T(8,128)S(1)}) fusion(f32[512]{0:T(512)S(1)} %bitcast.469, f32[512]{0:T(512)S(1)} %bitcast.456, f32[768]{0:T(1024)S(1)} %add_rsqrt_fusion, f32[768,512]{1,0:T(8,128)S(1)} %copy-done.3, f32[768]{0:T(1024)S(1)} %broadcast_multiply_fusion.5, ...), kind=kOutput, calls=%fused_computation.70 | convolution fusion | flops 1236664320 | bytes 12595200 | tf_op jit(solution)/shard_map/dot_general | solution.py:499
  98.5 1.6 convert_reduce_fusion.1
  100.1 1.1 convolution_bitcast_fusion.4
  101.3 0.9 dynamic-slice_add_fusion.1
  102.2 2.3 fusion.115
  104.5 1.7 convolution_bitcast_fusion
  106.2 3.7 %fusion.15.g_ref = f32[768,1536]{1,0:T(8,128)} fusion(bf16[768,512]{1,0:T(8,128)(2,1)S(1)} %get-tuple-element.304, bf16[2816,512]{1,0:T(8,128)(2,1)S(1)} %copy-done.30), kind=kOutput, calls=%fused_computation.73 | convolution fusion | flops 1207959552 | bytes 7077888 | tf_op jit(solution)/shard_map/dot_general | solution.py:406
  109.9 15.4 %shard_map.356 = (bf16[768,768]{1,0:T(8,128)(2,1)}, f32[4,384]{1,0:T(4,128)}) custom-call(s32[2]{0:T(128)} %starts_ref.7, s32[2]{0:T(128)} %lengths_ref.7, f32[4,8,384]{2,1,0:T(8,128)} %pad_maximum_fusion.9.pow_ref, f32[4,384]{1,0:T(4,128)} %pad_maximum_fusion.12.coef_ref, f32[768,4]{1,0:T(8,128)} %copy.86.masks_ref, f32[768,1536]{1,0:T(8,128)} %fusion.15.g_ref, ...), custom_call_target="tpu_custom_call" | custom-call | flops 17694720 | bytes 14155776 | tf_op jit(solution)/shard_map/pallas_call | solution.py:375
  125.4 1.8 convolution_bitcast_fusion.2
  127.3 3.9 %multiply_reduce_fusion.1 = (f32[512]{0:T(512)}, f32[768]{0:T(1024)S(1)}, f32[512]{0:T(512)}, f32[768]{0:T(1024)S(1)}, f32[512]{0:T(512)}, /*index=5*/f32[768,512]{1,0:T(8,128)S(1)}) fusion(f32[768]{0:T(1024)S(1)} %copy-done.57, f32[768,512]{1,0:T(8,128)S(1)} %copy-done.3, f32[768]{0:T(1024)S(1)} %copy-done.49, f32[512]{0:T(512)S(1)} %bitcast.457, ...), kind=kOutput, calls=%fused_computation.23 | convolution fusion | flops 609874944 | bytes 6711296 | tf_op jit(solution)/shard_map/dot_general | solution.py:543
  131.2 3.7 %convert_reduce_fusion.2 = (f32[512]{0:T(512)}, bf16[768,512]{1,0:T(8,128)(2,1)S(1)}, f32[768,512]{1,0:T(8,128)}) fusion(f32[768,512]{1,0:T(8,128)S(1)} %copy-done.22, f32[768,512]{1,0:T(8,128)S(1)} %copy-done.9, f32[768]{0:T(1024)S(1)} %broadcast_multiply_fusion.3, f32[768,512]{1,0:T(8,128)S(1)} %copy-done.3, f32[768]{0:T(1024)S(1)} %copy-done.49, ...), kind=kLoop, calls=%fused_computation.24 | loop fusion | flops 6684160 | bytes 9456640 | tf_op jit(solution)/shard_map/reduce_sum | solution.py:521
  135.1 1.2 convolution_bitcast_fusion.5
  137.7 1.2 rev.31
  138.9 7.6 %fusion.116 = (bf16[768,512]{1,0:T(8,128)(2,1)S(1)}, f32[768,512]{1,0:T(8,128)}) fusion(f32[768,512]{1,0:T(8,128)} %get-tuple-element.300, bf16[768,512]{1,0:T(8,128)(2,1)} %copy-done.23, bf16[2048,512]{1,0:T(8,128)(2,1)} %all-gather.6.cloned.1.call-done, f32[768,512]{1,0:T(8,128)S(1)} %copy-done.15, f32[768,512]{1,0:T(8,128)} %get-tuple-element.301), kind=kOutput, calls=%fused_computation.366 | convolution fusion | flops 431751168 | bytes 8388608 | tf_op jit(solution)/shard_map/dot_general | solution.py:406
  148.8 3.6 %fusion.18.g_ref = f32[768,1536]{1,0:T(8,128)} fusion(bf16[768,512]{1,0:T(8,128)(2,1)S(1)} %get-tuple-element.307, bf16[2048,512]{1,0:T(8,128)(2,1)S(1)} %copy-done.106), kind=kOutput, calls=%fused_computation.76 | convolution fusion | flops 1207959552 | bytes 7077888 | tf_op jit(solution)/shard_map/dot_general | solution.py:406
  152.4 15.4 %shard_map.357 = (bf16[768,768]{1,0:T(8,128)(2,1)}, f32[4,384]{1,0:T(4,128)}) custom-call(s32[2]{0:T(128)} %starts_ref.7, s32[2]{0:T(128)} %lengths_ref.7, f32[4,8,384]{2,1,0:T(8,128)} %pad_maximum_fusion.10.pow_ref, f32[4,384]{1,0:T(4,128)} %pad_maximum_fusion.13.coef_ref, f32[768,4]{1,0:T(8,128)} %copy.86.masks_ref, f32[768,1536]{1,0:T(8,128)} %fusion.18.g_ref, ...), custom_call_target="tpu_custom_call" | custom-call | flops 17694720 | bytes 14155776 | tf_op jit(solution)/shard_map/pallas_call | solution.py:375
  167.8 1.7 convolution_bitcast_fusion.3
  170.7 0.9 copy-done.26
  173.5 2.9 %fusion.96 = (f32[512]{0:T(512)S(1)}, f32[512]{0:T(512)S(1)}, f32[512]{0:T(512)S(1)}, f32[768]{0:T(1024)S(1)}, f32[768]{0:T(1024)S(1)}, /*index=5*/f32[768,512]{1,0:T(8,128)}, f32[768,512]{1,0:T(8,128)}) fusion(f32[768]{0:T(1024)S(1)} %copy-done.53, f32[768]{0:T(1024)S(1)} %copy-done.55, bf16[768,512]{1,0:T(8,128)(2,1)S(1)} %copy-done.5, ...), kind=kOutput, calls=%fused_computation.357 | convolution fusion | flops 610268160 | bytes 7497728 | tf_op jit(solution)/shard_map/dot_general | solution.py:543
  176.7 1.8 pad_bitcast_fusion.refs_0_
  178.5 61.3 %shard_map.358 = bf16[5888,128]{1,0:T(8,128)(2,1)} custom-call(f32[5888,128]{1,0:T(8,128)} %pad_bitcast_fusion.refs_0_), custom_call_target="tpu_custom_call" | custom-call | tf_op jit(solution)/shard_map/pallas_call | solution.py:267
  239.8 1.6 convert_element_type.134
  241.4 0.8 slice_multiply_fusion.2
  245.9 3.0 %add_multiply_fusion.4 = (f32[2,512,128]{2,1,0:T(8,128)}, f32[2,512,128]{2,1,0:T(8,128)}, f32[2,512,128]{2,1,0:T(8,128)}) fusion(f32[2,512,128]{2,1,0:T(8,128)} %param.35, f32[2,512,128]{2,1,0:T(8,128)} %param.25, f32[2,512,128]{2,1,0:T(8,128)} %bitcast.436, f32[2,512,128]{2,1,0:T(8,128)} %param.30), kind=kLoop, calls=%fused_computation.109 | loop fusion | flops 1310720 | bytes 3670016 | tf_op jit(solution)/shard_map/add | solution.py:395
  248.9 1.7 add_multiply_fusion.3
  250.7 0.9 copy-done.17
  252.1 2.7 %add_multiply_fusion = (f32[2,1536,128]{2,1,0:T(8,128)}, f32[2,1536,128]{2,1,0:T(8,128)}, f32[2,1536,128]{2,1,0:T(8,128)}) fusion(f32[2,1536,128]{2,1,0:T(8,128)S(1)} %copy-done.17, f32[2,1536,128]{2,1,0:T(8,128)S(1)} %copy-done.7, f32[2,1536,128]{2,1,0:T(8,128)S(1)} %bitcast.434, f32[2,1536,128]{2,1,0:T(8,128)S(1)} %copy-done.18), kind=kLoop, calls=%fused_computation.17 | loop fusion | flops 3932160 | bytes 11010048 | tf_op jit(solution)/shard_map/add | solution.py:395
  254.8 2.4 dynamic-slice_add_fusion
  (317 shorter events, 20.2 us)
Async XLA Ops:
  7.2 33.4 %all-gather.4.cloned.1.call-start = ((), (), s32[]{:S(2)}) async-start(), calls=%async_computation | async-start | bytes 1966080 | tf_op jit(solution)/shard_map/all_gather | solution.py:412
  9.3 51.9 %all-gather.6.cloned.1.call-start = ((), (), s32[]{:S(2)}) async-start(), calls=%async_computation.1 | async-start | bytes 2621440 | tf_op jit(solution)/shard_map/all_gather | solution.py:412
  10.5 80.3 %all-gather.8.cloned.1.call-start = ((), (), s32[]{:S(2)}) async-start(), calls=%async_computation.2 | async-start | bytes 3604480 | tf_op jit(solution)/shard_map/all_gather | solution.py:412
  10.6 12.5 %copy-start.32 = (bf16[768,128]{1,0:T(8,128)(2,1)S(1)}, bf16[768,128]{1,0:T(8,128)(2,1)}, u32[]{:S(2)}) copy-start(bf16[768,128]{1,0:T(8,128)(2,1)} %param.19) | copy-start | bytes 589828
  12.2 7.3 %copy-start.58 = (f32[1,384]{1,0:T(1,128)}, f32[1,384]{1,0:T(1,128)S(1)}, u32[]{:S(2)}) copy-start(f32[1,384]{1,0:T(1,128)S(1)} %get-tuple-element.183) | copy-start | bytes 4612
  12.2 24.6 %copy-start.42 = (f32[1,384]{1,0:T(1,128)}, f32[1,384]{1,0:T(1,128)S(1)}, u32[]{:S(2)}) copy-start(f32[1,384]{1,0:T(1,128)S(1)} %get-tuple-element.185) | copy-start | bytes 4612
  12.4 89.8 %copy-start.40 = (f32[768]{0:T(1024)}, f32[768]{0:T(1024)S(1)}, u32[]{:S(2)}) copy-start(f32[768]{0:T(1024)S(1)} %get-tuple-element.298) | copy-start | bytes 9220
  18.6 42.7 %copy-start.76 = (f32[1,1,512]{2,1,0:T(1,128)}, f32[1,1,512]{2,1,0:T(1,128)S(1)}, u32[]{:S(2)}) copy-start(f32[1,1,512]{2,1,0:T(1,128)S(1)} %get-tuple-element.251) | copy-start | bytes 6148
  18.6 42.7 %copy-start.78 = (f32[1,1,512]{2,1,0:T(1,128)}, f32[1,1,512]{2,1,0:T(1,128)S(1)}, u32[]{:S(2)}) copy-start(f32[1,1,512]{2,1,0:T(1,128)S(1)} %get-tuple-element.252) | copy-start | bytes 6148
  18.6 42.7 %copy-start.98 = (f32[1,1,512]{2,1,0:T(1,128)}, f32[1,1,512]{2,1,0:T(1,128)S(1)}, u32[]{:S(2)}) copy-start(f32[1,1,512]{2,1,0:T(1,128)S(1)} %get-tuple-element.250) | copy-start | bytes 6148
  18.6 72.2 %copy-start.64 = (f32[1,1,512]{2,1,0:T(1,128)}, f32[1,1,512]{2,1,0:T(1,128)S(1)}, u32[]{:S(2)}) copy-start(f32[1,1,512]{2,1,0:T(1,128)S(1)} %get-tuple-element.248) | copy-start | bytes 6148
  18.6 72.2 %copy-start.80 = (f32[1,1,512]{2,1,0:T(1,128)}, f32[1,1,512]{2,1,0:T(1,128)S(1)}, u32[]{:S(2)}) copy-start(f32[1,1,512]{2,1,0:T(1,128)S(1)} %get-tuple-element.247) | copy-start | bytes 6148
  18.6 72.2 %copy-start.100 = (f32[1,1,512]{2,1,0:T(1,128)}, f32[1,1,512]{2,1,0:T(1,128)S(1)}, u32[]{:S(2)}) copy-start(f32[1,1,512]{2,1,0:T(1,128)S(1)} %get-tuple-element.245) | copy-start | bytes 6148
  19.3 2.8 %copy-start.33 = (f32[1,384]{1,0:T(1,128)}, f32[1,384]{1,0:T(1,128)S(1)}, u32[]{:S(2)}) copy-start(f32[1,384]{1,0:T(1,128)S(1)} %get-tuple-element.259) | copy-start | bytes 4612
  19.3 17.4 %copy-start.44 = (f32[1,384]{1,0:T(1,128)}, f32[1,384]{1,0:T(1,128)S(1)}, u32[]{:S(2)}) copy-start(f32[1,384]{1,0:T(1,128)S(1)} %get-tuple-element.258) | copy-start | bytes 4612
  36.2 2.5 copy-start.4
  36.4 24.9 %copy-start.54 = (f32[768]{0:T(1024)}, f32[768]{0:T(1024)S(1)}, u32[]{:S(2)}) copy-start(f32[768]{0:T(1024)S(1)} %broadcast_multiply_fusion.6) | copy-start | bytes 9220
  36.8 24.5 %copy-start.52 = (f32[768]{0:T(1024)}, f32[768]{0:T(1024)S(1)}, u32[]{:S(2)}) copy-start(f32[768]{0:T(1024)S(1)} %add_rsqrt_fusion.1) | copy-start | bytes 9220
  45.8 15.5 %copy-start.5 = (bf16[768,512]{1,0:T(8,128)(2,1)S(1)}, bf16[768,512]{1,0:T(8,128)(2,1)}, u32[]{:S(2)}) copy-start(bf16[768,512]{1,0:T(8,128)(2,1)} %copy-done.4) | copy-start | bytes 2359300
  69.5 3.5 %copy-start.8 = (f32[768,512]{1,0:T(8,128)}, f32[768,512]{1,0:T(8,128)S(1)}, u32[]{:S(2)}) copy-start(f32[768,512]{1,0:T(8,128)S(1)} %get-tuple-element.299) | copy-start | bytes 4718596
  73.0 17.8 %copy-start.48 = (f32[768]{0:T(1024)}, f32[768]{0:T(1024)S(1)}, u32[]{:S(2)}) copy-start(f32[768]{0:T(1024)S(1)} %broadcast_multiply_fusion.5) | copy-start | bytes 9220
  73.4 17.5 %copy-start.56 = (f32[768]{0:T(1024)}, f32[768]{0:T(1024)S(1)}, u32[]{:S(2)}) copy-start(f32[768]{0:T(1024)S(1)} %add_rsqrt_fusion) | copy-start | bytes 9220
  78.9 11.9 %copy-start.3 = (f32[768,512]{1,0:T(8,128)S(1)}, f32[768,512]{1,0:T(8,128)}, u32[]{:S(2)}) copy-start(f32[768,512]{1,0:T(8,128)} %copy-done.2) | copy-start | bytes 4718596
  90.8 7.6 %copy-start.30 = (bf16[2816,512]{1,0:T(8,128)(2,1)S(1)}, bf16[2816,512]{1,0:T(8,128)(2,1)}, u32[]{:S(2)}) copy-start(bf16[2816,512]{1,0:T(8,128)(2,1)} %all-gather.8.cloned.1.call-done) | copy-start | bytes 8650756
  101.3 3.3 %slice-start.2 = ((s8[4718592]{0:T(1024)(128)(4,1)}), s8[4194304]{0:T(1024)(128)(4,1)S(1)}, s32[]{:S(2)}) async-start(s8[4718592]{0:T(1024)(128)(4,1)} %bitcast.431), calls=%async_computation.5 | async-start | bytes 8388608
  127.3 3.9 %copy-start.9 = (f32[768,512]{1,0:T(8,128)S(1)}, f32[768,512]{1,0:T(8,128)}, u32[]{:S(2)}) copy-start(f32[768,512]{1,0:T(8,128)} %copy-done.8) | copy-start | bytes 4718596
  127.3 3.9 %copy-start.22 = (f32[768,512]{1,0:T(8,128)S(1)}, f32[768,512]{1,0:T(8,128)}, u32[]{:S(2)}) copy-start(f32[768,512]{1,0:T(8,128)} %get-tuple-element.301) | copy-start | bytes 4718596
  127.3 3.9 %copy-start.41 = (f32[768]{0:T(1024)S(1)}, f32[768]{0:T(1024)}, u32[]{:S(2)}) copy-start(f32[768]{0:T(1024)} %copy-done.40) | copy-start | bytes 9220
  131.2 15.4 %slice-start = ((s8[4718592]{0:T(1024)(128)(4,1)}), s8[524288]{0:T(1024)(128)(4,1)S(1)}, s32[]{:S(2)}) async-start(s8[4718592]{0:T(1024)(128)(4,1)} %bitcast.429), calls=%async_computation.3 | async-start | bytes 1048576
  135.0 2.6 copy-start.86
  135.0 2.6 copy-start.87
  135.0 2.6 copy-start.88
  135.0 2.6 copy-start.89
  135.1 3.9 %copy-start.15 = (f32[768,512]{1,0:T(8,128)S(1)}, f32[768,512]{1,0:T(8,128)}, u32[]{:S(2)}) copy-start(f32[768,512]{1,0:T(8,128)} %get-tuple-element.159) | copy-start | bytes 4718596
  137.7 8.9 %copy-start.38 = (f32[8,384]{1,0:T(8,128)}, f32[8,384]{1,0:T(8,128)S(1)}, u32[]{:S(2)}) copy-start(f32[8,384]{1,0:T(8,128)S(1)} %stack.268) | copy-start | bytes 36868
  138.9 7.6 %slice-start.1 = ((s8[4718592]{0:T(1024)(128)(4,1)}), s8[4194304]{0:T(1024)(128)(4,1)S(1)}, s32[]{:S(2)}) async-start(s8[4718592]{0:T(1024)(128)(4,1)} %bitcast.429), calls=%async_computation.4 | async-start | bytes 8388608
  173.5 2.9 %copy-start.82 = (f32[512]{0:T(512)S(1)}, f32[512]{0:T(512)}, u32[]{:S(2)}) copy-start(f32[512]{0:T(512)} %get-tuple-element.157) | copy-start | bytes 6148
  241.4 3.8 %copy-start.69 = (f32[8,128]{1,0:T(8,128)}, f32[8,128]{1,0:T(8,128)S(1)}, u32[]{:S(2)}) copy-start(f32[8,128]{1,0:T(8,128)S(1)} %slice_multiply_fusion.4) | copy-start | bytes 12292
  242.5 8.1 %copy-start.10 = (f32[3072,128]{1,0:T(8,128)}, f32[3072,128]{1,0:T(8,128)S(1)}, u32[]{:S(2)}) copy-start(f32[3072,128]{1,0:T(8,128)S(1)} %slice_multiply_fusion) | copy-start | bytes 4718596
  242.5 2.7 %copy-start.68 = (f32[2,4,128]{2,1,0:T(4,128)S(1)}, f32[2,4,128]{2,1,0:T(4,128)}, u32[]{:S(2)}) copy-start(f32[2,4,128]{2,1,0:T(4,128)} %param.26) | copy-start | bytes 12292
  242.5 2.7 %copy-start.96 = (f32[2,4,128]{2,1,0:T(4,128)S(1)}, f32[2,4,128]{2,1,0:T(4,128)}, u32[]{:S(2)}) copy-start(f32[2,4,128]{2,1,0:T(4,128)} %param.36) | copy-start | bytes 12292
  242.5 2.7 %copy-start.97 = (f32[2,4,128]{2,1,0:T(4,128)S(1)}, f32[2,4,128]{2,1,0:T(4,128)}, u32[]{:S(2)}) copy-start(f32[2,4,128]{2,1,0:T(4,128)} %param.31) | copy-start | bytes 12292
  245.2 3.7 %copy-start.13 = (f32[2,128,768]{2,1,0:T(8,128)}, f32[2,128,768]{2,1,0:T(8,128)S(1)}, u32[]{:S(2)}) copy-start(f32[2,128,768]{2,1,0:T(8,128)S(1)} %mul.6070) | copy-start | bytes 2359300
  245.9 3.0 %copy-start.12 = (f32[2,128,768]{2,1,0:T(8,128)S(1)}, f32[2,128,768]{2,1,0:T(8,128)}, u32[]{:S(2)}) copy-start(f32[2,128,768]{2,1,0:T(8,128)} %param.23) | copy-start | bytes 2359300
  245.9 3.0 %copy-start.27 = (f32[2,128,768]{2,1,0:T(8,128)S(1)}, f32[2,128,768]{2,1,0:T(8,128)}, u32[]{:S(2)}) copy-start(f32[2,128,768]{2,1,0:T(8,128)} %param.33) | copy-start | bytes 2359300
  245.9 3.0 %copy-start.28 = (f32[2,128,768]{2,1,0:T(8,128)S(1)}, f32[2,128,768]{2,1,0:T(8,128)}, u32[]{:S(2)}) copy-start(f32[2,128,768]{2,1,0:T(8,128)} %param.28) | copy-start | bytes 2359300
  248.9 2.7 %copy-start.17 = (f32[2,1536,128]{2,1,0:T(8,128)S(1)}, f32[2,1536,128]{2,1,0:T(8,128)}, u32[]{:S(2)}) copy-start(f32[2,1536,128]{2,1,0:T(8,128)} %param.34) | copy-start | bytes 4718596
  248.9 3.2 %copy-start.18 = (f32[2,1536,128]{2,1,0:T(8,128)S(1)}, f32[2,1536,128]{2,1,0:T(8,128)}, u32[]{:S(2)}) copy-start(f32[2,1536,128]{2,1,0:T(8,128)} %param.29) | copy-start | bytes 4718596
  (67 other events, 91.8 us)
Sparse Core Ops, SparseCore 0:
  10.2 26.4 all-gather.3
  38.8 22.4 all-gather.5
  63.4 27.3 all-gather.7

commit v18 on v15

--- a/solution.py
+++ b/solution.py
@@ -412,6 +412,20 @@
     return lax.all_gather(value, "feat", axis=axis, tiled=True)
 
 
+def split_exact(value):
+    high = lax.reduce_precision(value, exponent_bits=8, mantissa_bits=7)
+    rest = value - high
+    middle = lax.reduce_precision(rest, exponent_bits=8, mantissa_bits=7)
+    little = rest - middle
+    return jnp.concatenate([high, middle, little], 0).astype(jnp.bfloat16)
+
+
+def join_exact(pieces):
+    third = pieces.shape[0] // 3
+    pieces = pieces.astype(jnp.float32)
+    return pieces[:third] + (pieces[third : 2 * third] + pieces[2 * third :])
+
+
 def body(
     activations_in,
     cotangent,
@@ -450,11 +464,32 @@
     mask_columns = jnp.stack([alive, carry_prev, carry_next, jnp.zeros_like(alive)], 1)
 
 
-    in_all = gather_feat(input_matrix.astype(jnp.bfloat16), 1)
-    out_all = [gather_feat(output_matrix[k].astype(jnp.bfloat16), 1) for k in range(layers)]
-    gate_all = gather_feat(gate_matrix.astype(jnp.bfloat16), 2)
-    feature_all = gather_feat(feature_vectors, 2)
-    stream = gather_feat(activations_in, 1).astype(jnp.float32)
+    def low(value):
+        return value.astype(jnp.bfloat16)
+
+    feature_pieces = split_exact(feature_vectors.reshape(-1, shard))
+    feature_rows = feature_pieces.shape[0]
+    feature_pad = -(-feature_rows // 16) * 16
+    feature_pieces = jnp.pad(feature_pieces, ((0, feature_pad - feature_rows), (0, 0)))
+    groups = [[low(input_matrix[0].T), activations_in, feature_pieces]]
+    for k in range(layers):
+        tail = [low(input_matrix[k + 1].T)] if k + 1 < layers else [cotangent]
+        groups.append([low(output_matrix[k]), low(gate_matrix[k])] + tail)
+    gathered = []
+    for group in groups:
+        whole = gather_feat(jnp.concatenate(group, 0), 1)
+        start = 0
+        pieces = []
+        for piece in group:
+            pieces.append(whole[start : start + piece.shape[0]])
+            start += piece.shape[0]
+        gathered.append(pieces)
+    in_all = [gathered[0][0]] + [gathered[k][2] for k in range(1, layers)]
+    out_all = [gathered[k + 1][0] for k in range(layers)]
+    gate_all = [gathered[k + 1][1] for k in range(layers)]
+    cotangent_all = gathered[layers][2]
+    stream = gathered[0][1].astype(jnp.float32)
+    feature_all = join_exact(gathered[0][2][:feature_rows]).reshape(feature_vectors.shape[:-1] + (-1,))
 
     saved = []
     for layer in range(layers):
@@ -469,7 +504,7 @@
         unit = spread * scale
         normed = unit * feature_row[0] + feature_row[1]
         normed_low = normed.astype(jnp.bfloat16)
-        drive = jnp.dot(normed_low, in_low, preferred_element_type=jnp.float32)
+        drive = contract_cols(normed_low, in_low)
         drive_re = drive[:, :width]
         drive_im = drive[:, width:]
         source = jnp.concatenate(
@@ -491,7 +526,7 @@
         saved.append((scale, unit, normed_low, drive, states, states_low, mixed, act, act_low, pre))
         stream = stream + act * jax.nn.sigmoid(pre)
 
-    grad = gather_feat(cotangent, 1).astype(jnp.float32) * alive[:, None]
+    grad = cotangent_all.astype(jnp.float32) * alive[:, None]
     layer_grads = [None] * layers
     for layer in reversed(range(layers)):
         scale, unit, normed_low, drive, states, states_low, mixed, act, act_low, pre = saved[layer]
@@ -527,7 +562,7 @@
         row_grad = jax.vjp(coefficients, state_row)[1]((gp_re, gp_im, gf_re, gf_im))[0]
         in_grad = contract_rows(mine(normed_low), drive_low)
         normed_grad = mixed_grad * feature_row[2] + jnp.dot(
-            drive_low, in_low.T, preferred_element_type=jnp.float32
+            drive_low, in_low, preferred_element_type=jnp.float32
         )
         gain_grad = jnp.sum(normed_grad * unit, 0)
         bias_grad = jnp.sum(normed_grad, 0)

time: 271 us -> 267 us (0.985)
  blocking collectives: 27.9 us -> 0 us
  waiting for transfers between devices: 9.26 us -> 27.5 us
  other arithmetic: 33.8 us -> 37.9 us
    all_gather x3 -> x0, blocking collectives: 27.9 us -> none  [gather_feat(): return lax.all_gather(value, 'feat', axis=axis, tiled=True)]
    all_gather x4 -> x3, waiting for transfers between devices: 8.69 us -> 27.4 us  [gather_feat(): return lax.all_gather(value, 'feat', axis=axis, tiled=True)]
    dot_general x4 -> x6, matrix products: 17.2 us -> 20.8 us  [contract_cols(): lax.dot_general(left, right, (((1,), (1,)), ((), ())), preferred_element_...]
    dot_general x4 -> x2, matrix products: 9.68 us -> 7.54 us  [body(): jnp.dot(drive_low, in_low, preferred_element_type=jnp.float32)]
    unnamed x236 -> x209, local copies, waits for them, and re-layouts: 11.1 us -> 12.3 us
  transfers between devices with their start and end apart: 4 -> 3, of which waited for: 2 -> 3; matrix products, arithmetic and copies ran while one was open for 11% -> 12% of each run, Pallas kernels for 7% -> 7%
where the time goes in v18:
time: 267 us
  Pallas kernels  110 us (41%)
  matrix products  57.9 us (22%)
  other arithmetic  37.9 us (14%)
  waiting for transfers between devices  27.5 us (10%)
  local copies, waits for them, and re-layouts  18.6 us (7%)
  between operations  15.1 us (6%)
    pallas_call x1, Pallas kernels, ring_sum(): pl.pallas_call(lambda *refs: ring_sum_kernel(n, *refs), out_shape=jax.Sha...  61.4 us
    pallas_call x2, Pallas kernels, adjoint(): pl.pallas_call(adjoint_kernel, out_shape=(jax.ShapeDtypeStruct((count, 2...  30.8 us
    all_gather x3, waiting for transfers between devices, gather_feat(): return lax.all_gather(value, 'feat', axis=axis, tiled=True)  27.4 us
    dot_general x6, matrix products, contract_cols(): lax.dot_general(left, right, (((1,), (1,)), ((), ())), preferred_element_...  20.8 us
    pallas_call x2, Pallas kernels, recurrence(): pl.pallas_call(recurrence_kernel, out_shape=jax.ShapeDtypeStruct((count,...  17.5 us
    dot_general x2, matrix products, body(): jnp.dot(states_low, out_low, preferred_element_type=jnp.float32)  16.1 us
    unnamed x209, local copies, waits for them, and re-layouts  12.3 us
    dot_general x6, matrix products, contract_rows(): lax.dot_general(left, right, (((0,), (0,)), ((), ())), preferred_element_...  8.42 us
  transfers between devices with their start and end apart: 3, of which 3 were waited for; matrix products, arithmetic and copies ran while one was open for 12% of the time, Pallas kernels for 7%

profile of v18, /device:TPU:0, one launch (start us, length us, event | category | flops | bytes accessed | tf_op | source)
XLA Modules:
  0.0 266.7 jit_solution(1979941914318313367)
XLA Ops:
  8.0 1.4 copy.85
  9.5 0.8 pad_maximum_fusion.7
  11.2 0.9 pad_maximum_fusion.4
  12.2 0.9 pad_maximum_fusion.5
  15.8 1.2 rev.30
  17.6 0.9 copy.90.masks_ref
  21.1 12.0 %all-gather.4.cloned.1.call-done = bf16[1568,512]{1,0:T(8,128)(2,1)} async-done(((bf16[1568,128]{1,0:T(8,128)(2,1)}), bf16[1568,512]{1,0:T(8,128)(2,1)}) %all-gather.4.cloned.1.call-update) | async-done | bytes 1605648 | tf_op jit(solution)/shard_map/all_gather | solution.py:412
  33.1 1.4 convert_reduce_fusion
  34.6 1.5 fusion.2
  37.3 0.8 fusion.31.drive_ref
  38.5 1.1 copy-done
  39.6 1.6 pad_maximum_fusion.x_ref
  41.2 8.8 %shard_map.354.states_ref = f32[768,1536]{1,0:T(8,128)} custom-call(s32[2]{0:T(128)} %starts_ref.7, s32[2]{0:T(128)} %lengths_ref.7, f32[4,8,384]{2,1,0:T(8,128)} %pad_maximum_fusion.8.pow_ref, f32[768,768]{1,0:T(8,128)} %pad_maximum_fusion.x_ref), custom_call_target="tpu_custom_call" | custom-call | flops 11796480 | bytes 9437184 | tf_op jit(solution)/shard_map/pallas_call | solution.py:144
  50.0 12.7 %all-gather.6.cloned.1.call-done = bf16[2816,512]{1,0:T(8,128)(2,1)} async-done(((bf16[2816,128]{1,0:T(8,128)(2,1)}), bf16[2816,512]{1,0:T(8,128)(2,1)}) %all-gather.6.cloned.1.call-update) | async-done | bytes 2883600 | tf_op jit(solution)/shard_map/all_gather | solution.py:412
  62.7 8.2 %multiply_multiply_fusion.11 = (f32[768,512]{1,0:T(8,128)S(1)}, f32[768,512]{1,0:T(8,128)}) fusion(f32[512]{0:T(512)S(1)} %bitcast.461, f32[512]{0:T(512)S(1)} %bitcast.464, f32[768]{0:T(1024)S(1)} %add_rsqrt_fusion.1, f32[768]{0:T(1024)S(1)} %broadcast_multiply_fusion.6, bf16[1568,512]{1,0:T(8,128)(2,1)S(1)} %copy-done.9, f32[512]{0:T(512)S(1)} %bitcast.470, ...), kind=kOutput, calls=%fused_computation.72 | convolution fusion | flops 1237057536 | bytes 10235904 | tf_op jit(solution)/shard_map/dot_general | solution.py:520
  71.0 3.5 %fusion.122 = (f32[768]{0:T(1024)S(1)}, f32[768,512]{1,0:T(8,128)S(1)}, f32[768,512]{1,0:T(8,128)}) fusion(f32[768,512]{1,0:T(8,128)S(1)} %get-tuple-element.300, bf16[1568,512]{1,0:T(8,128)(2,1)S(1)} %copy-done.9, f32[512]{0:T(512)S(1)} %bitcast.475, bf16[2816,512]{1,0:T(8,128)(2,1)} %all-gather.6.cloned.1.call-done), kind=kOutput, calls=%fused_computation.380 | convolution fusion | flops 406191360 | bytes 7607296 | tf_op jit(solution)/shard_map/dot_general | solution.py:525
  75.6 2.2 fusion.28.drive_ref
  78.2 1.1 copy-done.1
  79.3 1.6 pad_maximum_fusion.1.x_ref
  80.9 8.7 %shard_map.355.states_ref = f32[768,1536]{1,0:T(8,128)} custom-call(s32[2]{0:T(128)} %starts_ref.7, s32[2]{0:T(128)} %lengths_ref.7, f32[4,8,384]{2,1,0:T(8,128)} %pad_maximum_fusion.9.pow_ref, f32[768,768]{1,0:T(8,128)} %pad_maximum_fusion.1.x_ref), custom_call_target="tpu_custom_call" | custom-call | flops 11796480 | bytes 9437184 | tf_op jit(solution)/shard_map/pallas_call | solution.py:144
  89.6 2.6 all-gather.8.cloned.1.call-done
  92.3 7.9 %multiply_multiply_fusion.10 = (f32[768,512]{1,0:T(8,128)S(1)}, f32[768,512]{1,0:T(8,128)S(1)}, f32[768,512]{1,0:T(8,128)S(1)}) fusion(f32[512]{0:T(512)S(1)} %bitcast.467, f32[512]{0:T(512)S(1)} %bitcast.453, f32[768]{0:T(1024)S(1)} %add_rsqrt_fusion, f32[768,512]{1,0:T(8,128)S(1)} %copy-done.3, f32[768]{0:T(1024)S(1)} %broadcast_multiply_fusion.5, ...), kind=kOutput, calls=%fused_computation.70 | convolution fusion | flops 1236664320 | bytes 12595200 | tf_op jit(solution)/shard_map/dot_general | solution.py:520
  100.2 1.6 convert_reduce_fusion.1
  102.2 0.9 dynamic-slice_add_fusion.1
  103.1 2.3 fusion.124
  105.5 1.7 convolution_bitcast_fusion
  107.2 3.7 %fusion.15.g_ref = f32[768,1536]{1,0:T(8,128)} fusion(bf16[768,512]{1,0:T(8,128)(2,1)S(1)} %get-tuple-element.305, bf16[2816,512]{1,0:T(8,128)(2,1)S(1)} %copy-done.27), kind=kOutput, calls=%fused_computation.73 | convolution fusion | flops 1207959552 | bytes 7077888 | tf_op jit(solution)/shard_map/dot_general | solution.py:406
  110.9 15.4 %shard_map.356 = (bf16[768,768]{1,0:T(8,128)(2,1)}, f32[4,384]{1,0:T(4,128)}) custom-call(s32[2]{0:T(128)} %starts_ref.7, s32[2]{0:T(128)} %lengths_ref.7, f32[4,8,384]{2,1,0:T(8,128)} %pad_maximum_fusion.10.pow_ref, f32[4,384]{1,0:T(4,128)} %pad_maximum_fusion.13.coef_ref, f32[768,4]{1,0:T(8,128)} %copy.90.masks_ref, f32[768,1536]{1,0:T(8,128)} %fusion.15.g_ref, ...), custom_call_target="tpu_custom_call" | custom-call | flops 17694720 | bytes 14155776 | tf_op jit(solution)/shard_map/pallas_call | solution.py:375
  126.3 1.8 convolution_bitcast_fusion.2
  128.2 3.7 %multiply_reduce_fusion.1 = (f32[512]{0:T(512)}, f32[768]{0:T(1024)S(1)}, f32[512]{0:T(512)}, f32[768]{0:T(1024)S(1)}, f32[512]{0:T(512)}, /*index=5*/f32[768,512]{1,0:T(8,128)S(1)}) fusion(f32[768]{0:T(1024)S(1)} %add_rsqrt_fusion, f32[768,512]{1,0:T(8,128)S(1)} %copy-done.3, f32[768]{0:T(1024)S(1)} %broadcast_multiply_fusion.5, f32[512]{0:T(512)S(1)} %bitcast.454, ...), kind=kOutput, calls=%fused_computation.23 | convolution fusion | flops 609874944 | bytes 6709248 | tf_op jit(solution)/shard_map/dot_general | solution.py:564
  131.9 3.9 %convert_reduce_fusion.2 = (f32[512]{0:T(512)}, bf16[768,512]{1,0:T(8,128)(2,1)S(1)}, f32[768,512]{1,0:T(8,128)}) fusion(f32[768,512]{1,0:T(8,128)S(1)} %copy-done.18, f32[768,512]{1,0:T(8,128)S(1)} %copy-done.7, f32[768]{0:T(1024)S(1)} %broadcast_multiply_fusion.3, f32[768,512]{1,0:T(8,128)S(1)} %copy-done.3, f32[768]{0:T(1024)} %copy-done.45, ...), kind=kLoop, calls=%fused_computation.24 | loop fusion | flops 6684160 | bytes 9456640 | tf_op jit(solution)/shard_map/reduce_sum | solution.py:542
  135.9 1.1 convolution_bitcast_fusion.5
  139.1 1.2 rev.31
  140.3 8.1 %fusion.125 = (bf16[768,512]{1,0:T(8,128)(2,1)S(1)}, f32[768,512]{1,0:T(8,128)}) fusion(f32[768,512]{1,0:T(8,128)} %get-tuple-element.301, bf16[768,512]{1,0:T(8,128)(2,1)} %copy-done.19, bf16[2816,512]{1,0:T(8,128)(2,1)} %all-gather.6.cloned.1.call-done, f32[768,512]{1,0:T(8,128)} %get-tuple-element.159, f32[768,512]{1,0:T(8,128)} %get-tuple-element.302), kind=kOutput, calls=%fused_computation.383 | convolution fusion | flops 431751168 | bytes 8388608 | tf_op jit(solution)/shard_map/dot_general | solution.py:406
  148.5 1.7 convolution_bitcast_fusion.1
  151.5 3.6 %fusion.18.g_ref = f32[768,1536]{1,0:T(8,128)} fusion(bf16[768,512]{1,0:T(8,128)(2,1)S(1)} %get-tuple-element.308, bf16[2816,512]{1,0:T(8,128)(2,1)S(1)} %copy-done.26), kind=kOutput, calls=%fused_computation.76 | convolution fusion | flops 1207959552 | bytes 7077888 | tf_op jit(solution)/shard_map/dot_general | solution.py:406
  155.1 15.4 %shard_map.357 = (bf16[768,768]{1,0:T(8,128)(2,1)}, f32[4,384]{1,0:T(4,128)}) custom-call(s32[2]{0:T(128)} %starts_ref.7, s32[2]{0:T(128)} %lengths_ref.7, f32[4,8,384]{2,1,0:T(8,128)} %pad_maximum_fusion.11.pow_ref, f32[4,384]{1,0:T(4,128)} %pad_maximum_fusion.14.coef_ref, f32[768,4]{1,0:T(8,128)} %copy.90.masks_ref, f32[768,1536]{1,0:T(8,128)} %fusion.18.g_ref, ...), custom_call_target="tpu_custom_call" | custom-call | flops 17694720 | bytes 14155776 | tf_op jit(solution)/shard_map/pallas_call | solution.py:375
  170.5 1.6 convolution_bitcast_fusion.3
  175.6 3.8 %multiply_reduce_fusion.2 = (f32[512]{0:T(512)S(1)}, f32[512]{0:T(512)S(1)}, f32[768]{0:T(1024)S(1)}, f32[768]{0:T(1024)S(1)}, f32[512]{0:T(512)S(1)}, /*index=5*/f32[768,512]{1,0:T(8,128)}, f32[768,512]{1,0:T(8,128)}) fusion(f32[768,512]{1,0:T(8,128)S(1)} %copy-done.95, f32[512]{0:T(512)S(1)} %bitcast.462, f32[512]{0:T(512)S(1)} %bitcast.465, ...), kind=kOutput, calls=%fused_computation.25 | convolution fusion | flops 610268160 | bytes 7495680 | tf_op jit(solution)/shard_map/dot_general | solution.py:564
  179.7 1.8 pad_bitcast_fusion.refs_0_
  181.4 61.4 %shard_map.358 = bf16[5888,128]{1,0:T(8,128)(2,1)} custom-call(f32[5888,128]{1,0:T(8,128)} %pad_bitcast_fusion.refs_0_), custom_call_target="tpu_custom_call" | custom-call | tf_op jit(solution)/shard_map/pallas_call | solution.py:267
  242.8 1.6 convert_element_type.155
  244.4 0.8 slice_multiply_fusion.2
  249.0 3.0 %add_multiply_fusion.4 = (f32[2,512,128]{2,1,0:T(8,128)}, f32[2,512,128]{2,1,0:T(8,128)}, f32[2,512,128]{2,1,0:T(8,128)}) fusion(f32[2,512,128]{2,1,0:T(8,128)} %param.35, f32[2,512,128]{2,1,0:T(8,128)} %param.25, f32[2,512,128]{2,1,0:T(8,128)} %bitcast.433, f32[2,512,128]{2,1,0:T(8,128)} %param.30), kind=kLoop, calls=%fused_computation.111 | loop fusion | flops 1310720 | bytes 3670016 | tf_op jit(solution)/shard_map/add | solution.py:395
  252.0 1.7 add_multiply_fusion.3
  253.7 0.9 copy-done.16
  255.1 2.7 %add_multiply_fusion = (f32[2,1536,128]{2,1,0:T(8,128)}, f32[2,1536,128]{2,1,0:T(8,128)}, f32[2,1536,128]{2,1,0:T(8,128)}) fusion(f32[2,1536,128]{2,1,0:T(8,128)S(1)} %copy-done.16, f32[2,1536,128]{2,1,0:T(8,128)S(1)} %copy-done.5, f32[2,1536,128]{2,1,0:T(8,128)S(1)} %bitcast.431, f32[2,1536,128]{2,1,0:T(8,128)S(1)} %copy-done.17), kind=kLoop, calls=%fused_computation.17 | loop fusion | flops 3932160 | bytes 11010048 | tf_op jit(solution)/shard_map/add | solution.py:395
  257.8 2.4 dynamic-slice_add_fusion
  (297 shorter events, 21.9 us)
Async XLA Ops:
  7.2 25.9 %all-gather.4.cloned.1.call-start = ((), (), s32[]{:S(2)}) async-start(), calls=%async_computation | async-start | bytes 2007040 | tf_op jit(solution)/shard_map/all_gather | solution.py:412
  10.3 52.4 %all-gather.6.cloned.1.call-start = ((), (), s32[]{:S(2)}) async-start(), calls=%async_computation.1 | async-start | bytes 3604480 | tf_op jit(solution)/shard_map/all_gather | solution.py:412
  12.1 80.2 %all-gather.8.cloned.1.call-start = ((), (), s32[]{:S(2)}) async-start(), calls=%async_computation.2 | async-start | bytes 3604480 | tf_op jit(solution)/shard_map/all_gather | solution.py:412
  13.8 3.6 %copy-start.53 = (f32[1,384]{1,0:T(1,128)}, f32[1,384]{1,0:T(1,128)S(1)}, u32[]{:S(2)}) copy-start(f32[1,384]{1,0:T(1,128)S(1)} %get-tuple-element.183) | copy-start | bytes 4612
  13.8 23.1 %copy-start.39 = (f32[1,384]{1,0:T(1,128)}, f32[1,384]{1,0:T(1,128)S(1)}, u32[]{:S(2)}) copy-start(f32[1,384]{1,0:T(1,128)S(1)} %get-tuple-element.185) | copy-start | bytes 4612
  14.0 89.1 %copy-start.37 = (f32[768]{0:T(1024)}, f32[768]{0:T(1024)S(1)}, u32[]{:S(2)}) copy-start(f32[768]{0:T(1024)S(1)} %get-tuple-element.299) | copy-start | bytes 9220
  14.8 6.3 %copy-start.30 = (f32[1,384]{1,0:T(1,128)}, f32[1,384]{1,0:T(1,128)S(1)}, u32[]{:S(2)}) copy-start(f32[1,384]{1,0:T(1,128)S(1)} %get-tuple-element.257) | copy-start | bytes 4612
  14.8 22.6 %copy-start.41 = (f32[1,384]{1,0:T(1,128)}, f32[1,384]{1,0:T(1,128)S(1)}, u32[]{:S(2)}) copy-start(f32[1,384]{1,0:T(1,128)S(1)} %get-tuple-element.256) | copy-start | bytes 4612
  15.8 5.3 %copy-start.33 = (f32[8,384]{1,0:T(8,128)}, f32[8,384]{1,0:T(8,128)S(1)}, u32[]{:S(2)}) copy-start(f32[8,384]{1,0:T(8,128)S(1)} %stack.266) | copy-start | bytes 36868
  33.1 3.8 %copy-start.9 = (bf16[1568,512]{1,0:T(8,128)(2,1)S(1)}, bf16[1568,512]{1,0:T(8,128)(2,1)}, u32[]{:S(2)}) copy-start(bf16[1568,512]{1,0:T(8,128)(2,1)} %all-gather.4.cloned.1.call-done) | copy-start | bytes 4816900
  34.6 28.1 %copy-start.50 = (f32[768]{0:T(1024)}, f32[768]{0:T(1024)S(1)}, u32[]{:S(2)}) copy-start(f32[768]{0:T(1024)S(1)} %broadcast_multiply_fusion.6) | copy-start | bytes 9220
  36.1 26.6 %copy-start.48 = (f32[768]{0:T(1024)}, f32[768]{0:T(1024)S(1)}, u32[]{:S(2)}) copy-start(f32[768]{0:T(1024)S(1)} %add_rsqrt_fusion.1) | copy-start | bytes 9220
  36.9 25.8 %copy-start.69 = (f32[1,512]{1,0:T(1,128)}, f32[1,512]{1,0:T(1,128)S(1)}, u32[]{:S(2)}) copy-start(f32[1,512]{1,0:T(1,128)S(1)} %get-tuple-element.249) | copy-start | bytes 6148
  36.9 25.8 %copy-start.71 = (f32[1,512]{1,0:T(1,128)}, f32[1,512]{1,0:T(1,128)S(1)}, u32[]{:S(2)}) copy-start(f32[1,512]{1,0:T(1,128)S(1)} %get-tuple-element.250) | copy-start | bytes 6148
  36.9 25.8 %copy-start.89 = (f32[1,512]{1,0:T(1,128)}, f32[1,512]{1,0:T(1,128)S(1)}, u32[]{:S(2)}) copy-start(f32[1,512]{1,0:T(1,128)S(1)} %get-tuple-element.248) | copy-start | bytes 6148
  36.9 91.2 %copy-start.59 = (f32[1,512]{1,0:T(1,128)}, f32[1,512]{1,0:T(1,128)S(1)}, u32[]{:S(2)}) copy-start(f32[1,512]{1,0:T(1,128)S(1)} %get-tuple-element.246) | copy-start | bytes 6148
  71.0 3.5 %copy-start.6 = (f32[768,512]{1,0:T(8,128)}, f32[768,512]{1,0:T(8,128)S(1)}, u32[]{:S(2)}) copy-start(f32[768,512]{1,0:T(8,128)S(1)} %get-tuple-element.300) | copy-start | bytes 4718596
  74.5 53.6 %copy-start.45 = (f32[768]{0:T(1024)}, f32[768]{0:T(1024)S(1)}, u32[]{:S(2)}) copy-start(f32[768]{0:T(1024)S(1)} %broadcast_multiply_fusion.5) | copy-start | bytes 9220
  74.8 53.3 %copy-start.52 = (f32[768]{0:T(1024)}, f32[768]{0:T(1024)S(1)}, u32[]{:S(2)}) copy-start(f32[768]{0:T(1024)S(1)} %add_rsqrt_fusion) | copy-start | bytes 9220
  80.9 11.4 %copy-start.3 = (f32[768,512]{1,0:T(8,128)S(1)}, f32[768,512]{1,0:T(8,128)}, u32[]{:S(2)}) copy-start(f32[768,512]{1,0:T(8,128)} %copy-done.2) | copy-start | bytes 4718596
  92.3 7.9 %copy-start.27 = (bf16[2816,512]{1,0:T(8,128)(2,1)S(1)}, bf16[2816,512]{1,0:T(8,128)(2,1)}, u32[]{:S(2)}) copy-start(bf16[2816,512]{1,0:T(8,128)(2,1)} %all-gather.8.cloned.1.call-done) | copy-start | bytes 8650756
  102.2 3.3 %slice-start.2 = ((s8[4718592]{0:T(1024)(128)(4,1)}), s8[4194304]{0:T(1024)(128)(4,1)S(1)}, s32[]{:S(2)}) async-start(s8[4718592]{0:T(1024)(128)(4,1)} %bitcast.428), calls=%async_computation.5 | async-start | bytes 8388608
  128.1 3.8 %copy-start.7 = (f32[768,512]{1,0:T(8,128)S(1)}, f32[768,512]{1,0:T(8,128)}, u32[]{:S(2)}) copy-start(f32[768,512]{1,0:T(8,128)} %copy-done.6) | copy-start | bytes 4718596
  128.1 3.8 %copy-start.18 = (f32[768,512]{1,0:T(8,128)S(1)}, f32[768,512]{1,0:T(8,128)}, u32[]{:S(2)}) copy-start(f32[768,512]{1,0:T(8,128)} %get-tuple-element.302) | copy-start | bytes 4718596
  128.2 3.8 %copy-start.38 = (f32[768]{0:T(1024)S(1)}, f32[768]{0:T(1024)}, u32[]{:S(2)}) copy-start(f32[768]{0:T(1024)} %copy-done.37) | copy-start | bytes 9220
  131.9 16.5 %slice-start = ((s8[4718592]{0:T(1024)(128)(4,1)}), s8[524288]{0:T(1024)(128)(4,1)S(1)}, s32[]{:S(2)}) async-start(s8[4718592]{0:T(1024)(128)(4,1)} %bitcast.426), calls=%async_computation.3 | async-start | bytes 1048576
  135.9 2.6 copy-start.77
  135.9 2.6 copy-start.78
  135.9 2.6 copy-start.79
  135.9 2.6 copy-start.80
  140.3 8.1 %slice-start.1 = ((s8[4718592]{0:T(1024)(128)(4,1)}), s8[4194304]{0:T(1024)(128)(4,1)S(1)}, s32[]{:S(2)}) async-start(s8[4718592]{0:T(1024)(128)(4,1)} %bitcast.426), calls=%async_computation.4 | async-start | bytes 8388608
  148.5 2.4 copy-start.34
  148.5 2.4 copy-start.36
  148.5 2.4 copy-start.46
  148.5 2.4 copy-start.47
  148.5 3.0 %copy-start.26 = (bf16[2816,512]{1,0:T(8,128)(2,1)S(1)}, bf16[2816,512]{1,0:T(8,128)(2,1)}, u32[]{:S(2)}) copy-start(bf16[2816,512]{1,0:T(8,128)(2,1)} %all-gather.6.cloned.1.call-done) | copy-start | bytes 8650756
  175.6 3.8 %copy-start.73 = (f32[512]{0:T(512)S(1)}, f32[512]{0:T(512)}, u32[]{:S(2)}) copy-start(f32[512]{0:T(512)} %get-tuple-element.157) | copy-start | bytes 6148
  244.4 3.8 %copy-start.62 = (f32[8,128]{1,0:T(8,128)}, f32[8,128]{1,0:T(8,128)S(1)}, u32[]{:S(2)}) copy-start(f32[8,128]{1,0:T(8,128)S(1)} %slice_multiply_fusion.4) | copy-start | bytes 12292
  245.5 8.1 %copy-start.8 = (f32[3072,128]{1,0:T(8,128)}, f32[3072,128]{1,0:T(8,128)S(1)}, u32[]{:S(2)}) copy-start(f32[3072,128]{1,0:T(8,128)S(1)} %slice_multiply_fusion) | copy-start | bytes 4718596
  245.5 2.7 %copy-start.61 = (f32[2,4,128]{2,1,0:T(4,128)S(1)}, f32[2,4,128]{2,1,0:T(4,128)}, u32[]{:S(2)}) copy-start(f32[2,4,128]{2,1,0:T(4,128)} %param.26) | copy-start | bytes 12292
  245.5 2.7 %copy-start.87 = (f32[2,4,128]{2,1,0:T(4,128)S(1)}, f32[2,4,128]{2,1,0:T(4,128)}, u32[]{:S(2)}) copy-start(f32[2,4,128]{2,1,0:T(4,128)} %param.36) | copy-start | bytes 12292
  245.5 2.7 %copy-start.88 = (f32[2,4,128]{2,1,0:T(4,128)S(1)}, f32[2,4,128]{2,1,0:T(4,128)}, u32[]{:S(2)}) copy-start(f32[2,4,128]{2,1,0:T(4,128)} %param.31) | copy-start | bytes 12292
  248.2 3.7 %copy-start.12 = (f32[2,128,768]{2,1,0:T(8,128)}, f32[2,128,768]{2,1,0:T(8,128)S(1)}, u32[]{:S(2)}) copy-start(f32[2,128,768]{2,1,0:T(8,128)S(1)} %mul.6070) | copy-start | bytes 2359300
  248.9 3.0 %copy-start.11 = (f32[2,128,768]{2,1,0:T(8,128)S(1)}, f32[2,128,768]{2,1,0:T(8,128)}, u32[]{:S(2)}) copy-start(f32[2,128,768]{2,1,0:T(8,128)} %param.23) | copy-start | bytes 2359300
  249.0 3.0 %copy-start.23 = (f32[2,128,768]{2,1,0:T(8,128)S(1)}, f32[2,128,768]{2,1,0:T(8,128)}, u32[]{:S(2)}) copy-start(f32[2,128,768]{2,1,0:T(8,128)} %param.33) | copy-start | bytes 2359300
  249.0 3.0 %copy-start.24 = (f32[2,128,768]{2,1,0:T(8,128)S(1)}, f32[2,128,768]{2,1,0:T(8,128)}, u32[]{:S(2)}) copy-start(f32[2,128,768]{2,1,0:T(8,128)} %param.28) | copy-start | bytes 2359300
  251.9 2.7 %copy-start.16 = (f32[2,1536,128]{2,1,0:T(8,128)S(1)}, f32[2,1536,128]{2,1,0:T(8,128)}, u32[]{:S(2)}) copy-start(f32[2,1536,128]{2,1,0:T(8,128)} %param.34) | copy-start | bytes 4718596
  252.0 3.2 %copy-start.17 = (f32[2,1536,128]{2,1,0:T(8,128)S(1)}, f32[2,1536,128]{2,1,0:T(8,128)}, u32[]{:S(2)}) copy-start(f32[2,1536,128]{2,1,0:T(8,128)} %param.29) | copy-start | bytes 4718596
  (55 other events, 70.9 us)
Sparse Core Ops, SparseCore 0:
  10.4 22.7 all-gather.3
  35.3 27.3 all-gather.5
  64.8 27.3 all-gather.7

commit v19 on v16

--- a/solution.py
+++ b/solution.py
@@ -490,16 +490,17 @@
             jnp.dot(states_low, out_low, preferred_element_type=jnp.float32)
             + feature_row[2] * normed
         )
-        act = smooth(mixed)
+        cdf = (lax.erf(mixed * (1.0 / math.sqrt(2.0))) + 1.0) / 2.0
+        act = mixed * cdf
         act_low = act.astype(jnp.bfloat16)
         pre = jnp.dot(act_low, gate_low, preferred_element_type=jnp.float32) + feature_row[3]
-        saved.append((scale, unit, normed_low, drive, states, states_low, mixed, act, act_low, pre))
+        saved.append((scale, unit, normed_low, drive, states, states_low, mixed, act, act_low, pre, cdf))
         stream = stream + act * jax.nn.sigmoid(pre)
 
     grad = gather_feat(cotangent, 1).astype(jnp.float32) * alive[:, None]
     layer_grads = [None] * layers
     for layer in reversed(range(layers)):
-        scale, unit, normed_low, drive, states, states_low, mixed, act, act_low, pre = saved[layer]
+        scale, unit, normed_low, drive, states, states_low, mixed, act, act_low, pre, cdf = saved[layer]
         in_low = in_all[layer]
         out_low = out_all[layer]
         gate_low = gate_all[layer]
@@ -511,7 +512,8 @@
         gate_grad = contract_rows(act_low, mine(pre_grad))
         gate_bias_grad = jnp.sum(pre_grad.astype(jnp.float32), 0)
         act_grad = grad * gate + contract_cols(pre_grad, gate_low)
-        mixed_grad = jax.vjp(smooth, mixed)[1](act_grad)[0]
+        density = jnp.exp(mixed * mixed * -0.5) * (1.0 / math.sqrt(2.0 * math.pi))
+        mixed_grad = act_grad * (cdf + mixed * density)
         normed = unit * feature_row[0] + feature_row[1]
         skip_grad = jnp.sum(mixed_grad * normed, 0)
         mixed_low = mixed_grad.astype(jnp.bfloat16)

time: 264 us -> 257 us (0.973)
  matrix products: 56.3 us -> 48.1 us
  other arithmetic: 34.8 us -> 38.5 us
    dot_general x2, matrix products: 15.9 us -> 10 us  [body(): jnp.dot(states_low, out_low, preferred_element_type=jnp.float32)]
    dot_general x4, matrix products: 17.2 us -> 14.2 us  [contract_cols(): lax.dot_general(left, right, (((1,), (1,)), ((), ())), preferred_element_...]
    unnamed x234 -> x220, local copies, waits for them, and re-layouts: 11.1 us -> 8.31 us
  transfers between devices with their start and end apart: 3 -> 3, of which waited for: 0 -> 0; matrix products, arithmetic and copies ran while one was open for 12% -> 11% of each run, Pallas kernels for 7% -> 7%
where the time goes in v19:
time: 257 us
  Pallas kernels  110 us (43%)
  matrix products  48.1 us (19%)
  other arithmetic  38.5 us (15%)
  blocking collectives  28.4 us (11%)
  local copies, waits for them, and re-layouts  16.4 us (6%)
  between operations  15.2 us (6%)
    pallas_call x1, Pallas kernels, ring_sum(): pl.pallas_call(lambda *refs: ring_sum_kernel(n, *refs), out_shape=jax.Sha...  61.7 us
    pallas_call x2, Pallas kernels, adjoint(): pl.pallas_call(adjoint_kernel, out_shape=(jax.ShapeDtypeStruct((count, 2...  30.8 us
    all_gather x3, blocking collectives, gather_feat(): return lax.all_gather(value, 'feat', axis=axis, tiled=True)  28.4 us
    pallas_call x2, Pallas kernels, recurrence(): pl.pallas_call(recurrence_kernel, out_shape=jax.ShapeDtypeStruct((count,...  17.7 us
    dot_general x4, matrix products, contract_cols(): lax.dot_general(left, right, (((1,), (1,)), ((), ())), preferred_element_...  14.2 us
    dot_general x2, matrix products, body(): jnp.dot(states_low, out_low, preferred_element_type=jnp.float32)  10 us
    dot_general x6, matrix products, contract_rows(): lax.dot_general(left, right, (((0,), (0,)), ((), ())), preferred_element_...  9.29 us
    add x5, other arithmetic, update(): average_new = smoothing * average + (1.0 - smoothing) * weight_new  9.08 us
  transfers between devices with their start and end apart: 3, of which 0 were waited for; matrix products, arithmetic and copies ran while one was open for 11% of the time, Pallas kernels for 7%

profile of v19, /device:TPU:0, one launch (start us, length us, event | category | flops | bytes accessed | tf_op | source)
XLA Modules:
  0.0 256.9 jit_solution(15192444260892488965)
XLA Ops:
  7.3 2.1 convert_element_type.96
  12.4 6.1 %all_gather.19 = f32[2,4,512]{2,1,0:T(4,128)S(1)} all-gather(f32[2,4,128]{2,1,0:T(4,128)S(1)} %copy-done.64), channel_id=1, replica_groups=mesh['seq'=8,'feat'=4] {'feat'}, dimensions={2}, use_global_device_ids=true | all-gather | bytes 20480 | tf_op jit(solution)/shard_map/all_gather | solution.py:412
  20.3 1.2 rev.30
  22.1 0.9 copy.86.masks_ref
  23.0 13.1 %all_gather.18 = bf16[768,512]{1,0:T(8,128)(2,1)S(1)} all-gather(bf16[768,128]{1,0:T(8,128)(2,1)S(1)} %copy-done.31), channel_id=1, replica_groups=mesh['seq'=8,'feat'=4] {'feat'}, dimensions={1}, use_global_device_ids=true | all-gather | bytes 983040 | tf_op jit(solution)/shard_map/all_gather | solution.py:412
  36.8 9.2 %all_gather.23 = bf16[768,512]{1,0:T(8,128)(2,1)} all-gather(bf16[768,128]{1,0:T(8,128)(2,1)S(1)} %copy-done.32), channel_id=1, replica_groups=mesh['seq'=8,'feat'=4] {'feat'}, dimensions={1}, use_global_device_ids=true | all-gather | bytes 983040 | tf_op jit(solution)/shard_map/all_gather | solution.py:412
  46.6 1.2 fusion.9
  49.8 2.1 fusion.15.drive_ref
  52.3 1.0 copy-done
  53.3 1.6 pad_maximum_fusion.x_ref
  54.9 8.9 %shard_map.354.states_ref = f32[768,1536]{1,0:T(8,128)} custom-call(s32[2]{0:T(128)} %starts_ref.7, s32[2]{0:T(128)} %lengths_ref.7, f32[4,8,384]{2,1,0:T(8,128)} %pad_maximum_fusion.7.pow_ref, f32[768,768]{1,0:T(8,128)} %pad_maximum_fusion.x_ref), custom_call_target="tpu_custom_call" | custom-call | flops 11796480 | bytes 9437184 | tf_op jit(solution)/shard_map/pallas_call | solution.py:144
  63.8 5.7 %fusion.84 = (f32[768,512]{1,0:T(8,128)S(1)}, f32[768,512]{1,0:T(8,128)}) fusion(f32[512]{0:T(512)S(1)} %bitcast.463, f32[512]{0:T(512)S(1)} %bitcast.466, f32[768]{0:T(1024)S(1)} %add_rsqrt_fusion.1, f32[768]{0:T(1024)S(1)} %broadcast_multiply_fusion.6, bf16[768,512]{1,0:T(8,128)(2,1)S(1)} %copy-done.5, f32[512]{0:T(512)S(1)} %bitcast.472, ...), kind=kOutput, calls=%fused_computation.327 | convolution fusion | flops 1213464576 | bytes 10235904 | tf_op jit(solution)/shard_map/dot_general | solution.py:490
  69.6 3.5 %fusion.102 = (f32[768]{0:T(1024)S(1)}, f32[768,512]{1,0:T(8,128)S(1)}, f32[768,512]{1,0:T(8,128)}) fusion(f32[768,512]{1,0:T(8,128)S(1)} %get-tuple-element.297, bf16[768,512]{1,0:T(8,128)(2,1)S(1)} %copy-done.5, f32[512]{0:T(512)S(1)} %bitcast.477, bf16[2048,512]{1,0:T(8,128)(2,1)} %all-gather.6.cloned.1.call-done), kind=kOutput, calls=%fused_computation.335 | convolution fusion | flops 406191360 | bytes 7607296 | tf_op jit(solution)/shard_map/dot_general | solution.py:496
  74.2 0.8 copy-done.25
  76.2 1.0 copy-done.1
  77.3 1.6 pad_maximum_fusion.1.x_ref
  78.9 8.8 %shard_map.355.states_ref = f32[768,1536]{1,0:T(8,128)} custom-call(s32[2]{0:T(128)} %starts_ref.7, s32[2]{0:T(128)} %lengths_ref.7, f32[4,8,384]{2,1,0:T(8,128)} %pad_maximum_fusion.8.pow_ref, f32[768,768]{1,0:T(8,128)} %pad_maximum_fusion.1.x_ref), custom_call_target="tpu_custom_call" | custom-call | flops 11796480 | bytes 9437184 | tf_op jit(solution)/shard_map/pallas_call | solution.py:144
  87.8 4.3 %fusion.85 = (f32[768,512]{1,0:T(8,128)S(1)}, f32[768,512]{1,0:T(8,128)S(1)}) fusion(f32[512]{0:T(512)S(1)} %bitcast.469, f32[512]{0:T(512)S(1)} %bitcast.456, f32[768]{0:T(1024)S(1)} %add_rsqrt_fusion, f32[768,512]{1,0:T(8,128)S(1)} %copy-done.3, f32[768]{0:T(1024)S(1)} %broadcast_multiply_fusion.5, f32[512]{0:T(512)S(1)} %bitcast.474, ...), kind=kOutput, calls=%fused_computation.328 | convolution fusion | flops 1213071360 | bytes 11022336 | tf_op jit(solution)/shard_map/dot_general | solution.py:490
  92.1 1.6 convert_reduce_fusion.1
  93.7 1.1 convolution_bitcast_fusion.4
  94.9 0.9 dynamic-slice_add_fusion.1
  95.8 2.3 fusion.104
  98.1 1.7 convolution_bitcast_fusion
  99.8 3.6 %fusion.3.g_ref = f32[768,1536]{1,0:T(8,128)} fusion(bf16[768,512]{1,0:T(8,128)(2,1)S(1)} %get-tuple-element.303, bf16[2048,512]{1,0:T(8,128)(2,1)S(1)} %copy-done.34), kind=kOutput, calls=%fused_computation.43 | convolution fusion | flops 1207959552 | bytes 7077888 | tf_op jit(solution)/shard_map/dot_general | solution.py:406
  103.5 15.4 %shard_map.356 = (bf16[768,768]{1,0:T(8,128)(2,1)}, f32[4,384]{1,0:T(4,128)}) custom-call(s32[2]{0:T(128)} %starts_ref.7, s32[2]{0:T(128)} %lengths_ref.7, f32[4,8,384]{2,1,0:T(8,128)} %pad_maximum_fusion.9.pow_ref, f32[4,384]{1,0:T(4,128)} %pad_maximum_fusion.12.coef_ref, f32[768,4]{1,0:T(8,128)} %copy.86.masks_ref, f32[768,1536]{1,0:T(8,128)} %fusion.3.g_ref, ...), custom_call_target="tpu_custom_call" | custom-call | flops 17694720 | bytes 14155776 | tf_op jit(solution)/shard_map/pallas_call | solution.py:375
  118.9 1.8 convolution_bitcast_fusion.2
  120.8 3.6 %multiply_reduce_fusion.1 = (f32[512]{0:T(512)}, f32[768]{0:T(1024)S(1)}, f32[512]{0:T(512)}, f32[768]{0:T(1024)S(1)}, f32[512]{0:T(512)}, /*index=5*/f32[768,512]{1,0:T(8,128)S(1)}) fusion(f32[768]{0:T(1024)S(1)} %copy-done.54, f32[768,512]{1,0:T(8,128)S(1)} %copy-done.3, f32[768]{0:T(1024)S(1)} %copy-done.47, f32[512]{0:T(512)S(1)} %bitcast.457, ...), kind=kOutput, calls=%fused_computation.19 | convolution fusion | flops 609874944 | bytes 6709248 | tf_op jit(solution)/shard_map/dot_general | solution.py:536
  124.5 2.7 %convert_reduce_fusion.2 = (f32[512]{0:T(512)}, bf16[768,512]{1,0:T(8,128)(2,1)S(1)}, f32[768,512]{1,0:T(8,128)}) fusion(f32[768,512]{1,0:T(8,128)S(1)} %copy-done.8, f32[768,512]{1,0:T(8,128)S(1)} %copy-done.12, f32[768]{0:T(1024)S(1)} %broadcast_multiply_fusion.3, f32[768,512]{1,0:T(8,128)S(1)} %copy-done.3, f32[768]{0:T(1024)S(1)} %copy-done.47, ...), kind=kLoop, calls=%fused_computation.20 | loop fusion | flops 6684160 | bytes 9456640 | tf_op jit(solution)/shard_map/reduce_sum | solution.py:513
  127.3 1.1 convolution_bitcast_fusion.5
  130.1 4.6 %fusion.105 = (bf16[768,512]{1,0:T(8,128)(2,1)S(1)}, f32[768,512]{1,0:T(8,128)}) fusion(f32[768,512]{1,0:T(8,128)} %get-tuple-element.298, bf16[768,512]{1,0:T(8,128)(2,1)} %copy-done.15, bf16[2048,512]{1,0:T(8,128)(2,1)} %all-gather.6.cloned.1.call-done, f32[768,512]{1,0:T(8,128)S(1)} %copy-done.6, f32[768,512]{1,0:T(8,128)} %get-tuple-element.299), kind=kOutput, calls=%fused_computation.338 | convolution fusion | flops 407371776 | bytes 8388608 | tf_op jit(solution)/shard_map/dot_general | solution.py:406
  134.8 1.7 convolution_bitcast_fusion.1
  137.7 3.6 %fusion.6.g_ref = f32[768,1536]{1,0:T(8,128)} fusion(bf16[768,512]{1,0:T(8,128)(2,1)S(1)} %get-tuple-element.306, bf16[2048,512]{1,0:T(8,128)(2,1)S(1)} %copy-done.33), kind=kOutput, calls=%fused_computation.46 | convolution fusion | flops 1207959552 | bytes 7077888 | tf_op jit(solution)/shard_map/dot_general | solution.py:406
  141.3 15.4 %shard_map.357 = (bf16[768,768]{1,0:T(8,128)(2,1)}, f32[4,384]{1,0:T(4,128)}) custom-call(s32[2]{0:T(128)} %starts_ref.7, s32[2]{0:T(128)} %lengths_ref.7, f32[4,8,384]{2,1,0:T(8,128)} %pad_maximum_fusion.10.pow_ref, f32[4,384]{1,0:T(4,128)} %pad_maximum_fusion.13.coef_ref, f32[768,4]{1,0:T(8,128)} %copy.86.masks_ref, f32[768,1536]{1,0:T(8,128)} %fusion.6.g_ref, ...), custom_call_target="tpu_custom_call" | custom-call | flops 17694720 | bytes 14155776 | tf_op jit(solution)/shard_map/pallas_call | solution.py:375
  156.7 1.7 convolution_bitcast_fusion.3
  158.5 0.9 pad_maximum_fusion.3
  159.5 2.1 reshape.1858
  161.9 1.3 constant_dynamic-update-slice_fusion.4
  163.4 1.6 pad_maximum_fusion.2
  165.7 2.9 %fusion.86 = (f32[512]{0:T(512)S(1)}, f32[512]{0:T(512)S(1)}, f32[512]{0:T(512)S(1)}, f32[768]{0:T(1024)S(1)}, f32[768]{0:T(1024)S(1)}, /*index=5*/f32[768,512]{1,0:T(8,128)}, f32[768,512]{1,0:T(8,128)}) fusion(f32[768]{0:T(1024)S(1)} %copy-done.50, f32[768]{0:T(1024)S(1)} %copy-done.52, bf16[768,512]{1,0:T(8,128)(2,1)S(1)} %copy-done.5, ...), kind=kOutput, calls=%fused_computation.329 | convolution fusion | flops 610268160 | bytes 7497728 | tf_op jit(solution)/shard_map/dot_general | solution.py:536
  168.9 1.8 pad_bitcast_fusion.refs_0_
  170.7 61.7 %shard_map.358 = bf16[5888,128]{1,0:T(8,128)(2,1)} custom-call(f32[5888,128]{1,0:T(8,128)} %pad_bitcast_fusion.refs_0_), custom_call_target="tpu_custom_call" | custom-call | tf_op jit(solution)/shard_map/pallas_call | solution.py:267
  232.4 1.6 convert_element_type.116
  234.2 1.3 slice_multiply_fusion
  237.9 1.0 mul.6050
  239.6 2.6 %add_multiply_fusion.8 = (f32[2,512,128]{2,1,0:T(8,128)}, f32[2,512,128]{2,1,0:T(8,128)}, f32[2,512,128]{2,1,0:T(8,128)}) fusion(f32[2,512,128]{2,1,0:T(8,128)} %param.35, f32[2,512,128]{2,1,0:T(8,128)S(1)} %copy-done.19, f32[2,512,128]{2,1,0:T(8,128)S(1)} %bitcast.436, f32[2,512,128]{2,1,0:T(8,128)} %param.30), kind=kLoop, calls=%fused_computation.79 | loop fusion | flops 1310720 | bytes 3670016 | tf_op jit(solution)/shard_map/add | solution.py:395
  242.3 3.2 %add_multiply_fusion.7 = (f32[2,128,768]{2,1,0:T(8,128)}, f32[2,128,768]{2,1,0:T(8,128)}, f32[2,128,768]{2,1,0:T(8,128)}) fusion(f32[2,128,768]{2,1,0:T(8,128)} %param.33, f32[2,128,768]{2,1,0:T(8,128)S(1)} %copy-done.16, f32[2,128,768]{2,1,0:T(8,128)S(1)} %copy-done.17, f32[2,128,768]{2,1,0:T(8,128)} %param.28), kind=kLoop, calls=%fused_computation.68 | loop fusion | flops 1966080 | bytes 5505024 | tf_op jit(solution)/shard_map/add | solution.py:395
  245.5 2.6 %add_multiply_fusion = (f32[2,1536,128]{2,1,0:T(8,128)}, f32[2,1536,128]{2,1,0:T(8,128)}, f32[2,1536,128]{2,1,0:T(8,128)}) fusion(f32[2,1536,128]{2,1,0:T(8,128)S(1)} %copy-done.23, f32[2,1536,128]{2,1,0:T(8,128)S(1)} %copy-done.10, f32[2,1536,128]{2,1,0:T(8,128)S(1)} %bitcast.435, f32[2,1536,128]{2,1,0:T(8,128)S(1)} %copy-done.24), kind=kLoop, calls=%fused_computation.13 | loop fusion | flops 3932160 | bytes 11010048 | tf_op jit(solution)/shard_map/add | solution.py:395
  248.1 2.2 dynamic-slice_add_fusion
  (306 shorter events, 18.4 us)
Async XLA Ops:
  7.2 42.6 %all-gather.4.cloned.1.call-start = ((), (), s32[]{:S(2)}) async-start(), calls=%async_computation | async-start | bytes 1966080 | tf_op jit(solution)/shard_map/all_gather | solution.py:412
  9.3 54.4 %all-gather.6.cloned.1.call-start = ((), (), s32[]{:S(2)}) async-start(), calls=%async_computation.1 | async-start | bytes 2621440 | tf_op jit(solution)/shard_map/all_gather | solution.py:412
  10.5 12.5 %copy-start.31 = (bf16[768,128]{1,0:T(8,128)(2,1)S(1)}, bf16[768,128]{1,0:T(8,128)(2,1)}, u32[]{:S(2)}) copy-start(bf16[768,128]{1,0:T(8,128)(2,1)} %param.19) | copy-start | bytes 589828
  10.6 77.1 %all-gather.8.cloned.1.call-start = ((), (), s32[]{:S(2)}) async-start(), calls=%async_computation.2 | async-start | bytes 2621440 | tf_op jit(solution)/shard_map/all_gather | solution.py:412
  12.1 9.7 %copy-start.55 = (f32[1,384]{1,0:T(1,128)}, f32[1,384]{1,0:T(1,128)S(1)}, u32[]{:S(2)}) copy-start(f32[1,384]{1,0:T(1,128)S(1)} %get-tuple-element.183) | copy-start | bytes 4612
  12.1 33.9 %copy-start.35 = (f32[1,384]{1,0:T(1,128)}, f32[1,384]{1,0:T(1,128)S(1)}, u32[]{:S(2)}) copy-start(f32[1,384]{1,0:T(1,128)S(1)} %get-tuple-element.184) | copy-start | bytes 4612
  12.1 33.9 %copy-start.41 = (f32[1,384]{1,0:T(1,128)}, f32[1,384]{1,0:T(1,128)S(1)}, u32[]{:S(2)}) copy-start(f32[1,384]{1,0:T(1,128)S(1)} %get-tuple-element.185) | copy-start | bytes 4612
  18.5 45.3 %copy-start.73 = (f32[1,1,512]{2,1,0:T(1,128)}, f32[1,1,512]{2,1,0:T(1,128)S(1)}, u32[]{:S(2)}) copy-start(f32[1,1,512]{2,1,0:T(1,128)S(1)} %get-tuple-element.249) | copy-start | bytes 6148
  18.5 45.3 %copy-start.75 = (f32[1,1,512]{2,1,0:T(1,128)}, f32[1,1,512]{2,1,0:T(1,128)S(1)}, u32[]{:S(2)}) copy-start(f32[1,1,512]{2,1,0:T(1,128)S(1)} %get-tuple-element.250) | copy-start | bytes 6148
  18.5 45.3 %copy-start.94 = (f32[1,1,512]{2,1,0:T(1,128)}, f32[1,1,512]{2,1,0:T(1,128)S(1)}, u32[]{:S(2)}) copy-start(f32[1,1,512]{2,1,0:T(1,128)S(1)} %get-tuple-element.248) | copy-start | bytes 6148
  18.5 69.2 %copy-start.61 = (f32[1,1,512]{2,1,0:T(1,128)}, f32[1,1,512]{2,1,0:T(1,128)S(1)}, u32[]{:S(2)}) copy-start(f32[1,1,512]{2,1,0:T(1,128)S(1)} %get-tuple-element.246) | copy-start | bytes 6148
  18.5 69.2 %copy-start.77 = (f32[1,1,512]{2,1,0:T(1,128)}, f32[1,1,512]{2,1,0:T(1,128)S(1)}, u32[]{:S(2)}) copy-start(f32[1,1,512]{2,1,0:T(1,128)S(1)} %get-tuple-element.245) | copy-start | bytes 6148
  18.5 69.2 %copy-start.96 = (f32[1,1,512]{2,1,0:T(1,128)}, f32[1,1,512]{2,1,0:T(1,128)S(1)}, u32[]{:S(2)}) copy-start(f32[1,1,512]{2,1,0:T(1,128)S(1)} %get-tuple-element.243) | copy-start | bytes 6148
  21.6 15.2 %copy-start.32 = (bf16[768,128]{1,0:T(8,128)(2,1)S(1)}, bf16[768,128]{1,0:T(8,128)(2,1)}, u32[]{:S(2)}) copy-start(bf16[768,128]{1,0:T(8,128)(2,1)} %param.20) | copy-start | bytes 589828
  36.2 11.7 %copy-start.4 = (bf16[768,512]{1,0:T(8,128)(2,1)}, bf16[768,512]{1,0:T(8,128)(2,1)S(1)}, u32[]{:S(2)}) copy-start(bf16[768,512]{1,0:T(8,128)(2,1)S(1)} %all_gather.18) | copy-start | bytes 2359300
  36.4 27.4 %copy-start.51 = (f32[768]{0:T(1024)}, f32[768]{0:T(1024)S(1)}, u32[]{:S(2)}) copy-start(f32[768]{0:T(1024)S(1)} %broadcast_multiply_fusion.6) | copy-start | bytes 9220
  36.8 27.0 %copy-start.49 = (f32[768]{0:T(1024)}, f32[768]{0:T(1024)S(1)}, u32[]{:S(2)}) copy-start(f32[768]{0:T(1024)S(1)} %add_rsqrt_fusion.1) | copy-start | bytes 9220
  54.9 8.9 %copy-start.5 = (bf16[768,512]{1,0:T(8,128)(2,1)S(1)}, bf16[768,512]{1,0:T(8,128)(2,1)}, u32[]{:S(2)}) copy-start(bf16[768,512]{1,0:T(8,128)(2,1)} %copy-done.4) | copy-start | bytes 2359300
  69.5 3.5 %copy-start.11 = (f32[768,512]{1,0:T(8,128)}, f32[768,512]{1,0:T(8,128)S(1)}, u32[]{:S(2)}) copy-start(f32[768,512]{1,0:T(8,128)S(1)} %get-tuple-element.297) | copy-start | bytes 4718596
  73.0 14.7 %copy-start.46 = (f32[768]{0:T(1024)}, f32[768]{0:T(1024)S(1)}, u32[]{:S(2)}) copy-start(f32[768]{0:T(1024)S(1)} %broadcast_multiply_fusion.5) | copy-start | bytes 9220
  73.4 14.3 %copy-start.53 = (f32[768]{0:T(1024)}, f32[768]{0:T(1024)S(1)}, u32[]{:S(2)}) copy-start(f32[768]{0:T(1024)S(1)} %add_rsqrt_fusion) | copy-start | bytes 9220
  78.9 8.8 %copy-start.3 = (f32[768,512]{1,0:T(8,128)S(1)}, f32[768,512]{1,0:T(8,128)}, u32[]{:S(2)}) copy-start(f32[768,512]{1,0:T(8,128)} %copy-done.2) | copy-start | bytes 4718596
  87.7 4.3 %copy-start.7 = (bf16[768,512]{1,0:T(8,128)(2,1)S(1)}, bf16[768,512]{1,0:T(8,128)(2,1)}, u32[]{:S(2)}) copy-start(bf16[768,512]{1,0:T(8,128)(2,1)} %all_gather.23) | copy-start | bytes 2359300
  87.8 4.3 %copy-start.34 = (bf16[2048,512]{1,0:T(8,128)(2,1)S(1)}, bf16[2048,512]{1,0:T(8,128)(2,1)}, u32[]{:S(2)}) copy-start(bf16[2048,512]{1,0:T(8,128)(2,1)} %all-gather.8.cloned.1.call-done) | copy-start | bytes 6291460
  94.9 3.2 %slice-start.2 = ((s8[4718592]{0:T(1024)(128)(4,1)}), s8[4194304]{0:T(1024)(128)(4,1)S(1)}, s32[]{:S(2)}) async-start(s8[4718592]{0:T(1024)(128)(4,1)} %bitcast.431), calls=%async_computation.5 | async-start | bytes 8388608
  120.8 3.7 %copy-start.8 = (f32[768,512]{1,0:T(8,128)S(1)}, f32[768,512]{1,0:T(8,128)}, u32[]{:S(2)}) copy-start(f32[768,512]{1,0:T(8,128)} %get-tuple-element.299) | copy-start | bytes 4718596
  120.8 3.7 %copy-start.12 = (f32[768,512]{1,0:T(8,128)S(1)}, f32[768,512]{1,0:T(8,128)}, u32[]{:S(2)}) copy-start(f32[768,512]{1,0:T(8,128)} %copy-done.11) | copy-start | bytes 4718596
  127.3 7.4 %slice-start = ((s8[4718592]{0:T(1024)(128)(4,1)}), s8[524288]{0:T(1024)(128)(4,1)S(1)}, s32[]{:S(2)}) async-start(s8[4718592]{0:T(1024)(128)(4,1)} %bitcast.429), calls=%async_computation.3 | async-start | bytes 1048576
  130.1 4.7 %slice-start.1 = ((s8[4718592]{0:T(1024)(128)(4,1)}), s8[4194304]{0:T(1024)(128)(4,1)S(1)}, s32[]{:S(2)}) async-start(s8[4718592]{0:T(1024)(128)(4,1)} %bitcast.429), calls=%async_computation.4 | async-start | bytes 8388608
  158.4 3.1 %copy-start.45 = (f32[1,384]{1,0:T(1,128)S(1)}, f32[1,384]{1,0:T(1,128)}, u32[]{:S(2)}) copy-start(f32[1,384]{1,0:T(1,128)} %copy-done.43) | copy-start | bytes 4612
  158.5 3.1 %copy-start.58 = (f32[1,384]{1,0:T(1,128)S(1)}, f32[1,384]{1,0:T(1,128)}, u32[]{:S(2)}) copy-start(f32[1,384]{1,0:T(1,128)} %get-tuple-element.254) | copy-start | bytes 4612
  158.5 3.1 %copy-start.60 = (f32[4,384]{1,0:T(4,128)S(1)}, f32[4,384]{1,0:T(4,128)}, u32[]{:S(2)}) copy-start(f32[4,384]{1,0:T(4,128)} %get-tuple-element.28) | copy-start | bytes 18436
  158.5 3.3 %copy-start.87 = (f32[1,384]{1,0:T(1,128)S(1)}, f32[1,384]{1,0:T(1,128)}, u32[]{:S(2)}) copy-start(f32[1,384]{1,0:T(1,128)} %get-tuple-element.155) | copy-start | bytes 4612
  158.5 3.3 %copy-start.90 = (f32[1,384]{1,0:T(1,128)S(1)}, f32[1,384]{1,0:T(1,128)}, u32[]{:S(2)}) copy-start(f32[1,384]{1,0:T(1,128)} %get-tuple-element.241) | copy-start | bytes 4612
  158.5 3.3 %copy-start.91 = (f32[1,384]{1,0:T(1,128)S(1)}, f32[1,384]{1,0:T(1,128)}, u32[]{:S(2)}) copy-start(f32[1,384]{1,0:T(1,128)} %get-tuple-element.242) | copy-start | bytes 4612
  159.5 3.7 %copy-start.28 = (f32[1,512,128]{2,1,0:T(8,128)S(1)}, f32[1,512,128]{2,1,0:T(8,128)}, u32[]{:S(2)}) copy-start(f32[1,512,128]{2,1,0:T(8,128)} %convolution_bitcast_fusion.4) | copy-start | bytes 786436
  159.5 3.8 %copy-start.29 = (f32[1,512,128]{2,1,0:T(8,128)S(1)}, f32[1,512,128]{2,1,0:T(8,128)}, u32[]{:S(2)}) copy-start(f32[1,512,128]{2,1,0:T(8,128)} %convolution_bitcast_fusion.5) | copy-start | bytes 786436
  161.9 3.2 %copy-start.27 = (bf16[768,768]{1,0:T(8,128)(2,1)S(1)}, bf16[768,768]{1,0:T(8,128)(2,1)}, u32[]{:S(2)}) copy-start(bf16[768,768]{1,0:T(8,128)(2,1)} %get-tuple-element.27) | copy-start | bytes 3538948
  234.0 5.0 %copy-start.66 = (f32[8,128]{1,0:T(8,128)}, f32[8,128]{1,0:T(8,128)S(1)}, u32[]{:S(2)}) copy-start(f32[8,128]{1,0:T(8,128)S(1)} %slice_multiply_fusion.4) | copy-start | bytes 12292
  234.0 5.5 %copy-start.20 = (f32[1024,128]{1,0:T(8,128)}, f32[1024,128]{1,0:T(8,128)S(1)}, u32[]{:S(2)}) copy-start(f32[1024,128]{1,0:T(8,128)S(1)} %slice_multiply_fusion.2) | copy-start | bytes 1572868
  235.4 3.5 %copy-start.65 = (f32[2,4,128]{2,1,0:T(4,128)S(1)}, f32[2,4,128]{2,1,0:T(4,128)}, u32[]{:S(2)}) copy-start(f32[2,4,128]{2,1,0:T(4,128)} %param.26) | copy-start | bytes 12292
  235.4 3.5 %copy-start.92 = (f32[2,4,128]{2,1,0:T(4,128)S(1)}, f32[2,4,128]{2,1,0:T(4,128)}, u32[]{:S(2)}) copy-start(f32[2,4,128]{2,1,0:T(4,128)} %param.36) | copy-start | bytes 12292
  235.4 3.5 %copy-start.93 = (f32[2,4,128]{2,1,0:T(4,128)S(1)}, f32[2,4,128]{2,1,0:T(4,128)}, u32[]{:S(2)}) copy-start(f32[2,4,128]{2,1,0:T(4,128)} %param.31) | copy-start | bytes 12292
  235.4 4.1 %copy-start.19 = (f32[2,512,128]{2,1,0:T(8,128)S(1)}, f32[2,512,128]{2,1,0:T(8,128)}, u32[]{:S(2)}) copy-start(f32[2,512,128]{2,1,0:T(8,128)} %param.25) | copy-start | bytes 1572868
  239.6 5.9 %copy-start.24 = (f32[2,1536,128]{2,1,0:T(8,128)S(1)}, f32[2,1536,128]{2,1,0:T(8,128)}, u32[]{:S(2)}) copy-start(f32[2,1536,128]{2,1,0:T(8,128)} %param.29) | copy-start | bytes 4718596
  242.3 3.2 %copy-start.10 = (f32[2,1536,128]{2,1,0:T(8,128)S(1)}, f32[2,1536,128]{2,1,0:T(8,128)}, u32[]{:S(2)}) copy-start(f32[2,1536,128]{2,1,0:T(8,128)} %param.24) | copy-start | bytes 4718596
  242.3 3.2 %copy-start.13 = (f32[3072,128]{1,0:T(8,128)S(1)}, f32[3072,128]{1,0:T(8,128)}, u32[]{:S(2)}) copy-start(f32[3072,128]{1,0:T(8,128)} %slice_multiply_fusion) | copy-start | bytes 4718596
  242.3 3.2 %copy-start.23 = (f32[2,1536,128]{2,1,0:T(8,128)S(1)}, f32[2,1536,128]{2,1,0:T(8,128)}, u32[]{:S(2)}) copy-start(f32[2,1536,128]{2,1,0:T(8,128)} %param.34) | copy-start | bytes 4718596
  (61 other events, 123.6 us)
Sparse Core Ops, SparseCore 0:
  10.2 26.4 all-gather.3
  38.8 22.4 all-gather.5
  63.4 22.8 all-gather.7

commit v20 on v19

--- a/solution.py
+++ b/solution.py
@@ -412,6 +412,20 @@
     return lax.all_gather(value, "feat", axis=axis, tiled=True)
 
 
+def split_exact(value):
+    high = lax.reduce_precision(value, exponent_bits=8, mantissa_bits=7)
+    rest = value - high
+    middle = lax.reduce_precision(rest, exponent_bits=8, mantissa_bits=7)
+    little = rest - middle
+    return jnp.concatenate([high, middle, little], 0).astype(jnp.bfloat16)
+
+
+def join_exact(pieces):
+    third = pieces.shape[0] // 3
+    pieces = pieces.astype(jnp.float32)
+    return pieces[:third] + (pieces[third : 2 * third] + pieces[2 * third :])
+
+
 def body(
     activations_in,
     cotangent,
@@ -458,8 +472,13 @@
     ]
     out_all = [pair[:rows_out] for pair in paired]
     gate_all = [pair[rows_out:] for pair in paired]
-    feature_all = gather_feat(feature_vectors, 2)
-    stream = gather_feat(activations_in, 1).astype(jnp.float32)
+    feature_pieces = split_exact(feature_vectors.reshape(-1, activations_in.shape[1]))
+    feature_rows = feature_pieces.shape[0]
+    feature_pad = -(-feature_rows // 16) * 16
+    feature_pieces = jnp.pad(feature_pieces, ((0, feature_pad - feature_rows), (0, 0)))
+    first = gather_feat(jnp.concatenate([activations_in, feature_pieces], 0), 1)
+    stream = first[:count].astype(jnp.float32)
+    feature_all = join_exact(first[count : count + feature_rows]).reshape(feature_vectors.shape[:-1] + (-1,))
 
     saved = []
     for layer in range(layers):

time: 257 us -> 252 us (0.981)
  blocking collectives: 28.4 us -> 20.2 us
  waiting for transfers between devices: 0.05 us -> 4.76 us
    all_gather x3 -> x2, blocking collectives: 28.4 us -> 20.2 us  [gather_feat(): return lax.all_gather(value, 'feat', axis=axis, tiled=True)]
    all_gather x3, waiting for transfers between devices: 0.01 us -> 4.72 us  [gather_feat(): return lax.all_gather(value, 'feat', axis=axis, tiled=True)]
    unnamed x220 -> x140, local copies, waits for them, and re-layouts: 8.31 us -> 8.75 us
  transfers between devices with their start and end apart: 3 -> 3, of which waited for: 0 -> 2; matrix products, arithmetic and copies ran while one was open for 11% -> 11% of each run, Pallas kernels for 7% -> 7%
where the time goes in v20:
time: 252 us; the launch traced here: 251 us
  Pallas kernels  110 us (44%)
  matrix products  47.5 us (19%)
  other arithmetic  37.9 us (15%)
  blocking collectives  20.2 us (8%)
  local copies, waits for them, and re-layouts  16.6 us (7%)
  between operations  14.7 us (6%)
  waiting for transfers between devices  4.76 us (2%)
    pallas_call x1, Pallas kernels, ring_sum(): pl.pallas_call(lambda *refs: ring_sum_kernel(n, *refs), out_shape=jax.Sha...  61.3 us
    pallas_call x2, Pallas kernels, adjoint(): pl.pallas_call(adjoint_kernel, out_shape=(jax.ShapeDtypeStruct((count, 2...  30.8 us
    all_gather x2, blocking collectives, gather_feat(): return lax.all_gather(value, 'feat', axis=axis, tiled=True)  20.2 us
    pallas_call x2, Pallas kernels, recurrence(): pl.pallas_call(recurrence_kernel, out_shape=jax.ShapeDtypeStruct((count,...  17.6 us
    dot_general x4, matrix products, contract_cols(): lax.dot_general(left, right, (((1,), (1,)), ((), ())), preferred_element_...  14.2 us
    dot_general x2, matrix products, body(): jnp.dot(states_low, out_low, preferred_element_type=jnp.float32)  10 us
    add x5, other arithmetic, update(): average_new = smoothing * average + (1.0 - smoothing) * weight_new  9.08 us
    unnamed x140, local copies, waits for them, and re-layouts  8.75 us
  transfers between devices with their start and end apart: 3, of which 2 were waited for; matrix products, arithmetic and copies ran while one was open for 11% of the time, Pallas kernels for 7%

profile of v20, /device:TPU:0, one launch (start us, length us, event | category | flops | bytes accessed | tf_op | source)
XLA Modules:
  0.0 251.4 jit_solution(18427380373618553734)
XLA Ops:
  7.3 2.1 convert_element_type.103
  9.7 0.8 pad_maximum_fusion.4
  10.6 0.8 pad_maximum_fusion.5
  12.2 10.2 %all_gather.15 = bf16[800,512]{1,0:T(8,128)(2,1)S(1)} all-gather(bf16[800,128]{1,0:T(8,128)(2,1)S(1)} %pad_maximum_fusion.7), channel_id=1, replica_groups=mesh['seq'=8,'feat'=4] {'feat'}, dimensions={1}, use_global_device_ids=true | all-gather | bytes 1024000 | tf_op jit(solution)/shard_map/all_gather | solution.py:412
  25.2 0.9 copy.86.masks_ref
  26.6 10.0 %all_gather.19 = bf16[768,512]{1,0:T(8,128)(2,1)} all-gather(bf16[768,128]{1,0:T(8,128)(2,1)S(1)} %copy-done.31), channel_id=1, replica_groups=mesh['seq'=8,'feat'=4] {'feat'}, dimensions={1}, use_global_device_ids=true | all-gather | bytes 983040 | tf_op jit(solution)/shard_map/all_gather | solution.py:412
  37.2 1.2 fusion.9
  40.4 2.2 fusion.15.drive_ref
  43.0 1.0 copy-done
  44.0 1.6 pad_maximum_fusion.x_ref
  45.7 8.8 %shard_map.354.states_ref = f32[768,1536]{1,0:T(8,128)} custom-call(s32[2]{0:T(128)} %starts_ref.7, s32[2]{0:T(128)} %lengths_ref.7, f32[4,8,384]{2,1,0:T(8,128)} %pad_maximum_fusion.8.pow_ref, f32[768,768]{1,0:T(8,128)} %pad_maximum_fusion.x_ref), custom_call_target="tpu_custom_call" | custom-call | flops 11796480 | bytes 9437184 | tf_op jit(solution)/shard_map/pallas_call | solution.py:144
  54.5 3.6 %all-gather.6.cloned.1.call-done = bf16[2048,512]{1,0:T(8,128)(2,1)} async-done(((bf16[2048,128]{1,0:T(8,128)(2,1)}), bf16[2048,512]{1,0:T(8,128)(2,1)}) %all-gather.6.cloned.1.call-update) | async-done | bytes 2097168 | tf_op jit(solution)/shard_map/all_gather | solution.py:412
  58.1 5.7 %fusion.91 = (f32[768,512]{1,0:T(8,128)S(1)}, f32[768,512]{1,0:T(8,128)}) fusion(f32[512]{0:T(512)S(1)} %bitcast.465, f32[512]{0:T(512)S(1)} %bitcast.468, f32[768]{0:T(1024)S(1)} %add_rsqrt_fusion.1, f32[768]{0:T(1024)S(1)} %broadcast_multiply_fusion.6, bf16[800,512]{1,0:T(8,128)(2,1)S(1)} %copy-done.5, f32[512]{0:T(512)S(1)} %bitcast.474, ...), kind=kOutput, calls=%fused_computation.342 | convolution fusion | flops 1213464576 | bytes 10235904 | tf_op jit(solution)/shard_map/dot_general | solution.py:509
  63.8 3.4 %fusion.109 = (f32[768]{0:T(1024)S(1)}, f32[768,512]{1,0:T(8,128)S(1)}, f32[768,512]{1,0:T(8,128)}) fusion(f32[768,512]{1,0:T(8,128)S(1)} %get-tuple-element.300, bf16[800,512]{1,0:T(8,128)(2,1)S(1)} %copy-done.5, f32[512]{0:T(512)S(1)} %bitcast.479, bf16[2048,512]{1,0:T(8,128)(2,1)} %all-gather.6.cloned.1.call-done), kind=kOutput, calls=%fused_computation.350 | convolution fusion | flops 406191360 | bytes 7607296 | tf_op jit(solution)/shard_map/dot_general | solution.py:515
  68.3 0.9 copy-done.26
  70.5 1.1 copy-done.1
  71.6 1.6 pad_maximum_fusion.1.x_ref
  73.1 8.7 %shard_map.355.states_ref = f32[768,1536]{1,0:T(8,128)} custom-call(s32[2]{0:T(128)} %starts_ref.7, s32[2]{0:T(128)} %lengths_ref.7, f32[4,8,384]{2,1,0:T(8,128)} %pad_maximum_fusion.9.pow_ref, f32[768,768]{1,0:T(8,128)} %pad_maximum_fusion.1.x_ref), custom_call_target="tpu_custom_call" | custom-call | flops 11796480 | bytes 9437184 | tf_op jit(solution)/shard_map/pallas_call | solution.py:144
  81.9 1.2 all-gather.8.cloned.1.call-done
  83.1 4.3 %fusion.92 = (f32[768,512]{1,0:T(8,128)S(1)}, f32[768,512]{1,0:T(8,128)S(1)}) fusion(f32[512]{0:T(512)S(1)} %bitcast.471, f32[512]{0:T(512)S(1)} %bitcast.457, f32[768]{0:T(1024)S(1)} %add_rsqrt_fusion, f32[768,512]{1,0:T(8,128)S(1)} %copy-done.3, f32[768]{0:T(1024)S(1)} %broadcast_multiply_fusion.5, f32[512]{0:T(512)S(1)} %bitcast.476, ...), kind=kOutput, calls=%fused_computation.343 | convolution fusion | flops 1213071360 | bytes 11022336 | tf_op jit(solution)/shard_map/dot_general | solution.py:509
  87.4 1.6 convert_reduce_fusion.1
  89.4 0.9 dynamic-slice_add_fusion.1
  90.3 2.3 fusion.111
  92.7 1.7 convolution_bitcast_fusion
  94.4 3.6 %fusion.3.g_ref = f32[768,1536]{1,0:T(8,128)} fusion(bf16[768,512]{1,0:T(8,128)(2,1)S(1)} %get-tuple-element.306, bf16[2048,512]{1,0:T(8,128)(2,1)S(1)} %copy-done.33), kind=kOutput, calls=%fused_computation.43 | convolution fusion | flops 1207959552 | bytes 7077888 | tf_op jit(solution)/shard_map/dot_general | solution.py:406
  98.0 15.4 %shard_map.356 = (bf16[768,768]{1,0:T(8,128)(2,1)}, f32[4,384]{1,0:T(4,128)}) custom-call(s32[2]{0:T(128)} %starts_ref.7, s32[2]{0:T(128)} %lengths_ref.7, f32[4,8,384]{2,1,0:T(8,128)} %pad_maximum_fusion.10.pow_ref, f32[4,384]{1,0:T(4,128)} %pad_maximum_fusion.13.coef_ref, f32[768,4]{1,0:T(8,128)} %copy.86.masks_ref, f32[768,1536]{1,0:T(8,128)} %fusion.3.g_ref, ...), custom_call_target="tpu_custom_call" | custom-call | flops 17694720 | bytes 14155776 | tf_op jit(solution)/shard_map/pallas_call | solution.py:375
  113.4 2.6 %convolution_bitcast_fusion.2 = f32[1,128,768]{2,1,0:T(8,128)} fusion(bf16[768,768]{1,0:T(8,128)(2,1)} %get-tuple-element.26, bf16[768,512]{1,0:T(8,128)(2,1)} %copy-done.14, s32[]{:T(128)S(6)} %select_n.2), kind=kOutput, calls=%fused_computation.50 | convolution fusion | flops 150994944 | bytes 1769476 | tf_op jit(solution)/shard_map/dot_general | solution.py:400
  116.0 3.7 %multiply_reduce_fusion.1 = (f32[512]{0:T(512)}, f32[768]{0:T(1024)S(1)}, f32[512]{0:T(512)}, f32[768]{0:T(1024)S(1)}, f32[512]{0:T(512)}, /*index=5*/f32[768,512]{1,0:T(8,128)S(1)}) fusion(f32[768]{0:T(1024)S(1)} %add_rsqrt_fusion, f32[768,512]{1,0:T(8,128)S(1)} %copy-done.3, f32[768]{0:T(1024)S(1)} %broadcast_multiply_fusion.5, f32[512]{0:T(512)S(1)} %bitcast.458, ...), kind=kOutput, calls=%fused_computation.19 | convolution fusion | flops 609874944 | bytes 6709248 | tf_op jit(solution)/shard_map/dot_general | solution.py:555
  119.7 2.1 convert_reduce_fusion.2
  125.1 4.6 %fusion.112 = (bf16[768,512]{1,0:T(8,128)(2,1)S(1)}, f32[768,512]{1,0:T(8,128)}) fusion(f32[768,512]{1,0:T(8,128)} %get-tuple-element.301, bf16[768,512]{1,0:T(8,128)(2,1)} %copy-done.15, bf16[2048,512]{1,0:T(8,128)(2,1)} %all-gather.6.cloned.1.call-done, f32[768,512]{1,0:T(8,128)S(1)} %copy-done.6, f32[768,512]{1,0:T(8,128)} %get-tuple-element.302), kind=kOutput, calls=%fused_computation.353 | convolution fusion | flops 407371776 | bytes 8388608 | tf_op jit(solution)/shard_map/dot_general | solution.py:406
  129.8 1.7 convolution_bitcast_fusion.1
  132.8 3.6 %fusion.6.g_ref = f32[768,1536]{1,0:T(8,128)} fusion(bf16[768,512]{1,0:T(8,128)(2,1)S(1)} %get-tuple-element.309, bf16[2048,512]{1,0:T(8,128)(2,1)S(1)} %copy-done.32), kind=kOutput, calls=%fused_computation.46 | convolution fusion | flops 1207959552 | bytes 7077888 | tf_op jit(solution)/shard_map/dot_general | solution.py:406
  136.4 15.4 %shard_map.357 = (bf16[768,768]{1,0:T(8,128)(2,1)}, f32[4,384]{1,0:T(4,128)}) custom-call(s32[2]{0:T(128)} %starts_ref.7, s32[2]{0:T(128)} %lengths_ref.7, f32[4,8,384]{2,1,0:T(8,128)} %pad_maximum_fusion.11.pow_ref, f32[4,384]{1,0:T(4,128)} %pad_maximum_fusion.14.coef_ref, f32[768,4]{1,0:T(8,128)} %copy.86.masks_ref, f32[768,1536]{1,0:T(8,128)} %fusion.6.g_ref, ...), custom_call_target="tpu_custom_call" | custom-call | flops 17694720 | bytes 14155776 | tf_op jit(solution)/shard_map/pallas_call | solution.py:375
  151.8 1.8 convolution_bitcast_fusion.3
  153.6 0.9 pad_maximum_fusion.3
  154.6 2.1 reshape.1853
  156.9 1.3 constant_dynamic-update-slice_fusion.4
  158.3 1.6 pad_maximum_fusion.2
  160.7 2.9 %fusion.93 = (f32[512]{0:T(512)S(1)}, f32[512]{0:T(512)S(1)}, f32[512]{0:T(512)S(1)}, f32[768]{0:T(1024)S(1)}, f32[768]{0:T(1024)S(1)}, /*index=5*/f32[768,512]{1,0:T(8,128)}, f32[768,512]{1,0:T(8,128)}) fusion(f32[768]{0:T(1024)S(1)} %add_rsqrt_fusion.1, f32[768]{0:T(1024)S(1)} %broadcast_multiply_fusion.6, bf16[800,512]{1,0:T(8,128)(2,1)S(1)} %copy-done.5, ...), kind=kOutput, calls=%fused_computation.344 | convolution fusion | flops 610268160 | bytes 7497728 | tf_op jit(solution)/shard_map/dot_general | solution.py:555
  163.9 1.8 pad_bitcast_fusion.refs_0_
  165.7 61.3 %shard_map.358 = bf16[5888,128]{1,0:T(8,128)(2,1)} custom-call(f32[5888,128]{1,0:T(8,128)} %pad_bitcast_fusion.refs_0_), custom_call_target="tpu_custom_call" | custom-call | tf_op jit(solution)/shard_map/pallas_call | solution.py:267
  226.9 1.6 convert_element_type.123
  228.7 1.3 slice_multiply_fusion
  232.5 1.0 mul.6050
  234.2 2.6 %add_multiply_fusion.8 = (f32[2,512,128]{2,1,0:T(8,128)}, f32[2,512,128]{2,1,0:T(8,128)}, f32[2,512,128]{2,1,0:T(8,128)}) fusion(f32[2,512,128]{2,1,0:T(8,128)} %param.35, f32[2,512,128]{2,1,0:T(8,128)S(1)} %copy-done.19, f32[2,512,128]{2,1,0:T(8,128)S(1)} %bitcast.437, f32[2,512,128]{2,1,0:T(8,128)} %param.30), kind=kLoop, calls=%fused_computation.79 | loop fusion | flops 1310720 | bytes 3670016 | tf_op jit(solution)/shard_map/add | solution.py:395
  236.8 3.2 %add_multiply_fusion.7 = (f32[2,128,768]{2,1,0:T(8,128)}, f32[2,128,768]{2,1,0:T(8,128)}, f32[2,128,768]{2,1,0:T(8,128)}) fusion(f32[2,128,768]{2,1,0:T(8,128)} %param.33, f32[2,128,768]{2,1,0:T(8,128)S(1)} %copy-done.16, f32[2,128,768]{2,1,0:T(8,128)S(1)} %copy-done.17, f32[2,128,768]{2,1,0:T(8,128)} %param.28), kind=kLoop, calls=%fused_computation.68 | loop fusion | flops 1966080 | bytes 5505024 | tf_op jit(solution)/shard_map/add | solution.py:395
  240.0 2.6 %add_multiply_fusion = (f32[2,1536,128]{2,1,0:T(8,128)}, f32[2,1536,128]{2,1,0:T(8,128)}, f32[2,1536,128]{2,1,0:T(8,128)}) fusion(f32[2,1536,128]{2,1,0:T(8,128)S(1)} %copy-done.24, f32[2,1536,128]{2,1,0:T(8,128)S(1)} %copy-done.10, f32[2,1536,128]{2,1,0:T(8,128)S(1)} %bitcast.436, f32[2,1536,128]{2,1,0:T(8,128)S(1)} %copy-done.25), kind=kLoop, calls=%fused_computation.13 | loop fusion | flops 3932160 | bytes 11010048 | tf_op jit(solution)/shard_map/add | solution.py:395
  242.7 2.2 dynamic-slice_add_fusion
  (230 shorter events, 18.9 us)
Async XLA Ops:
  7.2 2.2 copy-start.9
  7.2 33.2 %all-gather.4.cloned.1.call-start = ((), (), s32[]{:S(2)}) async-start(), calls=%async_computation | async-start | bytes 1966080 | tf_op jit(solution)/shard_map/all_gather | solution.py:412
  9.3 48.7 %all-gather.6.cloned.1.call-start = ((), (), s32[]{:S(2)}) async-start(), calls=%async_computation.1 | async-start | bytes 2621440 | tf_op jit(solution)/shard_map/all_gather | solution.py:412
  9.7 2.5 copy-start.37
  9.7 2.5 copy-start.30
  10.5 72.5 %all-gather.8.cloned.1.call-start = ((), (), s32[]{:S(2)}) async-start(), calls=%async_computation.2 | async-start | bytes 2621440 | tf_op jit(solution)/shard_map/all_gather | solution.py:412
  11.4 11.2 %copy-start.36 = (s32[2]{0:T(128)S(1)}, s32[2]{0:T(128)}, u32[]{:S(2)}) copy-start(s32[2]{0:T(128)} %starts_ref.7) | copy-start | bytes 28
  11.4 11.2 %copy-start.39 = (s32[2]{0:T(128)S(1)}, s32[2]{0:T(128)}, u32[]{:S(2)}) copy-start(s32[2]{0:T(128)} %lengths_ref.7) | copy-start | bytes 28
  22.5 14.8 %copy-start.4 = (bf16[800,512]{1,0:T(8,128)(2,1)}, bf16[800,512]{1,0:T(8,128)(2,1)S(1)}, u32[]{:S(2)}) copy-start(bf16[800,512]{1,0:T(8,128)(2,1)S(1)} %all_gather.15) | copy-start | bytes 2457604
  22.5 4.2 %copy-start.31 = (bf16[768,128]{1,0:T(8,128)(2,1)S(1)}, bf16[768,128]{1,0:T(8,128)(2,1)}, u32[]{:S(2)}) copy-start(bf16[768,128]{1,0:T(8,128)(2,1)} %param.20) | copy-start | bytes 589828
  26.6 31.4 %copy-start.54 = (f32[1,512]{1,0:T(1,128)}, f32[1,512]{1,0:T(1,128)S(1)}, u32[]{:S(2)}) copy-start(f32[1,512]{1,0:T(1,128)S(1)} %get-tuple-element.248) | copy-start | bytes 6148
  26.6 56.4 %copy-start.56 = (f32[1,512]{1,0:T(1,128)}, f32[1,512]{1,0:T(1,128)S(1)}, u32[]{:S(2)}) copy-start(f32[1,512]{1,0:T(1,128)S(1)} %get-tuple-element.243) | copy-start | bytes 6148
  45.7 12.4 %copy-start.5 = (bf16[800,512]{1,0:T(8,128)(2,1)S(1)}, bf16[800,512]{1,0:T(8,128)(2,1)}, u32[]{:S(2)}) copy-start(bf16[800,512]{1,0:T(8,128)(2,1)} %copy-done.4) | copy-start | bytes 2457604
  63.8 3.4 %copy-start.11 = (f32[768,512]{1,0:T(8,128)}, f32[768,512]{1,0:T(8,128)S(1)}, u32[]{:S(2)}) copy-start(f32[768,512]{1,0:T(8,128)S(1)} %get-tuple-element.300) | copy-start | bytes 4718596
  73.1 9.9 %copy-start.3 = (f32[768,512]{1,0:T(8,128)S(1)}, f32[768,512]{1,0:T(8,128)}, u32[]{:S(2)}) copy-start(f32[768,512]{1,0:T(8,128)} %copy-done.2) | copy-start | bytes 4718596
  83.1 4.3 %copy-start.7 = (bf16[768,512]{1,0:T(8,128)(2,1)S(1)}, bf16[768,512]{1,0:T(8,128)(2,1)}, u32[]{:S(2)}) copy-start(bf16[768,512]{1,0:T(8,128)(2,1)} %all_gather.19) | copy-start | bytes 2359300
  83.1 4.3 %copy-start.33 = (bf16[2048,512]{1,0:T(8,128)(2,1)S(1)}, bf16[2048,512]{1,0:T(8,128)(2,1)}, u32[]{:S(2)}) copy-start(bf16[2048,512]{1,0:T(8,128)(2,1)} %all-gather.8.cloned.1.call-done) | copy-start | bytes 6291460
  89.4 3.2 %slice-start.2 = ((s8[4718592]{0:T(1024)(128)(4,1)}), s8[4194304]{0:T(1024)(128)(4,1)S(1)}, s32[]{:S(2)}) async-start(s8[4718592]{0:T(1024)(128)(4,1)} %bitcast.432), calls=%async_computation.5 | async-start | bytes 8388608
  90.3 2.3 slice-start.3
  113.4 2.6 %copy-start.22 = (f32[768,512]{1,0:T(8,128)S(1)}, f32[768,512]{1,0:T(8,128)}, u32[]{:S(2)}) copy-start(f32[768,512]{1,0:T(8,128)} %get-tuple-element.307) | copy-start | bytes 4718596
  113.4 2.6 %copy-start.57 = (f32[1,512]{1,0:T(1,128)S(1)}, f32[1,512]{1,0:T(1,128)}, u32[]{:S(2)}) copy-start(f32[1,512]{1,0:T(1,128)} %copy-done.56) | copy-start | bytes 6148
  116.0 3.7 %copy-start.8 = (f32[768,512]{1,0:T(8,128)S(1)}, f32[768,512]{1,0:T(8,128)}, u32[]{:S(2)}) copy-start(f32[768,512]{1,0:T(8,128)} %get-tuple-element.302) | copy-start | bytes 4718596
  116.0 3.7 %copy-start.12 = (f32[768,512]{1,0:T(8,128)S(1)}, f32[768,512]{1,0:T(8,128)}, u32[]{:S(2)}) copy-start(f32[768,512]{1,0:T(8,128)} %copy-done.11) | copy-start | bytes 4718596
  121.8 2.2 copy-start.45
  121.8 3.3 %copy-start.6 = (f32[768,512]{1,0:T(8,128)S(1)}, f32[768,512]{1,0:T(8,128)}, u32[]{:S(2)}) copy-start(f32[768,512]{1,0:T(8,128)} %get-tuple-element.159) | copy-start | bytes 4718596
  121.8 7.9 %slice-start = ((s8[4718592]{0:T(1024)(128)(4,1)}), s8[524288]{0:T(1024)(128)(4,1)S(1)}, s32[]{:S(2)}) async-start(s8[4718592]{0:T(1024)(128)(4,1)} %bitcast.430), calls=%async_computation.3 | async-start | bytes 1048576
  125.1 4.7 %slice-start.1 = ((s8[4718592]{0:T(1024)(128)(4,1)}), s8[4194304]{0:T(1024)(128)(4,1)S(1)}, s32[]{:S(2)}) async-start(s8[4718592]{0:T(1024)(128)(4,1)} %bitcast.430), calls=%async_computation.4 | async-start | bytes 8388608
  129.8 3.0 %copy-start.32 = (bf16[2048,512]{1,0:T(8,128)(2,1)S(1)}, bf16[2048,512]{1,0:T(8,128)(2,1)}, u32[]{:S(2)}) copy-start(bf16[2048,512]{1,0:T(8,128)(2,1)} %all-gather.6.cloned.1.call-done) | copy-start | bytes 6291460
  153.6 3.1 %copy-start.35 = (f32[4,384]{1,0:T(4,128)S(1)}, f32[4,384]{1,0:T(4,128)}, u32[]{:S(2)}) copy-start(f32[4,384]{1,0:T(4,128)} %get-tuple-element.28) | copy-start | bytes 18436
  153.6 3.1 %copy-start.48 = (f32[1,384]{1,0:T(1,128)S(1)}, f32[1,384]{1,0:T(1,128)}, u32[]{:S(2)}) copy-start(f32[1,384]{1,0:T(1,128)} %get-tuple-element.255) | copy-start | bytes 4612
  153.6 3.0 %copy-start.49 = (f32[1,384]{1,0:T(1,128)S(1)}, f32[1,384]{1,0:T(1,128)}, u32[]{:S(2)}) copy-start(f32[1,384]{1,0:T(1,128)} %get-tuple-element.252) | copy-start | bytes 4612
  153.6 3.2 %copy-start.47 = (f32[1,384]{1,0:T(1,128)S(1)}, f32[1,384]{1,0:T(1,128)}, u32[]{:S(2)}) copy-start(f32[1,384]{1,0:T(1,128)} %get-tuple-element.155) | copy-start | bytes 4612
  153.6 3.2 %copy-start.50 = (f32[1,384]{1,0:T(1,128)S(1)}, f32[1,384]{1,0:T(1,128)}, u32[]{:S(2)}) copy-start(f32[1,384]{1,0:T(1,128)} %get-tuple-element.241) | copy-start | bytes 4612
  153.6 3.2 %copy-start.51 = (f32[1,384]{1,0:T(1,128)S(1)}, f32[1,384]{1,0:T(1,128)}, u32[]{:S(2)}) copy-start(f32[1,384]{1,0:T(1,128)} %get-tuple-element.242) | copy-start | bytes 4612
  156.9 3.2 %copy-start.28 = (bf16[768,768]{1,0:T(8,128)(2,1)S(1)}, bf16[768,768]{1,0:T(8,128)(2,1)}, u32[]{:S(2)}) copy-start(bf16[768,768]{1,0:T(8,128)(2,1)} %get-tuple-element.27) | copy-start | bytes 3538948
  158.3 2.4 copy-start.27
  158.3 2.4 copy-start.55
  228.5 5.0 %copy-start.38 = (f32[8,128]{1,0:T(8,128)}, f32[8,128]{1,0:T(8,128)S(1)}, u32[]{:S(2)}) copy-start(f32[8,128]{1,0:T(8,128)S(1)} %slice_multiply_fusion.4) | copy-start | bytes 12292
  228.6 5.5 %copy-start.20 = (f32[1024,128]{1,0:T(8,128)}, f32[1024,128]{1,0:T(8,128)S(1)}, u32[]{:S(2)}) copy-start(f32[1024,128]{1,0:T(8,128)S(1)} %slice_multiply_fusion.2) | copy-start | bytes 1572868
  230.0 3.5 %copy-start.52 = (f32[2,4,128]{2,1,0:T(4,128)S(1)}, f32[2,4,128]{2,1,0:T(4,128)}, u32[]{:S(2)}) copy-start(f32[2,4,128]{2,1,0:T(4,128)} %param.36) | copy-start | bytes 12292
  230.0 3.5 %copy-start.53 = (f32[2,4,128]{2,1,0:T(4,128)S(1)}, f32[2,4,128]{2,1,0:T(4,128)}, u32[]{:S(2)}) copy-start(f32[2,4,128]{2,1,0:T(4,128)} %param.31) | copy-start | bytes 12292
  230.0 4.1 %copy-start.19 = (f32[2,512,128]{2,1,0:T(8,128)S(1)}, f32[2,512,128]{2,1,0:T(8,128)}, u32[]{:S(2)}) copy-start(f32[2,512,128]{2,1,0:T(8,128)} %param.25) | copy-start | bytes 1572868
  234.1 2.7 %copy-start.16 = (f32[2,128,768]{2,1,0:T(8,128)S(1)}, f32[2,128,768]{2,1,0:T(8,128)}, u32[]{:S(2)}) copy-start(f32[2,128,768]{2,1,0:T(8,128)} %param.23) | copy-start | bytes 2359300
  234.1 2.7 %copy-start.17 = (f32[2,128,768]{2,1,0:T(8,128)S(1)}, f32[2,128,768]{2,1,0:T(8,128)}, u32[]{:S(2)}) copy-start(f32[2,128,768]{2,1,0:T(8,128)} %mul.6050) | copy-start | bytes 2359300
  234.2 5.9 %copy-start.25 = (f32[2,1536,128]{2,1,0:T(8,128)S(1)}, f32[2,1536,128]{2,1,0:T(8,128)}, u32[]{:S(2)}) copy-start(f32[2,1536,128]{2,1,0:T(8,128)} %param.29) | copy-start | bytes 4718596
  236.8 3.2 %copy-start.10 = (f32[2,1536,128]{2,1,0:T(8,128)S(1)}, f32[2,1536,128]{2,1,0:T(8,128)}, u32[]{:S(2)}) copy-start(f32[2,1536,128]{2,1,0:T(8,128)} %param.24) | copy-start | bytes 4718596
  236.8 3.2 %copy-start.13 = (f32[3072,128]{1,0:T(8,128)S(1)}, f32[3072,128]{1,0:T(8,128)}, u32[]{:S(2)}) copy-start(f32[3072,128]{1,0:T(8,128)} %slice_multiply_fusion) | copy-start | bytes 4718596
  236.8 3.2 %copy-start.24 = (f32[2,1536,128]{2,1,0:T(8,128)S(1)}, f32[2,1536,128]{2,1,0:T(8,128)}, u32[]{:S(2)}) copy-start(f32[2,1536,128]{2,1,0:T(8,128)} %param.34) | copy-start | bytes 4718596
  (21 other events, 32.0 us)
Sparse Core Ops, SparseCore 0:
  10.2 23.1 all-gather.3
  35.5 22.4 all-gather.5
  60.2 22.8 all-gather.7

commit v21 on v20

--- a/solution.py
+++ b/solution.py
@@ -476,7 +476,8 @@
     feature_rows = feature_pieces.shape[0]
     feature_pad = -(-feature_rows // 16) * 16
     feature_pieces = jnp.pad(feature_pieces, ((0, feature_pad - feature_rows), (0, 0)))
-    first = gather_feat(jnp.concatenate([activations_in, feature_pieces], 0), 1)
+    first = gather_feat(jnp.concatenate([activations_in, feature_pieces, cotangent], 0), 1)
+    cotangent_all = first[count + feature_pad :]
     stream = first[:count].astype(jnp.float32)
     feature_all = join_exact(first[count : count + feature_rows]).reshape(feature_vectors.shape[:-1] + (-1,))
 
@@ -516,7 +517,7 @@
         saved.append((scale, unit, normed_low, drive, states, states_low, mixed, act, act_low, pre, cdf))
         stream = stream + act * jax.nn.sigmoid(pre)
 
-    grad = gather_feat(cotangent, 1).astype(jnp.float32) * alive[:, None]
+    grad = cotangent_all.astype(jnp.float32) * alive[:, None]
     layer_grads = [None] * layers
     for layer in reversed(range(layers)):
         scale, unit, normed_low, drive, states, states_low, mixed, act, act_low, pre, cdf = saved[layer]

time: 252 us -> 275 us (1.091)
  waiting for transfers between devices: 4.76 us -> 39.6 us
  blocking collectives: 20.2 us -> 0 us
  other arithmetic: 37.9 us -> 42 us
    all_gather x3 -> x4, waiting for transfers between devices: 4.72 us -> 39.5 us  [gather_feat(): return lax.all_gather(value, 'feat', axis=axis, tiled=True)]
    all_gather x2 -> x0, blocking collectives: 20.2 us -> none  [gather_feat(): return lax.all_gather(value, 'feat', axis=axis, tiled=True)]
    unnamed x140 -> x214, local copies, waits for them, and re-layouts: 8.75 us -> 11 us
  transfers between devices with their start and end apart: 3 -> 4, of which waited for: 2 -> 4; matrix products, arithmetic and copies ran while one was open for 11% -> 12% of each run, Pallas kernels for 7% -> 6%
where the time goes in v21:
time: 275 us; the launch traced here: 274 us
  Pallas kernels  110 us (40%)
  matrix products  49.2 us (18%)
  other arithmetic  42 us (15%)
  waiting for transfers between devices  39.6 us (14%)
  local copies, waits for them, and re-layouts  18.1 us (7%)
  between operations  15.2 us (6%)
    pallas_call x1, Pallas kernels, ring_sum(): pl.pallas_call(lambda *refs: ring_sum_kernel(n, *refs), out_shape=jax.Sha...  61.6 us
    all_gather x4, waiting for transfers between devices, gather_feat(): return lax.all_gather(value, 'feat', axis=axis, tiled=True)  39.5 us
    pallas_call x2, Pallas kernels, adjoint(): pl.pallas_call(adjoint_kernel, out_shape=(jax.ShapeDtypeStruct((count, 2...  30.9 us
    pallas_call x2, Pallas kernels, recurrence(): pl.pallas_call(recurrence_kernel, out_shape=jax.ShapeDtypeStruct((count,...  17.5 us
    dot_general x4, matrix products, contract_cols(): lax.dot_general(left, right, (((1,), (1,)), ((), ())), preferred_element_...  14.1 us
    unnamed x214, local copies, waits for them, and re-layouts  11 us
    dot_general x2, matrix products, body(): jnp.dot(states_low, out_low, preferred_element_type=jnp.float32)  10 us
    dot_general x6, matrix products, contract_rows(): lax.dot_general(left, right, (((0,), (0,)), ((), ())), preferred_element_...  9.22 us
  transfers between devices with their start and end apart: 4, of which 4 were waited for; matrix products, arithmetic and copies ran while one was open for 12% of the time, Pallas kernels for 6%

profile of v21, /device:TPU:0, one launch (start us, length us, event | category | flops | bytes accessed | tf_op | source)
XLA Modules:
  0.0 274.2 jit_solution(6583068132052442661)
XLA Ops:
  8.1 1.8 pad_maximum_fusion.7
  16.1 1.2 rev.30
  17.8 0.9 copy.86.masks_ref
  21.4 11.6 %all-gather.5.cloned.1.call-done = bf16[1568,512]{1,0:T(8,128)(2,1)} async-done(((bf16[1568,128]{1,0:T(8,128)(2,1)}), bf16[1568,512]{1,0:T(8,128)(2,1)}) %all-gather.5.cloned.1.call-update) | async-done | bytes 1605648 | tf_op jit(solution)/shard_map/all_gather | solution.py:412
  33.0 1.3 convert_reduce_fusion
  34.3 1.5 fusion.2
  36.7 2.4 fusion.9
  39.0 15.7 %all-gather.7.cloned.1.call-done = bf16[2,512,768]{2,1,0:T(8,128)(2,1)} async-done(((bf16[2,128,768]{2,1,0:T(8,128)(2,1)}), bf16[2,512,768]{2,1,0:T(8,128)(2,1)}) %all-gather.7.cloned.1.call-update) | async-done | bytes 1572880 | tf_op jit(solution)/shard_map/all_gather | solution.py:412
  54.8 2.1 fusion.15.drive_ref
  57.3 1.0 copy-done
  58.3 1.6 pad_maximum_fusion.x_ref
  59.9 8.7 %shard_map.354.states_ref = f32[768,1536]{1,0:T(8,128)} custom-call(s32[2]{0:T(128)} %starts_ref.7, s32[2]{0:T(128)} %lengths_ref.7, f32[4,8,384]{2,1,0:T(8,128)} %pad_maximum_fusion.8.pow_ref, f32[768,768]{1,0:T(8,128)} %pad_maximum_fusion.x_ref), custom_call_target="tpu_custom_call" | custom-call | flops 11796480 | bytes 9437184 | tf_op jit(solution)/shard_map/pallas_call | solution.py:144
  68.6 11.2 %all-gather.9.cloned.1.call-done = bf16[2048,512]{1,0:T(8,128)(2,1)} async-done(((bf16[2048,128]{1,0:T(8,128)(2,1)}), bf16[2048,512]{1,0:T(8,128)(2,1)}) %all-gather.9.cloned.1.call-update) | async-done | bytes 2097168 | tf_op jit(solution)/shard_map/all_gather | solution.py:412
  79.8 5.7 %fusion.91 = (f32[768,512]{1,0:T(8,128)S(1)}, f32[768,512]{1,0:T(8,128)}) fusion(f32[512]{0:T(512)S(1)} %bitcast.465, f32[512]{0:T(512)S(1)} %bitcast.468, f32[768]{0:T(1024)S(1)} %add_rsqrt_fusion.1, f32[768]{0:T(1024)S(1)} %broadcast_multiply_fusion.6, bf16[1568,512]{1,0:T(8,128)(2,1)S(1)} %copy-done.10, f32[512]{0:T(512)S(1)} %bitcast.474, ...), kind=kOutput, calls=%fused_computation.342 | convolution fusion | flops 1213464576 | bytes 10235904 | tf_op jit(solution)/shard_map/dot_general | solution.py:510
  85.5 3.4 %fusion.107 = (f32[768]{0:T(1024)S(1)}, f32[768,512]{1,0:T(8,128)S(1)}, f32[768,512]{1,0:T(8,128)}) fusion(f32[768,512]{1,0:T(8,128)S(1)} %get-tuple-element.296, bf16[1568,512]{1,0:T(8,128)(2,1)S(1)} %copy-done.10, f32[512]{0:T(512)S(1)} %bitcast.479, bf16[2048,512]{1,0:T(8,128)(2,1)} %all-gather.9.cloned.1.call-done), kind=kOutput, calls=%fused_computation.348 | convolution fusion | flops 406191360 | bytes 7607296 | tf_op jit(solution)/shard_map/dot_general | solution.py:516
  90.1 1.0 copy-done.22
  92.3 1.0 copy-done.1
  93.3 1.6 pad_maximum_fusion.1.x_ref
  94.9 8.7 %shard_map.355.states_ref = f32[768,1536]{1,0:T(8,128)} custom-call(s32[2]{0:T(128)} %starts_ref.7, s32[2]{0:T(128)} %lengths_ref.7, f32[4,8,384]{2,1,0:T(8,128)} %pad_maximum_fusion.9.pow_ref, f32[768,768]{1,0:T(8,128)} %pad_maximum_fusion.1.x_ref), custom_call_target="tpu_custom_call" | custom-call | flops 11796480 | bytes 9437184 | tf_op jit(solution)/shard_map/pallas_call | solution.py:144
  103.6 1.0 all-gather.11.cloned.1.call-done
  104.7 4.3 %fusion.92 = (f32[768,512]{1,0:T(8,128)S(1)}, f32[768,512]{1,0:T(8,128)S(1)}) fusion(f32[512]{0:T(512)S(1)} %bitcast.471, f32[512]{0:T(512)S(1)} %bitcast.457, f32[768]{0:T(1024)S(1)} %add_rsqrt_fusion, f32[768,512]{1,0:T(8,128)S(1)} %copy-done.3, f32[768]{0:T(1024)S(1)} %broadcast_multiply_fusion.5, f32[512]{0:T(512)S(1)} %bitcast.476, ...), kind=kOutput, calls=%fused_computation.343 | convolution fusion | flops 1213071360 | bytes 11022336 | tf_op jit(solution)/shard_map/dot_general | solution.py:510
  109.0 1.6 convert_reduce_fusion.1
  110.6 1.1 convolution_bitcast_fusion.4
  112.7 2.2 fusion.109
  114.9 1.7 convolution_bitcast_fusion
  116.7 3.7 %fusion.3.g_ref = f32[768,1536]{1,0:T(8,128)} fusion(bf16[768,512]{1,0:T(8,128)(2,1)S(1)} %get-tuple-element.302, bf16[2048,512]{1,0:T(8,128)(2,1)S(1)} %copy-done.98), kind=kOutput, calls=%fused_computation.43 | convolution fusion | flops 1207959552 | bytes 7077888 | tf_op jit(solution)/shard_map/dot_general | solution.py:406
  120.3 15.5 %shard_map.356 = (bf16[768,768]{1,0:T(8,128)(2,1)}, f32[4,384]{1,0:T(4,128)}) custom-call(s32[2]{0:T(128)} %starts_ref.7, s32[2]{0:T(128)} %lengths_ref.7, f32[4,8,384]{2,1,0:T(8,128)} %pad_maximum_fusion.10.pow_ref, f32[4,384]{1,0:T(4,128)} %pad_maximum_fusion.13.coef_ref, f32[768,4]{1,0:T(8,128)} %copy.86.masks_ref, f32[768,1536]{1,0:T(8,128)} %fusion.3.g_ref, ...), custom_call_target="tpu_custom_call" | custom-call | flops 17694720 | bytes 14155776 | tf_op jit(solution)/shard_map/pallas_call | solution.py:375
  135.8 1.7 convolution_bitcast_fusion.2
  137.7 3.8 %multiply_reduce_fusion.1 = (f32[512]{0:T(512)}, f32[768]{0:T(1024)S(1)}, f32[512]{0:T(512)}, f32[768]{0:T(1024)S(1)}, f32[512]{0:T(512)}, /*index=5*/f32[768,512]{1,0:T(8,128)S(1)}) fusion(f32[768]{0:T(1024)S(1)} %copy-done.51, f32[768,512]{1,0:T(8,128)S(1)} %copy-done.3, f32[768]{0:T(1024)S(1)} %copy-done.44, f32[512]{0:T(512)S(1)} %bitcast.458, ...), kind=kOutput, calls=%fused_computation.19 | convolution fusion | flops 609874944 | bytes 6711296 | tf_op jit(solution)/shard_map/dot_general | solution.py:556
  141.6 2.8 %convert_reduce_fusion.2 = (f32[512]{0:T(512)}, bf16[768,512]{1,0:T(8,128)(2,1)S(1)}, f32[768,512]{1,0:T(8,128)S(1)}) fusion(f32[768,512]{1,0:T(8,128)S(1)} %copy-done.4, f32[768,512]{1,0:T(8,128)S(1)} %copy-done.8, f32[768]{0:T(1024)S(1)} %broadcast_multiply_fusion.3, f32[768,512]{1,0:T(8,128)S(1)} %copy-done.3, f32[768]{0:T(1024)S(1)} %copy-done.44, ...), kind=kLoop, calls=%fused_computation.20 | loop fusion | flops 6684160 | bytes 9456640 | tf_op jit(solution)/shard_map/reduce_sum | solution.py:533
  144.4 1.2 convolution_bitcast_fusion.5
  147.2 4.6 %fusion.110 = (bf16[768,512]{1,0:T(8,128)(2,1)S(1)}, f32[768,512]{1,0:T(8,128)}) fusion(f32[768,512]{1,0:T(8,128)} %get-tuple-element.297, bf16[768,512]{1,0:T(8,128)(2,1)} %copy-done.12, bf16[2048,512]{1,0:T(8,128)(2,1)} %all-gather.9.cloned.1.call-done, f32[768,512]{1,0:T(8,128)S(1)} %get-tuple-element.159, f32[768,512]{1,0:T(8,128)} %get-tuple-element.298), kind=kOutput, calls=%fused_computation.351 | convolution fusion | flops 407371776 | bytes 8388608 | tf_op jit(solution)/shard_map/dot_general | solution.py:406
  151.9 1.7 convolution_bitcast_fusion.1
  154.8 3.6 %fusion.6.g_ref = f32[768,1536]{1,0:T(8,128)} fusion(bf16[768,512]{1,0:T(8,128)(2,1)S(1)} %get-tuple-element.305, bf16[2048,512]{1,0:T(8,128)(2,1)S(1)} %copy-done.30), kind=kOutput, calls=%fused_computation.46 | convolution fusion | flops 1207959552 | bytes 7077888 | tf_op jit(solution)/shard_map/dot_general | solution.py:406
  158.4 15.4 %shard_map.357 = (bf16[768,768]{1,0:T(8,128)(2,1)}, f32[4,384]{1,0:T(4,128)}) custom-call(s32[2]{0:T(128)} %starts_ref.7, s32[2]{0:T(128)} %lengths_ref.7, f32[4,8,384]{2,1,0:T(8,128)} %pad_maximum_fusion.11.pow_ref, f32[4,384]{1,0:T(4,128)} %pad_maximum_fusion.14.coef_ref, f32[768,4]{1,0:T(8,128)} %copy.86.masks_ref, f32[768,1536]{1,0:T(8,128)} %fusion.6.g_ref, ...), custom_call_target="tpu_custom_call" | custom-call | flops 17694720 | bytes 14155776 | tf_op jit(solution)/shard_map/pallas_call | solution.py:375
  173.8 1.7 convolution_bitcast_fusion.3
  176.8 1.1 pad_maximum_fusion.6
  178.4 1.1 copy-done.19
  180.0 4.1 %multiply_reduce_fusion.2 = (f32[512]{0:T(512)S(1)}, f32[512]{0:T(512)S(1)}, f32[768]{0:T(1024)S(1)}, f32[768]{0:T(1024)S(1)}, f32[512]{0:T(512)S(1)}, /*index=5*/f32[768,512]{1,0:T(8,128)}, f32[768,512]{1,0:T(8,128)}) fusion(f32[768,512]{1,0:T(8,128)S(1)} %copy-done.19, f32[512]{0:T(512)S(1)} %bitcast.466, f32[512]{0:T(512)S(1)} %bitcast.469, ...), kind=kOutput, calls=%fused_computation.21 | convolution fusion | flops 610268160 | bytes 7497728 | tf_op jit(solution)/shard_map/dot_general | solution.py:556
  184.3 1.8 pad_bitcast_fusion.refs_0_
  186.1 61.6 %shard_map.358 = bf16[5888,128]{1,0:T(8,128)(2,1)} custom-call(f32[5888,128]{1,0:T(8,128)} %pad_bitcast_fusion.refs_0_), custom_call_target="tpu_custom_call" | custom-call | tf_op jit(solution)/shard_map/pallas_call | solution.py:267
  247.7 1.6 convert_element_type.123
  250.1 0.9 slice_multiply_fusion.1
  253.7 2.2 mul.6050
  256.5 3.0 %add_multiply_fusion.8 = (f32[2,512,128]{2,1,0:T(8,128)}, f32[2,512,128]{2,1,0:T(8,128)}, f32[2,512,128]{2,1,0:T(8,128)}) fusion(f32[2,512,128]{2,1,0:T(8,128)} %param.35, f32[2,512,128]{2,1,0:T(8,128)} %param.25, f32[2,512,128]{2,1,0:T(8,128)} %bitcast.437, f32[2,512,128]{2,1,0:T(8,128)} %param.30), kind=kLoop, calls=%fused_computation.79 | loop fusion | flops 1310720 | bytes 3670016 | tf_op jit(solution)/shard_map/add | solution.py:395
  259.6 1.6 add_multiply_fusion.7
  262.7 2.7 add_multiply_fusion
  265.4 2.2 dynamic-slice_add_fusion
  (305 shorter events, 24.8 us)
Async XLA Ops:
  7.2 2.7 copy-start.13
  7.2 3.6 %copy-start.18 = (f32[2,512,128]{2,1,0:T(8,128)S(1)}, f32[2,512,128]{2,1,0:T(8,128)}, u32[]{:S(2)}) copy-start(f32[2,512,128]{2,1,0:T(8,128)} %param.25) | copy-start | bytes 1572868
  7.2 25.7 %all-gather.5.cloned.1.call-start = ((), (), s32[]{:S(2)}) async-start(), calls=%async_computation | async-start | bytes 2007040 | tf_op jit(solution)/shard_map/all_gather | solution.py:412
  9.9 44.9 %all-gather.7.cloned.1.call-start = ((), (), s32[]{:S(2)}) async-start(), calls=%async_computation.1 | async-start | bytes 1966080 | tf_op jit(solution)/shard_map/all_gather | solution.py:412
  10.7 69.0 %all-gather.9.cloned.1.call-start = ((), (), s32[]{:S(2)}) async-start(), calls=%async_computation.2 | async-start | bytes 2621440 | tf_op jit(solution)/shard_map/all_gather | solution.py:412
  12.5 92.2 %all-gather.11.cloned.1.call-start = ((), (), s32[]{:S(2)}) async-start(), calls=%async_computation.3 | async-start | bytes 2621440 | tf_op jit(solution)/shard_map/all_gather | solution.py:412
  14.1 3.6 %copy-start.52 = (f32[1,384]{1,0:T(1,128)}, f32[1,384]{1,0:T(1,128)S(1)}, u32[]{:S(2)}) copy-start(f32[1,384]{1,0:T(1,128)S(1)} %get-tuple-element.183) | copy-start | bytes 4612
  14.1 22.5 %copy-start.38 = (f32[1,384]{1,0:T(1,128)}, f32[1,384]{1,0:T(1,128)S(1)}, u32[]{:S(2)}) copy-start(f32[1,384]{1,0:T(1,128)S(1)} %get-tuple-element.185) | copy-start | bytes 4612
  14.3 98.4 %copy-start.36 = (f32[768]{0:T(1024)}, f32[768]{0:T(1024)S(1)}, u32[]{:S(2)}) copy-start(f32[768]{0:T(1024)S(1)} %get-tuple-element.295) | copy-start | bytes 9220
  15.0 24.0 %copy-start.31 = (f32[1,384]{1,0:T(1,128)}, f32[1,384]{1,0:T(1,128)S(1)}, u32[]{:S(2)}) copy-start(f32[1,384]{1,0:T(1,128)S(1)} %get-tuple-element.253) | copy-start | bytes 4612
  15.0 24.0 %copy-start.40 = (f32[1,384]{1,0:T(1,128)}, f32[1,384]{1,0:T(1,128)S(1)}, u32[]{:S(2)}) copy-start(f32[1,384]{1,0:T(1,128)S(1)} %get-tuple-element.252) | copy-start | bytes 4612
  16.1 23.0 %copy-start.34 = (f32[8,384]{1,0:T(8,128)}, f32[8,384]{1,0:T(8,128)S(1)}, u32[]{:S(2)}) copy-start(f32[8,384]{1,0:T(8,128)S(1)} %stack.266) | copy-start | bytes 36868
  34.3 45.5 %copy-start.48 = (f32[768]{0:T(1024)}, f32[768]{0:T(1024)S(1)}, u32[]{:S(2)}) copy-start(f32[768]{0:T(1024)S(1)} %broadcast_multiply_fusion.6) | copy-start | bytes 9220
  35.8 44.0 %copy-start.46 = (f32[768]{0:T(1024)}, f32[768]{0:T(1024)S(1)}, u32[]{:S(2)}) copy-start(f32[768]{0:T(1024)S(1)} %add_rsqrt_fusion.1) | copy-start | bytes 9220
  36.6 43.2 %copy-start.69 = (f32[1,512]{1,0:T(1,128)}, f32[1,512]{1,0:T(1,128)S(1)}, u32[]{:S(2)}) copy-start(f32[1,512]{1,0:T(1,128)S(1)} %get-tuple-element.245) | copy-start | bytes 6148
  36.6 43.2 %copy-start.71 = (f32[1,512]{1,0:T(1,128)}, f32[1,512]{1,0:T(1,128)S(1)}, u32[]{:S(2)}) copy-start(f32[1,512]{1,0:T(1,128)S(1)} %get-tuple-element.246) | copy-start | bytes 6148
  36.6 43.2 %copy-start.90 = (f32[1,512]{1,0:T(1,128)}, f32[1,512]{1,0:T(1,128)S(1)}, u32[]{:S(2)}) copy-start(f32[1,512]{1,0:T(1,128)S(1)} %get-tuple-element.244) | copy-start | bytes 6148
  36.6 68.0 %copy-start.58 = (f32[1,512]{1,0:T(1,128)}, f32[1,512]{1,0:T(1,128)S(1)}, u32[]{:S(2)}) copy-start(f32[1,512]{1,0:T(1,128)S(1)} %get-tuple-element.242) | copy-start | bytes 6148
  36.6 68.0 %copy-start.73 = (f32[1,512]{1,0:T(1,128)}, f32[1,512]{1,0:T(1,128)S(1)}, u32[]{:S(2)}) copy-start(f32[1,512]{1,0:T(1,128)S(1)} %get-tuple-element.241) | copy-start | bytes 6148
  36.6 68.0 %copy-start.92 = (f32[1,512]{1,0:T(1,128)}, f32[1,512]{1,0:T(1,128)S(1)}, u32[]{:S(2)}) copy-start(f32[1,512]{1,0:T(1,128)S(1)} %get-tuple-element.239) | copy-start | bytes 6148
  59.9 19.9 %copy-start.10 = (bf16[1568,512]{1,0:T(8,128)(2,1)S(1)}, bf16[1568,512]{1,0:T(8,128)(2,1)}, u32[]{:S(2)}) copy-start(bf16[1568,512]{1,0:T(8,128)(2,1)} %all-gather.5.cloned.1.call-done) | copy-start | bytes 4816900
  85.5 3.4 %copy-start.7 = (f32[768,512]{1,0:T(8,128)}, f32[768,512]{1,0:T(8,128)S(1)}, u32[]{:S(2)}) copy-start(f32[768,512]{1,0:T(8,128)S(1)} %get-tuple-element.296) | copy-start | bytes 4718596
  89.0 15.7 %copy-start.43 = (f32[768]{0:T(1024)}, f32[768]{0:T(1024)S(1)}, u32[]{:S(2)}) copy-start(f32[768]{0:T(1024)S(1)} %broadcast_multiply_fusion.5) | copy-start | bytes 9220
  89.3 15.3 %copy-start.50 = (f32[768]{0:T(1024)}, f32[768]{0:T(1024)S(1)}, u32[]{:S(2)}) copy-start(f32[768]{0:T(1024)S(1)} %add_rsqrt_fusion) | copy-start | bytes 9220
  94.9 9.8 %copy-start.3 = (f32[768,512]{1,0:T(8,128)S(1)}, f32[768,512]{1,0:T(8,128)}, u32[]{:S(2)}) copy-start(f32[768,512]{1,0:T(8,128)} %copy-done.2) | copy-start | bytes 4718596
  104.7 4.3 %copy-start.11 = (bf16[1568,512]{1,0:T(8,128)(2,1)S(1)}, bf16[1568,512]{1,0:T(8,128)(2,1)}, u32[]{:S(2)}) copy-start(bf16[1568,512]{1,0:T(8,128)(2,1)} %all-gather.5.cloned.1.call-done) | copy-start | bytes 4816900
  104.7 4.3 %copy-start.98 = (bf16[2048,512]{1,0:T(8,128)(2,1)S(1)}, bf16[2048,512]{1,0:T(8,128)(2,1)}, u32[]{:S(2)}) copy-start(bf16[2048,512]{1,0:T(8,128)(2,1)} %all-gather.11.cloned.1.call-done) | copy-start | bytes 6291460
  111.8 3.1 %slice-start.2 = ((s8[4718592]{0:T(1024)(128)(4,1)}), s8[4194304]{0:T(1024)(128)(4,1)S(1)}, s32[]{:S(2)}) async-start(s8[4718592]{0:T(1024)(128)(4,1)} %bitcast.432), calls=%async_computation.6 | async-start | bytes 8388608
  137.6 3.9 %copy-start.4 = (f32[768,512]{1,0:T(8,128)S(1)}, f32[768,512]{1,0:T(8,128)}, u32[]{:S(2)}) copy-start(f32[768,512]{1,0:T(8,128)} %get-tuple-element.298) | copy-start | bytes 4718596
  137.7 3.9 %copy-start.8 = (f32[768,512]{1,0:T(8,128)S(1)}, f32[768,512]{1,0:T(8,128)}, u32[]{:S(2)}) copy-start(f32[768,512]{1,0:T(8,128)} %copy-done.7) | copy-start | bytes 4718596
  137.7 3.9 %copy-start.37 = (f32[768]{0:T(1024)S(1)}, f32[768]{0:T(1024)}, u32[]{:S(2)}) copy-start(f32[768]{0:T(1024)} %copy-done.36) | copy-start | bytes 9220
  144.4 2.6 copy-start.79
  144.4 2.6 copy-start.80
  144.4 7.4 %slice-start = ((s8[4718592]{0:T(1024)(128)(4,1)}), s8[524288]{0:T(1024)(128)(4,1)S(1)}, s32[]{:S(2)}) async-start(s8[4718592]{0:T(1024)(128)(4,1)} %bitcast.430), calls=%async_computation.4 | async-start | bytes 1048576
  147.2 4.7 %slice-start.1 = ((s8[4718592]{0:T(1024)(128)(4,1)}), s8[4194304]{0:T(1024)(128)(4,1)S(1)}, s32[]{:S(2)}) async-start(s8[4718592]{0:T(1024)(128)(4,1)} %bitcast.430), calls=%async_computation.5 | async-start | bytes 8388608
  151.9 3.0 %copy-start.30 = (bf16[2048,512]{1,0:T(8,128)(2,1)S(1)}, bf16[2048,512]{1,0:T(8,128)(2,1)}, u32[]{:S(2)}) copy-start(bf16[2048,512]{1,0:T(8,128)(2,1)} %all-gather.9.cloned.1.call-done) | copy-start | bytes 6291460
  180.0 4.1 %copy-start.75 = (f32[512]{0:T(512)S(1)}, f32[512]{0:T(512)}, u32[]{:S(2)}) copy-start(f32[512]{0:T(512)} %get-tuple-element.157) | copy-start | bytes 6148
  249.3 6.7 %copy-start.62 = (f32[8,128]{1,0:T(8,128)}, f32[8,128]{1,0:T(8,128)S(1)}, u32[]{:S(2)}) copy-start(f32[8,128]{1,0:T(8,128)S(1)} %slice_multiply_fusion.4) | copy-start | bytes 12292
  251.2 10.0 %copy-start.9 = (f32[3072,128]{1,0:T(8,128)}, f32[3072,128]{1,0:T(8,128)S(1)}, u32[]{:S(2)}) copy-start(f32[3072,128]{1,0:T(8,128)S(1)} %slice_multiply_fusion) | copy-start | bytes 4718596
  251.2 4.7 %copy-start.61 = (f32[2,4,128]{2,1,0:T(4,128)S(1)}, f32[2,4,128]{2,1,0:T(4,128)}, u32[]{:S(2)}) copy-start(f32[2,4,128]{2,1,0:T(4,128)} %param.26) | copy-start | bytes 12292
  251.2 4.7 %copy-start.88 = (f32[2,4,128]{2,1,0:T(4,128)S(1)}, f32[2,4,128]{2,1,0:T(4,128)}, u32[]{:S(2)}) copy-start(f32[2,4,128]{2,1,0:T(4,128)} %param.36) | copy-start | bytes 12292
  251.2 4.7 %copy-start.89 = (f32[2,4,128]{2,1,0:T(4,128)S(1)}, f32[2,4,128]{2,1,0:T(4,128)}, u32[]{:S(2)}) copy-start(f32[2,4,128]{2,1,0:T(4,128)} %param.31) | copy-start | bytes 12292
  256.5 3.0 %copy-start.14 = (f32[2,128,768]{2,1,0:T(8,128)S(1)}, f32[2,128,768]{2,1,0:T(8,128)}, u32[]{:S(2)}) copy-start(f32[2,128,768]{2,1,0:T(8,128)} %param.23) | copy-start | bytes 2359300
  256.5 3.0 %copy-start.15 = (f32[2,128,768]{2,1,0:T(8,128)S(1)}, f32[2,128,768]{2,1,0:T(8,128)}, u32[]{:S(2)}) copy-start(f32[2,128,768]{2,1,0:T(8,128)} %mul.6050) | copy-start | bytes 2359300
  256.5 3.0 %copy-start.27 = (f32[2,128,768]{2,1,0:T(8,128)S(1)}, f32[2,128,768]{2,1,0:T(8,128)}, u32[]{:S(2)}) copy-start(f32[2,128,768]{2,1,0:T(8,128)} %param.33) | copy-start | bytes 2359300
  256.5 3.0 %copy-start.28 = (f32[2,128,768]{2,1,0:T(8,128)S(1)}, f32[2,128,768]{2,1,0:T(8,128)}, u32[]{:S(2)}) copy-start(f32[2,128,768]{2,1,0:T(8,128)} %param.28) | copy-start | bytes 2359300
  259.5 2.7 copy-start.20
  259.5 3.2 %copy-start.21 = (f32[2,1536,128]{2,1,0:T(8,128)S(1)}, f32[2,1536,128]{2,1,0:T(8,128)}, u32[]{:S(2)}) copy-start(f32[2,1536,128]{2,1,0:T(8,128)} %param.29) | copy-start | bytes 4718596
  (59 other events, 89.9 us)
Sparse Core Ops, SparseCore 0:
  10.2 22.7 all-gather.4
  35.1 19.6 all-gather.6
  56.9 22.8 all-gather.8
  81.8 22.8 all-gather.10

commit v22 on v20

--- a/solution.py
+++ b/solution.py
@@ -466,12 +466,21 @@
 
     in_all = gather_feat(input_matrix.astype(jnp.bfloat16), 1)
     rows_out = output_matrix.shape[1]
+    rows_gate = gate_matrix.shape[1]
     paired = [
-        gather_feat(jnp.concatenate([output_matrix[k], gate_matrix[k]], 0).astype(jnp.bfloat16), 1)
+        gather_feat(
+            jnp.concatenate(
+                [output_matrix[k].astype(jnp.bfloat16), gate_matrix[k].astype(jnp.bfloat16)]
+                + ([cotangent] if k == layers - 1 else []),
+                0,
+            ),
+            1,
+        )
         for k in range(layers)
     ]
     out_all = [pair[:rows_out] for pair in paired]
-    gate_all = [pair[rows_out:] for pair in paired]
+    gate_all = [pair[rows_out : rows_out + rows_gate] for pair in paired]
+    cotangent_all = paired[-1][rows_out + rows_gate :]
     feature_pieces = split_exact(feature_vectors.reshape(-1, activations_in.shape[1]))
     feature_rows = feature_pieces.shape[0]
     feature_pad = -(-feature_rows // 16) * 16
@@ -516,7 +525,7 @@
         saved.append((scale, unit, normed_low, drive, states, states_low, mixed, act, act_low, pre, cdf))
         stream = stream + act * jax.nn.sigmoid(pre)
 
-    grad = gather_feat(cotangent, 1).astype(jnp.float32) * alive[:, None]
+    grad = cotangent_all.astype(jnp.float32) * alive[:, None]
     layer_grads = [None] * layers
     for layer in reversed(range(layers)):
         scale, unit, normed_low, drive, states, states_low, mixed, act, act_low, pre, cdf = saved[layer]

time: 252 us -> 257 us (1.020)
  waiting for transfers between devices: 4.76 us -> 18.8 us
  blocking collectives: 20.2 us -> 10.2 us
    all_gather x3, waiting for transfers between devices: 4.72 us -> 18.8 us  [gather_feat(): return lax.all_gather(value, 'feat', axis=axis, tiled=True)]
    all_gather x2 -> x1, blocking collectives: 20.2 us -> 10.2 us  [gather_feat(): return lax.all_gather(value, 'feat', axis=axis, tiled=True)]
    unnamed x140 -> x130, local copies, waits for them, and re-layouts: 8.75 us -> 8.93 us
  transfers between devices with their start and end apart: 3 -> 3, of which waited for: 2 -> 3; matrix products, arithmetic and copies ran while one was open for 11% -> 11% of each run, Pallas kernels for 7% -> 7%
where the time goes in v22:
time: 257 us
  Pallas kernels  109 us (42%)
  matrix products  47.8 us (19%)
  other arithmetic  39 us (15%)
  waiting for transfers between devices  18.8 us (7%)
  local copies, waits for them, and re-layouts  16.6 us (6%)
  between operations  14.7 us (6%)
  blocking collectives  10.2 us (4%)
    pallas_call x1, Pallas kernels, ring_sum(): pl.pallas_call(lambda *refs: ring_sum_kernel(n, *refs), out_shape=jax.Sha...  61.3 us
    pallas_call x2, Pallas kernels, adjoint(): pl.pallas_call(adjoint_kernel, out_shape=(jax.ShapeDtypeStruct((count, 2...  30.8 us
    all_gather x3, waiting for transfers between devices, gather_feat(): return lax.all_gather(value, 'feat', axis=axis, tiled=True)  18.8 us
    pallas_call x2, Pallas kernels, recurrence(): pl.pallas_call(recurrence_kernel, out_shape=jax.ShapeDtypeStruct((count,...  17.4 us
    dot_general x4, matrix products, contract_cols(): lax.dot_general(left, right, (((1,), (1,)), ((), ())), preferred_element_...  14.1 us
    dot_general x2, matrix products, body(): jnp.dot(states_low, out_low, preferred_element_type=jnp.float32)  10.3 us
    all_gather x1, blocking collectives, gather_feat(): return lax.all_gather(value, 'feat', axis=axis, tiled=True)  10.2 us
    add x5, other arithmetic, update(): average_new = smoothing * average + (1.0 - smoothing) * weight_new  9.08 us
  transfers between devices with their start and end apart: 3, of which 3 were waited for; matrix products, arithmetic and copies ran while one was open for 11% of the time, Pallas kernels for 7%

profile of v22, /device:TPU:0, one launch (start us, length us, event | category | flops | bytes accessed | tf_op | source)
XLA Modules:
  0.0 256.6 jit_solution(97795475462057434)
XLA Ops:
  7.3 2.1 convert_element_type.117
  9.7 0.8 pad_maximum_fusion.5
  10.6 0.9 pad_maximum_fusion.4
  12.3 10.2 %all_gather.12 = bf16[800,512]{1,0:T(8,128)(2,1)S(1)} all-gather(bf16[800,128]{1,0:T(8,128)(2,1)S(1)} %pad_maximum_fusion.7), channel_id=1, replica_groups=mesh['seq'=8,'feat'=4] {'feat'}, dimensions={1}, use_global_device_ids=true | all-gather | bytes 1024000 | tf_op jit(solution)/shard_map/all_gather | solution.py:412
  28.3 0.9 copy.86.masks_ref
  29.3 1.2 fusion.9
  30.5 2.1 all-gather.4.cloned.1.call-done
  32.6 2.1 fusion.15.drive_ref
  35.1 1.1 copy-done
  36.2 1.6 pad_maximum_fusion.x_ref
  37.8 8.7 %shard_map.354.states_ref = f32[768,1536]{1,0:T(8,128)} custom-call(s32[2]{0:T(128)} %starts_ref.7, s32[2]{0:T(128)} %lengths_ref.7, f32[4,8,384]{2,1,0:T(8,128)} %pad_maximum_fusion.8.pow_ref, f32[768,768]{1,0:T(8,128)} %pad_maximum_fusion.x_ref), custom_call_target="tpu_custom_call" | custom-call | flops 11796480 | bytes 9437184 | tf_op jit(solution)/shard_map/pallas_call | solution.py:144
  46.5 11.1 %all-gather.6.cloned.1.call-done = bf16[2048,512]{1,0:T(8,128)(2,1)} async-done(((bf16[2048,128]{1,0:T(8,128)(2,1)}), bf16[2048,512]{1,0:T(8,128)(2,1)}) %all-gather.6.cloned.1.call-update) | async-done | bytes 2097168 | tf_op jit(solution)/shard_map/all_gather | solution.py:412
  57.6 5.7 %fusion.91 = (f32[768,512]{1,0:T(8,128)S(1)}, f32[768,512]{1,0:T(8,128)}) fusion(f32[512]{0:T(512)S(1)} %bitcast.465, f32[512]{0:T(512)S(1)} %bitcast.468, f32[768]{0:T(1024)S(1)} %add_rsqrt_fusion.1, f32[768]{0:T(1024)S(1)} %broadcast_multiply_fusion.6, bf16[800,512]{1,0:T(8,128)(2,1)S(1)} %copy-done.5, f32[512]{0:T(512)S(1)} %bitcast.474, ...), kind=kOutput, calls=%fused_computation.342 | convolution fusion | flops 1213464576 | bytes 10235904 | tf_op jit(solution)/shard_map/dot_general | solution.py:518
  63.3 3.4 %fusion.109 = (f32[768]{0:T(1024)S(1)}, f32[768,512]{1,0:T(8,128)S(1)}, f32[768,512]{1,0:T(8,128)}) fusion(f32[768,512]{1,0:T(8,128)S(1)} %get-tuple-element.300, bf16[800,512]{1,0:T(8,128)(2,1)S(1)} %copy-done.5, f32[512]{0:T(512)S(1)} %bitcast.479, bf16[2048,512]{1,0:T(8,128)(2,1)} %all-gather.6.cloned.1.call-done), kind=kOutput, calls=%fused_computation.350 | convolution fusion | flops 406191360 | bytes 7607296 | tf_op jit(solution)/shard_map/dot_general | solution.py:524
  67.9 1.1 copy-done.24
  70.2 1.1 copy-done.1
  71.3 1.6 pad_maximum_fusion.1.x_ref
  72.8 8.7 %shard_map.355.states_ref = f32[768,1536]{1,0:T(8,128)} custom-call(s32[2]{0:T(128)} %starts_ref.7, s32[2]{0:T(128)} %lengths_ref.7, f32[4,8,384]{2,1,0:T(8,128)} %pad_maximum_fusion.9.pow_ref, f32[768,768]{1,0:T(8,128)} %pad_maximum_fusion.1.x_ref), custom_call_target="tpu_custom_call" | custom-call | flops 11796480 | bytes 9437184 | tf_op jit(solution)/shard_map/pallas_call | solution.py:144
  81.6 5.6 %all-gather.8.cloned.1.call-done = bf16[2816,512]{1,0:T(8,128)(2,1)} async-done(((bf16[2816,128]{1,0:T(8,128)(2,1)}), bf16[2816,512]{1,0:T(8,128)(2,1)}) %all-gather.8.cloned.1.call-update) | async-done | bytes 2883600 | tf_op jit(solution)/shard_map/all_gather | solution.py:412
  87.2 4.6 %fusion.92 = (f32[768,512]{1,0:T(8,128)S(1)}, f32[768,512]{1,0:T(8,128)S(1)}) fusion(f32[512]{0:T(512)S(1)} %bitcast.471, f32[512]{0:T(512)S(1)} %bitcast.457, f32[768]{0:T(1024)S(1)} %add_rsqrt_fusion, f32[768,512]{1,0:T(8,128)S(1)} %copy-done.3, f32[768]{0:T(1024)S(1)} %broadcast_multiply_fusion.5, f32[512]{0:T(512)S(1)} %bitcast.476, ...), kind=kOutput, calls=%fused_computation.343 | convolution fusion | flops 1213071360 | bytes 11022336 | tf_op jit(solution)/shard_map/dot_general | solution.py:518
  91.8 1.6 convert_reduce_fusion.1
  93.8 0.9 dynamic-slice_add_fusion.1
  94.7 2.2 fusion.111
  96.9 1.7 convolution_bitcast_fusion
  98.7 3.7 %fusion.3.g_ref = f32[768,1536]{1,0:T(8,128)} fusion(bf16[768,512]{1,0:T(8,128)(2,1)S(1)} %get-tuple-element.306, bf16[2816,512]{1,0:T(8,128)(2,1)S(1)} %copy-done.29), kind=kOutput, calls=%fused_computation.43 | convolution fusion | flops 1207959552 | bytes 7077888 | tf_op jit(solution)/shard_map/dot_general | solution.py:406
  102.3 15.4 %shard_map.356 = (bf16[768,768]{1,0:T(8,128)(2,1)}, f32[4,384]{1,0:T(4,128)}) custom-call(s32[2]{0:T(128)} %starts_ref.7, s32[2]{0:T(128)} %lengths_ref.7, f32[4,8,384]{2,1,0:T(8,128)} %pad_maximum_fusion.10.pow_ref, f32[4,384]{1,0:T(4,128)} %pad_maximum_fusion.13.coef_ref, f32[768,4]{1,0:T(8,128)} %copy.86.masks_ref, f32[768,1536]{1,0:T(8,128)} %fusion.3.g_ref, ...), custom_call_target="tpu_custom_call" | custom-call | flops 17694720 | bytes 14155776 | tf_op jit(solution)/shard_map/pallas_call | solution.py:375
  117.7 2.6 %convolution_bitcast_fusion.2 = f32[1,128,768]{2,1,0:T(8,128)} fusion(bf16[768,768]{1,0:T(8,128)(2,1)} %get-tuple-element.26, bf16[768,512]{1,0:T(8,128)(2,1)} %copy-done.13, s32[]{:T(128)S(6)} %select_n.2), kind=kOutput, calls=%fused_computation.50 | convolution fusion | flops 150994944 | bytes 1769476 | tf_op jit(solution)/shard_map/dot_general | solution.py:400
  120.3 3.8 %multiply_reduce_fusion.1 = (f32[512]{0:T(512)}, f32[768]{0:T(1024)S(1)}, f32[512]{0:T(512)}, f32[768]{0:T(1024)S(1)}, f32[512]{0:T(512)}, /*index=5*/f32[768,512]{1,0:T(8,128)S(1)}) fusion(f32[768]{0:T(1024)S(1)} %add_rsqrt_fusion, f32[768,512]{1,0:T(8,128)S(1)} %copy-done.3, f32[768]{0:T(1024)S(1)} %broadcast_multiply_fusion.5, f32[512]{0:T(512)S(1)} %bitcast.458, ...), kind=kOutput, calls=%fused_computation.19 | convolution fusion | flops 609874944 | bytes 6711296 | tf_op jit(solution)/shard_map/dot_general | solution.py:564
  124.2 3.1 %convert_reduce_fusion.2 = (f32[512]{0:T(512)S(1)}, bf16[768,512]{1,0:T(8,128)(2,1)S(1)}, f32[768,512]{1,0:T(8,128)}) fusion(f32[768,512]{1,0:T(8,128)S(1)} %copy-done.7, f32[768,512]{1,0:T(8,128)S(1)} %copy-done.11, f32[768]{0:T(1024)S(1)} %broadcast_multiply_fusion.3, f32[768,512]{1,0:T(8,128)S(1)} %copy-done.3, f32[768]{0:T(1024)S(1)} %broadcast_multiply_fusion.5, ...), kind=kLoop, calls=%fused_computation.20 | loop fusion | flops 6684160 | bytes 9456640 | tf_op jit(solution)/shard_map/reduce_sum | solution.py:541
  130.3 4.6 %fusion.112 = (bf16[768,512]{1,0:T(8,128)(2,1)S(1)}, f32[768,512]{1,0:T(8,128)}) fusion(f32[768,512]{1,0:T(8,128)} %get-tuple-element.301, bf16[768,512]{1,0:T(8,128)(2,1)} %copy-done.14, bf16[2048,512]{1,0:T(8,128)(2,1)} %all-gather.6.cloned.1.call-done, f32[768,512]{1,0:T(8,128)S(1)} %copy-done.6, f32[768,512]{1,0:T(8,128)} %get-tuple-element.302), kind=kOutput, calls=%fused_computation.353 | convolution fusion | flops 407371776 | bytes 8388608 | tf_op jit(solution)/shard_map/dot_general | solution.py:406
  135.0 1.7 convolution_bitcast_fusion.1
  137.9 3.6 %fusion.6.g_ref = f32[768,1536]{1,0:T(8,128)} fusion(bf16[768,512]{1,0:T(8,128)(2,1)S(1)} %get-tuple-element.309, bf16[2048,512]{1,0:T(8,128)(2,1)S(1)} %copy-done.32), kind=kOutput, calls=%fused_computation.46 | convolution fusion | flops 1207959552 | bytes 7077888 | tf_op jit(solution)/shard_map/dot_general | solution.py:406
  141.5 15.4 %shard_map.357 = (bf16[768,768]{1,0:T(8,128)(2,1)}, f32[4,384]{1,0:T(4,128)}) custom-call(s32[2]{0:T(128)} %starts_ref.7, s32[2]{0:T(128)} %lengths_ref.7, f32[4,8,384]{2,1,0:T(8,128)} %pad_maximum_fusion.11.pow_ref, f32[4,384]{1,0:T(4,128)} %pad_maximum_fusion.14.coef_ref, f32[768,4]{1,0:T(8,128)} %copy.86.masks_ref, f32[768,1536]{1,0:T(8,128)} %fusion.6.g_ref, ...), custom_call_target="tpu_custom_call" | custom-call | flops 17694720 | bytes 14155776 | tf_op jit(solution)/shard_map/pallas_call | solution.py:375
  156.9 1.8 convolution_bitcast_fusion.3
  158.8 0.9 pad_maximum_fusion.3
  159.7 2.1 reshape.1857
  162.1 1.3 constant_dynamic-update-slice_fusion.4
  163.5 1.6 pad_maximum_fusion.2
  165.8 2.9 %fusion.93 = (f32[512]{0:T(512)S(1)}, f32[512]{0:T(512)S(1)}, f32[512]{0:T(512)S(1)}, f32[768]{0:T(1024)S(1)}, f32[768]{0:T(1024)S(1)}, /*index=5*/f32[768,512]{1,0:T(8,128)}, f32[768,512]{1,0:T(8,128)}) fusion(f32[768]{0:T(1024)S(1)} %add_rsqrt_fusion.1, f32[768]{0:T(1024)S(1)} %broadcast_multiply_fusion.6, bf16[800,512]{1,0:T(8,128)(2,1)S(1)} %copy-done.5, ...), kind=kOutput, calls=%fused_computation.344 | convolution fusion | flops 610268160 | bytes 7497728 | tf_op jit(solution)/shard_map/dot_general | solution.py:564
  169.0 1.8 pad_bitcast_fusion.refs_0_
  170.8 61.3 %shard_map.358 = bf16[5888,128]{1,0:T(8,128)(2,1)} custom-call(f32[5888,128]{1,0:T(8,128)} %pad_bitcast_fusion.refs_0_), custom_call_target="tpu_custom_call" | custom-call | tf_op jit(solution)/shard_map/pallas_call | solution.py:267
  232.1 1.6 convert_element_type.141
  233.9 1.3 slice_multiply_fusion
  237.7 1.0 mul.6050
  239.3 2.6 %add_multiply_fusion.8 = (f32[2,512,128]{2,1,0:T(8,128)}, f32[2,512,128]{2,1,0:T(8,128)}, f32[2,512,128]{2,1,0:T(8,128)}) fusion(f32[2,512,128]{2,1,0:T(8,128)} %param.35, f32[2,512,128]{2,1,0:T(8,128)S(1)} %copy-done.18, f32[2,512,128]{2,1,0:T(8,128)S(1)} %bitcast.437, f32[2,512,128]{2,1,0:T(8,128)} %param.30), kind=kLoop, calls=%fused_computation.79 | loop fusion | flops 1310720 | bytes 3670016 | tf_op jit(solution)/shard_map/add | solution.py:395
  242.0 3.2 %add_multiply_fusion.7 = (f32[2,128,768]{2,1,0:T(8,128)}, f32[2,128,768]{2,1,0:T(8,128)}, f32[2,128,768]{2,1,0:T(8,128)}) fusion(f32[2,128,768]{2,1,0:T(8,128)} %param.33, f32[2,128,768]{2,1,0:T(8,128)S(1)} %copy-done.15, f32[2,128,768]{2,1,0:T(8,128)S(1)} %copy-done.16, f32[2,128,768]{2,1,0:T(8,128)} %param.28), kind=kLoop, calls=%fused_computation.68 | loop fusion | flops 1966080 | bytes 5505024 | tf_op jit(solution)/shard_map/add | solution.py:395
  245.2 2.6 %add_multiply_fusion = (f32[2,1536,128]{2,1,0:T(8,128)}, f32[2,1536,128]{2,1,0:T(8,128)}, f32[2,1536,128]{2,1,0:T(8,128)}) fusion(f32[2,1536,128]{2,1,0:T(8,128)S(1)} %copy-done.22, f32[2,1536,128]{2,1,0:T(8,128)S(1)} %copy-done.9, f32[2,1536,128]{2,1,0:T(8,128)S(1)} %bitcast.436, f32[2,1536,128]{2,1,0:T(8,128)S(1)} %copy-done.23), kind=kLoop, calls=%fused_computation.13 | loop fusion | flops 3932160 | bytes 11010048 | tf_op jit(solution)/shard_map/add | solution.py:395
  247.8 2.2 dynamic-slice_add_fusion
  (219 shorter events, 18.7 us)
Async XLA Ops:
  7.2 2.2 copy-start.17
  7.2 2.2 copy-start.8
  7.2 25.4 %all-gather.4.cloned.1.call-start = ((), (), s32[]{:S(2)}) async-start(), calls=%async_computation | async-start | bytes 1966080 | tf_op jit(solution)/shard_map/all_gather | solution.py:412
  9.3 48.2 %all-gather.6.cloned.1.call-start = ((), (), s32[]{:S(2)}) async-start(), calls=%async_computation.1 | async-start | bytes 2621440 | tf_op jit(solution)/shard_map/all_gather | solution.py:412
  10.5 1.8 copy-start.30
  10.5 76.6 %all-gather.8.cloned.1.call-start = ((), (), s32[]{:S(2)}) async-start(), calls=%async_computation.2 | async-start | bytes 3604480 | tf_op jit(solution)/shard_map/all_gather | solution.py:412
  11.5 11.2 %copy-start.35 = (s32[2]{0:T(128)S(1)}, s32[2]{0:T(128)}, u32[]{:S(2)}) copy-start(s32[2]{0:T(128)} %starts_ref.7) | copy-start | bytes 28
  11.5 11.2 %copy-start.38 = (s32[2]{0:T(128)S(1)}, s32[2]{0:T(128)}, u32[]{:S(2)}) copy-start(s32[2]{0:T(128)} %lengths_ref.7) | copy-start | bytes 28
  22.5 6.7 %copy-start.4 = (bf16[800,512]{1,0:T(8,128)(2,1)}, bf16[800,512]{1,0:T(8,128)(2,1)S(1)}, u32[]{:S(2)}) copy-start(bf16[800,512]{1,0:T(8,128)(2,1)S(1)} %all_gather.12) | copy-start | bytes 2457604
  29.2 28.3 %copy-start.51 = (f32[1,512]{1,0:T(1,128)}, f32[1,512]{1,0:T(1,128)S(1)}, u32[]{:S(2)}) copy-start(f32[1,512]{1,0:T(1,128)S(1)} %get-tuple-element.248) | copy-start | bytes 6148
  37.8 19.8 %copy-start.5 = (bf16[800,512]{1,0:T(8,128)(2,1)S(1)}, bf16[800,512]{1,0:T(8,128)(2,1)}, u32[]{:S(2)}) copy-start(bf16[800,512]{1,0:T(8,128)(2,1)} %copy-done.4) | copy-start | bytes 2457604
  63.3 3.4 %copy-start.10 = (f32[768,512]{1,0:T(8,128)}, f32[768,512]{1,0:T(8,128)S(1)}, u32[]{:S(2)}) copy-start(f32[768,512]{1,0:T(8,128)S(1)} %get-tuple-element.300) | copy-start | bytes 4718596
  67.1 1.8 copy-start.24
  72.8 14.3 %copy-start.3 = (f32[768,512]{1,0:T(8,128)S(1)}, f32[768,512]{1,0:T(8,128)}, u32[]{:S(2)}) copy-start(f32[768,512]{1,0:T(8,128)} %copy-done.2) | copy-start | bytes 4718596
  87.2 4.6 %copy-start.29 = (bf16[2816,512]{1,0:T(8,128)(2,1)S(1)}, bf16[2816,512]{1,0:T(8,128)(2,1)}, u32[]{:S(2)}) copy-start(bf16[2816,512]{1,0:T(8,128)(2,1)} %all-gather.8.cloned.1.call-done) | copy-start | bytes 8650756
  93.8 3.1 %slice-start.2 = ((s8[4718592]{0:T(1024)(128)(4,1)}), s8[4194304]{0:T(1024)(128)(4,1)S(1)}, s32[]{:S(2)}) async-start(s8[4718592]{0:T(1024)(128)(4,1)} %bitcast.432), calls=%async_computation.5 | async-start | bytes 8388608
  94.7 2.2 slice-start.3
  117.7 2.6 %copy-start.25 = (bf16[2,512,768]{2,1,0:T(8,128)(2,1)S(1)}, bf16[2,512,768]{2,1,0:T(8,128)(2,1)}, u32[]{:S(2)}) copy-start(bf16[2,512,768]{2,1,0:T(8,128)(2,1)} %all-gather.4.cloned.1.call-done) | copy-start | bytes 4718596
  120.3 3.9 %copy-start.7 = (f32[768,512]{1,0:T(8,128)S(1)}, f32[768,512]{1,0:T(8,128)}, u32[]{:S(2)}) copy-start(f32[768,512]{1,0:T(8,128)} %get-tuple-element.302) | copy-start | bytes 4718596
  120.3 3.9 %copy-start.11 = (f32[768,512]{1,0:T(8,128)S(1)}, f32[768,512]{1,0:T(8,128)}, u32[]{:S(2)}) copy-start(f32[768,512]{1,0:T(8,128)} %copy-done.10) | copy-start | bytes 4718596
  127.3 2.2 copy-start.43
  127.3 3.0 %copy-start.6 = (f32[768,512]{1,0:T(8,128)S(1)}, f32[768,512]{1,0:T(8,128)}, u32[]{:S(2)}) copy-start(f32[768,512]{1,0:T(8,128)} %get-tuple-element.159) | copy-start | bytes 4718596
  127.3 7.7 %slice-start = ((s8[4718592]{0:T(1024)(128)(4,1)}), s8[524288]{0:T(1024)(128)(4,1)S(1)}, s32[]{:S(2)}) async-start(s8[4718592]{0:T(1024)(128)(4,1)} %bitcast.430), calls=%async_computation.3 | async-start | bytes 1048576
  130.3 4.7 %slice-start.1 = ((s8[4718592]{0:T(1024)(128)(4,1)}), s8[4194304]{0:T(1024)(128)(4,1)S(1)}, s32[]{:S(2)}) async-start(s8[4718592]{0:T(1024)(128)(4,1)} %bitcast.430), calls=%async_computation.4 | async-start | bytes 8388608
  135.0 3.0 %copy-start.32 = (bf16[2048,512]{1,0:T(8,128)(2,1)S(1)}, bf16[2048,512]{1,0:T(8,128)(2,1)}, u32[]{:S(2)}) copy-start(bf16[2048,512]{1,0:T(8,128)(2,1)} %all-gather.6.cloned.1.call-done) | copy-start | bytes 6291460
  156.9 1.8 copy-start.21
  158.7 3.1 %copy-start.34 = (f32[4,384]{1,0:T(4,128)S(1)}, f32[4,384]{1,0:T(4,128)}, u32[]{:S(2)}) copy-start(f32[4,384]{1,0:T(4,128)} %get-tuple-element.28) | copy-start | bytes 18436
  158.7 3.0 %copy-start.46 = (f32[1,384]{1,0:T(1,128)S(1)}, f32[1,384]{1,0:T(1,128)}, u32[]{:S(2)}) copy-start(f32[1,384]{1,0:T(1,128)} %get-tuple-element.255) | copy-start | bytes 4612
  158.7 3.0 %copy-start.47 = (f32[1,384]{1,0:T(1,128)S(1)}, f32[1,384]{1,0:T(1,128)}, u32[]{:S(2)}) copy-start(f32[1,384]{1,0:T(1,128)} %get-tuple-element.252) | copy-start | bytes 4612
  158.8 3.2 %copy-start.45 = (f32[1,384]{1,0:T(1,128)S(1)}, f32[1,384]{1,0:T(1,128)}, u32[]{:S(2)}) copy-start(f32[1,384]{1,0:T(1,128)} %get-tuple-element.155) | copy-start | bytes 4612
  158.8 3.2 %copy-start.48 = (f32[1,384]{1,0:T(1,128)S(1)}, f32[1,384]{1,0:T(1,128)}, u32[]{:S(2)}) copy-start(f32[1,384]{1,0:T(1,128)} %get-tuple-element.242) | copy-start | bytes 4612
  162.1 3.2 %copy-start.27 = (bf16[768,768]{1,0:T(8,128)(2,1)S(1)}, bf16[768,768]{1,0:T(8,128)(2,1)}, u32[]{:S(2)}) copy-start(bf16[768,768]{1,0:T(8,128)(2,1)} %get-tuple-element.27) | copy-start | bytes 3538948
  163.4 1.9 copy-start.20
  163.5 2.4 copy-start.26
  163.5 2.4 copy-start.52
  233.7 5.0 %copy-start.37 = (f32[8,128]{1,0:T(8,128)}, f32[8,128]{1,0:T(8,128)S(1)}, u32[]{:S(2)}) copy-start(f32[8,128]{1,0:T(8,128)S(1)} %slice_multiply_fusion.4) | copy-start | bytes 12292
  233.8 5.5 %copy-start.19 = (f32[1024,128]{1,0:T(8,128)}, f32[1024,128]{1,0:T(8,128)S(1)}, u32[]{:S(2)}) copy-start(f32[1024,128]{1,0:T(8,128)S(1)} %slice_multiply_fusion.2) | copy-start | bytes 1572868
  233.9 1.9 copy-start.39
  233.9 1.9 copy-start.40
  235.2 3.5 %copy-start.49 = (f32[2,4,128]{2,1,0:T(4,128)S(1)}, f32[2,4,128]{2,1,0:T(4,128)}, u32[]{:S(2)}) copy-start(f32[2,4,128]{2,1,0:T(4,128)} %param.36) | copy-start | bytes 12292
  235.2 3.5 %copy-start.50 = (f32[2,4,128]{2,1,0:T(4,128)S(1)}, f32[2,4,128]{2,1,0:T(4,128)}, u32[]{:S(2)}) copy-start(f32[2,4,128]{2,1,0:T(4,128)} %param.31) | copy-start | bytes 12292
  235.2 4.1 %copy-start.18 = (f32[2,512,128]{2,1,0:T(8,128)S(1)}, f32[2,512,128]{2,1,0:T(8,128)}, u32[]{:S(2)}) copy-start(f32[2,512,128]{2,1,0:T(8,128)} %param.25) | copy-start | bytes 1572868
  239.3 2.7 %copy-start.15 = (f32[2,128,768]{2,1,0:T(8,128)S(1)}, f32[2,128,768]{2,1,0:T(8,128)}, u32[]{:S(2)}) copy-start(f32[2,128,768]{2,1,0:T(8,128)} %param.23) | copy-start | bytes 2359300
  239.3 2.7 %copy-start.16 = (f32[2,128,768]{2,1,0:T(8,128)S(1)}, f32[2,128,768]{2,1,0:T(8,128)}, u32[]{:S(2)}) copy-start(f32[2,128,768]{2,1,0:T(8,128)} %mul.6050) | copy-start | bytes 2359300
  239.3 5.9 %copy-start.23 = (f32[2,1536,128]{2,1,0:T(8,128)S(1)}, f32[2,1536,128]{2,1,0:T(8,128)}, u32[]{:S(2)}) copy-start(f32[2,1536,128]{2,1,0:T(8,128)} %param.29) | copy-start | bytes 4718596
  242.0 3.2 %copy-start.9 = (f32[2,1536,128]{2,1,0:T(8,128)S(1)}, f32[2,1536,128]{2,1,0:T(8,128)}, u32[]{:S(2)}) copy-start(f32[2,1536,128]{2,1,0:T(8,128)} %param.24) | copy-start | bytes 4718596
  242.0 3.2 %copy-start.12 = (f32[3072,128]{1,0:T(8,128)S(1)}, f32[3072,128]{1,0:T(8,128)}, u32[]{:S(2)}) copy-start(f32[3072,128]{1,0:T(8,128)} %slice_multiply_fusion) | copy-start | bytes 4718596
  242.0 3.2 %copy-start.22 = (f32[2,1536,128]{2,1,0:T(8,128)S(1)}, f32[2,1536,128]{2,1,0:T(8,128)}, u32[]{:S(2)}) copy-start(f32[2,1536,128]{2,1,0:T(8,128)} %param.34) | copy-start | bytes 4718596
  (16 other events, 21.6 us)
Sparse Core Ops, SparseCore 0:
  10.2 22.3 all-gather.3
  34.7 22.8 all-gather.5
  59.7 27.3 all-gather.7

commit v23 on v20

--- a/solution.py
+++ b/solution.py
@@ -187,9 +187,9 @@
     def scatter_copy(ring, place, target, s):
         return pltpu.make_async_remote_copy(
             src_ref=low.at[block(ring, (place - s + n) % n)],
-            dst_ref=slots.at[ring, s % 2],
-            send_sem=rs_send.at[ring, s % 2],
-            recv_sem=rs_recv.at[ring, s % 2],
+            dst_ref=slots.at[ring, s % 3],
+            send_sem=rs_send.at[ring, s % 3],
+            recv_sem=rs_recv.at[ring, s % 3],
             device_id={"seq": target},
             device_id_type=MESH,
         )
@@ -198,7 +198,7 @@
         copies = []
         for ring, place, target, source in rings:
 
-            @pl.when(s >= 2)
+            @pl.when(s >= 3)
             def _():
                 pl.semaphore_wait(credit.at[ring], 1)
 
@@ -208,12 +208,12 @@
         for (ring, place, target, source), copy in zip(rings, copies):
             copy.wait_recv()
             into = block(ring, (place - s - 1 + 2 * n) % n)
-            total = o_ref[into] + slots[ring, s % 2].astype(jnp.float32)
+            total = o_ref[into] + slots[ring, s % 3].astype(jnp.float32)
             o_ref[into] = total
             low[into] = total.astype(low.dtype)
             copy.wait_send()
 
-            @pl.when(s <= n - 4)
+            @pl.when(s <= n - 5)
             def _():
                 pl.semaphore_signal(credit.at[ring], 1, device_id={"seq": source}, device_id_type=MESH)
 
@@ -272,9 +272,9 @@
         scratch_shapes=[
             pltpu.VMEM((rows, lanes), jnp.float32),
             pltpu.VMEM((rows, lanes), jnp.bfloat16),
-            pltpu.VMEM((2, 2, size, lanes), jnp.bfloat16),
-            pltpu.SemaphoreType.DMA((2, 2)),
-            pltpu.SemaphoreType.DMA((2, 2)),
+            pltpu.VMEM((2, 3, size, lanes), jnp.bfloat16),
+            pltpu.SemaphoreType.DMA((2, 3)),
+            pltpu.SemaphoreType.DMA((2, 3)),
             pltpu.SemaphoreType.REGULAR((2,)),
             pltpu.SemaphoreType.REGULAR((2,)),
             pltpu.SemaphoreType.DMA((2, n - 1)),

time: 252 us -> 252 us (level)
  no operation moved by 1% of the time
where the time goes in v23:
time: 252 us
  Pallas kernels  110 us (44%)
  matrix products  47.5 us (19%)
  other arithmetic  37.9 us (15%)
  blocking collectives  20.2 us (8%)
  local copies, waits for them, and re-layouts  16.6 us (7%)
  between operations  14.7 us (6%)
  waiting for transfers between devices  4.76 us (2%)
    pallas_call x1, Pallas kernels, ring_sum(): pl.pallas_call(lambda *refs: ring_sum_kernel(n, *refs), out_shape=jax.Sha...  61.3 us
    pallas_call x2, Pallas kernels, adjoint(): pl.pallas_call(adjoint_kernel, out_shape=(jax.ShapeDtypeStruct((count, 2...  30.8 us
    all_gather x2, blocking collectives, gather_feat(): return lax.all_gather(value, 'feat', axis=axis, tiled=True)  20.2 us
    pallas_call x2, Pallas kernels, recurrence(): pl.pallas_call(recurrence_kernel, out_shape=jax.ShapeDtypeStruct((count,...  17.6 us
    dot_general x4, matrix products, contract_cols(): lax.dot_general(left, right, (((1,), (1,)), ((), ())), preferred_element_...  14.2 us
    dot_general x2, matrix products, body(): jnp.dot(states_low, out_low, preferred_element_type=jnp.float32)  10 us
    add x5, other arithmetic, update(): average_new = smoothing * average + (1.0 - smoothing) * weight_new  9.08 us
    unnamed x140, local copies, waits for them, and re-layouts  8.75 us
  transfers between devices with their start and end apart: 3, of which 2 were waited for; matrix products, arithmetic and copies ran while one was open for 11% of the time, Pallas kernels for 7%

profile of v23, /device:TPU:0, one launch (start us, length us, event | category | flops | bytes accessed | tf_op | source)
XLA Modules:
  0.0 251.5 jit_solution(15038665603164244085)
XLA Ops:
  7.3 2.1 convert_element_type.103
  9.7 0.8 pad_maximum_fusion.4
  10.6 0.8 pad_maximum_fusion.5
  12.2 10.2 %all_gather.15 = bf16[800,512]{1,0:T(8,128)(2,1)S(1)} all-gather(bf16[800,128]{1,0:T(8,128)(2,1)S(1)} %pad_maximum_fusion.7), channel_id=1, replica_groups=mesh['seq'=8,'feat'=4] {'feat'}, dimensions={1}, use_global_device_ids=true | all-gather | bytes 1024000 | tf_op jit(solution)/shard_map/all_gather | solution.py:412
  25.2 0.9 copy.86.masks_ref
  26.6 10.0 %all_gather.19 = bf16[768,512]{1,0:T(8,128)(2,1)} all-gather(bf16[768,128]{1,0:T(8,128)(2,1)S(1)} %copy-done.31), channel_id=1, replica_groups=mesh['seq'=8,'feat'=4] {'feat'}, dimensions={1}, use_global_device_ids=true | all-gather | bytes 983040 | tf_op jit(solution)/shard_map/all_gather | solution.py:412
  37.2 1.2 fusion.9
  40.4 2.2 fusion.15.drive_ref
  43.0 1.0 copy-done
  44.0 1.6 pad_maximum_fusion.x_ref
  45.7 8.8 %shard_map.354.states_ref = f32[768,1536]{1,0:T(8,128)} custom-call(s32[2]{0:T(128)} %starts_ref.7, s32[2]{0:T(128)} %lengths_ref.7, f32[4,8,384]{2,1,0:T(8,128)} %pad_maximum_fusion.8.pow_ref, f32[768,768]{1,0:T(8,128)} %pad_maximum_fusion.x_ref), custom_call_target="tpu_custom_call" | custom-call | flops 11796480 | bytes 9437184 | tf_op jit(solution)/shard_map/pallas_call | solution.py:144
  54.5 3.6 %all-gather.6.cloned.1.call-done = bf16[2048,512]{1,0:T(8,128)(2,1)} async-done(((bf16[2048,128]{1,0:T(8,128)(2,1)}), bf16[2048,512]{1,0:T(8,128)(2,1)}) %all-gather.6.cloned.1.call-update) | async-done | bytes 2097168 | tf_op jit(solution)/shard_map/all_gather | solution.py:412
  58.1 5.7 %fusion.91 = (f32[768,512]{1,0:T(8,128)S(1)}, f32[768,512]{1,0:T(8,128)}) fusion(f32[512]{0:T(512)S(1)} %bitcast.465, f32[512]{0:T(512)S(1)} %bitcast.468, f32[768]{0:T(1024)S(1)} %add_rsqrt_fusion.1, f32[768]{0:T(1024)S(1)} %broadcast_multiply_fusion.6, bf16[800,512]{1,0:T(8,128)(2,1)S(1)} %copy-done.5, f32[512]{0:T(512)S(1)} %bitcast.474, ...), kind=kOutput, calls=%fused_computation.342 | convolution fusion | flops 1213464576 | bytes 10235904 | tf_op jit(solution)/shard_map/dot_general | solution.py:509
  63.8 3.4 %fusion.109 = (f32[768]{0:T(1024)S(1)}, f32[768,512]{1,0:T(8,128)S(1)}, f32[768,512]{1,0:T(8,128)}) fusion(f32[768,512]{1,0:T(8,128)S(1)} %get-tuple-element.300, bf16[800,512]{1,0:T(8,128)(2,1)S(1)} %copy-done.5, f32[512]{0:T(512)S(1)} %bitcast.479, bf16[2048,512]{1,0:T(8,128)(2,1)} %all-gather.6.cloned.1.call-done), kind=kOutput, calls=%fused_computation.350 | convolution fusion | flops 406191360 | bytes 7607296 | tf_op jit(solution)/shard_map/dot_general | solution.py:515
  68.3 0.9 copy-done.26
  70.5 1.1 copy-done.1
  71.6 1.6 pad_maximum_fusion.1.x_ref
  73.1 8.7 %shard_map.355.states_ref = f32[768,1536]{1,0:T(8,128)} custom-call(s32[2]{0:T(128)} %starts_ref.7, s32[2]{0:T(128)} %lengths_ref.7, f32[4,8,384]{2,1,0:T(8,128)} %pad_maximum_fusion.9.pow_ref, f32[768,768]{1,0:T(8,128)} %pad_maximum_fusion.1.x_ref), custom_call_target="tpu_custom_call" | custom-call | flops 11796480 | bytes 9437184 | tf_op jit(solution)/shard_map/pallas_call | solution.py:144
  81.9 1.2 all-gather.8.cloned.1.call-done
  83.1 4.3 %fusion.92 = (f32[768,512]{1,0:T(8,128)S(1)}, f32[768,512]{1,0:T(8,128)S(1)}) fusion(f32[512]{0:T(512)S(1)} %bitcast.471, f32[512]{0:T(512)S(1)} %bitcast.457, f32[768]{0:T(1024)S(1)} %add_rsqrt_fusion, f32[768,512]{1,0:T(8,128)S(1)} %copy-done.3, f32[768]{0:T(1024)S(1)} %broadcast_multiply_fusion.5, f32[512]{0:T(512)S(1)} %bitcast.476, ...), kind=kOutput, calls=%fused_computation.343 | convolution fusion | flops 1213071360 | bytes 11022336 | tf_op jit(solution)/shard_map/dot_general | solution.py:509
  87.4 1.6 convert_reduce_fusion.1
  89.4 0.9 dynamic-slice_add_fusion.1
  90.3 2.3 fusion.111
  92.7 1.7 convolution_bitcast_fusion
  94.4 3.6 %fusion.3.g_ref = f32[768,1536]{1,0:T(8,128)} fusion(bf16[768,512]{1,0:T(8,128)(2,1)S(1)} %get-tuple-element.306, bf16[2048,512]{1,0:T(8,128)(2,1)S(1)} %copy-done.33), kind=kOutput, calls=%fused_computation.43 | convolution fusion | flops 1207959552 | bytes 7077888 | tf_op jit(solution)/shard_map/dot_general | solution.py:406
  98.0 15.4 %shard_map.356 = (bf16[768,768]{1,0:T(8,128)(2,1)}, f32[4,384]{1,0:T(4,128)}) custom-call(s32[2]{0:T(128)} %starts_ref.7, s32[2]{0:T(128)} %lengths_ref.7, f32[4,8,384]{2,1,0:T(8,128)} %pad_maximum_fusion.10.pow_ref, f32[4,384]{1,0:T(4,128)} %pad_maximum_fusion.13.coef_ref, f32[768,4]{1,0:T(8,128)} %copy.86.masks_ref, f32[768,1536]{1,0:T(8,128)} %fusion.3.g_ref, ...), custom_call_target="tpu_custom_call" | custom-call | flops 17694720 | bytes 14155776 | tf_op jit(solution)/shard_map/pallas_call | solution.py:375
  113.4 2.6 %convolution_bitcast_fusion.2 = f32[1,128,768]{2,1,0:T(8,128)} fusion(bf16[768,768]{1,0:T(8,128)(2,1)} %get-tuple-element.26, bf16[768,512]{1,0:T(8,128)(2,1)} %copy-done.14, s32[]{:T(128)S(6)} %select_n.2), kind=kOutput, calls=%fused_computation.50 | convolution fusion | flops 150994944 | bytes 1769476 | tf_op jit(solution)/shard_map/dot_general | solution.py:400
  116.0 3.7 %multiply_reduce_fusion.1 = (f32[512]{0:T(512)}, f32[768]{0:T(1024)S(1)}, f32[512]{0:T(512)}, f32[768]{0:T(1024)S(1)}, f32[512]{0:T(512)}, /*index=5*/f32[768,512]{1,0:T(8,128)S(1)}) fusion(f32[768]{0:T(1024)S(1)} %add_rsqrt_fusion, f32[768,512]{1,0:T(8,128)S(1)} %copy-done.3, f32[768]{0:T(1024)S(1)} %broadcast_multiply_fusion.5, f32[512]{0:T(512)S(1)} %bitcast.458, ...), kind=kOutput, calls=%fused_computation.19 | convolution fusion | flops 609874944 | bytes 6709248 | tf_op jit(solution)/shard_map/dot_general | solution.py:555
  119.7 2.1 convert_reduce_fusion.2
  125.1 4.6 %fusion.112 = (bf16[768,512]{1,0:T(8,128)(2,1)S(1)}, f32[768,512]{1,0:T(8,128)}) fusion(f32[768,512]{1,0:T(8,128)} %get-tuple-element.301, bf16[768,512]{1,0:T(8,128)(2,1)} %copy-done.15, bf16[2048,512]{1,0:T(8,128)(2,1)} %all-gather.6.cloned.1.call-done, f32[768,512]{1,0:T(8,128)S(1)} %copy-done.6, f32[768,512]{1,0:T(8,128)} %get-tuple-element.302), kind=kOutput, calls=%fused_computation.353 | convolution fusion | flops 407371776 | bytes 8388608 | tf_op jit(solution)/shard_map/dot_general | solution.py:406
  129.8 1.7 convolution_bitcast_fusion.1
  132.8 3.6 %fusion.6.g_ref = f32[768,1536]{1,0:T(8,128)} fusion(bf16[768,512]{1,0:T(8,128)(2,1)S(1)} %get-tuple-element.309, bf16[2048,512]{1,0:T(8,128)(2,1)S(1)} %copy-done.32), kind=kOutput, calls=%fused_computation.46 | convolution fusion | flops 1207959552 | bytes 7077888 | tf_op jit(solution)/shard_map/dot_general | solution.py:406
  136.4 15.4 %shard_map.357 = (bf16[768,768]{1,0:T(8,128)(2,1)}, f32[4,384]{1,0:T(4,128)}) custom-call(s32[2]{0:T(128)} %starts_ref.7, s32[2]{0:T(128)} %lengths_ref.7, f32[4,8,384]{2,1,0:T(8,128)} %pad_maximum_fusion.11.pow_ref, f32[4,384]{1,0:T(4,128)} %pad_maximum_fusion.14.coef_ref, f32[768,4]{1,0:T(8,128)} %copy.86.masks_ref, f32[768,1536]{1,0:T(8,128)} %fusion.6.g_ref, ...), custom_call_target="tpu_custom_call" | custom-call | flops 17694720 | bytes 14155776 | tf_op jit(solution)/shard_map/pallas_call | solution.py:375
  151.8 1.8 convolution_bitcast_fusion.3
  153.6 0.9 pad_maximum_fusion.3
  154.6 2.1 reshape.1853
  156.9 1.3 constant_dynamic-update-slice_fusion.4
  158.3 1.6 pad_maximum_fusion.2
  160.7 2.9 %fusion.93 = (f32[512]{0:T(512)S(1)}, f32[512]{0:T(512)S(1)}, f32[512]{0:T(512)S(1)}, f32[768]{0:T(1024)S(1)}, f32[768]{0:T(1024)S(1)}, /*index=5*/f32[768,512]{1,0:T(8,128)}, f32[768,512]{1,0:T(8,128)}) fusion(f32[768]{0:T(1024)S(1)} %add_rsqrt_fusion.1, f32[768]{0:T(1024)S(1)} %broadcast_multiply_fusion.6, bf16[800,512]{1,0:T(8,128)(2,1)S(1)} %copy-done.5, ...), kind=kOutput, calls=%fused_computation.344 | convolution fusion | flops 610268160 | bytes 7497728 | tf_op jit(solution)/shard_map/dot_general | solution.py:555
  163.9 1.8 pad_bitcast_fusion.refs_0_
  165.7 61.3 %shard_map.358 = bf16[5888,128]{1,0:T(8,128)(2,1)} custom-call(f32[5888,128]{1,0:T(8,128)} %pad_bitcast_fusion.refs_0_), custom_call_target="tpu_custom_call" | custom-call | tf_op jit(solution)/shard_map/pallas_call | solution.py:267
  227.0 1.6 convert_element_type.123
  228.8 1.3 slice_multiply_fusion
  232.5 1.0 mul.6050
  234.2 2.6 %add_multiply_fusion.8 = (f32[2,512,128]{2,1,0:T(8,128)}, f32[2,512,128]{2,1,0:T(8,128)}, f32[2,512,128]{2,1,0:T(8,128)}) fusion(f32[2,512,128]{2,1,0:T(8,128)} %param.35, f32[2,512,128]{2,1,0:T(8,128)S(1)} %copy-done.19, f32[2,512,128]{2,1,0:T(8,128)S(1)} %bitcast.437, f32[2,512,128]{2,1,0:T(8,128)} %param.30), kind=kLoop, calls=%fused_computation.79 | loop fusion | flops 1310720 | bytes 3670016 | tf_op jit(solution)/shard_map/add | solution.py:395
  236.9 3.2 %add_multiply_fusion.7 = (f32[2,128,768]{2,1,0:T(8,128)}, f32[2,128,768]{2,1,0:T(8,128)}, f32[2,128,768]{2,1,0:T(8,128)}) fusion(f32[2,128,768]{2,1,0:T(8,128)} %param.33, f32[2,128,768]{2,1,0:T(8,128)S(1)} %copy-done.16, f32[2,128,768]{2,1,0:T(8,128)S(1)} %copy-done.17, f32[2,128,768]{2,1,0:T(8,128)} %param.28), kind=kLoop, calls=%fused_computation.68 | loop fusion | flops 1966080 | bytes 5505024 | tf_op jit(solution)/shard_map/add | solution.py:395
  240.1 2.6 %add_multiply_fusion = (f32[2,1536,128]{2,1,0:T(8,128)}, f32[2,1536,128]{2,1,0:T(8,128)}, f32[2,1536,128]{2,1,0:T(8,128)}) fusion(f32[2,1536,128]{2,1,0:T(8,128)S(1)} %copy-done.24, f32[2,1536,128]{2,1,0:T(8,128)S(1)} %copy-done.10, f32[2,1536,128]{2,1,0:T(8,128)S(1)} %bitcast.436, f32[2,1536,128]{2,1,0:T(8,128)S(1)} %copy-done.25), kind=kLoop, calls=%fused_computation.13 | loop fusion | flops 3932160 | bytes 11010048 | tf_op jit(solution)/shard_map/add | solution.py:395
  242.7 2.2 dynamic-slice_add_fusion
  (230 shorter events, 18.9 us)
Async XLA Ops:
  7.2 2.2 copy-start.9
  7.2 33.2 %all-gather.4.cloned.1.call-start = ((), (), s32[]{:S(2)}) async-start(), calls=%async_computation | async-start | bytes 1966080 | tf_op jit(solution)/shard_map/all_gather | solution.py:412
  9.3 48.7 %all-gather.6.cloned.1.call-start = ((), (), s32[]{:S(2)}) async-start(), calls=%async_computation.1 | async-start | bytes 2621440 | tf_op jit(solution)/shard_map/all_gather | solution.py:412
  9.7 2.5 copy-start.37
  9.7 2.5 copy-start.30
  10.5 72.5 %all-gather.8.cloned.1.call-start = ((), (), s32[]{:S(2)}) async-start(), calls=%async_computation.2 | async-start | bytes 2621440 | tf_op jit(solution)/shard_map/all_gather | solution.py:412
  11.4 11.2 %copy-start.36 = (s32[2]{0:T(128)S(1)}, s32[2]{0:T(128)}, u32[]{:S(2)}) copy-start(s32[2]{0:T(128)} %starts_ref.7) | copy-start | bytes 28
  11.4 11.2 %copy-start.39 = (s32[2]{0:T(128)S(1)}, s32[2]{0:T(128)}, u32[]{:S(2)}) copy-start(s32[2]{0:T(128)} %lengths_ref.7) | copy-start | bytes 28
  22.5 14.8 %copy-start.4 = (bf16[800,512]{1,0:T(8,128)(2,1)}, bf16[800,512]{1,0:T(8,128)(2,1)S(1)}, u32[]{:S(2)}) copy-start(bf16[800,512]{1,0:T(8,128)(2,1)S(1)} %all_gather.15) | copy-start | bytes 2457604
  22.5 4.2 %copy-start.31 = (bf16[768,128]{1,0:T(8,128)(2,1)S(1)}, bf16[768,128]{1,0:T(8,128)(2,1)}, u32[]{:S(2)}) copy-start(bf16[768,128]{1,0:T(8,128)(2,1)} %param.20) | copy-start | bytes 589828
  26.6 31.4 %copy-start.54 = (f32[1,512]{1,0:T(1,128)}, f32[1,512]{1,0:T(1,128)S(1)}, u32[]{:S(2)}) copy-start(f32[1,512]{1,0:T(1,128)S(1)} %get-tuple-element.248) | copy-start | bytes 6148
  26.6 56.4 %copy-start.56 = (f32[1,512]{1,0:T(1,128)}, f32[1,512]{1,0:T(1,128)S(1)}, u32[]{:S(2)}) copy-start(f32[1,512]{1,0:T(1,128)S(1)} %get-tuple-element.243) | copy-start | bytes 6148
  45.7 12.4 %copy-start.5 = (bf16[800,512]{1,0:T(8,128)(2,1)S(1)}, bf16[800,512]{1,0:T(8,128)(2,1)}, u32[]{:S(2)}) copy-start(bf16[800,512]{1,0:T(8,128)(2,1)} %copy-done.4) | copy-start | bytes 2457604
  63.8 3.4 %copy-start.11 = (f32[768,512]{1,0:T(8,128)}, f32[768,512]{1,0:T(8,128)S(1)}, u32[]{:S(2)}) copy-start(f32[768,512]{1,0:T(8,128)S(1)} %get-tuple-element.300) | copy-start | bytes 4718596
  73.1 9.9 %copy-start.3 = (f32[768,512]{1,0:T(8,128)S(1)}, f32[768,512]{1,0:T(8,128)}, u32[]{:S(2)}) copy-start(f32[768,512]{1,0:T(8,128)} %copy-done.2) | copy-start | bytes 4718596
  83.1 4.3 %copy-start.7 = (bf16[768,512]{1,0:T(8,128)(2,1)S(1)}, bf16[768,512]{1,0:T(8,128)(2,1)}, u32[]{:S(2)}) copy-start(bf16[768,512]{1,0:T(8,128)(2,1)} %all_gather.19) | copy-start | bytes 2359300
  83.1 4.3 %copy-start.33 = (bf16[2048,512]{1,0:T(8,128)(2,1)S(1)}, bf16[2048,512]{1,0:T(8,128)(2,1)}, u32[]{:S(2)}) copy-start(bf16[2048,512]{1,0:T(8,128)(2,1)} %all-gather.8.cloned.1.call-done) | copy-start | bytes 6291460
  89.4 3.2 %slice-start.2 = ((s8[4718592]{0:T(1024)(128)(4,1)}), s8[4194304]{0:T(1024)(128)(4,1)S(1)}, s32[]{:S(2)}) async-start(s8[4718592]{0:T(1024)(128)(4,1)} %bitcast.432), calls=%async_computation.5 | async-start | bytes 8388608
  90.3 2.3 slice-start.3
  113.4 2.6 %copy-start.22 = (f32[768,512]{1,0:T(8,128)S(1)}, f32[768,512]{1,0:T(8,128)}, u32[]{:S(2)}) copy-start(f32[768,512]{1,0:T(8,128)} %get-tuple-element.307) | copy-start | bytes 4718596
  113.4 2.6 %copy-start.57 = (f32[1,512]{1,0:T(1,128)S(1)}, f32[1,512]{1,0:T(1,128)}, u32[]{:S(2)}) copy-start(f32[1,512]{1,0:T(1,128)} %copy-done.56) | copy-start | bytes 6148
  116.0 3.7 %copy-start.8 = (f32[768,512]{1,0:T(8,128)S(1)}, f32[768,512]{1,0:T(8,128)}, u32[]{:S(2)}) copy-start(f32[768,512]{1,0:T(8,128)} %get-tuple-element.302) | copy-start | bytes 4718596
  116.0 3.7 %copy-start.12 = (f32[768,512]{1,0:T(8,128)S(1)}, f32[768,512]{1,0:T(8,128)}, u32[]{:S(2)}) copy-start(f32[768,512]{1,0:T(8,128)} %copy-done.11) | copy-start | bytes 4718596
  121.8 2.2 copy-start.45
  121.8 3.3 %copy-start.6 = (f32[768,512]{1,0:T(8,128)S(1)}, f32[768,512]{1,0:T(8,128)}, u32[]{:S(2)}) copy-start(f32[768,512]{1,0:T(8,128)} %get-tuple-element.159) | copy-start | bytes 4718596
  121.8 7.9 %slice-start = ((s8[4718592]{0:T(1024)(128)(4,1)}), s8[524288]{0:T(1024)(128)(4,1)S(1)}, s32[]{:S(2)}) async-start(s8[4718592]{0:T(1024)(128)(4,1)} %bitcast.430), calls=%async_computation.3 | async-start | bytes 1048576
  125.1 4.7 %slice-start.1 = ((s8[4718592]{0:T(1024)(128)(4,1)}), s8[4194304]{0:T(1024)(128)(4,1)S(1)}, s32[]{:S(2)}) async-start(s8[4718592]{0:T(1024)(128)(4,1)} %bitcast.430), calls=%async_computation.4 | async-start | bytes 8388608
  129.8 3.0 %copy-start.32 = (bf16[2048,512]{1,0:T(8,128)(2,1)S(1)}, bf16[2048,512]{1,0:T(8,128)(2,1)}, u32[]{:S(2)}) copy-start(bf16[2048,512]{1,0:T(8,128)(2,1)} %all-gather.6.cloned.1.call-done) | copy-start | bytes 6291460
  153.6 3.1 %copy-start.35 = (f32[4,384]{1,0:T(4,128)S(1)}, f32[4,384]{1,0:T(4,128)}, u32[]{:S(2)}) copy-start(f32[4,384]{1,0:T(4,128)} %get-tuple-element.28) | copy-start | bytes 18436
  153.6 3.1 %copy-start.48 = (f32[1,384]{1,0:T(1,128)S(1)}, f32[1,384]{1,0:T(1,128)}, u32[]{:S(2)}) copy-start(f32[1,384]{1,0:T(1,128)} %get-tuple-element.255) | copy-start | bytes 4612
  153.6 3.0 %copy-start.49 = (f32[1,384]{1,0:T(1,128)S(1)}, f32[1,384]{1,0:T(1,128)}, u32[]{:S(2)}) copy-start(f32[1,384]{1,0:T(1,128)} %get-tuple-element.252) | copy-start | bytes 4612
  153.6 3.2 %copy-start.47 = (f32[1,384]{1,0:T(1,128)S(1)}, f32[1,384]{1,0:T(1,128)}, u32[]{:S(2)}) copy-start(f32[1,384]{1,0:T(1,128)} %get-tuple-element.155) | copy-start | bytes 4612
  153.6 3.2 %copy-start.50 = (f32[1,384]{1,0:T(1,128)S(1)}, f32[1,384]{1,0:T(1,128)}, u32[]{:S(2)}) copy-start(f32[1,384]{1,0:T(1,128)} %get-tuple-element.241) | copy-start | bytes 4612
  153.6 3.2 %copy-start.51 = (f32[1,384]{1,0:T(1,128)S(1)}, f32[1,384]{1,0:T(1,128)}, u32[]{:S(2)}) copy-start(f32[1,384]{1,0:T(1,128)} %get-tuple-element.242) | copy-start | bytes 4612
  156.9 3.2 %copy-start.28 = (bf16[768,768]{1,0:T(8,128)(2,1)S(1)}, bf16[768,768]{1,0:T(8,128)(2,1)}, u32[]{:S(2)}) copy-start(bf16[768,768]{1,0:T(8,128)(2,1)} %get-tuple-element.27) | copy-start | bytes 3538948
  158.3 2.4 copy-start.27
  158.3 2.4 copy-start.55
  228.6 5.0 %copy-start.38 = (f32[8,128]{1,0:T(8,128)}, f32[8,128]{1,0:T(8,128)S(1)}, u32[]{:S(2)}) copy-start(f32[8,128]{1,0:T(8,128)S(1)} %slice_multiply_fusion.4) | copy-start | bytes 12292
  228.7 5.5 %copy-start.20 = (f32[1024,128]{1,0:T(8,128)}, f32[1024,128]{1,0:T(8,128)S(1)}, u32[]{:S(2)}) copy-start(f32[1024,128]{1,0:T(8,128)S(1)} %slice_multiply_fusion.2) | copy-start | bytes 1572868
  230.1 3.5 %copy-start.52 = (f32[2,4,128]{2,1,0:T(4,128)S(1)}, f32[2,4,128]{2,1,0:T(4,128)}, u32[]{:S(2)}) copy-start(f32[2,4,128]{2,1,0:T(4,128)} %param.36) | copy-start | bytes 12292
  230.1 3.5 %copy-start.53 = (f32[2,4,128]{2,1,0:T(4,128)S(1)}, f32[2,4,128]{2,1,0:T(4,128)}, u32[]{:S(2)}) copy-start(f32[2,4,128]{2,1,0:T(4,128)} %param.31) | copy-start | bytes 12292
  230.1 4.1 %copy-start.19 = (f32[2,512,128]{2,1,0:T(8,128)S(1)}, f32[2,512,128]{2,1,0:T(8,128)}, u32[]{:S(2)}) copy-start(f32[2,512,128]{2,1,0:T(8,128)} %param.25) | copy-start | bytes 1572868
  234.2 2.7 %copy-start.16 = (f32[2,128,768]{2,1,0:T(8,128)S(1)}, f32[2,128,768]{2,1,0:T(8,128)}, u32[]{:S(2)}) copy-start(f32[2,128,768]{2,1,0:T(8,128)} %param.23) | copy-start | bytes 2359300
  234.2 2.7 %copy-start.17 = (f32[2,128,768]{2,1,0:T(8,128)S(1)}, f32[2,128,768]{2,1,0:T(8,128)}, u32[]{:S(2)}) copy-start(f32[2,128,768]{2,1,0:T(8,128)} %mul.6050) | copy-start | bytes 2359300
  234.2 5.9 %copy-start.25 = (f32[2,1536,128]{2,1,0:T(8,128)S(1)}, f32[2,1536,128]{2,1,0:T(8,128)}, u32[]{:S(2)}) copy-start(f32[2,1536,128]{2,1,0:T(8,128)} %param.29) | copy-start | bytes 4718596
  236.9 3.2 %copy-start.10 = (f32[2,1536,128]{2,1,0:T(8,128)S(1)}, f32[2,1536,128]{2,1,0:T(8,128)}, u32[]{:S(2)}) copy-start(f32[2,1536,128]{2,1,0:T(8,128)} %param.24) | copy-start | bytes 4718596
  236.9 3.2 %copy-start.13 = (f32[3072,128]{1,0:T(8,128)S(1)}, f32[3072,128]{1,0:T(8,128)}, u32[]{:S(2)}) copy-start(f32[3072,128]{1,0:T(8,128)} %slice_multiply_fusion) | copy-start | bytes 4718596
  236.9 3.2 %copy-start.24 = (f32[2,1536,128]{2,1,0:T(8,128)S(1)}, f32[2,1536,128]{2,1,0:T(8,128)}, u32[]{:S(2)}) copy-start(f32[2,1536,128]{2,1,0:T(8,128)} %param.34) | copy-start | bytes 4718596
  (21 other events, 32.0 us)
Sparse Core Ops, SparseCore 0:
  10.2 23.1 all-gather.3
  35.5 22.4 all-gather.5
  60.2 22.8 all-gather.7

commit v24 on v23

--- a/solution.py
+++ b/solution.py
@@ -219,7 +219,7 @@
 
         return carry
 
-    lax.fori_loop(0, n - 1, scatter_step, 0)
+    lax.fori_loop(0, n - 1, scatter_step, 0, unroll=True)
     for ring, place, target, source in rings:
         pl.semaphore_signal(done.at[ring], 1, device_id={"seq": source}, device_id_type=MESH)
     for ring, place, target, source in rings:
@@ -254,7 +254,7 @@
 
         return carry
 
-    lax.fori_loop(0, n - 1, gather_step, 0)
+    lax.fori_loop(0, n - 1, gather_step, 0, unroll=True)
     for ring, place, target, source in rings:
         last = gather_copy(ring, place, target, n - 2)
         last.wait_recv()

time: 252 us -> 252 us (level)
  no operation moved by 1% of the time
where the time goes in v24:
time: 252 us; the launch traced here: 251 us
  Pallas kernels  109 us (43%)
  matrix products  47.5 us (19%)
  other arithmetic  37.9 us (15%)
  blocking collectives  20.2 us (8%)
  local copies, waits for them, and re-layouts  16.6 us (7%)
  between operations  14.7 us (6%)
  waiting for transfers between devices  4.76 us (2%)
    pallas_call x1, Pallas kernels, ring_sum(): pl.pallas_call(lambda *refs: ring_sum_kernel(n, *refs), out_shape=jax.Sha...  61.1 us
    pallas_call x2, Pallas kernels, adjoint(): pl.pallas_call(adjoint_kernel, out_shape=(jax.ShapeDtypeStruct((count, 2...  30.8 us
    all_gather x2, blocking collectives, gather_feat(): return lax.all_gather(value, 'feat', axis=axis, tiled=True)  20.2 us
    pallas_call x2, Pallas kernels, recurrence(): pl.pallas_call(recurrence_kernel, out_shape=jax.ShapeDtypeStruct((count,...  17.6 us
    dot_general x4, matrix products, contract_cols(): lax.dot_general(left, right, (((1,), (1,)), ((), ())), preferred_element_...  14.2 us
    dot_general x2, matrix products, body(): jnp.dot(states_low, out_low, preferred_element_type=jnp.float32)  10 us
    add x5, other arithmetic, update(): average_new = smoothing * average + (1.0 - smoothing) * weight_new  9.08 us
    unnamed x140, local copies, waits for them, and re-layouts  8.75 us
  transfers between devices with their start and end apart: 3, of which 2 were waited for; matrix products, arithmetic and copies ran while one was open for 11% of the time, Pallas kernels for 7%

profile of v24, /device:TPU:0, one launch (start us, length us, event | category | flops | bytes accessed | tf_op | source)
XLA Modules:
  0.0 251.3 jit_solution(17094094236605160990)
XLA Ops:
  7.3 2.1 convert_element_type.103
  9.7 0.8 pad_maximum_fusion.4
  10.6 0.8 pad_maximum_fusion.5
  12.2 10.2 %all_gather.15 = bf16[800,512]{1,0:T(8,128)(2,1)S(1)} all-gather(bf16[800,128]{1,0:T(8,128)(2,1)S(1)} %pad_maximum_fusion.7), channel_id=1, replica_groups=mesh['seq'=8,'feat'=4] {'feat'}, dimensions={1}, use_global_device_ids=true | all-gather | bytes 1024000 | tf_op jit(solution)/shard_map/all_gather | solution.py:412
  25.2 0.9 copy.86.masks_ref
  26.6 10.0 %all_gather.19 = bf16[768,512]{1,0:T(8,128)(2,1)} all-gather(bf16[768,128]{1,0:T(8,128)(2,1)S(1)} %copy-done.31), channel_id=1, replica_groups=mesh['seq'=8,'feat'=4] {'feat'}, dimensions={1}, use_global_device_ids=true | all-gather | bytes 983040 | tf_op jit(solution)/shard_map/all_gather | solution.py:412
  37.2 1.2 fusion.9
  40.4 2.2 fusion.15.drive_ref
  43.0 1.0 copy-done
  44.0 1.6 pad_maximum_fusion.x_ref
  45.7 8.8 %shard_map.354.states_ref = f32[768,1536]{1,0:T(8,128)} custom-call(s32[2]{0:T(128)} %starts_ref.7, s32[2]{0:T(128)} %lengths_ref.7, f32[4,8,384]{2,1,0:T(8,128)} %pad_maximum_fusion.8.pow_ref, f32[768,768]{1,0:T(8,128)} %pad_maximum_fusion.x_ref), custom_call_target="tpu_custom_call" | custom-call | flops 11796480 | bytes 9437184 | tf_op jit(solution)/shard_map/pallas_call | solution.py:144
  54.5 3.6 %all-gather.6.cloned.1.call-done = bf16[2048,512]{1,0:T(8,128)(2,1)} async-done(((bf16[2048,128]{1,0:T(8,128)(2,1)}), bf16[2048,512]{1,0:T(8,128)(2,1)}) %all-gather.6.cloned.1.call-update) | async-done | bytes 2097168 | tf_op jit(solution)/shard_map/all_gather | solution.py:412
  58.1 5.7 %fusion.91 = (f32[768,512]{1,0:T(8,128)S(1)}, f32[768,512]{1,0:T(8,128)}) fusion(f32[512]{0:T(512)S(1)} %bitcast.465, f32[512]{0:T(512)S(1)} %bitcast.468, f32[768]{0:T(1024)S(1)} %add_rsqrt_fusion.1, f32[768]{0:T(1024)S(1)} %broadcast_multiply_fusion.6, bf16[800,512]{1,0:T(8,128)(2,1)S(1)} %copy-done.5, f32[512]{0:T(512)S(1)} %bitcast.474, ...), kind=kOutput, calls=%fused_computation.342 | convolution fusion | flops 1213464576 | bytes 10235904 | tf_op jit(solution)/shard_map/dot_general | solution.py:509
  63.8 3.4 %fusion.109 = (f32[768]{0:T(1024)S(1)}, f32[768,512]{1,0:T(8,128)S(1)}, f32[768,512]{1,0:T(8,128)}) fusion(f32[768,512]{1,0:T(8,128)S(1)} %get-tuple-element.300, bf16[800,512]{1,0:T(8,128)(2,1)S(1)} %copy-done.5, f32[512]{0:T(512)S(1)} %bitcast.479, bf16[2048,512]{1,0:T(8,128)(2,1)} %all-gather.6.cloned.1.call-done), kind=kOutput, calls=%fused_computation.350 | convolution fusion | flops 406191360 | bytes 7607296 | tf_op jit(solution)/shard_map/dot_general | solution.py:515
  68.3 0.9 copy-done.26
  70.5 1.1 copy-done.1
  71.6 1.6 pad_maximum_fusion.1.x_ref
  73.1 8.7 %shard_map.355.states_ref = f32[768,1536]{1,0:T(8,128)} custom-call(s32[2]{0:T(128)} %starts_ref.7, s32[2]{0:T(128)} %lengths_ref.7, f32[4,8,384]{2,1,0:T(8,128)} %pad_maximum_fusion.9.pow_ref, f32[768,768]{1,0:T(8,128)} %pad_maximum_fusion.1.x_ref), custom_call_target="tpu_custom_call" | custom-call | flops 11796480 | bytes 9437184 | tf_op jit(solution)/shard_map/pallas_call | solution.py:144
  81.9 1.2 all-gather.8.cloned.1.call-done
  83.1 4.3 %fusion.92 = (f32[768,512]{1,0:T(8,128)S(1)}, f32[768,512]{1,0:T(8,128)S(1)}) fusion(f32[512]{0:T(512)S(1)} %bitcast.471, f32[512]{0:T(512)S(1)} %bitcast.457, f32[768]{0:T(1024)S(1)} %add_rsqrt_fusion, f32[768,512]{1,0:T(8,128)S(1)} %copy-done.3, f32[768]{0:T(1024)S(1)} %broadcast_multiply_fusion.5, f32[512]{0:T(512)S(1)} %bitcast.476, ...), kind=kOutput, calls=%fused_computation.343 | convolution fusion | flops 1213071360 | bytes 11022336 | tf_op jit(solution)/shard_map/dot_general | solution.py:509
  87.4 1.6 convert_reduce_fusion.1
  89.4 0.9 dynamic-slice_add_fusion.1
  90.3 2.3 fusion.111
  92.7 1.7 convolution_bitcast_fusion
  94.4 3.6 %fusion.3.g_ref = f32[768,1536]{1,0:T(8,128)} fusion(bf16[768,512]{1,0:T(8,128)(2,1)S(1)} %get-tuple-element.306, bf16[2048,512]{1,0:T(8,128)(2,1)S(1)} %copy-done.33), kind=kOutput, calls=%fused_computation.43 | convolution fusion | flops 1207959552 | bytes 7077888 | tf_op jit(solution)/shard_map/dot_general | solution.py:406
  98.0 15.4 %shard_map.356 = (bf16[768,768]{1,0:T(8,128)(2,1)}, f32[4,384]{1,0:T(4,128)}) custom-call(s32[2]{0:T(128)} %starts_ref.7, s32[2]{0:T(128)} %lengths_ref.7, f32[4,8,384]{2,1,0:T(8,128)} %pad_maximum_fusion.10.pow_ref, f32[4,384]{1,0:T(4,128)} %pad_maximum_fusion.13.coef_ref, f32[768,4]{1,0:T(8,128)} %copy.86.masks_ref, f32[768,1536]{1,0:T(8,128)} %fusion.3.g_ref, ...), custom_call_target="tpu_custom_call" | custom-call | flops 17694720 | bytes 14155776 | tf_op jit(solution)/shard_map/pallas_call | solution.py:375
  113.4 2.6 %convolution_bitcast_fusion.2 = f32[1,128,768]{2,1,0:T(8,128)} fusion(bf16[768,768]{1,0:T(8,128)(2,1)} %get-tuple-element.26, bf16[768,512]{1,0:T(8,128)(2,1)} %copy-done.14, s32[]{:T(128)S(6)} %select_n.2), kind=kOutput, calls=%fused_computation.50 | convolution fusion | flops 150994944 | bytes 1769476 | tf_op jit(solution)/shard_map/dot_general | solution.py:400
  116.0 3.7 %multiply_reduce_fusion.1 = (f32[512]{0:T(512)}, f32[768]{0:T(1024)S(1)}, f32[512]{0:T(512)}, f32[768]{0:T(1024)S(1)}, f32[512]{0:T(512)}, /*index=5*/f32[768,512]{1,0:T(8,128)S(1)}) fusion(f32[768]{0:T(1024)S(1)} %add_rsqrt_fusion, f32[768,512]{1,0:T(8,128)S(1)} %copy-done.3, f32[768]{0:T(1024)S(1)} %broadcast_multiply_fusion.5, f32[512]{0:T(512)S(1)} %bitcast.458, ...), kind=kOutput, calls=%fused_computation.19 | convolution fusion | flops 609874944 | bytes 6709248 | tf_op jit(solution)/shard_map/dot_general | solution.py:555
  119.7 2.1 convert_reduce_fusion.2
  125.1 4.6 %fusion.112 = (bf16[768,512]{1,0:T(8,128)(2,1)S(1)}, f32[768,512]{1,0:T(8,128)}) fusion(f32[768,512]{1,0:T(8,128)} %get-tuple-element.301, bf16[768,512]{1,0:T(8,128)(2,1)} %copy-done.15, bf16[2048,512]{1,0:T(8,128)(2,1)} %all-gather.6.cloned.1.call-done, f32[768,512]{1,0:T(8,128)S(1)} %copy-done.6, f32[768,512]{1,0:T(8,128)} %get-tuple-element.302), kind=kOutput, calls=%fused_computation.353 | convolution fusion | flops 407371776 | bytes 8388608 | tf_op jit(solution)/shard_map/dot_general | solution.py:406
  129.8 1.7 convolution_bitcast_fusion.1
  132.8 3.6 %fusion.6.g_ref = f32[768,1536]{1,0:T(8,128)} fusion(bf16[768,512]{1,0:T(8,128)(2,1)S(1)} %get-tuple-element.309, bf16[2048,512]{1,0:T(8,128)(2,1)S(1)} %copy-done.32), kind=kOutput, calls=%fused_computation.46 | convolution fusion | flops 1207959552 | bytes 7077888 | tf_op jit(solution)/shard_map/dot_general | solution.py:406
  136.4 15.4 %shard_map.357 = (bf16[768,768]{1,0:T(8,128)(2,1)}, f32[4,384]{1,0:T(4,128)}) custom-call(s32[2]{0:T(128)} %starts_ref.7, s32[2]{0:T(128)} %lengths_ref.7, f32[4,8,384]{2,1,0:T(8,128)} %pad_maximum_fusion.11.pow_ref, f32[4,384]{1,0:T(4,128)} %pad_maximum_fusion.14.coef_ref, f32[768,4]{1,0:T(8,128)} %copy.86.masks_ref, f32[768,1536]{1,0:T(8,128)} %fusion.6.g_ref, ...), custom_call_target="tpu_custom_call" | custom-call | flops 17694720 | bytes 14155776 | tf_op jit(solution)/shard_map/pallas_call | solution.py:375
  151.8 1.8 convolution_bitcast_fusion.3
  153.6 0.9 pad_maximum_fusion.3
  154.6 2.1 reshape.1853
  156.9 1.3 constant_dynamic-update-slice_fusion.4
  158.3 1.6 pad_maximum_fusion.2
  160.7 2.9 %fusion.93 = (f32[512]{0:T(512)S(1)}, f32[512]{0:T(512)S(1)}, f32[512]{0:T(512)S(1)}, f32[768]{0:T(1024)S(1)}, f32[768]{0:T(1024)S(1)}, /*index=5*/f32[768,512]{1,0:T(8,128)}, f32[768,512]{1,0:T(8,128)}) fusion(f32[768]{0:T(1024)S(1)} %add_rsqrt_fusion.1, f32[768]{0:T(1024)S(1)} %broadcast_multiply_fusion.6, bf16[800,512]{1,0:T(8,128)(2,1)S(1)} %copy-done.5, ...), kind=kOutput, calls=%fused_computation.344 | convolution fusion | flops 610268160 | bytes 7497728 | tf_op jit(solution)/shard_map/dot_general | solution.py:555
  163.9 1.8 pad_bitcast_fusion.refs_0_
  165.7 61.1 %shard_map.358 = bf16[5888,128]{1,0:T(8,128)(2,1)} custom-call(f32[5888,128]{1,0:T(8,128)} %pad_bitcast_fusion.refs_0_), custom_call_target="tpu_custom_call" | custom-call | tf_op jit(solution)/shard_map/pallas_call | solution.py:267
  226.8 1.6 convert_element_type.123
  228.6 1.3 slice_multiply_fusion
  232.3 1.0 mul.6050
  234.0 2.6 %add_multiply_fusion.8 = (f32[2,512,128]{2,1,0:T(8,128)}, f32[2,512,128]{2,1,0:T(8,128)}, f32[2,512,128]{2,1,0:T(8,128)}) fusion(f32[2,512,128]{2,1,0:T(8,128)} %param.35, f32[2,512,128]{2,1,0:T(8,128)S(1)} %copy-done.19, f32[2,512,128]{2,1,0:T(8,128)S(1)} %bitcast.437, f32[2,512,128]{2,1,0:T(8,128)} %param.30), kind=kLoop, calls=%fused_computation.79 | loop fusion | flops 1310720 | bytes 3670016 | tf_op jit(solution)/shard_map/add | solution.py:395
  236.7 3.2 %add_multiply_fusion.7 = (f32[2,128,768]{2,1,0:T(8,128)}, f32[2,128,768]{2,1,0:T(8,128)}, f32[2,128,768]{2,1,0:T(8,128)}) fusion(f32[2,128,768]{2,1,0:T(8,128)} %param.33, f32[2,128,768]{2,1,0:T(8,128)S(1)} %copy-done.16, f32[2,128,768]{2,1,0:T(8,128)S(1)} %copy-done.17, f32[2,128,768]{2,1,0:T(8,128)} %param.28), kind=kLoop, calls=%fused_computation.68 | loop fusion | flops 1966080 | bytes 5505024 | tf_op jit(solution)/shard_map/add | solution.py:395
  239.9 2.6 %add_multiply_fusion = (f32[2,1536,128]{2,1,0:T(8,128)}, f32[2,1536,128]{2,1,0:T(8,128)}, f32[2,1536,128]{2,1,0:T(8,128)}) fusion(f32[2,1536,128]{2,1,0:T(8,128)S(1)} %copy-done.24, f32[2,1536,128]{2,1,0:T(8,128)S(1)} %copy-done.10, f32[2,1536,128]{2,1,0:T(8,128)S(1)} %bitcast.436, f32[2,1536,128]{2,1,0:T(8,128)S(1)} %copy-done.25), kind=kLoop, calls=%fused_computation.13 | loop fusion | flops 3932160 | bytes 11010048 | tf_op jit(solution)/shard_map/add | solution.py:395
  242.5 2.2 dynamic-slice_add_fusion
  (230 shorter events, 18.9 us)
Async XLA Ops:
  7.2 2.2 copy-start.9
  7.2 33.2 %all-gather.4.cloned.1.call-start = ((), (), s32[]{:S(2)}) async-start(), calls=%async_computation | async-start | bytes 1966080 | tf_op jit(solution)/shard_map/all_gather | solution.py:412
  9.3 48.7 %all-gather.6.cloned.1.call-start = ((), (), s32[]{:S(2)}) async-start(), calls=%async_computation.1 | async-start | bytes 2621440 | tf_op jit(solution)/shard_map/all_gather | solution.py:412
  9.7 2.5 copy-start.37
  9.7 2.5 %copy-start.30 = (bf16[768,128]{1,0:T(8,128)(2,1)S(1)}, bf16[768,128]{1,0:T(8,128)(2,1)}, u32[]{:S(2)}) copy-start(bf16[768,128]{1,0:T(8,128)(2,1)} %param.19) | copy-start | bytes 589828
  10.5 72.5 %all-gather.8.cloned.1.call-start = ((), (), s32[]{:S(2)}) async-start(), calls=%async_computation.2 | async-start | bytes 2621440 | tf_op jit(solution)/shard_map/all_gather | solution.py:412
  11.4 11.2 %copy-start.36 = (s32[2]{0:T(128)S(1)}, s32[2]{0:T(128)}, u32[]{:S(2)}) copy-start(s32[2]{0:T(128)} %starts_ref.7) | copy-start | bytes 28
  11.4 11.2 %copy-start.39 = (s32[2]{0:T(128)S(1)}, s32[2]{0:T(128)}, u32[]{:S(2)}) copy-start(s32[2]{0:T(128)} %lengths_ref.7) | copy-start | bytes 28
  22.5 14.8 %copy-start.4 = (bf16[800,512]{1,0:T(8,128)(2,1)}, bf16[800,512]{1,0:T(8,128)(2,1)S(1)}, u32[]{:S(2)}) copy-start(bf16[800,512]{1,0:T(8,128)(2,1)S(1)} %all_gather.15) | copy-start | bytes 2457604
  22.5 4.2 %copy-start.31 = (bf16[768,128]{1,0:T(8,128)(2,1)S(1)}, bf16[768,128]{1,0:T(8,128)(2,1)}, u32[]{:S(2)}) copy-start(bf16[768,128]{1,0:T(8,128)(2,1)} %param.20) | copy-start | bytes 589828
  26.6 31.4 %copy-start.54 = (f32[1,512]{1,0:T(1,128)}, f32[1,512]{1,0:T(1,128)S(1)}, u32[]{:S(2)}) copy-start(f32[1,512]{1,0:T(1,128)S(1)} %get-tuple-element.248) | copy-start | bytes 6148
  26.6 56.4 %copy-start.56 = (f32[1,512]{1,0:T(1,128)}, f32[1,512]{1,0:T(1,128)S(1)}, u32[]{:S(2)}) copy-start(f32[1,512]{1,0:T(1,128)S(1)} %get-tuple-element.243) | copy-start | bytes 6148
  45.7 12.4 %copy-start.5 = (bf16[800,512]{1,0:T(8,128)(2,1)S(1)}, bf16[800,512]{1,0:T(8,128)(2,1)}, u32[]{:S(2)}) copy-start(bf16[800,512]{1,0:T(8,128)(2,1)} %copy-done.4) | copy-start | bytes 2457604
  63.8 3.4 %copy-start.11 = (f32[768,512]{1,0:T(8,128)}, f32[768,512]{1,0:T(8,128)S(1)}, u32[]{:S(2)}) copy-start(f32[768,512]{1,0:T(8,128)S(1)} %get-tuple-element.300) | copy-start | bytes 4718596
  73.1 9.9 %copy-start.3 = (f32[768,512]{1,0:T(8,128)S(1)}, f32[768,512]{1,0:T(8,128)}, u32[]{:S(2)}) copy-start(f32[768,512]{1,0:T(8,128)} %copy-done.2) | copy-start | bytes 4718596
  83.1 4.3 %copy-start.7 = (bf16[768,512]{1,0:T(8,128)(2,1)S(1)}, bf16[768,512]{1,0:T(8,128)(2,1)}, u32[]{:S(2)}) copy-start(bf16[768,512]{1,0:T(8,128)(2,1)} %all_gather.19) | copy-start | bytes 2359300
  83.1 4.3 %copy-start.33 = (bf16[2048,512]{1,0:T(8,128)(2,1)S(1)}, bf16[2048,512]{1,0:T(8,128)(2,1)}, u32[]{:S(2)}) copy-start(bf16[2048,512]{1,0:T(8,128)(2,1)} %all-gather.8.cloned.1.call-done) | copy-start | bytes 6291460
  89.4 3.2 %slice-start.2 = ((s8[4718592]{0:T(1024)(128)(4,1)}), s8[4194304]{0:T(1024)(128)(4,1)S(1)}, s32[]{:S(2)}) async-start(s8[4718592]{0:T(1024)(128)(4,1)} %bitcast.432), calls=%async_computation.5 | async-start | bytes 8388608
  90.3 2.3 slice-start.3
  113.4 2.6 %copy-start.22 = (f32[768,512]{1,0:T(8,128)S(1)}, f32[768,512]{1,0:T(8,128)}, u32[]{:S(2)}) copy-start(f32[768,512]{1,0:T(8,128)} %get-tuple-element.307) | copy-start | bytes 4718596
  113.4 2.6 %copy-start.57 = (f32[1,512]{1,0:T(1,128)S(1)}, f32[1,512]{1,0:T(1,128)}, u32[]{:S(2)}) copy-start(f32[1,512]{1,0:T(1,128)} %copy-done.56) | copy-start | bytes 6148
  116.0 3.7 %copy-start.8 = (f32[768,512]{1,0:T(8,128)S(1)}, f32[768,512]{1,0:T(8,128)}, u32[]{:S(2)}) copy-start(f32[768,512]{1,0:T(8,128)} %get-tuple-element.302) | copy-start | bytes 4718596
  116.0 3.7 %copy-start.12 = (f32[768,512]{1,0:T(8,128)S(1)}, f32[768,512]{1,0:T(8,128)}, u32[]{:S(2)}) copy-start(f32[768,512]{1,0:T(8,128)} %copy-done.11) | copy-start | bytes 4718596
  121.8 2.2 copy-start.45
  121.8 3.3 %copy-start.6 = (f32[768,512]{1,0:T(8,128)S(1)}, f32[768,512]{1,0:T(8,128)}, u32[]{:S(2)}) copy-start(f32[768,512]{1,0:T(8,128)} %get-tuple-element.159) | copy-start | bytes 4718596
  121.8 7.9 %slice-start = ((s8[4718592]{0:T(1024)(128)(4,1)}), s8[524288]{0:T(1024)(128)(4,1)S(1)}, s32[]{:S(2)}) async-start(s8[4718592]{0:T(1024)(128)(4,1)} %bitcast.430), calls=%async_computation.3 | async-start | bytes 1048576
  125.1 4.7 %slice-start.1 = ((s8[4718592]{0:T(1024)(128)(4,1)}), s8[4194304]{0:T(1024)(128)(4,1)S(1)}, s32[]{:S(2)}) async-start(s8[4718592]{0:T(1024)(128)(4,1)} %bitcast.430), calls=%async_computation.4 | async-start | bytes 8388608
  129.8 3.0 %copy-start.32 = (bf16[2048,512]{1,0:T(8,128)(2,1)S(1)}, bf16[2048,512]{1,0:T(8,128)(2,1)}, u32[]{:S(2)}) copy-start(bf16[2048,512]{1,0:T(8,128)(2,1)} %all-gather.6.cloned.1.call-done) | copy-start | bytes 6291460
  153.6 3.1 %copy-start.35 = (f32[4,384]{1,0:T(4,128)S(1)}, f32[4,384]{1,0:T(4,128)}, u32[]{:S(2)}) copy-start(f32[4,384]{1,0:T(4,128)} %get-tuple-element.28) | copy-start | bytes 18436
  153.6 3.1 %copy-start.48 = (f32[1,384]{1,0:T(1,128)S(1)}, f32[1,384]{1,0:T(1,128)}, u32[]{:S(2)}) copy-start(f32[1,384]{1,0:T(1,128)} %get-tuple-element.255) | copy-start | bytes 4612
  153.6 3.0 %copy-start.49 = (f32[1,384]{1,0:T(1,128)S(1)}, f32[1,384]{1,0:T(1,128)}, u32[]{:S(2)}) copy-start(f32[1,384]{1,0:T(1,128)} %get-tuple-element.252) | copy-start | bytes 4612
  153.6 3.2 %copy-start.47 = (f32[1,384]{1,0:T(1,128)S(1)}, f32[1,384]{1,0:T(1,128)}, u32[]{:S(2)}) copy-start(f32[1,384]{1,0:T(1,128)} %get-tuple-element.155) | copy-start | bytes 4612
  153.6 3.2 %copy-start.50 = (f32[1,384]{1,0:T(1,128)S(1)}, f32[1,384]{1,0:T(1,128)}, u32[]{:S(2)}) copy-start(f32[1,384]{1,0:T(1,128)} %get-tuple-element.241) | copy-start | bytes 4612
  153.6 3.2 %copy-start.51 = (f32[1,384]{1,0:T(1,128)S(1)}, f32[1,384]{1,0:T(1,128)}, u32[]{:S(2)}) copy-start(f32[1,384]{1,0:T(1,128)} %get-tuple-element.242) | copy-start | bytes 4612
  156.9 3.2 %copy-start.28 = (bf16[768,768]{1,0:T(8,128)(2,1)S(1)}, bf16[768,768]{1,0:T(8,128)(2,1)}, u32[]{:S(2)}) copy-start(bf16[768,768]{1,0:T(8,128)(2,1)} %get-tuple-element.27) | copy-start | bytes 3538948
  158.3 2.4 copy-start.27
  158.3 2.4 copy-start.55
  228.4 5.0 %copy-start.38 = (f32[8,128]{1,0:T(8,128)}, f32[8,128]{1,0:T(8,128)S(1)}, u32[]{:S(2)}) copy-start(f32[8,128]{1,0:T(8,128)S(1)} %slice_multiply_fusion.4) | copy-start | bytes 12292
  228.5 5.5 %copy-start.20 = (f32[1024,128]{1,0:T(8,128)}, f32[1024,128]{1,0:T(8,128)S(1)}, u32[]{:S(2)}) copy-start(f32[1024,128]{1,0:T(8,128)S(1)} %slice_multiply_fusion.2) | copy-start | bytes 1572868
  229.9 3.5 %copy-start.52 = (f32[2,4,128]{2,1,0:T(4,128)S(1)}, f32[2,4,128]{2,1,0:T(4,128)}, u32[]{:S(2)}) copy-start(f32[2,4,128]{2,1,0:T(4,128)} %param.36) | copy-start | bytes 12292
  229.9 3.5 %copy-start.53 = (f32[2,4,128]{2,1,0:T(4,128)S(1)}, f32[2,4,128]{2,1,0:T(4,128)}, u32[]{:S(2)}) copy-start(f32[2,4,128]{2,1,0:T(4,128)} %param.31) | copy-start | bytes 12292
  229.9 4.1 %copy-start.19 = (f32[2,512,128]{2,1,0:T(8,128)S(1)}, f32[2,512,128]{2,1,0:T(8,128)}, u32[]{:S(2)}) copy-start(f32[2,512,128]{2,1,0:T(8,128)} %param.25) | copy-start | bytes 1572868
  234.0 2.7 %copy-start.16 = (f32[2,128,768]{2,1,0:T(8,128)S(1)}, f32[2,128,768]{2,1,0:T(8,128)}, u32[]{:S(2)}) copy-start(f32[2,128,768]{2,1,0:T(8,128)} %param.23) | copy-start | bytes 2359300
  234.0 2.7 %copy-start.17 = (f32[2,128,768]{2,1,0:T(8,128)S(1)}, f32[2,128,768]{2,1,0:T(8,128)}, u32[]{:S(2)}) copy-start(f32[2,128,768]{2,1,0:T(8,128)} %mul.6050) | copy-start | bytes 2359300
  234.0 5.9 %copy-start.25 = (f32[2,1536,128]{2,1,0:T(8,128)S(1)}, f32[2,1536,128]{2,1,0:T(8,128)}, u32[]{:S(2)}) copy-start(f32[2,1536,128]{2,1,0:T(8,128)} %param.29) | copy-start | bytes 4718596
  236.7 3.2 %copy-start.10 = (f32[2,1536,128]{2,1,0:T(8,128)S(1)}, f32[2,1536,128]{2,1,0:T(8,128)}, u32[]{:S(2)}) copy-start(f32[2,1536,128]{2,1,0:T(8,128)} %param.24) | copy-start | bytes 4718596
  236.7 3.2 %copy-start.13 = (f32[3072,128]{1,0:T(8,128)S(1)}, f32[3072,128]{1,0:T(8,128)}, u32[]{:S(2)}) copy-start(f32[3072,128]{1,0:T(8,128)} %slice_multiply_fusion) | copy-start | bytes 4718596
  236.7 3.2 %copy-start.24 = (f32[2,1536,128]{2,1,0:T(8,128)S(1)}, f32[2,1536,128]{2,1,0:T(8,128)}, u32[]{:S(2)}) copy-start(f32[2,1536,128]{2,1,0:T(8,128)} %param.34) | copy-start | bytes 4718596
  (21 other events, 32.0 us)
Sparse Core Ops, SparseCore 0:
  10.2 23.1 all-gather.3
  35.5 22.4 all-gather.5
  60.2 22.8 all-gather.7

commit v25 on v23

--- a/solution.py
+++ b/solution.py
@@ -105,7 +105,7 @@
         return (hu_re[7:8], hu_im[7:8], hd_re[0:1], hd_im[0:1])
 
     zeros = jnp.zeros((1, width), jnp.float32)
-    lax.fori_loop(0, tiles, step, (zeros, zeros, zeros, zeros), unroll=2)
+    lax.fori_loop(0, tiles, step, (zeros, zeros, zeros, zeros), unroll=4)
 
 
 def pole_powers(p_re, p_im):

time: 252 us -> 252 us (level)
  no operation moved by 1% of the time
where the time goes in v25:
time: 252 us; the launch traced here: 251 us
  Pallas kernels  109 us (43%)
  matrix products  47.4 us (19%)
  other arithmetic  37.9 us (15%)
  blocking collectives  20.2 us (8%)
  local copies, waits for them, and re-layouts  16.4 us (7%)
  between operations  14.7 us (6%)
  waiting for transfers between devices  5.19 us (2%)
    pallas_call x1, Pallas kernels, ring_sum(): pl.pallas_call(lambda *refs: ring_sum_kernel(n, *refs), out_shape=jax.Sha...  61.4 us
    pallas_call x2, Pallas kernels, adjoint(): pl.pallas_call(adjoint_kernel, out_shape=(jax.ShapeDtypeStruct((count, 2...  30.6 us
    all_gather x2, blocking collectives, gather_feat(): return lax.all_gather(value, 'feat', axis=axis, tiled=True)  20.2 us
    pallas_call x2, Pallas kernels, recurrence(): pl.pallas_call(recurrence_kernel, out_shape=jax.ShapeDtypeStruct((count,...  17.1 us
    dot_general x4, matrix products, contract_cols(): lax.dot_general(left, right, (((1,), (1,)), ((), ())), preferred_element_...  14.2 us
    dot_general x2, matrix products, body(): jnp.dot(states_low, out_low, preferred_element_type=jnp.float32)  10 us
    add x5, other arithmetic, update(): average_new = smoothing * average + (1.0 - smoothing) * weight_new  9.08 us
    unnamed x140, local copies, waits for them, and re-layouts  8.76 us
  transfers between devices with their start and end apart: 3, of which 2 were waited for; matrix products, arithmetic and copies ran while one was open for 11% of the time, Pallas kernels for 7%

profile of v25, /device:TPU:0, one launch (start us, length us, event | category | flops | bytes accessed | tf_op | source)
XLA Modules:
  0.0 251.2 jit_solution(11858994888122537585)
XLA Ops:
  7.3 2.1 convert_element_type.103
  9.7 0.8 pad_maximum_fusion.4
  10.6 0.8 pad_maximum_fusion.5
  12.2 10.2 %all_gather.15 = bf16[800,512]{1,0:T(8,128)(2,1)S(1)} all-gather(bf16[800,128]{1,0:T(8,128)(2,1)S(1)} %pad_maximum_fusion.7), channel_id=1, replica_groups=mesh['seq'=8,'feat'=4] {'feat'}, dimensions={1}, use_global_device_ids=true | all-gather | bytes 1024000 | tf_op jit(solution)/shard_map/all_gather | solution.py:412
  25.2 0.9 copy.86.masks_ref
  26.6 10.0 %all_gather.19 = bf16[768,512]{1,0:T(8,128)(2,1)} all-gather(bf16[768,128]{1,0:T(8,128)(2,1)S(1)} %copy-done.31), channel_id=1, replica_groups=mesh['seq'=8,'feat'=4] {'feat'}, dimensions={1}, use_global_device_ids=true | all-gather | bytes 983040 | tf_op jit(solution)/shard_map/all_gather | solution.py:412
  37.2 1.2 fusion.9
  40.4 2.2 fusion.15.drive_ref
  43.0 1.0 copy-done
  44.0 1.6 pad_maximum_fusion.x_ref
  45.7 8.6 %shard_map.354.states_ref = f32[768,1536]{1,0:T(8,128)} custom-call(s32[2]{0:T(128)} %starts_ref.7, s32[2]{0:T(128)} %lengths_ref.7, f32[4,8,384]{2,1,0:T(8,128)} %pad_maximum_fusion.8.pow_ref, f32[768,768]{1,0:T(8,128)} %pad_maximum_fusion.x_ref), custom_call_target="tpu_custom_call" | custom-call | flops 11796480 | bytes 9437184 | tf_op jit(solution)/shard_map/pallas_call | solution.py:144
  54.3 3.8 %all-gather.6.cloned.1.call-done = bf16[2048,512]{1,0:T(8,128)(2,1)} async-done(((bf16[2048,128]{1,0:T(8,128)(2,1)}), bf16[2048,512]{1,0:T(8,128)(2,1)}) %all-gather.6.cloned.1.call-update) | async-done | bytes 2097168 | tf_op jit(solution)/shard_map/all_gather | solution.py:412
  58.1 5.7 %fusion.91 = (f32[768,512]{1,0:T(8,128)S(1)}, f32[768,512]{1,0:T(8,128)}) fusion(f32[512]{0:T(512)S(1)} %bitcast.465, f32[512]{0:T(512)S(1)} %bitcast.468, f32[768]{0:T(1024)S(1)} %add_rsqrt_fusion.1, f32[768]{0:T(1024)S(1)} %broadcast_multiply_fusion.6, bf16[800,512]{1,0:T(8,128)(2,1)S(1)} %copy-done.5, f32[512]{0:T(512)S(1)} %bitcast.474, ...), kind=kOutput, calls=%fused_computation.342 | convolution fusion | flops 1213464576 | bytes 10235904 | tf_op jit(solution)/shard_map/dot_general | solution.py:509
  63.8 3.4 %fusion.109 = (f32[768]{0:T(1024)S(1)}, f32[768,512]{1,0:T(8,128)S(1)}, f32[768,512]{1,0:T(8,128)}) fusion(f32[768,512]{1,0:T(8,128)S(1)} %get-tuple-element.300, bf16[800,512]{1,0:T(8,128)(2,1)S(1)} %copy-done.5, f32[512]{0:T(512)S(1)} %bitcast.479, bf16[2048,512]{1,0:T(8,128)(2,1)} %all-gather.6.cloned.1.call-done), kind=kOutput, calls=%fused_computation.350 | convolution fusion | flops 406191360 | bytes 7607296 | tf_op jit(solution)/shard_map/dot_general | solution.py:515
  68.3 0.9 copy-done.26
  70.5 1.1 copy-done.1
  71.6 1.6 pad_maximum_fusion.1.x_ref
  73.1 8.5 %shard_map.355.states_ref = f32[768,1536]{1,0:T(8,128)} custom-call(s32[2]{0:T(128)} %starts_ref.7, s32[2]{0:T(128)} %lengths_ref.7, f32[4,8,384]{2,1,0:T(8,128)} %pad_maximum_fusion.9.pow_ref, f32[768,768]{1,0:T(8,128)} %pad_maximum_fusion.1.x_ref), custom_call_target="tpu_custom_call" | custom-call | flops 11796480 | bytes 9437184 | tf_op jit(solution)/shard_map/pallas_call | solution.py:144
  81.7 1.4 all-gather.8.cloned.1.call-done
  83.1 4.3 %fusion.92 = (f32[768,512]{1,0:T(8,128)S(1)}, f32[768,512]{1,0:T(8,128)S(1)}) fusion(f32[512]{0:T(512)S(1)} %bitcast.471, f32[512]{0:T(512)S(1)} %bitcast.457, f32[768]{0:T(1024)S(1)} %add_rsqrt_fusion, f32[768,512]{1,0:T(8,128)S(1)} %copy-done.3, f32[768]{0:T(1024)S(1)} %broadcast_multiply_fusion.5, f32[512]{0:T(512)S(1)} %bitcast.476, ...), kind=kOutput, calls=%fused_computation.343 | convolution fusion | flops 1213071360 | bytes 11022336 | tf_op jit(solution)/shard_map/dot_general | solution.py:509
  87.4 1.6 convert_reduce_fusion.1
  89.4 0.9 dynamic-slice_add_fusion.1
  90.3 2.3 fusion.111
  92.7 1.7 convolution_bitcast_fusion
  94.4 3.6 %fusion.3.g_ref = f32[768,1536]{1,0:T(8,128)} fusion(bf16[768,512]{1,0:T(8,128)(2,1)S(1)} %get-tuple-element.306, bf16[2048,512]{1,0:T(8,128)(2,1)S(1)} %copy-done.33), kind=kOutput, calls=%fused_computation.43 | convolution fusion | flops 1207959552 | bytes 7077888 | tf_op jit(solution)/shard_map/dot_general | solution.py:406
  98.0 15.3 %shard_map.356 = (bf16[768,768]{1,0:T(8,128)(2,1)}, f32[4,384]{1,0:T(4,128)}) custom-call(s32[2]{0:T(128)} %starts_ref.7, s32[2]{0:T(128)} %lengths_ref.7, f32[4,8,384]{2,1,0:T(8,128)} %pad_maximum_fusion.10.pow_ref, f32[4,384]{1,0:T(4,128)} %pad_maximum_fusion.13.coef_ref, f32[768,4]{1,0:T(8,128)} %copy.86.masks_ref, f32[768,1536]{1,0:T(8,128)} %fusion.3.g_ref, ...), custom_call_target="tpu_custom_call" | custom-call | flops 17694720 | bytes 14155776 | tf_op jit(solution)/shard_map/pallas_call | solution.py:375
  113.3 2.6 %convolution_bitcast_fusion.2 = f32[1,128,768]{2,1,0:T(8,128)} fusion(bf16[768,768]{1,0:T(8,128)(2,1)} %get-tuple-element.26, bf16[768,512]{1,0:T(8,128)(2,1)} %copy-done.14, s32[]{:T(128)S(6)} %select_n.2), kind=kOutput, calls=%fused_computation.50 | convolution fusion | flops 150994944 | bytes 1769476 | tf_op jit(solution)/shard_map/dot_general | solution.py:400
  116.0 3.7 %multiply_reduce_fusion.1 = (f32[512]{0:T(512)}, f32[768]{0:T(1024)S(1)}, f32[512]{0:T(512)}, f32[768]{0:T(1024)S(1)}, f32[512]{0:T(512)}, /*index=5*/f32[768,512]{1,0:T(8,128)S(1)}) fusion(f32[768]{0:T(1024)S(1)} %add_rsqrt_fusion, f32[768,512]{1,0:T(8,128)S(1)} %copy-done.3, f32[768]{0:T(1024)S(1)} %broadcast_multiply_fusion.5, f32[512]{0:T(512)S(1)} %bitcast.458, ...), kind=kOutput, calls=%fused_computation.19 | convolution fusion | flops 609874944 | bytes 6709248 | tf_op jit(solution)/shard_map/dot_general | solution.py:555
  119.6 2.1 convert_reduce_fusion.2
  124.8 4.6 %fusion.112 = (bf16[768,512]{1,0:T(8,128)(2,1)S(1)}, f32[768,512]{1,0:T(8,128)}) fusion(f32[768,512]{1,0:T(8,128)} %get-tuple-element.301, bf16[768,512]{1,0:T(8,128)(2,1)} %copy-done.15, bf16[2048,512]{1,0:T(8,128)(2,1)} %all-gather.6.cloned.1.call-done, f32[768,512]{1,0:T(8,128)S(1)} %copy-done.6, f32[768,512]{1,0:T(8,128)} %get-tuple-element.302), kind=kOutput, calls=%fused_computation.353 | convolution fusion | flops 407371776 | bytes 8388608 | tf_op jit(solution)/shard_map/dot_general | solution.py:406
  129.5 1.7 convolution_bitcast_fusion.1
  132.4 3.6 %fusion.6.g_ref = f32[768,1536]{1,0:T(8,128)} fusion(bf16[768,512]{1,0:T(8,128)(2,1)S(1)} %get-tuple-element.309, bf16[2048,512]{1,0:T(8,128)(2,1)S(1)} %copy-done.32), kind=kOutput, calls=%fused_computation.46 | convolution fusion | flops 1207959552 | bytes 7077888 | tf_op jit(solution)/shard_map/dot_general | solution.py:406
  136.1 15.3 %shard_map.357 = (bf16[768,768]{1,0:T(8,128)(2,1)}, f32[4,384]{1,0:T(4,128)}) custom-call(s32[2]{0:T(128)} %starts_ref.7, s32[2]{0:T(128)} %lengths_ref.7, f32[4,8,384]{2,1,0:T(8,128)} %pad_maximum_fusion.11.pow_ref, f32[4,384]{1,0:T(4,128)} %pad_maximum_fusion.14.coef_ref, f32[768,4]{1,0:T(8,128)} %copy.86.masks_ref, f32[768,1536]{1,0:T(8,128)} %fusion.6.g_ref, ...), custom_call_target="tpu_custom_call" | custom-call | flops 17694720 | bytes 14155776 | tf_op jit(solution)/shard_map/pallas_call | solution.py:375
  151.4 1.8 convolution_bitcast_fusion.3
  153.2 0.9 pad_maximum_fusion.3
  154.2 2.1 reshape.1853
  156.5 1.3 constant_dynamic-update-slice_fusion.4
  157.9 1.6 pad_maximum_fusion.2
  160.3 2.9 %fusion.93 = (f32[512]{0:T(512)S(1)}, f32[512]{0:T(512)S(1)}, f32[512]{0:T(512)S(1)}, f32[768]{0:T(1024)S(1)}, f32[768]{0:T(1024)S(1)}, /*index=5*/f32[768,512]{1,0:T(8,128)}, f32[768,512]{1,0:T(8,128)}) fusion(f32[768]{0:T(1024)S(1)} %add_rsqrt_fusion.1, f32[768]{0:T(1024)S(1)} %broadcast_multiply_fusion.6, bf16[800,512]{1,0:T(8,128)(2,1)S(1)} %copy-done.5, ...), kind=kOutput, calls=%fused_computation.344 | convolution fusion | flops 610268160 | bytes 7497728 | tf_op jit(solution)/shard_map/dot_general | solution.py:555
  163.5 1.8 pad_bitcast_fusion.refs_0_
  165.3 61.4 %shard_map.358 = bf16[5888,128]{1,0:T(8,128)(2,1)} custom-call(f32[5888,128]{1,0:T(8,128)} %pad_bitcast_fusion.refs_0_), custom_call_target="tpu_custom_call" | custom-call | tf_op jit(solution)/shard_map/pallas_call | solution.py:267
  226.6 1.6 convert_element_type.123
  228.4 1.3 slice_multiply_fusion
  232.2 1.0 mul.6050
  233.9 2.6 %add_multiply_fusion.8 = (f32[2,512,128]{2,1,0:T(8,128)}, f32[2,512,128]{2,1,0:T(8,128)}, f32[2,512,128]{2,1,0:T(8,128)}) fusion(f32[2,512,128]{2,1,0:T(8,128)} %param.35, f32[2,512,128]{2,1,0:T(8,128)S(1)} %copy-done.19, f32[2,512,128]{2,1,0:T(8,128)S(1)} %bitcast.437, f32[2,512,128]{2,1,0:T(8,128)} %param.30), kind=kLoop, calls=%fused_computation.79 | loop fusion | flops 1310720 | bytes 3670016 | tf_op jit(solution)/shard_map/add | solution.py:395
  236.6 3.2 %add_multiply_fusion.7 = (f32[2,128,768]{2,1,0:T(8,128)}, f32[2,128,768]{2,1,0:T(8,128)}, f32[2,128,768]{2,1,0:T(8,128)}) fusion(f32[2,128,768]{2,1,0:T(8,128)} %param.33, f32[2,128,768]{2,1,0:T(8,128)S(1)} %copy-done.16, f32[2,128,768]{2,1,0:T(8,128)S(1)} %copy-done.17, f32[2,128,768]{2,1,0:T(8,128)} %param.28), kind=kLoop, calls=%fused_computation.68 | loop fusion | flops 1966080 | bytes 5505024 | tf_op jit(solution)/shard_map/add | solution.py:395
  239.7 2.6 %add_multiply_fusion = (f32[2,1536,128]{2,1,0:T(8,128)}, f32[2,1536,128]{2,1,0:T(8,128)}, f32[2,1536,128]{2,1,0:T(8,128)}) fusion(f32[2,1536,128]{2,1,0:T(8,128)S(1)} %copy-done.24, f32[2,1536,128]{2,1,0:T(8,128)S(1)} %copy-done.10, f32[2,1536,128]{2,1,0:T(8,128)S(1)} %bitcast.436, f32[2,1536,128]{2,1,0:T(8,128)S(1)} %copy-done.25), kind=kLoop, calls=%fused_computation.13 | loop fusion | flops 3932160 | bytes 11010048 | tf_op jit(solution)/shard_map/add | solution.py:395
  242.4 2.2 dynamic-slice_add_fusion
  (230 shorter events, 18.7 us)
Async XLA Ops:
  7.2 2.2 copy-start.9
  7.2 33.2 %all-gather.4.cloned.1.call-start = ((), (), s32[]{:S(2)}) async-start(), calls=%async_computation | async-start | bytes 1966080 | tf_op jit(solution)/shard_map/all_gather | solution.py:412
  9.3 48.7 %all-gather.6.cloned.1.call-start = ((), (), s32[]{:S(2)}) async-start(), calls=%async_computation.1 | async-start | bytes 2621440 | tf_op jit(solution)/shard_map/all_gather | solution.py:412
  9.7 2.5 copy-start.37
  9.7 2.5 %copy-start.30 = (bf16[768,128]{1,0:T(8,128)(2,1)S(1)}, bf16[768,128]{1,0:T(8,128)(2,1)}, u32[]{:S(2)}) copy-start(bf16[768,128]{1,0:T(8,128)(2,1)} %param.19) | copy-start | bytes 589828
  10.5 72.5 %all-gather.8.cloned.1.call-start = ((), (), s32[]{:S(2)}) async-start(), calls=%async_computation.2 | async-start | bytes 2621440 | tf_op jit(solution)/shard_map/all_gather | solution.py:412
  11.4 11.2 %copy-start.36 = (s32[2]{0:T(128)S(1)}, s32[2]{0:T(128)}, u32[]{:S(2)}) copy-start(s32[2]{0:T(128)} %starts_ref.7) | copy-start | bytes 28
  11.4 11.2 %copy-start.39 = (s32[2]{0:T(128)S(1)}, s32[2]{0:T(128)}, u32[]{:S(2)}) copy-start(s32[2]{0:T(128)} %lengths_ref.7) | copy-start | bytes 28
  22.5 14.8 %copy-start.4 = (bf16[800,512]{1,0:T(8,128)(2,1)}, bf16[800,512]{1,0:T(8,128)(2,1)S(1)}, u32[]{:S(2)}) copy-start(bf16[800,512]{1,0:T(8,128)(2,1)S(1)} %all_gather.15) | copy-start | bytes 2457604
  22.5 4.2 %copy-start.31 = (bf16[768,128]{1,0:T(8,128)(2,1)S(1)}, bf16[768,128]{1,0:T(8,128)(2,1)}, u32[]{:S(2)}) copy-start(bf16[768,128]{1,0:T(8,128)(2,1)} %param.20) | copy-start | bytes 589828
  26.6 31.4 %copy-start.54 = (f32[1,512]{1,0:T(1,128)}, f32[1,512]{1,0:T(1,128)S(1)}, u32[]{:S(2)}) copy-start(f32[1,512]{1,0:T(1,128)S(1)} %get-tuple-element.248) | copy-start | bytes 6148
  26.6 56.4 %copy-start.56 = (f32[1,512]{1,0:T(1,128)}, f32[1,512]{1,0:T(1,128)S(1)}, u32[]{:S(2)}) copy-start(f32[1,512]{1,0:T(1,128)S(1)} %get-tuple-element.243) | copy-start | bytes 6148
  45.7 12.4 %copy-start.5 = (bf16[800,512]{1,0:T(8,128)(2,1)S(1)}, bf16[800,512]{1,0:T(8,128)(2,1)}, u32[]{:S(2)}) copy-start(bf16[800,512]{1,0:T(8,128)(2,1)} %copy-done.4) | copy-start | bytes 2457604
  63.8 3.4 %copy-start.11 = (f32[768,512]{1,0:T(8,128)}, f32[768,512]{1,0:T(8,128)S(1)}, u32[]{:S(2)}) copy-start(f32[768,512]{1,0:T(8,128)S(1)} %get-tuple-element.300) | copy-start | bytes 4718596
  73.1 9.9 %copy-start.3 = (f32[768,512]{1,0:T(8,128)S(1)}, f32[768,512]{1,0:T(8,128)}, u32[]{:S(2)}) copy-start(f32[768,512]{1,0:T(8,128)} %copy-done.2) | copy-start | bytes 4718596
  83.1 4.3 %copy-start.7 = (bf16[768,512]{1,0:T(8,128)(2,1)S(1)}, bf16[768,512]{1,0:T(8,128)(2,1)}, u32[]{:S(2)}) copy-start(bf16[768,512]{1,0:T(8,128)(2,1)} %all_gather.19) | copy-start | bytes 2359300
  83.1 4.3 %copy-start.33 = (bf16[2048,512]{1,0:T(8,128)(2,1)S(1)}, bf16[2048,512]{1,0:T(8,128)(2,1)}, u32[]{:S(2)}) copy-start(bf16[2048,512]{1,0:T(8,128)(2,1)} %all-gather.8.cloned.1.call-done) | copy-start | bytes 6291460
  89.4 3.2 %slice-start.2 = ((s8[4718592]{0:T(1024)(128)(4,1)}), s8[4194304]{0:T(1024)(128)(4,1)S(1)}, s32[]{:S(2)}) async-start(s8[4718592]{0:T(1024)(128)(4,1)} %bitcast.432), calls=%async_computation.5 | async-start | bytes 8388608
  90.3 2.3 slice-start.3
  113.3 2.6 %copy-start.22 = (f32[768,512]{1,0:T(8,128)S(1)}, f32[768,512]{1,0:T(8,128)}, u32[]{:S(2)}) copy-start(f32[768,512]{1,0:T(8,128)} %get-tuple-element.307) | copy-start | bytes 4718596
  113.3 2.6 %copy-start.57 = (f32[1,512]{1,0:T(1,128)S(1)}, f32[1,512]{1,0:T(1,128)}, u32[]{:S(2)}) copy-start(f32[1,512]{1,0:T(1,128)} %copy-done.56) | copy-start | bytes 6148
  115.9 3.7 %copy-start.8 = (f32[768,512]{1,0:T(8,128)S(1)}, f32[768,512]{1,0:T(8,128)}, u32[]{:S(2)}) copy-start(f32[768,512]{1,0:T(8,128)} %get-tuple-element.302) | copy-start | bytes 4718596
  115.9 3.7 %copy-start.12 = (f32[768,512]{1,0:T(8,128)S(1)}, f32[768,512]{1,0:T(8,128)}, u32[]{:S(2)}) copy-start(f32[768,512]{1,0:T(8,128)} %copy-done.11) | copy-start | bytes 4718596
  121.7 2.2 copy-start.45
  121.7 3.1 %copy-start.6 = (f32[768,512]{1,0:T(8,128)S(1)}, f32[768,512]{1,0:T(8,128)}, u32[]{:S(2)}) copy-start(f32[768,512]{1,0:T(8,128)} %get-tuple-element.159) | copy-start | bytes 4718596
  121.8 7.7 %slice-start = ((s8[4718592]{0:T(1024)(128)(4,1)}), s8[524288]{0:T(1024)(128)(4,1)S(1)}, s32[]{:S(2)}) async-start(s8[4718592]{0:T(1024)(128)(4,1)} %bitcast.430), calls=%async_computation.3 | async-start | bytes 1048576
  124.8 4.7 %slice-start.1 = ((s8[4718592]{0:T(1024)(128)(4,1)}), s8[4194304]{0:T(1024)(128)(4,1)S(1)}, s32[]{:S(2)}) async-start(s8[4718592]{0:T(1024)(128)(4,1)} %bitcast.430), calls=%async_computation.4 | async-start | bytes 8388608
  129.5 3.0 %copy-start.32 = (bf16[2048,512]{1,0:T(8,128)(2,1)S(1)}, bf16[2048,512]{1,0:T(8,128)(2,1)}, u32[]{:S(2)}) copy-start(bf16[2048,512]{1,0:T(8,128)(2,1)} %all-gather.6.cloned.1.call-done) | copy-start | bytes 6291460
  153.2 3.1 %copy-start.35 = (f32[4,384]{1,0:T(4,128)S(1)}, f32[4,384]{1,0:T(4,128)}, u32[]{:S(2)}) copy-start(f32[4,384]{1,0:T(4,128)} %get-tuple-element.28) | copy-start | bytes 18436
  153.2 3.1 %copy-start.48 = (f32[1,384]{1,0:T(1,128)S(1)}, f32[1,384]{1,0:T(1,128)}, u32[]{:S(2)}) copy-start(f32[1,384]{1,0:T(1,128)} %get-tuple-element.255) | copy-start | bytes 4612
  153.2 3.0 %copy-start.49 = (f32[1,384]{1,0:T(1,128)S(1)}, f32[1,384]{1,0:T(1,128)}, u32[]{:S(2)}) copy-start(f32[1,384]{1,0:T(1,128)} %get-tuple-element.252) | copy-start | bytes 4612
  153.2 3.2 %copy-start.47 = (f32[1,384]{1,0:T(1,128)S(1)}, f32[1,384]{1,0:T(1,128)}, u32[]{:S(2)}) copy-start(f32[1,384]{1,0:T(1,128)} %get-tuple-element.155) | copy-start | bytes 4612
  153.2 3.2 %copy-start.50 = (f32[1,384]{1,0:T(1,128)S(1)}, f32[1,384]{1,0:T(1,128)}, u32[]{:S(2)}) copy-start(f32[1,384]{1,0:T(1,128)} %get-tuple-element.241) | copy-start | bytes 4612
  153.2 3.2 %copy-start.51 = (f32[1,384]{1,0:T(1,128)S(1)}, f32[1,384]{1,0:T(1,128)}, u32[]{:S(2)}) copy-start(f32[1,384]{1,0:T(1,128)} %get-tuple-element.242) | copy-start | bytes 4612
  156.5 3.2 %copy-start.28 = (bf16[768,768]{1,0:T(8,128)(2,1)S(1)}, bf16[768,768]{1,0:T(8,128)(2,1)}, u32[]{:S(2)}) copy-start(bf16[768,768]{1,0:T(8,128)(2,1)} %get-tuple-element.27) | copy-start | bytes 3538948
  157.9 2.4 copy-start.27
  157.9 2.4 copy-start.55
  228.2 5.0 %copy-start.38 = (f32[8,128]{1,0:T(8,128)}, f32[8,128]{1,0:T(8,128)S(1)}, u32[]{:S(2)}) copy-start(f32[8,128]{1,0:T(8,128)S(1)} %slice_multiply_fusion.4) | copy-start | bytes 12292
  228.3 5.5 %copy-start.20 = (f32[1024,128]{1,0:T(8,128)}, f32[1024,128]{1,0:T(8,128)S(1)}, u32[]{:S(2)}) copy-start(f32[1024,128]{1,0:T(8,128)S(1)} %slice_multiply_fusion.2) | copy-start | bytes 1572868
  229.7 3.5 %copy-start.52 = (f32[2,4,128]{2,1,0:T(4,128)S(1)}, f32[2,4,128]{2,1,0:T(4,128)}, u32[]{:S(2)}) copy-start(f32[2,4,128]{2,1,0:T(4,128)} %param.36) | copy-start | bytes 12292
  229.7 3.5 %copy-start.53 = (f32[2,4,128]{2,1,0:T(4,128)S(1)}, f32[2,4,128]{2,1,0:T(4,128)}, u32[]{:S(2)}) copy-start(f32[2,4,128]{2,1,0:T(4,128)} %param.31) | copy-start | bytes 12292
  229.7 4.1 %copy-start.19 = (f32[2,512,128]{2,1,0:T(8,128)S(1)}, f32[2,512,128]{2,1,0:T(8,128)}, u32[]{:S(2)}) copy-start(f32[2,512,128]{2,1,0:T(8,128)} %param.25) | copy-start | bytes 1572868
  233.9 2.7 %copy-start.16 = (f32[2,128,768]{2,1,0:T(8,128)S(1)}, f32[2,128,768]{2,1,0:T(8,128)}, u32[]{:S(2)}) copy-start(f32[2,128,768]{2,1,0:T(8,128)} %param.23) | copy-start | bytes 2359300
  233.9 2.7 %copy-start.17 = (f32[2,128,768]{2,1,0:T(8,128)S(1)}, f32[2,128,768]{2,1,0:T(8,128)}, u32[]{:S(2)}) copy-start(f32[2,128,768]{2,1,0:T(8,128)} %mul.6050) | copy-start | bytes 2359300
  233.9 5.9 %copy-start.25 = (f32[2,1536,128]{2,1,0:T(8,128)S(1)}, f32[2,1536,128]{2,1,0:T(8,128)}, u32[]{:S(2)}) copy-start(f32[2,1536,128]{2,1,0:T(8,128)} %param.29) | copy-start | bytes 4718596
  236.5 3.2 %copy-start.10 = (f32[2,1536,128]{2,1,0:T(8,128)S(1)}, f32[2,1536,128]{2,1,0:T(8,128)}, u32[]{:S(2)}) copy-start(f32[2,1536,128]{2,1,0:T(8,128)} %param.24) | copy-start | bytes 4718596
  236.5 3.2 %copy-start.13 = (f32[3072,128]{1,0:T(8,128)S(1)}, f32[3072,128]{1,0:T(8,128)}, u32[]{:S(2)}) copy-start(f32[3072,128]{1,0:T(8,128)} %slice_multiply_fusion) | copy-start | bytes 4718596
  236.5 3.2 %copy-start.24 = (f32[2,1536,128]{2,1,0:T(8,128)S(1)}, f32[2,1536,128]{2,1,0:T(8,128)}, u32[]{:S(2)}) copy-start(f32[2,1536,128]{2,1,0:T(8,128)} %param.34) | copy-start | bytes 4718596
  (21 other events, 32.0 us)
Sparse Core Ops, SparseCore 0:
  10.2 23.1 all-gather.3
  35.5 22.4 all-gather.5
  60.2 22.8 all-gather.7
